TPU v7x, 32 devices: a whole 2x2x4 slice. The times are simulated.
32 devices in a mesh: expert: 8 (over z, core), dp: 4 (over y, x).
Axes of the slice: x: 2, y: 2, z: 4, core: 2. Of those that a mesh axis runs over, the one named last changes fastest.
Arguments:
- layer_input: bfloat16 [8192, 1024], P(('expert', 'dp')), may hold values from -6 to 6
- attn_gain: bfloat16 [1024], P('dp'), may hold values from 0.5 to 1.5
- w_query: bfloat16 [1024, 1024], P('dp'), may hold values from -0.25 to 0.25
- w_key: bfloat16 [1024, 512], P('dp'), may hold values from -0.25 to 0.25
- w_value: bfloat16 [1024, 512], P('dp'), may hold values from -0.1875 to 0.1875
- w_output: bfloat16 [1024, 1024], P('dp'), may hold values from -0.75 to 0.75
- moe_gain: bfloat16 [1024], P('dp'), may hold values from 0.5 to 1.5
- w_router: bfloat16 [1024, 32], P('dp'), may hold values from -0.09375 to 0.09375
- w_gate: bfloat16 [32, 1024, 512], P('expert', 'dp'), may hold values from -0.1875 to 0.1875
- w_up: bfloat16 [32, 1024, 512], P('expert', 'dp'), may hold values from -0.1875 to 0.1875
- w_down: bfloat16 [32, 512, 1024], P('expert', 'dp'), may hold values from -1 to 1
- routes: int32 [8192, 8], P(('expert', 'dp')), may hold values from 0 to 31, all different within a row
- priority: int32 [8192, 8], P(('expert', 'dp')), may hold values from 0 to 2047, as said below
- prefix_len: int32 [8], P('expert'), may hold values from 102 to 512
- out_grad: bfloat16 [8192, 1024], P(('expert', 'dp')), may hold values from -6 to 6
Outputs:
- layer_output: bfloat16 [8192, 1024], P(('expert', 'dp'))
- input_grad: float32 [8192, 1024], P(('expert', 'dp'))
- attn_gain_grad: float32 [1024], P('dp')
- w_query_grad: float32 [1024, 1024], P('dp')
- w_key_grad: float32 [1024, 512], P('dp')
- w_value_grad: float32 [1024, 512], P('dp')
- w_output_grad: float32 [1024, 1024], P('dp')
- moe_gain_grad: float32 [1024], P('dp')
- w_router_grad: float32 [1024, 32], P('dp')
- w_gate_grad: float32 [32, 1024, 512], P('expert', 'dp')
- w_up_grad: float32 [32, 1024, 512], P('expert', 'dp')
- w_down_grad: float32 [32, 512, 1024], P('expert', 'dp')
Inputs may be any that keep to these rules, and one draw needn't show every extreme that they name: `routes`: each row names 8 different experts. `priority`: within each aligned block of 256 rows the entries are a permutation of 0 to 2047.
All inputs are finite; a program needn't handle non-finite values.
Results may differ from a plain program's by a relative error of at most 0.017.
Values may be sent and summed in bfloat16 or wider, within the bound.
No kernel may reach another device: no remote copies, remote signals or barrier semaphores. Data moves between devices by JAX's collectives and lax.ppermute only.
A program may use at most 320 MiB of HBM per device.

v0:
```python
import math

import jax
import jax.numpy as jnp
from jax import lax
from jax.sharding import PartitionSpec as P

H = 16
KVH = 8
HD = 64
EXPERTS = 32


EPSILON = 1e-06
ROPE_BASE = 10000.0
MASKED_SCORE = -1e30


def rms_norm(values, gain_vec):
    return (
        values * lax.rsqrt(jnp.mean(values * values, axis=-1, keepdims=True) + EPSILON) * gain_vec
    )


def rotate(vectors, places):
    half_dim = vectors.shape[-1] // 2
    frequency = jnp.exp(
        jnp.arange(half_dim, dtype=jnp.float32) * (-2.0 * math.log(ROPE_BASE) / vectors.shape[-1])
    )
    angles = places[:, None] * frequency[None, :]
    cosine = jnp.cos(angles)[:, None, :]
    sine_vals = jnp.sin(angles)[:, None, :]
    first_half = vectors[..., :half_dim]
    second = vectors[..., half_dim:]
    return jnp.concatenate(
        [first_half * cosine - second * sine_vals, second * cosine + first_half * sine_vals],
        axis=-1,
    )


def slot_table(route_blk, prio_blk, experts, capacity):
    tok_rows = route_blk.shape[0]
    top_count = route_blk.shape[1]
    pair_count = tok_rows * top_count
    flat_route = route_blk.reshape(pair_count)
    flat_prio = prio_blk.reshape(pair_count)
    counter = jnp.arange(pair_count, dtype=jnp.int32)
    by_priority = jnp.zeros((pair_count,), jnp.int32).at[flat_prio].set(counter)
    ranked = flat_route[by_priority]
    onehot = (ranked[:, None] == jnp.arange(experts, dtype=jnp.int32)[None, :]).astype(jnp.int32)
    before = jnp.cumsum(onehot, axis=0) - onehot
    rank_sorted = jnp.sum(before * onehot, axis=1)
    pair_rank = rank_sorted[flat_prio]
    slot_index = jnp.where(
        pair_rank < capacity, flat_route * capacity + pair_rank, experts * capacity
    )
    token_sources = (
        jnp.full((experts * capacity + 1,), tok_rows, jnp.int32)
        .at[slot_index]
        .set(counter // top_count)
    )
    pair_sources = (
        jnp.full((experts * capacity + 1,), pair_count, jnp.int32).at[slot_index].set(counter)
    )
    return (
        slot_index.reshape(tok_rows, top_count),
        token_sources[: experts * capacity],
        pair_sources[: experts * capacity],
    )


def body(
    layer_input,
    attn_gain,
    w_query,
    w_key,
    w_value,
    w_output,
    moe_gain,
    w_router,
    w_gate,
    w_up,
    w_down,
    routes,
    priority,
    prefix_len,
    out_grad,
):
    tok_rows = layer_input.shape[0]
    model_width = layer_input.shape[1]
    dp_size = lax.axis_size("dp")
    seq_len = tok_rows * dp_size
    top_count = routes.shape[1]
    capacity = 5 * tok_rows * top_count // (4 * EXPERTS)
    group_size = H // KVH
    score_scale = HD ** (-0.5)
    f32 = jnp.float32
    b16 = jnp.bfloat16
    gathered = (
        lax.all_gather(attn_gain, "dp", axis=0, tiled=True),
        lax.all_gather(w_query, "dp", axis=0, tiled=True),
        lax.all_gather(w_key, "dp", axis=0, tiled=True),
        lax.all_gather(w_value, "dp", axis=0, tiled=True),
        lax.all_gather(w_output, "dp", axis=0, tiled=True),
        lax.all_gather(moe_gain, "dp", axis=0, tiled=True),
        lax.all_gather(w_router, "dp", axis=0, tiled=True),
        lax.all_gather(w_gate, "dp", axis=1, tiled=True),
        lax.all_gather(w_up, "dp", axis=1, tiled=True),
        lax.all_gather(w_down, "dp", axis=1, tiled=True),
    )
    (
        full_attn_gain,
        full_query,
        full_key,
        full_value,
        full_output,
        full_moe_gain,
        full_router,
        full_gate,
        full_up,
        full_down,
    ) = gathered
    query_pos = lax.axis_index("dp") * tok_rows + jnp.arange(tok_rows, dtype=jnp.int32)
    places = query_pos.astype(f32)
    in_float = layer_input.astype(f32)
    normed = rms_norm(in_float, full_attn_gain.astype(f32)).astype(b16)
    query_lin = jnp.dot(normed, full_query, preferred_element_type=f32)
    key_lin = jnp.dot(normed, full_key, preferred_element_type=f32)
    value_low = jnp.dot(normed, full_value, preferred_element_type=f32).astype(b16)
    query_rot = (rotate(query_lin.reshape(tok_rows, H, HD), places) * score_scale).astype(b16)
    key_rot = (
        rotate(key_lin.reshape(tok_rows, KVH, HD), places).astype(b16).reshape(tok_rows, KVH * HD)
    )
    key_all, value_all = (
        lax.all_gather(key_rot, "dp", axis=0, tiled=True),
        lax.all_gather(value_low, "dp", axis=0, tiled=True),
    )
    key_pos = jnp.arange(seq_len, dtype=jnp.int32)
    visible = (key_pos[None, :] <= query_pos[:, None]) | (key_pos[None, :] < prefix_len[0])

    def head_scores(key_src, head_idx):
        query_head = query_rot[:, head_idx * group_size : (head_idx + 1) * group_size, :]
        key_head = key_src[:, head_idx * HD : (head_idx + 1) * HD]
        scores = jnp.einsum("qgd,kd->gqk", query_head, key_head, preferred_element_type=f32)
        return jnp.where(visible[None, :, :], scores, MASKED_SCORE)

    mixed_heads = []
    log_totals = []
    for head_idx in range(KVH):
        scores = head_scores(key_all, head_idx)
        row_max = jnp.max(scores, axis=-1, keepdims=True)
        log_total = row_max + jnp.log(jnp.sum(jnp.exp(scores - row_max), axis=-1, keepdims=True))
        probs_low = jnp.exp(scores - log_total).astype(b16)
        value_head = value_all[:, head_idx * HD : (head_idx + 1) * HD]
        mixed_heads.append(
            jnp.einsum("gqk,kd->qgd", probs_low, value_head, preferred_element_type=f32)
        )
        log_totals.append(log_total)
    attended = jnp.concatenate(mixed_heads, axis=1).reshape(tok_rows, H * HD).astype(b16)
    residual = in_float + jnp.dot(attended, full_output, preferred_element_type=f32)
    moe_in = rms_norm(residual, full_moe_gain.astype(f32)).astype(b16)
    logits = jnp.dot(moe_in, full_router, preferred_element_type=f32)

    def routed_gates(logit_vals):
        return jax.nn.softmax(jnp.take_along_axis(logit_vals, routes, axis=1), axis=-1)

    gate_weights, gate_pull = jax.vjp(routed_gates, logits)
    slot_index, token_sources, pair_sources = slot_table(routes, priority, EXPERTS, capacity)
    moe_pad = jnp.concatenate([moe_in, jnp.zeros((1, model_width), b16)], axis=0)
    dispatch_buf = moe_pad[token_sources].reshape(EXPERTS, capacity, model_width)
    expert_in = lax.all_to_all(dispatch_buf, "expert", split_axis=0, concat_axis=1, tiled=True)
    gate_proj = jnp.einsum("erd,edf->erf", expert_in, full_gate, preferred_element_type=f32)
    up_proj = jnp.einsum("erd,edf->erf", expert_in, full_up, preferred_element_type=f32)
    activated = (jax.nn.silu(gate_proj) * up_proj).astype(b16)
    expert_out = jnp.einsum(
        "erf,efd->erd", activated, full_down, preferred_element_type=f32
    ).astype(b16)
    returned = lax.all_to_all(expert_out, "expert", split_axis=1, concat_axis=0, tiled=True)
    return_pad = jnp.concatenate(
        [returned.reshape(EXPERTS * capacity, model_width), jnp.zeros((1, model_width), b16)],
        axis=0,
    )
    pair_float = return_pad[slot_index].astype(f32)
    mixture = jnp.sum(gate_weights[:, :, None] * pair_float, axis=1)
    layer_output = (residual + mixture).astype(b16)
    back_attn_gain, back_query, back_key, back_value, back_output = (
        full_attn_gain,
        full_query,
        full_key,
        full_value,
        full_output,
    )
    back_moe_gain, back_router, back_gate, back_up, back_down = (
        full_moe_gain,
        full_router,
        full_gate,
        full_up,
        full_down,
    )
    key_back, value_back = (key_all, value_all)
    grad_out = out_grad.astype(f32)
    gate_grad = jnp.sum(pair_float * grad_out[:, None, :], axis=-1)
    gate_pad = jnp.concatenate([gate_weights.reshape(-1), jnp.zeros((1,), f32)], axis=0)
    grad_pad = jnp.concatenate([grad_out, jnp.zeros((1, model_width), f32)], axis=0)
    slot_grad = (
        (gate_pad[pair_sources][:, None] * grad_pad[token_sources])
        .astype(b16)
        .reshape(EXPERTS, capacity, model_width)
    )
    expert_out_grad = lax.all_to_all(slot_grad, "expert", split_axis=0, concat_axis=1, tiled=True)
    wdown_grad = jnp.einsum("erf,erd->efd", activated, expert_out_grad, preferred_element_type=f32)
    act_grad = jnp.einsum("erd,efd->erf", expert_out_grad, back_down, preferred_element_type=f32)
    swiglu_value, swiglu_pull = jax.vjp(
        lambda gate_in, up_in: jax.nn.silu(gate_in) * up_in, gate_proj, up_proj
    )
    proj_gate_grad, proj_up_grad = swiglu_pull(act_grad)
    proj_gate_grad = proj_gate_grad.astype(b16)
    proj_up_grad = proj_up_grad.astype(b16)
    wgate_grad = jnp.einsum("erd,erf->edf", expert_in, proj_gate_grad, preferred_element_type=f32)
    wup_grad = jnp.einsum("erd,erf->edf", expert_in, proj_up_grad, preferred_element_type=f32)
    rows_grad = (
        jnp.einsum("erf,edf->erd", proj_gate_grad, back_gate, preferred_element_type=f32)
        + jnp.einsum("erf,edf->erd", proj_up_grad, back_up, preferred_element_type=f32)
    ).astype(b16)
    slots_back = lax.all_to_all(rows_grad, "expert", split_axis=1, concat_axis=0, tiled=True)
    back_pad = jnp.concatenate(
        [slots_back.reshape(EXPERTS * capacity, model_width), jnp.zeros((1, model_width), b16)],
        axis=0,
    )
    moe_in_grad = jnp.sum(back_pad[slot_index].astype(f32), axis=1)
    (logit_grad,) = gate_pull(gate_grad)
    logit_low = logit_grad.astype(b16)
    router_grad = jnp.einsum("td,te->de", moe_in, logit_low, preferred_element_type=f32)
    moe_in_grad = moe_in_grad + jnp.einsum(
        "te,de->td", logit_low, back_router, preferred_element_type=f32
    )
    norm_value, second_pull = jax.vjp(rms_norm, residual, back_moe_gain.astype(f32))
    resid_norm_grad, moe_gain_grad = second_pull(moe_in_grad)
    residual_grad = grad_out + resid_norm_grad
    attn_out_grad = residual_grad.astype(b16)
    wout_grad = jnp.einsum("tc,td->cd", attended, attn_out_grad, preferred_element_type=f32)
    attended_grad = (
        jnp.einsum("td,cd->tc", attn_out_grad, back_output, preferred_element_type=f32)
        .astype(b16)
        .reshape(tok_rows, H, HD)
    )
    query_grads = []
    key_grads = []
    value_grads = []
    half_heads = KVH // 2
    for half_idx in range(2):
        key_parts = []
        value_parts = []
        for head_idx in range(half_idx * half_heads, (half_idx + 1) * half_heads):
            scores = head_scores(key_back, head_idx)
            attention_probs = jnp.exp(scores - log_totals[head_idx])
            probs_low = attention_probs.astype(b16)
            grad_head = attended_grad[:, head_idx * group_size : (head_idx + 1) * group_size, :]
            query_head = query_rot[:, head_idx * group_size : (head_idx + 1) * group_size, :]
            key_head = key_back[:, head_idx * HD : (head_idx + 1) * HD]
            value_head = value_back[:, head_idx * HD : (head_idx + 1) * HD]
            probs_grad = jnp.einsum(
                "qgd,kd->gqk", grad_head, value_head, preferred_element_type=f32
            )
            row_delta = jnp.sum(attention_probs * probs_grad, axis=-1, keepdims=True)
            score_grad = (attention_probs * (probs_grad - row_delta)).astype(b16)
            query_grads.append(
                jnp.einsum("gqk,kd->qgd", score_grad, key_head, preferred_element_type=f32)
            )
            key_parts.append(
                jnp.einsum("gqk,qgd->kd", score_grad, query_head, preferred_element_type=f32)
            )
            value_parts.append(
                jnp.einsum("gqk,qgd->kd", probs_low, grad_head, preferred_element_type=f32)
            )
        key_sum, value_sum = (
            lax.psum_scatter(
                jnp.concatenate(key_parts, axis=1), "dp", scatter_dimension=0, tiled=True
            ),
            lax.psum_scatter(
                jnp.concatenate(value_parts, axis=1), "dp", scatter_dimension=0, tiled=True
            ),
        )
        key_grads.append(key_sum)
        value_grads.append(value_sum)
    query_rot_grad = jnp.concatenate(query_grads, axis=1) * score_scale
    key_rot_grad = jnp.concatenate(key_grads, axis=1).reshape(tok_rows, KVH, HD)
    value_grad = jnp.concatenate(value_grads, axis=1).astype(b16)
    query_value, query_pull = jax.vjp(
        lambda vectors: rotate(vectors, places), query_lin.reshape(tok_rows, H, HD)
    )
    (query_grad,) = query_pull(query_rot_grad)
    query_grad = query_grad.reshape(tok_rows, H * HD).astype(b16)
    key_value, key_pull = jax.vjp(
        lambda vectors: rotate(vectors, places), key_lin.reshape(tok_rows, KVH, HD)
    )
    (key_grad,) = key_pull(key_rot_grad)
    key_grad = key_grad.reshape(tok_rows, KVH * HD).astype(b16)
    wq_grad = jnp.einsum("td,tc->dc", normed, query_grad, preferred_element_type=f32)
    wk_grad = jnp.einsum("td,tc->dc", normed, key_grad, preferred_element_type=f32)
    wv_grad = jnp.einsum("td,tc->dc", normed, value_grad, preferred_element_type=f32)
    normed_grad = jnp.einsum("tc,dc->td", query_grad, back_query, preferred_element_type=f32)
    normed_grad = normed_grad + jnp.einsum(
        "tc,dc->td", key_grad, back_key, preferred_element_type=f32
    )
    normed_grad = normed_grad + jnp.einsum(
        "tc,dc->td", value_grad, back_value, preferred_element_type=f32
    )
    first_value, first_pull = jax.vjp(rms_norm, in_float, back_attn_gain.astype(f32))
    input_norm_grad, attn_gain_grad = first_pull(normed_grad)
    input_grad = residual_grad + input_norm_grad
    whole_sums = lax.psum(
        (attn_gain_grad, wq_grad, wk_grad, wv_grad, wout_grad, moe_gain_grad, router_grad), "expert"
    )
    results = (
        lax.psum_scatter(whole_sums[0], "dp", scatter_dimension=0, tiled=True),
        lax.psum_scatter(whole_sums[1], "dp", scatter_dimension=0, tiled=True),
        lax.psum_scatter(whole_sums[2], "dp", scatter_dimension=0, tiled=True),
        lax.psum_scatter(whole_sums[3], "dp", scatter_dimension=0, tiled=True),
        lax.psum_scatter(whole_sums[4], "dp", scatter_dimension=0, tiled=True),
        lax.psum_scatter(whole_sums[5], "dp", scatter_dimension=0, tiled=True),
        lax.psum_scatter(whole_sums[6], "dp", scatter_dimension=0, tiled=True),
        lax.psum_scatter(wgate_grad, "dp", scatter_dimension=1, tiled=True),
        lax.psum_scatter(wup_grad, "dp", scatter_dimension=1, tiled=True),
        lax.psum_scatter(wdown_grad, "dp", scatter_dimension=1, tiled=True),
    )
    return (
        layer_output,
        input_grad,
        results[0],
        results[1],
        results[2],
        results[3],
        results[4],
        results[5],
        results[6],
        results[7],
        results[8],
        results[9],
    )


def solution(mesh):
    placed = (
        P(("expert", "dp"), None),
        P("dp"),
        P("dp", None),
        P("dp", None),
        P("dp", None),
        P("dp", None),
        P("dp"),
        P("dp", None),
        P("expert", "dp", None),
        P("expert", "dp", None),
        P("expert", "dp", None),
        P(("expert", "dp"), None),
        P(("expert", "dp"), None),
        P("expert"),
        P(("expert", "dp"), None),
    )
    return jax.shard_map(
        body,
        mesh=mesh,
        in_specs=placed,
        out_specs=(
            P(("expert", "dp"), None),
            P(("expert", "dp"), None),
            P("dp"),
            P("dp", None),
            P("dp", None),
            P("dp", None),
            P("dp", None),
            P("dp"),
            P("dp", None),
            P("expert", "dp", None),
            P("expert", "dp", None),
            P("expert", "dp", None),
        ),
        check_vma=False,
    )
```

profile of v0, /device:TPU:0, one launch (start us, length us, event | category | flops | bytes accessed | tf_op | source)
XLA Modules:
  0.0 1508.0 jit_solution(9316852701059070005)
XLA Ops:
  10.1 9.6 all-gather
  21.3 17.8 %all-gather.16.cloned.1.call-done = bf16[1024,512]{1,0:T(8,128)(2,1)} async-done(((bf16[256,512]{1,0:T(8,128)(2,1)}), bf16[1024,512]{1,0:T(8,128)(2,1)}) %all-gather.16.cloned.1.call-update) | async-done | bytes 1048592 | tf_op jit(solution)/shard_map/all_gather | solution.py:102
  42.0 25.4 %all-gather.12.cloned.1.call-done = bf16[1024,512]{1,0:T(8,128)(2,1)} async-done(((bf16[256,512]{1,0:T(8,128)(2,1)}), bf16[1024,512]{1,0:T(8,128)(2,1)}) %all-gather.12.cloned.1.call-update) | async-done | bytes 1048592 | tf_op jit(solution)/shard_map/all_gather | solution.py:103
  71.3 8.1 all-gather.1
  79.4 8.0 all_gather.44
  87.9 8.0 scatter_custom_fusion
  96.1 11.8 gather_fusion
  107.9 9.1 reduce-window.6
  117.8 11.8 gather_fusion.1
  130.7 8.1 scatter_custom_fusion.2
  138.8 8.3 scatter_custom_fusion.1
  147.5 8.9 gather_fusion.5
  179.1 20.1 %all-gather.22.cloned.1.call-done = bf16[1024,1024]{1,0:T(8,128)(2,1)} async-done(((bf16[256,1024]{1,0:T(8,128)(2,1)}), bf16[1024,1024]{1,0:T(8,128)(2,1)}) %all-gather.22.cloned.1.call-update) | async-done | bytes 2097168 | tf_op jit(solution)/shard_map/all_gather | solution.py:104
  203.1 16.8 %gather_fusion.7 = f32[2048]{0:T(1024)S(1)} fusion(f32[256,32]{0,1:T(8,128)S(1)} %fusion.199, s32[2048]{0:T(1024)S(1)} %reshape.491), kind=kCustom, calls=%fused_computation.7 | custom fusion | bytes 32768 | tf_op jit(solution)/shard_map/jvp(jit(take_along_axis))/gather | solution.py:165
  220.4 13.6 gather_fusion.4
  234.1 7.0 multiply_convert_fusion
  241.1 4.6 all-to-all-start.2
  247.3 8.8 gather_fusion.2
  256.2 106.1 %all-to-all-done.2 = bf16[32,80,1024]{2,1,0:T(8,128)(2,1)} async-done(((bf16[32,80,1024]{2,1,0:T(8,128)(2,1)}), bf16[32,80,1024]{2,1,0:T(8,128)(2,1)}, u32[]{:S(2)}, u32[]{:S(2)}) %all-to-all-start.2) | async-done | bytes 5242912 | tf_op jit(solution)/shard_map/all_to_all | solution.py:210
  362.3 4.7 all-to-all-start
  367.7 5.7 copy.416
  373.4 110.0 %all-to-all-done = bf16[32,80,1024]{2,1,0:T(8,128)(2,1)} async-done(((bf16[32,80,1024]{2,1,0:T(8,128)(2,1)}), bf16[32,80,1024]{2,1,0:T(8,128)(2,1)}, u32[]{:S(2)}, u32[]{:S(2)}) %all-to-all-start) | async-done | bytes 5242912 | tf_op jit(solution)/shard_map/all_to_all | solution.py:171
  483.4 5.7 copy.409
  489.1 8.9 fusion.200
  498.1 8.9 fusion.201
  507.0 11.8 multiply_convert_fusion.1
  518.8 3.1 convolution_convert_fusion
  521.9 6.3 copy.410
  528.2 4.9 all-to-all-start.1
  533.1 5.5 fusion.202
  538.6 8.4 add_convert_fusion
  547.0 8.8 copy.417
  555.9 93.7 %all-to-all-done.1 = bf16[4,640,1024]{2,0,1:T(4,128)(2,1)} async-done(((bf16[4,640,1024]{2,0,1:T(4,128)(2,1)}), bf16[4,640,1024]{2,0,1:T(4,128)(2,1)}, u32[]{:S(2)}, u32[]{:S(2)}) %all-to-all-start.1) | async-done | bytes 5242912 | tf_op jit(solution)/shard_map/all_to_all | solution.py:178
  649.5 4.7 all-to-all-start.3
  655.1 4.4 copy.411
  659.5 2.8 concatenate.52
  662.3 14.5 gather_fusion.3
  676.9 6.2 fusion.1
  683.4 11.3 scatter_custom_fusion.3
  694.7 75.9 %all-to-all-done.3 = bf16[4,640,1024]{2,0,1:T(4,128)(2,1)} async-done(((bf16[4,640,1024]{2,0,1:T(4,128)(2,1)}), bf16[4,640,1024]{2,0,1:T(4,128)(2,1)}, u32[]{:S(2)}, u32[]{:S(2)}) %all-to-all-start.3) | async-done | bytes 5242912 | tf_op jit(solution)/shard_map/all_to_all | solution.py:225
  770.6 4.4 copy.418
  775.1 2.9 concatenate.55
  777.9 14.3 gather_fusion.6
  792.3 5.5 convert_reduce_fusion
  831.3 6.0 fusion.6
  837.3 5.0 fusion.11
  842.8 2.9 fusion.8
  855.0 14.7 reduce-scatter.19.cloned.1.call-done
  872.8 27.6 %reduce-scatter.13.cloned.1.call-done = f32[256,256]{0,1:T(8,128)} async-done(((f32[1024,256]{0,1:T(8,128)}), f32[256,256]{0,1:T(8,128)}) %reduce-scatter.13.cloned.1.call-update) | async-done | bytes 262160 | tf_op jit(solution)/shard_map/reduce_scatter | solution.py:277
  900.4 31.4 %reduce-scatter.15.cloned.1.call-done = f32[256,256]{0,1:T(8,128)} async-done(((f32[1024,256]{0,1:T(8,128)}), f32[256,256]{0,1:T(8,128)}) %reduce-scatter.15.cloned.1.call-update) | async-done | bytes 262160 | tf_op jit(solution)/shard_map/reduce_scatter | solution.py:277
  943.0 2.9 fusion.191
  951.6 10.0 fusion.206
  963.4 9.0 fusion.204
  974.1 9.0 fusion.205
  983.6 24.3 %reduce-scatter.29.cloned.1.call-done = f32[256,512]{1,0:T(8,128)} async-done(((f32[1024,512]{1,0:T(8,128)}), f32[256,512]{1,0:T(8,128)}) %reduce-scatter.29.cloned.1.call-update) | async-done | bytes 524304 | tf_op jit(solution)/shard_map/reduce_scatter | solution.py:318
  1007.9 55.4 %reduce-scatter.27.cloned.1.call-done = f32[256,1024]{1,0:T(8,128)} async-done(((f32[1024,1024]{1,0:T(8,128)}), f32[256,1024]{1,0:T(8,128)}) %reduce-scatter.27.cloned.1.call-update) | async-done | bytes 1048592 | tf_op jit(solution)/shard_map/reduce_scatter | solution.py:317
  1063.3 55.4 %reduce-scatter.33.cloned.1.call-done = f32[256,1024]{1,0:T(8,128)} async-done(((f32[1024,1024]{1,0:T(8,128)}), f32[256,1024]{1,0:T(8,128)}) %reduce-scatter.33.cloned.1.call-update) | async-done | bytes 1048592 | tf_op jit(solution)/shard_map/reduce_scatter | solution.py:320
  1123.3 9.1 all-reduce.12
  1132.6 13.6 reduce-scatter.35.cloned.1.call-done
  1146.1 28.9 %all-reduce.10 = (f32[256]{0:T(256)}, f32[256]{0:T(256)}, f32[256,32]{0,1:T(8,128)}) all-reduce(f32[256]{0:T(256)S(1)} %dynamic-slice.1, f32[256]{0:T(256)S(1)} %dynamic-slice.3, f32[256,32]{0,1:T(8,128)} %reduce-scatter.35.cloned.1.call-done), channel_id=1, replica_groups=mesh['expert'=8,'dp'=4] {'expert'}, use_global_device_ids=true, to_apply=%region_46.47 | all-reduce | flops 8704 | bytes 69632 | tf_op jit(solution)/shard_map/psum | solution.py:312
  1176.3 59.8 %reduce-scatter.25.cloned.1.call-done = f32[4,128,1024]{2,1,0:T(8,128)} async-done(((f32[4,512,1024]{2,1,0:T(8,128)}), f32[4,128,1024]{2,1,0:T(8,128)}) %reduce-scatter.25.cloned.1.call-update) | async-done | bytes 2097168 | tf_op jit(solution)/shard_map/reduce_scatter | solution.py:325
  1236.1 89.8 %reduce-scatter.21.cloned.1.call-done = f32[4,256,512]{2,1,0:T(8,128)} async-done(((f32[4,1024,512]{2,1,0:T(8,128)}), f32[4,256,512]{2,1,0:T(8,128)}) %reduce-scatter.21.cloned.1.call-update) | async-done | bytes 2097168 | tf_op jit(solution)/shard_map/reduce_scatter | solution.py:323
  1326.0 90.0 %reduce-scatter.23.cloned.1.call-done = f32[4,256,512]{2,1,0:T(8,128)} async-done(((f32[4,1024,512]{2,1,0:T(8,128)}), f32[4,256,512]{2,1,0:T(8,128)}) %reduce-scatter.23.cloned.1.call-update) | async-done | bytes 2097168 | tf_op jit(solution)/shard_map/reduce_scatter | solution.py:324
  1416.0 79.6 %all-reduce.15.cloned.1.call-done = (f32[256,1024]{1,0:T(8,128)}, f32[256,512]{1,0:T(8,128)}, f32[256,512]{1,0:T(8,128)}, f32[256,1024]{1,0:T(8,128)}) async-done(((f32[256,1024]{1,0:T(8,128)}, f32[256,512]{1,0:T(8,128)}, f32[256,512]{1,0:T(8,128)}, f32[256,1024]{1,0:T(8,128)}), (f32[256,1024]{1,0:T(8,128)}, f32[256,512]{1,0:T(8,128)}, f32[256,512]{1,0:T(8,128)}, ...) | async-done | bytes 3145744 | tf_op jit(solution)/shard_map/psum | solution.py:312
  (466 shorter events, 119.8 us)
Async XLA Ops:
  7.2 31.9 %all-gather.16.cloned.1.call-start = ((), (), s32[]{:S(2)}) async-start(), calls=%async_computation.18 | async-start | bytes 1310720 | tf_op jit(solution)/shard_map/all_gather | solution.py:102
  7.9 59.5 %all-gather.12.cloned.1.call-start = ((), (), s32[]{:S(2)}) async-start(), calls=%async_computation.16 | async-start | bytes 1310720 | tf_op jit(solution)/shard_map/all_gather | solution.py:103
  8.7 147.7 %all-gather.20.cloned.1.call-start = ((), (), s32[]{:S(2)}) async-start(), calls=%async_computation.20 | async-start | bytes 2621440 | tf_op jit(solution)/shard_map/all_gather | solution.py:101
  9.4 149.9 %all-gather.18.cloned.1.call-start = ((), (), s32[]{:S(2)}) async-start(), calls=%async_computation.19 | async-start | bytes 1310720 | tf_op jit(solution)/shard_map/all_gather | solution.py:135
  19.7 136.7 %copy-start.84 = (f32[4,1,256]{2,1,0:T(1,128)}, f32[4,1,256]{2,1,0:T(1,128)S(1)}, u32[]{:S(2)}) copy-start(f32[4,1,256]{2,1,0:T(1,128)S(1)} %convert_element_type.204) | copy-start | bytes 12292
  19.7 47.8 %copy-start.20 = (bf16[256,1024]{1,0:T(8,128)(2,1)S(1)}, bf16[256,1024]{1,0:T(8,128)(2,1)}, u32[]{:S(2)}) copy-start(bf16[256,1024]{1,0:T(8,128)(2,1)} %param.15) | copy-start | bytes 1572868
  21.0 20.1 %copy-start.114 = (f32[256]{0:T(256)}, f32[256]{0:T(256)S(1)}, u32[]{:S(2)}) copy-start(f32[256]{0:T(256)S(1)} %fusion.76) | copy-start | bytes 3076
  21.0 135.3 %copy-start.92 = (f32[256]{0:T(256)}, f32[256]{0:T(256)S(1)}, u32[]{:S(2)}) copy-start(f32[256]{0:T(256)S(1)} %fusion.167) | copy-start | bytes 3076
  21.2 137.8 %copy-start.76 = (f32[256,32]{0,1:T(8,128)}, f32[256,32]{0,1:T(8,128)S(1)}, u32[]{:S(2)}) copy-start(f32[256,32]{0,1:T(8,128)S(1)} %get-tuple-element.77) | copy-start | bytes 98308
  21.2 137.8 %copy-start.78 = (f32[256,32]{0,1:T(8,128)}, f32[256,32]{0,1:T(8,128)S(1)}, u32[]{:S(2)}) copy-start(f32[256,32]{0,1:T(8,128)S(1)} %get-tuple-element.78) | copy-start | bytes 98308
  41.2 29.3 %copy-start.88 = (s32[256,8]{0,1:T(8,128)S(1)}, s32[256,8]{0,1:T(8,128)}, u32[]{:S(2)}) copy-start(s32[256,8]{0,1:T(8,128)} %param.26) | copy-start | bytes 24580
  41.2 30.1 %copy-start.122 = (bf16[256]{0:T(256)(128)(2,1)S(1)}, bf16[256]{0:T(256)(128)(2,1)}, u32[]{:S(2)}) copy-start(bf16[256]{0:T(256)(128)(2,1)} %param.21) | copy-start | bytes 1540
  41.2 38.2 %copy-start.111 = (bf16[256,32]{0,1:T(8,128)(2,1)S(1)}, bf16[256,32]{0,1:T(8,128)(2,1)}, u32[]{:S(2)}) copy-start(bf16[256,32]{0,1:T(8,128)(2,1)} %param.22) | copy-start | bytes 49156
  41.2 46.4 %copy-start.118 = (s32[256,8]{0,1:T(8,128)S(1)}, s32[256,8]{0,1:T(8,128)}, u32[]{:S(2)}) copy-start(s32[256,8]{0,1:T(8,128)} %param.27) | copy-start | bytes 24580
  42.0 126.9 %all-gather.14.cloned.1.call-start = ((), (), s32[]{:S(2)}) async-start(), calls=%async_computation.17 | async-start | bytes 1310720 | tf_op jit(solution)/shard_map/all_gather | solution.py:136
  69.9 129.4 %all-gather.22.cloned.1.call-start = ((), (), s32[]{:S(2)}) async-start(), calls=%async_computation.21 | async-start | bytes 2621440 | tf_op jit(solution)/shard_map/all_gather | solution.py:104
  79.4 122.3 %copy-start.90 = (f32[4,1,256]{2,1,0:T(1,128)}, f32[4,1,256]{2,1,0:T(1,128)S(1)}, u32[]{:S(2)}) copy-start(f32[4,1,256]{2,1,0:T(1,128)S(1)} %convert_element_type.205) | copy-start | bytes 12292
  87.4 115.4 %copy-start.80 = (bf16[1024,32]{0,1:T(8,128)(2,1)}, bf16[1024,32]{0,1:T(8,128)(2,1)S(1)}, u32[]{:S(2)}) copy-start(bf16[1024,32]{0,1:T(8,128)(2,1)S(1)} %all_gather.44) | copy-start | bytes 196612
  117.8 29.5 %copy-start.58 = (bf16[256,1024]{1,0:T(8,128)(2,1)S(1)}, bf16[256,1024]{1,0:T(8,128)(2,1)}, u32[]{:S(2)}) copy-start(bf16[256,1024]{1,0:T(8,128)(2,1)} %param.29) | copy-start | bytes 1572868
  147.3 31.0 %copy-start.30 = (pred[256,1024]{0,1:T(8,128)(4,1)}, pred[256,1024]{0,1:T(8,128)(4,1)S(1)}, u32[]{:S(2)}) copy-start(pred[256,1024]{0,1:T(8,128)(4,1)S(1)} %fusion.79) | copy-start | bytes 786436
  161.9 14.3 copy-start
  168.7 7.5 copy-start.97
  168.7 8.1 copy-start.95
  168.8 9.5 copy-start.103
  179.1 22.5 %copy-start.68 = (bf16[256,16,64]{0,2,1:T(8,128)(2,1)}, bf16[256,16,64]{0,2,1:T(8,128)(2,1)S(1)}, u32[]{:S(2)}) copy-start(bf16[256,16,64]{0,2,1:T(8,128)(2,1)S(1)} %fusion.71) | copy-start | bytes 1572868
  201.7 18.2 %copy-start.116 = (f32[256]{0:T(256)}, f32[256]{0:T(256)S(1)}, u32[]{:S(2)}) copy-start(f32[256]{0:T(256)S(1)} %get-tuple-element.81) | copy-start | bytes 3076
  201.7 18.2 %copy-start.112 = (f32[256]{0:T(256)}, f32[256]{0:T(256)S(1)}, u32[]{:S(2)}) copy-start(f32[256]{0:T(256)S(1)} %fusion.168) | copy-start | bytes 3076
  202.8 44.4 %copy-start.50 = (bf16[256,1024]{1,0:T(8,128)(2,1)}, bf16[256,1024]{1,0:T(8,128)(2,1)S(1)}, u32[]{:S(2)}) copy-start(bf16[256,1024]{1,0:T(8,128)(2,1)S(1)} %multiply_convert_fusion.3) | copy-start | bytes 1572868
  241.1 121.2 %all-to-all-start.2 = ((bf16[32,80,1024]{2,1,0:T(8,128)(2,1)}), bf16[32,80,1024]{2,1,0:T(8,128)(2,1)}, u32[]{:S(2)}, u32[]{:S(2)}) async-start(bf16[32,80,1024]{2,1,0:T(8,128)(2,1)} %multiply_convert_fusion), calls=%async_computation.2 | async-start | bytes 10485760 | tf_op jit(solution)/shard_map/all_to_all | solution.py:210
  245.8 243.4 %all-gather.24.cloned.1.call-start = ((), (), s32[]{:S(2)}) async-start(), calls=%async_computation.22 | async-start | bytes 5242880 | tf_op jit(solution)/shard_map/all_gather | solution.py:107
  246.5 251.5 %all-gather.26.cloned.1.call-start = ((), (), s32[]{:S(2)}) async-start(), calls=%async_computation.23 | async-start | bytes 5242880 | tf_op jit(solution)/shard_map/all_gather | solution.py:108
  362.3 121.1 %all-to-all-start = ((bf16[32,80,1024]{2,1,0:T(8,128)(2,1)}), bf16[32,80,1024]{2,1,0:T(8,128)(2,1)}, u32[]{:S(2)}, u32[]{:S(2)}) async-start(bf16[32,80,1024]{2,1,0:T(8,128)(2,1)} %bitcast.503), calls=%async_computation | async-start | bytes 10485760 | tf_op jit(solution)/shard_map/all_to_all | solution.py:171
  366.9 140.0 %all-gather.28.cloned.1.call-start = ((), (), s32[]{:S(2)}) async-start(), calls=%async_computation.24 | async-start | bytes 5242880 | tf_op jit(solution)/shard_map/all_gather | solution.py:109
  507.0 11.8 copy-start.121
  528.2 121.3 %all-to-all-start.1 = ((bf16[4,640,1024]{2,0,1:T(4,128)(2,1)}), bf16[4,640,1024]{2,0,1:T(4,128)(2,1)}, u32[]{:S(2)}, u32[]{:S(2)}) async-start(bf16[4,640,1024]{2,0,1:T(4,128)(2,1)} %copy.410), calls=%async_computation.1 | async-start | bytes 10485760 | tf_op jit(solution)/shard_map/all_to_all | solution.py:178
  555.8 98.4 %copy-start.59 = (bf16[256,1024]{1,0:T(8,128)(2,1)S(1)}, bf16[256,1024]{1,0:T(8,128)(2,1)}, u32[]{:S(2)}) copy-start(bf16[256,1024]{1,0:T(8,128)(2,1)} %param.29) | copy-start | bytes 1572868
  555.8 98.5 %copy-start.94 = (s32[256,8]{0,1:T(8,128)S(1)}, s32[256,8]{0,1:T(8,128)}, u32[]{:S(2)}) copy-start(s32[256,8]{0,1:T(8,128)} %get-tuple-element.75) | copy-start | bytes 24580
  555.8 98.8 %copy-start.89 = (s32[256,8,1]{0,1,2:T(8,128)S(1)}, s32[256,8,1]{0,1,2:T(8,128)}, u32[]{:S(2)}) copy-start(s32[256,8,1]{0,1,2:T(8,128)} %get-tuple-element.74) | copy-start | bytes 24580
  555.8 98.8 %copy-start.120 = (s32[2]{0:T(128)S(1)}, s32[2]{0:T(128)}, u32[]{:S(2)}) copy-start(s32[2]{0:T(128)} %constant.116) | copy-start | bytes 28
  555.9 98.9 %copy-start.119 = (s32[2]{0:T(128)S(1)}, s32[2]{0:T(128)}, u32[]{:S(2)}) copy-start(s32[2]{0:T(128)} %constant.119) | copy-start | bytes 28
  649.5 121.1 %all-to-all-start.3 = ((bf16[4,640,1024]{2,0,1:T(4,128)(2,1)}), bf16[4,640,1024]{2,0,1:T(4,128)(2,1)}, u32[]{:S(2)}, u32[]{:S(2)}) async-start(bf16[4,640,1024]{2,0,1:T(4,128)(2,1)} %copy.417), calls=%async_computation.3 | async-start | bytes 10485760 | tf_op jit(solution)/shard_map/all_to_all | solution.py:225
  654.2 199.8 %reduce-scatter.17.cloned.1.call-start = ((), (), s32[]{:S(2)}) async-start(), calls=%async_computation.27 | async-start | bytes 1310720 | tf_op jit(solution)/shard_map/reduce_scatter | solution.py:280
  694.7 103.1 %copy-start.86 = (bf16[32,256]{1,0:T(8,128)(2,1)}, bf16[32,256]{1,0:T(8,128)(2,1)S(1)}, u32[]{:S(2)}) copy-start(bf16[32,256]{1,0:T(8,128)(2,1)S(1)} %reshape.434) | copy-start | bytes 49156
  800.3 145.7 %copy-start.34 = (f32[256,1024]{1,0:T(8,128)}, f32[256,1024]{1,0:T(8,128)S(1)}, u32[]{:S(2)}) copy-start(f32[256,1024]{1,0:T(8,128)S(1)} %get-tuple-element.60) | copy-start | bytes 3145732
  812.8 56.9 %reduce-scatter.19.cloned.1.call-start = ((), (), s32[]{:S(2)}) async-start(), calls=%async_computation.28 | async-start | bytes 1310720 | tf_op jit(solution)/shard_map/reduce_scatter | solution.py:280
  821.2 79.2 %reduce-scatter.13.cloned.1.call-start = ((), (), s32[]{:S(2)}) async-start(), calls=%async_computation.25 | async-start | bytes 1310720 | tf_op jit(solution)/shard_map/reduce_scatter | solution.py:277
  848.4 83.4 %reduce-scatter.15.cloned.1.call-start = ((), (), s32[]{:S(2)}) async-start(), calls=%async_computation.26 | async-start | bytes 1310720 | tf_op jit(solution)/shard_map/reduce_scatter | solution.py:277
  852.8 17.8 %copy-start.21 = (bf16[256,1024]{1,0:T(8,128)(2,1)S(1)}, bf16[256,1024]{1,0:T(8,128)(2,1)}, u32[]{:S(2)}) copy-start(bf16[256,1024]{1,0:T(8,128)(2,1)} %param.15) | copy-start | bytes 1572868
  852.8 17.8 %copy-start.85 = (f32[4,1,256]{2,1,0:T(1,128)S(1)}, f32[4,1,256]{2,1,0:T(1,128)}, u32[]{:S(2)}) copy-start(f32[4,1,256]{2,1,0:T(1,128)} %copy-done.84) | copy-start | bytes 12292
  852.9 17.8 %copy-start.93 = (f32[256]{0:T(256)S(1)}, f32[256]{0:T(256)}, u32[]{:S(2)}) copy-start(f32[256]{0:T(256)} %copy-done.92) | copy-start | bytes 3076
  853.9 129.6 %reduce-scatter.31.cloned.1.call-start = ((), (), s32[]{:S(2)}) async-start(), calls=%async_computation.34 | async-start | bytes 2621440 | tf_op jit(solution)/shard_map/reduce_scatter | solution.py:319
  872.7 135.1 %reduce-scatter.29.cloned.1.call-start = ((), (), s32[]{:S(2)}) async-start(), calls=%async_computation.33 | async-start | bytes 2621440 | tf_op jit(solution)/shard_map/reduce_scatter | solution.py:318
  935.7 127.6 %reduce-scatter.27.cloned.1.call-start = ((), (), s32[]{:S(2)}) async-start(), calls=%async_computation.32 | async-start | bytes 5242880 | tf_op jit(solution)/shard_map/reduce_scatter | solution.py:317
  945.9 172.8 %reduce-scatter.33.cloned.1.call-start = ((), (), s32[]{:S(2)}) async-start(), calls=%async_computation.35 | async-start | bytes 5242880 | tf_op jit(solution)/shard_map/reduce_scatter | solution.py:320
  949.7 196.5 %reduce-scatter.35.cloned.1.call-start = ((), (), s32[]{:S(2)}) async-start(), calls=%async_computation.36 | async-start | bytes 163840 | tf_op jit(solution)/shard_map/reduce_scatter | solution.py:322
  951.6 284.5 %reduce-scatter.25.cloned.1.call-start = ((), (), s32[]{:S(2)}) async-start(), calls=%async_computation.31 | async-start | bytes 10485760 | tf_op jit(solution)/shard_map/reduce_scatter | solution.py:325
  961.7 364.3 %reduce-scatter.21.cloned.1.call-start = ((), (), s32[]{:S(2)}) async-start(), calls=%async_computation.29 | async-start | bytes 10485760 | tf_op jit(solution)/shard_map/reduce_scatter | solution.py:323
  972.4 443.5 %reduce-scatter.23.cloned.1.call-start = ((), (), s32[]{:S(2)}) async-start(), calls=%async_computation.30 | async-start | bytes 10485760 | tf_op jit(solution)/shard_map/reduce_scatter | solution.py:324
  983.2 135.6 %copy-start.123 = (u32[32]{0:T(128)S(1)}, u32[32]{0:T(128)}, u32[]{:S(2)}) copy-start(u32[32]{0:T(128)} %constant.139) | copy-start | bytes 388
  983.2 136.9 %copy-start.48 = (bf16[1024,1024]{1,0:T(8,128)(2,1)S(1)}, bf16[1024,1024]{1,0:T(8,128)(2,1)}, u32[]{:S(2)}) copy-start(bf16[1024,1024]{1,0:T(8,128)(2,1)} %all-gather.20.cloned.1.call-done) | copy-start | bytes 6291460
  983.2 136.9 %copy-start.54 = (bf16[256,16,64]{0,2,1:T(8,128)(2,1)S(1)}, bf16[256,16,64]{0,2,1:T(8,128)(2,1)}, u32[]{:S(2)}) copy-start(bf16[256,16,64]{0,2,1:T(8,128)(2,1)} %copy-done.53) | copy-start | bytes 1572868
  983.2 512.4 %all-reduce.15.cloned.1.call-start = ((), (), s32[]{:S(2)}) async-start(), calls=%async_computation.37 | async-start | bytes 6291456 | tf_op jit(solution)/shard_map/psum | solution.py:312
  1122.6 52.4 %copy-start.115 = (f32[256]{0:T(256)S(1)}, f32[256]{0:T(256)}, u32[]{:S(2)}) copy-start(f32[256]{0:T(256)} %copy-done.114) | copy-start | bytes 3076
  1122.6 52.4 %copy-start.35 = (f32[256,1024]{1,0:T(8,128)S(1)}, f32[256,1024]{1,0:T(8,128)}, u32[]{:S(2)}) copy-start(f32[256,1024]{1,0:T(8,128)} %copy-done.34) | copy-start | bytes 3145732
  (86 other events, 239.7 us)
Sparse Core Ops, SparseCore 0:
  9.8 29.2 all-gather.15
  40.9 26.4 all-gather.11
  69.3 35.5 all-gather.19
  107.1 26.3 all-gather.17
  135.8 26.4 all-gather.13
  164.0 35.1 all-gather.21
  248.4 52.9 all-gather.23
  303.3 52.5 all-gather.25
  369.6 52.9 all-gather.27
  812.9 25.8 reduce-scatter.16
  841.7 27.9 reduce-scatter.18
  872.4 27.9 reduce-scatter.12
  903.9 27.9 reduce-scatter.14
  934.6 35.1 reduce-scatter.30
  972.7 35.1 reduce-scatter.28
  1010.7 52.5 reduce-scatter.26
  1066.1 52.5 reduce-scatter.32
  1121.9 24.1 reduce-scatter.34
  1149.8 86.3 reduce-scatter.24
  1239.6 86.3 reduce-scatter.20
  1329.6 86.3 reduce-scatter.22
  1418.6 76.9 all-reduce.14
where the time goes:
time: 1520 us; the launch traced here: 1510 us
  waiting for transfers between devices  995 us (65%)
  local copies, waits for them, and re-layouts  192 us (13%)
  matrix products  152 us (10%)
  other arithmetic  64.8 us (4%)
  blocking collectives  63.6 us (4%)
  starting transfers between devices  21 us (1%)
  between operations  18.3 us (1%)
    all_to_all x1, waiting for transfers between devices, body(): lax.all_to_all(dispatch_buf, 'expert', split_axis=0, concat_axis=1, tiled...  110 us
    all_to_all x1, waiting for transfers between devices, body(): lax.all_to_all(slot_grad, 'expert', split_axis=0, concat_axis=1, tiled=True)  106 us
    all_to_all x1, waiting for transfers between devices, body(): lax.all_to_all(expert_out, 'expert', split_axis=1, concat_axis=0, tiled=T...  93.7 us
    reduce_scatter x1, waiting for transfers between devices, body(): lax.psum_scatter(wup_grad, 'dp', scatter_dimension=1, tiled=True)  90 us
    reduce_scatter x1, waiting for transfers between devices, body(): lax.psum_scatter(wgate_grad, 'dp', scatter_dimension=1, tiled=True)  89.8 us
    psum x1, waiting for transfers between devices, body(): lax.psum((attn_gain_grad, wq_grad, wk_grad, wv_grad, wout_grad, moe_gain_...  79.6 us
    all_to_all x1, waiting for transfers between devices, body(): lax.all_to_all(rows_grad, 'expert', split_axis=1, concat_axis=0, tiled=True)  75.9 us
    reduce_scatter x1, waiting for transfers between devices, body(): lax.psum_scatter(wdown_grad, 'dp', scatter_dimension=1, tiled=True)  59.8 us
  transfers between devices with their start and end apart: 26, of which 18 were waited for; matrix products, arithmetic and copies ran while one was open for 19% of the time, Pallas kernels for 0%

commit v1 on v0

v1 whole, which is shorter than its diff:
```python
import math

import jax
import jax.numpy as jnp
from jax import lax
from jax.experimental import pallas as pl
from jax.experimental.pallas import tpu as pltpu
from jax.sharding import Mesh
from jax.sharding import PartitionSpec as P

H = 16
KVH = 8
HD = 64
EXPERTS = 32
EPSILON = 1e-06
ROPE_BASE = 10000.0
MASKED_SCORE = -1e30
F32 = jnp.float32
B16 = jnp.bfloat16
SWAP = [(0, 1), (1, 0)]
VMEM_LIMIT = 60 * 1024 * 1024


def rms_norm(values, gain_vec):
    return (
        values * lax.rsqrt(jnp.mean(values * values, axis=-1, keepdims=True) + EPSILON) * gain_vec
    )


def rotate(vectors, places):
    half_dim = vectors.shape[-1] // 2
    frequency = jnp.exp(
        jnp.arange(half_dim, dtype=F32) * (-2.0 * math.log(ROPE_BASE) / vectors.shape[-1])
    )
    angles = places[:, None] * frequency[None, :]
    cosine = jnp.cos(angles)[:, None, :]
    sine_vals = jnp.sin(angles)[:, None, :]
    first_half = vectors[..., :half_dim]
    second = vectors[..., half_dim:]
    return jnp.concatenate(
        [first_half * cosine - second * sine_vals, second * cosine + first_half * sine_vals],
        axis=-1,
    )


def swap_core(rows):
    return lax.ppermute(rows, "core", SWAP)


def cyclic(rows, size, shift):
    return lax.ppermute(rows, "z", [(i, (i + shift) % size) for i in range(size)])


def after(value, *others):
    return lax.optimization_barrier((value, *others))[0]


def grid_gather(shard):
    half = shard.shape[0] // 2
    from_x = lax.ppermute(shard, "x", SWAP)
    from_y = lax.ppermute(shard, "y", SWAP)
    diag_a = lax.ppermute(from_x[:half], "y", SWAP)
    diag_b = lax.ppermute(from_y[half:], "x", SWAP)
    return shard, from_x, from_y, diag_a, diag_b


def grid_scatter(first_a, rest_a, first_b, rest_b):
    got_a = lax.ppermute(first_a, "x", SWAP)
    got_b = lax.ppermute(first_b, "y", SWAP)
    onward_a = (rest_a[1].astype(F32) + got_a[1].astype(F32)).astype(B16)
    onward_b = (rest_b[1].astype(F32) + got_b[1].astype(F32)).astype(B16)
    last_a = lax.ppermute(onward_a, "y", SWAP)
    last_b = lax.ppermute(onward_b, "x", SWAP)
    return (
        rest_a[0].astype(F32) + got_a[0].astype(F32) + last_a.astype(F32),
        rest_b[0].astype(F32) + got_b[0].astype(F32) + last_b.astype(F32),
    )


def grid_scatter_rows(parts):
    own, to_x, to_y, diag = parts
    half = own.shape[0] // 2
    total = grid_scatter(
        jnp.stack([to_x[:half], diag[:half]]),
        (own[:half], to_y[:half]),
        jnp.stack([to_y[half:], diag[half:]]),
        (own[half:], to_x[half:]),
    )
    return jnp.concatenate(total, axis=0)


def column_gather(rows, size):
    mine = jnp.stack([rows] + [cyclic(rows, size, -k) for k in range(1, size)])
    return mine, swap_core(mine)


def column_scatter(mine, other, size):
    both = mine.astype(F32) + swap_core(other).astype(F32)
    low = both.astype(B16)
    total = both[0]
    for k in range(1, size):
        total = total + cyclic(low[k], size, k).astype(F32)
    return total


def assemble(places, parts, blocks):
    rows = blocks
    cols = parts[0].shape[1]

    def kernel(places_ref, *refs):
        out = refs[len(parts)]
        sems = refs[len(parts) + 1]
        copies = []
        for i, part in enumerate(parts):
            start = pl.multiple_of(places_ref[i] * rows, rows)
            copies.append(
                pltpu.make_async_copy(
                    refs[i], out.at[pl.ds(start, part.shape[0]), :], sems.at[i]
                )
            )
        for copy in copies:
            copy.start()
        for copy in copies:
            copy.wait()

    total = sum(part.shape[0] for part in parts)
    return pl.pallas_call(
        kernel,
        out_shape=jax.ShapeDtypeStruct((total, cols), parts[0].dtype),
        grid_spec=pltpu.PrefetchScalarGridSpec(
            num_scalar_prefetch=1,
            grid=(1,),
            in_specs=[pl.BlockSpec(memory_space=pl.ANY) for _ in parts],
            out_specs=pl.BlockSpec(memory_space=pl.ANY),
            scratch_shapes=[pltpu.SemaphoreType.DMA((len(parts),))],
        ),
        name="assemble",
    )(places, *parts)


def one_hot_slots(codes, capacity):
    slots = lax.broadcasted_iota(jnp.int32, (capacity, codes.shape[1]), 0).astype(F32)
    return [(slots == codes[e : e + 1, :]).astype(F32) for e in range(codes.shape[0])]


def row_of(table, index):
    at = lax.broadcasted_iota(jnp.int32, table.shape, 0)
    return jnp.sum(jnp.where(at == index, table, 0.0), axis=0, keepdims=True)


def dispatch_rows(ids, rows, code, router, local, capacity):
    pieces, tokens, width = rows.shape
    slots = local * capacity
    with_gates = router is not None

    def kernel(ids_ref, rows_ref, code_ref, *rest):
        table = code_ref[0]
        first = ids_ref[pieces]
        codes = jnp.concatenate([row_of(table, first + e) for e in range(local)], axis=0)
        picks = one_hot_slots(codes, capacity)
        select = jnp.concatenate([p.astype(B16) for p in picks], axis=0)
        out_ref = rest[1] if with_gates else rest[0]
        out_ref[0] = jnp.dot(select, rows_ref[0], preferred_element_type=F32).astype(B16)
        if with_gates:
            router_ref, gate_out = rest[0], rest[2]
            logits = lax.dot_general(
                router_ref[...], rows_ref[0], (((1,), (1,)), ((), ())), preferred_element_type=F32
            )
            routed = table >= 0.0
            peak = jnp.max(jnp.where(routed, logits, MASKED_SCORE), axis=0, keepdims=True)
            lifted = jnp.where(routed, jnp.exp(jnp.minimum(logits - peak, 0.0)), 0.0)
            gates = lifted / jnp.sum(lifted, axis=0, keepdims=True)
            for e in range(local):
                gate_row = row_of(gates, first + e)
                column = jnp.sum(picks[e] * gate_row, axis=1, keepdims=True)
                gate_out[0, e * capacity : (e + 1) * capacity, :] = jnp.broadcast_to(
                    column, (capacity, 128)
                )

    in_specs = [
        pl.BlockSpec((1, tokens, width), lambda p, ids: (p, 0, 0)),
        pl.BlockSpec((1, EXPERTS, tokens), lambda p, ids: (ids[p], 0, 0)),
    ]
    out_specs = [pl.BlockSpec((1, slots, width), lambda p, ids: (p, 0, 0))]
    out_shape = [jax.ShapeDtypeStruct((pieces, slots, width), B16)]
    args = [rows, code]
    if with_gates:
        in_specs.append(pl.BlockSpec((EXPERTS, width), lambda p, ids: (0, 0)))
        out_specs.append(pl.BlockSpec((1, slots, 128), lambda p, ids: (p, 0, 0)))
        out_shape.append(jax.ShapeDtypeStruct((pieces, slots, 128), F32))
        args.append(router)
    return pl.pallas_call(
        kernel,
        out_shape=out_shape,
        grid_spec=pltpu.PrefetchScalarGridSpec(
            num_scalar_prefetch=1, grid=(pieces,), in_specs=in_specs, out_specs=out_specs
        ),
        compiler_params=pltpu.CompilerParams(vmem_limit_bytes=VMEM_LIMIT),
        name="dispatch",
    )(ids, *args)


def combine_rows(ids, first, pieces, slot_rows, code, local, capacity):
    halves = len(slot_rows)
    slots, width = slot_rows[0].shape[1:]
    tokens = code.shape[-1]
    per = local // halves

    def kernel(ids_ref, code_ref, *rest):
        table = code_ref[0]
        lead = ids_ref[pieces]
        codes = jnp.concatenate([row_of(table, lead + e) for e in range(local)], axis=0)
        picks = one_hot_slots(codes, capacity)
        total = None
        for h in range(halves):
            select = jnp.concatenate(
                [p.astype(B16) for p in picks[h * per : (h + 1) * per]], axis=0
            )
            part = lax.dot_general(
                select, rest[h][0], (((0,), (0,)), ((), ())), preferred_element_type=F32
            )
            total = part if total is None else total + part
        rest[halves][0] = total.astype(B16)

    in_specs = [pl.BlockSpec((1, EXPERTS, tokens), lambda p, ids: (ids[p], 0, 0))]
    in_specs += [
        pl.BlockSpec((1, slots, width), lambda p, ids: (p + first, 0, 0)) for _ in range(halves)
    ]
    return pl.pallas_call(
        kernel,
        out_shape=jax.ShapeDtypeStruct((pieces, tokens, width), B16),
        grid_spec=pltpu.PrefetchScalarGridSpec(
            num_scalar_prefetch=1,
            grid=(pieces,),
            in_specs=in_specs,
            out_specs=pl.BlockSpec((1, tokens, width), lambda p, ids: (p, 0, 0)),
        ),
        compiler_params=pltpu.CompilerParams(vmem_limit_bytes=VMEM_LIMIT),
        name="combine",
    )(ids, code, *slot_rows)


def experts(order, start, count, skip, rows, grads, gates, weights, capacity, in_rows, mid_rows):
    half, _, width = rows[0].shape
    pieces = 2 * half
    n = len(weights)
    pack_rows, eff = weights[0].shape[1:]
    folds = width // eff
    total_rows = pieces * capacity
    split = n == 4
    first_half = count // 2
    large = total_rows > 1000

    def kernel(order_ref, *refs):
        rows_a, rows_b, grads_a, grads_b, gates_a, gates_b = refs[:6]
        pack = refs[6 : 6 + n]
        y_out, dx_out = refs[6 + n : 8 + n]
        outs = refs[8 + n : -6]
        full_g, full_u, full_d, grad_g, grad_u, grad_d = refs[-6:]

        def at_in(j):
            return pl.ds(pl.multiple_of(order_ref[j] * in_rows, in_rows), in_rows)

        def at_mid(j):
            return pl.ds(pl.multiple_of(order_ref[j] * mid_rows, mid_rows), mid_rows)

        for j in range(n):
            full_g[at_in(j), :] = pack[j][0, :in_rows]
            full_u[at_in(j), :] = pack[j][0, in_rows : 2 * in_rows]
            for f in range(folds):
                full_d[at_mid(j), f * eff : (f + 1) * eff] = pack[j][
                    0, 2 * in_rows + f * mid_rows : 2 * in_rows + (f + 1) * mid_rows
                ]

        def joined(a, b, w):
            return jnp.concatenate(
                [
                    a[...].reshape(half * capacity, w),
                    b[...].reshape(half * capacity, w),
                ],
                axis=0,
            )

        x = joined(rows_a, rows_b, width)
        g = joined(grads_a, grads_b, width)
        gate = joined(gates_a, gates_b, 128)[:, 0:1]
        nt = (((1,), (1,)), ((), ()))
        tn = (((0,), (0,)), ((), ()))
        gate_proj = jnp.dot(x, full_g[...], preferred_element_type=F32)
        up_proj = jnp.dot(x, full_u[...], preferred_element_type=F32)
        down_grad = lax.dot_general(g, full_d[...], nt, preferred_element_type=F32)
        sigmoid = 1.0 / (1.0 + jnp.exp(-gate_proj))
        silu = gate_proj * sigmoid
        activated = silu * up_proj
        slot_grad = jnp.sum(activated * down_grad, axis=1, keepdims=True)
        here = order_ref[n] + start + pl.program_id(0)
        lane = lax.broadcasted_iota(jnp.int32, (total_rows, 128), 1)
        high = slot_grad.astype(B16).astype(F32)
        tail = jnp.where(lane == here, high, jnp.where(lane == here + EXPERTS, slot_grad - high, 0.0))
        dx_out[:, :, width:] = tail.astype(B16).reshape(pieces, capacity, 128)
        scaled = (gate * activated).astype(B16)
        act_grad = gate * down_grad
        gate_grad = (act_grad * up_proj * (sigmoid * (1.0 + gate_proj * (1.0 - sigmoid)))).astype(
            B16
        )
        up_grad = (act_grad * silu).astype(B16)
        y = jnp.dot(scaled, full_d[...], preferred_element_type=F32)
        y_out[...] = y.astype(B16).reshape(pieces, capacity, width)
        dx = lax.dot_general(gate_grad, full_g[...], nt, preferred_element_type=F32)
        dx = dx + lax.dot_general(up_grad, full_u[...], nt, preferred_element_type=F32)
        dx_out[:, :, :width] = dx.astype(B16).reshape(pieces, capacity, width)
        grad_g[...] = lax.dot_general(x, gate_grad, tn, preferred_element_type=F32).astype(B16)
        grad_u[...] = lax.dot_general(x, up_grad, tn, preferred_element_type=F32).astype(B16)
        grad_d[...] = lax.dot_general(scaled, g, tn, preferred_element_type=F32).astype(B16)

        def give(ref, slot, j):
            ref[slot, 0, :in_rows] = grad_g[at_in(j), :]
            ref[slot, 0, in_rows : 2 * in_rows] = grad_u[at_in(j), :]
            for f in range(folds):
                ref[slot, 0, 2 * in_rows + f * mid_rows : 2 * in_rows + (f + 1) * mid_rows] = grad_d[
                    at_mid(j), f * eff : (f + 1) * eff
                ]

        if split:
            first_a, rest_a, first_b, rest_b = outs

            @pl.when(pl.program_id(0) < first_half)
            def _():
                give(first_a, 0, 1)
                give(first_a, 1, 3)
                give(rest_a, 0, 0)
                give(rest_a, 1, 2)

            @pl.when(pl.program_id(0) >= first_half)
            def _():
                give(first_b, 0, 2)
                give(first_b, 1, 3)
                give(rest_b, 0, 0)
                give(rest_b, 1, 1)
        else:
            for j in range(n):
                give(outs[0], j, j)

    def single():
        return dict(pipeline_mode=pl.Buffered(1)) if large else {}

    def rows_spec(w):
        return pl.BlockSpec((half, capacity, w), lambda e, o: (0, e + start, 0), **single())

    in_specs = [rows_spec(width)] * 4 + [rows_spec(128)] * 2
    for j in range(n):
        in_specs.append(
            pl.BlockSpec((1, pack_rows, eff), lambda e, o, lead=start - skip[j]: (e + lead, 0, 0))
        )
    slots = count * capacity
    out_specs = [
        pl.BlockSpec((pieces, capacity, w), lambda e, o: (0, e, 0), **single())
        for w in (width, width + 128)
    ]
    out_shape = [
        jax.ShapeDtypeStruct((pieces, slots, width), B16),
        jax.ShapeDtypeStruct((pieces, slots, width + 128), B16),
    ]
    if split:
        for at in (
            lambda e, o: (0, jnp.minimum(e, first_half - 1), 0, 0),
            lambda e, o: (0, jnp.maximum(e - first_half, 0), 0, 0),
        ):
            for _ in range(2):
                out_specs.append(pl.BlockSpec((2, 1, pack_rows, eff), at))
                out_shape.append(jax.ShapeDtypeStruct((2, first_half, pack_rows, eff), B16))
    else:
        out_specs.append(pl.BlockSpec((n, 1, pack_rows, eff), lambda e, o: (0, e, 0, 0)))
        out_shape.append(jax.ShapeDtypeStruct((n, count, pack_rows, eff), B16))
    results = pl.pallas_call(
        kernel,
        out_shape=out_shape,
        grid_spec=pltpu.PrefetchScalarGridSpec(
            num_scalar_prefetch=1,
            grid=(count,),
            in_specs=in_specs,
            out_specs=out_specs,
            scratch_shapes=[
                pltpu.VMEM((n * in_rows, eff), B16),
                pltpu.VMEM((n * in_rows, eff), B16),
                pltpu.VMEM((n * mid_rows, width), B16),
                pltpu.VMEM((n * in_rows, eff), B16),
                pltpu.VMEM((n * in_rows, eff), B16),
                pltpu.VMEM((n * mid_rows, width), B16),
            ],
        ),
        compiler_params=pltpu.CompilerParams(vmem_limit_bytes=VMEM_LIMIT),
        name="experts",
    )(order, *rows, *grads, *gates, *weights)
    return results[0], results[1], results[2:]


def make_body(z_size, small_grid):
    def dense_gather(shard, dp_index):
        if not small_grid:
            return lax.all_gather(shard, ("y", "x"), axis=0, tiled=True), shard
        rows = shard.shape[0]
        core = lax.axis_index("core")
        mine = lax.dynamic_slice_in_dim(shard, core * (rows // 2), rows // 2, 0)
        _, from_x, from_y, diag_a, diag_b = grid_gather(mine)
        moved = jnp.concatenate([from_x, from_y, diag_a, diag_b], axis=0)
        other = swap_core(moved)
        places = [2 * dp_index]
        parts = [shard]
        for source, which in ((moved, core), (other, 1 - core)):
            for j in range(3):
                places.append(2 * (dp_index ^ (j + 1)) + which)
                parts.append(source[j * (rows // 2) : (j + 1) * (rows // 2)])
        return assemble(jnp.stack(places), parts, rows // 2), moved

    def dense_sum(grads, dp_index):
        if not small_grid:
            return lax.psum_scatter(
                lax.psum(grads, ("z", "core")), ("y", "x"), scatter_dimension=0, tiled=True
            )
        rows, cols = grads.shape
        eighth = rows // 8
        core = lax.axis_index("core")
        split = grads.astype(B16).reshape(4, 2, eighth, cols)
        keep = lax.dynamic_index_in_dim(split, core, 1, keepdims=False)
        give = lax.dynamic_index_in_dim(split, 1 - core, 1, keepdims=False)
        both = (keep.astype(F32) + swap_core(give).astype(F32)).astype(B16)
        mine = grid_scatter_rows(
            [lax.dynamic_index_in_dim(both, dp_index ^ j, 0, keepdims=False) for j in range(4)]
        )
        step = 1
        while step < z_size:
            pairs = [(i, i ^ step) for i in range(z_size)]
            mine = mine + lax.ppermute(mine.astype(B16), "z", pairs).astype(F32)
            step *= 2
        low = mine.astype(B16)
        other = swap_core(low)
        first = jnp.where(core == 0, low, other)
        second = jnp.where(core == 0, other, low)
        return jnp.concatenate([first, second], axis=0).astype(F32)

    def body(
        layer_input,
        attn_gain,
        w_query,
        w_key,
        w_value,
        w_output,
        moe_gain,
        w_router,
        w_gate,
        w_up,
        w_down,
        routes,
        priority,
        prefix_len,
        out_grad,
    ):
        tok_rows, model_width = layer_input.shape
        dp_size = lax.axis_size("y") * lax.axis_size("x")
        dp_index = lax.axis_index("y") * lax.axis_size("x") + lax.axis_index("x")
        z = lax.axis_index("z")
        core = lax.axis_index("core")
        seq_len = tok_rows * dp_size
        top_count = routes.shape[1]
        local = w_gate.shape[0]
        capacity = 5 * tok_rows * top_count // (4 * EXPERTS)
        group_size = H // KVH
        score_scale = HD ** (-0.5)

        gains = jnp.stack([attn_gain, moe_gain], axis=1)
        rows = w_query.shape[0]
        head_pack = jnp.concatenate(
            [w_query, w_key, w_value, w_router, gains, jnp.zeros((rows, 94), B16)], axis=1
        )
        head_full, head_moved = dense_gather(head_pack, dp_index)
        full_output, tail_moved = dense_gather(after(w_output, head_moved), dp_index)
        wide = H * HD
        narrow = KVH * HD
        full_query = head_full[:, :wide]
        full_key = head_full[:, wide : wide + narrow]
        full_value = head_full[:, wide + narrow : wide + 2 * narrow]
        full_router = head_full[:, wide + 2 * narrow : wide + 2 * narrow + EXPERTS]
        full_attn_gain = head_full[:, wide + 2 * narrow + EXPERTS].astype(F32)
        full_moe_gain = head_full[:, wide + 2 * narrow + EXPERTS + 1].astype(F32)

        expert_ids = jnp.arange(EXPERTS, dtype=jnp.int32)
        hits = routes[:, :, None] == expert_ids[None, None, :]
        routed = jnp.any(hits, axis=1)
        place = jnp.where(
            routed, jnp.sum(jnp.where(hits, priority[:, :, None], 0), axis=1), jnp.int32(1 << 20)
        )
        ranks = jnp.sum((place[:, :, None] < place.T[None, :, :]).astype(F32), axis=0)
        code = lax.all_gather(jnp.where(routed.T, ranks, -1.0), ("z", "core"), axis=0, tiled=False)
        sources = (z + jnp.arange(z_size, dtype=jnp.int32)) % z_size
        lead = ((2 * z + core) * local).astype(jnp.int32)[None]
        ids_mine = jnp.concatenate([2 * sources + core, lead])
        ids_other = jnp.concatenate([2 * sources + 1 - core, lead])
        grads_mine, grads_other = column_gather(out_grad, z_size)
        (slot_grads_mine,) = dispatch_rows(ids_mine, grads_mine, code, None, local, capacity)
        (slot_grads_other,) = dispatch_rows(ids_other, grads_other, code, None, local, capacity)

        query_pos = dp_index * tok_rows + jnp.arange(tok_rows, dtype=jnp.int32)
        places = query_pos.astype(F32)
        in_float = layer_input.astype(F32)
        normed = rms_norm(in_float, full_attn_gain).astype(B16)
        query_lin = jnp.dot(normed, full_query, preferred_element_type=F32)
        key_lin = jnp.dot(normed, full_key, preferred_element_type=F32)
        value_low = jnp.dot(normed, full_value, preferred_element_type=F32).astype(B16)
        query_rot = (rotate(query_lin.reshape(tok_rows, H, HD), places) * score_scale).astype(B16)
        key_rot = rotate(key_lin.reshape(tok_rows, KVH, HD), places).astype(B16)
        key_rot = key_rot.reshape(tok_rows, narrow)
        both = jnp.concatenate([key_rot, value_low], axis=1)
        steps = jnp.arange(tok_rows, dtype=jnp.int32)
        eff = w_gate.shape[2]
        in_rows, mid_rows = w_gate.shape[1], w_down.shape[1]
        folds = [w_down[:, :, f * eff : (f + 1) * eff] for f in range(model_width // eff)]
        pack = jnp.concatenate([w_gate, w_up, *folds], axis=1)
        if small_grid:
            relative = dp_index ^ jnp.arange(4, dtype=jnp.int32)
            both_parts = grid_gather(both)
            both_all = jnp.concatenate(both_parts, axis=0)
            key_pos = (relative[:, None] * tok_rows + steps[None, :]).reshape(seq_len)
            halves, per = 2, local // 2
            expert_weights, skips = [], []
            for half in range(2):
                own = after(pack[half * per : (half + 1) * per], both_parts[1], both_parts[2])
                parts = grid_gather(own)
                diag = jnp.concatenate([parts[3], parts[4]], axis=0)
                expert_weights.append([own, parts[1], parts[2], diag])
                skips.append([half * per] * 4)
        else:
            relative = jnp.arange(dp_size, dtype=jnp.int32)
            both_all = lax.all_gather(both, ("y", "x"), axis=0, tiled=True)
            key_pos = jnp.arange(seq_len, dtype=jnp.int32)
            halves, per = 1, local
            every = lax.all_gather(pack, ("y", "x"), axis=0, tiled=False)
            expert_weights = [[every[j] for j in range(dp_size)]]
            skips = [[0] * dp_size]
        order = jnp.concatenate([relative, lead])
        key_all = both_all[:, :narrow]
        value_all = both_all[:, narrow:]
        visible = (key_pos[None, :] <= query_pos[:, None]) | (key_pos[None, :] < prefix_len[0])

        def head_scores(head_idx):
            query_head = query_rot[:, head_idx * group_size : (head_idx + 1) * group_size, :]
            key_head = key_all[:, head_idx * HD : (head_idx + 1) * HD]
            scores = jnp.einsum("qgd,kd->gqk", query_head, key_head, preferred_element_type=F32)
            return jnp.where(visible[None, :, :], scores, MASKED_SCORE)

        mixed_heads = []
        log_totals = []
        for head_idx in range(KVH):
            scores = head_scores(head_idx)
            row_max = jnp.max(scores, axis=-1, keepdims=True)
            log_total = row_max + jnp.log(
                jnp.sum(jnp.exp(scores - row_max), axis=-1, keepdims=True)
            )
            probs_low = jnp.exp(scores - log_total).astype(B16)
            value_head = value_all[:, head_idx * HD : (head_idx + 1) * HD]
            mixed_heads.append(
                jnp.einsum("gqk,kd->qgd", probs_low, value_head, preferred_element_type=F32)
            )
            log_totals.append(log_total)
        attended = jnp.concatenate(mixed_heads, axis=1).reshape(tok_rows, wide).astype(B16)
        residual = in_float + jnp.dot(attended, full_output, preferred_element_type=F32)
        moe_in = rms_norm(residual, full_moe_gain).astype(B16)

        rows_mine, rows_other = column_gather(moe_in, z_size)
        router_rows = full_router.T
        slot_rows_mine, slot_gates_mine = dispatch_rows(
            ids_mine, rows_mine, code, router_rows, local, capacity
        )
        slot_rows_other, slot_gates_other = dispatch_rows(
            ids_other, rows_other, code, router_rows, local, capacity
        )
        logits = jnp.dot(moe_in, full_router, preferred_element_type=F32)
        peak = jnp.max(jnp.where(routed, logits, MASKED_SCORE), axis=-1, keepdims=True)
        lifted = jnp.where(routed, jnp.exp(jnp.minimum(logits - peak, 0.0)), 0.0)
        gate_weights = lifted / jnp.sum(lifted, axis=-1, keepdims=True)
        ys, dxs, weight_grads = [], [], []
        for half in range(halves):
            y, dx, grads = experts(
                order,
                half * per,
                per,
                skips[half],
                (slot_rows_mine, slot_rows_other),
                (slot_grads_mine, slot_grads_other),
                (slot_gates_mine, slot_gates_other),
                expert_weights[half],
                capacity,
                in_rows,
                mid_rows,
            )
            ys.append(y)
            dxs.append(dx)
            weight_grads.append(grads)
        dx_other = combine_rows(ids_other, z_size, z_size, dxs, code, local, capacity)
        dx_mine = combine_rows(ids_mine, 0, z_size, dxs, code, local, capacity)
        moe_sum = column_scatter(dx_mine, dx_other, z_size)
        moe_in_grad = moe_sum[:, :model_width]
        gate_grad = (
            moe_sum[:, model_width : model_width + EXPERTS]
            + moe_sum[:, model_width + EXPERTS : model_width + 2 * EXPERTS]
        )
        y_other = combine_rows(ids_other, z_size, z_size, ys, code, local, capacity)
        y_mine = combine_rows(ids_mine, 0, z_size, ys, code, local, capacity)
        mixture = column_scatter(y_mine, y_other, z_size)
        layer_output = (residual + mixture).astype(B16)
        if small_grid:
            sums = []
            for grads in weight_grads:
                sums += list(grid_scatter(*grads))
            pack_grad = jnp.concatenate(sums, axis=0)
        else:
            pack_grad = lax.psum_scatter(
                weight_grads[0][0].astype(F32), ("y", "x"), scatter_dimension=0, tiled=False
            )
        down = 2 * in_rows
        expert_grads = [
            pack_grad[:, :in_rows],
            pack_grad[:, in_rows:down],
            jnp.concatenate(
                [
                    pack_grad[:, down + f * mid_rows : down + (f + 1) * mid_rows]
                    for f in range(model_width // eff)
                ],
                axis=2,
            ),
        ]

        grad_out = out_grad.astype(F32)
        centre = jnp.sum(gate_weights * gate_grad, axis=-1, keepdims=True)
        logit_low = (gate_weights * (gate_grad - centre)).astype(B16)
        router_grad = jnp.einsum("td,te->de", moe_in, logit_low, preferred_element_type=F32)
        moe_in_grad = moe_in_grad + jnp.einsum(
            "te,de->td", logit_low, full_router, preferred_element_type=F32
        )
        norm_value, second_pull = jax.vjp(rms_norm, residual, full_moe_gain)
        resid_norm_grad, moe_gain_grad = second_pull(moe_in_grad)
        residual_grad = grad_out + resid_norm_grad
        attn_out_grad = residual_grad.astype(B16)
        wout_grad = jnp.einsum("tc,td->cd", attended, attn_out_grad, preferred_element_type=F32)
        attended_grad = (
            jnp.einsum("td,cd->tc", attn_out_grad, full_output, preferred_element_type=F32)
            .astype(B16)
            .reshape(tok_rows, H, HD)
        )
        tail_grad = dense_sum(
            jnp.concatenate(
                [
                    wout_grad,
                    router_grad,
                    moe_gain_grad[:, None],
                    jnp.zeros((model_width, 95), F32),
                ],
                axis=1,
            ),
            dp_index,
        )
        query_grads = []
        key_parts = []
        value_parts = []
        for head_idx in range(KVH):
            scores = head_scores(head_idx)
            attention_probs = jnp.exp(scores - log_totals[head_idx])
            probs_low = attention_probs.astype(B16)
            grad_head = attended_grad[:, head_idx * group_size : (head_idx + 1) * group_size, :]
            query_head = query_rot[:, head_idx * group_size : (head_idx + 1) * group_size, :]
            key_head = key_all[:, head_idx * HD : (head_idx + 1) * HD]
            value_head = value_all[:, head_idx * HD : (head_idx + 1) * HD]
            probs_grad = jnp.einsum("qgd,kd->gqk", grad_head, value_head, preferred_element_type=F32)
            row_delta = jnp.sum(attention_probs * probs_grad, axis=-1, keepdims=True)
            score_grad = (attention_probs * (probs_grad - row_delta)).astype(B16)
            query_grads.append(
                jnp.einsum("gqk,kd->qgd", score_grad, key_head, preferred_element_type=F32)
            )
            key_parts.append(
                jnp.einsum("gqk,qgd->kd", score_grad, query_head, preferred_element_type=F32)
            )
            value_parts.append(
                jnp.einsum("gqk,qgd->kd", probs_low, grad_head, preferred_element_type=F32)
            )
        both_part = jnp.concatenate(key_parts + value_parts, axis=1)
        if small_grid:
            both_sum = grid_scatter_rows(both_part.astype(B16).reshape(4, tok_rows, 2 * narrow))
        else:
            both_sum = lax.psum_scatter(both_part, ("y", "x"), scatter_dimension=0, tiled=True)
        query_rot_grad = jnp.concatenate(query_grads, axis=1) * score_scale
        key_rot_grad = both_sum[:, :narrow].reshape(tok_rows, KVH, HD)
        value_grad = both_sum[:, narrow:].astype(B16)
        query_grad = rotate(query_rot_grad, -places).reshape(tok_rows, wide).astype(B16)
        key_grad = rotate(key_rot_grad, -places).reshape(tok_rows, narrow).astype(B16)
        wq_grad = jnp.einsum("td,tc->dc", normed, query_grad, preferred_element_type=F32)
        query_sum = dense_sum(wq_grad, dp_index)
        wk_grad = jnp.einsum("td,tc->dc", normed, key_grad, preferred_element_type=F32)
        wv_grad = jnp.einsum("td,tc->dc", normed, value_grad, preferred_element_type=F32)
        normed_grad = jnp.einsum("tc,dc->td", query_grad, full_query, preferred_element_type=F32)
        normed_grad = normed_grad + jnp.einsum(
            "tc,dc->td", key_grad, full_key, preferred_element_type=F32
        )
        normed_grad = normed_grad + jnp.einsum(
            "tc,dc->td", value_grad, full_value, preferred_element_type=F32
        )
        first_value, first_pull = jax.vjp(rms_norm, in_float, full_attn_gain)
        input_norm_grad, attn_gain_grad = first_pull(normed_grad)
        input_grad = residual_grad + input_norm_grad
        head_grad = dense_sum(
            jnp.concatenate(
                [
                    wk_grad,
                    wv_grad,
                    attn_gain_grad[:, None],
                    jnp.zeros((model_width, 127), F32),
                ],
                axis=1,
            ),
            dp_index,
        )
        return (
            layer_output,
            input_grad,
            head_grad[:, 2 * narrow],
            query_sum,
            head_grad[:, :narrow],
            head_grad[:, narrow : 2 * narrow],
            tail_grad[:, :wide],
            tail_grad[:, wide + EXPERTS],
            tail_grad[:, wide : wide + EXPERTS],
            expert_grads[0],
            expert_grads[1],
            expert_grads[2],
        )

    return body


def solution(mesh):
    groups = mesh.shape["expert"]
    members = mesh.shape["dp"]
    z_size = groups // 2
    side = math.isqrt(members)
    grid = Mesh(
        mesh.devices.reshape(z_size, 2, members // side, side), ("z", "core", "y", "x")
    )
    expert = ("z", "core")
    dp = ("y", "x")
    every = expert + dp
    placed = (
        P(every, None),
        P(dp),
        P(dp, None),
        P(dp, None),
        P(dp, None),
        P(dp, None),
        P(dp),
        P(dp, None),
        P(expert, dp, None),
        P(expert, dp, None),
        P(expert, dp, None),
        P(every, None),
        P(every, None),
        P(expert),
        P(every, None),
    )
    return jax.shard_map(
        make_body(z_size, members == 4 and side == 2),
        mesh=grid,
        in_specs=placed,
        out_specs=(
            P(every, None),
            P(every, None),
            P(dp),
            P(dp, None),
            P(dp, None),
            P(dp, None),
            P(dp, None),
            P(dp),
            P(dp, None),
            P(expert, dp, None),
            P(expert, dp, None),
            P(expert, dp, None),
        ),
        check_vma=False,
    )
```

time: 1520 us -> 858 us (0.56)
  waiting for transfers between devices: 995 us -> 258 us
  Pallas kernels: 0 us -> 290 us
  local copies, waits for them, and re-layouts: 192 us -> 56.5 us
  matrix products: 152 us -> 70.3 us
  starting transfers between devices: 21 us -> 83 us
  blocking collectives: 63.6 us -> 17.9 us
    reduce_scatter x12 -> x0, waiting for transfers between devices: 462 us -> none  [the longest x1 90 us: body(): lax.psum_scatter(wup_grad, 'dp', scatter_dimension=1, tiled=True)]
    all_to_all x4 -> x0, waiting for transfers between devices: 386 us -> none  [the longest x1 110 us: body(): lax.all_to_all(dispatch_buf, 'expert', split_axis=0, concat_axis=1, tiled...]
    pallas_call x0 -> x12, Pallas kernels: none -> 290 us  [the longest x2 202 us: assemble(): pl.pallas_call(kernel, out_shape=jax.ShapeDtypeStruct((total, cols), part...]
    ppermute x0 -> x74, waiting for transfers between devices: none -> 258 us  [the longest x12 92.7 us: cyclic(): lax.ppermute(rows, 'z', [(i, (i + shift) % size) for i in range(size)])]
    gather x15 -> x0, local copies, waits for them, and re-layouts: 101 us -> none  [the longest x6 17.2 us: routed_gates(): jnp.take_along_axis(logit_vals, routes, axis=1)]
    dot_general x64 -> x55, matrix products: 146 us -> 61.6 us  [the longest x8 17.6 us: body(): jnp.einsum('qgd,kd->gqk', grad_head, value_head, preferred_element_type=F32)]
    ppermute x0 -> x74, starting transfers between devices: none -> 83 us  [the longest x12 18.8 us: cyclic(): lax.ppermute(rows, 'z', [(i, (i + shift) % size) for i in range(size)])]
    psum x1 -> x0, waiting for transfers between devices: 79.6 us -> none  [body(): lax.psum((attn_gain_grad, wq_grad, wk_grad, wv_grad, wout_grad, moe_gain_...]
  transfers between devices with their start and end apart: 26 -> 74, of which waited for: 18 -> 33; matrix products, arithmetic and copies ran while one was open for 19% -> 16% of each run, Pallas kernels for 0% -> 34%
where the time goes in v1:
time: 858 us; the launch traced here: 853 us
  Pallas kernels  290 us (34%)
  waiting for transfers between devices  258 us (30%)
  starting transfers between devices  83 us (10%)
  other arithmetic  73.3 us (9%)
  matrix products  70.3 us (8%)
  local copies, waits for them, and re-layouts  56.5 us (7%)
  blocking collectives  17.9 us (2%)
    pallas_call x2, Pallas kernels, assemble(): pl.pallas_call(kernel, out_shape=jax.ShapeDtypeStruct((total, cols), part...  202 us
    ppermute x12, waiting for transfers between devices, cyclic(): lax.ppermute(rows, 'z', [(i, (i + shift) % size) for i in range(size)])  92.7 us
    pallas_call x2, Pallas kernels, experts(): pl.pallas_call(kernel, out_shape=out_shape, grid_spec=pltpu.PrefetchScala...  44.5 us
    ppermute x6, waiting for transfers between devices, dense_sum(): mine = mine + lax.ppermute(mine.astype(B16), 'z', pairs).astype(F32)  44 us
    ppermute x5, waiting for transfers between devices, grid_gather(): diag_a = lax.ppermute(from_x[:half], 'y', SWAP)  31.5 us
    ppermute x5, waiting for transfers between devices, grid_gather(): diag_b = lax.ppermute(from_y[half:], 'x', SWAP)  30.4 us
    ppermute x6, waiting for transfers between devices, grid_scatter(): last_a = lax.ppermute(onward_a, 'y', SWAP)  24.8 us
    pallas_call x4, Pallas kernels, combine_rows(): pl.pallas_call(kernel, out_shape=jax.ShapeDtypeStruct((pieces, tokens, wi...  22.2 us
  transfers between devices with their start and end apart: 74, of which 33 were waited for; matrix products, arithmetic and copies ran while one was open for 16% of the time, Pallas kernels for 34%

profile of v1, /device:TPU:0, one launch (start us, length us, event | category | flops | bytes accessed | tf_op | source)
XLA Modules:
  0.0 853.1 jit_solution(15754117582482323379)
XLA Ops:
  3.1 2.4 concatenate.109.refs_0_
  6.5 3.0 collective-permute-start
  11.0 3.6 collective-permute-start.18
  19.7 2.6 collective-permute-done.refs_1_
  27.4 2.9 collective-permute-done.2
  35.9 5.3 collective-permute-done.9.refs_1_
  43.8 2.6 collective-permute-done.11
  48.5 3.9 fusion.265
  54.9 65.4 %assemble.3 = bf16[1024,1024]{1,0:T(8,128)(2,1)} custom-call(s32[7]{0:T(128)} %stack.123.places_ref, bf16[256,1024]{1,0:T(8,128)(2,1)} %refs_0_, bf16[128,1024]{1,0:T(8,128)(2,1)} %copy-done.45, bf16[128,1024]{1,0:T(8,128)(2,1)} %copy-done.46, bf16[128,1024]{1,0:T(8,128)(2,1)} %pad_maximum_fusion.28.refs_3_, bf16[128,1024]{1,0:T(8,128)(2,1)} %get-tuple-element.185.refs_4_, ...), custom_call_target="tpu_custom_call" | custom-call | tf_op jit(solution)/shard_map/assemble/pallas_call | solution.py:127
  120.2 2.6 fusion.266
  122.9 136.8 %assemble.2 = bf16[1024,2176]{1,0:T(8,128)(2,1)} custom-call(s32[7]{0:T(128)} %stack.123.places_ref, bf16[256,2176]{1,0:T(8,128)(2,1)} %copy-done.30, bf16[128,2176]{1,0:T(8,128)(2,1)} %copy-done.37, bf16[128,2176]{1,0:T(8,128)(2,1)} %copy-done.38, bf16[128,2176]{1,0:T(8,128)(2,1)} %pad_maximum_fusion.15.refs_3_, ...), custom_call_target="tpu_custom_call" | custom-call | tf_op jit(solution)/shard_map/assemble/pallas_call | solution.py:127
  267.5 2.6 fusion.38
  270.3 9.2 %collective-permute-done.5 = bf16[256,1024]{1,0:T(8,128)(2,1)S(1)} collective-permute-done((bf16[256,1024]{1,0:T(8,128)(2,1)S(1)}, bf16[256,1024]{1,0:T(8,128)(2,1)S(1)}, u32[]{:S(2)}, u32[]{:S(2)}) %collective-permute-start.5) | collective-permute-done | bytes 524320 | tf_op jit(solution)/shard_map/ppermute | solution.py:60
  282.3 5.1 collective-permute-done.7
  303.8 2.5 collective-permute-start.14
  306.4 3.1 pad_maximum_fusion.9.rows_ref
  311.7 7.0 collective-permute-done.14
  320.0 30.9 %collective-permute-done.15 = bf16[256,1024]{1,0:T(8,128)(2,1)S(1)} collective-permute-done((bf16[256,1024]{1,0:T(8,128)(2,1)S(1)}, bf16[256,1024]{1,0:T(8,128)(2,1)S(1)}, u32[]{:S(2)}, u32[]{:S(2)}) %collective-permute-start.15) | collective-permute-done | bytes 524320 | tf_op jit(solution)/shard_map/ppermute | solution.py:51
  364.9 2.6 convert_reduce_fusion
  367.5 17.9 %all-gather = f32[256,256]{1,0:T(8,128)} all-gather(f32[32,256]{1,0:T(8,128)S(1)} %bitcast_select_fusion.9), channel_id=2, replica_groups=mesh['z'=4,'core'=2,'y'=2,'x'=2] {'z','core'}, dimensions={0}, use_global_device_ids=true | all-gather | bytes 294912 | tf_op jit(solution)/shard_map/all_gather | solution.py:494
  385.4 5.4 dispatch.6.refs_2_
  394.1 5.2 dispatch.7.refs_3_
  399.3 5.5 dispatch.4
  404.8 4.5 collective-permute-done.24
  409.3 2.7 pad_maximum_fusion.10.refs_9_
  412.0 5.5 dispatch.5
  417.5 22.1 %experts.2 = (bf16[8,160,1024]{2,1,0:T(8,128)(2,1)}, bf16[8,160,1152]{2,1,0:T(8,128)(2,1)}, bf16[2,1,768,512]{3,2,1,0:T(8,128)(2,1)}, bf16[2,1,768,512]{3,2,1,0:...) custom-call(s32[5]{0:T(128)} %pad_add_fusion.1.order_ref, ...), custom_call_target="tpu_custom_call" | custom-call | tf_op jit(solution)/shard_map/experts/pallas_call | solution.py:375
  446.2 16.3 %collective-permute-done.28 = bf16[1,768,512]{2,1,0:T(8,128)(2,1)S(1)} collective-permute-done((bf16[1,768,512]{2,1,0:T(8,128)(2,1)S(1)}, bf16[1,768,512]{2,1,0:T(8,128)(2,1)S(1)}, u32[]{:S(2)}, u32[]{:S(2)}) %collective-permute-start.28) | collective-permute-done | bytes 786464 | tf_op jit(solution)/shard_map/ppermute | solution.py:62
  462.5 29.8 %collective-permute-done.29 = bf16[1,768,512]{2,1,0:T(8,128)(2,1)S(1)} collective-permute-done((bf16[1,768,512]{2,1,0:T(8,128)(2,1)S(1)}, bf16[1,768,512]{2,1,0:T(8,128)(2,1)S(1)}, u32[]{:S(2)}, u32[]{:S(2)}) %collective-permute-start.29) | collective-permute-done | bytes 786464 | tf_op jit(solution)/shard_map/ppermute | solution.py:63
  493.6 22.4 %experts.3 = (bf16[8,160,1024]{2,1,0:T(8,128)(2,1)}, bf16[8,160,1152]{2,1,0:T(8,128)(2,1)}, bf16[2,1,768,512]{3,2,1,0:T(8,128)(2,1)}, bf16[2,1,768,512]{3,2,1,0:...) custom-call(s32[5]{0:T(128)} %pad_add_fusion.1.order_ref, ...), custom_call_target="tpu_custom_call" | custom-call | tf_op jit(solution)/shard_map/experts/pallas_call | solution.py:375
  517.3 5.4 combine.5
  523.7 5.7 combine.7
  530.3 2.6 select_reduce_fusion.1
  534.7 5.4 combine.4
  540.1 5.7 combine.6
  554.1 6.3 collective-permute-done.72
  563.7 2.7 fusion.256
  570.6 6.5 collective-permute-done.67
  577.1 3.2 collective-permute-start.32
  583.2 10.3 %collective-permute-done.71 = bf16[1,768,512]{2,1,0:T(8,128)(2,1)S(1)} collective-permute-done((bf16[1,768,512]{2,1,0:T(8,128)(2,1)S(1)}, bf16[1,768,512]{2,1,0:T(8,128)(2,1)S(1)}, u32[]{:S(2)}, u32[]{:S(2)}) %collective-permute-start.71) | collective-permute-done | bytes 786464 | tf_op jit(solution)/shard_map/ppermute | solution.py:72
  593.5 3.2 collective-permute-start.36
  602.2 2.8 fusion.264
  606.3 35.3 %collective-permute-done.36 = bf16[256,1152]{1,0:T(8,128)(2,1)S(1)} collective-permute-done((bf16[256,1152]{1,0:T(8,128)(2,1)S(1)}, bf16[256,1152]{1,0:T(8,128)(2,1)S(1)}, u32[]{:S(2)}, u32[]{:S(2)}) %collective-permute-start.36) | collective-permute-done | bytes 589856 | tf_op jit(solution)/shard_map/ppermute | solution.py:51
  643.9 18.1 %collective-permute-done.33 = bf16[256,1024]{1,0:T(8,128)(2,1)S(1)} collective-permute-done((bf16[256,1024]{1,0:T(8,128)(2,1)S(1)}, bf16[256,1024]{1,0:T(8,128)(2,1)S(1)}, u32[]{:S(2)}, u32[]{:S(2)}) %collective-permute-start.33) | collective-permute-done | bytes 524320 | tf_op jit(solution)/shard_map/ppermute | solution.py:51
  662.0 2.5 fusion.117
  675.9 5.1 fusion.4
  681.0 4.6 fusion.6
  689.9 3.4 fusion.7
  695.4 3.6 fusion.9
  727.5 5.3 concatenate.139
  735.3 2.4 dynamic-slice_bitcast_fusion
  737.7 3.0 collective-permute-done.40
  740.7 5.2 collective-permute-done.39
  764.0 3.9 concatenate.132
  782.7 5.1 collective-permute-start.55
  787.9 2.5 collective-permute-start.63
  790.4 7.3 collective-permute-done.55
  797.8 2.5 collective-permute-start.56
  801.9 2.8 collective-permute-start.64
  804.7 13.3 %collective-permute-done.56 = bf16[128,1024]{1,0:T(8,128)(2,1)S(1)} collective-permute-done((bf16[128,1024]{1,0:T(8,128)(2,1)S(1)}, bf16[128,1024]{1,0:T(8,128)(2,1)S(1)}, u32[]{:S(2)}, u32[]{:S(2)}) %collective-permute-start.56) | collective-permute-done | bytes 262176 | tf_op jit(solution)/shard_map/ppermute | solution.py:434
  818.9 3.0 collective-permute-done.64
  822.1 2.5 collective-permute-done.44
  826.2 7.2 collective-permute-done.47
  835.1 13.1 %collective-permute-done.48 = bf16[128,1152]{1,0:T(8,128)(2,1)S(1)} collective-permute-done((bf16[128,1152]{1,0:T(8,128)(2,1)S(1)}, bf16[128,1152]{1,0:T(8,128)(2,1)S(1)}, u32[]{:S(2)}, u32[]{:S(2)}) %collective-permute-start.48) | collective-permute-done | bytes 294944 | tf_op jit(solution)/shard_map/ppermute | solution.py:434
  (518 shorter events, 206.5 us)
Async XLA Ops:
  6.5 15.8 %collective-permute-start = (bf16[128,2176]{1,0:T(8,128)(2,1)}, bf16[128,2176]{1,0:T(8,128)(2,1)S(1)}, u32[]{:S(2)}, u32[]{:S(2)}) collective-permute-start(bf16[128,2176]{1,0:T(8,128)(2,1)} %constant_dynamic-slice_fusion.13), channel_id=1, source_target_pairs={{0,1},{1,0},{2,3},{3,2},{4,5},{5,4},{6,7},{7,6},{8,9},{9,8},{10,11... | collective-permute-start | bytes 1671176 | tf_op jit(solution)/shard_map/ppermute | solution.py:60
  9.5 14.7 %collective-permute-start.1 = (bf16[128,2176]{1,0:T(8,128)(2,1)}, bf16[128,2176]{1,0:T(8,128)(2,1)S(1)}, u32[]{:S(2)}, u32[]{:S(2)}) collective-permute-start(bf16[128,2176]{1,0:T(8,128)(2,1)} %constant_dynamic-slice_fusion.13), channel_id=1, source_target_pairs={{0,2},{2,0},{1,3},{3,1},{4,6},{6,4},{5,7},{7,5},{8,10},{10,8},{9,1... | collective-permute-start | bytes 1671176 | tf_op jit(solution)/shard_map/ppermute | solution.py:61
  11.0 295.4 %collective-permute-start.18 = (bf16[256,1024]{1,0:T(8,128)(2,1)}, bf16[256,1024]{1,0:T(8,128)(2,1)}, u32[]{:S(2)}, u32[]{:S(2)}) collective-permute-start(bf16[256,1024]{1,0:T(8,128)(2,1)} %param.29), channel_id=1, source_target_pairs={{0,24},{8,0},{16,8},{24,16},{1,25},{9,1},{17,9},{25,17},{2,26},{10... | collective-permute-start | bytes 1572872 | tf_op jit(solution)/shard_map/ppermute | solution.py:51
  14.6 291.8 %collective-permute-start.19 = (bf16[256,1024]{1,0:T(8,128)(2,1)}, bf16[256,1024]{1,0:T(8,128)(2,1)}, u32[]{:S(2)}, u32[]{:S(2)}) collective-permute-start(bf16[256,1024]{1,0:T(8,128)(2,1)} %param.29), channel_id=1, source_target_pairs={{0,16},{8,24},{16,0},{24,8},{1,17},{9,25},{17,1},{25,9},{2,18},{10... | collective-permute-start | bytes 1572872 | tf_op jit(solution)/shard_map/ppermute | solution.py:51
  22.3 8.0 collective-permute-start.2
  32.4 87.9 %collective-permute-start.4 = (bf16[384,2176]{1,0:T(8,128)(2,1)}, bf16[384,2176]{1,0:T(8,128)(2,1)}, u32[]{:S(2)}, u32[]{:S(2)}) collective-permute-start(bf16[384,2176]{1,0:T(8,128)(2,1)} %constant_dynamic-update-slice_fusion), channel_id=1, source_target_pairs={{0,4},{4,0},{1,5},{5,1},{2,6},{6,2},{3,7},{7,3},{8,12},{12,8},{9,1... | collective-permute-start | bytes 5013512 | tf_op jit(solution)/shard_map/ppermute | solution.py:47
  32.4 8.8 %collective-permute-start.9 = (bf16[128,1024]{1,0:T(8,128)(2,1)S(1)}, bf16[128,1024]{1,0:T(8,128)(2,1)S(1)}, u32[]{:S(2)}, u32[]{:S(2)}) collective-permute-start(bf16[128,1024]{1,0:T(8,128)(2,1)S(1)} %constant_dynamic-slice_fusion.12), channel_id=1, source_target_pairs={{0,1},{1,0},{2,3},{3,2},{4,5},{5,4},{6,7},{7,6},{8,9},{9,8},{10,11... | collective-permute-start | bytes 786440 | tf_op jit(solution)/shard_map/ppermute | solution.py:60
  34.0 8.4 collective-permute-start.10
  46.4 260.0 %collective-permute-start.20 = (bf16[256,1024]{1,0:T(8,128)(2,1)}, bf16[256,1024]{1,0:T(8,128)(2,1)}, u32[]{:S(2)}, u32[]{:S(2)}) collective-permute-start(bf16[256,1024]{1,0:T(8,128)(2,1)} %param.29), channel_id=1, source_target_pairs={{0,8},{8,16},{16,24},{24,0},{1,9},{9,17},{17,25},{25,1},{2,10},{10... | collective-permute-start | bytes 1572872 | tf_op jit(solution)/shard_map/ppermute | solution.py:51
  265.1 14.4 %collective-permute-start.5 = (bf16[256,1024]{1,0:T(8,128)(2,1)S(1)}, bf16[256,1024]{1,0:T(8,128)(2,1)S(1)}, u32[]{:S(2)}, u32[]{:S(2)}) collective-permute-start(bf16[256,1024]{1,0:T(8,128)(2,1)S(1)} %get-tuple-element.200), channel_id=1, source_target_pairs={{0,1},{1,0},{2,3},{3,2},{4,5},{5,4},{6,7},{7,6},{8,9},{9,8},{10,11... | collective-permute-start | bytes 1572872 | tf_op jit(solution)/shard_map/ppermute | solution.py:60
  266.6 14.2 %collective-permute-start.6 = (bf16[256,1024]{1,0:T(8,128)(2,1)S(1)}, bf16[256,1024]{1,0:T(8,128)(2,1)S(1)}, u32[]{:S(2)}, u32[]{:S(2)}) collective-permute-start(bf16[256,1024]{1,0:T(8,128)(2,1)S(1)} %get-tuple-element.200), channel_id=1, source_target_pairs={{0,2},{2,0},{1,3},{3,1},{4,6},{6,4},{5,7},{7,5},{8,10},{10,8},{9,1... | collective-permute-start | bytes 1572872 | tf_op jit(solution)/shard_map/ppermute | solution.py:61
  279.5 7.9 collective-permute-start.7
  280.8 8.1 collective-permute-start.8
  287.4 68.2 %collective-permute-start.22 = (bf16[2,768,512]{2,1,0:T(8,128)(2,1)}, bf16[2,768,512]{2,1,0:T(8,128)(2,1)}, u32[]{:S(2)}, u32[]{:S(2)}) collective-permute-start(bf16[2,768,512]{2,1,0:T(8,128)(2,1)} %get-tuple-element.36.refs_6_), channel_id=1, source_target_pairs={{0,1},{1,0},{2,3},{3,2},{4,5},{5,4},{6,7},{7,6},{8,9},{9,8},{10,11... | collective-permute-start | bytes 4718600 | tf_op jit(solution)/shard_map/ppermute | solution.py:60
  303.8 14.9 %collective-permute-start.14 = (bf16[256,1024]{1,0:T(8,128)(2,1)S(1)}, bf16[256,1024]{1,0:T(8,128)(2,1)S(1)}, u32[]{:S(2)}, u32[]{:S(2)}) collective-permute-start(bf16[256,1024]{1,0:T(8,128)(2,1)S(1)} %multiply_convert_fusion), channel_id=1, source_target_pairs={{0,24},{8,0},{16,8},{24,16},{1,25},{9,1},{17,9},{25,17},{2,26},{10... | collective-permute-start | bytes 1572872 | tf_op jit(solution)/shard_map/ppermute | solution.py:51
  309.5 54.2 %collective-permute-start.21 = (bf16[4,256,1024]{2,1,0:T(8,128)(2,1)}, bf16[4,256,1024]{2,1,0:T(8,128)(2,1)}, u32[]{:S(2)}, u32[]{:S(2)}) collective-permute-start(bf16[4,256,1024]{2,1,0:T(8,128)(2,1)} %pad_maximum_fusion.9.rows_ref), channel_id=1, source_target_pairs={{0,4},{4,0},{1,5},{5,1},{2,6},{6,2},{3,7},{7,3},{8,12},{12,8},{9,1... | collective-permute-start | bytes 6291464 | tf_op jit(solution)/shard_map/ppermute | solution.py:47
  309.5 41.5 %collective-permute-start.15 = (bf16[256,1024]{1,0:T(8,128)(2,1)S(1)}, bf16[256,1024]{1,0:T(8,128)(2,1)S(1)}, u32[]{:S(2)}, u32[]{:S(2)}) collective-permute-start(bf16[256,1024]{1,0:T(8,128)(2,1)S(1)} %multiply_convert_fusion), channel_id=1, source_target_pairs={{0,16},{8,24},{16,0},{24,8},{1,17},{9,25},{17,1},{25,9},{2,18},{10... | collective-permute-start | bytes 1572872 | tf_op jit(solution)/shard_map/ppermute | solution.py:51
  310.0 40.9 %collective-permute-start.16 = (bf16[256,1024]{1,0:T(8,128)(2,1)S(1)}, bf16[256,1024]{1,0:T(8,128)(2,1)S(1)}, u32[]{:S(2)}, u32[]{:S(2)}) collective-permute-start(bf16[256,1024]{1,0:T(8,128)(2,1)S(1)} %multiply_convert_fusion), channel_id=1, source_target_pairs={{0,8},{8,16},{16,24},{24,0},{1,9},{9,17},{17,25},{25,1},{2,10},{10... | collective-permute-start | bytes 1572872 | tf_op jit(solution)/shard_map/ppermute | solution.py:51
  318.8 42.0 %collective-permute-start.23 = (bf16[2,768,512]{2,1,0:T(8,128)(2,1)}, bf16[2,768,512]{2,1,0:T(8,128)(2,1)}, u32[]{:S(2)}, u32[]{:S(2)}) collective-permute-start(bf16[2,768,512]{2,1,0:T(8,128)(2,1)} %get-tuple-element.36.refs_6_), channel_id=1, source_target_pairs={{0,2},{2,0},{1,3},{3,1},{4,6},{6,4},{5,7},{7,5},{8,10},{10,8},{9,1... | collective-permute-start | bytes 4718600 | tf_op jit(solution)/shard_map/ppermute | solution.py:61
  352.5 59.5 %collective-permute-start.17 = (bf16[4,256,1024]{2,1,0:T(8,128)(2,1)}, bf16[4,256,1024]{2,1,0:T(8,128)(2,1)}, u32[]{:S(2)}, u32[]{:S(2)}) collective-permute-start(bf16[4,256,1024]{2,1,0:T(8,128)(2,1)} %pad_maximum_fusion.8.rows_ref), channel_id=1, source_target_pairs={{0,4},{4,0},{1,5},{5,1},{2,6},{6,2},{3,7},{7,3},{8,12},{12,8},{9,1... | collective-permute-start | bytes 6291464 | tf_op jit(solution)/shard_map/ppermute | solution.py:47
  354.7 86.1 %collective-permute-start.26 = (bf16[2,768,512]{2,1,0:T(8,128)(2,1)}, bf16[2,768,512]{2,1,0:T(8,128)(2,1)}, u32[]{:S(2)}, u32[]{:S(2)}) collective-permute-start(bf16[2,768,512]{2,1,0:T(8,128)(2,1)} %get-tuple-element.38.refs_6_), channel_id=1, source_target_pairs={{0,1},{1,0},{2,3},{3,2},{4,5},{5,4},{6,7},{7,6},{8,9},{9,8},{10,11... | collective-permute-start | bytes 4718600 | tf_op jit(solution)/shard_map/ppermute | solution.py:60
  355.6 87.4 %collective-permute-start.27 = (bf16[2,768,512]{2,1,0:T(8,128)(2,1)}, bf16[2,768,512]{2,1,0:T(8,128)(2,1)}, u32[]{:S(2)}, u32[]{:S(2)}) collective-permute-start(bf16[2,768,512]{2,1,0:T(8,128)(2,1)} %get-tuple-element.38.refs_6_), channel_id=1, source_target_pairs={{0,2},{2,0},{1,3},{3,1},{4,6},{6,4},{5,7},{7,5},{8,10},{10,8},{9,1... | collective-permute-start | bytes 4718600 | tf_op jit(solution)/shard_map/ppermute | solution.py:61
  360.7 48.6 %collective-permute-start.24 = (bf16[1,768,512]{2,1,0:T(8,128)(2,1)}, bf16[1,768,512]{2,1,0:T(8,128)(2,1)}, u32[]{:S(2)}, u32[]{:S(2)}) collective-permute-start(bf16[1,768,512]{2,1,0:T(8,128)(2,1)} %slice.762), channel_id=1, source_target_pairs={{0,2},{2,0},{1,3},{3,1},{4,6},{6,4},{5,7},{7,5},{8,10},{10,8},{9,1... | collective-permute-start | bytes 2359304 | tf_op jit(solution)/shard_map/ppermute | solution.py:62
  363.7 45.6 %collective-permute-start.25 = (bf16[1,768,512]{2,1,0:T(8,128)(2,1)}, bf16[1,768,512]{2,1,0:T(8,128)(2,1)}, u32[]{:S(2)}, u32[]{:S(2)}) collective-permute-start(bf16[1,768,512]{2,1,0:T(8,128)(2,1)} %slice.763), channel_id=1, source_target_pairs={{0,1},{1,0},{2,3},{3,2},{4,5},{5,4},{6,7},{7,6},{8,9},{9,8},{10,11... | collective-permute-start | bytes 2359304 | tf_op jit(solution)/shard_map/ppermute | solution.py:63
  439.5 89.8 %collective-permute-start.66 = (bf16[2,1,768,512]{3,2,1,0:T(8,128)(2,1)}, bf16[2,1,768,512]{3,2,1,0:T(8,128)(2,1)}, u32[]{:S(2)}, u32[]{:S(2)}) collective-permute-start(bf16[2,1,768,512]{3,2,1,0:T(8,128)(2,1)} %get-tuple-element.43), channel_id=1, source_target_pairs={{0,1},{1,0},{2,3},{3,2},{4,5},{5,4},{6,7},{7,6},{8,9},{9,8},{10,11... | collective-permute-start | bytes 4718600 | tf_op jit(solution)/shard_map/ppermute | solution.py:68
  442.0 20.5 %collective-permute-start.28 = (bf16[1,768,512]{2,1,0:T(8,128)(2,1)S(1)}, bf16[1,768,512]{2,1,0:T(8,128)(2,1)S(1)}, u32[]{:S(2)}, u32[]{:S(2)}) collective-permute-start(bf16[1,768,512]{2,1,0:T(8,128)(2,1)S(1)} %slice.765), channel_id=1, source_target_pairs={{0,2},{2,0},{1,3},{3,1},{4,6},{6,4},{5,7},{7,5},{8,10},{10,8},{9,1... | collective-permute-start | bytes 2359304 | tf_op jit(solution)/shard_map/ppermute | solution.py:62
  444.2 48.2 %collective-permute-start.29 = (bf16[1,768,512]{2,1,0:T(8,128)(2,1)S(1)}, bf16[1,768,512]{2,1,0:T(8,128)(2,1)S(1)}, u32[]{:S(2)}, u32[]{:S(2)}) collective-permute-start(bf16[1,768,512]{2,1,0:T(8,128)(2,1)S(1)} %slice.766), channel_id=1, source_target_pairs={{0,1},{1,0},{2,3},{3,2},{4,5},{5,4},{6,7},{7,6},{8,9},{9,8},{10,11... | collective-permute-start | bytes 2359304 | tf_op jit(solution)/shard_map/ppermute | solution.py:63
  445.3 102.3 %collective-permute-start.68 = (bf16[2,1,768,512]{3,2,1,0:T(8,128)(2,1)}, bf16[2,1,768,512]{3,2,1,0:T(8,128)(2,1)}, u32[]{:S(2)}, u32[]{:S(2)}) collective-permute-start(bf16[2,1,768,512]{3,2,1,0:T(8,128)(2,1)} %get-tuple-element.45), channel_id=1, source_target_pairs={{0,2},{2,0},{1,3},{3,1},{4,6},{6,4},{5,7},{7,5},{8,10},{10,8},{9,1... | collective-permute-start | bytes 4718600 | tf_op jit(solution)/shard_map/ppermute | solution.py:69
  516.0 35.3 %collective-permute-start.70 = (bf16[2,1,768,512]{3,2,1,0:T(8,128)(2,1)}, bf16[2,1,768,512]{3,2,1,0:T(8,128)(2,1)}, u32[]{:S(2)}, u32[]{:S(2)}) collective-permute-start(bf16[2,1,768,512]{3,2,1,0:T(8,128)(2,1)} %get-tuple-element.47), channel_id=1, source_target_pairs={{0,1},{1,0},{2,3},{3,2},{4,5},{5,4},{6,7},{7,6},{8,9},{9,8},{10,11... | collective-permute-start | bytes 4718600 | tf_op jit(solution)/shard_map/ppermute | solution.py:68
  522.8 39.8 %collective-permute-start.30 = (bf16[4,256,1024]{2,1,0:T(8,128)(2,1)}, bf16[4,256,1024]{2,1,0:T(8,128)(2,1)}, u32[]{:S(2)}, u32[]{:S(2)}) collective-permute-start(bf16[4,256,1024]{2,1,0:T(8,128)(2,1)} %combine.5), channel_id=1, source_target_pairs={{0,4},{4,0},{1,5},{5,1},{2,6},{6,2},{3,7},{7,3},{8,12},{12,8},{9,1... | collective-permute-start | bytes 6291464 | tf_op jit(solution)/shard_map/ppermute | solution.py:47
  522.8 37.6 %collective-permute-start.72 = (bf16[2,1,768,512]{3,2,1,0:T(8,128)(2,1)}, bf16[2,1,768,512]{3,2,1,0:T(8,128)(2,1)}, u32[]{:S(2)}, u32[]{:S(2)}) collective-permute-start(bf16[2,1,768,512]{3,2,1,0:T(8,128)(2,1)} %get-tuple-element.49), channel_id=1, source_target_pairs={{0,2},{2,0},{1,3},{3,1},{4,6},{6,4},{5,7},{7,5},{8,10},{10,8},{9,1... | collective-permute-start | bytes 4718600 | tf_op jit(solution)/shard_map/ppermute | solution.py:69
  529.4 37.2 %collective-permute-start.34 = (bf16[4,256,1152]{2,1,0:T(8,128)(2,1)}, bf16[4,256,1152]{2,1,0:T(8,128)(2,1)}, u32[]{:S(2)}, u32[]{:S(2)}) collective-permute-start(bf16[4,256,1152]{2,1,0:T(8,128)(2,1)} %combine.7), channel_id=1, source_target_pairs={{0,4},{4,0},{1,5},{5,1},{2,6},{6,2},{3,7},{7,3},{8,12},{12,8},{9,1... | collective-permute-start | bytes 7077896 | tf_op jit(solution)/shard_map/ppermute | solution.py:47
  547.5 29.6 %collective-permute-start.67 = (bf16[1,768,512]{2,1,0:T(8,128)(2,1)S(1)}, bf16[1,768,512]{2,1,0:T(8,128)(2,1)S(1)}, u32[]{:S(2)}, u32[]{:S(2)}) collective-permute-start(bf16[1,768,512]{2,1,0:T(8,128)(2,1)S(1)} %fusion.134), channel_id=1, source_target_pairs={{0,2},{2,0},{1,3},{3,1},{4,6},{6,4},{5,7},{7,5},{8,10},{10,8},{9,1... | collective-permute-start | bytes 2359304 | tf_op jit(solution)/shard_map/ppermute | solution.py:72
  551.3 30.4 %collective-permute-start.69 = (bf16[1,768,512]{2,1,0:T(8,128)(2,1)S(1)}, bf16[1,768,512]{2,1,0:T(8,128)(2,1)S(1)}, u32[]{:S(2)}, u32[]{:S(2)}) collective-permute-start(bf16[1,768,512]{2,1,0:T(8,128)(2,1)S(1)} %fusion.135), channel_id=1, source_target_pairs={{0,1},{1,0},{2,3},{3,2},{4,5},{5,4},{6,7},{7,6},{8,9},{9,8},{10,11... | collective-permute-start | bytes 2359304 | tf_op jit(solution)/shard_map/ppermute | solution.py:73
  560.4 33.1 %collective-permute-start.71 = (bf16[1,768,512]{2,1,0:T(8,128)(2,1)S(1)}, bf16[1,768,512]{2,1,0:T(8,128)(2,1)S(1)}, u32[]{:S(2)}, u32[]{:S(2)}) collective-permute-start(bf16[1,768,512]{2,1,0:T(8,128)(2,1)S(1)} %fusion.136), channel_id=1, source_target_pairs={{0,2},{2,0},{1,3},{3,1},{4,6},{6,4},{5,7},{7,5},{8,10},{10,8},{9,1... | collective-permute-start | bytes 2359304 | tf_op jit(solution)/shard_map/ppermute | solution.py:72
  562.6 35.5 %collective-permute-start.73 = (bf16[1,768,512]{2,1,0:T(8,128)(2,1)S(1)}, bf16[1,768,512]{2,1,0:T(8,128)(2,1)S(1)}, u32[]{:S(2)}, u32[]{:S(2)}) collective-permute-start(bf16[1,768,512]{2,1,0:T(8,128)(2,1)S(1)} %fusion.137), channel_id=1, source_target_pairs={{0,1},{1,0},{2,3},{3,2},{4,5},{5,4},{6,7},{7,6},{8,9},{9,8},{10,11... | collective-permute-start | bytes 2359304 | tf_op jit(solution)/shard_map/ppermute | solution.py:73
  566.5 77.3 %collective-permute-start.31 = (bf16[256,1024]{1,0:T(8,128)(2,1)S(1)}, bf16[256,1024]{1,0:T(8,128)(2,1)S(1)}, u32[]{:S(2)}, u32[]{:S(2)}) collective-permute-start(bf16[256,1024]{1,0:T(8,128)(2,1)S(1)} %get-tuple-element.145), channel_id=1, source_target_pairs={{0,8},{8,16},{16,24},{24,0},{1,9},{9,17},{17,25},{25,1},{2,10},{10... | collective-permute-start | bytes 1572872 | tf_op jit(solution)/shard_map/ppermute | solution.py:51
  577.1 66.8 %collective-permute-start.32 = (bf16[256,1024]{1,0:T(8,128)(2,1)S(1)}, bf16[256,1024]{1,0:T(8,128)(2,1)S(1)}, u32[]{:S(2)}, u32[]{:S(2)}) collective-permute-start(bf16[256,1024]{1,0:T(8,128)(2,1)S(1)} %get-tuple-element.147), channel_id=1, source_target_pairs={{0,16},{8,24},{16,0},{24,8},{1,17},{9,25},{17,1},{25,9},{2,18},{10... | collective-permute-start | bytes 1572872 | tf_op jit(solution)/shard_map/ppermute | solution.py:51
  581.7 24.5 %collective-permute-start.35 = (bf16[256,1152]{1,0:T(8,128)(2,1)S(1)}, bf16[256,1152]{1,0:T(8,128)(2,1)S(1)}, u32[]{:S(2)}, u32[]{:S(2)}) collective-permute-start(bf16[256,1152]{1,0:T(8,128)(2,1)S(1)} %get-tuple-element.136), channel_id=1, source_target_pairs={{0,8},{8,16},{16,24},{24,0},{1,9},{9,17},{17,25},{25,1},{2,10},{10... | collective-permute-start | bytes 1769480 | tf_op jit(solution)/shard_map/ppermute | solution.py:51
  593.5 48.1 %collective-permute-start.36 = (bf16[256,1152]{1,0:T(8,128)(2,1)S(1)}, bf16[256,1152]{1,0:T(8,128)(2,1)S(1)}, u32[]{:S(2)}, u32[]{:S(2)}) collective-permute-start(bf16[256,1152]{1,0:T(8,128)(2,1)S(1)} %get-tuple-element.138), channel_id=1, source_target_pairs={{0,16},{8,24},{16,0},{24,8},{1,17},{9,25},{17,1},{25,9},{2,18},{10... | collective-permute-start | bytes 1769480 | tf_op jit(solution)/shard_map/ppermute | solution.py:51
  598.1 43.5 %collective-permute-start.37 = (bf16[256,1152]{1,0:T(8,128)(2,1)S(1)}, bf16[256,1152]{1,0:T(8,128)(2,1)S(1)}, u32[]{:S(2)}, u32[]{:S(2)}) collective-permute-start(bf16[256,1152]{1,0:T(8,128)(2,1)S(1)} %get-tuple-element.137), channel_id=1, source_target_pairs={{0,24},{8,0},{16,8},{24,16},{1,25},{9,1},{17,9},{25,17},{2,26},{10... | collective-permute-start | bytes 1769480 | tf_op jit(solution)/shard_map/ppermute | solution.py:51
  606.2 55.7 %collective-permute-start.33 = (bf16[256,1024]{1,0:T(8,128)(2,1)S(1)}, bf16[256,1024]{1,0:T(8,128)(2,1)S(1)}, u32[]{:S(2)}, u32[]{:S(2)}) collective-permute-start(bf16[256,1024]{1,0:T(8,128)(2,1)S(1)} %get-tuple-element.146), channel_id=1, source_target_pairs={{0,24},{8,0},{16,8},{24,16},{1,25},{9,1},{17,9},{25,17},{2,26},{10... | collective-permute-start | bytes 1572872 | tf_op jit(solution)/shard_map/ppermute | solution.py:51
  717.2 15.6 %collective-permute-start.38 = (bf16[2,128,1024]{1,2,0:T(8,128)(2,1)}, bf16[2,128,1024]{1,2,0:T(8,128)(2,1)}, u32[]{:S(2)}, u32[]{:S(2)}) collective-permute-start(bf16[2,128,1024]{1,2,0:T(8,128)(2,1)} %pad_maximum_fusion.19), channel_id=1, source_target_pairs={{0,1},{1,0},{2,3},{3,2},{4,5},{5,4},{6,7},{7,6},{8,9},{9,8},{10,11... | collective-permute-start | bytes 1572872 | tf_op jit(solution)/shard_map/ppermute | solution.py:68
  725.8 22.2 %collective-permute-start.50 = (bf16[4,128,1024]{2,1,0:T(8,128)(2,1)}, bf16[4,128,1024]{2,1,0:T(8,128)(2,1)}, u32[]{:S(2)}, u32[]{:S(2)}) collective-permute-start(bf16[4,128,1024]{2,1,0:T(8,128)(2,1)} %dynamic-slice_bitcast_fusion.2), channel_id=1, source_target_pairs={{0,4},{4,0},{1,5},{5,1},{2,6},{6,2},{3,7},{7,3},{8,12},{12,8},{9,1... | collective-permute-start | bytes 3145736 | tf_op jit(solution)/shard_map/ppermute | solution.py:47
  725.8 14.9 %collective-permute-start.40 = (bf16[2,128,1024]{1,2,0:T(8,128)(2,1)S(1)}, bf16[2,128,1024]{1,2,0:T(8,128)(2,1)S(1)}, u32[]{:S(2)}, u32[]{:S(2)}) collective-permute-start(bf16[2,128,1024]{1,2,0:T(8,128)(2,1)S(1)} %pad_maximum_fusion.20), channel_id=1, source_target_pairs={{0,2},{2,0},{1,3},{3,1},{4,6},{6,4},{5,7},{7,5},{8,10},{10,8},{9,1... | collective-permute-start | bytes 1572872 | tf_op jit(solution)/shard_map/ppermute | solution.py:69
  734.1 11.7 %collective-permute-start.39 = (bf16[128,1024]{0,1:T(8,128)(2,1)S(1)}, bf16[128,1024]{0,1:T(8,128)(2,1)S(1)}, u32[]{:S(2)}, u32[]{:S(2)}) collective-permute-start(bf16[128,1024]{0,1:T(8,128)(2,1)S(1)} %fusion.142), channel_id=1, source_target_pairs={{0,2},{2,0},{1,3},{3,1},{4,6},{6,4},{5,7},{7,5},{8,10},{10,8},{9,1... | collective-permute-start | bytes 786440 | tf_op jit(solution)/shard_map/ppermute | solution.py:72
  737.7 30.2 %collective-permute-start.58 = (bf16[4,128,1152]{2,1,0:T(8,128)(2,1)}, bf16[4,128,1152]{2,1,0:T(8,128)(2,1)}, u32[]{:S(2)}, u32[]{:S(2)}) collective-permute-start(bf16[4,128,1152]{2,1,0:T(8,128)(2,1)} %dynamic-slice_bitcast_fusion), channel_id=1, source_target_pairs={{0,4},{4,0},{1,5},{5,1},{2,6},{6,2},{3,7},{7,3},{8,12},{12,8},{9,1... | collective-permute-start | bytes 3538952 | tf_op jit(solution)/shard_map/ppermute | solution.py:47
  747.1 8.6 %collective-permute-start.41 = (bf16[128,1024]{0,1:T(8,128)(2,1)S(1)}, bf16[128,1024]{0,1:T(8,128)(2,1)S(1)}, u32[]{:S(2)}, u32[]{:S(2)}) collective-permute-start(bf16[128,1024]{0,1:T(8,128)(2,1)S(1)} %get-tuple-element.140), channel_id=1, source_target_pairs={{0,1},{1,0},{2,3},{3,2},{4,5},{5,4},{6,7},{7,6},{8,9},{9,8},{10,11... | collective-permute-start | bytes 786440 | tf_op jit(solution)/shard_map/ppermute | solution.py:73
  750.6 21.5 %collective-permute-start.53 = (bf16[2,64,1024]{2,1,0:T(8,128)(2,1)}, bf16[2,64,1024]{2,1,0:T(8,128)(2,1)}, u32[]{:S(2)}, u32[]{:S(2)}) collective-permute-start(bf16[2,64,1024]{2,1,0:T(8,128)(2,1)} %pad_maximum_fusion.30), channel_id=1, source_target_pairs={{0,2},{2,0},{1,3},{3,1},{4,6},{6,4},{5,7},{7,5},{8,10},{10,8},{9,1... | collective-permute-start | bytes 786440 | tf_op jit(solution)/shard_map/ppermute | solution.py:69
  752.5 19.6 %collective-permute-start.51 = (bf16[2,64,1024]{2,1,0:T(8,128)(2,1)}, bf16[2,64,1024]{2,1,0:T(8,128)(2,1)}, u32[]{:S(2)}, u32[]{:S(2)}) collective-permute-start(bf16[2,64,1024]{2,1,0:T(8,128)(2,1)} %pad_maximum_fusion.29), channel_id=1, source_target_pairs={{0,1},{1,0},{2,3},{3,2},{4,5},{5,4},{6,7},{7,6},{8,9},{9,8},{10,11... | collective-permute-start | bytes 786440 | tf_op jit(solution)/shard_map/ppermute | solution.py:68
  769.9 7.8 collective-permute-start.61
  771.0 7.7 collective-permute-start.59
  772.0 28.3 %collective-permute-start.42 = (bf16[4,128,1152]{2,1,0:T(8,128)(2,1)S(1)}, bf16[4,128,1152]{2,1,0:T(8,128)(2,1)S(1)}, u32[]{:S(2)}, u32[]{:S(2)}) collective-permute-start(bf16[4,128,1152]{2,1,0:T(8,128)(2,1)S(1)} %dynamic-slice_bitcast_fusion.1), channel_id=1, source_target_pairs={{0,4},{4,0},{1,5},{5,1},{2,6},{6,2},{3,7},{7,3},{8,12},{12,8},{9,1... | collective-permute-start | bytes 3538952 | tf_op jit(solution)/shard_map/ppermute | solution.py:47
  778.8 8.9 %collective-permute-start.60 = (bf16[64,1152]{1,0:T(8,128)(2,1)S(1)}, bf16[64,1152]{1,0:T(8,128)(2,1)S(1)}, u32[]{:S(2)}, u32[]{:S(2)}) collective-permute-start(bf16[64,1152]{1,0:T(8,128)(2,1)S(1)} %get-tuple-element.153), channel_id=1, source_target_pairs={{0,2},{2,0},{1,3},{3,1},{4,6},{6,4},{5,7},{7,5},{8,10},{10,8},{9,1... | collective-permute-start | bytes 442376 | tf_op jit(solution)/shard_map/ppermute | solution.py:72
  779.8 7.9 collective-permute-start.62
  782.7 15.0 %collective-permute-start.55 = (bf16[128,1024]{1,0:T(8,128)(2,1)S(1)}, bf16[128,1024]{1,0:T(8,128)(2,1)S(1)}, u32[]{:S(2)}, u32[]{:S(2)}) collective-permute-start(bf16[128,1024]{1,0:T(8,128)(2,1)S(1)} %fusion.148), channel_id=1, source_target_pairs={{0,8},{8,0},{16,24},{24,16},{1,9},{9,1},{17,25},{25,17},{2,10},{10... | collective-permute-start | bytes 786440 | tf_op jit(solution)/shard_map/ppermute | solution.py:434
  787.9 13.9 %collective-permute-start.63 = (bf16[128,1152]{1,0:T(8,128)(2,1)S(1)}, bf16[128,1152]{1,0:T(8,128)(2,1)S(1)}, u32[]{:S(2)}, u32[]{:S(2)}) collective-permute-start(bf16[128,1152]{1,0:T(8,128)(2,1)S(1)} %fusion.146), channel_id=1, source_target_pairs={{0,8},{8,0},{16,24},{24,16},{1,9},{9,1},{17,25},{25,17},{2,10},{10... | collective-permute-start | bytes 884744 | tf_op jit(solution)/shard_map/ppermute | solution.py:434
  797.8 20.3 %collective-permute-start.56 = (bf16[128,1024]{1,0:T(8,128)(2,1)S(1)}, bf16[128,1024]{1,0:T(8,128)(2,1)S(1)}, u32[]{:S(2)}, u32[]{:S(2)}) collective-permute-start(bf16[128,1024]{1,0:T(8,128)(2,1)S(1)} %fusion.151), channel_id=1, source_target_pairs={{0,16},{8,24},{16,0},{24,8},{1,17},{9,25},{17,1},{25,9},{2,18},{10... | collective-permute-start | bytes 786440 | tf_op jit(solution)/shard_map/ppermute | solution.py:434
  800.7 17.5 %collective-permute-start.45 = (bf16[2,64,1152]{2,1,0:T(8,128)(2,1)S(1)}, bf16[2,64,1152]{2,1,0:T(8,128)(2,1)S(1)}, u32[]{:S(2)}, u32[]{:S(2)}) collective-permute-start(bf16[2,64,1152]{2,1,0:T(8,128)(2,1)S(1)} %pad_maximum_fusion.23), channel_id=1, source_target_pairs={{0,2},{2,0},{1,3},{3,1},{4,6},{6,4},{5,7},{7,5},{8,10},{10,8},{9,1... | collective-permute-start | bytes 884744 | tf_op jit(solution)/shard_map/ppermute | solution.py:69
  801.7 16.5 %collective-permute-start.43 = (bf16[2,64,1152]{2,1,0:T(8,128)(2,1)S(1)}, bf16[2,64,1152]{2,1,0:T(8,128)(2,1)S(1)}, u32[]{:S(2)}, u32[]{:S(2)}) collective-permute-start(bf16[2,64,1152]{2,1,0:T(8,128)(2,1)S(1)} %pad_maximum_fusion.22), channel_id=1, source_target_pairs={{0,1},{1,0},{2,3},{3,2},{4,5},{5,4},{6,7},{7,6},{8,9},{9,8},{10,11... | collective-permute-start | bytes 884744 | tf_op jit(solution)/shard_map/ppermute | solution.py:68
  801.9 20.0 %collective-permute-start.64 = (bf16[128,1152]{1,0:T(8,128)(2,1)S(1)}, bf16[128,1152]{1,0:T(8,128)(2,1)S(1)}, u32[]{:S(2)}, u32[]{:S(2)}) collective-permute-start(bf16[128,1152]{1,0:T(8,128)(2,1)S(1)} %fusion.150), channel_id=1, source_target_pairs={{0,16},{8,24},{16,0},{24,8},{1,17},{9,25},{17,1},{25,9},{2,18},{10... | collective-permute-start | bytes 884744 | tf_op jit(solution)/shard_map/ppermute | solution.py:434
  822.0 13.0 %collective-permute-start.65 = (bf16[128,1152]{1,0:T(8,128)(2,1)S(1)}, bf16[128,1152]{1,0:T(8,128)(2,1)S(1)}, u32[]{:S(2)}, u32[]{:S(2)}) collective-permute-start(bf16[128,1152]{1,0:T(8,128)(2,1)S(1)} %add_convert_fusion.4), channel_id=1, source_target_pairs={{0,4},{4,0},{1,5},{5,1},{2,6},{6,2},{3,7},{7,3},{8,12},{12,8},{9,1... | collective-permute-start | bytes 884744 | tf_op jit(solution)/shard_map/ppermute | solution.py:47
  825.0 8.4 collective-permute-start.47
  833.4 14.8 %collective-permute-start.48 = (bf16[128,1152]{1,0:T(8,128)(2,1)S(1)}, bf16[128,1152]{1,0:T(8,128)(2,1)S(1)}, u32[]{:S(2)}, u32[]{:S(2)}) collective-permute-start(bf16[128,1152]{1,0:T(8,128)(2,1)S(1)} %fusion.149), channel_id=1, source_target_pairs={{0,16},{8,24},{16,0},{24,8},{1,17},{9,25},{17,1},{25,9},{2,18},{10... | collective-permute-start | bytes 884744 | tf_op jit(solution)/shard_map/ppermute | solution.py:434
  (103 other events, 870.1 us)

commit v2 on v1

--- a/solution.py
+++ b/solution.py
@@ -103,39 +103,33 @@
     return total
 
 
-def assemble(places, parts, blocks):
-    rows = blocks
-    cols = parts[0].shape[1]
-
-    def kernel(places_ref, *refs):
-        out = refs[len(parts)]
-        sems = refs[len(parts) + 1]
-        copies = []
-        for i, part in enumerate(parts):
+def assemble(places, shard, moved, other, rows):
+    def kernel(places_ref, shard_ref, moved_ref, other_ref, out_ref):
+        def put(i, value):
             start = pl.multiple_of(places_ref[i] * rows, rows)
-            copies.append(
-                pltpu.make_async_copy(
-                    refs[i], out.at[pl.ds(start, part.shape[0]), :], sems.at[i]
-                )
-            )
-        for copy in copies:
-            copy.start()
-        for copy in copies:
-            copy.wait()
-
-    total = sum(part.shape[0] for part in parts)
+            out_ref[pl.ds(start, value.shape[0]), :] = value
+
+        put(0, shard_ref[...])
+        for j in range(3):
+            put(1 + j, moved_ref[j * rows : (j + 1) * rows, :])
+            put(4 + j, other_ref[j * rows : (j + 1) * rows, :])
+
+    def whole(array_shape):
+        return pl.BlockSpec(array_shape, lambda i, places: (0, 0))
+
+    out_rows, cols = 8 * rows, shard.shape[1]
     return pl.pallas_call(
         kernel,
-        out_shape=jax.ShapeDtypeStruct((total, cols), parts[0].dtype),
+        out_shape=jax.ShapeDtypeStruct((out_rows, cols), shard.dtype),
         grid_spec=pltpu.PrefetchScalarGridSpec(
             num_scalar_prefetch=1,
             grid=(1,),
-            in_specs=[pl.BlockSpec(memory_space=pl.ANY) for _ in parts],
-            out_specs=pl.BlockSpec(memory_space=pl.ANY),
-            scratch_shapes=[pltpu.SemaphoreType.DMA((len(parts),))],
+            in_specs=[whole(a.shape) for a in (shard, moved, other)],
+            out_specs=whole((out_rows, cols)),
         ),
+        compiler_params=pltpu.CompilerParams(vmem_limit_bytes=VMEM_LIMIT),
         name="assemble",
-    )(places, *parts)
+    )(places, shard, moved, other)
 
 
 def one_hot_slots(codes, capacity):
@@ -148,23 +142,43 @@
     return jnp.sum(jnp.where(at == index, table, 0.0), axis=0, keepdims=True)
 
 
-def dispatch_rows(ids, rows, code, router, local, capacity):
-    pieces, tokens, width = rows.shape
+def pack_code(code):
+    rows = code.shape[0] // 4
+    wide = jnp.concatenate([code[c * rows : (c + 1) * rows] for c in range(4)], axis=1)
+    return jnp.concatenate([wide, jnp.full((16 - rows, wide.shape[1]), -1.0, B16)], axis=0)
+
+
+def unpack_code(block, tokens):
+    rows = EXPERTS // 4
+    wide = block.astype(F32)
+    return jnp.concatenate(
+        [wide[:rows, c * tokens : (c + 1) * tokens] for c in range(4)], axis=0
+    )
+
+
+def dispatch_rows(lead, packed, rows, router, local, capacity):
+    pieces, packed_rows, width = packed.shape
+    tokens = packed_rows - 16
     slots = local * capacity
     with_gates = router is not None
 
-    def kernel(ids_ref, rows_ref, code_ref, *rest):
-        table = code_ref[0]
-        first = ids_ref[pieces]
+    def kernel(lead_ref, packed_ref, *rest):
+        first = lead_ref[0]
+        if with_gates:
+            rows_ref, router_ref, out_ref, gate_out = rest
+            table = unpack_code(packed_ref[0], tokens)
+            source = rows_ref[0]
+        else:
+            (out_ref,) = rest
+            table = unpack_code(packed_ref[0, tokens:, :], tokens)
+            source = packed_ref[0, :tokens, :]
         codes = jnp.concatenate([row_of(table, first + e) for e in range(local)], axis=0)
         picks = one_hot_slots(codes, capacity)
         select = jnp.concatenate([p.astype(B16) for p in picks], axis=0)
-        out_ref = rest[1] if with_gates else rest[0]
-        out_ref[0] = jnp.dot(select, rows_ref[0], preferred_element_type=F32).astype(B16)
+        out_ref[0] = jnp.dot(select, source, preferred_element_type=F32).astype(B16)
         if with_gates:
-            router_ref, gate_out = rest[0], rest[2]
             logits = lax.dot_general(
-                router_ref[...], rows_ref[0], (((1,), (1,)), ((), ())), preferred_element_type=F32
+                router_ref[...], source, (((1,), (1,)), ((), ())), preferred_element_type=F32
             )
             routed = table >= 0.0
             peak = jnp.max(jnp.where(routed, logits, MASKED_SCORE), axis=0, keepdims=True)
@@ -177,18 +191,20 @@
                     column, (capacity, 128)
                 )
 
-    in_specs = [
-        pl.BlockSpec((1, tokens, width), lambda p, ids: (p, 0, 0)),
-        pl.BlockSpec((1, EXPERTS, tokens), lambda p, ids: (ids[p], 0, 0)),
-    ]
-    out_specs = [pl.BlockSpec((1, slots, width), lambda p, ids: (p, 0, 0))]
+    out_specs = [pl.BlockSpec((1, slots, width), lambda p, lead: (p, 0, 0))]
     out_shape = [jax.ShapeDtypeStruct((pieces, slots, width), B16)]
-    args = [rows, code]
+    args = [packed]
     if with_gates:
-        in_specs.append(pl.BlockSpec((EXPERTS, width), lambda p, ids: (0, 0)))
-        out_specs.append(pl.BlockSpec((1, slots, 128), lambda p, ids: (p, 0, 0)))
+        in_specs = [
+            pl.BlockSpec((1, 16, width), lambda p, lead: (p, tokens // 16, 0)),
+            pl.BlockSpec((1, tokens, width), lambda p, lead: (p, 0, 0)),
+            pl.BlockSpec((EXPERTS, width), lambda p, lead: (0, 0)),
+        ]
+        out_specs.append(pl.BlockSpec((1, slots, 128), lambda p, lead: (p, 0, 0)))
         out_shape.append(jax.ShapeDtypeStruct((pieces, slots, 128), F32))
-        args.append(router)
+        args += [rows, router]
+    else:
+        in_specs = [pl.BlockSpec((1, packed_rows, width), lambda p, lead: (p, 0, 0))]
     return pl.pallas_call(
         kernel,
         out_shape=out_shape,
@@ -197,19 +213,20 @@
         ),
         compiler_params=pltpu.CompilerParams(vmem_limit_bytes=VMEM_LIMIT),
         name="dispatch",
-    )(ids, *args)
-
-
-def combine_rows(ids, first, pieces, slot_rows, code, local, capacity):
+    )(lead, *args)
+
+
+def combine_rows(lead, first, packed, slot_rows, local, capacity):
+    pieces, packed_rows, code_width = packed.shape
+    tokens = packed_rows - 16
     halves = len(slot_rows)
     slots, width = slot_rows[0].shape[1:]
-    tokens = code.shape[-1]
     per = local // halves
 
-    def kernel(ids_ref, code_ref, *rest):
-        table = code_ref[0]
-        lead = ids_ref[pieces]
-        codes = jnp.concatenate([row_of(table, lead + e) for e in range(local)], axis=0)
+    def kernel(lead_ref, code_ref, *rest):
+        table = unpack_code(code_ref[0], tokens)
+        here = lead_ref[0]
+        codes = jnp.concatenate([row_of(table, here + e) for e in range(local)], axis=0)
         picks = one_hot_slots(codes, capacity)
         total = None
         for h in range(halves):
@@ -222,9 +239,9 @@
             total = part if total is None else total + part
         rest[halves][0] = total.astype(B16)
 
-    in_specs = [pl.BlockSpec((1, EXPERTS, tokens), lambda p, ids: (ids[p], 0, 0))]
+    in_specs = [pl.BlockSpec((1, 16, code_width), lambda p, lead: (p, tokens // 16, 0))]
     in_specs += [
-        pl.BlockSpec((1, slots, width), lambda p, ids: (p + first, 0, 0)) for _ in range(halves)
+        pl.BlockSpec((1, slots, width), lambda p, lead: (p + first, 0, 0)) for _ in range(halves)
     ]
     return pl.pallas_call(
         kernel,
@@ -233,11 +250,11 @@
             num_scalar_prefetch=1,
             grid=(pieces,),
             in_specs=in_specs,
-            out_specs=pl.BlockSpec((1, tokens, width), lambda p, ids: (p, 0, 0)),
+            out_specs=pl.BlockSpec((1, tokens, width), lambda p, lead: (p, 0, 0)),
         ),
         compiler_params=pltpu.CompilerParams(vmem_limit_bytes=VMEM_LIMIT),
         name="combine",
-    )(ids, code, *slot_rows)
+    )(lead, packed, *slot_rows)
 
 
 def experts(order, start, count, skip, rows, grads, gates, weights, capacity, in_rows, mid_rows):
@@ -406,12 +423,9 @@
         moved = jnp.concatenate([from_x, from_y, diag_a, diag_b], axis=0)
         other = swap_core(moved)
         places = [2 * dp_index]
-        parts = [shard]
-        for source, which in ((moved, core), (other, 1 - core)):
-            for j in range(3):
-                places.append(2 * (dp_index ^ (j + 1)) + which)
-                parts.append(source[j * (rows // 2) : (j + 1) * (rows // 2)])
-        return assemble(jnp.stack(places), parts, rows // 2), moved
+        for which in (core, 1 - core):
+            places += [2 * (dp_index ^ (j + 1)) + which for j in range(3)]
+        return assemble(jnp.stack(places), shard, moved, other, rows // 2), moved
 
     def dense_sum(grads, dp_index):
         if not small_grid:
@@ -491,14 +505,13 @@
             routed, jnp.sum(jnp.where(hits, priority[:, :, None], 0), axis=1), jnp.int32(1 << 20)
         )
         ranks = jnp.sum((place[:, :, None] < place.T[None, :, :]).astype(F32), axis=0)
-        code = lax.all_gather(jnp.where(routed.T, ranks, -1.0), ("z", "core"), axis=0, tiled=False)
-        sources = (z + jnp.arange(z_size, dtype=jnp.int32)) % z_size
+        code = pack_code(jnp.where(routed.T, ranks, -1.0).astype(B16))
         lead = ((2 * z + core) * local).astype(jnp.int32)[None]
-        ids_mine = jnp.concatenate([2 * sources + core, lead])
-        ids_other = jnp.concatenate([2 * sources + 1 - core, lead])
-        grads_mine, grads_other = column_gather(out_grad, z_size)
-        (slot_grads_mine,) = dispatch_rows(ids_mine, grads_mine, code, None, local, capacity)
-        (slot_grads_other,) = dispatch_rows(ids_other, grads_other, code, None, local, capacity)
+        grads_mine, grads_other = column_gather(
+            jnp.concatenate([out_grad, code], axis=0), z_size
+        )
+        (slot_grads_mine,) = dispatch_rows(lead, grads_mine, None, None, local, capacity)
+        (slot_grads_other,) = dispatch_rows(lead, grads_other, None, None, local, capacity)
 
         query_pos = dp_index * tok_rows + jnp.arange(tok_rows, dtype=jnp.int32)
         places = query_pos.astype(F32)
@@ -569,10 +582,10 @@
         rows_mine, rows_other = column_gather(moe_in, z_size)
         router_rows = full_router.T
         slot_rows_mine, slot_gates_mine = dispatch_rows(
-            ids_mine, rows_mine, code, router_rows, local, capacity
+            lead, grads_mine, rows_mine, router_rows, local, capacity
         )
         slot_rows_other, slot_gates_other = dispatch_rows(
-            ids_other, rows_other, code, router_rows, local, capacity
+            lead, grads_other, rows_other, router_rows, local, capacity
         )
         logits = jnp.dot(moe_in, full_router, preferred_element_type=F32)
         peak = jnp.max(jnp.where(routed, logits, MASKED_SCORE), axis=-1, keepdims=True)
@@ -596,16 +609,16 @@
             ys.append(y)
             dxs.append(dx)
             weight_grads.append(grads)
-        dx_other = combine_rows(ids_other, z_size, z_size, dxs, code, local, capacity)
-        dx_mine = combine_rows(ids_mine, 0, z_size, dxs, code, local, capacity)
+        dx_other = combine_rows(lead, z_size, grads_other, dxs, local, capacity)
+        dx_mine = combine_rows(lead, 0, grads_mine, dxs, local, capacity)
         moe_sum = column_scatter(dx_mine, dx_other, z_size)
         moe_in_grad = moe_sum[:, :model_width]
         gate_grad = (
             moe_sum[:, model_width : model_width + EXPERTS]
             + moe_sum[:, model_width + EXPERTS : model_width + 2 * EXPERTS]
         )
-        y_other = combine_rows(ids_other, z_size, z_size, ys, code, local, capacity)
-        y_mine = combine_rows(ids_mine, 0, z_size, ys, code, local, capacity)
+        y_other = combine_rows(lead, z_size, grads_other, ys, local, capacity)
+        y_mine = combine_rows(lead, 0, grads_mine, ys, local, capacity)
         mixture = column_scatter(y_mine, y_other, z_size)
         layer_output = (residual + mixture).astype(B16)
         if small_grid:

time: 858 us -> 675 us (0.79)
  Pallas kernels: 290 us -> 92.6 us
  waiting for transfers between devices: 258 us -> 294 us
  blocking collectives: 17.9 us -> 0 us
    pallas_call x2, Pallas kernels: 202 us -> 9.17 us  [assemble(): pl.pallas_call(kernel, out_shape=jax.ShapeDtypeStruct((out_rows, cols), s...]
    ppermute x5, waiting for transfers between devices: 31.5 us -> 58.7 us  [grid_gather(): diag_a = lax.ppermute(from_x[:half], 'y', SWAP)]
    all_gather x1 -> x0, blocking collectives: 17.9 us -> none  [body(): lax.all_gather(jnp.where(routed.T, ranks, -1.0), ('z', 'core'), axis=0, t...]
    ppermute x12, waiting for transfers between devices: 92.7 us -> 109 us  [cyclic(): lax.ppermute(rows, 'z', [(i, (i + shift) % size) for i in range(size)])]
  transfers between devices with their start and end apart: 74 -> 74, of which waited for: 33 -> 35; matrix products, arithmetic and copies ran while one was open for 16% -> 19% of each run, Pallas kernels for 34% -> 14%
where the time goes in v2:
time: 675 us; the launch traced here: 670 us
  waiting for transfers between devices  294 us (44%)
  Pallas kernels  92.6 us (14%)
  starting transfers between devices  88.4 us (13%)
  other arithmetic  72.2 us (11%)
  matrix products  65.6 us (10%)
  local copies, waits for them, and re-layouts  53.4 us (8%)
    ppermute x12, waiting for transfers between devices, cyclic(): lax.ppermute(rows, 'z', [(i, (i + shift) % size) for i in range(size)])  109 us
    ppermute x5, waiting for transfers between devices, grid_gather(): diag_a = lax.ppermute(from_x[:half], 'y', SWAP)  58.7 us
    pallas_call x2, Pallas kernels, experts(): pl.pallas_call(kernel, out_shape=out_shape, grid_spec=pltpu.PrefetchScala...  44.7 us
    ppermute x6, waiting for transfers between devices, dense_sum(): mine = mine + lax.ppermute(mine.astype(B16), 'z', pairs).astype(F32)  38.5 us
    ppermute x5, waiting for transfers between devices, grid_gather(): diag_b = lax.ppermute(from_y[half:], 'x', SWAP)  31.2 us
    ppermute x12, starting transfers between devices, cyclic(): lax.ppermute(rows, 'z', [(i, (i + shift) % size) for i in range(size)])  21.9 us
    ppermute x6, waiting for transfers between devices, grid_scatter(): last_a = lax.ppermute(onward_a, 'y', SWAP)  21 us
    pallas_call x4, Pallas kernels, combine_rows(): pl.pallas_call(kernel, out_shape=jax.ShapeDtypeStruct((pieces, tokens, wi...  19.8 us
  transfers between devices with their start and end apart: 74, of which 35 were waited for; matrix products, arithmetic and copies ran while one was open for 19% of the time, Pallas kernels for 14%

profile of v2, /device:TPU:0, one launch (start us, length us, event | category | flops | bytes accessed | tf_op | source)
XLA Modules:
  0.0 669.8 jit_solution(630975384206713626)
XLA Ops:
  3.1 2.5 concatenate.103.shard_ref
  6.5 3.0 collective-permute-start
  11.2 2.6 convert_reduce_fusion
  14.9 3.6 collective-permute-start.14
  27.5 2.9 collective-permute-done.2
  35.2 3.6 collective-permute-done.9
  48.8 3.1 pad_maximum_fusion.1
  51.9 14.0 %collective-permute-done.15 = bf16[272,1024]{1,0:T(8,128)(2,1)} collective-permute-done((bf16[272,1024]{1,0:T(8,128)(2,1)}, bf16[272,1024]{1,0:T(8,128)(2,1)}, u32[]{:S(2)}, u32[]{:S(2)}) %collective-permute-start.15) | collective-permute-done | bytes 557088 | tf_op jit(solution)/shard_map/ppermute | solution.py:51
  68.5 3.7 assemble.3
  72.2 5.5 assemble.2
  81.0 2.4 convolution_convert_fusion.5
  85.9 2.6 fusion.38
  88.7 10.5 %collective-permute-done.5 = bf16[256,1024]{1,0:T(8,128)(2,1)S(1)} collective-permute-done((bf16[256,1024]{1,0:T(8,128)(2,1)S(1)}, bf16[256,1024]{1,0:T(8,128)(2,1)S(1)}, u32[]{:S(2)}, u32[]{:S(2)}) %collective-permute-start.5) | collective-permute-done | bytes 524320 | tf_op jit(solution)/shard_map/ppermute | solution.py:60
  101.0 6.0 collective-permute-done.7
  113.4 2.4 exponential_reduce_fusion.1
  122.9 3.5 collective-permute-start.17
  129.9 8.9 %collective-permute-done.17 = bf16[256,1024]{1,0:T(8,128)(2,1)S(1)} collective-permute-done((bf16[256,1024]{1,0:T(8,128)(2,1)S(1)}, bf16[256,1024]{1,0:T(8,128)(2,1)S(1)}, u32[]{:S(2)}, u32[]{:S(2)}) %collective-permute-start.17) | collective-permute-done | bytes 524320 | tf_op jit(solution)/shard_map/ppermute | solution.py:51
  140.5 29.4 %collective-permute-done.18 = bf16[256,1024]{1,0:T(8,128)(2,1)S(1)} collective-permute-done((bf16[256,1024]{1,0:T(8,128)(2,1)S(1)}, bf16[256,1024]{1,0:T(8,128)(2,1)S(1)}, u32[]{:S(2)}, u32[]{:S(2)}) %collective-permute-start.18) | collective-permute-done | bytes 524320 | tf_op jit(solution)/shard_map/ppermute | solution.py:51
  178.1 4.7 dispatch.6.refs_2_
  183.6 4.5 dispatch.7.refs_3_
  188.1 4.8 dispatch.4
  193.0 33.2 %collective-permute-done.24 = bf16[1,768,512]{2,1,0:T(8,128)(2,1)} collective-permute-done((bf16[1,768,512]{2,1,0:T(8,128)(2,1)}, bf16[1,768,512]{2,1,0:T(8,128)(2,1)}, u32[]{:S(2)}, u32[]{:S(2)}) %collective-permute-start.24) | collective-permute-done | bytes 786464 | tf_op jit(solution)/shard_map/ppermute | solution.py:62
  226.1 2.5 pad_maximum_fusion.10.refs_9_
  228.6 4.8 dispatch.5
  233.5 22.1 %experts.2 = (bf16[8,160,1024]{2,1,0:T(8,128)(2,1)}, bf16[8,160,1152]{2,1,0:T(8,128)(2,1)}, bf16[2,1,768,512]{3,2,1,0:T(8,128)(2,1)}, bf16[2,1,768,512]{3,2,1,0:...) custom-call(s32[5]{0:T(128)} %pad_add_fusion.order_ref, ...), custom_call_target="tpu_custom_call" | custom-call | tf_op jit(solution)/shard_map/experts/pallas_call | solution.py:392
  262.2 16.2 %collective-permute-done.28 = bf16[1,768,512]{2,1,0:T(8,128)(2,1)S(1)} collective-permute-done((bf16[1,768,512]{2,1,0:T(8,128)(2,1)S(1)}, bf16[1,768,512]{2,1,0:T(8,128)(2,1)S(1)}, u32[]{:S(2)}, u32[]{:S(2)}) %collective-permute-start.28) | collective-permute-done | bytes 786464 | tf_op jit(solution)/shard_map/ppermute | solution.py:62
  278.4 30.0 %collective-permute-done.29 = bf16[1,768,512]{2,1,0:T(8,128)(2,1)S(1)} collective-permute-done((bf16[1,768,512]{2,1,0:T(8,128)(2,1)S(1)}, bf16[1,768,512]{2,1,0:T(8,128)(2,1)S(1)}, u32[]{:S(2)}, u32[]{:S(2)}) %collective-permute-start.29) | collective-permute-done | bytes 786464 | tf_op jit(solution)/shard_map/ppermute | solution.py:63
  309.7 22.6 %experts.3 = (bf16[8,160,1024]{2,1,0:T(8,128)(2,1)}, bf16[8,160,1152]{2,1,0:T(8,128)(2,1)}, bf16[2,1,768,512]{3,2,1,0:T(8,128)(2,1)}, bf16[2,1,768,512]{3,2,1,0:...) custom-call(s32[5]{0:T(128)} %pad_add_fusion.order_ref, ...), custom_call_target="tpu_custom_call" | custom-call | tf_op jit(solution)/shard_map/experts/pallas_call | solution.py:392
  333.3 4.8 combine.5
  339.6 5.1 combine.7
  345.8 2.4 select_reduce_fusion.1
  350.6 4.8 combine.4
  355.4 5.2 combine.6
  364.2 3.4 collective-permute-done.70
  370.1 5.6 collective-permute-done.72
  379.2 2.6 fusion.254
  382.9 2.5 collective-permute-start.31
  389.0 3.5 collective-permute-done.67
  392.5 4.2 collective-permute-start.32
  398.5 10.4 %collective-permute-done.71 = bf16[1,768,512]{2,1,0:T(8,128)(2,1)S(1)} collective-permute-done((bf16[1,768,512]{2,1,0:T(8,128)(2,1)S(1)}, bf16[1,768,512]{2,1,0:T(8,128)(2,1)S(1)}, u32[]{:S(2)}, u32[]{:S(2)}) %collective-permute-start.71) | collective-permute-done | bytes 786464 | tf_op jit(solution)/shard_map/ppermute | solution.py:72
  408.9 4.2 collective-permute-start.36
  418.6 2.8 fusion.262
  422.9 35.2 %collective-permute-done.36 = bf16[256,1152]{1,0:T(8,128)(2,1)S(1)} collective-permute-done((bf16[256,1152]{1,0:T(8,128)(2,1)}, bf16[256,1152]{1,0:T(8,128)(2,1)S(1)}, u32[]{:S(2)}, u32[]{:S(2)}) %collective-permute-start.36) | collective-permute-done | bytes 589856 | tf_op jit(solution)/shard_map/ppermute | solution.py:51
  459.4 20.3 %collective-permute-done.33 = bf16[256,1024]{1,0:T(8,128)(2,1)S(1)} collective-permute-done((bf16[256,1024]{1,0:T(8,128)(2,1)S(1)}, bf16[256,1024]{1,0:T(8,128)(2,1)S(1)}, u32[]{:S(2)}, u32[]{:S(2)}) %collective-permute-start.33) | collective-permute-done | bytes 524320 | tf_op jit(solution)/shard_map/ppermute | solution.py:51
  479.7 2.5 fusion.117
  492.6 5.2 fusion.4
  497.8 4.5 fusion.6
  506.5 3.4 fusion.7
  512.1 3.6 fusion.9
  544.1 5.3 concatenate.131
  552.3 2.4 dynamic-slice_bitcast_fusion
  554.7 3.1 collective-permute-done.40
  557.8 5.1 collective-permute-done.39
  570.1 3.2 collective-permute-done.41
  582.0 3.7 concatenate.124
  593.3 2.6 collective-permute-done.61
  596.1 2.6 collective-permute-start.60
  599.9 4.4 collective-permute-start.55
  604.5 3.9 collective-permute-start.63
  608.3 3.1 collective-permute-done.55
  611.5 5.1 collective-permute-start.56
  621.2 12.6 %collective-permute-done.56 = bf16[128,1024]{1,0:T(8,128)(2,1)S(1)} collective-permute-done((bf16[128,1024]{1,0:T(8,128)(2,1)S(1)}, bf16[128,1024]{1,0:T(8,128)(2,1)S(1)}, u32[]{:S(2)}, u32[]{:S(2)}) %collective-permute-start.56) | collective-permute-done | bytes 262176 | tf_op jit(solution)/shard_map/ppermute | solution.py:448
  642.3 7.4 %collective-permute-done.47 = bf16[128,1152]{1,0:T(8,128)(2,1)S(1)} collective-permute-done((bf16[128,1152]{1,0:T(8,128)(2,1)S(1)}, bf16[128,1152]{1,0:T(8,128)(2,1)S(1)}, u32[]{:S(2)}, u32[]{:S(2)}) %collective-permute-start.47) | collective-permute-done | bytes 294944 | tf_op jit(solution)/shard_map/ppermute | solution.py:448
  651.1 13.6 %collective-permute-done.48 = bf16[128,1152]{1,0:T(8,128)(2,1)S(1)} collective-permute-done((bf16[128,1152]{1,0:T(8,128)(2,1)S(1)}, bf16[128,1152]{1,0:T(8,128)(2,1)S(1)}, u32[]{:S(2)}, u32[]{:S(2)}) %collective-permute-start.48) | collective-permute-done | bytes 294944 | tf_op jit(solution)/shard_map/ppermute | solution.py:448
  (541 shorter events, 196.4 us)
Async XLA Ops:
  6.5 15.8 %collective-permute-start = (bf16[128,2176]{1,0:T(8,128)(2,1)}, bf16[128,2176]{1,0:T(8,128)(2,1)S(1)}, u32[]{:S(2)}, u32[]{:S(2)}) collective-permute-start(bf16[128,2176]{1,0:T(8,128)(2,1)} %constant_dynamic-slice_fusion.13), channel_id=1, source_target_pairs={{0,1},{1,0},{2,3},{3,2},{4,5},{5,4},{6,7},{7,6},{8,9},{9,8},{10,11... | collective-permute-start | bytes 1671176 | tf_op jit(solution)/shard_map/ppermute | solution.py:60
  9.5 14.7 %collective-permute-start.1 = (bf16[128,2176]{1,0:T(8,128)(2,1)}, bf16[128,2176]{1,0:T(8,128)(2,1)S(1)}, u32[]{:S(2)}, u32[]{:S(2)}) collective-permute-start(bf16[128,2176]{1,0:T(8,128)(2,1)} %constant_dynamic-slice_fusion.13), channel_id=1, source_target_pairs={{0,2},{2,0},{1,3},{3,1},{4,6},{6,4},{5,7},{7,5},{8,10},{10,8},{9,1... | collective-permute-start | bytes 1671176 | tf_op jit(solution)/shard_map/ppermute | solution.py:61
  14.9 37.0 %collective-permute-start.14 = (bf16[272,1024]{1,0:T(8,128)(2,1)}, bf16[272,1024]{1,0:T(8,128)(2,1)}, u32[]{:S(2)}, u32[]{:S(2)}) collective-permute-start(bf16[272,1024]{1,0:T(8,128)(2,1)} %maximum_maximum_fusion), channel_id=1, source_target_pairs={{0,24},{8,0},{16,8},{24,16},{1,25},{9,1},{17,9},{25,17},{2,26},{10... | collective-permute-start | bytes 1671176 | tf_op jit(solution)/shard_map/ppermute | solution.py:51
  18.5 47.3 %collective-permute-start.15 = (bf16[272,1024]{1,0:T(8,128)(2,1)}, bf16[272,1024]{1,0:T(8,128)(2,1)}, u32[]{:S(2)}, u32[]{:S(2)}) collective-permute-start(bf16[272,1024]{1,0:T(8,128)(2,1)} %maximum_maximum_fusion), channel_id=1, source_target_pairs={{0,16},{8,24},{16,0},{24,8},{1,17},{9,25},{17,1},{25,9},{2,18},{10... | collective-permute-start | bytes 1671176 | tf_op jit(solution)/shard_map/ppermute | solution.py:51
  22.3 8.0 %collective-permute-start.2 = (bf16[64,2176]{1,0:T(8,128)(2,1)S(1)}, bf16[64,2176]{1,0:T(8,128)(2,1)S(1)}, u32[]{:S(2)}, u32[]{:S(2)}) collective-permute-start(bf16[64,2176]{1,0:T(8,128)(2,1)S(1)} %slice.703), channel_id=1, source_target_pairs={{0,2},{2,0},{1,3},{3,1},{4,6},{6,4},{5,7},{7,5},{8,10},{10,8},{9,1... | collective-permute-start | bytes 835592 | tf_op jit(solution)/shard_map/ppermute | solution.py:62
  34.0 7.8 %collective-permute-start.10 = (bf16[128,1024]{1,0:T(8,128)(2,1)S(1)}, bf16[128,1024]{1,0:T(8,128)(2,1)S(1)}, u32[]{:S(2)}, u32[]{:S(2)}) collective-permute-start(bf16[128,1024]{1,0:T(8,128)(2,1)S(1)} %constant_dynamic-slice_fusion.12), channel_id=1, source_target_pairs={{0,2},{2,0},{1,3},{3,1},{4,6},{6,4},{5,7},{7,5},{8,10},{10,8},{9,1... | collective-permute-start | bytes 786440 | tf_op jit(solution)/shard_map/ppermute | solution.py:61
  34.9 37.3 %collective-permute-start.4 = (bf16[384,2176]{1,0:T(8,128)(2,1)}, bf16[384,2176]{1,0:T(8,128)(2,1)}, u32[]{:S(2)}, u32[]{:S(2)}) collective-permute-start(bf16[384,2176]{1,0:T(8,128)(2,1)} %constant_dynamic-update-slice_fusion.moved_ref), channel_id=1, source_target_pairs={{0,4},{4,0},{1,5},{5,1},{2,6},{6,2},{3,7},{7,3},{8,12},{12,8},{9,1... | collective-permute-start | bytes 5013512 | tf_op jit(solution)/shard_map/ppermute | solution.py:47
  43.9 22.0 %collective-permute-start.16 = (bf16[272,1024]{1,0:T(8,128)(2,1)}, bf16[272,1024]{1,0:T(8,128)(2,1)S(1)}, u32[]{:S(2)}, u32[]{:S(2)}) collective-permute-start(bf16[272,1024]{1,0:T(8,128)(2,1)} %maximum_maximum_fusion), channel_id=1, source_target_pairs={{0,8},{8,16},{16,24},{24,0},{1,9},{9,17},{17,25},{25,1},{2,10},{10... | collective-permute-start | bytes 1671176 | tf_op jit(solution)/shard_map/ppermute | solution.py:51
  47.4 21.0 %collective-permute-start.13 = (bf16[384,1024]{1,0:T(8,128)(2,1)}, bf16[384,1024]{1,0:T(8,128)(2,1)}, u32[]{:S(2)}, u32[]{:S(2)}) collective-permute-start(bf16[384,1024]{1,0:T(8,128)(2,1)} %constant_dynamic-update-slice_fusion.9.moved_ref), channel_id=1, source_target_pairs={{0,4},{4,0},{1,5},{5,1},{2,6},{6,2},{3,7},{7,3},{8,12},{12,8},{9,1... | collective-permute-start | bytes 2359304 | tf_op jit(solution)/shard_map/ppermute | solution.py:47
  68.4 108.0 %collective-permute-start.20 = (bf16[4,272,1024]{2,1,0:T(8,128)(2,1)S(1)}, bf16[4,272,1024]{2,1,0:T(8,128)(2,1)}, u32[]{:S(2)}, u32[]{:S(2)}) collective-permute-start(bf16[4,272,1024]{2,1,0:T(8,128)(2,1)S(1)} %pad_maximum_fusion.2.packed_ref.code_ref), channel_id=1, source_target_pairs={{0,4},{4,0},{1,5},{5,1},{2,6},{6,2},{3,7},{7,3},{8,12},{12,8},{9,1... | collective-permute-start | bytes 6684680 | tf_op jit(solution)/shard_map/ppermute | solution.py:47
  84.7 14.4 %collective-permute-start.5 = (bf16[256,1024]{1,0:T(8,128)(2,1)S(1)}, bf16[256,1024]{1,0:T(8,128)(2,1)S(1)}, u32[]{:S(2)}, u32[]{:S(2)}) collective-permute-start(bf16[256,1024]{1,0:T(8,128)(2,1)S(1)} %get-tuple-element.182), channel_id=1, source_target_pairs={{0,1},{1,0},{2,3},{3,2},{4,5},{5,4},{6,7},{7,6},{8,9},{9,8},{10,11... | collective-permute-start | bytes 1572872 | tf_op jit(solution)/shard_map/ppermute | solution.py:60
  85.3 14.5 %collective-permute-start.6 = (bf16[256,1024]{1,0:T(8,128)(2,1)S(1)}, bf16[256,1024]{1,0:T(8,128)(2,1)S(1)}, u32[]{:S(2)}, u32[]{:S(2)}) collective-permute-start(bf16[256,1024]{1,0:T(8,128)(2,1)S(1)} %get-tuple-element.182), channel_id=1, source_target_pairs={{0,2},{2,0},{1,3},{3,1},{4,6},{6,4},{5,7},{7,5},{8,10},{10,8},{9,1... | collective-permute-start | bytes 1572872 | tf_op jit(solution)/shard_map/ppermute | solution.py:61
  99.1 7.9 %collective-permute-start.7 = (bf16[128,1024]{1,0:T(8,128)(2,1)S(1)}, bf16[128,1024]{1,0:T(8,128)(2,1)S(1)}, u32[]{:S(2)}, u32[]{:S(2)}) collective-permute-start(bf16[128,1024]{1,0:T(8,128)(2,1)S(1)} %slice.710), channel_id=1, source_target_pairs={{0,2},{2,0},{1,3},{3,1},{4,6},{6,4},{5,7},{7,5},{8,10},{10,8},{9,1... | collective-permute-start | bytes 786440 | tf_op jit(solution)/shard_map/ppermute | solution.py:62
  99.9 7.6 %collective-permute-start.8 = (bf16[128,1024]{1,0:T(8,128)(2,1)S(1)}, bf16[128,1024]{1,0:T(8,128)(2,1)S(1)}, u32[]{:S(2)}, u32[]{:S(2)}) collective-permute-start(bf16[128,1024]{1,0:T(8,128)(2,1)S(1)} %slice.711), channel_id=1, source_target_pairs={{0,1},{1,0},{2,3},{3,2},{4,5},{5,4},{6,7},{7,6},{8,9},{9,8},{10,11... | collective-permute-start | bytes 786440 | tf_op jit(solution)/shard_map/ppermute | solution.py:63
  122.9 15.9 %collective-permute-start.17 = (bf16[256,1024]{1,0:T(8,128)(2,1)S(1)}, bf16[256,1024]{1,0:T(8,128)(2,1)S(1)}, u32[]{:S(2)}, u32[]{:S(2)}) collective-permute-start(bf16[256,1024]{1,0:T(8,128)(2,1)S(1)} %multiply_convert_fusion), channel_id=1, source_target_pairs={{0,24},{8,0},{16,8},{24,16},{1,25},{9,1},{17,9},{25,17},{2,26},{10... | collective-permute-start | bytes 1572872 | tf_op jit(solution)/shard_map/ppermute | solution.py:51
  127.8 44.7 %collective-permute-start.22 = (bf16[2,768,512]{2,1,0:T(8,128)(2,1)S(1)}, bf16[2,768,512]{2,1,0:T(8,128)(2,1)S(1)}, u32[]{:S(2)}, u32[]{:S(2)}) collective-permute-start(bf16[2,768,512]{2,1,0:T(8,128)(2,1)S(1)} %get-tuple-element.36.refs_6_), channel_id=1, source_target_pairs={{0,1},{1,0},{2,3},{3,2},{4,5},{5,4},{6,7},{7,6},{8,9},{9,8},{10,11... | collective-permute-start | bytes 4718600 | tf_op jit(solution)/shard_map/ppermute | solution.py:60
  128.8 41.1 %collective-permute-start.18 = (bf16[256,1024]{1,0:T(8,128)(2,1)S(1)}, bf16[256,1024]{1,0:T(8,128)(2,1)S(1)}, u32[]{:S(2)}, u32[]{:S(2)}) collective-permute-start(bf16[256,1024]{1,0:T(8,128)(2,1)S(1)} %multiply_convert_fusion), channel_id=1, source_target_pairs={{0,16},{8,24},{16,0},{24,8},{1,17},{9,25},{17,1},{25,9},{2,18},{10... | collective-permute-start | bytes 1572872 | tf_op jit(solution)/shard_map/ppermute | solution.py:51
  128.8 41.1 %collective-permute-start.19 = (bf16[256,1024]{1,0:T(8,128)(2,1)S(1)}, bf16[256,1024]{1,0:T(8,128)(2,1)S(1)}, u32[]{:S(2)}, u32[]{:S(2)}) collective-permute-start(bf16[256,1024]{1,0:T(8,128)(2,1)S(1)} %multiply_convert_fusion), channel_id=1, source_target_pairs={{0,8},{8,16},{16,24},{24,0},{1,9},{9,17},{17,25},{25,1},{2,10},{10... | collective-permute-start | bytes 1572872 | tf_op jit(solution)/shard_map/ppermute | solution.py:51
  138.8 35.6 %collective-permute-start.23 = (bf16[2,768,512]{2,1,0:T(8,128)(2,1)S(1)}, bf16[2,768,512]{2,1,0:T(8,128)(2,1)S(1)}, u32[]{:S(2)}, u32[]{:S(2)}) collective-permute-start(bf16[2,768,512]{2,1,0:T(8,128)(2,1)S(1)} %get-tuple-element.36.refs_6_), channel_id=1, source_target_pairs={{0,2},{2,0},{1,3},{3,1},{4,6},{6,4},{5,7},{7,5},{8,10},{10,8},{9,1... | collective-permute-start | bytes 4718600 | tf_op jit(solution)/shard_map/ppermute | solution.py:61
  171.5 57.2 %collective-permute-start.21 = (bf16[4,256,1024]{2,1,0:T(8,128)(2,1)}, bf16[4,256,1024]{2,1,0:T(8,128)(2,1)}, u32[]{:S(2)}, u32[]{:S(2)}) collective-permute-start(bf16[4,256,1024]{2,1,0:T(8,128)(2,1)} %pad_maximum_fusion.9.rest_0_), channel_id=1, source_target_pairs={{0,4},{4,0},{1,5},{5,1},{2,6},{6,2},{3,7},{7,3},{8,12},{12,8},{9,1... | collective-permute-start | bytes 6291464 | tf_op jit(solution)/shard_map/ppermute | solution.py:47
  171.5 85.2 %collective-permute-start.26 = (bf16[2,768,512]{2,1,0:T(8,128)(2,1)}, bf16[2,768,512]{2,1,0:T(8,128)(2,1)}, u32[]{:S(2)}, u32[]{:S(2)}) collective-permute-start(bf16[2,768,512]{2,1,0:T(8,128)(2,1)} %get-tuple-element.38.refs_6_), channel_id=1, source_target_pairs={{0,1},{1,0},{2,3},{3,2},{4,5},{5,4},{6,7},{7,6},{8,9},{9,8},{10,11... | collective-permute-start | bytes 4718600 | tf_op jit(solution)/shard_map/ppermute | solution.py:60
  172.4 87.0 %collective-permute-start.27 = (bf16[2,768,512]{2,1,0:T(8,128)(2,1)}, bf16[2,768,512]{2,1,0:T(8,128)(2,1)}, u32[]{:S(2)}, u32[]{:S(2)}) collective-permute-start(bf16[2,768,512]{2,1,0:T(8,128)(2,1)} %get-tuple-element.38.refs_6_), channel_id=1, source_target_pairs={{0,2},{2,0},{1,3},{3,1},{4,6},{6,4},{5,7},{7,5},{8,10},{10,8},{9,1... | collective-permute-start | bytes 4718600 | tf_op jit(solution)/shard_map/ppermute | solution.py:61
  174.4 51.7 %collective-permute-start.24 = (bf16[1,768,512]{2,1,0:T(8,128)(2,1)}, bf16[1,768,512]{2,1,0:T(8,128)(2,1)}, u32[]{:S(2)}, u32[]{:S(2)}) collective-permute-start(bf16[1,768,512]{2,1,0:T(8,128)(2,1)} %slice.748), channel_id=1, source_target_pairs={{0,2},{2,0},{1,3},{3,1},{4,6},{6,4},{5,7},{7,5},{8,10},{10,8},{9,1... | collective-permute-start | bytes 2359304 | tf_op jit(solution)/shard_map/ppermute | solution.py:62
  176.3 49.8 %collective-permute-start.25 = (bf16[1,768,512]{2,1,0:T(8,128)(2,1)}, bf16[1,768,512]{2,1,0:T(8,128)(2,1)S(1)}, u32[]{:S(2)}, u32[]{:S(2)}) collective-permute-start(bf16[1,768,512]{2,1,0:T(8,128)(2,1)} %slice.749), channel_id=1, source_target_pairs={{0,1},{1,0},{2,3},{3,2},{4,5},{5,4},{6,7},{7,6},{8,9},{9,8},{10,11... | collective-permute-start | bytes 2359304 | tf_op jit(solution)/shard_map/ppermute | solution.py:63
  255.6 89.1 %collective-permute-start.66 = (bf16[2,1,768,512]{3,2,1,0:T(8,128)(2,1)}, bf16[2,1,768,512]{3,2,1,0:T(8,128)(2,1)S(1)}, u32[]{:S(2)}, u32[]{:S(2)}) collective-permute-start(bf16[2,1,768,512]{3,2,1,0:T(8,128)(2,1)} %get-tuple-element.43), channel_id=1, source_target_pairs={{0,1},{1,0},{2,3},{3,2},{4,5},{5,4},{6,7},{7,6},{8,9},{9,8},{10,11... | collective-permute-start | bytes 4718600 | tf_op jit(solution)/shard_map/ppermute | solution.py:68
  257.9 20.5 %collective-permute-start.28 = (bf16[1,768,512]{2,1,0:T(8,128)(2,1)S(1)}, bf16[1,768,512]{2,1,0:T(8,128)(2,1)S(1)}, u32[]{:S(2)}, u32[]{:S(2)}) collective-permute-start(bf16[1,768,512]{2,1,0:T(8,128)(2,1)S(1)} %slice.751), channel_id=1, source_target_pairs={{0,2},{2,0},{1,3},{3,1},{4,6},{6,4},{5,7},{7,5},{8,10},{10,8},{9,1... | collective-permute-start | bytes 2359304 | tf_op jit(solution)/shard_map/ppermute | solution.py:62
  260.6 47.8 %collective-permute-start.29 = (bf16[1,768,512]{2,1,0:T(8,128)(2,1)S(1)}, bf16[1,768,512]{2,1,0:T(8,128)(2,1)S(1)}, u32[]{:S(2)}, u32[]{:S(2)}) collective-permute-start(bf16[1,768,512]{2,1,0:T(8,128)(2,1)S(1)} %slice.752), channel_id=1, source_target_pairs={{0,1},{1,0},{2,3},{3,2},{4,5},{5,4},{6,7},{7,6},{8,9},{9,8},{10,11... | collective-permute-start | bytes 2359304 | tf_op jit(solution)/shard_map/ppermute | solution.py:63
  261.2 100.8 %collective-permute-start.68 = (bf16[2,1,768,512]{3,2,1,0:T(8,128)(2,1)}, bf16[2,1,768,512]{3,2,1,0:T(8,128)(2,1)}, u32[]{:S(2)}, u32[]{:S(2)}) collective-permute-start(bf16[2,1,768,512]{3,2,1,0:T(8,128)(2,1)} %get-tuple-element.45), channel_id=1, source_target_pairs={{0,2},{2,0},{1,3},{3,1},{4,6},{6,4},{5,7},{7,5},{8,10},{10,8},{9,1... | collective-permute-start | bytes 4718600 | tf_op jit(solution)/shard_map/ppermute | solution.py:69
  332.2 35.3 %collective-permute-start.70 = (bf16[2,1,768,512]{3,2,1,0:T(8,128)(2,1)}, bf16[2,1,768,512]{3,2,1,0:T(8,128)(2,1)}, u32[]{:S(2)}, u32[]{:S(2)}) collective-permute-start(bf16[2,1,768,512]{3,2,1,0:T(8,128)(2,1)} %get-tuple-element.47), channel_id=1, source_target_pairs={{0,1},{1,0},{2,3},{3,2},{4,5},{5,4},{6,7},{7,6},{8,9},{9,8},{10,11... | collective-permute-start | bytes 4718600 | tf_op jit(solution)/shard_map/ppermute | solution.py:68
  338.1 40.4 %collective-permute-start.30 = (bf16[4,256,1024]{2,1,0:T(8,128)(2,1)}, bf16[4,256,1024]{2,1,0:T(8,128)(2,1)}, u32[]{:S(2)}, u32[]{:S(2)}) collective-permute-start(bf16[4,256,1024]{2,1,0:T(8,128)(2,1)} %combine.5), channel_id=1, source_target_pairs={{0,4},{4,0},{1,5},{5,1},{2,6},{6,2},{3,7},{7,3},{8,12},{12,8},{9,1... | collective-permute-start | bytes 6291464 | tf_op jit(solution)/shard_map/ppermute | solution.py:47
  338.1 37.6 %collective-permute-start.72 = (bf16[2,1,768,512]{3,2,1,0:T(8,128)(2,1)}, bf16[2,1,768,512]{3,2,1,0:T(8,128)(2,1)}, u32[]{:S(2)}, u32[]{:S(2)}) collective-permute-start(bf16[2,1,768,512]{3,2,1,0:T(8,128)(2,1)} %get-tuple-element.49), channel_id=1, source_target_pairs={{0,2},{2,0},{1,3},{3,1},{4,6},{6,4},{5,7},{7,5},{8,10},{10,8},{9,1... | collective-permute-start | bytes 4718600 | tf_op jit(solution)/shard_map/ppermute | solution.py:69
  344.7 38.2 %collective-permute-start.34 = (bf16[4,256,1152]{2,1,0:T(8,128)(2,1)}, bf16[4,256,1152]{2,1,0:T(8,128)(2,1)}, u32[]{:S(2)}, u32[]{:S(2)}) collective-permute-start(bf16[4,256,1152]{2,1,0:T(8,128)(2,1)} %combine.7), channel_id=1, source_target_pairs={{0,4},{4,0},{1,5},{5,1},{2,6},{6,2},{3,7},{7,3},{8,12},{12,8},{9,1... | collective-permute-start | bytes 7077896 | tf_op jit(solution)/shard_map/ppermute | solution.py:47
  362.1 30.4 %collective-permute-start.67 = (bf16[1,768,512]{2,1,0:T(8,128)(2,1)S(1)}, bf16[1,768,512]{2,1,0:T(8,128)(2,1)S(1)}, u32[]{:S(2)}, u32[]{:S(2)}) collective-permute-start(bf16[1,768,512]{2,1,0:T(8,128)(2,1)S(1)} %fusion.134), channel_id=1, source_target_pairs={{0,2},{2,0},{1,3},{3,1},{4,6},{6,4},{5,7},{7,5},{8,10},{10,8},{9,1... | collective-permute-start | bytes 2359304 | tf_op jit(solution)/shard_map/ppermute | solution.py:72
  367.5 29.5 %collective-permute-start.69 = (bf16[1,768,512]{2,1,0:T(8,128)(2,1)S(1)}, bf16[1,768,512]{2,1,0:T(8,128)(2,1)S(1)}, u32[]{:S(2)}, u32[]{:S(2)}) collective-permute-start(bf16[1,768,512]{2,1,0:T(8,128)(2,1)S(1)} %fusion.135), channel_id=1, source_target_pairs={{0,1},{1,0},{2,3},{3,2},{4,5},{5,4},{6,7},{7,6},{8,9},{9,8},{10,11... | collective-permute-start | bytes 2359304 | tf_op jit(solution)/shard_map/ppermute | solution.py:73
  375.7 33.1 %collective-permute-start.71 = (bf16[1,768,512]{2,1,0:T(8,128)(2,1)S(1)}, bf16[1,768,512]{2,1,0:T(8,128)(2,1)S(1)}, u32[]{:S(2)}, u32[]{:S(2)}) collective-permute-start(bf16[1,768,512]{2,1,0:T(8,128)(2,1)S(1)} %fusion.136), channel_id=1, source_target_pairs={{0,2},{2,0},{1,3},{3,1},{4,6},{6,4},{5,7},{7,5},{8,10},{10,8},{9,1... | collective-permute-start | bytes 2359304 | tf_op jit(solution)/shard_map/ppermute | solution.py:72
  378.6 36.0 %collective-permute-start.73 = (bf16[1,768,512]{2,1,0:T(8,128)(2,1)S(1)}, bf16[1,768,512]{2,1,0:T(8,128)(2,1)S(1)}, u32[]{:S(2)}, u32[]{:S(2)}) collective-permute-start(bf16[1,768,512]{2,1,0:T(8,128)(2,1)S(1)} %fusion.137), channel_id=1, source_target_pairs={{0,1},{1,0},{2,3},{3,2},{4,5},{5,4},{6,7},{7,6},{8,9},{9,8},{10,11... | collective-permute-start | bytes 2359304 | tf_op jit(solution)/shard_map/ppermute | solution.py:73
  382.9 76.5 %collective-permute-start.31 = (bf16[256,1024]{1,0:T(8,128)(2,1)}, bf16[256,1024]{1,0:T(8,128)(2,1)}, u32[]{:S(2)}, u32[]{:S(2)}) collective-permute-start(bf16[256,1024]{1,0:T(8,128)(2,1)} %get-tuple-element.133), channel_id=1, source_target_pairs={{0,8},{8,16},{16,24},{24,0},{1,9},{9,17},{17,25},{25,1},{2,10},{10... | collective-permute-start | bytes 1572872 | tf_op jit(solution)/shard_map/ppermute | solution.py:51
  392.5 66.9 %collective-permute-start.32 = (bf16[256,1024]{1,0:T(8,128)(2,1)}, bf16[256,1024]{1,0:T(8,128)(2,1)S(1)}, u32[]{:S(2)}, u32[]{:S(2)}) collective-permute-start(bf16[256,1024]{1,0:T(8,128)(2,1)} %get-tuple-element.135), channel_id=1, source_target_pairs={{0,16},{8,24},{16,0},{24,8},{1,17},{9,25},{17,1},{25,9},{2,18},{10... | collective-permute-start | bytes 1572872 | tf_op jit(solution)/shard_map/ppermute | solution.py:51
  397.0 25.8 %collective-permute-start.35 = (bf16[256,1152]{1,0:T(8,128)(2,1)}, bf16[256,1152]{1,0:T(8,128)(2,1)S(1)}, u32[]{:S(2)}, u32[]{:S(2)}) collective-permute-start(bf16[256,1152]{1,0:T(8,128)(2,1)} %get-tuple-element.124), channel_id=1, source_target_pairs={{0,8},{8,16},{16,24},{24,0},{1,9},{9,17},{17,25},{25,1},{2,10},{10... | collective-permute-start | bytes 1769480 | tf_op jit(solution)/shard_map/ppermute | solution.py:51
  408.9 49.2 %collective-permute-start.36 = (bf16[256,1152]{1,0:T(8,128)(2,1)}, bf16[256,1152]{1,0:T(8,128)(2,1)S(1)}, u32[]{:S(2)}, u32[]{:S(2)}) collective-permute-start(bf16[256,1152]{1,0:T(8,128)(2,1)} %get-tuple-element.126), channel_id=1, source_target_pairs={{0,16},{8,24},{16,0},{24,8},{1,17},{9,25},{17,1},{25,9},{2,18},{10... | collective-permute-start | bytes 1769480 | tf_op jit(solution)/shard_map/ppermute | solution.py:51
  414.5 43.5 %collective-permute-start.37 = (bf16[256,1152]{1,0:T(8,128)(2,1)}, bf16[256,1152]{1,0:T(8,128)(2,1)S(1)}, u32[]{:S(2)}, u32[]{:S(2)}) collective-permute-start(bf16[256,1152]{1,0:T(8,128)(2,1)} %get-tuple-element.125), channel_id=1, source_target_pairs={{0,24},{8,0},{16,8},{24,16},{1,25},{9,1},{17,9},{25,17},{2,26},{10... | collective-permute-start | bytes 1769480 | tf_op jit(solution)/shard_map/ppermute | solution.py:51
  422.9 56.8 %collective-permute-start.33 = (bf16[256,1024]{1,0:T(8,128)(2,1)S(1)}, bf16[256,1024]{1,0:T(8,128)(2,1)S(1)}, u32[]{:S(2)}, u32[]{:S(2)}) collective-permute-start(bf16[256,1024]{1,0:T(8,128)(2,1)S(1)} %get-tuple-element.134), channel_id=1, source_target_pairs={{0,24},{8,0},{16,8},{24,16},{1,25},{9,1},{17,9},{25,17},{2,26},{10... | collective-permute-start | bytes 1572872 | tf_op jit(solution)/shard_map/ppermute | solution.py:51
  533.9 15.5 %collective-permute-start.38 = (bf16[2,128,1024]{1,2,0:T(8,128)(2,1)}, bf16[2,128,1024]{1,2,0:T(8,128)(2,1)}, u32[]{:S(2)}, u32[]{:S(2)}) collective-permute-start(bf16[2,128,1024]{1,2,0:T(8,128)(2,1)} %pad_maximum_fusion.17), channel_id=1, source_target_pairs={{0,1},{1,0},{2,3},{3,2},{4,5},{5,4},{6,7},{7,6},{8,9},{9,8},{10,11... | collective-permute-start | bytes 1572872 | tf_op jit(solution)/shard_map/ppermute | solution.py:68
  542.7 22.0 %collective-permute-start.50 = (bf16[4,128,1024]{2,1,0:T(8,128)(2,1)}, bf16[4,128,1024]{2,1,0:T(8,128)(2,1)}, u32[]{:S(2)}, u32[]{:S(2)}) collective-permute-start(bf16[4,128,1024]{2,1,0:T(8,128)(2,1)} %dynamic-slice_bitcast_fusion.2), channel_id=1, source_target_pairs={{0,4},{4,0},{1,5},{5,1},{2,6},{6,2},{3,7},{7,3},{8,12},{12,8},{9,1... | collective-permute-start | bytes 3145736 | tf_op jit(solution)/shard_map/ppermute | solution.py:47
  542.8 15.0 %collective-permute-start.40 = (bf16[2,128,1024]{1,2,0:T(8,128)(2,1)S(1)}, bf16[2,128,1024]{1,2,0:T(8,128)(2,1)}, u32[]{:S(2)}, u32[]{:S(2)}) collective-permute-start(bf16[2,128,1024]{1,2,0:T(8,128)(2,1)S(1)} %pad_maximum_fusion.18), channel_id=1, source_target_pairs={{0,2},{2,0},{1,3},{3,1},{4,6},{6,4},{5,7},{7,5},{8,10},{10,8},{9,1... | collective-permute-start | bytes 1572872 | tf_op jit(solution)/shard_map/ppermute | solution.py:69
  550.7 12.2 %collective-permute-start.39 = (bf16[128,1024]{0,1:T(8,128)(2,1)S(1)}, bf16[128,1024]{0,1:T(8,128)(2,1)S(1)}, u32[]{:S(2)}, u32[]{:S(2)}) collective-permute-start(bf16[128,1024]{0,1:T(8,128)(2,1)S(1)} %fusion.142), channel_id=1, source_target_pairs={{0,2},{2,0},{1,3},{3,1},{4,6},{6,4},{5,7},{7,5},{8,10},{10,8},{9,1... | collective-permute-start | bytes 786440 | tf_op jit(solution)/shard_map/ppermute | solution.py:72
  554.7 31.1 %collective-permute-start.58 = (bf16[4,128,1152]{2,1,0:T(8,128)(2,1)}, bf16[4,128,1152]{2,1,0:T(8,128)(2,1)}, u32[]{:S(2)}, u32[]{:S(2)}) collective-permute-start(bf16[4,128,1152]{2,1,0:T(8,128)(2,1)} %dynamic-slice_bitcast_fusion), channel_id=1, source_target_pairs={{0,4},{4,0},{1,5},{5,1},{2,6},{6,2},{3,7},{7,3},{8,12},{12,8},{9,1... | collective-permute-start | bytes 3538952 | tf_op jit(solution)/shard_map/ppermute | solution.py:47
  564.2 9.1 %collective-permute-start.41 = (bf16[128,1024]{0,1:T(8,128)(2,1)S(1)}, bf16[128,1024]{0,1:T(8,128)(2,1)S(1)}, u32[]{:S(2)}, u32[]{:S(2)}) collective-permute-start(bf16[128,1024]{0,1:T(8,128)(2,1)S(1)} %get-tuple-element.128), channel_id=1, source_target_pairs={{0,1},{1,0},{2,3},{3,2},{4,5},{5,4},{6,7},{7,6},{8,9},{9,8},{10,11... | collective-permute-start | bytes 786440 | tf_op jit(solution)/shard_map/ppermute | solution.py:73
  567.3 21.4 %collective-permute-start.53 = (bf16[2,64,1024]{2,1,0:T(8,128)(2,1)}, bf16[2,64,1024]{2,1,0:T(8,128)(2,1)}, u32[]{:S(2)}, u32[]{:S(2)}) collective-permute-start(bf16[2,64,1024]{2,1,0:T(8,128)(2,1)} %pad_maximum_fusion.27), channel_id=1, source_target_pairs={{0,2},{2,0},{1,3},{3,1},{4,6},{6,4},{5,7},{7,5},{8,10},{10,8},{9,1... | collective-permute-start | bytes 786440 | tf_op jit(solution)/shard_map/ppermute | solution.py:69
  569.1 19.6 %collective-permute-start.51 = (bf16[2,64,1024]{2,1,0:T(8,128)(2,1)}, bf16[2,64,1024]{2,1,0:T(8,128)(2,1)}, u32[]{:S(2)}, u32[]{:S(2)}) collective-permute-start(bf16[2,64,1024]{2,1,0:T(8,128)(2,1)} %pad_maximum_fusion.26), channel_id=1, source_target_pairs={{0,1},{1,0},{2,3},{3,2},{4,5},{5,4},{6,7},{7,6},{8,9},{9,8},{10,11... | collective-permute-start | bytes 786440 | tf_op jit(solution)/shard_map/ppermute | solution.py:68
  587.8 8.2 %collective-permute-start.61 = (bf16[2,64,1152]{2,1,0:T(8,128)(2,1)S(1)}, bf16[2,64,1152]{2,1,0:T(8,128)(2,1)S(1)}, u32[]{:S(2)}, u32[]{:S(2)}) collective-permute-start(bf16[2,64,1152]{2,1,0:T(8,128)(2,1)S(1)} %pad_maximum_fusion.23), channel_id=1, source_target_pairs={{0,2},{2,0},{1,3},{3,1},{4,6},{6,4},{5,7},{7,5},{8,10},{10,8},{9,1... | collective-permute-start | bytes 884744 | tf_op jit(solution)/shard_map/ppermute | solution.py:69
  587.9 8.1 %collective-permute-start.59 = (bf16[2,64,1152]{2,1,0:T(8,128)(2,1)S(1)}, bf16[2,64,1152]{2,1,0:T(8,128)(2,1)S(1)}, u32[]{:S(2)}, u32[]{:S(2)}) collective-permute-start(bf16[2,64,1152]{2,1,0:T(8,128)(2,1)S(1)} %pad_maximum_fusion.22), channel_id=1, source_target_pairs={{0,1},{1,0},{2,3},{3,2},{4,5},{5,4},{6,7},{7,6},{8,9},{9,8},{10,11... | collective-permute-start | bytes 884744 | tf_op jit(solution)/shard_map/ppermute | solution.py:68
  588.6 28.1 %collective-permute-start.42 = (bf16[4,128,1152]{2,1,0:T(8,128)(2,1)S(1)}, bf16[4,128,1152]{2,1,0:T(8,128)(2,1)S(1)}, u32[]{:S(2)}, u32[]{:S(2)}) collective-permute-start(bf16[4,128,1152]{2,1,0:T(8,128)(2,1)S(1)} %dynamic-slice_bitcast_fusion.1), channel_id=1, source_target_pairs={{0,4},{4,0},{1,5},{5,1},{2,6},{6,2},{3,7},{7,3},{8,12},{12,8},{9,1... | collective-permute-start | bytes 3538952 | tf_op jit(solution)/shard_map/ppermute | solution.py:47
  589.9 8.8 %collective-permute-start.52 = (bf16[64,1024]{1,0:T(8,128)(2,1)S(1)}, bf16[64,1024]{1,0:T(8,128)(2,1)S(1)}, u32[]{:S(2)}, u32[]{:S(2)}) collective-permute-start(bf16[64,1024]{1,0:T(8,128)(2,1)S(1)} %get-tuple-element.158), channel_id=1, source_target_pairs={{0,2},{2,0},{1,3},{3,1},{4,6},{6,4},{5,7},{7,5},{8,10},{10,8},{9,1... | collective-permute-start | bytes 393224 | tf_op jit(solution)/shard_map/ppermute | solution.py:72
  596.1 8.3 %collective-permute-start.60 = (bf16[64,1152]{1,0:T(8,128)(2,1)S(1)}, bf16[64,1152]{1,0:T(8,128)(2,1)S(1)}, u32[]{:S(2)}, u32[]{:S(2)}) collective-permute-start(bf16[64,1152]{1,0:T(8,128)(2,1)S(1)} %get-tuple-element.138), channel_id=1, source_target_pairs={{0,2},{2,0},{1,3},{3,1},{4,6},{6,4},{5,7},{7,5},{8,10},{10,8},{9,1... | collective-permute-start | bytes 442376 | tf_op jit(solution)/shard_map/ppermute | solution.py:72
  599.9 11.6 %collective-permute-start.55 = (bf16[128,1024]{1,0:T(8,128)(2,1)S(1)}, bf16[128,1024]{1,0:T(8,128)(2,1)S(1)}, u32[]{:S(2)}, u32[]{:S(2)}) collective-permute-start(bf16[128,1024]{1,0:T(8,128)(2,1)S(1)} %fusion.148), channel_id=1, source_target_pairs={{0,8},{8,0},{16,24},{24,16},{1,9},{9,1},{17,25},{25,17},{2,10},{10... | collective-permute-start | bytes 786440 | tf_op jit(solution)/shard_map/ppermute | solution.py:448
  604.5 15.0 %collective-permute-start.63 = (bf16[128,1152]{1,0:T(8,128)(2,1)S(1)}, bf16[128,1152]{1,0:T(8,128)(2,1)S(1)}, u32[]{:S(2)}, u32[]{:S(2)}) collective-permute-start(bf16[128,1152]{1,0:T(8,128)(2,1)S(1)} %fusion.146), channel_id=1, source_target_pairs={{0,8},{8,0},{16,24},{24,16},{1,9},{9,1},{17,25},{25,17},{2,10},{10... | collective-permute-start | bytes 884744 | tf_op jit(solution)/shard_map/ppermute | solution.py:448
  611.5 22.3 %collective-permute-start.56 = (bf16[128,1024]{1,0:T(8,128)(2,1)S(1)}, bf16[128,1024]{1,0:T(8,128)(2,1)S(1)}, u32[]{:S(2)}, u32[]{:S(2)}) collective-permute-start(bf16[128,1024]{1,0:T(8,128)(2,1)S(1)} %fusion.151), channel_id=1, source_target_pairs={{0,16},{8,24},{16,0},{24,8},{1,17},{9,25},{17,1},{25,9},{2,18},{10... | collective-permute-start | bytes 786440 | tf_op jit(solution)/shard_map/ppermute | solution.py:448
  617.1 17.0 %collective-permute-start.45 = (bf16[2,64,1152]{2,1,0:T(8,128)(2,1)S(1)}, bf16[2,64,1152]{2,1,0:T(8,128)(2,1)S(1)}, u32[]{:S(2)}, u32[]{:S(2)}) collective-permute-start(bf16[2,64,1152]{2,1,0:T(8,128)(2,1)S(1)} %pad_maximum_fusion.21), channel_id=1, source_target_pairs={{0,2},{2,0},{1,3},{3,1},{4,6},{6,4},{5,7},{7,5},{8,10},{10,8},{9,1... | collective-permute-start | bytes 884744 | tf_op jit(solution)/shard_map/ppermute | solution.py:69
  618.8 15.3 %collective-permute-start.43 = (bf16[2,64,1152]{2,1,0:T(8,128)(2,1)S(1)}, bf16[2,64,1152]{2,1,0:T(8,128)(2,1)S(1)}, u32[]{:S(2)}, u32[]{:S(2)}) collective-permute-start(bf16[2,64,1152]{2,1,0:T(8,128)(2,1)S(1)} %pad_maximum_fusion.20), channel_id=1, source_target_pairs={{0,1},{1,0},{2,3},{3,2},{4,5},{5,4},{6,7},{7,6},{8,9},{9,8},{10,11... | collective-permute-start | bytes 884744 | tf_op jit(solution)/shard_map/ppermute | solution.py:68
  619.6 18.7 %collective-permute-start.64 = (bf16[128,1152]{1,0:T(8,128)(2,1)S(1)}, bf16[128,1152]{1,0:T(8,128)(2,1)S(1)}, u32[]{:S(2)}, u32[]{:S(2)}) collective-permute-start(bf16[128,1152]{1,0:T(8,128)(2,1)S(1)} %fusion.150), channel_id=1, source_target_pairs={{0,16},{8,24},{16,0},{24,8},{1,17},{9,25},{17,1},{25,9},{2,18},{10... | collective-permute-start | bytes 884744 | tf_op jit(solution)/shard_map/ppermute | solution.py:448
  638.3 12.7 %collective-permute-start.65 = (bf16[128,1152]{1,0:T(8,128)(2,1)S(1)}, bf16[128,1152]{1,0:T(8,128)(2,1)S(1)}, u32[]{:S(2)}, u32[]{:S(2)}) collective-permute-start(bf16[128,1152]{1,0:T(8,128)(2,1)S(1)} %add_convert_fusion.4), channel_id=1, source_target_pairs={{0,4},{4,0},{1,5},{5,1},{2,6},{6,2},{3,7},{7,3},{8,12},{12,8},{9,1... | collective-permute-start | bytes 884744 | tf_op jit(solution)/shard_map/ppermute | solution.py:47
  641.1 8.6 %collective-permute-start.47 = (bf16[128,1152]{1,0:T(8,128)(2,1)S(1)}, bf16[128,1152]{1,0:T(8,128)(2,1)S(1)}, u32[]{:S(2)}, u32[]{:S(2)}) collective-permute-start(bf16[128,1152]{1,0:T(8,128)(2,1)S(1)} %fusion.147), channel_id=1, source_target_pairs={{0,8},{8,0},{16,24},{24,16},{1,9},{9,1},{17,25},{25,17},{2,10},{10... | collective-permute-start | bytes 884744 | tf_op jit(solution)/shard_map/ppermute | solution.py:448
  649.7 14.9 %collective-permute-start.48 = (bf16[128,1152]{1,0:T(8,128)(2,1)S(1)}, bf16[128,1152]{1,0:T(8,128)(2,1)S(1)}, u32[]{:S(2)}, u32[]{:S(2)}) collective-permute-start(bf16[128,1152]{1,0:T(8,128)(2,1)S(1)} %fusion.149), channel_id=1, source_target_pairs={{0,16},{8,24},{16,0},{24,8},{1,17},{9,25},{17,1},{25,9},{2,18},{10... | collective-permute-start | bytes 884744 | tf_op jit(solution)/shard_map/ppermute | solution.py:448
  (115 other events, 883.1 us)

commit v3 on v2

--- a/solution.py
+++ b/solution.py
@@ -412,6 +412,275 @@
     return results[0], results[1], results[2:]
 
 
+NT = (((1,), (1,)), ((), ()))
+TN = (((0,), (0,)), ((), ()))
+GROUPS = KVH // 2
+EXTRA = 128
+
+
+def turn(vectors, cosine, sine):
+    lane = lax.broadcasted_iota(jnp.int32, vectors.shape, 1)
+    ahead = pltpu.roll(vectors, 2 * HD - HD // 2, 1)
+    behind = pltpu.roll(vectors, HD // 2, 1)
+    return vectors * cosine + jnp.where(lane % HD < HD // 2, ahead, behind) * sine
+
+
+def turn_tables(places):
+    lane = jnp.arange(2 * HD, dtype=jnp.int32)
+    frequency = jnp.exp(
+        (lane % (HD // 2)).astype(F32) * (-2.0 * math.log(ROPE_BASE) / HD)
+    )
+    angles = places[:, None] * frequency[None, :]
+    sign = jnp.where(lane % HD < HD // 2, -1.0, 1.0)
+    return jnp.cos(angles), jnp.sin(angles) * sign[None, :]
+
+
+def attention_forward(x_all, head_full, bias, cosine, sine, tok_rows):
+    seq_len, width = x_all.shape
+    scale = HD ** (-0.5)
+    wide, narrow = H * HD, KVH * HD
+
+    def kernel(
+        x_ref, tail_ref, wq_ref, wk_ref, wv_ref, bias_ref, cos_ref, sin_ref,
+        normed_ref, q_out, k_out, v_out, att_out, total_out, misc_out,
+    ):
+        @pl.when(pl.program_id(0) == 0)
+        def _():
+            rows = jnp.transpose(tail_ref[...].astype(F32))
+            misc_out[...] = rows
+            x = x_ref[...].astype(F32)
+            scaled = x * lax.rsqrt(jnp.mean(x * x, axis=1, keepdims=True) + EPSILON)
+            normed_ref[...] = (scaled * rows[EXPERTS : EXPERTS + 1, :]).astype(B16)
+
+        normed = normed_ref[...]
+        cos, sin = cos_ref[...], sin_ref[...]
+        key = turn(jnp.dot(normed, wk_ref[...], preferred_element_type=F32), cos, sin).astype(B16)
+        value = jnp.dot(normed, wv_ref[...], preferred_element_type=F32).astype(B16)
+        query = jnp.dot(normed[:tok_rows], wq_ref[...], preferred_element_type=F32)
+        cos, sin = cos[:tok_rows], sin[:tok_rows]
+        query = jnp.concatenate(
+            [turn(query[:, 128 * j : 128 * (j + 1)], cos, sin) for j in range(2)], axis=1
+        )
+        query = (query * scale).astype(B16)
+        k_out[...] = key
+        v_out[...] = value
+        q_out[...] = query
+        mixed, totals = [], []
+        for j in range(4):
+            lanes = slice(HD * (j // 2), HD * (j // 2 + 1))
+            scores = lax.dot_general(
+                key[:, lanes], query[:, HD * j : HD * (j + 1)], NT, preferred_element_type=F32
+            )
+            scores = scores + bias_ref[...]
+            peak = jnp.max(scores, axis=0, keepdims=True)
+            probs = jnp.exp(scores - peak)
+            total = jnp.sum(probs, axis=0, keepdims=True)
+            out = lax.dot_general(
+                value[:, lanes], probs.astype(B16), TN, preferred_element_type=F32
+            )
+            mixed.append(out / total)
+            totals.append(peak + jnp.log(total))
+        att_out[...] = jnp.transpose(jnp.concatenate(mixed, axis=0)).astype(B16)
+        total_out[0] = jnp.concatenate(totals + totals, axis=0)
+
+    def fixed(*block):
+        return pl.BlockSpec(block, lambda i: (0,) * len(block))
+
+    def columns(rows, cols, lead=0):
+        return pl.BlockSpec((rows, cols), lambda i: (0, lead + i))
+
+    return pl.pallas_call(
+        kernel,
+        grid=(GROUPS,),
+        in_specs=[
+            fixed(seq_len, width),
+            pl.BlockSpec((width, 128), lambda i: (0, (wide + 2 * narrow) // 128)),
+            columns(width, 256),
+            columns(width, 128, wide // 128),
+            columns(width, 128, (wide + narrow) // 128),
+            fixed(seq_len, tok_rows),
+            fixed(seq_len, 128),
+            fixed(seq_len, 128),
+        ],
+        out_specs=[
+            fixed(seq_len, width),
+            columns(tok_rows, 256),
+            columns(seq_len, 128),
+            columns(seq_len, 128),
+            columns(tok_rows, 256),
+            pl.BlockSpec((1, 8, tok_rows), lambda i: (i, 0, 0)),
+            fixed(128, width),
+        ],
+        out_shape=[
+            jax.ShapeDtypeStruct((seq_len, width), B16),
+            jax.ShapeDtypeStruct((tok_rows, wide), B16),
+            jax.ShapeDtypeStruct((seq_len, narrow), B16),
+            jax.ShapeDtypeStruct((seq_len, narrow), B16),
+            jax.ShapeDtypeStruct((tok_rows, wide), B16),
+            jax.ShapeDtypeStruct((GROUPS, 8, tok_rows), F32),
+            jax.ShapeDtypeStruct((128, width), F32),
+        ],
+        compiler_params=pltpu.CompilerParams(vmem_limit_bytes=VMEM_LIMIT),
+        name="attention",
+    )(x_all, head_full, head_full, head_full, head_full, bias, cosine, sine)
+
+
+def attention_backward(
+    where_here, out_grad_low, full_output, attended, moe_in, logit_low, moe_gain_row, saved,
+    x_all, head_full, bias, cosine, sine,
+):
+    normed_all, query_rot, key_rot, value_all, totals = saved
+    seq_len, width = x_all.shape
+    tok_rows = query_rot.shape[0]
+    scale = HD ** (-0.5)
+    wide, narrow = H * HD, KVH * HD
+    block = width // 8
+    half = width // 2
+
+    def kernel(
+        here_ref, og_ref, wo_ref, att_ref, moe_ref, logit_ref, gain_ref,
+        normed_ref, q_ref, k_ref, v_ref, total_ref,
+        x_ref, wq_ref, wk_ref, wv_ref, bias_ref, cos_ref, sin_ref,
+        first_out, second_out, normed_out, normed_t, grad_sum,
+    ):
+        step = pl.program_id(0)
+        dp, core = here_ref[0], here_ref[1]
+
+        @pl.when(step == 0)
+        def _():
+            normed_t[...] = jnp.transpose(normed_ref[...])
+            grad_sum[...] = jnp.zeros((seq_len, width), F32)
+
+        og = og_ref[...]
+        att_grad = lax.dot_general(og, wo_ref[...], NT, preferred_element_type=F32).astype(B16)
+        query, key, value = q_ref[...], k_ref[...], v_ref[...]
+        query_grads, key_grads, value_grads = [], [], []
+        for j in range(4):
+            lanes = slice(HD * (j // 2), HD * (j // 2 + 1))
+            mine = slice(HD * j, HD * (j + 1))
+            scores = lax.dot_general(
+                key[:, lanes], query[:, mine], NT, preferred_element_type=F32
+            )
+            probs = jnp.exp(scores + bias_ref[...] - total_ref[0, j : j + 1, :])
+            probs_grad = lax.dot_general(
+                value[:, lanes], att_grad[:, mine], NT, preferred_element_type=F32
+            )
+            delta = jnp.sum(probs * probs_grad, axis=0, keepdims=True)
+            score_grad = (probs * (probs_grad - delta)).astype(B16)
+            query_grads.append(
+                lax.dot_general(key[:, lanes], score_grad, TN, preferred_element_type=F32)
+            )
+            key_part = jnp.dot(score_grad, query[:, mine], preferred_element_type=F32)
+            value_part = jnp.dot(probs.astype(B16), att_grad[:, mine], preferred_element_type=F32)
+            if j % 2 == 0:
+                key_grads.append(key_part)
+                value_grads.append(value_part)
+            else:
+                key_grads[-1] = key_grads[-1] + key_part
+                value_grads[-1] = value_grads[-1] + value_part
+        cos, sin = cos_ref[...], -sin_ref[...]
+        kv_grad = jnp.concatenate(
+            [turn(jnp.concatenate(key_grads, axis=1), cos, sin)] + value_grads, axis=1
+        ).astype(B16)
+        cos, sin = cos[:tok_rows], sin[:tok_rows]
+        query_grad = jnp.transpose(jnp.concatenate(query_grads, axis=0)) * scale
+        query_grad = jnp.concatenate(
+            [turn(query_grad[:, 128 * j : 128 * (j + 1)], cos, sin) for j in range(2)], axis=1
+        ).astype(B16)
+
+        def give(out_ref, grad, lanes):
+            for m in range(4):
+                for c in range(2):
+                    out_ref[core ^ c, dp ^ m, :, lanes] = grad[
+                        (2 * m + c) * block : (2 * m + c + 1) * block
+                    ].astype(B16)
+
+        lanes = pl.ds(pl.multiple_of(step * 256, 256), 256)
+        give(
+            first_out,
+            jnp.dot(normed_t[:, :tok_rows], query_grad, preferred_element_type=F32),
+            lanes,
+        )
+        give(second_out, jnp.dot(normed_t[...], kv_grad, preferred_element_type=F32), lanes)
+        out_part = lax.dot_general(att_ref[...], og, TN, preferred_element_type=F32).astype(B16)
+        for c in range(2):
+            rows = slice(c * block, (c + 1) * block)
+            first_out[core ^ c, dp ^ step, :, wide : wide + half] = out_part[rows, :half]
+            second_out[core ^ c, dp ^ step, :, wide : wide + half] = out_part[rows, half:]
+        kv_weights = jnp.concatenate([wk_ref[...], wv_ref[...]], axis=1)
+        grad_sum[...] += lax.dot_general(kv_grad, kv_weights, NT, preferred_element_type=F32)
+        grad_sum[:tok_rows, :] += lax.dot_general(
+            query_grad, wq_ref[...], NT, preferred_element_type=F32
+        )
+
+        @pl.when(step == GROUPS - 1)
+        def _():
+            total = grad_sum[...]
+            normed_out[...] = total.astype(B16)
+            x = x_ref[...].astype(F32)
+            lifted = x * lax.rsqrt(jnp.mean(x * x, axis=1, keepdims=True) + EPSILON)
+            gain = jnp.sum(total * lifted, axis=0, keepdims=True)
+            row = lax.broadcasted_iota(jnp.int32, (EXTRA, width), 0)
+            gains = jnp.where(
+                row == EXPERTS, gain, jnp.where(row == EXPERTS + 1, gain_ref[...], 0.0)
+            )
+            extra = lax.dot_general(
+                moe_ref[...], logit_ref[...], TN, preferred_element_type=F32
+            ) + jnp.transpose(gains)
+            give(first_out, extra, slice(wide + half, wide + half + EXTRA))
+
+    def fixed(*shape):
+        return pl.BlockSpec(shape, lambda i, here: (0,) * len(shape))
+
+    def columns(rows, cols, lead=0):
+        return pl.BlockSpec((rows, cols), lambda i, here: (0, lead + i))
+
+    shapes = [
+        jax.ShapeDtypeStruct((2, 4, block, wide + half + EXTRA), B16),
+        jax.ShapeDtypeStruct((2, 4, block, 2 * narrow + half), B16),
+        jax.ShapeDtypeStruct((seq_len, width), B16),
+    ]
+    return pl.pallas_call(
+        kernel,
+        out_shape=shapes,
+        grid_spec=pltpu.PrefetchScalarGridSpec(
+            num_scalar_prefetch=1,
+            grid=(GROUPS,),
+            in_specs=[
+                fixed(tok_rows, width),
+                pl.BlockSpec((256, width), lambda i, here: (i, 0)),
+                columns(tok_rows, 256),
+                fixed(tok_rows, width),
+                fixed(tok_rows, EXTRA),
+                fixed(1, width),
+                fixed(seq_len, width),
+                columns(tok_rows, 256),
+                columns(seq_len, 128),
+                columns(seq_len, 128),
+                pl.BlockSpec((1, 8, tok_rows), lambda i, here: (i, 0, 0)),
+                fixed(seq_len, width),
+                columns(width, 256),
+                columns(width, 128, wide // 128),
+                columns(width, 128, (wide + narrow) // 128),
+                fixed(seq_len, tok_rows),
+                fixed(seq_len, 128),
+                fixed(seq_len, 128),
+            ],
+            out_specs=[fixed(*shape.shape) for shape in shapes],
+            scratch_shapes=[
+                pltpu.VMEM((width, seq_len), B16),
+                pltpu.VMEM((seq_len, width), F32),
+            ],
+        ),
+        compiler_params=pltpu.CompilerParams(vmem_limit_bytes=VMEM_LIMIT),
+        name="attention_grad",
+    )(
+        where_here, out_grad_low, full_output, attended, moe_in, logit_low, moe_gain_row,
+        normed_all, query_rot, key_rot, value_all, totals,
+        x_all, head_full, head_full, head_full, bias, cosine, sine,
+    )
+
+
 def make_body(z_size, small_grid):
     def dense_gather(shard, dp_index):
         if not small_grid:
@@ -427,31 +696,32 @@
             places += [2 * (dp_index ^ (j + 1)) + which for j in range(3)]
         return assemble(jnp.stack(places), shard, moved, other, rows // 2), moved
 
-    def dense_sum(grads, dp_index):
-        if not small_grid:
-            return lax.psum_scatter(
-                lax.psum(grads, ("z", "core")), ("y", "x"), scatter_dimension=0, tiled=True
-            )
-        rows, cols = grads.shape
-        eighth = rows // 8
-        core = lax.axis_index("core")
-        split = grads.astype(B16).reshape(4, 2, eighth, cols)
-        keep = lax.dynamic_index_in_dim(split, core, 1, keepdims=False)
-        give = lax.dynamic_index_in_dim(split, 1 - core, 1, keepdims=False)
-        both = (keep.astype(F32) + swap_core(give).astype(F32)).astype(B16)
-        mine = grid_scatter_rows(
-            [lax.dynamic_index_in_dim(both, dp_index ^ j, 0, keepdims=False) for j in range(4)]
-        )
-        step = 1
-        while step < z_size:
-            pairs = [(i, i ^ step) for i in range(z_size)]
-            mine = mine + lax.ppermute(mine.astype(B16), "z", pairs).astype(F32)
-            step *= 2
+    def across_z(mine, z):
+        if z_size != 4:
+            return lax.psum(mine.astype(F32), "z")
+        rows = mine.shape[0] // z_size
         low = mine.astype(B16)
+        total = lax.dynamic_slice_in_dim(mine, z * rows, rows, 0)
+        for k in range(1, z_size):
+            theirs = lax.dynamic_slice_in_dim(low, (z + k) % z_size * rows, rows, 0)
+            total = total + cyclic(theirs, z_size, k).astype(F32)
+        total = total.astype(B16)
+        quarters = [total] + [cyclic(total, z_size, -k) for k in range(1, z_size)]
+        places = (jnp.arange(z_size, dtype=jnp.int32) - z) % z_size
+        return jnp.take(jnp.stack(quarters), places, axis=0).reshape(mine.shape).astype(F32)
+
+    def dense_blocks_sum(blocks, z, core):
+        both = (blocks[0].astype(F32) + swap_core(blocks[1]).astype(F32)).astype(B16)
+        low = across_z(grid_scatter_rows(both), z).astype(B16)
         other = swap_core(low)
         first = jnp.where(core == 0, low, other)
         second = jnp.where(core == 0, other, low)
         return jnp.concatenate([first, second], axis=0).astype(F32)
+
+    def dense_sum(grads):
+        return lax.psum_scatter(
+            lax.psum(grads, ("z", "core")), ("y", "x"), scatter_dimension=0, tiled=True
+        )
 
     def body(
         layer_input,
@@ -487,6 +757,7 @@
         head_pack = jnp.concatenate(
             [w_query, w_key, w_value, w_router, gains, jnp.zeros((rows, 94), B16)], axis=1
         )
+        x_parts = grid_gather(layer_input) if small_grid else None
         head_full, head_moved = dense_gather(head_pack, dp_index)
         full_output, tail_moved = dense_gather(after(w_output, head_moved), dp_index)
         wide = H * HD
@@ -494,9 +765,6 @@
         full_query = head_full[:, :wide]
         full_key = head_full[:, wide : wide + narrow]
         full_value = head_full[:, wide + narrow : wide + 2 * narrow]
-        full_router = head_full[:, wide + 2 * narrow : wide + 2 * narrow + EXPERTS]
-        full_attn_gain = head_full[:, wide + 2 * narrow + EXPERTS].astype(F32)
-        full_moe_gain = head_full[:, wide + 2 * narrow + EXPERTS + 1].astype(F32)
 
         expert_ids = jnp.arange(EXPERTS, dtype=jnp.int32)
         hits = routes[:, :, None] == expert_ids[None, None, :]
@@ -514,16 +782,7 @@
         (slot_grads_other,) = dispatch_rows(lead, grads_other, None, None, local, capacity)
 
         query_pos = dp_index * tok_rows + jnp.arange(tok_rows, dtype=jnp.int32)
-        places = query_pos.astype(F32)
         in_float = layer_input.astype(F32)
-        normed = rms_norm(in_float, full_attn_gain).astype(B16)
-        query_lin = jnp.dot(normed, full_query, preferred_element_type=F32)
-        key_lin = jnp.dot(normed, full_key, preferred_element_type=F32)
-        value_low = jnp.dot(normed, full_value, preferred_element_type=F32).astype(B16)
-        query_rot = (rotate(query_lin.reshape(tok_rows, H, HD), places) * score_scale).astype(B16)
-        key_rot = rotate(key_lin.reshape(tok_rows, KVH, HD), places).astype(B16)
-        key_rot = key_rot.reshape(tok_rows, narrow)
-        both = jnp.concatenate([key_rot, value_low], axis=1)
         steps = jnp.arange(tok_rows, dtype=jnp.int32)
         eff = w_gate.shape[2]
         in_rows, mid_rows = w_gate.shape[1], w_down.shape[1]
@@ -531,63 +790,85 @@
         pack = jnp.concatenate([w_gate, w_up, *folds], axis=1)
         if small_grid:
             relative = dp_index ^ jnp.arange(4, dtype=jnp.int32)
-            both_parts = grid_gather(both)
-            both_all = jnp.concatenate(both_parts, axis=0)
             key_pos = (relative[:, None] * tok_rows + steps[None, :]).reshape(seq_len)
             halves, per = 2, local // 2
             expert_weights, skips = [], []
+            first = head_moved
             for half in range(2):
-                own = after(pack[half * per : (half + 1) * per], both_parts[1], both_parts[2])
+                own = after(pack[half * per : (half + 1) * per], first)
                 parts = grid_gather(own)
                 diag = jnp.concatenate([parts[3], parts[4]], axis=0)
                 expert_weights.append([own, parts[1], parts[2], diag])
                 skips.append([half * per] * 4)
+                first = parts[1]
         else:
             relative = jnp.arange(dp_size, dtype=jnp.int32)
-            both_all = lax.all_gather(both, ("y", "x"), axis=0, tiled=True)
             key_pos = jnp.arange(seq_len, dtype=jnp.int32)
             halves, per = 1, local
             every = lax.all_gather(pack, ("y", "x"), axis=0, tiled=False)
             expert_weights = [[every[j] for j in range(dp_size)]]
             skips = [[0] * dp_size]
         order = jnp.concatenate([relative, lead])
-        key_all = both_all[:, :narrow]
-        value_all = both_all[:, narrow:]
         visible = (key_pos[None, :] <= query_pos[:, None]) | (key_pos[None, :] < prefix_len[0])
-
-        def head_scores(head_idx):
-            query_head = query_rot[:, head_idx * group_size : (head_idx + 1) * group_size, :]
-            key_head = key_all[:, head_idx * HD : (head_idx + 1) * HD]
-            scores = jnp.einsum("qgd,kd->gqk", query_head, key_head, preferred_element_type=F32)
-            return jnp.where(visible[None, :, :], scores, MASKED_SCORE)
-
-        mixed_heads = []
-        log_totals = []
-        for head_idx in range(KVH):
-            scores = head_scores(head_idx)
-            row_max = jnp.max(scores, axis=-1, keepdims=True)
-            log_total = row_max + jnp.log(
-                jnp.sum(jnp.exp(scores - row_max), axis=-1, keepdims=True)
-            )
-            probs_low = jnp.exp(scores - log_total).astype(B16)
-            value_head = value_all[:, head_idx * HD : (head_idx + 1) * HD]
-            mixed_heads.append(
-                jnp.einsum("gqk,kd->qgd", probs_low, value_head, preferred_element_type=F32)
-            )
-            log_totals.append(log_total)
-        attended = jnp.concatenate(mixed_heads, axis=1).reshape(tok_rows, wide).astype(B16)
+        if small_grid:
+            x_all = jnp.concatenate(x_parts, axis=0)
+            bias = jnp.where(visible.T, 0.0, MASKED_SCORE)
+            cosine, sine = turn_tables(key_pos.astype(F32))
+            normed_all, query_rot, key_rot, value_all, attended, totals, misc = attention_forward(
+                x_all, head_full, bias, cosine, sine, tok_rows
+            )
+            router_rows = misc[:EXPERTS].astype(B16)
+            full_attn_gain = misc[EXPERTS]
+            full_moe_gain = misc[EXPERTS + 1]
+        else:
+            places = query_pos.astype(F32)
+            router_rows = head_full[:, wide + 2 * narrow : wide + 2 * narrow + EXPERTS].T
+            full_attn_gain = head_full[:, wide + 2 * narrow + EXPERTS].astype(F32)
+            full_moe_gain = head_full[:, wide + 2 * narrow + EXPERTS + 1].astype(F32)
+            normed = rms_norm(in_float, full_attn_gain).astype(B16)
+            query_lin = jnp.dot(normed, full_query, preferred_element_type=F32)
+            key_lin = jnp.dot(normed, full_key, preferred_element_type=F32)
+            value_low = jnp.dot(normed, full_value, preferred_element_type=F32).astype(B16)
+            query_rot = (rotate(query_lin.reshape(tok_rows, H, HD), places) * score_scale).astype(B16)
+            key_rot = rotate(key_lin.reshape(tok_rows, KVH, HD), places).astype(B16)
+            key_rot = key_rot.reshape(tok_rows, narrow)
+            both = jnp.concatenate([key_rot, value_low], axis=1)
+            both_all = lax.all_gather(both, ("y", "x"), axis=0, tiled=True)
+            key_all = both_all[:, :narrow]
+            value_all = both_all[:, narrow:]
+
+            def head_scores(head_idx):
+                query_head = query_rot[:, head_idx * group_size : (head_idx + 1) * group_size, :]
+                key_head = key_all[:, head_idx * HD : (head_idx + 1) * HD]
+                scores = jnp.einsum("qgd,kd->gqk", query_head, key_head, preferred_element_type=F32)
+                return jnp.where(visible[None, :, :], scores, MASKED_SCORE)
+
+            mixed_heads = []
+            log_totals = []
+            for head_idx in range(KVH):
+                scores = head_scores(head_idx)
+                row_max = jnp.max(scores, axis=-1, keepdims=True)
+                log_total = row_max + jnp.log(
+                    jnp.sum(jnp.exp(scores - row_max), axis=-1, keepdims=True)
+                )
+                probs_low = jnp.exp(scores - log_total).astype(B16)
+                value_head = value_all[:, head_idx * HD : (head_idx + 1) * HD]
+                mixed_heads.append(
+                    jnp.einsum("gqk,kd->qgd", probs_low, value_head, preferred_element_type=F32)
+                )
+                log_totals.append(log_total)
+            attended = jnp.concatenate(mixed_heads, axis=1).reshape(tok_rows, wide).astype(B16)
         residual = in_float + jnp.dot(attended, full_output, preferred_element_type=F32)
         moe_in = rms_norm(residual, full_moe_gain).astype(B16)
 
         rows_mine, rows_other = column_gather(moe_in, z_size)
-        router_rows = full_router.T
         slot_rows_mine, slot_gates_mine = dispatch_rows(
             lead, grads_mine, rows_mine, router_rows, local, capacity
         )
         slot_rows_other, slot_gates_other = dispatch_rows(
             lead, grads_other, rows_other, router_rows, local, capacity
         )
-        logits = jnp.dot(moe_in, full_router, preferred_element_type=F32)
+        logits = lax.dot_general(moe_in, router_rows, NT, preferred_element_type=F32)
         peak = jnp.max(jnp.where(routed, logits, MASKED_SCORE), axis=-1, keepdims=True)
         lifted = jnp.where(routed, jnp.exp(jnp.minimum(logits - peak, 0.0)), 0.0)
         gate_weights = lifted / jnp.sum(lifted, axis=-1, keepdims=True)
@@ -646,101 +927,130 @@
         grad_out = out_grad.astype(F32)
         centre = jnp.sum(gate_weights * gate_grad, axis=-1, keepdims=True)
         logit_low = (gate_weights * (gate_grad - centre)).astype(B16)
-        router_grad = jnp.einsum("td,te->de", moe_in, logit_low, preferred_element_type=F32)
-        moe_in_grad = moe_in_grad + jnp.einsum(
-            "te,de->td", logit_low, full_router, preferred_element_type=F32
-        )
+        moe_in_grad = moe_in_grad + jnp.dot(logit_low, router_rows, preferred_element_type=F32)
         norm_value, second_pull = jax.vjp(rms_norm, residual, full_moe_gain)
         resid_norm_grad, moe_gain_grad = second_pull(moe_in_grad)
         residual_grad = grad_out + resid_norm_grad
         attn_out_grad = residual_grad.astype(B16)
-        wout_grad = jnp.einsum("tc,td->cd", attended, attn_out_grad, preferred_element_type=F32)
-        attended_grad = (
-            jnp.einsum("td,cd->tc", attn_out_grad, full_output, preferred_element_type=F32)
-            .astype(B16)
-            .reshape(tok_rows, H, HD)
-        )
-        tail_grad = dense_sum(
-            jnp.concatenate(
-                [
-                    wout_grad,
-                    router_grad,
-                    moe_gain_grad[:, None],
-                    jnp.zeros((model_width, 95), F32),
-                ],
-                axis=1,
-            ),
-            dp_index,
-        )
-        query_grads = []
-        key_parts = []
-        value_parts = []
-        for head_idx in range(KVH):
-            scores = head_scores(head_idx)
-            attention_probs = jnp.exp(scores - log_totals[head_idx])
-            probs_low = attention_probs.astype(B16)
-            grad_head = attended_grad[:, head_idx * group_size : (head_idx + 1) * group_size, :]
-            query_head = query_rot[:, head_idx * group_size : (head_idx + 1) * group_size, :]
-            key_head = key_all[:, head_idx * HD : (head_idx + 1) * HD]
-            value_head = value_all[:, head_idx * HD : (head_idx + 1) * HD]
-            probs_grad = jnp.einsum("qgd,kd->gqk", grad_head, value_head, preferred_element_type=F32)
-            row_delta = jnp.sum(attention_probs * probs_grad, axis=-1, keepdims=True)
-            score_grad = (attention_probs * (probs_grad - row_delta)).astype(B16)
-            query_grads.append(
-                jnp.einsum("gqk,kd->qgd", score_grad, key_head, preferred_element_type=F32)
-            )
-            key_parts.append(
-                jnp.einsum("gqk,qgd->kd", score_grad, query_head, preferred_element_type=F32)
-            )
-            value_parts.append(
-                jnp.einsum("gqk,qgd->kd", probs_low, grad_head, preferred_element_type=F32)
-            )
-        both_part = jnp.concatenate(key_parts + value_parts, axis=1)
         if small_grid:
-            both_sum = grid_scatter_rows(both_part.astype(B16).reshape(4, tok_rows, 2 * narrow))
+            logit_wide = jnp.pad(logit_low, ((0, 0), (0, EXTRA - EXPERTS)))
+            first_blocks, second_blocks, normed_part = attention_backward(
+                jnp.stack([dp_index, core]).astype(jnp.int32),
+                attn_out_grad,
+                full_output,
+                attended,
+                moe_in,
+                logit_wide,
+                moe_gain_grad[None, :],
+                (normed_all, query_rot, key_rot, value_all, totals),
+                x_all,
+                head_full,
+                bias,
+                cosine,
+                sine,
+            )
+            first_sum = dense_blocks_sum(first_blocks, z, core)
+            second_sum = dense_blocks_sum(second_blocks, z, core)
+            normed_grad = grid_scatter_rows(normed_part.reshape(4, tok_rows, model_width))
+            first_value, first_pull = jax.vjp(lambda v: rms_norm(v, full_attn_gain), in_float)
+            input_grad = residual_grad + first_pull(normed_grad)[0]
+            at = wide + model_width // 2
+            query_sum = first_sum[:, :wide]
+            output_sum = jnp.concatenate(
+                [first_sum[:, wide:at], second_sum[:, 2 * narrow :]], axis=1
+            )
+            router_sum = first_sum[:, at : at + EXPERTS]
+            attn_gain_sum = first_sum[:, at + EXPERTS]
+            moe_gain_sum = first_sum[:, at + EXPERTS + 1]
+            key_sum, value_sum = [
+                jnp.concatenate(
+                    [
+                        second_sum[:, 256 * i + lead_col : 256 * i + lead_col + 128]
+                        for i in range(GROUPS)
+                    ],
+                    axis=1,
+                )
+                for lead_col in (0, 128)
+            ]
         else:
+            router_grad = jnp.einsum("td,te->de", moe_in, logit_low, preferred_element_type=F32)
+            wout_grad = jnp.einsum("tc,td->cd", attended, attn_out_grad, preferred_element_type=F32)
+            attended_grad = (
+                jnp.einsum("td,cd->tc", attn_out_grad, full_output, preferred_element_type=F32)
+                .astype(B16)
+                .reshape(tok_rows, H, HD)
+            )
+            query_grads = []
+            key_parts = []
+            value_parts = []
+            for head_idx in range(KVH):
+                scores = head_scores(head_idx)
+                attention_probs = jnp.exp(scores - log_totals[head_idx])
+                probs_low = attention_probs.astype(B16)
+                grad_head = attended_grad[:, head_idx * group_size : (head_idx + 1) * group_size, :]
+                query_head = query_rot[:, head_idx * group_size : (head_idx + 1) * group_size, :]
+                key_head = key_all[:, head_idx * HD : (head_idx + 1) * HD]
+                value_head = value_all[:, head_idx * HD : (head_idx + 1) * HD]
+                probs_grad = jnp.einsum("qgd,kd->gqk", grad_head, value_head, preferred_element_type=F32)
+                row_delta = jnp.sum(attention_probs * probs_grad, axis=-1, keepdims=True)
+                score_grad = (attention_probs * (probs_grad - row_delta)).astype(B16)
+                query_grads.append(
+                    jnp.einsum("gqk,kd->qgd", score_grad, key_head, preferred_element_type=F32)
+                )
+                key_parts.append(
+                    jnp.einsum("gqk,qgd->kd", score_grad, query_head, preferred_element_type=F32)
+                )
+                value_parts.append(
+                    jnp.einsum("gqk,qgd->kd", probs_low, grad_head, preferred_element_type=F32)
+                )
+            both_part = jnp.concatenate(key_parts + value_parts, axis=1)
             both_sum = lax.psum_scatter(both_part, ("y", "x"), scatter_dimension=0, tiled=True)
-        query_rot_grad = jnp.concatenate(query_grads, axis=1) * score_scale
-        key_rot_grad = both_sum[:, :narrow].reshape(tok_rows, KVH, HD)
-        value_grad = both_sum[:, narrow:].astype(B16)
-        query_grad = rotate(query_rot_grad, -places).reshape(tok_rows, wide).astype(B16)
-        key_grad = rotate(key_rot_grad, -places).reshape(tok_rows, narrow).astype(B16)
-        wq_grad = jnp.einsum("td,tc->dc", normed, query_grad, preferred_element_type=F32)
-        query_sum = dense_sum(wq_grad, dp_index)
-        wk_grad = jnp.einsum("td,tc->dc", normed, key_grad, preferred_element_type=F32)
-        wv_grad = jnp.einsum("td,tc->dc", normed, value_grad, preferred_element_type=F32)
-        normed_grad = jnp.einsum("tc,dc->td", query_grad, full_query, preferred_element_type=F32)
-        normed_grad = normed_grad + jnp.einsum(
-            "tc,dc->td", key_grad, full_key, preferred_element_type=F32
-        )
-        normed_grad = normed_grad + jnp.einsum(
-            "tc,dc->td", value_grad, full_value, preferred_element_type=F32
-        )
-        first_value, first_pull = jax.vjp(rms_norm, in_float, full_attn_gain)
-        input_norm_grad, attn_gain_grad = first_pull(normed_grad)
-        input_grad = residual_grad + input_norm_grad
-        head_grad = dense_sum(
-            jnp.concatenate(
-                [
-                    wk_grad,
-                    wv_grad,
-                    attn_gain_grad[:, None],
-                    jnp.zeros((model_width, 127), F32),
-                ],
-                axis=1,
-            ),
-            dp_index,
-        )
+            query_rot_grad = jnp.concatenate(query_grads, axis=1) * score_scale
+            key_rot_grad = both_sum[:, :narrow].reshape(tok_rows, KVH, HD)
+            value_grad = both_sum[:, narrow:].astype(B16)
+            query_grad = rotate(query_rot_grad, -places).reshape(tok_rows, wide).astype(B16)
+            key_grad = rotate(key_rot_grad, -places).reshape(tok_rows, narrow).astype(B16)
+            wq_grad = jnp.einsum("td,tc->dc", normed, query_grad, preferred_element_type=F32)
+            wk_grad = jnp.einsum("td,tc->dc", normed, key_grad, preferred_element_type=F32)
+            wv_grad = jnp.einsum("td,tc->dc", normed, value_grad, preferred_element_type=F32)
+            normed_grad = jnp.einsum("tc,dc->td", query_grad, full_query, preferred_element_type=F32)
+            normed_grad = normed_grad + jnp.einsum(
+                "tc,dc->td", key_grad, full_key, preferred_element_type=F32
+            )
+            normed_grad = normed_grad + jnp.einsum(
+                "tc,dc->td", value_grad, full_value, preferred_element_type=F32
+            )
+            first_value, first_pull = jax.vjp(rms_norm, in_float, full_attn_gain)
+            input_norm_grad, attn_gain_grad = first_pull(normed_grad)
+            input_grad = residual_grad + input_norm_grad
+            query_sum = dense_sum(wq_grad)
+            key_sum = dense_sum(wk_grad)
+            value_sum = dense_sum(wv_grad)
+            output_sum = dense_sum(wout_grad)
+            extra_sum = dense_sum(
+                jnp.concatenate(
+                    [
+                        router_grad,
+                        attn_gain_grad[:, None],
+                        moe_gain_grad[:, None],
+                        jnp.zeros((model_width, EXTRA - EXPERTS - 2), F32),
+                    ],
+                    axis=1,
+                )
+            )
+            router_sum = extra_sum[:, :EXPERTS]
+            attn_gain_sum = extra_sum[:, EXPERTS]
+            moe_gain_sum = extra_sum[:, EXPERTS + 1]
         return (
             layer_output,
             input_grad,
-            head_grad[:, 2 * narrow],
+            attn_gain_sum,
             query_sum,
-            head_grad[:, :narrow],
-            head_grad[:, narrow : 2 * narrow],
-            tail_grad[:, :wide],
-            tail_grad[:, wide + EXPERTS],
-            tail_grad[:, wide : wide + EXPERTS],
+            key_sum,
+            value_sum,
+            output_sum,
+            moe_gain_sum,
+            router_sum,
             expert_grads[0],
             expert_grads[1],
             expert_grads[2],

time: 675 us -> 648 us (0.960)
  matrix products: 65.6 us -> 5.9 us
  Pallas kernels: 92.6 us -> 147 us
  other arithmetic: 72.2 us -> 45.8 us
  waiting for transfers between devices: 294 us -> 312 us
  local copies, waits for them, and re-layouts: 53.4 us -> 40.3 us
    dot_general x62 -> x2, matrix products: 64.8 us -> 3.19 us  [the longest x1 2.01 us: body(): jnp.dot(logit_low, router_rows, preferred_element_type=F32)]
    pallas_call x0 -> x2, Pallas kernels: none -> 55.2 us  [the longest x1 34.1 us: attention_backward(): pl.pallas_call(kernel, out_shape=shapes, grid_spec=pltpu.PrefetchScalarGr...]
    ppermute x12 -> x24, waiting for transfers between devices: 109 us -> 150 us  [cyclic(): lax.ppermute(rows, 'z', [(i, (i + shift) % size) for i in range(size)])]
    ppermute x6 -> x0, waiting for transfers between devices: 38.5 us -> none  [dense_sum(): mine = mine + lax.ppermute(mine.astype(B16), 'z', pairs).astype(F32)]
    ppermute x6 -> x0, starting transfers between devices: 16.4 us -> none  [dense_sum(): mine = mine + lax.ppermute(mine.astype(B16), 'z', pairs).astype(F32)]
    ppermute x12 -> x24, starting transfers between devices: 21.9 us -> 37.1 us  [cyclic(): lax.ppermute(rows, 'z', [(i, (i + shift) % size) for i in range(size)])]
    convert_element_type x21 -> x10, other arithmetic: 16.3 us -> 3.13 us  [the longest x1 1.93 us: body(): attn_out_grad = residual_grad.astype(B16)]
    ppermute x6 -> x5, waiting for transfers between devices: 3.38 us -> 15.2 us  [grid_scatter(): got_a = lax.ppermute(first_a, 'x', SWAP)]
  transfers between devices with their start and end apart: 74 -> 74, of which waited for: 35 -> 32; matrix products, arithmetic and copies ran while one was open for 19% -> 12% of each run, Pallas kernels for 14% -> 18%
where the time goes in v3:
time: 648 us; the launch traced here: 638 us
  waiting for transfers between devices  312 us (48%)
  Pallas kernels  147 us (23%)
  starting transfers between devices  83.7 us (13%)
  other arithmetic  45.8 us (7%)
  local copies, waits for them, and re-layouts  40.3 us (6%)
    ppermute x24, waiting for transfers between devices, cyclic(): lax.ppermute(rows, 'z', [(i, (i + shift) % size) for i in range(size)])  150 us
    ppermute x5, waiting for transfers between devices, grid_gather(): diag_a = lax.ppermute(from_x[:half], 'y', SWAP)  61 us
    pallas_call x2, Pallas kernels, experts(): pl.pallas_call(kernel, out_shape=out_shape, grid_spec=pltpu.PrefetchScala...  44.4 us
    ppermute x24, starting transfers between devices, cyclic(): lax.ppermute(rows, 'z', [(i, (i + shift) % size) for i in range(size)])  37.1 us
    pallas_call x1, Pallas kernels, attention_backward(): pl.pallas_call(kernel, out_shape=shapes, grid_spec=pltpu.PrefetchScalarGr...  34.1 us
    ppermute x5, waiting for transfers between devices, grid_gather(): diag_b = lax.ppermute(from_y[half:], 'x', SWAP)  34 us
    ppermute x5, waiting for transfers between devices, grid_scatter(): last_a = lax.ppermute(onward_a, 'y', SWAP)  24 us
    pallas_call x1, Pallas kernels, attention_forward(): pl.pallas_call(kernel, grid=(GROUPS,), in_specs=[fixed(seq_len, width), p...  21.2 us
  transfers between devices with their start and end apart: 74, of which 32 were waited for; matrix products, arithmetic and copies ran while one was open for 12% of the time, Pallas kernels for 18%

profile of v3, /device:TPU:0, one launch (start us, length us, event | category | flops | bytes accessed | tf_op | source)
XLA Modules:
  0.0 638.4 jit_solution(5282633548604678745)
XLA Ops:
  3.1 2.5 concatenate.61.shard_ref
  6.5 3.0 collective-permute-start.4
  12.5 2.6 convert_reduce_fusion
  16.5 3.0 fusion.21
  23.2 2.1 collective-permute-start.6
  28.6 12.4 %collective-permute-done.6 = bf16[64,2176]{1,0:T(8,128)(2,1)S(1)} collective-permute-done((bf16[64,2176]{1,0:T(8,128)(2,1)S(1)}, bf16[64,2176]{1,0:T(8,128)(2,1)S(1)}, u32[]{:S(2)}, u32[]{:S(2)}) %collective-permute-start.6) | collective-permute-done | bytes 278560 | tf_op jit(solution)/shard_map/ppermute | solution.py:62
  46.3 3.1 collective-permute-done.9
  51.7 3.7 collective-permute-start.14
  62.7 5.7 collective-permute-done.14
  71.0 29.3 %collective-permute-done.15 = bf16[272,1024]{1,0:T(8,128)(2,1)S(1)} collective-permute-done((bf16[272,1024]{1,0:T(8,128)(2,1)S(1)}, bf16[272,1024]{1,0:T(8,128)(2,1)S(1)}, u32[]{:S(2)}, u32[]{:S(2)}) %collective-permute-start.15) | collective-permute-done | bytes 557088 | tf_op jit(solution)/shard_map/ppermute | solution.py:51
  103.2 3.6 collective-permute-done.3
  107.5 3.6 assemble.3.wo_ref
  111.1 5.3 assemble.2.tail_ref.wq_ref.wk_ref.wv_ref
  116.5 21.2 %attention.1 = (bf16[1024,1024]{1,0:T(8,128)(2,1)}, bf16[256,1024]{1,0:T(8,128)(2,1)}, bf16[1024,512]{1,0:T(8,128)(2,1)}, bf16[1024,512]{1,0:T(8,128)(2,1)}, bf1...) custom-call(bf16[1024,1024]{1,0:T(8,128)(2,1)} %constant_dynamic-update-slice_fusion.x_ref, ...), custom_call_target="tpu_custom_call" | custom-call | tf_op jit(solution)/shard_map/attention/pallas_call | solution.py:492
  137.6 2.7 multiply_reduce_fusion.2
  144.3 2.4 collective-permute-start.19
  146.8 7.1 %collective-permute-done.17 = bf16[256,1024]{1,0:T(8,128)(2,1)S(1)} collective-permute-done((bf16[256,1024]{1,0:T(8,128)(2,1)S(1)}, bf16[256,1024]{1,0:T(8,128)(2,1)S(1)}, u32[]{:S(2)}, u32[]{:S(2)}) %collective-permute-start.17) | collective-permute-done | bytes 524320 | tf_op jit(solution)/shard_map/ppermute | solution.py:51
  155.1 31.0 %collective-permute-done.18 = bf16[256,1024]{1,0:T(8,128)(2,1)S(1)} collective-permute-done((bf16[256,1024]{1,0:T(8,128)(2,1)S(1)}, bf16[256,1024]{1,0:T(8,128)(2,1)S(1)}, u32[]{:S(2)}, u32[]{:S(2)}) %collective-permute-start.18) | collective-permute-done | bytes 524320 | tf_op jit(solution)/shard_map/ppermute | solution.py:51
  194.5 4.5 dispatch.6.refs_2_
  200.6 4.5 dispatch.7.refs_3_
  205.1 4.8 dispatch.4
  209.9 33.0 %collective-permute-done.24 = bf16[1,768,512]{2,1,0:T(8,128)(2,1)} collective-permute-done((bf16[1,768,512]{2,1,0:T(8,128)(2,1)}, bf16[1,768,512]{2,1,0:T(8,128)(2,1)}, u32[]{:S(2)}, u32[]{:S(2)}) %collective-permute-start.24) | collective-permute-done | bytes 786464 | tf_op jit(solution)/shard_map/ppermute | solution.py:62
  242.9 2.4 pad_maximum_fusion.10.refs_9_
  245.4 4.9 dispatch.5
  250.3 22.1 %experts.2 = (bf16[8,160,1024]{2,1,0:T(8,128)(2,1)}, bf16[8,160,1152]{2,1,0:T(8,128)(2,1)}, bf16[2,1,768,512]{3,2,1,0:T(8,128)(2,1)}, bf16[2,1,768,512]{3,2,1,0:...) custom-call(s32[5]{0:T(128)} %pad_add_fusion.order_ref, ...), custom_call_target="tpu_custom_call" | custom-call | tf_op jit(solution)/shard_map/experts/pallas_call | solution.py:392
  279.0 15.6 %collective-permute-done.28 = bf16[1,768,512]{2,1,0:T(8,128)(2,1)S(1)} collective-permute-done((bf16[1,768,512]{2,1,0:T(8,128)(2,1)S(1)}, bf16[1,768,512]{2,1,0:T(8,128)(2,1)S(1)}, u32[]{:S(2)}, u32[]{:S(2)}) %collective-permute-start.28) | collective-permute-done | bytes 786464 | tf_op jit(solution)/shard_map/ppermute | solution.py:62
  294.6 30.5 %collective-permute-done.29 = bf16[1,768,512]{2,1,0:T(8,128)(2,1)S(1)} collective-permute-done((bf16[1,768,512]{2,1,0:T(8,128)(2,1)S(1)}, bf16[1,768,512]{2,1,0:T(8,128)(2,1)S(1)}, u32[]{:S(2)}, u32[]{:S(2)}) %collective-permute-start.29) | collective-permute-done | bytes 786464 | tf_op jit(solution)/shard_map/ppermute | solution.py:63
  326.4 22.3 %experts.3 = (bf16[8,160,1024]{2,1,0:T(8,128)(2,1)}, bf16[8,160,1152]{2,1,0:T(8,128)(2,1)}, bf16[2,1,768,512]{3,2,1,0:T(8,128)(2,1)}, bf16[2,1,768,512]{3,2,1,0:...) custom-call(s32[5]{0:T(128)} %pad_add_fusion.order_ref, ...), custom_call_target="tpu_custom_call" | custom-call | tf_op jit(solution)/shard_map/experts/pallas_call | solution.py:392
  349.3 4.8 combine.5
  355.6 5.1 combine.7
  363.4 4.9 combine.4
  368.3 5.2 combine.6
  377.3 6.6 %collective-permute-done.70 = bf16[2,1,768,512]{3,2,1,0:T(8,128)(2,1)} collective-permute-done((bf16[2,1,768,512]{3,2,1,0:T(8,128)(2,1)}, bf16[2,1,768,512]{3,2,1,0:T(8,128)(2,1)}, u32[]{:S(2)}, u32[]{:S(2)}) %collective-permute-start.70) | collective-permute-done | bytes 1572896 | tf_op jit(solution)/shard_map/ppermute | solution.py:68
  385.8 5.9 collective-permute-done.72
  395.1 2.7 fusion.52
  400.0 2.3 fusion.53
  402.5 5.9 collective-permute-done.67
  411.1 13.8 %collective-permute-done.71 = bf16[1,768,512]{2,1,0:T(8,128)(2,1)S(1)} collective-permute-done((bf16[1,768,512]{2,1,0:T(8,128)(2,1)S(1)}, bf16[1,768,512]{2,1,0:T(8,128)(2,1)S(1)}, u32[]{:S(2)}, u32[]{:S(2)}) %collective-permute-start.71) | collective-permute-done | bytes 786464 | tf_op jit(solution)/shard_map/ppermute | solution.py:72
  429.9 3.2 pad_maximum_fusion
  433.0 7.0 %collective-permute-done.35 = bf16[256,1152]{1,0:T(8,128)(2,1)S(1)} collective-permute-done((bf16[256,1152]{1,0:T(8,128)(2,1)S(1)}, bf16[256,1152]{1,0:T(8,128)(2,1)S(1)}, u32[]{:S(2)}, u32[]{:S(2)}) %collective-permute-start.35) | collective-permute-done | bytes 589856 | tf_op jit(solution)/shard_map/ppermute | solution.py:51
  440.0 34.2 %collective-permute-done.36 = bf16[256,1152]{1,0:T(8,128)(2,1)S(1)} collective-permute-done((bf16[256,1152]{1,0:T(8,128)(2,1)S(1)}, bf16[256,1152]{1,0:T(8,128)(2,1)S(1)}, u32[]{:S(2)}, u32[]{:S(2)}) %collective-permute-start.36) | collective-permute-done | bytes 589856 | tf_op jit(solution)/shard_map/ppermute | solution.py:51
  475.6 2.0 multiply_reduce_fusion
  477.6 14.4 %collective-permute-done.33 = bf16[256,1024]{1,0:T(8,128)(2,1)S(1)} collective-permute-done((bf16[256,1024]{1,0:T(8,128)(2,1)S(1)}, bf16[256,1024]{1,0:T(8,128)(2,1)S(1)}, u32[]{:S(2)}, u32[]{:S(2)}) %collective-permute-start.33) | collective-permute-done | bytes 524320 | tf_op jit(solution)/shard_map/ppermute | solution.py:51
  491.9 1.9 fusion.54
  493.9 34.1 %attention_grad.1 = (bf16[2,4,128,1664]{3,2,1,0:T(8,128)(2,1)}, bf16[2,4,128,1536]{3,2,1,0:T(8,128)(2,1)}, bf16[1024,1024]{1,0:T(8,128)(2,1)}) custom-call(s32[2]{0:T(128)} %pad_add_fusion.1.here_ref, bf16[256,1024]{1,0:T(8,128)(2,1)} %get-tuple-element.122.og_ref, bf16[1024,1024]{1,0:T(8,128)(2,1)} %assemble.3.wo_ref, ...), custom_call_target="tpu_custom_call" | custom-call | tf_op jit(solution)/shard_map/attention_grad/pallas_call | solution.py:643
  533.0 2.9 fusion.56
  536.4 2.3 collective-permute-done.38
  540.0 7.5 %collective-permute-done.40 = bf16[2,128,1024]{2,1,0:T(8,128)(2,1)S(1)} collective-permute-done((bf16[2,128,1024]{2,1,0:T(8,128)(2,1)S(1)}, bf16[2,128,1024]{2,1,0:T(8,128)(2,1)S(1)}, u32[]{:S(2)}, u32[]{:S(2)}) %collective-permute-start.40) | collective-permute-done | bytes 524320 | tf_op jit(solution)/shard_map/ppermute | solution.py:69
  547.5 2.8 collective-permute-done.39
  551.7 5.3 collective-permute-done.41
  560.2 2.0 collective-permute-start.57
  562.6 6.3 collective-permute-done.55
  568.9 2.7 collective-permute-done.57
  571.7 2.5 collective-permute-start.56
  574.3 2.1 collective-permute-start.43
  577.9 2.0 collective-permute-done.58
  580.2 10.2 %collective-permute-start.59 = (bf16[32,1536]{1,0:T(8,128)(2,1)S(1)}, bf16[32,1536]{1,0:T(8,128)(2,1)S(1)}, u32[]{:S(2)}, u32[]{:S(2)}) collective-permute-start(bf16[32,1536]{1,0:T(8,128)(2,1)S(1)} %get-tuple-element.178), channel_id=1, source_target_pairs={{0,8},{8,16},{16,24},{24,0},{1,9},{9,17},{17,25},{25,1},{2,10},{10... | collective-permute-start | bytes 294920 | tf_op jit(solution)/shard_map/ppermute | solution.py:51
  590.7 2.1 collective-permute-start.61
  595.1 6.9 %collective-permute-done.60 = bf16[32,1536]{1,0:T(8,128)(2,1)S(1)} collective-permute-done((bf16[32,1536]{1,0:T(8,128)(2,1)S(1)}, bf16[32,1536]{1,0:T(8,128)(2,1)S(1)}, u32[]{:S(2)}, u32[]{:S(2)}) %collective-permute-start.60) | collective-permute-done | bytes 98336 | tf_op jit(solution)/shard_map/ppermute | solution.py:51
  602.2 4.1 collective-permute-start.63
  607.2 3.8 collective-permute-start.48
  611.1 6.6 %collective-permute-done.63 = bf16[32,1536]{1,0:T(8,128)(2,1)S(1)} collective-permute-done((bf16[32,1536]{1,0:T(8,128)(2,1)S(1)}, bf16[32,1536]{1,0:T(8,128)(2,1)S(1)}, u32[]{:S(2)}, u32[]{:S(2)}) %collective-permute-start.63) | collective-permute-done | bytes 98336 | tf_op jit(solution)/shard_map/ppermute | solution.py:51
  620.1 2.1 collective-permute-start.50
  624.9 3.5 collective-permute-done.51
  (340 shorter events, 114.7 us)
Async XLA Ops:
  6.5 16.7 %collective-permute-start.4 = (bf16[128,2176]{1,0:T(8,128)(2,1)}, bf16[128,2176]{1,0:T(8,128)(2,1)S(1)}, u32[]{:S(2)}, u32[]{:S(2)}) collective-permute-start(bf16[128,2176]{1,0:T(8,128)(2,1)} %constant_dynamic-slice_fusion.7), channel_id=1, source_target_pairs={{0,1},{1,0},{2,3},{3,2},{4,5},{5,4},{6,7},{7,6},{8,9},{9,8},{10,11... | collective-permute-start | bytes 1671176 | tf_op jit(solution)/shard_map/ppermute | solution.py:60
  9.4 15.8 %collective-permute-start.5 = (bf16[128,2176]{1,0:T(8,128)(2,1)}, bf16[128,2176]{1,0:T(8,128)(2,1)S(1)}, u32[]{:S(2)}, u32[]{:S(2)}) collective-permute-start(bf16[128,2176]{1,0:T(8,128)(2,1)} %constant_dynamic-slice_fusion.7), channel_id=1, source_target_pairs={{0,2},{2,0},{1,3},{3,1},{4,6},{6,4},{5,7},{7,5},{8,10},{10,8},{9,1... | collective-permute-start | bytes 1671176 | tf_op jit(solution)/shard_map/ppermute | solution.py:61
  11.0 40.7 %collective-permute-start = (bf16[256,1024]{1,0:T(8,128)(2,1)S(1)}, bf16[256,1024]{1,0:T(8,128)(2,1)}, u32[]{:S(2)}, u32[]{:S(2)}) collective-permute-start(bf16[256,1024]{1,0:T(8,128)(2,1)S(1)} %copy-done.10), channel_id=1, source_target_pairs={{0,1},{1,0},{2,3},{3,2},{4,5},{5,4},{6,7},{7,6},{8,9},{9,8},{10,11... | collective-permute-start | bytes 1572872 | tf_op jit(solution)/shard_map/ppermute | solution.py:60
  11.5 47.2 %collective-permute-start.1 = (bf16[256,1024]{1,0:T(8,128)(2,1)S(1)}, bf16[256,1024]{1,0:T(8,128)(2,1)S(1)}, u32[]{:S(2)}, u32[]{:S(2)}) collective-permute-start(bf16[256,1024]{1,0:T(8,128)(2,1)S(1)} %copy-done.10), channel_id=1, source_target_pairs={{0,2},{2,0},{1,3},{3,1},{4,6},{6,4},{5,7},{7,5},{8,10},{10,8},{9,1... | collective-permute-start | bytes 1572872 | tf_op jit(solution)/shard_map/ppermute | solution.py:61
  23.2 17.8 %collective-permute-start.6 = (bf16[64,2176]{1,0:T(8,128)(2,1)S(1)}, bf16[64,2176]{1,0:T(8,128)(2,1)S(1)}, u32[]{:S(2)}, u32[]{:S(2)}) collective-permute-start(bf16[64,2176]{1,0:T(8,128)(2,1)S(1)} %slice.469), channel_id=1, source_target_pairs={{0,2},{2,0},{1,3},{3,1},{4,6},{6,4},{5,7},{7,5},{8,10},{10,8},{9,1... | collective-permute-start | bytes 835592 | tf_op jit(solution)/shard_map/ppermute | solution.py:62
  25.3 16.4 %collective-permute-start.7 = (bf16[64,2176]{1,0:T(8,128)(2,1)S(1)}, bf16[64,2176]{1,0:T(8,128)(2,1)S(1)}, u32[]{:S(2)}, u32[]{:S(2)}) collective-permute-start(bf16[64,2176]{1,0:T(8,128)(2,1)S(1)} %slice.470), channel_id=1, source_target_pairs={{0,1},{1,0},{2,3},{3,2},{4,5},{5,4},{6,7},{7,6},{8,9},{9,8},{10,11... | collective-permute-start | bytes 835592 | tf_op jit(solution)/shard_map/ppermute | solution.py:63
  42.4 7.0 %collective-permute-start.9 = (bf16[128,1024]{1,0:T(8,128)(2,1)S(1)}, bf16[128,1024]{1,0:T(8,128)(2,1)S(1)}, u32[]{:S(2)}, u32[]{:S(2)}) collective-permute-start(bf16[128,1024]{1,0:T(8,128)(2,1)S(1)} %constant_dynamic-slice_fusion.6), channel_id=1, source_target_pairs={{0,1},{1,0},{2,3},{3,2},{4,5},{5,4},{6,7},{7,6},{8,9},{9,8},{10,11... | collective-permute-start | bytes 786440 | tf_op jit(solution)/shard_map/ppermute | solution.py:60
  42.8 8.2 %collective-permute-start.10 = (bf16[128,1024]{1,0:T(8,128)(2,1)S(1)}, bf16[128,1024]{1,0:T(8,128)(2,1)S(1)}, u32[]{:S(2)}, u32[]{:S(2)}) collective-permute-start(bf16[128,1024]{1,0:T(8,128)(2,1)S(1)} %constant_dynamic-slice_fusion.6), channel_id=1, source_target_pairs={{0,2},{2,0},{1,3},{3,1},{4,6},{6,4},{5,7},{7,5},{8,10},{10,8},{9,1... | collective-permute-start | bytes 786440 | tf_op jit(solution)/shard_map/ppermute | solution.py:61
  44.6 66.5 %collective-permute-start.8 = (bf16[384,2176]{1,0:T(8,128)(2,1)}, bf16[384,2176]{1,0:T(8,128)(2,1)}, u32[]{:S(2)}, u32[]{:S(2)}) collective-permute-start(bf16[384,2176]{1,0:T(8,128)(2,1)} %constant_dynamic-update-slice_fusion.5.moved_ref), channel_id=1, source_target_pairs={{0,4},{4,0},{1,5},{5,1},{2,6},{6,2},{3,7},{7,3},{8,12},{12,8},{9,1... | collective-permute-start | bytes 5013512 | tf_op jit(solution)/shard_map/ppermute | solution.py:47
  51.7 16.7 %collective-permute-start.14 = (bf16[272,1024]{1,0:T(8,128)(2,1)S(1)}, bf16[272,1024]{1,0:T(8,128)(2,1)S(1)}, u32[]{:S(2)}, u32[]{:S(2)}) collective-permute-start(bf16[272,1024]{1,0:T(8,128)(2,1)S(1)} %maximum_maximum_fusion), channel_id=1, source_target_pairs={{0,24},{8,0},{16,8},{24,16},{1,25},{9,1},{17,9},{25,17},{2,26},{10... | collective-permute-start | bytes 1671176 | tf_op jit(solution)/shard_map/ppermute | solution.py:51
  55.3 45.0 %collective-permute-start.15 = (bf16[272,1024]{1,0:T(8,128)(2,1)S(1)}, bf16[272,1024]{1,0:T(8,128)(2,1)S(1)}, u32[]{:S(2)}, u32[]{:S(2)}) collective-permute-start(bf16[272,1024]{1,0:T(8,128)(2,1)S(1)} %maximum_maximum_fusion), channel_id=1, source_target_pairs={{0,16},{8,24},{16,0},{24,8},{1,17},{9,25},{17,1},{25,9},{2,18},{10... | collective-permute-start | bytes 1671176 | tf_op jit(solution)/shard_map/ppermute | solution.py:51
  57.1 44.8 %collective-permute-start.16 = (bf16[272,1024]{1,0:T(8,128)(2,1)S(1)}, bf16[272,1024]{1,0:T(8,128)(2,1)S(1)}, u32[]{:S(2)}, u32[]{:S(2)}) collective-permute-start(bf16[272,1024]{1,0:T(8,128)(2,1)S(1)} %maximum_maximum_fusion), channel_id=1, source_target_pairs={{0,8},{8,16},{16,24},{24,0},{1,9},{9,17},{17,25},{25,1},{2,10},{10... | collective-permute-start | bytes 1671176 | tf_op jit(solution)/shard_map/ppermute | solution.py:51
  58.7 48.8 %collective-permute-start.13 = (bf16[384,1024]{1,0:T(8,128)(2,1)S(1)}, bf16[384,1024]{1,0:T(8,128)(2,1)}, u32[]{:S(2)}, u32[]{:S(2)}) collective-permute-start(bf16[384,1024]{1,0:T(8,128)(2,1)S(1)} %constant_dynamic-update-slice_fusion.9.moved_ref), channel_id=1, source_target_pairs={{0,4},{4,0},{1,5},{5,1},{2,6},{6,2},{3,7},{7,3},{8,12},{12,8},{9,1... | collective-permute-start | bytes 2359304 | tf_op jit(solution)/shard_map/ppermute | solution.py:47
  68.4 33.9 %collective-permute-start.2 = (bf16[128,1024]{1,0:T(8,128)(2,1)S(1)}, bf16[128,1024]{1,0:T(8,128)(2,1)S(1)}, u32[]{:S(2)}, u32[]{:S(2)}) collective-permute-start(bf16[128,1024]{1,0:T(8,128)(2,1)S(1)} %slice.467), channel_id=1, source_target_pairs={{0,2},{2,0},{1,3},{3,1},{4,6},{6,4},{5,7},{7,5},{8,10},{10,8},{9,1... | collective-permute-start | bytes 786440 | tf_op jit(solution)/shard_map/ppermute | solution.py:62
  102.1 91.1 %collective-permute-start.20 = (bf16[4,272,1024]{2,1,0:T(8,128)(2,1)S(1)}, bf16[4,272,1024]{2,1,0:T(8,128)(2,1)}, u32[]{:S(2)}, u32[]{:S(2)}) collective-permute-start(bf16[4,272,1024]{2,1,0:T(8,128)(2,1)S(1)} %pad_maximum_fusion.2.packed_ref.code_ref), channel_id=1, source_target_pairs={{0,4},{4,0},{1,5},{5,1},{2,6},{6,2},{3,7},{7,3},{8,12},{12,8},{9,1... | collective-permute-start | bytes 6684680 | tf_op jit(solution)/shard_map/ppermute | solution.py:47
  141.4 12.5 %collective-permute-start.17 = (bf16[256,1024]{1,0:T(8,128)(2,1)S(1)}, bf16[256,1024]{1,0:T(8,128)(2,1)S(1)}, u32[]{:S(2)}, u32[]{:S(2)}) collective-permute-start(bf16[256,1024]{1,0:T(8,128)(2,1)S(1)} %multiply_convert_fusion.moe_ref), channel_id=1, source_target_pairs={{0,24},{8,0},{16,8},{24,16},{1,25},{9,1},{17,9},{25,17},{2,26},{10... | collective-permute-start | bytes 1572872 | tf_op jit(solution)/shard_map/ppermute | solution.py:51
  142.8 44.9 %collective-permute-start.22 = (bf16[2,768,512]{2,1,0:T(8,128)(2,1)S(1)}, bf16[2,768,512]{2,1,0:T(8,128)(2,1)S(1)}, u32[]{:S(2)}, u32[]{:S(2)}) collective-permute-start(bf16[2,768,512]{2,1,0:T(8,128)(2,1)S(1)} %get-tuple-element.48.refs_6_), channel_id=1, source_target_pairs={{0,1},{1,0},{2,3},{3,2},{4,5},{5,4},{6,7},{7,6},{8,9},{9,8},{10,11... | collective-permute-start | bytes 4718600 | tf_op jit(solution)/shard_map/ppermute | solution.py:60
  144.3 41.8 %collective-permute-start.18 = (bf16[256,1024]{1,0:T(8,128)(2,1)S(1)}, bf16[256,1024]{1,0:T(8,128)(2,1)S(1)}, u32[]{:S(2)}, u32[]{:S(2)}) collective-permute-start(bf16[256,1024]{1,0:T(8,128)(2,1)S(1)} %multiply_convert_fusion.moe_ref), channel_id=1, source_target_pairs={{0,16},{8,24},{16,0},{24,8},{1,17},{9,25},{17,1},{25,9},{2,18},{10... | collective-permute-start | bytes 1572872 | tf_op jit(solution)/shard_map/ppermute | solution.py:51
  144.3 41.8 %collective-permute-start.19 = (bf16[256,1024]{1,0:T(8,128)(2,1)S(1)}, bf16[256,1024]{1,0:T(8,128)(2,1)S(1)}, u32[]{:S(2)}, u32[]{:S(2)}) collective-permute-start(bf16[256,1024]{1,0:T(8,128)(2,1)S(1)} %multiply_convert_fusion.moe_ref), channel_id=1, source_target_pairs={{0,8},{8,16},{16,24},{24,0},{1,9},{9,17},{17,25},{25,1},{2,10},{10... | collective-permute-start | bytes 1572872 | tf_op jit(solution)/shard_map/ppermute | solution.py:51
  153.8 36.9 %collective-permute-start.23 = (bf16[2,768,512]{2,1,0:T(8,128)(2,1)S(1)}, bf16[2,768,512]{2,1,0:T(8,128)(2,1)S(1)}, u32[]{:S(2)}, u32[]{:S(2)}) collective-permute-start(bf16[2,768,512]{2,1,0:T(8,128)(2,1)S(1)} %get-tuple-element.48.refs_6_), channel_id=1, source_target_pairs={{0,2},{2,0},{1,3},{3,1},{4,6},{6,4},{5,7},{7,5},{8,10},{10,8},{9,1... | collective-permute-start | bytes 4718600 | tf_op jit(solution)/shard_map/ppermute | solution.py:61
  187.7 57.7 %collective-permute-start.21 = (bf16[4,256,1024]{2,1,0:T(8,128)(2,1)}, bf16[4,256,1024]{2,1,0:T(8,128)(2,1)}, u32[]{:S(2)}, u32[]{:S(2)}) collective-permute-start(bf16[4,256,1024]{2,1,0:T(8,128)(2,1)} %pad_maximum_fusion.9.rest_0_), channel_id=1, source_target_pairs={{0,4},{4,0},{1,5},{5,1},{2,6},{6,2},{3,7},{7,3},{8,12},{12,8},{9,1... | collective-permute-start | bytes 6291464 | tf_op jit(solution)/shard_map/ppermute | solution.py:47
  187.7 85.2 %collective-permute-start.26 = (bf16[2,768,512]{2,1,0:T(8,128)(2,1)}, bf16[2,768,512]{2,1,0:T(8,128)(2,1)}, u32[]{:S(2)}, u32[]{:S(2)}) collective-permute-start(bf16[2,768,512]{2,1,0:T(8,128)(2,1)} %get-tuple-element.50.refs_6_), channel_id=1, source_target_pairs={{0,1},{1,0},{2,3},{3,2},{4,5},{5,4},{6,7},{7,6},{8,9},{9,8},{10,11... | collective-permute-start | bytes 4718600 | tf_op jit(solution)/shard_map/ppermute | solution.py:60
  189.3 86.0 %collective-permute-start.27 = (bf16[2,768,512]{2,1,0:T(8,128)(2,1)}, bf16[2,768,512]{2,1,0:T(8,128)(2,1)}, u32[]{:S(2)}, u32[]{:S(2)}) collective-permute-start(bf16[2,768,512]{2,1,0:T(8,128)(2,1)} %get-tuple-element.50.refs_6_), channel_id=1, source_target_pairs={{0,2},{2,0},{1,3},{3,1},{4,6},{6,4},{5,7},{7,5},{8,10},{10,8},{9,1... | collective-permute-start | bytes 4718600 | tf_op jit(solution)/shard_map/ppermute | solution.py:61
  190.7 52.2 %collective-permute-start.24 = (bf16[1,768,512]{2,1,0:T(8,128)(2,1)}, bf16[1,768,512]{2,1,0:T(8,128)(2,1)}, u32[]{:S(2)}, u32[]{:S(2)}) collective-permute-start(bf16[1,768,512]{2,1,0:T(8,128)(2,1)} %slice.479), channel_id=1, source_target_pairs={{0,2},{2,0},{1,3},{3,1},{4,6},{6,4},{5,7},{7,5},{8,10},{10,8},{9,1... | collective-permute-start | bytes 2359304 | tf_op jit(solution)/shard_map/ppermute | solution.py:62
  193.3 49.7 %collective-permute-start.25 = (bf16[1,768,512]{2,1,0:T(8,128)(2,1)}, bf16[1,768,512]{2,1,0:T(8,128)(2,1)S(1)}, u32[]{:S(2)}, u32[]{:S(2)}) collective-permute-start(bf16[1,768,512]{2,1,0:T(8,128)(2,1)} %slice.480), channel_id=1, source_target_pairs={{0,1},{1,0},{2,3},{3,2},{4,5},{5,4},{6,7},{7,6},{8,9},{9,8},{10,11... | collective-permute-start | bytes 2359304 | tf_op jit(solution)/shard_map/ppermute | solution.py:63
  272.4 88.4 %collective-permute-start.66 = (bf16[2,1,768,512]{3,2,1,0:T(8,128)(2,1)}, bf16[2,1,768,512]{3,2,1,0:T(8,128)(2,1)S(1)}, u32[]{:S(2)}, u32[]{:S(2)}) collective-permute-start(bf16[2,1,768,512]{3,2,1,0:T(8,128)(2,1)} %get-tuple-element.63), channel_id=1, source_target_pairs={{0,1},{1,0},{2,3},{3,2},{4,5},{5,4},{6,7},{7,6},{8,9},{9,8},{10,11... | collective-permute-start | bytes 4718600 | tf_op jit(solution)/shard_map/ppermute | solution.py:68
  274.2 20.5 %collective-permute-start.28 = (bf16[1,768,512]{2,1,0:T(8,128)(2,1)S(1)}, bf16[1,768,512]{2,1,0:T(8,128)(2,1)S(1)}, u32[]{:S(2)}, u32[]{:S(2)}) collective-permute-start(bf16[1,768,512]{2,1,0:T(8,128)(2,1)S(1)} %slice.482), channel_id=1, source_target_pairs={{0,2},{2,0},{1,3},{3,1},{4,6},{6,4},{5,7},{7,5},{8,10},{10,8},{9,1... | collective-permute-start | bytes 2359304 | tf_op jit(solution)/shard_map/ppermute | solution.py:62
  276.5 48.6 %collective-permute-start.29 = (bf16[1,768,512]{2,1,0:T(8,128)(2,1)S(1)}, bf16[1,768,512]{2,1,0:T(8,128)(2,1)S(1)}, u32[]{:S(2)}, u32[]{:S(2)}) collective-permute-start(bf16[1,768,512]{2,1,0:T(8,128)(2,1)S(1)} %slice.483), channel_id=1, source_target_pairs={{0,1},{1,0},{2,3},{3,2},{4,5},{5,4},{6,7},{7,6},{8,9},{9,8},{10,11... | collective-permute-start | bytes 2359304 | tf_op jit(solution)/shard_map/ppermute | solution.py:63
  277.5 97.5 %collective-permute-start.68 = (bf16[2,1,768,512]{3,2,1,0:T(8,128)(2,1)}, bf16[2,1,768,512]{3,2,1,0:T(8,128)(2,1)}, u32[]{:S(2)}, u32[]{:S(2)}) collective-permute-start(bf16[2,1,768,512]{3,2,1,0:T(8,128)(2,1)} %get-tuple-element.65), channel_id=1, source_target_pairs={{0,2},{2,0},{1,3},{3,1},{4,6},{6,4},{5,7},{7,5},{8,10},{10,8},{9,1... | collective-permute-start | bytes 4718600 | tf_op jit(solution)/shard_map/ppermute | solution.py:69
  348.7 35.2 %collective-permute-start.70 = (bf16[2,1,768,512]{3,2,1,0:T(8,128)(2,1)}, bf16[2,1,768,512]{3,2,1,0:T(8,128)(2,1)}, u32[]{:S(2)}, u32[]{:S(2)}) collective-permute-start(bf16[2,1,768,512]{3,2,1,0:T(8,128)(2,1)} %get-tuple-element.67), channel_id=1, source_target_pairs={{0,1},{1,0},{2,3},{3,2},{4,5},{5,4},{6,7},{7,6},{8,9},{9,8},{10,11... | collective-permute-start | bytes 4718600 | tf_op jit(solution)/shard_map/ppermute | solution.py:68
  354.1 40.0 %collective-permute-start.30 = (bf16[4,256,1024]{2,1,0:T(8,128)(2,1)}, bf16[4,256,1024]{2,1,0:T(8,128)(2,1)}, u32[]{:S(2)}, u32[]{:S(2)}) collective-permute-start(bf16[4,256,1024]{2,1,0:T(8,128)(2,1)} %combine.5), channel_id=1, source_target_pairs={{0,4},{4,0},{1,5},{5,1},{2,6},{6,2},{3,7},{7,3},{8,12},{12,8},{9,1... | collective-permute-start | bytes 6291464 | tf_op jit(solution)/shard_map/ppermute | solution.py:47
  354.1 37.6 %collective-permute-start.72 = (bf16[2,1,768,512]{3,2,1,0:T(8,128)(2,1)}, bf16[2,1,768,512]{3,2,1,0:T(8,128)(2,1)}, u32[]{:S(2)}, u32[]{:S(2)}) collective-permute-start(bf16[2,1,768,512]{3,2,1,0:T(8,128)(2,1)} %get-tuple-element.69), channel_id=1, source_target_pairs={{0,2},{2,0},{1,3},{3,1},{4,6},{6,4},{5,7},{7,5},{8,10},{10,8},{9,1... | collective-permute-start | bytes 4718600 | tf_op jit(solution)/shard_map/ppermute | solution.py:69
  360.7 38.3 %collective-permute-start.34 = (bf16[4,256,1152]{2,1,0:T(8,128)(2,1)}, bf16[4,256,1152]{2,1,0:T(8,128)(2,1)}, u32[]{:S(2)}, u32[]{:S(2)}) collective-permute-start(bf16[4,256,1152]{2,1,0:T(8,128)(2,1)} %combine.7), channel_id=1, source_target_pairs={{0,4},{4,0},{1,5},{5,1},{2,6},{6,2},{3,7},{7,3},{8,12},{12,8},{9,1... | collective-permute-start | bytes 7077896 | tf_op jit(solution)/shard_map/ppermute | solution.py:47
  374.9 33.5 %collective-permute-start.67 = (bf16[1,768,512]{2,1,0:T(8,128)(2,1)S(1)}, bf16[1,768,512]{2,1,0:T(8,128)(2,1)S(1)}, u32[]{:S(2)}, u32[]{:S(2)}) collective-permute-start(bf16[1,768,512]{2,1,0:T(8,128)(2,1)S(1)} %fusion.17), channel_id=1, source_target_pairs={{0,2},{2,0},{1,3},{3,1},{4,6},{6,4},{5,7},{7,5},{8,10},{10,8},{9,1... | collective-permute-start | bytes 2359304 | tf_op jit(solution)/shard_map/ppermute | solution.py:72
  383.9 25.7 %collective-permute-start.69 = (bf16[1,768,512]{2,1,0:T(8,128)(2,1)S(1)}, bf16[1,768,512]{2,1,0:T(8,128)(2,1)S(1)}, u32[]{:S(2)}, u32[]{:S(2)}) collective-permute-start(bf16[1,768,512]{2,1,0:T(8,128)(2,1)S(1)} %fusion.18), channel_id=1, source_target_pairs={{0,1},{1,0},{2,3},{3,2},{4,5},{5,4},{6,7},{7,6},{8,9},{9,8},{10,11... | collective-permute-start | bytes 2359304 | tf_op jit(solution)/shard_map/ppermute | solution.py:73
  391.7 33.1 %collective-permute-start.71 = (bf16[1,768,512]{2,1,0:T(8,128)(2,1)S(1)}, bf16[1,768,512]{2,1,0:T(8,128)(2,1)S(1)}, u32[]{:S(2)}, u32[]{:S(2)}) collective-permute-start(bf16[1,768,512]{2,1,0:T(8,128)(2,1)S(1)} %fusion.19), channel_id=1, source_target_pairs={{0,2},{2,0},{1,3},{3,1},{4,6},{6,4},{5,7},{7,5},{8,10},{10,8},{9,1... | collective-permute-start | bytes 2359304 | tf_op jit(solution)/shard_map/ppermute | solution.py:72
  394.2 32.9 %collective-permute-start.73 = (bf16[1,768,512]{2,1,0:T(8,128)(2,1)S(1)}, bf16[1,768,512]{2,1,0:T(8,128)(2,1)S(1)}, u32[]{:S(2)}, u32[]{:S(2)}) collective-permute-start(bf16[1,768,512]{2,1,0:T(8,128)(2,1)S(1)} %fusion.20), channel_id=1, source_target_pairs={{0,1},{1,0},{2,3},{3,2},{4,5},{5,4},{6,7},{7,6},{8,9},{9,8},{10,11... | collective-permute-start | bytes 2359304 | tf_op jit(solution)/shard_map/ppermute | solution.py:73
  399.0 78.6 %collective-permute-start.31 = (bf16[256,1024]{1,0:T(8,128)(2,1)}, bf16[256,1024]{1,0:T(8,128)(2,1)S(1)}, u32[]{:S(2)}, u32[]{:S(2)}) collective-permute-start(bf16[256,1024]{1,0:T(8,128)(2,1)} %get-tuple-element.141), channel_id=1, source_target_pairs={{0,8},{8,16},{16,24},{24,0},{1,9},{9,17},{17,25},{25,1},{2,10},{10... | collective-permute-start | bytes 1572872 | tf_op jit(solution)/shard_map/ppermute | solution.py:51
  408.5 69.1 %collective-permute-start.32 = (bf16[256,1024]{1,0:T(8,128)(2,1)}, bf16[256,1024]{1,0:T(8,128)(2,1)S(1)}, u32[]{:S(2)}, u32[]{:S(2)}) collective-permute-start(bf16[256,1024]{1,0:T(8,128)(2,1)} %get-tuple-element.143), channel_id=1, source_target_pairs={{0,16},{8,24},{16,0},{24,8},{1,17},{9,25},{17,1},{25,9},{2,18},{10... | collective-permute-start | bytes 1572872 | tf_op jit(solution)/shard_map/ppermute | solution.py:51
  409.6 30.5 %collective-permute-start.35 = (bf16[256,1152]{1,0:T(8,128)(2,1)S(1)}, bf16[256,1152]{1,0:T(8,128)(2,1)S(1)}, u32[]{:S(2)}, u32[]{:S(2)}) collective-permute-start(bf16[256,1152]{1,0:T(8,128)(2,1)S(1)} %get-tuple-element.132), channel_id=1, source_target_pairs={{0,8},{8,16},{16,24},{24,0},{1,9},{9,17},{17,25},{25,1},{2,10},{10... | collective-permute-start | bytes 1769480 | tf_op jit(solution)/shard_map/ppermute | solution.py:51
  424.9 49.3 %collective-permute-start.36 = (bf16[256,1152]{1,0:T(8,128)(2,1)S(1)}, bf16[256,1152]{1,0:T(8,128)(2,1)S(1)}, u32[]{:S(2)}, u32[]{:S(2)}) collective-permute-start(bf16[256,1152]{1,0:T(8,128)(2,1)S(1)} %get-tuple-element.134), channel_id=1, source_target_pairs={{0,16},{8,24},{16,0},{24,8},{1,17},{9,25},{17,1},{25,9},{2,18},{10... | collective-permute-start | bytes 1769480 | tf_op jit(solution)/shard_map/ppermute | solution.py:51
  427.1 47.1 %collective-permute-start.37 = (bf16[256,1152]{1,0:T(8,128)(2,1)S(1)}, bf16[256,1152]{1,0:T(8,128)(2,1)S(1)}, u32[]{:S(2)}, u32[]{:S(2)}) collective-permute-start(bf16[256,1152]{1,0:T(8,128)(2,1)S(1)} %get-tuple-element.133), channel_id=1, source_target_pairs={{0,24},{8,0},{16,8},{24,16},{1,25},{9,1},{17,9},{25,17},{2,26},{10... | collective-permute-start | bytes 1769480 | tf_op jit(solution)/shard_map/ppermute | solution.py:51
  440.0 51.9 %collective-permute-start.33 = (bf16[256,1024]{1,0:T(8,128)(2,1)S(1)}, bf16[256,1024]{1,0:T(8,128)(2,1)S(1)}, u32[]{:S(2)}, u32[]{:S(2)}) collective-permute-start(bf16[256,1024]{1,0:T(8,128)(2,1)S(1)} %copy-done.39), channel_id=1, source_target_pairs={{0,24},{8,0},{16,8},{24,16},{1,25},{9,1},{17,9},{25,17},{2,26},{10... | collective-permute-start | bytes 1572872 | tf_op jit(solution)/shard_map/ppermute | solution.py:51
  529.5 9.2 %collective-permute-start.38 = (bf16[2,128,1024]{2,1,0:T(8,128)(2,1)S(1)}, bf16[2,128,1024]{2,1,0:T(8,128)(2,1)S(1)}, u32[]{:S(2)}, u32[]{:S(2)}) collective-permute-start(bf16[2,128,1024]{2,1,0:T(8,128)(2,1)S(1)} %pad_maximum_fusion.15), channel_id=1, source_target_pairs={{0,1},{1,0},{2,3},{3,2},{4,5},{5,4},{6,7},{7,6},{8,9},{9,8},{10,11... | collective-permute-start | bytes 1572872 | tf_op jit(solution)/shard_map/ppermute | solution.py:68
  535.9 11.6 %collective-permute-start.40 = (bf16[2,128,1024]{2,1,0:T(8,128)(2,1)S(1)}, bf16[2,128,1024]{2,1,0:T(8,128)(2,1)S(1)}, u32[]{:S(2)}, u32[]{:S(2)}) collective-permute-start(bf16[2,128,1024]{2,1,0:T(8,128)(2,1)S(1)} %pad_maximum_fusion.16), channel_id=1, source_target_pairs={{0,2},{2,0},{1,3},{3,1},{4,6},{6,4},{5,7},{7,5},{8,10},{10,8},{9,1... | collective-permute-start | bytes 1572872 | tf_op jit(solution)/shard_map/ppermute | solution.py:69
  538.8 11.5 %collective-permute-start.39 = (bf16[128,1024]{1,0:T(8,128)(2,1)S(1)}, bf16[128,1024]{1,0:T(8,128)(2,1)S(1)}, u32[]{:S(2)}, u32[]{:S(2)}) collective-permute-start(bf16[128,1024]{1,0:T(8,128)(2,1)S(1)} %fusion.24), channel_id=1, source_target_pairs={{0,2},{2,0},{1,3},{3,1},{4,6},{6,4},{5,7},{7,5},{8,10},{10,8},{9,1... | collective-permute-start | bytes 786440 | tf_op jit(solution)/shard_map/ppermute | solution.py:72
  539.9 18.8 %collective-permute-start.54 = (bf16[4,128,1536]{2,1,0:T(8,128)(2,1)S(1)}, bf16[4,128,1536]{2,1,0:T(8,128)(2,1)S(1)}, u32[]{:S(2)}, u32[]{:S(2)}) collective-permute-start(bf16[4,128,1536]{2,1,0:T(8,128)(2,1)S(1)} %slice_bitcast_fusion.1), channel_id=1, source_target_pairs={{0,4},{4,0},{1,5},{5,1},{2,6},{6,2},{3,7},{7,3},{8,12},{12,8},{9,1... | collective-permute-start | bytes 4718600 | tf_op jit(solution)/shard_map/ppermute | solution.py:47
  551.6 10.5 %collective-permute-start.42 = (bf16[4,128,1664]{2,1,0:T(8,128)(2,1)S(1)}, bf16[4,128,1664]{2,1,0:T(8,128)(2,1)S(1)}, u32[]{:S(2)}, u32[]{:S(2)}) collective-permute-start(bf16[4,128,1664]{2,1,0:T(8,128)(2,1)S(1)} %slice_bitcast_fusion), channel_id=1, source_target_pairs={{0,4},{4,0},{1,5},{5,1},{2,6},{6,2},{3,7},{7,3},{8,12},{12,8},{9,1... | collective-permute-start | bytes 5111816 | tf_op jit(solution)/shard_map/ppermute | solution.py:47
  559.2 9.7 %collective-permute-start.55 = (bf16[2,64,1536]{2,1,0:T(8,128)(2,1)S(1)}, bf16[2,64,1536]{2,1,0:T(8,128)(2,1)S(1)}, u32[]{:S(2)}, u32[]{:S(2)}) collective-permute-start(bf16[2,64,1536]{2,1,0:T(8,128)(2,1)S(1)} %pad_maximum_fusion.21), channel_id=1, source_target_pairs={{0,1},{1,0},{2,3},{3,2},{4,5},{5,4},{6,7},{7,6},{8,9},{9,8},{10,11... | collective-permute-start | bytes 1179656 | tf_op jit(solution)/shard_map/ppermute | solution.py:68
  560.2 11.5 %collective-permute-start.57 = (bf16[2,64,1536]{2,1,0:T(8,128)(2,1)S(1)}, bf16[2,64,1536]{2,1,0:T(8,128)(2,1)S(1)}, u32[]{:S(2)}, u32[]{:S(2)}) collective-permute-start(bf16[2,64,1536]{2,1,0:T(8,128)(2,1)S(1)} %stack.191), channel_id=1, source_target_pairs={{0,2},{2,0},{1,3},{3,1},{4,6},{6,4},{5,7},{7,5},{8,10},{10,8},{9,1... | collective-permute-start | bytes 1179656 | tf_op jit(solution)/shard_map/ppermute | solution.py:69
  574.3 18.4 %collective-permute-start.43 = (bf16[2,64,1664]{2,1,0:T(8,128)(2,1)S(1)}, bf16[2,64,1664]{2,1,0:T(8,128)(2,1)S(1)}, u32[]{:S(2)}, u32[]{:S(2)}) collective-permute-start(bf16[2,64,1664]{2,1,0:T(8,128)(2,1)S(1)} %pad_maximum_fusion.19), channel_id=1, source_target_pairs={{0,1},{1,0},{2,3},{3,2},{4,5},{5,4},{6,7},{7,6},{8,9},{9,8},{10,11... | collective-permute-start | bytes 1277960 | tf_op jit(solution)/shard_map/ppermute | solution.py:68
  576.4 16.4 %collective-permute-start.45 = (bf16[2,64,1664]{2,1,0:T(8,128)(2,1)S(1)}, bf16[2,64,1664]{2,1,0:T(8,128)(2,1)S(1)}, u32[]{:S(2)}, u32[]{:S(2)}) collective-permute-start(bf16[2,64,1664]{2,1,0:T(8,128)(2,1)S(1)} %stack.190), channel_id=1, source_target_pairs={{0,2},{2,0},{1,3},{3,1},{4,6},{6,4},{5,7},{7,5},{8,10},{10,8},{9,1... | collective-permute-start | bytes 1277960 | tf_op jit(solution)/shard_map/ppermute | solution.py:69
  580.2 15.0 %collective-permute-start.59 = (bf16[32,1536]{1,0:T(8,128)(2,1)S(1)}, bf16[32,1536]{1,0:T(8,128)(2,1)S(1)}, u32[]{:S(2)}, u32[]{:S(2)}) collective-permute-start(bf16[32,1536]{1,0:T(8,128)(2,1)S(1)} %get-tuple-element.178), channel_id=1, source_target_pairs={{0,8},{8,16},{16,24},{24,0},{1,9},{9,17},{17,25},{25,1},{2,10},{10... | collective-permute-start | bytes 294920 | tf_op jit(solution)/shard_map/ppermute | solution.py:51
  590.3 11.7 %collective-permute-start.60 = (bf16[32,1536]{1,0:T(8,128)(2,1)S(1)}, bf16[32,1536]{1,0:T(8,128)(2,1)S(1)}, u32[]{:S(2)}, u32[]{:S(2)}) collective-permute-start(bf16[32,1536]{1,0:T(8,128)(2,1)S(1)} %get-tuple-element.180), channel_id=1, source_target_pairs={{0,16},{8,24},{16,0},{24,8},{1,17},{9,25},{17,1},{25,9},{2,18},{10... | collective-permute-start | bytes 294920 | tf_op jit(solution)/shard_map/ppermute | solution.py:51
  590.7 11.4 %collective-permute-start.61 = (bf16[32,1536]{1,0:T(8,128)(2,1)S(1)}, bf16[32,1536]{1,0:T(8,128)(2,1)S(1)}, u32[]{:S(2)}, u32[]{:S(2)}) collective-permute-start(bf16[32,1536]{1,0:T(8,128)(2,1)S(1)} %get-tuple-element.179), channel_id=1, source_target_pairs={{0,24},{8,0},{16,8},{24,16},{1,25},{9,1},{17,9},{25,17},{2,26},{10... | collective-permute-start | bytes 294920 | tf_op jit(solution)/shard_map/ppermute | solution.py:51
  592.9 13.4 %collective-permute-start.44 = (bf16[64,1664]{1,0:T(8,128)(2,1)S(1)}, bf16[64,1664]{1,0:T(8,128)(2,1)S(1)}, u32[]{:S(2)}, u32[]{:S(2)}) collective-permute-start(bf16[64,1664]{1,0:T(8,128)(2,1)S(1)} %get-tuple-element.147), channel_id=1, source_target_pairs={{0,2},{2,0},{1,3},{3,1},{4,6},{6,4},{5,7},{7,5},{8,10},{10,8},{9,1... | collective-permute-start | bytes 638984 | tf_op jit(solution)/shard_map/ppermute | solution.py:72
  593.3 13.0 %collective-permute-start.46 = (bf16[64,1664]{1,0:T(8,128)(2,1)S(1)}, bf16[64,1664]{1,0:T(8,128)(2,1)S(1)}, u32[]{:S(2)}, u32[]{:S(2)}) collective-permute-start(bf16[64,1664]{1,0:T(8,128)(2,1)S(1)} %get-tuple-element.146), channel_id=1, source_target_pairs={{0,1},{1,0},{2,3},{3,2},{4,5},{5,4},{6,7},{7,6},{8,9},{9,8},{10,11... | collective-permute-start | bytes 638984 | tf_op jit(solution)/shard_map/ppermute | solution.py:73
  602.1 8.9 %collective-permute-start.62 = (bf16[32,1536]{1,0:T(8,128)(2,1)S(1)}, bf16[32,1536]{1,0:T(8,128)(2,1)S(1)}, u32[]{:S(2)}, u32[]{:S(2)}) collective-permute-start(bf16[32,1536]{1,0:T(8,128)(2,1)S(1)} %fusion.41), channel_id=1, source_target_pairs={{0,24},{8,0},{16,8},{24,16},{1,25},{9,1},{17,9},{25,17},{2,26},{10... | collective-permute-start | bytes 294920 | tf_op jit(solution)/shard_map/ppermute | solution.py:51
  602.2 15.5 %collective-permute-start.63 = (bf16[32,1536]{1,0:T(8,128)(2,1)S(1)}, bf16[32,1536]{1,0:T(8,128)(2,1)S(1)}, u32[]{:S(2)}, u32[]{:S(2)}) collective-permute-start(bf16[32,1536]{1,0:T(8,128)(2,1)S(1)} %fusion.41), channel_id=1, source_target_pairs={{0,16},{8,24},{16,0},{24,8},{1,17},{9,25},{17,1},{25,9},{2,18},{10... | collective-permute-start | bytes 294920 | tf_op jit(solution)/shard_map/ppermute | solution.py:51
  606.3 11.4 %collective-permute-start.64 = (bf16[32,1536]{1,0:T(8,128)(2,1)S(1)}, bf16[32,1536]{1,0:T(8,128)(2,1)S(1)}, u32[]{:S(2)}, u32[]{:S(2)}) collective-permute-start(bf16[32,1536]{1,0:T(8,128)(2,1)S(1)} %fusion.41), channel_id=1, source_target_pairs={{0,8},{8,16},{16,24},{24,0},{1,9},{9,17},{17,25},{25,1},{2,10},{10... | collective-permute-start | bytes 294920 | tf_op jit(solution)/shard_map/ppermute | solution.py:51
  606.6 12.0 %collective-permute-start.47 = (bf16[32,1664]{1,0:T(8,128)(2,1)S(1)}, bf16[32,1664]{1,0:T(8,128)(2,1)S(1)}, u32[]{:S(2)}, u32[]{:S(2)}) collective-permute-start(bf16[32,1664]{1,0:T(8,128)(2,1)S(1)} %get-tuple-element.175), channel_id=1, source_target_pairs={{0,8},{8,16},{16,24},{24,0},{1,9},{9,17},{17,25},{25,1},{2,10},{10... | collective-permute-start | bytes 319496 | tf_op jit(solution)/shard_map/ppermute | solution.py:51
  607.2 12.8 %collective-permute-start.48 = (bf16[32,1664]{1,0:T(8,128)(2,1)S(1)}, bf16[32,1664]{1,0:T(8,128)(2,1)S(1)}, u32[]{:S(2)}, u32[]{:S(2)}) collective-permute-start(bf16[32,1664]{1,0:T(8,128)(2,1)S(1)} %get-tuple-element.177), channel_id=1, source_target_pairs={{0,16},{8,24},{16,0},{24,8},{1,17},{9,25},{17,1},{25,9},{2,18},{10... | collective-permute-start | bytes 319496 | tf_op jit(solution)/shard_map/ppermute | solution.py:51
  611.0 9.0 %collective-permute-start.49 = (bf16[32,1664]{1,0:T(8,128)(2,1)S(1)}, bf16[32,1664]{1,0:T(8,128)(2,1)S(1)}, u32[]{:S(2)}, u32[]{:S(2)}) collective-permute-start(bf16[32,1664]{1,0:T(8,128)(2,1)S(1)} %get-tuple-element.176), channel_id=1, source_target_pairs={{0,24},{8,0},{16,8},{24,16},{1,25},{9,1},{17,9},{25,17},{2,26},{10... | collective-permute-start | bytes 319496 | tf_op jit(solution)/shard_map/ppermute | solution.py:51
  623.4 7.5 %collective-permute-start.65 = (bf16[128,1536]{0,1:T(8,128)(2,1)S(1)}, bf16[128,1536]{0,1:T(8,128)(2,1)S(1)}, u32[]{:S(2)}, u32[]{:S(2)}) collective-permute-start(bf16[128,1536]{0,1:T(8,128)(2,1)S(1)} %broadcast_select_fusion.3), channel_id=1, source_target_pairs={{0,4},{4,0},{1,5},{5,1},{2,6},{6,2},{3,7},{7,3},{8,12},{12,8},{9,1... | collective-permute-start | bytes 1179656 | tf_op jit(solution)/shard_map/ppermute | solution.py:47
  (55 other events, 494.8 us)

commit v4 on v3

--- a/solution.py
+++ b/solution.py
@@ -55,52 +55,80 @@
     return lax.optimization_barrier((value, *others))[0]
 
 
+def gather_near(shard):
+    return [lax.ppermute(shard, "x", SWAP), lax.ppermute(shard, "y", SWAP)]
+
+
+def gather_far(near):
+    from_x, from_y = near
+    half = from_x.shape[0] // 2
+    return [lax.ppermute(from_x[:half], "y", SWAP), lax.ppermute(from_y[half:], "x", SWAP)]
+
+
 def grid_gather(shard):
+    near = gather_near(shard)
+    return near + gather_far(near)
+
+
+def cross(to_x, to_y):
+    return lax.ppermute(to_x, "x", SWAP), lax.ppermute(to_y, "y", SWAP)
+
+
+def far_and_next(near, shard):
+    from_x, from_y = near
     half = shard.shape[0] // 2
-    from_x = lax.ppermute(shard, "x", SWAP)
-    from_y = lax.ppermute(shard, "y", SWAP)
-    diag_a = lax.ppermute(from_x[:half], "y", SWAP)
-    diag_b = lax.ppermute(from_y[half:], "x", SWAP)
-    return shard, from_x, from_y, diag_a, diag_b
-
-
-def grid_scatter(first_a, rest_a, first_b, rest_b):
-    got_a = lax.ppermute(first_a, "x", SWAP)
-    got_b = lax.ppermute(first_b, "y", SWAP)
+    return cross(
+        jnp.concatenate([from_y[-half:], shard], axis=0),
+        jnp.concatenate([from_x[-2 * half : -half], shard], axis=0),
+    )
+
+
+def plus_low(a, b):
+    return (a.astype(F32) + b.astype(F32)).astype(B16)
+
+
+def grid_scatter_first(first_a, first_b):
+    return lax.ppermute(first_a, "x", SWAP), lax.ppermute(first_b, "y", SWAP)
+
+
+def grid_scatter_second(got, rest_a, rest_b, *hold):
+    got_a, got_b = got
     onward_a = (rest_a[1].astype(F32) + got_a[1].astype(F32)).astype(B16)
     onward_b = (rest_b[1].astype(F32) + got_b[1].astype(F32)).astype(B16)
     last_a = lax.ppermute(onward_a, "y", SWAP)
     last_b = lax.ppermute(onward_b, "x", SWAP)
+    last_a, last_b = after((last_a, last_b), *hold)
     return (
         rest_a[0].astype(F32) + got_a[0].astype(F32) + last_a.astype(F32),
         rest_b[0].astype(F32) + got_b[0].astype(F32) + last_b.astype(F32),
     )
 
 
-def grid_scatter_rows(parts):
-    own, to_x, to_y, diag = parts
+def row_halves(parts):
+    own, to_x, to_y, diag = [parts[j] for j in range(4)]
     half = own.shape[0] // 2
-    total = grid_scatter(
+    first = (
         jnp.stack([to_x[:half], diag[:half]]),
-        (own[:half], to_y[:half]),
         jnp.stack([to_y[half:], diag[half:]]),
-        (own[half:], to_x[half:]),
     )
-    return jnp.concatenate(total, axis=0)
-
-
-def column_gather(rows, size):
-    mine = jnp.stack([rows] + [cyclic(rows, size, -k) for k in range(1, size)])
-    return mine, swap_core(mine)
-
-
-def column_scatter(mine, other, size):
+    return first, (own[:half], to_y[:half]), (own[half:], to_x[half:])
+
+
+def column_pieces(rows, size):
+    return [rows] + [cyclic(rows, size, -k) for k in range(1, size)]
+
+
+def column_low(mine, other):
     both = mine.astype(F32) + swap_core(other).astype(F32)
-    low = both.astype(B16)
-    total = both[0]
-    for k in range(1, size):
-        total = total + cyclic(low[k], size, k).astype(F32)
-    return total
+    return both[0], both.astype(B16)
+
+
+def column_send(low, size):
+    return [cyclic(low[k], size, k) for k in range(1, size)]
+
+
+def column_sum(own, pieces):
+    return own + sum(piece.astype(F32) for piece in pieces)
 
 
 def assemble(places, shard, moved, other, rows):
@@ -257,22 +285,24 @@
     )(lead, packed, *slot_rows)
 
 
-def experts(order, start, count, skip, rows, grads, gates, weights, capacity, in_rows, mid_rows):
+def experts(order, start, count, rows, grads, gates, weights, chunks, capacity, in_rows, mid_rows):
     half, _, width = rows[0].shape
     pieces = 2 * half
-    n = len(weights)
+    split = bool(chunks)
+    n = 4 if split else len(weights)
+    extra = [array for chunk in chunks for array, _ in chunk]
+    given = len(weights) + len(extra)
     pack_rows, eff = weights[0].shape[1:]
     folds = width // eff
     total_rows = pieces * capacity
-    split = n == 4
     first_half = count // 2
     large = total_rows > 1000
 
     def kernel(order_ref, *refs):
         rows_a, rows_b, grads_a, grads_b, gates_a, gates_b = refs[:6]
-        pack = refs[6 : 6 + n]
-        y_out, dx_out = refs[6 + n : 8 + n]
-        outs = refs[8 + n : -6]
+        pack = refs[6 : 6 + given]
+        y_out, dx_out = refs[6 + given : 8 + given]
+        outs = refs[8 + given : -6]
         full_g, full_u, full_d, grad_g, grad_u, grad_d = refs[-6:]
 
         def at_in(j):
@@ -281,13 +311,41 @@
         def at_mid(j):
             return pl.ds(pl.multiple_of(order_ref[j] * mid_rows, mid_rows), mid_rows)
 
-        for j in range(n):
-            full_g[at_in(j), :] = pack[j][0, :in_rows]
-            full_u[at_in(j), :] = pack[j][0, in_rows : 2 * in_rows]
+        def load(j, take):
+            full_g[at_in(j), :] = take(0, in_rows)
+            full_u[at_in(j), :] = take(in_rows, 2 * in_rows)
             for f in range(folds):
-                full_d[at_mid(j), f * eff : (f + 1) * eff] = pack[j][
-                    0, 2 * in_rows + f * mid_rows : 2 * in_rows + (f + 1) * mid_rows
-                ]
+                full_d[at_mid(j), f * eff : (f + 1) * eff] = take(
+                    2 * in_rows + f * mid_rows, 2 * in_rows + (f + 1) * mid_rows
+                )
+
+        def rows_from(ref, offset):
+            return lambda lo, hi: ref[offset + lo : offset + hi, :]
+
+        def two_halves(a, b):
+            middle = pack_rows // 2
+
+            def take(lo, hi):
+                if hi <= middle:
+                    return a(lo, hi)
+                if lo >= middle:
+                    return b(lo - middle, hi - middle)
+                return jnp.concatenate([a(lo, middle), b(0, hi - middle)], axis=0)
+
+            return take
+
+        for j in range(len(weights)):
+            load(j, lambda lo, hi, ref=pack[j]: ref[0, lo:hi])
+        for c in range(len(chunks)):
+            from_x, from_y, diag_a, diag_b = [
+                rows_from(pack[1 + 4 * c + i], chunks[c][i][1]) for i in range(4)
+            ]
+
+            @pl.when(pl.program_id(0) == c)
+            def _():
+                load(1, from_x)
+                load(2, from_y)
+                load(3, two_halves(diag_a, diag_b))
 
         def joined(a, b, w):
             return jnp.concatenate(
@@ -339,21 +397,16 @@
                 ]
 
         if split:
-            first_a, rest_a, first_b, rest_b = outs
 
             @pl.when(pl.program_id(0) < first_half)
             def _():
-                give(first_a, 0, 1)
-                give(first_a, 1, 3)
-                give(rest_a, 0, 0)
-                give(rest_a, 1, 2)
+                for j in range(4):
+                    give(outs[j], 0, j)
 
             @pl.when(pl.program_id(0) >= first_half)
             def _():
-                give(first_b, 0, 2)
-                give(first_b, 1, 3)
-                give(rest_b, 0, 0)
-                give(rest_b, 1, 1)
+                for j in range(4):
+                    give(outs[4 + j], 0, j)
         else:
             for j in range(n):
                 give(outs[0], j, j)
@@ -365,10 +418,10 @@
         return pl.BlockSpec((half, capacity, w), lambda e, o: (0, e + start, 0), **single())
 
     in_specs = [rows_spec(width)] * 4 + [rows_spec(128)] * 2
-    for j in range(n):
-        in_specs.append(
-            pl.BlockSpec((1, pack_rows, eff), lambda e, o, lead=start - skip[j]: (e + lead, 0, 0))
-        )
+    for _ in weights:
+        in_specs.append(pl.BlockSpec((1, pack_rows, eff), lambda e, o: (e + start, 0, 0)))
+    for part in extra:
+        in_specs.append(pl.BlockSpec(part.shape, lambda e, o: (0, 0)))
     slots = count * capacity
     out_specs = [
         pl.BlockSpec((pieces, capacity, w), lambda e, o: (0, e, 0), **single())
@@ -383,9 +436,9 @@
             lambda e, o: (0, jnp.minimum(e, first_half - 1), 0, 0),
             lambda e, o: (0, jnp.maximum(e - first_half, 0), 0, 0),
         ):
-            for _ in range(2):
-                out_specs.append(pl.BlockSpec((2, 1, pack_rows, eff), at))
-                out_shape.append(jax.ShapeDtypeStruct((2, first_half, pack_rows, eff), B16))
+            for _ in range(4):
+                out_specs.append(pl.BlockSpec((1, 1, pack_rows, eff), at))
+                out_shape.append(jax.ShapeDtypeStruct((1, first_half, pack_rows, eff), B16))
     else:
         out_specs.append(pl.BlockSpec((n, 1, pack_rows, eff), lambda e, o: (0, e, 0, 0)))
         out_shape.append(jax.ShapeDtypeStruct((n, count, pack_rows, eff), B16))
@@ -408,7 +461,7 @@
         ),
         compiler_params=pltpu.CompilerParams(vmem_limit_bytes=VMEM_LIMIT),
         name="experts",
-    )(order, *rows, *grads, *gates, *weights)
+    )(order, *rows, *grads, *gates, *weights, *extra)
     return results[0], results[1], results[2:]
 
 
@@ -435,22 +488,25 @@
     return jnp.cos(angles), jnp.sin(angles) * sign[None, :]
 
 
-def attention_forward(x_all, head_full, bias, cosine, sine, tok_rows):
+def attention_forward(x_all, dense_full, bias, cosine, sine, tok_rows):
     seq_len, width = x_all.shape
     scale = HD ** (-0.5)
     wide, narrow = H * HD, KVH * HD
 
     def kernel(
-        x_ref, tail_ref, wq_ref, wk_ref, wv_ref, bias_ref, cos_ref, sin_ref,
-        normed_ref, q_out, k_out, v_out, att_out, total_out, misc_out,
+        x_ref, tail_ref, wo_ref, wq_ref, wk_ref, wv_ref, bias_ref, cos_ref, sin_ref,
+        normed_ref, q_out, k_out, v_out, att_out, total_out, misc_out, residual_out, moe_out,
     ):
-        @pl.when(pl.program_id(0) == 0)
+        step = pl.program_id(0)
+
+        @pl.when(step == 0)
         def _():
             rows = jnp.transpose(tail_ref[...].astype(F32))
             misc_out[...] = rows
             x = x_ref[...].astype(F32)
             scaled = x * lax.rsqrt(jnp.mean(x * x, axis=1, keepdims=True) + EPSILON)
             normed_ref[...] = (scaled * rows[EXPERTS : EXPERTS + 1, :]).astype(B16)
+            residual_out[...] = x[:tok_rows]
 
         normed = normed_ref[...]
         cos, sin = cos_ref[...], sin_ref[...]
@@ -480,8 +536,16 @@
             )
             mixed.append(out / total)
             totals.append(peak + jnp.log(total))
-        att_out[...] = jnp.transpose(jnp.concatenate(mixed, axis=0)).astype(B16)
+        attended = jnp.transpose(jnp.concatenate(mixed, axis=0)).astype(B16)
+        att_out[...] = attended
         total_out[0] = jnp.concatenate(totals + totals, axis=0)
+        residual_out[...] += jnp.dot(attended, wo_ref[...], preferred_element_type=F32)
+
+        @pl.when(step == GROUPS - 1)
+        def _():
+            total = residual_out[...]
+            scaled = total * lax.rsqrt(jnp.mean(total * total, axis=1, keepdims=True) + EPSILON)
+            moe_out[...] = (scaled * misc_out[EXPERTS + 1 : EXPERTS + 2, :]).astype(B16)
 
     def fixed(*block):
         return pl.BlockSpec(block, lambda i: (0,) * len(block))
@@ -494,10 +558,11 @@
         grid=(GROUPS,),
         in_specs=[
             fixed(seq_len, width),
-            pl.BlockSpec((width, 128), lambda i: (0, (wide + 2 * narrow) // 128)),
-            columns(width, 256),
-            columns(width, 128, wide // 128),
-            columns(width, 128, (wide + narrow) // 128),
+            pl.BlockSpec((width, 128), lambda i: (0, (width + wide + 2 * narrow) // 128)),
+            pl.BlockSpec((256, width), lambda i: (i, 0)),
+            columns(width, 256, width // 256),
+            columns(width, 128, (width + wide) // 128),
+            columns(width, 128, (width + wide + narrow) // 128),
             fixed(seq_len, tok_rows),
             fixed(seq_len, 128),
             fixed(seq_len, 128),
@@ -510,6 +575,8 @@
             columns(tok_rows, 256),
             pl.BlockSpec((1, 8, tok_rows), lambda i: (i, 0, 0)),
             fixed(128, width),
+            fixed(tok_rows, width),
+            fixed(tok_rows, width),
         ],
         out_shape=[
             jax.ShapeDtypeStruct((seq_len, width), B16),
@@ -519,15 +586,17 @@
             jax.ShapeDtypeStruct((tok_rows, wide), B16),
             jax.ShapeDtypeStruct((GROUPS, 8, tok_rows), F32),
             jax.ShapeDtypeStruct((128, width), F32),
+            jax.ShapeDtypeStruct((tok_rows, width), F32),
+            jax.ShapeDtypeStruct((tok_rows, width), B16),
         ],
         compiler_params=pltpu.CompilerParams(vmem_limit_bytes=VMEM_LIMIT),
         name="attention",
-    )(x_all, head_full, head_full, head_full, head_full, bias, cosine, sine)
+    )(x_all, *[dense_full] * 5, bias, cosine, sine)
 
 
 def attention_backward(
-    where_here, out_grad_low, full_output, attended, moe_in, logit_low, moe_gain_row, saved,
-    x_all, head_full, bias, cosine, sine,
+    where_here, out_grad_low, attended, moe_in, logit_low, moe_gain_row, saved,
+    x_all, dense_full, bias, cosine, sine,
 ):
     normed_all, query_rot, key_rot, value_all, totals = saved
     seq_len, width = x_all.shape
@@ -659,9 +728,9 @@
                 columns(seq_len, 128),
                 pl.BlockSpec((1, 8, tok_rows), lambda i, here: (i, 0, 0)),
                 fixed(seq_len, width),
-                columns(width, 256),
-                columns(width, 128, wide // 128),
-                columns(width, 128, (wide + narrow) // 128),
+                columns(width, 256, width // 256),
+                columns(width, 128, (width + wide) // 128),
+                columns(width, 128, (width + wide + narrow) // 128),
                 fixed(seq_len, tok_rows),
                 fixed(seq_len, 128),
                 fixed(seq_len, 128),
@@ -675,26 +744,25 @@
         compiler_params=pltpu.CompilerParams(vmem_limit_bytes=VMEM_LIMIT),
         name="attention_grad",
     )(
-        where_here, out_grad_low, full_output, attended, moe_in, logit_low, moe_gain_row,
+        where_here, out_grad_low, dense_full, attended, moe_in, logit_low, moe_gain_row,
         normed_all, query_rot, key_rot, value_all, totals,
-        x_all, head_full, head_full, head_full, bias, cosine, sine,
+        x_all, dense_full, dense_full, dense_full, bias, cosine, sine,
     )
 
 
 def make_body(z_size, small_grid):
-    def dense_gather(shard, dp_index):
-        if not small_grid:
-            return lax.all_gather(shard, ("y", "x"), axis=0, tiled=True), shard
-        rows = shard.shape[0]
-        core = lax.axis_index("core")
-        mine = lax.dynamic_slice_in_dim(shard, core * (rows // 2), rows // 2, 0)
-        _, from_x, from_y, diag_a, diag_b = grid_gather(mine)
-        moved = jnp.concatenate([from_x, from_y, diag_a, diag_b], axis=0)
+    def core_half(shard, core):
+        rows = shard.shape[0] // 2
+        return lax.dynamic_slice_in_dim(shard, core * rows, rows, 0)
+
+    def dense_assemble(shard, parts, dp_index, core, *hold):
+        rows = shard.shape[0] // 2
+        moved = after(jnp.concatenate(parts, axis=0), *hold)
         other = swap_core(moved)
         places = [2 * dp_index]
         for which in (core, 1 - core):
             places += [2 * (dp_index ^ (j + 1)) + which for j in range(3)]
-        return assemble(jnp.stack(places), shard, moved, other, rows // 2), moved
+        return assemble(jnp.stack(places), shard, moved, other, rows)
 
     def across_z(mine, z):
         if z_size != 4:
@@ -710,9 +778,11 @@
         places = (jnp.arange(z_size, dtype=jnp.int32) - z) % z_size
         return jnp.take(jnp.stack(quarters), places, axis=0).reshape(mine.shape).astype(F32)
 
-    def dense_blocks_sum(blocks, z, core):
-        both = (blocks[0].astype(F32) + swap_core(blocks[1]).astype(F32)).astype(B16)
-        low = across_z(grid_scatter_rows(both), z).astype(B16)
+    def core_sum(blocks):
+        return (blocks[0].astype(F32) + swap_core(blocks[1]).astype(F32)).astype(B16)
+
+    def dense_finish(halves, z, core):
+        low = across_z(jnp.concatenate(halves, axis=0), z).astype(B16)
         other = swap_core(low)
         first = jnp.where(core == 0, low, other)
         second = jnp.where(core == 0, other, low)
@@ -754,18 +824,11 @@
 
         gains = jnp.stack([attn_gain, moe_gain], axis=1)
         rows = w_query.shape[0]
-        head_pack = jnp.concatenate(
-            [w_query, w_key, w_value, w_router, gains, jnp.zeros((rows, 94), B16)], axis=1
+        dense_pack = jnp.concatenate(
+            [w_output, w_query, w_key, w_value, w_router, gains, jnp.zeros((rows, 94), B16)], axis=1
         )
-        x_parts = grid_gather(layer_input) if small_grid else None
-        head_full, head_moved = dense_gather(head_pack, dp_index)
-        full_output, tail_moved = dense_gather(after(w_output, head_moved), dp_index)
         wide = H * HD
         narrow = KVH * HD
-        full_query = head_full[:, :wide]
-        full_key = head_full[:, wide : wide + narrow]
-        full_value = head_full[:, wide + narrow : wide + 2 * narrow]
-
         expert_ids = jnp.arange(EXPERTS, dtype=jnp.int32)
         hits = routes[:, :, None] == expert_ids[None, None, :]
         routed = jnp.any(hits, axis=1)
@@ -775,11 +838,28 @@
         ranks = jnp.sum((place[:, :, None] < place.T[None, :, :]).astype(F32), axis=0)
         code = pack_code(jnp.where(routed.T, ranks, -1.0).astype(B16))
         lead = ((2 * z + core) * local).astype(jnp.int32)[None]
-        grads_mine, grads_other = column_gather(
-            jnp.concatenate([out_grad, code], axis=0), z_size
-        )
-        (slot_grads_mine,) = dispatch_rows(lead, grads_mine, None, None, local, capacity)
-        (slot_grads_other,) = dispatch_rows(lead, grads_other, None, None, local, capacity)
+        grad_pieces = column_pieces(jnp.concatenate([out_grad, code], axis=0), z_size)
+
+        if small_grid:
+            side = tok_rows // 2
+            x_pack = jnp.concatenate([layer_input[:side], layer_input[side:]], axis=1)
+            start_parts = grid_gather(jnp.concatenate([x_pack, core_half(dense_pack, core)], axis=1))
+            dense_parts = [part[:, 2 * model_width :] for part in start_parts]
+            from_x, from_y, diag_a, diag_b = [
+                [part[:, :model_width], part[:, model_width : 2 * model_width]]
+                for part in start_parts
+            ]
+            x_all = jnp.concatenate(
+                [layer_input, *from_x, *from_y, diag_a[0], diag_b[0], diag_a[1], diag_b[1]], axis=0
+            )
+            dense_full = dense_assemble(dense_pack, dense_parts, dp_index, core, grad_pieces[1])
+        else:
+            dense_full = lax.all_gather(dense_pack, ("y", "x"), axis=0, tiled=True)
+            full_output = dense_full[:, :model_width]
+            head_full = dense_full[:, model_width:]
+            full_query = head_full[:, :wide]
+            full_key = head_full[:, wide : wide + narrow]
+            full_value = head_full[:, wide + narrow : wide + 2 * narrow]
 
         query_pos = dp_index * tok_rows + jnp.arange(tok_rows, dtype=jnp.int32)
         in_float = layer_input.astype(F32)
@@ -792,31 +872,30 @@
             relative = dp_index ^ jnp.arange(4, dtype=jnp.int32)
             key_pos = (relative[:, None] * tok_rows + steps[None, :]).reshape(seq_len)
             halves, per = 2, local // 2
-            expert_weights, skips = [], []
-            first = head_moved
-            for half in range(2):
-                own = after(pack[half * per : (half + 1) * per], first)
-                parts = grid_gather(own)
-                diag = jnp.concatenate([parts[3], parts[4]], axis=0)
-                expert_weights.append([own, parts[1], parts[2], diag])
-                skips.append([half * per] * 4)
-                first = parts[1]
+            weights = [pack]
+            near_0 = gather_near(after(pack[0], *start_parts[2:]))
+            far_0 = gather_far(after(near_0, dense_full))
+            near_1 = gather_near(after(pack[1], *near_0, dense_full))
         else:
             relative = jnp.arange(dp_size, dtype=jnp.int32)
             key_pos = jnp.arange(seq_len, dtype=jnp.int32)
             halves, per = 1, local
             every = lax.all_gather(pack, ("y", "x"), axis=0, tiled=False)
-            expert_weights = [[every[j] for j in range(dp_size)]]
-            skips = [[0] * dp_size]
+            weights = [every[j] for j in range(dp_size)]
+            near_0 = ()
         order = jnp.concatenate([relative, lead])
+        grads_mine = jnp.stack(after(grad_pieces, *near_0))
+        grads_other = swap_core(grads_mine)
         visible = (key_pos[None, :] <= query_pos[:, None]) | (key_pos[None, :] < prefix_len[0])
+        chunks = []
         if small_grid:
-            x_all = jnp.concatenate(x_parts, axis=0)
+            x_all = after(x_all, grads_mine, *near_0)
             bias = jnp.where(visible.T, 0.0, MASKED_SCORE)
             cosine, sine = turn_tables(key_pos.astype(F32))
-            normed_all, query_rot, key_rot, value_all, attended, totals, misc = attention_forward(
-                x_all, head_full, bias, cosine, sine, tok_rows
-            )
+            (
+                normed_all, query_rot, key_rot, value_all, attended, totals, misc, residual, moe_in,
+            ) = attention_forward(x_all, dense_full, bias, cosine, sine, tok_rows)
+            moe_in = after(moe_in, grads_other, *near_1, *far_0)
             router_rows = misc[:EXPERTS].astype(B16)
             full_attn_gain = misc[EXPERTS]
             full_moe_gain = misc[EXPERTS + 1]
@@ -858,31 +937,51 @@
                 )
                 log_totals.append(log_total)
             attended = jnp.concatenate(mixed_heads, axis=1).reshape(tok_rows, wide).astype(B16)
-        residual = in_float + jnp.dot(attended, full_output, preferred_element_type=F32)
-        moe_in = rms_norm(residual, full_moe_gain).astype(B16)
-
-        rows_mine, rows_other = column_gather(moe_in, z_size)
+            residual = in_float + jnp.dot(attended, full_output, preferred_element_type=F32)
+            moe_in = rms_norm(residual, full_moe_gain).astype(B16)
+
+        row_pieces = column_pieces(moe_in, z_size)
+        stage_1 = stage_2 = last_far = ()
+        if small_grid:
+            middle = pack.shape[1] // 2
+            stage_1 = far_and_next(after(near_1, moe_in), pack[2])
+        (slot_grads_mine,) = dispatch_rows(lead, after(grads_mine, moe_in), None, None, local, capacity)
+        (slot_grads_other,) = dispatch_rows(
+            lead, after(grads_other, slot_grads_mine, *stage_1), None, None, local, capacity
+        )
+        if small_grid:
+            stage_2 = far_and_next(after(stage_1, slot_grads_other), pack[3])
+            last_far = gather_far([part[middle:] for part in stage_2])
+            chunks = [
+                [(part, 0) for part in [*near_0, *far_0]],
+                [(part, 0) for part in [*near_1, *stage_1[::-1]]],
+                [(part, middle) for part in stage_1] + [(part, 0) for part in stage_2[::-1]],
+                [(part, middle) for part in stage_2] + [(part, 0) for part in last_far],
+            ]
+        rows_mine = jnp.stack(after(row_pieces, slot_grads_other, *stage_1))
+        rows_other = swap_core(rows_mine)
         slot_rows_mine, slot_gates_mine = dispatch_rows(
-            lead, grads_mine, rows_mine, router_rows, local, capacity
+            lead, grads_mine, after(rows_mine, *stage_2), router_rows, local, capacity
         )
         slot_rows_other, slot_gates_other = dispatch_rows(
-            lead, grads_other, rows_other, router_rows, local, capacity
+            lead, grads_other, after(rows_other, slot_rows_mine), router_rows, local, capacity
         )
+        slot_rows_other = after(slot_rows_other, *last_far)
         logits = lax.dot_general(moe_in, router_rows, NT, preferred_element_type=F32)
         peak = jnp.max(jnp.where(routed, logits, MASKED_SCORE), axis=-1, keepdims=True)
         lifted = jnp.where(routed, jnp.exp(jnp.minimum(logits - peak, 0.0)), 0.0)
         gate_weights = lifted / jnp.sum(lifted, axis=-1, keepdims=True)
-        ys, dxs, weight_grads = [], [], []
+        ys, dxs, weight_grads, sums = [], [], [], []
         for half in range(halves):
             y, dx, grads = experts(
                 order,
                 half * per,
                 per,
-                skips[half],
                 (slot_rows_mine, slot_rows_other),
                 (slot_grads_mine, slot_grads_other),
                 (slot_gates_mine, slot_gates_other),
-                expert_weights[half],
+                weights,
+                chunks[half * per : (half + 1) * per],
                 capacity,
                 in_rows,
                 mid_rows,
@@ -890,40 +989,46 @@
             ys.append(y)
             dxs.append(dx)
             weight_grads.append(grads)
+
+        def grid_sum(grads, got):
+            totals = []
+            for half in range(2):
+                own = grads[4 * half][0]
+                direct, last = got[half][0], got[1 - half][1]
+                totals.append(own.astype(F32) + direct.astype(F32) + last.astype(F32))
+            return totals
+
+        def second_step(grads, via, *more):
+            _, x_a, y_a, _, _, x_b, y_b, _ = grads
+            to_x = [x_a, plus_low(x_b, via[1])]
+            to_y = [y_b, plus_low(y_a, via[0])]
+            if more:
+                to_x.append(more[0])
+                to_y.append(more[1])
+            return cross(jnp.concatenate(to_x, axis=0), jnp.concatenate(to_y, axis=0))
+
+        if small_grid:
+            early, late = weight_grads
+            via = cross(early[3], early[7])
+            dxs = after(dxs, *via)
+            early_got = second_step(early, via, late[3], late[7])
         dx_other = combine_rows(lead, z_size, grads_other, dxs, local, capacity)
         dx_mine = combine_rows(lead, 0, grads_mine, dxs, local, capacity)
-        moe_sum = column_scatter(dx_mine, dx_other, z_size)
+        dx_own, dx_low = column_low(dx_mine, dx_other)
+        dx_pieces = column_send(dx_low, z_size)
+        ys = after(ys, dx_low)
+        y_other = combine_rows(lead, z_size, grads_other, ys, local, capacity)
+        y_mine = combine_rows(lead, 0, grads_mine, ys, local, capacity)
+        moe_sum = column_sum(dx_own, after(dx_pieces, y_other, y_mine))
+        y_own, y_low = column_low(y_mine, after(y_other, moe_sum))
+        y_pieces = [cyclic(y_low[k], z_size, k) for k in range(1, z_size) if 2 * k != z_size]
+        if small_grid:
+            late_got = second_step(late, [got[2:3] for got in after(early_got, moe_sum)])
         moe_in_grad = moe_sum[:, :model_width]
         gate_grad = (
             moe_sum[:, model_width : model_width + EXPERTS]
             + moe_sum[:, model_width + EXPERTS : model_width + 2 * EXPERTS]
         )
-        y_other = combine_rows(lead, z_size, grads_other, ys, local, capacity)
-        y_mine = combine_rows(lead, 0, grads_mine, ys, local, capacity)
-        mixture = column_scatter(y_mine, y_other, z_size)
-        layer_output = (residual + mixture).astype(B16)
-        if small_grid:
-            sums = []
-            for grads in weight_grads:
-                sums += list(grid_scatter(*grads))
-            pack_grad = jnp.concatenate(sums, axis=0)
-        else:
-            pack_grad = lax.psum_scatter(
-                weight_grads[0][0].astype(F32), ("y", "x"), scatter_dimension=0, tiled=False
-            )
-        down = 2 * in_rows
-        expert_grads = [
-            pack_grad[:, :in_rows],
-            pack_grad[:, in_rows:down],
-            jnp.concatenate(
-                [
-                    pack_grad[:, down + f * mid_rows : down + (f + 1) * mid_rows]
-                    for f in range(model_width // eff)
-                ],
-                axis=2,
-            ),
-        ]
-
         grad_out = out_grad.astype(F32)
         centre = jnp.sum(gate_weights * gate_grad, axis=-1, keepdims=True)
         logit_low = (gate_weights * (gate_grad - centre)).astype(B16)
@@ -936,24 +1041,36 @@
             logit_wide = jnp.pad(logit_low, ((0, 0), (0, EXTRA - EXPERTS)))
             first_blocks, second_blocks, normed_part = attention_backward(
                 jnp.stack([dp_index, core]).astype(jnp.int32),
-                attn_out_grad,
-                full_output,
+                after(attn_out_grad, y_low),
                 attended,
                 moe_in,
                 logit_wide,
                 moe_gain_grad[None, :],
                 (normed_all, query_rot, key_rot, value_all, totals),
                 x_all,
-                head_full,
+                dense_full,
                 bias,
                 cosine,
                 sine,
             )
-            first_sum = dense_blocks_sum(first_blocks, z, core)
-            second_sum = dense_blocks_sum(second_blocks, z, core)
-            normed_grad = grid_scatter_rows(normed_part.reshape(4, tok_rows, model_width))
+            y_pieces, late_got = after((y_pieces, late_got), normed_part)
+            y_pieces.append(cyclic(after(y_low[z_size // 2], *y_pieces), z_size, z_size // 2))
+            normed_first, normed_a, normed_b = row_halves(
+                normed_part.reshape(4, tok_rows, model_width)
+            )
+            second_first, second_a, second_b = row_halves(core_sum(second_blocks))
+            first_first, first_a, first_b = row_halves(core_sum(first_blocks))
+            normed_got = grid_scatter_first(*normed_first)
+            second_got = grid_scatter_first(*after(second_first, *normed_got))
+            first_got = grid_scatter_first(*after(first_first, *second_got))
+            second_sum = dense_finish(grid_scatter_second(second_got, second_a, second_b, *first_got), z, core)
+            first_sum = dense_finish(grid_scatter_second(first_got, first_a, first_b), z, core)
+            normed_grad = jnp.concatenate(
+                grid_scatter_second(normed_got, normed_a, normed_b, *first_got), axis=0
+            )
             first_value, first_pull = jax.vjp(lambda v: rms_norm(v, full_attn_gain), in_float)
             input_grad = residual_grad + first_pull(normed_grad)[0]
+            y_pieces = after(y_pieces, second_sum)
             at = wide + model_width // 2
             query_sum = first_sum[:, :wide]
             output_sum = jnp.concatenate(
@@ -1023,6 +1140,7 @@
             first_value, first_pull = jax.vjp(rms_norm, in_float, full_attn_gain)
             input_norm_grad, attn_gain_grad = first_pull(normed_grad)
             input_grad = residual_grad + input_norm_grad
+            y_pieces.append(cyclic(y_low[z_size // 2], z_size, z_size // 2))
             query_sum = dense_sum(wq_grad)
             key_sum = dense_sum(wk_grad)
             value_sum = dense_sum(wv_grad)
@@ -1041,6 +1159,27 @@
             router_sum = extra_sum[:, :EXPERTS]
             attn_gain_sum = extra_sum[:, EXPERTS]
             moe_gain_sum = extra_sum[:, EXPERTS + 1]
+        layer_output = (residual + column_sum(y_own, y_pieces)).astype(B16)
+        if small_grid:
+            parts = grid_sum(early, early_got) + grid_sum(late, late_got)
+            pack_grad = jnp.concatenate(parts, axis=0)
+        else:
+            pack_grad = lax.psum_scatter(
+                weight_grads[0][0].astype(F32), ("y", "x"), scatter_dimension=0, tiled=False
+            )
+        down = 2 * in_rows
+        expert_grads = [
+            pack_grad[:, :in_rows],
+            pack_grad[:, in_rows:down],
+            jnp.concatenate(
+                [
+                    pack_grad[:, down + f * mid_rows : down + (f + 1) * mid_rows]
+                    for f in range(model_width // eff)
+                ],
+                axis=2,
+            ),
+        ]
+
         return (
             layer_output,
             input_grad,
@@ -1088,7 +1227,7 @@
         P(every, None),
     )
     return jax.shard_map(
-        make_body(z_size, members == 4 and side == 2),
+        make_body(z_size, members == 4 and side == 2 and EXPERTS == 4 * groups),
         mesh=grid,
         in_specs=placed,
         out_specs=(

time: 648 us -> 543 us (0.84)
  waiting for transfers between devices: 312 us -> 169 us
  other arithmetic: 45.8 us -> 62.5 us
  local copies, waits for them, and re-layouts: 40.3 us -> 53 us
  starting transfers between devices: 83.7 us -> 91.2 us
    ppermute x24, waiting for transfers between devices: 150 us -> 29.2 us  [cyclic(): lax.ppermute(rows, 'z', [(i, (i + shift) % size) for i in range(size)])]
    ppermute x40 -> x34, waiting for transfers between devices: 162 us -> 139 us  [the longest x10 64 us: cross(): return (lax.ppermute(to_x, 'x', SWAP), lax.ppermute(to_y, 'y', SWAP))]
    ppermute x24, starting transfers between devices: 37.1 us -> 50.8 us  [cyclic(): lax.ppermute(rows, 'z', [(i, (i + shift) % size) for i in range(size)])]
    add x9 -> x7, other arithmetic: 5.41 us -> 14.6 us  [the longest x2 6.71 us: grid_sum(): totals.append(own.astype(F32) + direct.astype(F32) + last.astype(F32))]
    unnamed x104 -> x118, local copies, waits for them, and re-layouts: 15.2 us -> 21.5 us
    ppermute x40 -> x34, starting transfers between devices: 45.9 us -> 40 us  [the longest x10 11 us: cross(): return (lax.ppermute(to_x, 'x', SWAP), lax.ppermute(to_y, 'y', SWAP))]
  transfers between devices with their start and end apart: 74 -> 67, of which waited for: 32 -> 27; matrix products, arithmetic and copies ran while one was open for 12% -> 17% of each run, Pallas kernels for 18% -> 23%
where the time goes in v4:
time: 543 us; the launch traced here: 534 us
  waiting for transfers between devices  169 us (31%)
  Pallas kernels  153 us (28%)
  starting transfers between devices  91.2 us (17%)
  other arithmetic  62.5 us (12%)
  local copies, waits for them, and re-layouts  53 us (10%)
    ppermute x10, waiting for transfers between devices, cross(): return (lax.ppermute(to_x, 'x', SWAP), lax.ppermute(to_y, 'y', SWAP))  64 us
    ppermute x24, starting transfers between devices, cyclic(): lax.ppermute(rows, 'z', [(i, (i + shift) % size) for i in range(size)])  50.8 us
    pallas_call x2, Pallas kernels, experts(): pl.pallas_call(kernel, out_shape=out_shape, grid_spec=pltpu.PrefetchScala...  48.6 us
    pallas_call x1, Pallas kernels, attention_backward(): pl.pallas_call(kernel, out_shape=shapes, grid_spec=pltpu.PrefetchScalarGr...  33.9 us
    ppermute x6, waiting for transfers between devices, gather_near(): return [lax.ppermute(shard, 'x', SWAP), lax.ppermute(shard, 'y', SWAP)]  33.4 us
    ppermute x24, waiting for transfers between devices, cyclic(): lax.ppermute(rows, 'z', [(i, (i + shift) % size) for i in range(size)])  29.2 us
    ppermute x6, waiting for transfers between devices, grid_scatter_first(): return (lax.ppermute(first_a, 'x', SWAP), lax.ppermute(first_b, 'y', SWAP))  27.8 us
    pallas_call x1, Pallas kernels, attention_forward(): pl.pallas_call(kernel, grid=(GROUPS,), in_specs=[fixed(seq_len, width), p...  24.2 us
  transfers between devices with their start and end apart: 67, of which 27 were waited for; matrix products, arithmetic and copies ran while one was open for 17% of the time, Pallas kernels for 23%

profile of v4, /device:TPU:0, one launch (start us, length us, event | category | flops | bytes accessed | tf_op | source)
XLA Modules:
  0.0 534.2 jit_solution(2971585582565470968)
XLA Ops:
  4.1 2.4 concatenate.78.shard_ref
  8.1 3.0 collective-permute-start
  12.9 2.6 convert_reduce_fusion
  16.5 3.6 collective-permute-start.4
  21.2 19.6 %collective-permute-done = bf16[128,5248]{1,0:T(8,128)(2,1)S(1)} collective-permute-done((bf16[128,5248]{1,0:T(8,128)(2,1)}, bf16[128,5248]{1,0:T(8,128)(2,1)S(1)}, u32[]{:S(2)}, u32[]{:S(2)}) %collective-permute-start) | collective-permute-done | bytes 1343520 | tf_op jit(solution)/shard_map/ppermute | solution.py:59
  41.7 1.8 collective-permute-start.2
  46.3 1.6 copy-done.1
  48.0 1.7 slice_bitcast_fusion.4
  49.7 8.6 %collective-permute-done.2 = bf16[64,5248]{1,0:T(8,128)(2,1)} collective-permute-done((bf16[64,5248]{1,0:T(8,128)(2,1)}, bf16[64,5248]{1,0:T(8,128)(2,1)}, u32[]{:S(2)}, u32[]{:S(2)}) %collective-permute-start.2) | collective-permute-done | bytes 671776 | tf_op jit(solution)/shard_map/ppermute | solution.py:65
  61.6 1.7 pad_maximum_fusion.2.moved_ref
  67.6 3.1 fusion.13
  70.7 12.5 %collective-permute-done.7.refs_7_ = bf16[768,512]{1,0:T(8,128)(2,1)S(1)} collective-permute-done((bf16[768,512]{1,0:T(8,128)(2,1)S(1)}, bf16[768,512]{1,0:T(8,128)(2,1)S(1)}, u32[]{:S(2)}, u32[]{:S(2)}) %collective-permute-start.7) | collective-permute-done | bytes 786464 | tf_op jit(solution)/shard_map/ppermute | solution.py:59
  85.3 1.9 pad_maximum_fusion.5.packed_ref.code_ref
  91.6 6.7 %assemble.1.tail_ref.wo_ref.wq_ref.wk_ref.wv_ref = bf16[1024,3200]{1,0:T(8,128)(2,1)} custom-call(s32[7]{0:T(128)} %stack.151.places_ref, bf16[256,3200]{1,0:T(8,128)(2,1)} %copy-done.4, bf16[384,3200]{1,0:T(8,128)(2,1)} %pad_maximum_fusion.2.moved_ref, bf16[384,3200]{1,0:T(8,128)(2,1)} %collective-permute-done.9.other_ref), custom_call_target="tpu_custom_call" | custom-call | tf_op jit(solution)/shard_map/assemble/pallas_call | solution.py:149
  102.6 1.6 collective-permute-start.13
  109.9 24.2 %attention.1 = (bf16[1024,1024]{1,0:T(8,128)(2,1)}, bf16[256,1024]{1,0:T(8,128)(2,1)}, bf16[1024,512]{1,0:T(8,128)(2,1)}, bf16[1024,512]{1,0:T(8,128)(2,1)}, bf1...) custom-call(bf16[1024,1024]{1,0:T(8,128)(2,1)} %slice_dynamic-update, ...), custom_call_target="tpu_custom_call" | custom-call | tf_op jit(solution)/shard_map/attention/pallas_call | solution.py:556
  136.3 1.6 pad_maximum_fusion.16
  139.1 3.7 collective-permute-start.15
  144.2 4.5 dispatch.4.refs_2_
  148.8 16.7 %collective-permute-done.18.refs_14_.refs_7_ = bf16[1152,512]{1,0:T(8,128)(2,1)S(1)} collective-permute-done((bf16[1152,512]{1,0:T(8,128)(2,1)}, bf16[1152,512]{1,0:T(8,128)(2,1)S(1)}, u32[]{:S(2)}, u32[]{:S(2)}) %collective-permute-start.18) | collective-permute-done | bytes 1179680 | tf_op jit(solution)/shard_map/ppermute | solution.py:74
  165.7 4.9 dispatch.5.refs_3_
  170.7 16.2 %collective-permute-done.16 = bf16[256,1024]{1,0:T(8,128)(2,1)} collective-permute-done((bf16[256,1024]{1,0:T(8,128)(2,1)}, bf16[256,1024]{1,0:T(8,128)(2,1)}, u32[]{:S(2)}, u32[]{:S(2)}) %collective-permute-start.16) | collective-permute-done | bytes 524320 | tf_op jit(solution)/shard_map/ppermute | solution.py:51
  186.9 1.9 pad_maximum_fusion.12.rest_0_
  193.0 24.5 %collective-permute-done.20.refs_10_.refs_11_ = bf16[1152,512]{1,0:T(8,128)(2,1)S(1)} collective-permute-done((bf16[1152,512]{1,0:T(8,128)(2,1)S(1)}, bf16[1152,512]{1,0:T(8,128)(2,1)S(1)}, u32[]{:S(2)}, u32[]{:S(2)}) %collective-permute-start.20) | collective-permute-done | bytes 1179680 | tf_op jit(solution)/shard_map/ppermute | solution.py:74
  225.3 4.9 dispatch.6
  230.2 4.9 dispatch.7
  235.1 23.4 %experts.2 = (bf16[8,160,1024]{2,1,0:T(8,128)(2,1)}, bf16[8,160,1152]{2,1,0:T(8,128)(2,1)}, bf16[1,1,768,512]{3,2,1,0:T(8,128)(2,1)}, bf16[1,1,768,512]{3,2,1,0:...) custom-call(s32[5]{0:T(128)} %pad_add_fusion.order_ref, ...), custom_call_target="tpu_custom_call" | custom-call | tf_op jit(solution)/shard_map/experts/pallas_call | solution.py:445
  259.7 25.2 %experts.3 = (bf16[8,160,1024]{2,1,0:T(8,128)(2,1)}, bf16[8,160,1152]{2,1,0:T(8,128)(2,1)}, bf16[1,1,768,512]{3,2,1,0:T(8,128)(2,1)}, bf16[1,1,768,512]{3,2,1,0:...) custom-call(s32[5]{0:T(128)} %pad_add_fusion.order_ref, ...), custom_call_target="tpu_custom_call" | custom-call | tf_op jit(solution)/shard_map/experts/pallas_call | solution.py:445
  286.0 5.2 combine.5
  293.6 1.7 pad_maximum_fusion.4
  297.0 1.7 pad_maximum_fusion.3
  301.1 5.1 combine.4
  306.2 5.1 convert_add_fusion
  313.5 1.9 collective-permute-start.29
  315.4 2.9 collective-permute-start.30
  320.0 5.0 combine.6
  325.0 4.8 combine.7
  329.8 19.4 %collective-permute-done.35 = bf16[3,1,768,512]{3,2,1,0:T(8,128)(2,1)} collective-permute-done((bf16[3,1,768,512]{3,2,1,0:T(8,128)(2,1)}, bf16[3,1,768,512]{3,2,1,0:T(8,128)(2,1)}, u32[]{:S(2)}, u32[]{:S(2)}) %collective-permute-start.35) | collective-permute-done | bytes 2359328 | tf_op jit(solution)/shard_map/ppermute | solution.py:74
  349.2 3.2 collective-permute-done.34
  352.4 4.1 add_bitcast_fusion.3
  356.5 2.2 fusion.3
  368.4 2.0 multiply_reduce_fusion
  372.5 3.2 fusion.43
  376.8 10.5 %collective-permute-start.32 = (bf16[256,1024]{1,0:T(8,128)(2,1)}, bf16[256,1024]{1,0:T(8,128)(2,1)}, u32[]{:S(2)}, u32[]{:S(2)}) collective-permute-start(bf16[256,1024]{1,0:T(8,128)(2,1)} %get-tuple-element.271), channel_id=1, source_target_pairs={{0,8},{8,16},{16,24},{24,0},{1,9},{9,17},{17,25},{25,1},{2,10},{10... | collective-permute-start | bytes 1572872 | tf_op jit(solution)/shard_map/ppermute | solution.py:51
  387.3 1.6 collective-permute-start.33
  388.9 33.9 %attention_grad.1 = (bf16[2,4,128,1664]{3,2,1,0:T(8,128)(2,1)}, bf16[2,4,128,1536]{3,2,1,0:T(8,128)(2,1)}, bf16[1024,1024]{1,0:T(8,128)(2,1)}) custom-call(s32[2]{0:T(128)} %pad_add_fusion.1.here_ref, bf16[256,1024]{1,0:T(8,128)(2,1)} %get-tuple-element.158.og_ref, bf16[1024,3200]{1,0:T(8,128)(2,1)} %assemble.1.tail_ref.wo_ref.wq_ref.wk_ref.wv_ref, ...), custom_call_target="tpu_custom_call" | custom-call | tf_op jit(solution)/shard_map/attention_grad/pallas_call | solution.py:712
  427.4 10.4 %collective-permute-done.41 = bf16[2,128,1024]{2,1,0:T(8,128)(2,1)S(1)} collective-permute-done((bf16[2,128,1024]{2,1,0:T(8,128)(2,1)S(1)}, bf16[2,128,1024]{2,1,0:T(8,128)(2,1)S(1)}, u32[]{:S(2)}, u32[]{:S(2)}) %collective-permute-start.41) | collective-permute-done | bytes 524320 | tf_op jit(solution)/shard_map/ppermute | solution.py:91
  438.9 2.6 add_bitcast_fusion.1
  447.1 2.8 fusion.47
  452.5 7.5 %collective-permute-done.42 = bf16[2,64,1536]{2,1,0:T(8,128)(2,1)S(1)} collective-permute-done((bf16[2,64,1536]{2,1,0:T(8,128)(2,1)S(1)}, bf16[2,64,1536]{2,1,0:T(8,128)(2,1)S(1)}, u32[]{:S(2)}, u32[]{:S(2)}) %collective-permute-start.42) | collective-permute-done | bytes 393248 | tf_op jit(solution)/shard_map/ppermute | solution.py:91
  462.6 7.3 %collective-permute-done.47 = bf16[2,64,1664]{2,1,0:T(8,128)(2,1)S(1)} collective-permute-done((bf16[2,64,1664]{2,1,0:T(8,128)(2,1)S(1)}, bf16[2,64,1664]{2,1,0:T(8,128)(2,1)S(1)}, u32[]{:S(2)}, u32[]{:S(2)}) %collective-permute-start.47) | collective-permute-done | bytes 426016 | tf_op jit(solution)/shard_map/ppermute | solution.py:91
  471.1 1.7 collective-permute-done.48
  472.9 2.7 collective-permute-done.43
  476.7 1.7 collective-permute-done.45
  479.3 1.7 collective-permute-start.50
  481.0 1.8 collective-permute-start.51
  488.0 4.5 collective-permute-start.52
  492.5 2.4 collective-permute-start.53
  496.4 3.2 collective-permute-start.61
  500.2 2.0 collective-permute-start.62
  503.1 4.3 collective-permute-done.61
  507.5 3.6 collective-permute-start.63
  513.9 3.7 collective-permute-done.64
  525.3 2.9 fusion.10
  (345 shorter events, 121.9 us)
Async XLA Ops:
  8.1 32.7 %collective-permute-start = (bf16[128,5248]{1,0:T(8,128)(2,1)}, bf16[128,5248]{1,0:T(8,128)(2,1)S(1)}, u32[]{:S(2)}, u32[]{:S(2)}) collective-permute-start(bf16[128,5248]{1,0:T(8,128)(2,1)} %pad_maximum_fusion.15), channel_id=1, source_target_pairs={{0,1},{1,0},{2,3},{3,2},{4,5},{5,4},{6,7},{7,6},{8,9},{9,8},{10,11... | collective-permute-start | bytes 4030472 | tf_op jit(solution)/shard_map/ppermute | solution.py:59
  11.1 32.4 %collective-permute-start.1 = (bf16[128,5248]{1,0:T(8,128)(2,1)}, bf16[128,5248]{1,0:T(8,128)(2,1)S(1)}, u32[]{:S(2)}, u32[]{:S(2)}) collective-permute-start(bf16[128,5248]{1,0:T(8,128)(2,1)} %pad_maximum_fusion.15), channel_id=1, source_target_pairs={{0,2},{2,0},{1,3},{3,1},{4,6},{6,4},{5,7},{7,5},{8,10},{10,8},{9,1... | collective-permute-start | bytes 4030472 | tf_op jit(solution)/shard_map/ppermute | solution.py:59
  16.5 46.7 %collective-permute-start.4 = (bf16[272,1024]{1,0:T(8,128)(2,1)}, bf16[272,1024]{1,0:T(8,128)(2,1)}, u32[]{:S(2)}, u32[]{:S(2)}) collective-permute-start(bf16[272,1024]{1,0:T(8,128)(2,1)} %maximum_maximum_fusion), channel_id=1, source_target_pairs={{0,24},{8,0},{16,8},{24,16},{1,25},{9,1},{17,9},{25,17},{2,26},{10... | collective-permute-start | bytes 1671176 | tf_op jit(solution)/shard_map/ppermute | solution.py:51
  20.1 50.5 %collective-permute-start.5 = (bf16[272,1024]{1,0:T(8,128)(2,1)}, bf16[272,1024]{1,0:T(8,128)(2,1)}, u32[]{:S(2)}, u32[]{:S(2)}) collective-permute-start(bf16[272,1024]{1,0:T(8,128)(2,1)} %maximum_maximum_fusion), channel_id=1, source_target_pairs={{0,16},{8,24},{16,0},{24,8},{1,17},{9,25},{17,1},{25,9},{2,18},{10... | collective-permute-start | bytes 1671176 | tf_op jit(solution)/shard_map/ppermute | solution.py:51
  20.1 50.5 %collective-permute-start.6 = (bf16[272,1024]{1,0:T(8,128)(2,1)}, bf16[272,1024]{1,0:T(8,128)(2,1)}, u32[]{:S(2)}, u32[]{:S(2)}) collective-permute-start(bf16[272,1024]{1,0:T(8,128)(2,1)} %maximum_maximum_fusion), channel_id=1, source_target_pairs={{0,8},{8,16},{16,24},{24,0},{1,9},{9,17},{17,25},{25,1},{2,10},{10... | collective-permute-start | bytes 1671176 | tf_op jit(solution)/shard_map/ppermute | solution.py:51
  41.7 16.6 %collective-permute-start.2 = (bf16[64,5248]{1,0:T(8,128)(2,1)}, bf16[64,5248]{1,0:T(8,128)(2,1)}, u32[]{:S(2)}, u32[]{:S(2)}) collective-permute-start(bf16[64,5248]{1,0:T(8,128)(2,1)} %slice.527), channel_id=1, source_target_pairs={{0,2},{2,0},{1,3},{3,1},{4,6},{6,4},{5,7},{7,5},{8,10},{10,8},{9,1... | collective-permute-start | bytes 2015240 | tf_op jit(solution)/shard_map/ppermute | solution.py:65
  44.5 16.0 %collective-permute-start.3 = (bf16[64,5248]{1,0:T(8,128)(2,1)}, bf16[64,5248]{1,0:T(8,128)(2,1)}, u32[]{:S(2)}, u32[]{:S(2)}) collective-permute-start(bf16[64,5248]{1,0:T(8,128)(2,1)} %slice.529), channel_id=1, source_target_pairs={{0,1},{1,0},{2,3},{3,2},{4,5},{5,4},{6,7},{7,6},{8,9},{9,8},{10,11... | collective-permute-start | bytes 2015240 | tf_op jit(solution)/shard_map/ppermute | solution.py:65
  63.2 28.4 %collective-permute-start.9 = (bf16[384,3200]{1,0:T(8,128)(2,1)}, bf16[384,3200]{1,0:T(8,128)(2,1)}, u32[]{:S(2)}, u32[]{:S(2)}) collective-permute-start(bf16[384,3200]{1,0:T(8,128)(2,1)} %pad_maximum_fusion.2.moved_ref), channel_id=1, source_target_pairs={{0,4},{4,0},{1,5},{5,1},{2,6},{6,2},{3,7},{7,3},{8,12},{12,8},{9,1... | collective-permute-start | bytes 7372808 | tf_op jit(solution)/shard_map/ppermute | solution.py:47
  63.3 19.9 %collective-permute-start.7 = (bf16[768,512]{1,0:T(8,128)(2,1)S(1)}, bf16[768,512]{1,0:T(8,128)(2,1)S(1)}, u32[]{:S(2)}, u32[]{:S(2)}) collective-permute-start(bf16[768,512]{1,0:T(8,128)(2,1)S(1)} %copy-done.37), channel_id=1, source_target_pairs={{0,1},{1,0},{2,3},{3,2},{4,5},{5,4},{6,7},{7,6},{8,9},{9,8},{10,11... | collective-permute-start | bytes 2359304 | tf_op jit(solution)/shard_map/ppermute | solution.py:59
  64.8 19.6 %collective-permute-start.8 = (bf16[768,512]{1,0:T(8,128)(2,1)S(1)}, bf16[768,512]{1,0:T(8,128)(2,1)S(1)}, u32[]{:S(2)}, u32[]{:S(2)}) collective-permute-start(bf16[768,512]{1,0:T(8,128)(2,1)S(1)} %copy-done.37), channel_id=1, source_target_pairs={{0,2},{2,0},{1,3},{3,1},{4,6},{6,4},{5,7},{7,5},{8,10},{10,8},{9,1... | collective-permute-start | bytes 2359304 | tf_op jit(solution)/shard_map/ppermute | solution.py:59
  87.3 46.8 %collective-permute-start.10 = (bf16[4,272,1024]{2,1,0:T(8,128)(2,1)S(1)}, bf16[4,272,1024]{2,1,0:T(8,128)(2,1)}, u32[]{:S(2)}, u32[]{:S(2)}) collective-permute-start(bf16[4,272,1024]{2,1,0:T(8,128)(2,1)S(1)} %pad_maximum_fusion.5.packed_ref.code_ref), channel_id=1, source_target_pairs={{0,4},{4,0},{1,5},{5,1},{2,6},{6,2},{3,7},{7,3},{8,12},{12,8},{9,1... | collective-permute-start | bytes 6684680 | tf_op jit(solution)/shard_map/ppermute | solution.py:47
  98.3 35.7 %collective-permute-start.11 = (bf16[768,512]{1,0:T(8,128)(2,1)}, bf16[768,512]{1,0:T(8,128)(2,1)}, u32[]{:S(2)}, u32[]{:S(2)}) collective-permute-start(bf16[768,512]{1,0:T(8,128)(2,1)} %get-tuple-element.110), channel_id=1, source_target_pairs={{0,1},{1,0},{2,3},{3,2},{4,5},{5,4},{6,7},{7,6},{8,9},{9,8},{10,11... | collective-permute-start | bytes 2359304 | tf_op jit(solution)/shard_map/ppermute | solution.py:59
  98.9 35.2 %collective-permute-start.12 = (bf16[768,512]{1,0:T(8,128)(2,1)}, bf16[768,512]{1,0:T(8,128)(2,1)}, u32[]{:S(2)}, u32[]{:S(2)}) collective-permute-start(bf16[768,512]{1,0:T(8,128)(2,1)} %get-tuple-element.110), channel_id=1, source_target_pairs={{0,2},{2,0},{1,3},{3,1},{4,6},{6,4},{5,7},{7,5},{8,10},{10,8},{9,1... | collective-permute-start | bytes 2359304 | tf_op jit(solution)/shard_map/ppermute | solution.py:59
  102.6 31.4 %collective-permute-start.13 = (bf16[384,512]{1,0:T(8,128)(2,1)S(1)}, bf16[384,512]{1,0:T(8,128)(2,1)S(1)}, u32[]{:S(2)}, u32[]{:S(2)}) collective-permute-start(bf16[384,512]{1,0:T(8,128)(2,1)S(1)} %slice.431), channel_id=1, source_target_pairs={{0,2},{2,0},{1,3},{3,1},{4,6},{6,4},{5,7},{7,5},{8,10},{10,8},{9,1... | collective-permute-start | bytes 1179656 | tf_op jit(solution)/shard_map/ppermute | solution.py:65
  105.2 28.9 %collective-permute-start.14 = (bf16[384,512]{1,0:T(8,128)(2,1)S(1)}, bf16[384,512]{1,0:T(8,128)(2,1)}, u32[]{:S(2)}, u32[]{:S(2)}) collective-permute-start(bf16[384,512]{1,0:T(8,128)(2,1)S(1)} %slice.432), channel_id=1, source_target_pairs={{0,1},{1,0},{2,3},{3,2},{4,5},{5,4},{6,7},{7,6},{8,9},{9,8},{10,11... | collective-permute-start | bytes 1179656 | tf_op jit(solution)/shard_map/ppermute | solution.py:65
  138.0 27.4 %collective-permute-start.18 = (bf16[1152,512]{1,0:T(8,128)(2,1)}, bf16[1152,512]{1,0:T(8,128)(2,1)S(1)}, u32[]{:S(2)}, u32[]{:S(2)}) collective-permute-start(bf16[1152,512]{1,0:T(8,128)(2,1)} %get-tuple-element.303), channel_id=1, source_target_pairs={{0,1},{1,0},{2,3},{3,2},{4,5},{5,4},{6,7},{7,6},{8,9},{9,8},{10,11... | collective-permute-start | bytes 3538952 | tf_op jit(solution)/shard_map/ppermute | solution.py:74
  138.6 27.2 %collective-permute-start.19 = (bf16[1152,512]{1,0:T(8,128)(2,1)}, bf16[1152,512]{1,0:T(8,128)(2,1)S(1)}, u32[]{:S(2)}, u32[]{:S(2)}) collective-permute-start(bf16[1152,512]{1,0:T(8,128)(2,1)} %get-tuple-element.302), channel_id=1, source_target_pairs={{0,2},{2,0},{1,3},{3,1},{4,6},{6,4},{5,7},{7,5},{8,10},{10,8},{9,1... | collective-permute-start | bytes 3538952 | tf_op jit(solution)/shard_map/ppermute | solution.py:74
  139.1 31.6 %collective-permute-start.15 = (bf16[256,1024]{1,0:T(8,128)(2,1)}, bf16[256,1024]{1,0:T(8,128)(2,1)}, u32[]{:S(2)}, u32[]{:S(2)}) collective-permute-start(bf16[256,1024]{1,0:T(8,128)(2,1)} %get-tuple-element.118.moe_ref), channel_id=1, source_target_pairs={{0,24},{8,0},{16,8},{24,16},{1,25},{9,1},{17,9},{25,17},{2,26},{10... | collective-permute-start | bytes 1572872 | tf_op jit(solution)/shard_map/ppermute | solution.py:51
  142.8 44.1 %collective-permute-start.16 = (bf16[256,1024]{1,0:T(8,128)(2,1)}, bf16[256,1024]{1,0:T(8,128)(2,1)}, u32[]{:S(2)}, u32[]{:S(2)}) collective-permute-start(bf16[256,1024]{1,0:T(8,128)(2,1)} %get-tuple-element.118.moe_ref), channel_id=1, source_target_pairs={{0,16},{8,24},{16,0},{24,8},{1,17},{9,25},{17,1},{25,9},{2,18},{10... | collective-permute-start | bytes 1572872 | tf_op jit(solution)/shard_map/ppermute | solution.py:51
  142.8 44.1 %collective-permute-start.17 = (bf16[256,1024]{1,0:T(8,128)(2,1)}, bf16[256,1024]{1,0:T(8,128)(2,1)}, u32[]{:S(2)}, u32[]{:S(2)}) collective-permute-start(bf16[256,1024]{1,0:T(8,128)(2,1)} %get-tuple-element.118.moe_ref), channel_id=1, source_target_pairs={{0,8},{8,16},{16,24},{24,0},{1,9},{9,17},{17,25},{25,1},{2,10},{10... | collective-permute-start | bytes 1572872 | tf_op jit(solution)/shard_map/ppermute | solution.py:51
  188.8 41.4 %collective-permute-start.22 = (bf16[4,256,1024]{2,1,0:T(8,128)(2,1)S(1)}, bf16[4,256,1024]{2,1,0:T(8,128)(2,1)}, u32[]{:S(2)}, u32[]{:S(2)}) collective-permute-start(bf16[4,256,1024]{2,1,0:T(8,128)(2,1)S(1)} %pad_maximum_fusion.12.rest_0_), channel_id=1, source_target_pairs={{0,4},{4,0},{1,5},{5,1},{2,6},{6,2},{3,7},{7,3},{8,12},{12,8},{9,1... | collective-permute-start | bytes 6291464 | tf_op jit(solution)/shard_map/ppermute | solution.py:47
  190.1 27.4 %collective-permute-start.20 = (bf16[1152,512]{1,0:T(8,128)(2,1)S(1)}, bf16[1152,512]{1,0:T(8,128)(2,1)S(1)}, u32[]{:S(2)}, u32[]{:S(2)}) collective-permute-start(bf16[1152,512]{1,0:T(8,128)(2,1)S(1)} %get-tuple-element.301), channel_id=1, source_target_pairs={{0,1},{1,0},{2,3},{3,2},{4,5},{5,4},{6,7},{7,6},{8,9},{9,8},{10,11... | collective-permute-start | bytes 3538952 | tf_op jit(solution)/shard_map/ppermute | solution.py:74
  191.5 28.3 %collective-permute-start.21 = (bf16[1152,512]{1,0:T(8,128)(2,1)S(1)}, bf16[1152,512]{1,0:T(8,128)(2,1)S(1)}, u32[]{:S(2)}, u32[]{:S(2)}) collective-permute-start(bf16[1152,512]{1,0:T(8,128)(2,1)S(1)} %get-tuple-element.300), channel_id=1, source_target_pairs={{0,2},{2,0},{1,3},{3,1},{4,6},{6,4},{5,7},{7,5},{8,10},{10,8},{9,1... | collective-permute-start | bytes 3538952 | tf_op jit(solution)/shard_map/ppermute | solution.py:74
  218.3 16.8 %collective-permute-start.23 = (bf16[384,512]{1,0:T(8,128)(2,1)}, bf16[384,512]{1,0:T(8,128)(2,1)}, u32[]{:S(2)}, u32[]{:S(2)}) collective-permute-start(bf16[384,512]{1,0:T(8,128)(2,1)} %slice.546), channel_id=1, source_target_pairs={{0,2},{2,0},{1,3},{3,1},{4,6},{6,4},{5,7},{7,5},{8,10},{10,8},{9,1... | collective-permute-start | bytes 1179656 | tf_op jit(solution)/shard_map/ppermute | solution.py:65
  221.7 13.4 %collective-permute-start.24 = (bf16[384,512]{1,0:T(8,128)(2,1)}, bf16[384,512]{1,0:T(8,128)(2,1)}, u32[]{:S(2)}, u32[]{:S(2)}) collective-permute-start(bf16[384,512]{1,0:T(8,128)(2,1)} %slice.547), channel_id=1, source_target_pairs={{0,1},{1,0},{2,3},{3,2},{4,5},{5,4},{6,7},{7,6},{8,9},{9,8},{10,11... | collective-permute-start | bytes 1179656 | tf_op jit(solution)/shard_map/ppermute | solution.py:65
  258.6 26.3 %collective-permute-start.25 = (bf16[1,1,768,512]{3,2,1,0:T(8,128)(2,1)}, bf16[1,1,768,512]{3,2,1,0:T(8,128)(2,1)S(1)}, u32[]{:S(2)}, u32[]{:S(2)}) collective-permute-start(bf16[1,1,768,512]{3,2,1,0:T(8,128)(2,1)} %get-tuple-element.136), channel_id=1, source_target_pairs={{0,1},{1,0},{2,3},{3,2},{4,5},{5,4},{6,7},{7,6},{8,9},{9,8},{10,11... | collective-permute-start | bytes 2359304 | tf_op jit(solution)/shard_map/ppermute | solution.py:74
  259.2 25.7 %collective-permute-start.26 = (bf16[1,1,768,512]{3,2,1,0:T(8,128)(2,1)}, bf16[1,1,768,512]{3,2,1,0:T(8,128)(2,1)S(1)}, u32[]{:S(2)}, u32[]{:S(2)}) collective-permute-start(bf16[1,1,768,512]{3,2,1,0:T(8,128)(2,1)} %get-tuple-element.137), channel_id=1, source_target_pairs={{0,2},{2,0},{1,3},{3,1},{4,6},{6,4},{5,7},{7,5},{8,10},{10,8},{9,1... | collective-permute-start | bytes 2359304 | tf_op jit(solution)/shard_map/ppermute | solution.py:74
  291.2 15.0 %collective-permute-start.27 = (bf16[4,256,1152]{2,1,0:T(8,128)(2,1)}, bf16[4,256,1152]{2,1,0:T(8,128)(2,1)}, u32[]{:S(2)}, u32[]{:S(2)}) collective-permute-start(bf16[4,256,1152]{2,1,0:T(8,128)(2,1)} %combine.5), channel_id=1, source_target_pairs={{0,4},{4,0},{1,5},{5,1},{2,6},{6,2},{3,7},{7,3},{8,12},{12,8},{9,1... | collective-permute-start | bytes 7077896 | tf_op jit(solution)/shard_map/ppermute | solution.py:47
  295.2 54.0 %collective-permute-start.35 = (bf16[3,1,768,512]{3,2,1,0:T(8,128)(2,1)}, bf16[3,1,768,512]{3,2,1,0:T(8,128)(2,1)}, u32[]{:S(2)}, u32[]{:S(2)}) collective-permute-start(bf16[3,1,768,512]{3,2,1,0:T(8,128)(2,1)} %pad_maximum_fusion.4), channel_id=1, source_target_pairs={{0,2},{2,0},{1,3},{3,1},{4,6},{6,4},{5,7},{7,5},{8,10},{10,8},{9,1... | collective-permute-start | bytes 7077896 | tf_op jit(solution)/shard_map/ppermute | solution.py:74
  298.7 53.7 %collective-permute-start.34 = (bf16[3,1,768,512]{3,2,1,0:T(8,128)(2,1)}, bf16[3,1,768,512]{3,2,1,0:T(8,128)(2,1)}, u32[]{:S(2)}, u32[]{:S(2)}) collective-permute-start(bf16[3,1,768,512]{3,2,1,0:T(8,128)(2,1)} %pad_maximum_fusion.3), channel_id=1, source_target_pairs={{0,1},{1,0},{2,3},{3,2},{4,5},{5,4},{6,7},{7,6},{8,9},{9,8},{10,11... | collective-permute-start | bytes 7077896 | tf_op jit(solution)/shard_map/ppermute | solution.py:74
  312.7 43.9 %collective-permute-start.28 = (bf16[256,1152]{1,0:T(8,128)(2,1)}, bf16[256,1152]{1,0:T(8,128)(2,1)}, u32[]{:S(2)}, u32[]{:S(2)}) collective-permute-start(bf16[256,1152]{1,0:T(8,128)(2,1)} %get-tuple-element.260), channel_id=1, source_target_pairs={{0,8},{8,16},{16,24},{24,0},{1,9},{9,17},{17,25},{25,1},{2,10},{10... | collective-permute-start | bytes 1769480 | tf_op jit(solution)/shard_map/ppermute | solution.py:51
  313.5 43.0 %collective-permute-start.29 = (bf16[256,1152]{1,0:T(8,128)(2,1)}, bf16[256,1152]{1,0:T(8,128)(2,1)}, u32[]{:S(2)}, u32[]{:S(2)}) collective-permute-start(bf16[256,1152]{1,0:T(8,128)(2,1)} %get-tuple-element.259), channel_id=1, source_target_pairs={{0,16},{8,24},{16,0},{24,8},{1,17},{9,25},{17,1},{25,9},{2,18},{10... | collective-permute-start | bytes 1769480 | tf_op jit(solution)/shard_map/ppermute | solution.py:51
  315.4 41.1 %collective-permute-start.30 = (bf16[256,1152]{1,0:T(8,128)(2,1)}, bf16[256,1152]{1,0:T(8,128)(2,1)}, u32[]{:S(2)}, u32[]{:S(2)}) collective-permute-start(bf16[256,1152]{1,0:T(8,128)(2,1)} %get-tuple-element.258), channel_id=1, source_target_pairs={{0,24},{8,0},{16,8},{24,16},{1,25},{9,1},{17,9},{25,17},{2,26},{10... | collective-permute-start | bytes 1769480 | tf_op jit(solution)/shard_map/ppermute | solution.py:51
  359.0 12.9 %collective-permute-start.31 = (bf16[4,256,1024]{2,1,0:T(8,128)(2,1)S(1)}, bf16[4,256,1024]{2,1,0:T(8,128)(2,1)S(1)}, u32[]{:S(2)}, u32[]{:S(2)}) collective-permute-start(bf16[4,256,1024]{2,1,0:T(8,128)(2,1)S(1)} %copy-done.24), channel_id=1, source_target_pairs={{0,4},{4,0},{1,5},{5,1},{2,6},{6,2},{3,7},{7,3},{8,12},{12,8},{9,1... | collective-permute-start | bytes 6291464 | tf_op jit(solution)/shard_map/ppermute | solution.py:47
  362.8 62.3 %collective-permute-start.37 = (bf16[2,1,768,512]{3,2,1,0:T(8,128)(2,1)}, bf16[2,1,768,512]{3,2,1,0:T(8,128)(2,1)}, u32[]{:S(2)}, u32[]{:S(2)}) collective-permute-start(bf16[2,1,768,512]{3,2,1,0:T(8,128)(2,1)} %pad_maximum_fusion.14), channel_id=1, source_target_pairs={{0,2},{2,0},{1,3},{3,1},{4,6},{6,4},{5,7},{7,5},{8,10},{10,8},{9,1... | collective-permute-start | bytes 4718600 | tf_op jit(solution)/shard_map/ppermute | solution.py:74
  366.9 59.7 %collective-permute-start.36 = (bf16[2,1,768,512]{3,2,1,0:T(8,128)(2,1)}, bf16[2,1,768,512]{3,2,1,0:T(8,128)(2,1)}, u32[]{:S(2)}, u32[]{:S(2)}) collective-permute-start(bf16[2,1,768,512]{3,2,1,0:T(8,128)(2,1)} %pad_maximum_fusion.13), channel_id=1, source_target_pairs={{0,1},{1,0},{2,3},{3,2},{4,5},{5,4},{6,7},{7,6},{8,9},{9,8},{10,11... | collective-permute-start | bytes 4718600 | tf_op jit(solution)/shard_map/ppermute | solution.py:74
  376.8 50.3 %collective-permute-start.32 = (bf16[256,1024]{1,0:T(8,128)(2,1)}, bf16[256,1024]{1,0:T(8,128)(2,1)}, u32[]{:S(2)}, u32[]{:S(2)}) collective-permute-start(bf16[256,1024]{1,0:T(8,128)(2,1)} %get-tuple-element.271), channel_id=1, source_target_pairs={{0,8},{8,16},{16,24},{24,0},{1,9},{9,17},{17,25},{25,1},{2,10},{10... | collective-permute-start | bytes 1572872 | tf_op jit(solution)/shard_map/ppermute | solution.py:51
  387.3 40.1 %collective-permute-start.33 = (bf16[256,1024]{1,0:T(8,128)(2,1)S(1)}, bf16[256,1024]{1,0:T(8,128)(2,1)}, u32[]{:S(2)}, u32[]{:S(2)}) collective-permute-start(bf16[256,1024]{1,0:T(8,128)(2,1)S(1)} %get-tuple-element.270), channel_id=1, source_target_pairs={{0,24},{8,0},{16,8},{24,16},{1,25},{9,1},{17,9},{25,17},{2,26},{10... | collective-permute-start | bytes 1572872 | tf_op jit(solution)/shard_map/ppermute | solution.py:51
  424.3 13.5 %collective-permute-start.41 = (bf16[2,128,1024]{2,1,0:T(8,128)(2,1)S(1)}, bf16[2,128,1024]{2,1,0:T(8,128)(2,1)S(1)}, u32[]{:S(2)}, u32[]{:S(2)}) collective-permute-start(bf16[2,128,1024]{2,1,0:T(8,128)(2,1)S(1)} %pad_maximum_fusion.24), channel_id=1, source_target_pairs={{0,2},{2,0},{1,3},{3,1},{4,6},{6,4},{5,7},{7,5},{8,10},{10,8},{9,1... | collective-permute-start | bytes 1572872 | tf_op jit(solution)/shard_map/ppermute | solution.py:91
  425.1 13.5 %collective-permute-start.40 = (bf16[2,128,1024]{2,1,0:T(8,128)(2,1)S(1)}, bf16[2,128,1024]{2,1,0:T(8,128)(2,1)S(1)}, u32[]{:S(2)}, u32[]{:S(2)}) collective-permute-start(bf16[2,128,1024]{2,1,0:T(8,128)(2,1)S(1)} %pad_maximum_fusion.23), channel_id=1, source_target_pairs={{0,1},{1,0},{2,3},{3,2},{4,5},{5,4},{6,7},{7,6},{8,9},{9,8},{10,11... | collective-permute-start | bytes 1572872 | tf_op jit(solution)/shard_map/ppermute | solution.py:91
  426.6 23.2 %collective-permute-start.39 = (bf16[4,128,1536]{2,1,0:T(8,128)(2,1)S(1)}, bf16[4,128,1536]{2,1,0:T(8,128)(2,1)S(1)}, u32[]{:S(2)}, u32[]{:S(2)}) collective-permute-start(bf16[4,128,1536]{2,1,0:T(8,128)(2,1)S(1)} %slice_bitcast_fusion.1), channel_id=1, source_target_pairs={{0,4},{4,0},{1,5},{5,1},{2,6},{6,2},{3,7},{7,3},{8,12},{12,8},{9,1... | collective-permute-start | bytes 4718600 | tf_op jit(solution)/shard_map/ppermute | solution.py:47
  427.1 24.0 %collective-permute-start.46 = (bf16[4,128,1664]{2,1,0:T(8,128)(2,1)S(1)}, bf16[4,128,1664]{2,1,0:T(8,128)(2,1)S(1)}, u32[]{:S(2)}, u32[]{:S(2)}) collective-permute-start(bf16[4,128,1664]{2,1,0:T(8,128)(2,1)S(1)} %slice_bitcast_fusion), channel_id=1, source_target_pairs={{0,4},{4,0},{1,5},{5,1},{2,6},{6,2},{3,7},{7,3},{8,12},{12,8},{9,1... | collective-permute-start | bytes 5111816 | tf_op jit(solution)/shard_map/ppermute | solution.py:47
  443.9 35.3 %collective-permute-start.56 = (bf16[128,1024]{1,0:T(8,128)(2,1)S(1)}, bf16[128,1024]{1,0:T(8,128)(2,1)S(1)}, u32[]{:S(2)}, u32[]{:S(2)}) collective-permute-start(bf16[128,1024]{1,0:T(8,128)(2,1)S(1)} %get-tuple-element.264), channel_id=1, source_target_pairs={{0,2},{2,0},{1,3},{3,1},{4,6},{6,4},{5,7},{7,5},{8,10},{10,8},{9,1... | collective-permute-start | bytes 786440 | tf_op jit(solution)/shard_map/ppermute | solution.py:98
  445.1 35.9 %collective-permute-start.57 = (bf16[128,1024]{1,0:T(8,128)(2,1)S(1)}, bf16[128,1024]{1,0:T(8,128)(2,1)S(1)}, u32[]{:S(2)}, u32[]{:S(2)}) collective-permute-start(bf16[128,1024]{1,0:T(8,128)(2,1)S(1)} %get-tuple-element.263), channel_id=1, source_target_pairs={{0,1},{1,0},{2,3},{3,2},{4,5},{5,4},{6,7},{7,6},{8,9},{9,8},{10,11... | collective-permute-start | bytes 786440 | tf_op jit(solution)/shard_map/ppermute | solution.py:99
  446.5 78.8 %collective-permute-start.38 = (bf16[256,1024]{1,0:T(8,128)(2,1)}, bf16[256,1024]{1,0:T(8,128)(2,1)}, u32[]{:S(2)}, u32[]{:S(2)}) collective-permute-start(bf16[256,1024]{1,0:T(8,128)(2,1)} %get-tuple-element.168), channel_id=1, source_target_pairs={{0,16},{8,24},{16,0},{24,8},{1,17},{9,25},{17,1},{25,9},{2,18},{10... | collective-permute-start | bytes 1572872 | tf_op jit(solution)/shard_map/ppermute | solution.py:51
  450.4 9.6 %collective-permute-start.42 = (bf16[2,64,1536]{2,1,0:T(8,128)(2,1)S(1)}, bf16[2,64,1536]{2,1,0:T(8,128)(2,1)S(1)}, u32[]{:S(2)}, u32[]{:S(2)}) collective-permute-start(bf16[2,64,1536]{2,1,0:T(8,128)(2,1)S(1)} %pad_maximum_fusion.29), channel_id=1, source_target_pairs={{0,1},{1,0},{2,3},{3,2},{4,5},{5,4},{6,7},{7,6},{8,9},{9,8},{10,11... | collective-permute-start | bytes 1179656 | tf_op jit(solution)/shard_map/ppermute | solution.py:91
  451.0 8.9 %collective-permute-start.44 = (bf16[2,64,1536]{2,1,0:T(8,128)(2,1)S(1)}, bf16[2,64,1536]{2,1,0:T(8,128)(2,1)S(1)}, u32[]{:S(2)}, u32[]{:S(2)}) collective-permute-start(bf16[2,64,1536]{2,1,0:T(8,128)(2,1)S(1)} %stack.182), channel_id=1, source_target_pairs={{0,2},{2,0},{1,3},{3,1},{4,6},{6,4},{5,7},{7,5},{8,10},{10,8},{9,1... | collective-permute-start | bytes 1179656 | tf_op jit(solution)/shard_map/ppermute | solution.py:91
  460.0 10.0 %collective-permute-start.47 = (bf16[2,64,1664]{2,1,0:T(8,128)(2,1)S(1)}, bf16[2,64,1664]{2,1,0:T(8,128)(2,1)S(1)}, u32[]{:S(2)}, u32[]{:S(2)}) collective-permute-start(bf16[2,64,1664]{2,1,0:T(8,128)(2,1)S(1)} %pad_maximum_fusion.27), channel_id=1, source_target_pairs={{0,1},{1,0},{2,3},{3,2},{4,5},{5,4},{6,7},{7,6},{8,9},{9,8},{10,11... | collective-permute-start | bytes 1277960 | tf_op jit(solution)/shard_map/ppermute | solution.py:91
  461.4 11.4 %collective-permute-start.48 = (bf16[2,64,1664]{2,1,0:T(8,128)(2,1)S(1)}, bf16[2,64,1664]{2,1,0:T(8,128)(2,1)S(1)}, u32[]{:S(2)}, u32[]{:S(2)}) collective-permute-start(bf16[2,64,1664]{2,1,0:T(8,128)(2,1)S(1)} %stack.183), channel_id=1, source_target_pairs={{0,2},{2,0},{1,3},{3,1},{4,6},{6,4},{5,7},{7,5},{8,10},{10,8},{9,1... | collective-permute-start | bytes 1277960 | tf_op jit(solution)/shard_map/ppermute | solution.py:91
  475.6 19.3 %collective-permute-start.58 = (bf16[64,1664]{1,0:T(8,128)(2,1)S(1)}, bf16[64,1664]{1,0:T(8,128)(2,1)S(1)}, u32[]{:S(2)}, u32[]{:S(2)}) collective-permute-start(bf16[64,1664]{1,0:T(8,128)(2,1)S(1)} %get-tuple-element.275), channel_id=1, source_target_pairs={{0,2},{2,0},{1,3},{3,1},{4,6},{6,4},{5,7},{7,5},{8,10},{10,8},{9,1... | collective-permute-start | bytes 638984 | tf_op jit(solution)/shard_map/ppermute | solution.py:98
  478.7 6.7 %collective-permute-start.49 = (bf16[32,1536]{1,0:T(8,128)(2,1)S(1)}, bf16[32,1536]{1,0:T(8,128)(2,1)S(1)}, u32[]{:S(2)}, u32[]{:S(2)}) collective-permute-start(bf16[32,1536]{1,0:T(8,128)(2,1)S(1)} %get-tuple-element.311), channel_id=1, source_target_pairs={{0,8},{8,16},{16,24},{24,0},{1,9},{9,17},{17,25},{25,1},{2,10},{10... | collective-permute-start | bytes 294920 | tf_op jit(solution)/shard_map/ppermute | solution.py:51
  479.3 8.4 %collective-permute-start.50 = (bf16[32,1536]{1,0:T(8,128)(2,1)S(1)}, bf16[32,1536]{1,0:T(8,128)(2,1)S(1)}, u32[]{:S(2)}, u32[]{:S(2)}) collective-permute-start(bf16[32,1536]{1,0:T(8,128)(2,1)S(1)} %get-tuple-element.313), channel_id=1, source_target_pairs={{0,16},{8,24},{16,0},{24,8},{1,17},{9,25},{17,1},{25,9},{2,18},{10... | collective-permute-start | bytes 294920 | tf_op jit(solution)/shard_map/ppermute | solution.py:51
  481.0 7.0 %collective-permute-start.51 = (bf16[32,1536]{1,0:T(8,128)(2,1)S(1)}, bf16[32,1536]{1,0:T(8,128)(2,1)S(1)}, u32[]{:S(2)}, u32[]{:S(2)}) collective-permute-start(bf16[32,1536]{1,0:T(8,128)(2,1)S(1)} %get-tuple-element.312), channel_id=1, source_target_pairs={{0,24},{8,0},{16,8},{24,16},{1,25},{9,1},{17,9},{25,17},{2,26},{10... | collective-permute-start | bytes 294920 | tf_op jit(solution)/shard_map/ppermute | solution.py:51
  485.3 9.6 %collective-permute-start.59 = (bf16[64,1664]{1,0:T(8,128)(2,1)S(1)}, bf16[64,1664]{1,0:T(8,128)(2,1)S(1)}, u32[]{:S(2)}, u32[]{:S(2)}) collective-permute-start(bf16[64,1664]{1,0:T(8,128)(2,1)S(1)} %get-tuple-element.274), channel_id=1, source_target_pairs={{0,1},{1,0},{2,3},{3,2},{4,5},{5,4},{6,7},{7,6},{8,9},{9,8},{10,11... | collective-permute-start | bytes 638984 | tf_op jit(solution)/shard_map/ppermute | solution.py:99
  488.0 8.4 %collective-permute-start.52 = (bf16[32,1536]{1,0:T(8,128)(2,1)S(1)}, bf16[32,1536]{1,0:T(8,128)(2,1)S(1)}, u32[]{:S(2)}, u32[]{:S(2)}) collective-permute-start(bf16[32,1536]{1,0:T(8,128)(2,1)S(1)} %fusion.32), channel_id=1, source_target_pairs={{0,24},{8,0},{16,8},{24,16},{1,25},{9,1},{17,9},{25,17},{2,26},{10... | collective-permute-start | bytes 294920 | tf_op jit(solution)/shard_map/ppermute | solution.py:51
  492.5 7.6 %collective-permute-start.53 = (bf16[32,1536]{1,0:T(8,128)(2,1)S(1)}, bf16[32,1536]{1,0:T(8,128)(2,1)S(1)}, u32[]{:S(2)}, u32[]{:S(2)}) collective-permute-start(bf16[32,1536]{1,0:T(8,128)(2,1)S(1)} %fusion.32), channel_id=1, source_target_pairs={{0,16},{8,24},{16,0},{24,8},{1,17},{9,25},{17,1},{25,9},{2,18},{10... | collective-permute-start | bytes 294920 | tf_op jit(solution)/shard_map/ppermute | solution.py:51
  495.0 7.3 %collective-permute-start.54 = (bf16[32,1536]{1,0:T(8,128)(2,1)S(1)}, bf16[32,1536]{1,0:T(8,128)(2,1)S(1)}, u32[]{:S(2)}, u32[]{:S(2)}) collective-permute-start(bf16[32,1536]{1,0:T(8,128)(2,1)S(1)} %fusion.32), channel_id=1, source_target_pairs={{0,8},{8,16},{16,24},{24,0},{1,9},{9,17},{17,25},{25,1},{2,10},{10... | collective-permute-start | bytes 294920 | tf_op jit(solution)/shard_map/ppermute | solution.py:51
  495.2 7.8 %collective-permute-start.60 = (bf16[32,1664]{1,0:T(8,128)(2,1)S(1)}, bf16[32,1664]{1,0:T(8,128)(2,1)S(1)}, u32[]{:S(2)}, u32[]{:S(2)}) collective-permute-start(bf16[32,1664]{1,0:T(8,128)(2,1)S(1)} %get-tuple-element.308), channel_id=1, source_target_pairs={{0,8},{8,16},{16,24},{24,0},{1,9},{9,17},{17,25},{25,1},{2,10},{10... | collective-permute-start | bytes 319496 | tf_op jit(solution)/shard_map/ppermute | solution.py:51
  496.4 10.9 %collective-permute-start.61 = (bf16[32,1664]{1,0:T(8,128)(2,1)S(1)}, bf16[32,1664]{1,0:T(8,128)(2,1)S(1)}, u32[]{:S(2)}, u32[]{:S(2)}) collective-permute-start(bf16[32,1664]{1,0:T(8,128)(2,1)S(1)} %get-tuple-element.310), channel_id=1, source_target_pairs={{0,16},{8,24},{16,0},{24,8},{1,17},{9,25},{17,1},{25,9},{2,18},{10... | collective-permute-start | bytes 319496 | tf_op jit(solution)/shard_map/ppermute | solution.py:51
  500.2 7.2 %collective-permute-start.62 = (bf16[32,1664]{1,0:T(8,128)(2,1)S(1)}, bf16[32,1664]{1,0:T(8,128)(2,1)S(1)}, u32[]{:S(2)}, u32[]{:S(2)}) collective-permute-start(bf16[32,1664]{1,0:T(8,128)(2,1)S(1)} %get-tuple-element.309), channel_id=1, source_target_pairs={{0,24},{8,0},{16,8},{24,16},{1,25},{9,1},{17,9},{25,17},{2,26},{10... | collective-permute-start | bytes 319496 | tf_op jit(solution)/shard_map/ppermute | solution.py:51
  511.1 6.5 %collective-permute-start.64 = (bf16[32,1664]{1,0:T(8,128)(2,1)S(1)}, bf16[32,1664]{1,0:T(8,128)(2,1)S(1)}, u32[]{:S(2)}, u32[]{:S(2)}) collective-permute-start(bf16[32,1664]{1,0:T(8,128)(2,1)S(1)} %fusion.25), channel_id=1, source_target_pairs={{0,16},{8,24},{16,0},{24,8},{1,17},{9,25},{17,1},{25,9},{2,18},{10... | collective-permute-start | bytes 319496 | tf_op jit(solution)/shard_map/ppermute | solution.py:51
  512.6 6.5 %collective-permute-start.65 = (bf16[32,1664]{1,0:T(8,128)(2,1)S(1)}, bf16[32,1664]{1,0:T(8,128)(2,1)S(1)}, u32[]{:S(2)}, u32[]{:S(2)}) collective-permute-start(bf16[32,1664]{1,0:T(8,128)(2,1)S(1)} %fusion.25), channel_id=1, source_target_pairs={{0,8},{8,16},{16,24},{24,0},{1,9},{9,17},{17,25},{25,1},{2,10},{10... | collective-permute-start | bytes 319496 | tf_op jit(solution)/shard_map/ppermute | solution.py:51
  513.4 7.6 %collective-permute-start.55 = (bf16[128,1536]{0,1:T(8,128)(2,1)}, bf16[128,1536]{0,1:T(8,128)(2,1)S(1)}, u32[]{:S(2)}, u32[]{:S(2)}) collective-permute-start(bf16[128,1536]{0,1:T(8,128)(2,1)} %broadcast_select_fusion.3), channel_id=1, source_target_pairs={{0,4},{4,0},{1,5},{5,1},{2,6},{6,2},{3,7},{7,3},{8,12},{12,8},{9,1... | collective-permute-start | bytes 1179656 | tf_op jit(solution)/shard_map/ppermute | solution.py:47
  521.0 7.2 %collective-permute-start.66 = (bf16[128,1664]{0,1:T(8,128)(2,1)}, bf16[128,1664]{0,1:T(8,128)(2,1)}, u32[]{:S(2)}, u32[]{:S(2)}) collective-permute-start(bf16[128,1664]{0,1:T(8,128)(2,1)} %broadcast_select_fusion), channel_id=1, source_target_pairs={{0,4},{4,0},{1,5},{5,1},{2,6},{6,2},{3,7},{7,3},{8,12},{12,8},{9,1... | collective-permute-start | bytes 1277960 | tf_op jit(solution)/shard_map/ppermute | solution.py:47
  (59 other events, 387.2 us)

commit v5 on v4

--- a/solution.py
+++ b/solution.py
@@ -118,17 +118,16 @@
     return [rows] + [cyclic(rows, size, -k) for k in range(1, size)]
 
 
-def column_low(mine, other):
-    both = mine.astype(F32) + swap_core(other).astype(F32)
-    return both[0], both.astype(B16)
-
-
-def column_send(low, size):
-    return [cyclic(low[k], size, k) for k in range(1, size)]
+def column_send_some(low, size):
+    return [cyclic(low[k], size, k) for k in range(1, size) if 2 * k != size]
+
+
+def column_send_last(low, size, *hold):
+    return [cyclic(after(low[size // 2], *hold), size, size // 2)]
 
 
 def column_sum(own, pieces):
-    return own + sum(piece.astype(F32) for piece in pieces)
+    return own.astype(F32) + sum(piece.astype(F32) for piece in pieces)
 
 
 def assemble(places, shard, moved, other, rows):
@@ -244,7 +243,7 @@
     )(lead, *args)
 
 
-def combine_rows(lead, first, packed, slot_rows, local, capacity):
+def combine_rows(lead, first, packed, slot_rows, local, capacity, addend=None):
     pieces, packed_rows, code_width = packed.shape
     tokens = packed_rows - 16
     halves = len(slot_rows)
@@ -265,12 +264,16 @@
                 select, rest[h][0], (((0,), (0,)), ((), ())), preferred_element_type=F32
             )
             total = part if total is None else total + part
-        rest[halves][0] = total.astype(B16)
+        if addend is not None:
+            total = total + rest[halves][0].astype(F32)
+        rest[-1][0] = total.astype(B16)
 
     in_specs = [pl.BlockSpec((1, 16, code_width), lambda p, lead: (p, tokens // 16, 0))]
     in_specs += [
         pl.BlockSpec((1, slots, width), lambda p, lead: (p + first, 0, 0)) for _ in range(halves)
     ]
+    added = [] if addend is None else [addend]
+    in_specs += [pl.BlockSpec((1, tokens, width), lambda p, lead: (p, 0, 0)) for _ in added]
     return pl.pallas_call(
         kernel,
         out_shape=jax.ShapeDtypeStruct((pieces, tokens, width), B16),
@@ -282,7 +285,7 @@
         ),
         compiler_params=pltpu.CompilerParams(vmem_limit_bytes=VMEM_LIMIT),
         name="combine",
-    )(lead, packed, *slot_rows)
+    )(lead, packed, *slot_rows, *added)
 
 
 def experts(order, start, count, rows, grads, gates, weights, chunks, capacity, in_rows, mid_rows):
@@ -488,14 +491,17 @@
     return jnp.cos(angles), jnp.sin(angles) * sign[None, :]
 
 
-def attention_forward(x_all, dense_full, bias, cosine, sine, tok_rows):
-    seq_len, width = x_all.shape
+def attention_forward(x_own, x_parts, dense_full, bias, cosine, sine, routed):
+    tok_rows, width = x_own.shape
+    seq_len = 4 * tok_rows
     scale = HD ** (-0.5)
     wide, narrow = H * HD, KVH * HD
 
     def kernel(
-        x_ref, tail_ref, wo_ref, wq_ref, wk_ref, wv_ref, bias_ref, cos_ref, sin_ref,
-        normed_ref, q_out, k_out, v_out, att_out, total_out, misc_out, residual_out, moe_out,
+        own_ref, xa_ref, xb_ref, ya_ref, yb_ref, da_ref, db_ref, ea_ref, eb_ref,
+        tail_ref, wo_ref, wq_ref, wk_ref, wv_ref, bias_ref, cos_ref, sin_ref, routed_ref,
+        x_ref, normed_ref, q_out, k_out, v_out, att_out, total_out, misc_out, residual_out, moe_out,
+        gates_out,
     ):
         step = pl.program_id(0)
 
@@ -503,6 +509,10 @@
         def _():
             rows = jnp.transpose(tail_ref[...].astype(F32))
             misc_out[...] = rows
+            at = 0
+            for ref in (own_ref, xa_ref, xb_ref, ya_ref, yb_ref, da_ref, ea_ref, db_ref, eb_ref):
+                x_ref[at : at + ref.shape[0], :] = ref[...]
+                at += ref.shape[0]
             x = x_ref[...].astype(F32)
             scaled = x * lax.rsqrt(jnp.mean(x * x, axis=1, keepdims=True) + EPSILON)
             normed_ref[...] = (scaled * rows[EXPERTS : EXPERTS + 1, :]).astype(B16)
@@ -545,7 +555,13 @@
         def _():
             total = residual_out[...]
             scaled = total * lax.rsqrt(jnp.mean(total * total, axis=1, keepdims=True) + EPSILON)
-            moe_out[...] = (scaled * misc_out[EXPERTS + 1 : EXPERTS + 2, :]).astype(B16)
+            moe_in = (scaled * misc_out[EXPERTS + 1 : EXPERTS + 2, :]).astype(B16)
+            moe_out[...] = moe_in
+            logits = jnp.dot(moe_in, tail_ref[...], preferred_element_type=F32)
+            here = routed_ref[...] > 0.0
+            peak = jnp.max(jnp.where(here, logits, MASKED_SCORE), axis=1, keepdims=True)
+            lifted = jnp.where(here, jnp.exp(jnp.minimum(logits - peak, 0.0)), 0.0)
+            gates_out[...] = lifted / jnp.sum(lifted, axis=1, keepdims=True)
 
     def fixed(*block):
         return pl.BlockSpec(block, lambda i: (0,) * len(block))
@@ -557,7 +573,12 @@
         kernel,
         grid=(GROUPS,),
         in_specs=[
-            fixed(seq_len, width),
+            fixed(tok_rows, width),
+            *[
+                pl.BlockSpec((part.shape[0], width), lambda i, c=c: (0, c))
+                for part in x_parts
+                for c in range(2)
+            ],
             pl.BlockSpec((width, 128), lambda i: (0, (width + wide + 2 * narrow) // 128)),
             pl.BlockSpec((256, width), lambda i: (i, 0)),
             columns(width, 256, width // 256),
@@ -566,8 +587,10 @@
             fixed(seq_len, tok_rows),
             fixed(seq_len, 128),
             fixed(seq_len, 128),
+            fixed(tok_rows, 128),
         ],
         out_specs=[
+            fixed(seq_len, width),
             fixed(seq_len, width),
             columns(tok_rows, 256),
             columns(seq_len, 128),
@@ -577,8 +600,10 @@
             fixed(128, width),
             fixed(tok_rows, width),
             fixed(tok_rows, width),
+            fixed(tok_rows, 128),
         ],
         out_shape=[
+            jax.ShapeDtypeStruct((seq_len, width), B16),
             jax.ShapeDtypeStruct((seq_len, width), B16),
             jax.ShapeDtypeStruct((tok_rows, wide), B16),
             jax.ShapeDtypeStruct((seq_len, narrow), B16),
@@ -588,30 +613,38 @@
             jax.ShapeDtypeStruct((128, width), F32),
             jax.ShapeDtypeStruct((tok_rows, width), F32),
             jax.ShapeDtypeStruct((tok_rows, width), B16),
+            jax.ShapeDtypeStruct((tok_rows, 128), F32),
         ],
         compiler_params=pltpu.CompilerParams(vmem_limit_bytes=VMEM_LIMIT),
         name="attention",
-    )(x_all, *[dense_full] * 5, bias, cosine, sine)
+    )(
+        x_own, *[part for part in x_parts for _ in range(2)], *[dense_full] * 5,
+        bias, cosine, sine, routed,
+    )
 
 
 def attention_backward(
-    where_here, out_grad_low, attended, moe_in, logit_low, moe_gain_row, saved,
-    x_all, dense_full, bias, cosine, sine,
+    where_here, moe_sums, out_grad, residual, gates, misc, attended, moe_in, saved,
+    dense_full, bias, cosine, sine,
 ):
-    normed_all, query_rot, key_rot, value_all, totals = saved
+    x_all, normed_all, query_rot, key_rot, value_all, totals = saved
+    terms = len(moe_sums)
     seq_len, width = x_all.shape
     tok_rows = query_rot.shape[0]
     scale = HD ** (-0.5)
     wide, narrow = H * HD, KVH * HD
     block = width // 8
-    half = width // 2
-
-    def kernel(
-        here_ref, og_ref, wo_ref, att_ref, moe_ref, logit_ref, gain_ref,
-        normed_ref, q_ref, k_ref, v_ref, total_ref,
-        x_ref, wq_ref, wk_ref, wv_ref, bias_ref, cos_ref, sin_ref,
-        first_out, second_out, normed_out, normed_t, grad_sum,
-    ):
+    output_at = wide + 2 * narrow
+
+    def kernel(here_ref, *refs):
+        sums = refs[:terms]
+        (
+            grad_ref, residual_ref, gates_ref, misc_ref, tail_ref, wo_ref, att_ref, moe_ref,
+            normed_ref, q_ref, k_ref, v_ref, total_ref,
+            x_ref, wq_ref, wk_ref, wv_ref, bias_ref, cos_ref, sin_ref,
+            dense_out, normed_out, residual_out,
+            normed_t, grad_sum, og_ref, logit_ref, gain_ref,
+        ) = refs[terms:]
         step = pl.program_id(0)
         dp, core = here_ref[0], here_ref[1]
 
@@ -619,6 +652,28 @@
         def _():
             normed_t[...] = jnp.transpose(normed_ref[...])
             grad_sum[...] = jnp.zeros((seq_len, width), F32)
+            total = sums[0][0].astype(F32)
+            for ref in sums[1:]:
+                total = total + ref[...].astype(F32)
+            behind = total[:, width:]
+            gate_grad = behind + pltpu.roll(behind, 128 - EXPERTS, 1)
+            gate = gates_ref[...]
+            centre = jnp.sum(gate * gate_grad, axis=1, keepdims=True)
+            logit_low = (gate * (gate_grad - centre)).astype(B16)
+            logit_ref[...] = logit_low
+            moe_grad = total[:, :width] + lax.dot_general(
+                logit_low, tail_ref[...], NT, preferred_element_type=F32
+            )
+            residual = residual_ref[...]
+            rate = lax.rsqrt(jnp.mean(residual * residual, axis=1, keepdims=True) + EPSILON)
+            gain_ref[...] = jnp.sum(moe_grad * residual * rate, axis=0, keepdims=True)
+            lifted = moe_grad * misc_ref[EXPERTS + 1 : EXPERTS + 2, :]
+            inner = jnp.mean(lifted * residual, axis=1, keepdims=True)
+            residual_grad = (
+                grad_ref[...].astype(F32) + rate * lifted - residual * (rate * rate * rate * inner)
+            )
+            residual_out[...] = residual_grad
+            og_ref[...] = residual_grad.astype(B16)
 
         og = og_ref[...]
         att_grad = lax.dot_general(og, wo_ref[...], NT, preferred_element_type=F32).astype(B16)
@@ -657,25 +712,25 @@
             [turn(query_grad[:, 128 * j : 128 * (j + 1)], cos, sin) for j in range(2)], axis=1
         ).astype(B16)
 
-        def give(out_ref, grad, lanes):
+        def give(grad, lanes):
             for m in range(4):
                 for c in range(2):
-                    out_ref[core ^ c, dp ^ m, :, lanes] = grad[
+                    dense_out[core ^ c, dp ^ m, :, lanes] = grad[
                         (2 * m + c) * block : (2 * m + c + 1) * block
                     ].astype(B16)
 
-        lanes = pl.ds(pl.multiple_of(step * 256, 256), 256)
         give(
-            first_out,
             jnp.dot(normed_t[:, :tok_rows], query_grad, preferred_element_type=F32),
-            lanes,
+            pl.ds(pl.multiple_of(step * 256, 256), 256),
         )
-        give(second_out, jnp.dot(normed_t[...], kv_grad, preferred_element_type=F32), lanes)
+        give(
+            jnp.dot(normed_t[...], kv_grad, preferred_element_type=F32),
+            pl.ds(pl.multiple_of(wide + step * 256, 256), 256),
+        )
         out_part = lax.dot_general(att_ref[...], og, TN, preferred_element_type=F32).astype(B16)
         for c in range(2):
             rows = slice(c * block, (c + 1) * block)
-            first_out[core ^ c, dp ^ step, :, wide : wide + half] = out_part[rows, :half]
-            second_out[core ^ c, dp ^ step, :, wide : wide + half] = out_part[rows, half:]
+            dense_out[core ^ c, dp ^ step, :, output_at : output_at + width] = out_part[rows]
         kv_weights = jnp.concatenate([wk_ref[...], wv_ref[...]], axis=1)
         grad_sum[...] += lax.dot_general(kv_grad, kv_weights, NT, preferred_element_type=F32)
         grad_sum[:tok_rows, :] += lax.dot_general(
@@ -696,7 +751,7 @@
             extra = lax.dot_general(
                 moe_ref[...], logit_ref[...], TN, preferred_element_type=F32
             ) + jnp.transpose(gains)
-            give(first_out, extra, slice(wide + half, wide + half + EXTRA))
+            give(extra, slice(output_at + width, output_at + width + EXTRA))
 
     def fixed(*shape):
         return pl.BlockSpec(shape, lambda i, here: (0,) * len(shape))
@@ -705,9 +760,9 @@
         return pl.BlockSpec((rows, cols), lambda i, here: (0, lead + i))
 
     shapes = [
-        jax.ShapeDtypeStruct((2, 4, block, wide + half + EXTRA), B16),
-        jax.ShapeDtypeStruct((2, 4, block, 2 * narrow + half), B16),
+        jax.ShapeDtypeStruct((2, 4, block, output_at + width + EXTRA), B16),
         jax.ShapeDtypeStruct((seq_len, width), B16),
+        jax.ShapeDtypeStruct((tok_rows, width), F32),
     ]
     return pl.pallas_call(
         kernel,
@@ -716,12 +771,18 @@
             num_scalar_prefetch=1,
             grid=(GROUPS,),
             in_specs=[
+                pl.BlockSpec((1, tok_rows, width + 128), lambda i, here: (0, 0, 0)),
+                *[fixed(tok_rows, width + 128)] * (terms - 1),
                 fixed(tok_rows, width),
+                fixed(tok_rows, width),
+                fixed(tok_rows, 128),
+                fixed(128, width),
+                pl.BlockSpec(
+                    (width, 128), lambda i, here: (0, (width + wide + 2 * narrow) // 128)
+                ),
                 pl.BlockSpec((256, width), lambda i, here: (i, 0)),
                 columns(tok_rows, 256),
                 fixed(tok_rows, width),
-                fixed(tok_rows, EXTRA),
-                fixed(1, width),
                 fixed(seq_len, width),
                 columns(tok_rows, 256),
                 columns(seq_len, 128),
@@ -739,13 +800,16 @@
             scratch_shapes=[
                 pltpu.VMEM((width, seq_len), B16),
                 pltpu.VMEM((seq_len, width), F32),
+                pltpu.VMEM((tok_rows, width), B16),
+                pltpu.VMEM((tok_rows, EXTRA), B16),
+                pltpu.VMEM((1, width), F32),
             ],
         ),
         compiler_params=pltpu.CompilerParams(vmem_limit_bytes=VMEM_LIMIT),
         name="attention_grad",
     )(
-        where_here, out_grad_low, dense_full, attended, moe_in, logit_low, moe_gain_row,
-        normed_all, query_rot, key_rot, value_all, totals,
+        where_here, *moe_sums, out_grad, residual, gates, misc, dense_full, dense_full, attended,
+        moe_in, normed_all, query_rot, key_rot, value_all, totals,
         x_all, dense_full, dense_full, dense_full, bias, cosine, sine,
     )
 
@@ -845,13 +909,6 @@
             x_pack = jnp.concatenate([layer_input[:side], layer_input[side:]], axis=1)
             start_parts = grid_gather(jnp.concatenate([x_pack, core_half(dense_pack, core)], axis=1))
             dense_parts = [part[:, 2 * model_width :] for part in start_parts]
-            from_x, from_y, diag_a, diag_b = [
-                [part[:, :model_width], part[:, model_width : 2 * model_width]]
-                for part in start_parts
-            ]
-            x_all = jnp.concatenate(
-                [layer_input, *from_x, *from_y, diag_a[0], diag_b[0], diag_a[1], diag_b[1]], axis=0
-            )
             dense_full = dense_assemble(dense_pack, dense_parts, dp_index, core, grad_pieces[1])
         else:
             dense_full = lax.all_gather(dense_pack, ("y", "x"), axis=0, tiled=True)
@@ -884,17 +941,26 @@
             weights = [every[j] for j in range(dp_size)]
             near_0 = ()
         order = jnp.concatenate([relative, lead])
-        grads_mine = jnp.stack(after(grad_pieces, *near_0))
+        grads_mine = jnp.stack(after(grad_pieces, *near_0, dense_full))
         grads_other = swap_core(grads_mine)
         visible = (key_pos[None, :] <= query_pos[:, None]) | (key_pos[None, :] < prefix_len[0])
         chunks = []
         if small_grid:
-            x_all = after(x_all, grads_mine, *near_0)
-            bias = jnp.where(visible.T, 0.0, MASKED_SCORE)
+            bias_hold = (grads_mine, *near_0)
+            bias = after(jnp.where(visible.T, 0.0, MASKED_SCORE), *bias_hold)
             cosine, sine = turn_tables(key_pos.astype(F32))
             (
-                normed_all, query_rot, key_rot, value_all, attended, totals, misc, residual, moe_in,
-            ) = attention_forward(x_all, dense_full, bias, cosine, sine, tok_rows)
+                x_all, normed_all, query_rot, key_rot, value_all, attended, totals, misc, residual,
+                moe_in, gates,
+            ) = attention_forward(
+                layer_input,
+                start_parts,
+                dense_full,
+                bias,
+                cosine,
+                sine,
+                jnp.pad(routed.astype(F32), ((0, 0), (0, 128 - EXPERTS))),
+            )
             moe_in = after(moe_in, grads_other, *near_1, *far_0)
             router_rows = misc[:EXPERTS].astype(B16)
             full_attn_gain = misc[EXPERTS]
@@ -947,7 +1013,12 @@
             stage_1 = far_and_next(after(near_1, moe_in), pack[2])
         (slot_grads_mine,) = dispatch_rows(lead, after(grads_mine, moe_in), None, None, local, capacity)
         (slot_grads_other,) = dispatch_rows(
-            lead, after(grads_other, slot_grads_mine, *stage_1), None, None, local, capacity
+            lead,
+            after(grads_other, slot_grads_mine, *stage_1, row_pieces[1], row_pieces[-1]),
+            None,
+            None,
+            local,
+            capacity,
         )
         if small_grid:
             stage_2 = far_and_next(after(stage_1, slot_grads_other), pack[3])
@@ -958,19 +1029,16 @@
                 [(part, middle) for part in stage_1] + [(part, 0) for part in stage_2[::-1]],
                 [(part, middle) for part in stage_2] + [(part, 0) for part in last_far],
             ]
-        rows_mine = jnp.stack(after(row_pieces, slot_grads_other, *stage_1))
-        rows_other = swap_core(rows_mine)
+        row_pieces = after(row_pieces, slot_grads_other)
+        rows_mine = after(jnp.stack(row_pieces), *stage_2)
+        rows_other = jnp.stack([swap_core(piece) for piece in row_pieces])
         slot_rows_mine, slot_gates_mine = dispatch_rows(
-            lead, grads_mine, after(rows_mine, *stage_2), router_rows, local, capacity
+            lead, grads_mine, rows_mine, router_rows, local, capacity
         )
         slot_rows_other, slot_gates_other = dispatch_rows(
             lead, grads_other, after(rows_other, slot_rows_mine), router_rows, local, capacity
         )
         slot_rows_other = after(slot_rows_other, *last_far)
-        logits = lax.dot_general(moe_in, router_rows, NT, preferred_element_type=F32)
-        peak = jnp.max(jnp.where(routed, logits, MASKED_SCORE), axis=-1, keepdims=True)
-        lifted = jnp.where(routed, jnp.exp(jnp.minimum(logits - peak, 0.0)), 0.0)
-        gate_weights = lifted / jnp.sum(lifted, axis=-1, keepdims=True)
         ys, dxs, weight_grads, sums = [], [], [], []
         for half in range(halves):
             y, dx, grads = experts(
@@ -1012,84 +1080,87 @@
             via = cross(early[3], early[7])
             dxs = after(dxs, *via)
             early_got = second_step(early, via, late[3], late[7])
-        dx_other = combine_rows(lead, z_size, grads_other, dxs, local, capacity)
-        dx_mine = combine_rows(lead, 0, grads_mine, dxs, local, capacity)
-        dx_own, dx_low = column_low(dx_mine, dx_other)
-        dx_pieces = column_send(dx_low, z_size)
-        ys = after(ys, dx_low)
-        y_other = combine_rows(lead, z_size, grads_other, ys, local, capacity)
-        y_mine = combine_rows(lead, 0, grads_mine, ys, local, capacity)
-        moe_sum = column_sum(dx_own, after(dx_pieces, y_other, y_mine))
-        y_own, y_low = column_low(y_mine, after(y_other, moe_sum))
-        y_pieces = [cyclic(y_low[k], z_size, k) for k in range(1, z_size) if 2 * k != z_size]
+        dx_other = swap_core(combine_rows(lead, z_size, grads_other, dxs, local, capacity))
+        dx_low = combine_rows(lead, 0, grads_mine, dxs, local, capacity, dx_other)
+        dx_pieces = column_send_some(dx_low, z_size)
+        y_other = combine_rows(lead, z_size, grads_other, after(ys, dx_low), local, capacity)
+        dx_pieces, y_other = after((dx_pieces, y_other), y_other, *dx_pieces)
+        dx_pieces += column_send_last(dx_low, z_size, *dx_pieces)
+        ys, y_other = after((ys, swap_core(y_other)), *dx_pieces)
+        y_low = combine_rows(lead, 0, grads_mine, ys, local, capacity, y_other)
+        dx_pieces = after(dx_pieces, y_low)
+        y_pieces = column_send_some(y_low, z_size)
         if small_grid:
-            late_got = second_step(late, [got[2:3] for got in after(early_got, moe_sum)])
-        moe_in_grad = moe_sum[:, :model_width]
-        gate_grad = (
-            moe_sum[:, model_width : model_width + EXPERTS]
-            + moe_sum[:, model_width + EXPERTS : model_width + 2 * EXPERTS]
-        )
-        grad_out = out_grad.astype(F32)
-        centre = jnp.sum(gate_weights * gate_grad, axis=-1, keepdims=True)
-        logit_low = (gate_weights * (gate_grad - centre)).astype(B16)
-        moe_in_grad = moe_in_grad + jnp.dot(logit_low, router_rows, preferred_element_type=F32)
-        norm_value, second_pull = jax.vjp(rms_norm, residual, full_moe_gain)
-        resid_norm_grad, moe_gain_grad = second_pull(moe_in_grad)
-        residual_grad = grad_out + resid_norm_grad
-        attn_out_grad = residual_grad.astype(B16)
+            early_got = after(early_got, y_low)
+            late_got = second_step(late, [got[2:3] for got in early_got])
         if small_grid:
-            logit_wide = jnp.pad(logit_low, ((0, 0), (0, EXTRA - EXPERTS)))
-            first_blocks, second_blocks, normed_part = attention_backward(
+            dense_blocks, normed_part, residual_grad = attention_backward(
                 jnp.stack([dp_index, core]).astype(jnp.int32),
-                after(attn_out_grad, y_low),
+                (dx_low, *dx_pieces),
+                out_grad,
+                residual,
+                gates,
+                misc,
                 attended,
                 moe_in,
-                logit_wide,
-                moe_gain_grad[None, :],
-                (normed_all, query_rot, key_rot, value_all, totals),
-                x_all,
+                (x_all, normed_all, query_rot, key_rot, value_all, totals),
                 dense_full,
-                bias,
+                after(bias, *early_got),
                 cosine,
                 sine,
             )
-            y_pieces, late_got = after((y_pieces, late_got), normed_part)
-            y_pieces.append(cyclic(after(y_low[z_size // 2], *y_pieces), z_size, z_size // 2))
+            late_got, y_pieces = after((late_got, y_pieces), normed_part)
+            normed_part, dense_blocks = after((normed_part, dense_blocks), *late_got, *y_pieces)
+            y_pieces += column_send_last(y_low, z_size, *y_pieces)
             normed_first, normed_a, normed_b = row_halves(
                 normed_part.reshape(4, tok_rows, model_width)
             )
-            second_first, second_a, second_b = row_halves(core_sum(second_blocks))
-            first_first, first_a, first_b = row_halves(core_sum(first_blocks))
+            dense_first, dense_a, dense_b = row_halves(core_sum(dense_blocks))
             normed_got = grid_scatter_first(*normed_first)
-            second_got = grid_scatter_first(*after(second_first, *normed_got))
-            first_got = grid_scatter_first(*after(first_first, *second_got))
-            second_sum = dense_finish(grid_scatter_second(second_got, second_a, second_b, *first_got), z, core)
-            first_sum = dense_finish(grid_scatter_second(first_got, first_a, first_b), z, core)
+            dense_got = grid_scatter_first(*after(dense_first, *normed_got))
+            dense_halves = after(grid_scatter_second(dense_got, dense_a, dense_b), *y_pieces)
+            dense_total = dense_finish(dense_halves, z, core)
             normed_grad = jnp.concatenate(
-                grid_scatter_second(normed_got, normed_a, normed_b, *first_got), axis=0
+                grid_scatter_second(normed_got, normed_a, normed_b, *dense_got), axis=0
             )
             first_value, first_pull = jax.vjp(lambda v: rms_norm(v, full_attn_gain), in_float)
             input_grad = residual_grad + first_pull(normed_grad)[0]
-            y_pieces = after(y_pieces, second_sum)
-            at = wide + model_width // 2
-            query_sum = first_sum[:, :wide]
-            output_sum = jnp.concatenate(
-                [first_sum[:, wide:at], second_sum[:, 2 * narrow :]], axis=1
-            )
-            router_sum = first_sum[:, at : at + EXPERTS]
-            attn_gain_sum = first_sum[:, at + EXPERTS]
-            moe_gain_sum = first_sum[:, at + EXPERTS + 1]
+            kv_at = wide + 2 * narrow
+            query_sum = dense_total[:, :wide]
             key_sum, value_sum = [
                 jnp.concatenate(
                     [
-                        second_sum[:, 256 * i + lead_col : 256 * i + lead_col + 128]
+                        dense_total[:, wide + 256 * i + lead_col : wide + 256 * i + lead_col + 128]
                         for i in range(GROUPS)
                     ],
                     axis=1,
                 )
                 for lead_col in (0, 128)
             ]
+            output_sum = dense_total[:, kv_at : kv_at + model_width]
+            router_sum = dense_total[:, kv_at + model_width : kv_at + model_width + EXPERTS]
+            attn_gain_sum = dense_total[:, kv_at + model_width + EXPERTS]
+            moe_gain_sum = dense_total[:, kv_at + model_width + EXPERTS + 1]
         else:
+            y_pieces += column_send_last(y_low, z_size)
+            moe_sum = column_sum(dx_low[0], dx_pieces)
+            moe_in_grad = moe_sum[:, :model_width]
+            gate_grad = (
+                moe_sum[:, model_width : model_width + EXPERTS]
+                + moe_sum[:, model_width + EXPERTS : model_width + 2 * EXPERTS]
+            )
+            logits = lax.dot_general(moe_in, router_rows, NT, preferred_element_type=F32)
+            peak = jnp.max(jnp.where(routed, logits, MASKED_SCORE), axis=-1, keepdims=True)
+            lifted = jnp.where(routed, jnp.exp(jnp.minimum(logits - peak, 0.0)), 0.0)
+            gate_weights = lifted / jnp.sum(lifted, axis=-1, keepdims=True)
+            grad_out = out_grad.astype(F32)
+            centre = jnp.sum(gate_weights * gate_grad, axis=-1, keepdims=True)
+            logit_low = (gate_weights * (gate_grad - centre)).astype(B16)
+            moe_in_grad = moe_in_grad + jnp.dot(logit_low, router_rows, preferred_element_type=F32)
+            norm_value, second_pull = jax.vjp(rms_norm, residual, full_moe_gain)
+            resid_norm_grad, moe_gain_grad = second_pull(moe_in_grad)
+            residual_grad = grad_out + resid_norm_grad
+            attn_out_grad = residual_grad.astype(B16)
             router_grad = jnp.einsum("td,te->de", moe_in, logit_low, preferred_element_type=F32)
             wout_grad = jnp.einsum("tc,td->cd", attended, attn_out_grad, preferred_element_type=F32)
             attended_grad = (
@@ -1140,7 +1211,6 @@
             first_value, first_pull = jax.vjp(rms_norm, in_float, full_attn_gain)
             input_norm_grad, attn_gain_grad = first_pull(normed_grad)
             input_grad = residual_grad + input_norm_grad
-            y_pieces.append(cyclic(y_low[z_size // 2], z_size, z_size // 2))
             query_sum = dense_sum(wq_grad)
             key_sum = dense_sum(wk_grad)
             value_sum = dense_sum(wv_grad)
@@ -1159,7 +1229,7 @@
             router_sum = extra_sum[:, :EXPERTS]
             attn_gain_sum = extra_sum[:, EXPERTS]
             moe_gain_sum = extra_sum[:, EXPERTS + 1]
-        layer_output = (residual + column_sum(y_own, y_pieces)).astype(B16)
+        layer_output = (residual + column_sum(y_low[0], y_pieces)).astype(B16)
         if small_grid:
             parts = grid_sum(early, early_got) + grid_sum(late, late_got)
             pack_grad = jnp.concatenate(parts, axis=0)

time: 543 us -> 552 us (1.017)
  waiting for transfers between devices: 169 us -> 212 us
  starting transfers between devices: 91.2 us -> 67.9 us
  other arithmetic: 62.5 us -> 54 us
    ppermute x24 -> x18, waiting for transfers between devices: 29.2 us -> 151 us  [cyclic(): lax.ppermute(rows, 'z', [(i, (i + shift) % size) for i in range(size)])]
    ppermute x10, waiting for transfers between devices: 64 us -> 0.03 us  [cross(): return (lax.ppermute(to_x, 'x', SWAP), lax.ppermute(to_y, 'y', SWAP))]
    ppermute x24 -> x18, starting transfers between devices: 50.8 us -> 31.4 us  [cyclic(): lax.ppermute(rows, 'z', [(i, (i + shift) % size) for i in range(size)])]
    ppermute x6, waiting for transfers between devices: 33.4 us -> 25.3 us  [gather_near(): return [lax.ppermute(shard, 'x', SWAP), lax.ppermute(shard, 'y', SWAP)]]
    add x2 -> x0, other arithmetic: 7.3 us -> none  [the longest x1 5.14 us: column_low(): both = mine.astype(F32) + swap_core(other).astype(F32)]
    ppermute x6 -> x4, waiting for transfers between devices: 27.8 us -> 20.7 us  [grid_scatter_first(): return (lax.ppermute(first_a, 'x', SWAP), lax.ppermute(first_b, 'y', SWAP))]
    unnamed x118 -> x109, local copies, waits for them, and re-layouts: 21.5 us -> 19.2 us
  transfers between devices with their start and end apart: 67 -> 58, of which waited for: 27 -> 23; matrix products, arithmetic and copies ran while one was open for 17% -> 10% of each run, Pallas kernels for 23% -> 23%
where the time goes in v5:
time: 552 us; the launch traced here: 543 us
  waiting for transfers between devices  212 us (38%)
  Pallas kernels  158 us (29%)
  starting transfers between devices  67.9 us (12%)
  other arithmetic  54 us (10%)
  local copies, waits for them, and re-layouts  48.6 us (9%)
    ppermute x18, waiting for transfers between devices, cyclic(): lax.ppermute(rows, 'z', [(i, (i + shift) % size) for i in range(size)])  151 us
    pallas_call x2, Pallas kernels, experts(): pl.pallas_call(kernel, out_shape=out_shape, grid_spec=pltpu.PrefetchScala...  48.5 us
    pallas_call x1, Pallas kernels, attention_backward(): pl.pallas_call(kernel, out_shape=shapes, grid_spec=pltpu.PrefetchScalarGr...  36.5 us
    ppermute x18, starting transfers between devices, cyclic(): lax.ppermute(rows, 'z', [(i, (i + shift) % size) for i in range(size)])  31.4 us
    pallas_call x1, Pallas kernels, attention_forward(): pl.pallas_call(kernel, grid=(GROUPS,), in_specs=[fixed(tok_rows, width),...  25.3 us
    ppermute x6, waiting for transfers between devices, gather_near(): return [lax.ppermute(shard, 'x', SWAP), lax.ppermute(shard, 'y', SWAP)]  25.3 us
    pallas_call x4, Pallas kernels, combine_rows(): pl.pallas_call(kernel, out_shape=jax.ShapeDtypeStruct((pieces, tokens, wi...  21 us
    ppermute x4, waiting for transfers between devices, grid_scatter_first(): return (lax.ppermute(first_a, 'x', SWAP), lax.ppermute(first_b, 'y', SWAP))  20.7 us
  transfers between devices with their start and end apart: 58, of which 23 were waited for; matrix products, arithmetic and copies ran while one was open for 10% of the time, Pallas kernels for 23%

profile of v5, /device:TPU:0, one launch (start us, length us, event | category | flops | bytes accessed | tf_op | source)
XLA Modules:
  0.0 543.2 jit_solution(13434807788048932058)
XLA Ops:
  4.1 2.4 concatenate.66.shard_ref
  8.8 3.0 collective-permute-start
  13.6 2.6 convert_reduce_fusion
  16.2 25.3 %collective-permute-done.xa_ref.xb_ref = bf16[128,5248]{1,0:T(8,128)(2,1)S(1)} collective-permute-done((bf16[128,5248]{1,0:T(8,128)(2,1)}, bf16[128,5248]{1,0:T(8,128)(2,1)S(1)}, u32[]{:S(2)}, u32[]{:S(2)}) %collective-permute-start) | collective-permute-done | bytes 1343520 | tf_op jit(solution)/shard_map/ppermute | solution.py:59
  41.5 1.8 collective-permute-start.2
  43.4 1.6 collective-permute-start.3
  46.0 3.6 collective-permute-start.4
  49.6 8.3 %collective-permute-done.2.da_ref.db_ref = bf16[64,5248]{1,0:T(8,128)(2,1)S(1)} collective-permute-done((bf16[64,5248]{1,0:T(8,128)(2,1)S(1)}, bf16[64,5248]{1,0:T(8,128)(2,1)S(1)}, u32[]{:S(2)}, u32[]{:S(2)}) %collective-permute-start.2) | collective-permute-done | bytes 671776 | tf_op jit(solution)/shard_map/ppermute | solution.py:65
  60.1 1.7 pad_maximum_fusion.2.moved_ref
  63.8 1.5 slice_bitcast_fusion.1
  68.6 2.6 collective-permute-start.6
  71.2 1.6 collective-permute-start.7
  73.4 6.9 %assemble.1.tail_ref.wo_ref.wq_ref.wk_ref.wv_ref.refs_8_.refs_9_.refs_18_.refs_19_.refs_20_ = bf16[1024,3200]{1,0:T(8,128)(2,1)} custom-call(s32[7]{0:T(128)} %stack.136.places_ref, bf16[256,3200]{1,0:T(8,128)(2,1)} %copy-done.6, bf16[384,3200]{1,0:T(8,128)(2,1)} %pad_maximum_fusion.2.moved_ref, bf16[384,3200]{1,0:T(8,128)(2,1)} %collective-permute-done.5.other_ref), custom_call_target="tpu_custom_call" | custom-call | tf_op jit(solution)/shard_map/assemble/pallas_call | solution.py:148
  80.2 26.4 %collective-permute-done.6 = bf16[272,1024]{1,0:T(8,128)(2,1)} collective-permute-done((bf16[272,1024]{1,0:T(8,128)(2,1)}, bf16[272,1024]{1,0:T(8,128)(2,1)}, u32[]{:S(2)}, u32[]{:S(2)}) %collective-permute-start.6) | collective-permute-done | bytes 557088 | tf_op jit(solution)/shard_map/ppermute | solution.py:51
  107.8 1.7 pad_maximum_fusion.5.packed_ref.code_ref
  112.4 3.1 fusion.7
  121.9 25.3 %attention.1 = (bf16[1024,1024]{1,0:T(8,128)(2,1)}, bf16[1024,1024]{1,0:T(8,128)(2,1)}, bf16[256,1024]{1,0:T(8,128)(2,1)}, bf16[1024,512]{1,0:T(8,128)(2,1)}, bf...) custom-call(bf16[256,1024]{1,0:T(8,128)(2,1)} %own_ref.1, ...), custom_call_target="tpu_custom_call" | custom-call | tf_op jit(solution)/shard_map/attention/pallas_call | solution.py:572
  149.5 1.7 pad_maximum_fusion.17
  152.7 2.5 collective-permute-start.17
  155.1 4.6 dispatch.4.refs_2_
  159.7 5.6 %collective-permute-done.15 = bf16[256,1024]{1,0:T(8,128)(2,1)} collective-permute-done((bf16[256,1024]{1,0:T(8,128)(2,1)}, bf16[256,1024]{1,0:T(8,128)(2,1)}, u32[]{:S(2)}, u32[]{:S(2)}) %collective-permute-start.15) | collective-permute-done | bytes 524320 | tf_op jit(solution)/shard_map/ppermute | solution.py:51
  165.4 13.3 %collective-permute-done.17 = bf16[256,1024]{1,0:T(8,128)(2,1)} collective-permute-done((bf16[256,1024]{1,0:T(8,128)(2,1)}, bf16[256,1024]{1,0:T(8,128)(2,1)}, u32[]{:S(2)}, u32[]{:S(2)}) %collective-permute-start.17) | collective-permute-done | bytes 524320 | tf_op jit(solution)/shard_map/ppermute | solution.py:51
  178.7 5.0 dispatch.5.refs_3_
  184.0 1.6 collective-permute-start.20
  186.5 2.5 collective-permute-start.16
  189.0 21.0 %collective-permute-done.16 = bf16[256,1024]{1,0:T(8,128)(2,1)S(1)} collective-permute-done((bf16[256,1024]{1,0:T(8,128)(2,1)}, bf16[256,1024]{1,0:T(8,128)(2,1)S(1)}, u32[]{:S(2)}, u32[]{:S(2)}) %collective-permute-start.16) | collective-permute-done | bytes 524320 | tf_op jit(solution)/shard_map/ppermute | solution.py:51
  215.0 2.9 pad_maximum_fusion.12.rest_0_
  218.0 1.7 pad_maximum_fusion.13.rest_0_
  219.7 4.9 dispatch.6
  224.6 4.9 dispatch.7
  229.5 23.5 %experts.2 = (bf16[8,160,1024]{2,1,0:T(8,128)(2,1)}, bf16[8,160,1152]{2,1,0:T(8,128)(2,1)}, bf16[1,1,768,512]{3,2,1,0:T(8,128)(2,1)}, bf16[1,1,768,512]{3,2,1,0:...) custom-call(s32[5]{0:T(128)} %pad_add_fusion.order_ref, ...), custom_call_target="tpu_custom_call" | custom-call | tf_op jit(solution)/shard_map/experts/pallas_call | solution.py:448
  255.4 25.0 %experts.3 = (bf16[8,160,1024]{2,1,0:T(8,128)(2,1)}, bf16[8,160,1152]{2,1,0:T(8,128)(2,1)}, bf16[1,1,768,512]{3,2,1,0:T(8,128)(2,1)}, bf16[1,1,768,512]{3,2,1,0:...) custom-call(s32[5]{0:T(128)} %pad_add_fusion.order_ref, ...), custom_call_target="tpu_custom_call" | custom-call | tf_op jit(solution)/shard_map/experts/pallas_call | solution.py:448
  281.4 5.2 combine.4
  288.2 1.7 pad_maximum_fusion.4
  292.8 5.5 %combine.5.refs_0_ = bf16[4,256,1152]{2,1,0:T(8,128)(2,1)} custom-call(s32[1]{0:T(128)} %bitcast.15.lead_ref, bf16[4,272,1024]{2,1,0:T(8,128)(2,1)} %copy-done, bf16[8,160,1152]{2,1,0:T(8,128)(2,1)} %get-tuple-element.143.rest_0_, bf16[8,160,1152]{2,1,0:T(8,128)(2,1)} %get-tuple-element.144.rest_1_, bf16[4,256,1152]{2,1,0:T(8,128)(2,1)} %copy-done.19), custom_call_target="tpu_custom_call" | custom-call | tf_op jit(solution)/shard_map/combine/pallas_call | solution.py:277
  298.4 2.7 slice_bitcast_fusion.5
  301.7 3.3 collective-permute-start.32
  306.1 4.8 combine.6
  310.9 8.5 %collective-permute-done.31.refs_1_ = bf16[256,1152]{1,0:T(8,128)(2,1)} collective-permute-done((bf16[256,1152]{1,0:T(8,128)(2,1)}, bf16[256,1152]{1,0:T(8,128)(2,1)}, u32[]{:S(2)}, u32[]{:S(2)}) %collective-permute-start.31) | collective-permute-done | bytes 589856 | tf_op jit(solution)/shard_map/ppermute | solution.py:51
  319.5 11.0 %collective-permute-done.32.refs_2_ = bf16[256,1152]{1,0:T(8,128)(2,1)} collective-permute-done((bf16[256,1152]{1,0:T(8,128)(2,1)}, bf16[256,1152]{1,0:T(8,128)(2,1)}, u32[]{:S(2)}, u32[]{:S(2)}) %collective-permute-start.32) | collective-permute-done | bytes 589856 | tf_op jit(solution)/shard_map/ppermute | solution.py:51
  331.9 27.8 %collective-permute-done.34.refs_3_ = bf16[256,1152]{1,0:T(8,128)(2,1)S(1)} collective-permute-done((bf16[256,1152]{1,0:T(8,128)(2,1)S(1)}, bf16[256,1152]{1,0:T(8,128)(2,1)S(1)}, u32[]{:S(2)}, u32[]{:S(2)}) %collective-permute-start.34) | collective-permute-done | bytes 589856 | tf_op jit(solution)/shard_map/ppermute | solution.py:51
  359.7 5.4 combine.7
  365.2 4.4 add_bitcast_fusion.3
  375.2 4.0 collective-permute-start.40
  379.8 36.5 %attention_grad.1 = (bf16[2,4,128,3200]{3,2,1,0:T(8,128)(2,1)}, bf16[1024,1024]{1,0:T(8,128)(2,1)}, f32[256,1024]{1,0:T(8,128)}) custom-call(s32[2]{0:T(128)} %pad_add_fusion.1.here_ref, bf16[4,256,1152]{2,1,0:T(8,128)(2,1)} %combine.5.refs_0_, bf16[256,1152]{1,0:T(8,128)(2,1)} %collective-permute-done.31.refs_1_, ...), custom_call_target="tpu_custom_call" | custom-call | tf_op jit(solution)/shard_map/attention_grad/pallas_call | solution.py:767
  416.4 2.4 slice_bitcast_fusion
  418.9 1.8 slice_bitcast_fusion.17
  427.7 6.9 %collective-permute-done.42 = bf16[2,128,1024]{2,1,0:T(8,128)(2,1)S(1)} collective-permute-done((bf16[2,128,1024]{2,1,0:T(8,128)(2,1)S(1)}, bf16[2,128,1024]{2,1,0:T(8,128)(2,1)S(1)}, u32[]{:S(2)}, u32[]{:S(2)}) %collective-permute-start.42) | collective-permute-done | bytes 524320 | tf_op jit(solution)/shard_map/ppermute | solution.py:91
  439.6 2.9 add_bitcast_fusion.1
  443.5 12.4 %collective-permute-done.47 = bf16[2,64,3200]{2,1,0:T(8,128)(2,1)} collective-permute-done((bf16[2,64,3200]{2,1,0:T(8,128)(2,1)}, bf16[2,64,3200]{2,1,0:T(8,128)(2,1)}, u32[]{:S(2)}, u32[]{:S(2)}) %collective-permute-start.47) | collective-permute-done | bytes 819232 | tf_op jit(solution)/shard_map/ppermute | solution.py:91
  461.6 2.8 fusion.22
  464.4 3.3 collective-permute-done.49
  469.8 12.6 %collective-permute-done.41 = bf16[256,1024]{1,0:T(8,128)(2,1)S(1)} collective-permute-done((bf16[256,1024]{1,0:T(8,128)(2,1)S(1)}, bf16[256,1024]{1,0:T(8,128)(2,1)S(1)}, u32[]{:S(2)}, u32[]{:S(2)}) %collective-permute-start.41) | collective-permute-done | bytes 524320 | tf_op jit(solution)/shard_map/ppermute | solution.py:51
  482.8 2.9 collective-permute-start.52
  490.4 2.3 collective-permute-done.51
  492.7 7.8 %collective-permute-done.52 = bf16[32,3200]{1,0:T(8,128)(2,1)S(1)} collective-permute-done((bf16[32,3200]{1,0:T(8,128)(2,1)S(1)}, bf16[32,3200]{1,0:T(8,128)(2,1)S(1)}, u32[]{:S(2)}, u32[]{:S(2)}) %collective-permute-start.52) | collective-permute-done | bytes 204832 | tf_op jit(solution)/shard_map/ppermute | solution.py:51
  500.6 2.9 collective-permute-start.54
  503.6 2.6 collective-permute-start.55
  506.2 2.4 fusion.6
  509.2 14.3 %collective-permute-done.55 = bf16[32,3200]{1,0:T(8,128)(2,1)S(1)} collective-permute-done((bf16[32,3200]{1,0:T(8,128)(2,1)S(1)}, bf16[32,3200]{1,0:T(8,128)(2,1)S(1)}, u32[]{:S(2)}, u32[]{:S(2)}) %collective-permute-start.55) | collective-permute-done | bytes 204832 | tf_op jit(solution)/shard_map/ppermute | solution.py:51
  531.5 2.0 copy.57
  533.5 1.8 pad_maximum_fusion.25
  535.3 2.0 copy.56
  538.8 2.6 copy.55
  (283 shorter events, 90.2 us)
Async XLA Ops:
  8.8 36.2 %copy-start.20 = (bf16[256,1024]{1,0:T(8,128)(2,1)S(1)}, bf16[256,1024]{1,0:T(8,128)(2,1)}, u32[]{:S(2)}) copy-start(bf16[256,1024]{1,0:T(8,128)(2,1)} %refs_4_.1) | copy-start | bytes 1572868
  8.8 32.7 %collective-permute-start = (bf16[128,5248]{1,0:T(8,128)(2,1)}, bf16[128,5248]{1,0:T(8,128)(2,1)S(1)}, u32[]{:S(2)}, u32[]{:S(2)}) collective-permute-start(bf16[128,5248]{1,0:T(8,128)(2,1)} %pad_maximum_fusion.16), channel_id=1, source_target_pairs={{0,1},{1,0},{2,3},{3,2},{4,5},{5,4},{6,7},{7,6},{8,9},{9,8},{10,11... | collective-permute-start | bytes 4030472 | tf_op jit(solution)/shard_map/ppermute | solution.py:59
  11.8 31.6 %collective-permute-start.1 = (bf16[128,5248]{1,0:T(8,128)(2,1)}, bf16[128,5248]{1,0:T(8,128)(2,1)S(1)}, u32[]{:S(2)}, u32[]{:S(2)}) collective-permute-start(bf16[128,5248]{1,0:T(8,128)(2,1)} %pad_maximum_fusion.16), channel_id=1, source_target_pairs={{0,2},{2,0},{1,3},{3,1},{4,6},{6,4},{5,7},{7,5},{8,10},{10,8},{9,1... | collective-permute-start | bytes 4030472 | tf_op jit(solution)/shard_map/ppermute | solution.py:59
  41.5 16.3 %collective-permute-start.2 = (bf16[64,5248]{1,0:T(8,128)(2,1)S(1)}, bf16[64,5248]{1,0:T(8,128)(2,1)S(1)}, u32[]{:S(2)}, u32[]{:S(2)}) collective-permute-start(bf16[64,5248]{1,0:T(8,128)(2,1)S(1)} %slice.394), channel_id=1, source_target_pairs={{0,2},{2,0},{1,3},{3,1},{4,6},{6,4},{5,7},{7,5},{8,10},{10,8},{9,1... | collective-permute-start | bytes 2015240 | tf_op jit(solution)/shard_map/ppermute | solution.py:65
  43.4 15.8 %collective-permute-start.3 = (bf16[64,5248]{1,0:T(8,128)(2,1)S(1)}, bf16[64,5248]{1,0:T(8,128)(2,1)S(1)}, u32[]{:S(2)}, u32[]{:S(2)}) collective-permute-start(bf16[64,5248]{1,0:T(8,128)(2,1)S(1)} %slice.395), channel_id=1, source_target_pairs={{0,1},{1,0},{2,3},{3,2},{4,5},{5,4},{6,7},{7,6},{8,9},{9,8},{10,11... | collective-permute-start | bytes 2015240 | tf_op jit(solution)/shard_map/ppermute | solution.py:65
  46.0 15.8 %collective-permute-start.4 = (bf16[272,1024]{1,0:T(8,128)(2,1)}, bf16[272,1024]{1,0:T(8,128)(2,1)S(1)}, u32[]{:S(2)}, u32[]{:S(2)}) collective-permute-start(bf16[272,1024]{1,0:T(8,128)(2,1)} %maximum_maximum_fusion), channel_id=1, source_target_pairs={{0,24},{8,0},{16,8},{24,16},{1,25},{9,1},{17,9},{25,17},{2,26},{10... | collective-permute-start | bytes 1671176 | tf_op jit(solution)/shard_map/ppermute | solution.py:51
  61.8 11.5 %collective-permute-start.5 = (bf16[384,3200]{1,0:T(8,128)(2,1)}, bf16[384,3200]{1,0:T(8,128)(2,1)}, u32[]{:S(2)}, u32[]{:S(2)}) collective-permute-start(bf16[384,3200]{1,0:T(8,128)(2,1)} %pad_maximum_fusion.2.moved_ref), channel_id=1, source_target_pairs={{0,4},{4,0},{1,5},{5,1},{2,6},{6,2},{3,7},{7,3},{8,12},{12,8},{9,1... | collective-permute-start | bytes 7372808 | tf_op jit(solution)/shard_map/ppermute | solution.py:47
  66.0 40.6 %collective-permute-start.8 = (bf16[768,512]{1,0:T(8,128)(2,1)S(1)}, bf16[768,512]{1,0:T(8,128)(2,1)S(1)}, u32[]{:S(2)}, u32[]{:S(2)}) collective-permute-start(bf16[768,512]{1,0:T(8,128)(2,1)S(1)} %get-tuple-element.107), channel_id=1, source_target_pairs={{0,1},{1,0},{2,3},{3,2},{4,5},{5,4},{6,7},{7,6},{8,9},{9,8},{10,11... | collective-permute-start | bytes 2359304 | tf_op jit(solution)/shard_map/ppermute | solution.py:59
  67.5 39.1 %collective-permute-start.9 = (bf16[768,512]{1,0:T(8,128)(2,1)S(1)}, bf16[768,512]{1,0:T(8,128)(2,1)S(1)}, u32[]{:S(2)}, u32[]{:S(2)}) collective-permute-start(bf16[768,512]{1,0:T(8,128)(2,1)S(1)} %get-tuple-element.107), channel_id=1, source_target_pairs={{0,2},{2,0},{1,3},{3,1},{4,6},{6,4},{5,7},{7,5},{8,10},{10,8},{9,1... | collective-permute-start | bytes 2359304 | tf_op jit(solution)/shard_map/ppermute | solution.py:59
  68.6 38.0 %collective-permute-start.6 = (bf16[272,1024]{1,0:T(8,128)(2,1)}, bf16[272,1024]{1,0:T(8,128)(2,1)}, u32[]{:S(2)}, u32[]{:S(2)}) collective-permute-start(bf16[272,1024]{1,0:T(8,128)(2,1)} %maximum_maximum_fusion), channel_id=1, source_target_pairs={{0,16},{8,24},{16,0},{24,8},{1,17},{9,25},{17,1},{25,9},{2,18},{10... | collective-permute-start | bytes 1671176 | tf_op jit(solution)/shard_map/ppermute | solution.py:51
  71.2 35.5 %collective-permute-start.7 = (bf16[272,1024]{1,0:T(8,128)(2,1)}, bf16[272,1024]{1,0:T(8,128)(2,1)}, u32[]{:S(2)}, u32[]{:S(2)}) collective-permute-start(bf16[272,1024]{1,0:T(8,128)(2,1)} %maximum_maximum_fusion), channel_id=1, source_target_pairs={{0,8},{8,16},{16,24},{24,0},{1,9},{9,17},{17,25},{25,1},{2,10},{10... | collective-permute-start | bytes 1671176 | tf_op jit(solution)/shard_map/ppermute | solution.py:51
  73.4 34.4 %copy-start.39 = (bf16[272,1024]{1,0:T(8,128)(2,1)S(1)}, bf16[272,1024]{1,0:T(8,128)(2,1)}, u32[]{:S(2)}) copy-start(bf16[272,1024]{1,0:T(8,128)(2,1)} %copy-done.38) | copy-start | bytes 1671172
  109.4 37.9 %copy-start = (bf16[4,272,1024]{2,1,0:T(8,128)(2,1)}, bf16[4,272,1024]{2,1,0:T(8,128)(2,1)S(1)}, u32[]{:S(2)}) copy-start(bf16[4,272,1024]{2,1,0:T(8,128)(2,1)S(1)} %pad_maximum_fusion.5.packed_ref.code_ref) | copy-start | bytes 6684676
  109.4 37.9 %collective-permute-start.10 = (bf16[4,272,1024]{2,1,0:T(8,128)(2,1)S(1)}, bf16[4,272,1024]{2,1,0:T(8,128)(2,1)}, u32[]{:S(2)}, u32[]{:S(2)}) collective-permute-start(bf16[4,272,1024]{2,1,0:T(8,128)(2,1)S(1)} %pad_maximum_fusion.5.packed_ref.code_ref), channel_id=1, source_target_pairs={{0,4},{4,0},{1,5},{5,1},{2,6},{6,2},{3,7},{7,3},{8,12},{12,8},{9,1... | collective-permute-start | bytes 6684680 | tf_op jit(solution)/shard_map/ppermute | solution.py:47
  110.8 36.6 %collective-permute-start.11 = (bf16[768,512]{1,0:T(8,128)(2,1)}, bf16[768,512]{1,0:T(8,128)(2,1)}, u32[]{:S(2)}, u32[]{:S(2)}) collective-permute-start(bf16[768,512]{1,0:T(8,128)(2,1)} %get-tuple-element.115), channel_id=1, source_target_pairs={{0,1},{1,0},{2,3},{3,2},{4,5},{5,4},{6,7},{7,6},{8,9},{9,8},{10,11... | collective-permute-start | bytes 2359304 | tf_op jit(solution)/shard_map/ppermute | solution.py:59
  111.4 35.9 %collective-permute-start.12 = (bf16[768,512]{1,0:T(8,128)(2,1)}, bf16[768,512]{1,0:T(8,128)(2,1)}, u32[]{:S(2)}, u32[]{:S(2)}) collective-permute-start(bf16[768,512]{1,0:T(8,128)(2,1)} %get-tuple-element.115), channel_id=1, source_target_pairs={{0,2},{2,0},{1,3},{3,1},{4,6},{6,4},{5,7},{7,5},{8,10},{10,8},{9,1... | collective-permute-start | bytes 2359304 | tf_op jit(solution)/shard_map/ppermute | solution.py:59
  116.5 30.8 %collective-permute-start.13 = (bf16[384,512]{1,0:T(8,128)(2,1)S(1)}, bf16[384,512]{1,0:T(8,128)(2,1)}, u32[]{:S(2)}, u32[]{:S(2)}) collective-permute-start(bf16[384,512]{1,0:T(8,128)(2,1)S(1)} %slice.322), channel_id=1, source_target_pairs={{0,2},{2,0},{1,3},{3,1},{4,6},{6,4},{5,7},{7,5},{8,10},{10,8},{9,1... | collective-permute-start | bytes 1179656 | tf_op jit(solution)/shard_map/ppermute | solution.py:65
  118.4 28.9 %collective-permute-start.14 = (bf16[384,512]{1,0:T(8,128)(2,1)}, bf16[384,512]{1,0:T(8,128)(2,1)}, u32[]{:S(2)}, u32[]{:S(2)}) collective-permute-start(bf16[384,512]{1,0:T(8,128)(2,1)} %slice.323), channel_id=1, source_target_pairs={{0,1},{1,0},{2,3},{3,2},{4,5},{5,4},{6,7},{7,6},{8,9},{9,8},{10,11... | collective-permute-start | bytes 1179656 | tf_op jit(solution)/shard_map/ppermute | solution.py:65
  151.1 27.5 %collective-permute-start.18 = (bf16[1152,512]{1,0:T(8,128)(2,1)}, bf16[1152,512]{1,0:T(8,128)(2,1)S(1)}, u32[]{:S(2)}, u32[]{:S(2)}) collective-permute-start(bf16[1152,512]{1,0:T(8,128)(2,1)} %get-tuple-element.292), channel_id=1, source_target_pairs={{0,1},{1,0},{2,3},{3,2},{4,5},{5,4},{6,7},{7,6},{8,9},{9,8},{10,11... | collective-permute-start | bytes 3538952 | tf_op jit(solution)/shard_map/ppermute | solution.py:74
  151.7 26.9 %collective-permute-start.19 = (bf16[1152,512]{1,0:T(8,128)(2,1)}, bf16[1152,512]{1,0:T(8,128)(2,1)S(1)}, u32[]{:S(2)}, u32[]{:S(2)}) collective-permute-start(bf16[1152,512]{1,0:T(8,128)(2,1)} %get-tuple-element.291), channel_id=1, source_target_pairs={{0,2},{2,0},{1,3},{3,1},{4,6},{6,4},{5,7},{7,5},{8,10},{10,8},{9,1... | collective-permute-start | bytes 3538952 | tf_op jit(solution)/shard_map/ppermute | solution.py:74
  152.7 12.7 %collective-permute-start.15 = (bf16[256,1024]{1,0:T(8,128)(2,1)}, bf16[256,1024]{1,0:T(8,128)(2,1)}, u32[]{:S(2)}, u32[]{:S(2)}) collective-permute-start(bf16[256,1024]{1,0:T(8,128)(2,1)} %get-tuple-element.123.refs_11_), channel_id=1, source_target_pairs={{0,24},{8,0},{16,8},{24,16},{1,25},{9,1},{17,9},{25,17},{2,26},{10... | collective-permute-start | bytes 1572872 | tf_op jit(solution)/shard_map/ppermute | solution.py:51
  152.7 26.0 %collective-permute-start.17 = (bf16[256,1024]{1,0:T(8,128)(2,1)}, bf16[256,1024]{1,0:T(8,128)(2,1)}, u32[]{:S(2)}, u32[]{:S(2)}) collective-permute-start(bf16[256,1024]{1,0:T(8,128)(2,1)} %get-tuple-element.123.refs_11_), channel_id=1, source_target_pairs={{0,8},{8,16},{16,24},{24,0},{1,9},{9,17},{17,25},{25,1},{2,10},{10... | collective-permute-start | bytes 1572872 | tf_op jit(solution)/shard_map/ppermute | solution.py:51
  184.0 26.5 %collective-permute-start.20 = (bf16[1152,512]{1,0:T(8,128)(2,1)S(1)}, bf16[1152,512]{1,0:T(8,128)(2,1)S(1)}, u32[]{:S(2)}, u32[]{:S(2)}) collective-permute-start(bf16[1152,512]{1,0:T(8,128)(2,1)S(1)} %get-tuple-element.290), channel_id=1, source_target_pairs={{0,1},{1,0},{2,3},{3,2},{4,5},{5,4},{6,7},{7,6},{8,9},{9,8},{10,11... | collective-permute-start | bytes 3538952 | tf_op jit(solution)/shard_map/ppermute | solution.py:74
  185.5 25.5 %collective-permute-start.21 = (bf16[1152,512]{1,0:T(8,128)(2,1)S(1)}, bf16[1152,512]{1,0:T(8,128)(2,1)S(1)}, u32[]{:S(2)}, u32[]{:S(2)}) collective-permute-start(bf16[1152,512]{1,0:T(8,128)(2,1)S(1)} %get-tuple-element.289), channel_id=1, source_target_pairs={{0,2},{2,0},{1,3},{3,1},{4,6},{6,4},{5,7},{7,5},{8,10},{10,8},{9,1... | collective-permute-start | bytes 3538952 | tf_op jit(solution)/shard_map/ppermute | solution.py:74
  186.5 23.4 %collective-permute-start.16 = (bf16[256,1024]{1,0:T(8,128)(2,1)}, bf16[256,1024]{1,0:T(8,128)(2,1)S(1)}, u32[]{:S(2)}, u32[]{:S(2)}) collective-permute-start(bf16[256,1024]{1,0:T(8,128)(2,1)} %get-tuple-element.123.refs_11_), channel_id=1, source_target_pairs={{0,16},{8,24},{16,0},{24,8},{1,17},{9,25},{17,1},{25,9},{2,18},{10... | collective-permute-start | bytes 1572872 | tf_op jit(solution)/shard_map/ppermute | solution.py:51
  210.0 2.2 collective-permute-start.22
  210.0 8.0 %collective-permute-start.23 = (bf16[256,1024]{1,0:T(8,128)(2,1)}, bf16[256,1024]{1,0:T(8,128)(2,1)S(1)}, u32[]{:S(2)}, u32[]{:S(2)}) collective-permute-start(bf16[256,1024]{1,0:T(8,128)(2,1)} %collective-permute-done.15), channel_id=1, source_target_pairs={{0,4},{4,0},{1,5},{5,1},{2,6},{6,2},{3,7},{7,3},{8,12},{12,8},{9,1... | collective-permute-start | bytes 1572872 | tf_op jit(solution)/shard_map/ppermute | solution.py:47
  210.5 7.5 %collective-permute-start.24 = (bf16[256,1024]{1,0:T(8,128)(2,1)S(1)}, bf16[256,1024]{1,0:T(8,128)(2,1)S(1)}, u32[]{:S(2)}, u32[]{:S(2)}) collective-permute-start(bf16[256,1024]{1,0:T(8,128)(2,1)S(1)} %collective-permute-done.16), channel_id=1, source_target_pairs={{0,4},{4,0},{1,5},{5,1},{2,6},{6,2},{3,7},{7,3},{8,12},{12,8},{9,1... | collective-permute-start | bytes 1572872 | tf_op jit(solution)/shard_map/ppermute | solution.py:47
  210.5 7.5 %collective-permute-start.25 = (bf16[256,1024]{1,0:T(8,128)(2,1)}, bf16[256,1024]{1,0:T(8,128)(2,1)S(1)}, u32[]{:S(2)}, u32[]{:S(2)}) collective-permute-start(bf16[256,1024]{1,0:T(8,128)(2,1)} %collective-permute-done.17), channel_id=1, source_target_pairs={{0,4},{4,0},{1,5},{5,1},{2,6},{6,2},{3,7},{7,3},{8,12},{12,8},{9,1... | collective-permute-start | bytes 1572872 | tf_op jit(solution)/shard_map/ppermute | solution.py:47
  211.1 18.4 %collective-permute-start.26 = (bf16[384,512]{1,0:T(8,128)(2,1)S(1)}, bf16[384,512]{1,0:T(8,128)(2,1)S(1)}, u32[]{:S(2)}, u32[]{:S(2)}) collective-permute-start(bf16[384,512]{1,0:T(8,128)(2,1)S(1)} %slice.409), channel_id=1, source_target_pairs={{0,2},{2,0},{1,3},{3,1},{4,6},{6,4},{5,7},{7,5},{8,10},{10,8},{9,1... | collective-permute-start | bytes 1179656 | tf_op jit(solution)/shard_map/ppermute | solution.py:65
  212.2 17.3 %collective-permute-start.27 = (bf16[384,512]{1,0:T(8,128)(2,1)S(1)}, bf16[384,512]{1,0:T(8,128)(2,1)S(1)}, u32[]{:S(2)}, u32[]{:S(2)}) collective-permute-start(bf16[384,512]{1,0:T(8,128)(2,1)S(1)} %slice.410), channel_id=1, source_target_pairs={{0,1},{1,0},{2,3},{3,2},{4,5},{5,4},{6,7},{7,6},{8,9},{9,8},{10,11... | collective-permute-start | bytes 1179656 | tf_op jit(solution)/shard_map/ppermute | solution.py:65
  229.5 23.5 %copy-start.47 = (bf16[384,512]{1,0:T(8,128)(2,1)}, bf16[384,512]{1,0:T(8,128)(2,1)S(1)}, u32[]{:S(2)}) copy-start(bf16[384,512]{1,0:T(8,128)(2,1)S(1)} %collective-permute-done.26.refs_13_) | copy-start | bytes 1179652
  253.0 27.5 %collective-permute-start.28 = (bf16[1,1,768,512]{3,2,1,0:T(8,128)(2,1)}, bf16[1,1,768,512]{3,2,1,0:T(8,128)(2,1)S(1)}, u32[]{:S(2)}, u32[]{:S(2)}) collective-permute-start(bf16[1,1,768,512]{3,2,1,0:T(8,128)(2,1)} %get-tuple-element.141), channel_id=1, source_target_pairs={{0,1},{1,0},{2,3},{3,2},{4,5},{5,4},{6,7},{7,6},{8,9},{9,8},{10,11... | collective-permute-start | bytes 2359304 | tf_op jit(solution)/shard_map/ppermute | solution.py:74
  254.4 26.1 %collective-permute-start.29 = (bf16[1,1,768,512]{3,2,1,0:T(8,128)(2,1)}, bf16[1,1,768,512]{3,2,1,0:T(8,128)(2,1)S(1)}, u32[]{:S(2)}, u32[]{:S(2)}) collective-permute-start(bf16[1,1,768,512]{3,2,1,0:T(8,128)(2,1)} %get-tuple-element.142), channel_id=1, source_target_pairs={{0,2},{2,0},{1,3},{3,1},{4,6},{6,4},{5,7},{7,5},{8,10},{10,8},{9,1... | collective-permute-start | bytes 2359304 | tf_op jit(solution)/shard_map/ppermute | solution.py:74
  286.6 4.7 collective-permute-start.30
  290.0 75.2 %collective-permute-start.36 = (bf16[3,1,768,512]{3,2,1,0:T(8,128)(2,1)}, bf16[3,1,768,512]{3,2,1,0:T(8,128)(2,1)}, u32[]{:S(2)}, u32[]{:S(2)}) collective-permute-start(bf16[3,1,768,512]{3,2,1,0:T(8,128)(2,1)} %pad_maximum_fusion.4), channel_id=1, source_target_pairs={{0,2},{2,0},{1,3},{3,1},{4,6},{6,4},{5,7},{7,5},{8,10},{10,8},{9,1... | collective-permute-start | bytes 7077896 | tf_op jit(solution)/shard_map/ppermute | solution.py:74
  301.1 18.4 %collective-permute-start.31 = (bf16[256,1152]{1,0:T(8,128)(2,1)}, bf16[256,1152]{1,0:T(8,128)(2,1)}, u32[]{:S(2)}, u32[]{:S(2)}) collective-permute-start(bf16[256,1152]{1,0:T(8,128)(2,1)} %get-tuple-element.260), channel_id=1, source_target_pairs={{0,8},{8,16},{16,24},{24,0},{1,9},{9,17},{17,25},{25,1},{2,10},{10... | collective-permute-start | bytes 1769480 | tf_op jit(solution)/shard_map/ppermute | solution.py:51
  301.7 28.8 %collective-permute-start.32 = (bf16[256,1152]{1,0:T(8,128)(2,1)}, bf16[256,1152]{1,0:T(8,128)(2,1)}, u32[]{:S(2)}, u32[]{:S(2)}) collective-permute-start(bf16[256,1152]{1,0:T(8,128)(2,1)} %get-tuple-element.259), channel_id=1, source_target_pairs={{0,24},{8,0},{16,8},{24,16},{1,25},{9,1},{17,9},{25,17},{2,26},{10... | collective-permute-start | bytes 1769480 | tf_op jit(solution)/shard_map/ppermute | solution.py:51
  305.5 59.7 %collective-permute-start.35 = (bf16[3,1,768,512]{3,2,1,0:T(8,128)(2,1)S(1)}, bf16[3,1,768,512]{3,2,1,0:T(8,128)(2,1)}, u32[]{:S(2)}, u32[]{:S(2)}) collective-permute-start(bf16[3,1,768,512]{3,2,1,0:T(8,128)(2,1)S(1)} %pad_maximum_fusion.3), channel_id=1, source_target_pairs={{0,1},{1,0},{2,3},{3,2},{4,5},{5,4},{6,7},{7,6},{8,9},{9,8},{10,11... | collective-permute-start | bytes 7077896 | tf_op jit(solution)/shard_map/ppermute | solution.py:74
  330.5 29.3 %collective-permute-start.33 = (bf16[4,256,1024]{2,1,0:T(8,128)(2,1)}, bf16[4,256,1024]{2,1,0:T(8,128)(2,1)}, u32[]{:S(2)}, u32[]{:S(2)}) collective-permute-start(bf16[4,256,1024]{2,1,0:T(8,128)(2,1)} %combine.6), channel_id=1, source_target_pairs={{0,4},{4,0},{1,5},{5,1},{2,6},{6,2},{3,7},{7,3},{8,12},{12,8},{9,1... | collective-permute-start | bytes 6291464 | tf_op jit(solution)/shard_map/ppermute | solution.py:47
  330.5 29.3 %collective-permute-start.34 = (bf16[256,1152]{1,0:T(8,128)(2,1)S(1)}, bf16[256,1152]{1,0:T(8,128)(2,1)S(1)}, u32[]{:S(2)}, u32[]{:S(2)}) collective-permute-start(bf16[256,1152]{1,0:T(8,128)(2,1)S(1)} %get-tuple-element.150), channel_id=1, source_target_pairs={{0,16},{8,24},{16,0},{24,8},{1,17},{9,25},{17,1},{25,9},{2,18},{10... | collective-permute-start | bytes 1769480 | tf_op jit(solution)/shard_map/ppermute | solution.py:51
  371.0 45.4 %collective-permute-start.38 = (bf16[2,1,768,512]{3,2,1,0:T(8,128)(2,1)}, bf16[2,1,768,512]{3,2,1,0:T(8,128)(2,1)}, u32[]{:S(2)}, u32[]{:S(2)}) collective-permute-start(bf16[2,1,768,512]{3,2,1,0:T(8,128)(2,1)} %pad_maximum_fusion.15), channel_id=1, source_target_pairs={{0,2},{2,0},{1,3},{3,1},{4,6},{6,4},{5,7},{7,5},{8,10},{10,8},{9,1... | collective-permute-start | bytes 4718600 | tf_op jit(solution)/shard_map/ppermute | solution.py:74
  373.3 43.1 %collective-permute-start.37 = (bf16[2,1,768,512]{3,2,1,0:T(8,128)(2,1)}, bf16[2,1,768,512]{3,2,1,0:T(8,128)(2,1)}, u32[]{:S(2)}, u32[]{:S(2)}) collective-permute-start(bf16[2,1,768,512]{3,2,1,0:T(8,128)(2,1)} %pad_maximum_fusion.14), channel_id=1, source_target_pairs={{0,1},{1,0},{2,3},{3,2},{4,5},{5,4},{6,7},{7,6},{8,9},{9,8},{10,11... | collective-permute-start | bytes 4718600 | tf_op jit(solution)/shard_map/ppermute | solution.py:74
  375.2 41.2 %collective-permute-start.39 = (bf16[256,1024]{1,0:T(8,128)(2,1)}, bf16[256,1024]{1,0:T(8,128)(2,1)S(1)}, u32[]{:S(2)}, u32[]{:S(2)}) collective-permute-start(bf16[256,1024]{1,0:T(8,128)(2,1)} %get-tuple-element.271), channel_id=1, source_target_pairs={{0,8},{8,16},{16,24},{24,0},{1,9},{9,17},{17,25},{25,1},{2,10},{10... | collective-permute-start | bytes 1572872 | tf_op jit(solution)/shard_map/ppermute | solution.py:51
  375.2 41.2 %collective-permute-start.40 = (bf16[256,1024]{1,0:T(8,128)(2,1)}, bf16[256,1024]{1,0:T(8,128)(2,1)}, u32[]{:S(2)}, u32[]{:S(2)}) collective-permute-start(bf16[256,1024]{1,0:T(8,128)(2,1)} %get-tuple-element.269), channel_id=1, source_target_pairs={{0,24},{8,0},{16,8},{24,16},{1,25},{9,1},{17,9},{25,17},{2,26},{10... | collective-permute-start | bytes 1572872 | tf_op jit(solution)/shard_map/ppermute | solution.py:51
  418.8 5.9 %collective-permute-start.46 = (bf16[4,128,3200]{2,1,0:T(8,128)(2,1)S(1)}, bf16[4,128,3200]{2,1,0:T(8,128)(2,1)S(1)}, u32[]{:S(2)}, u32[]{:S(2)}) collective-permute-start(bf16[4,128,3200]{2,1,0:T(8,128)(2,1)S(1)} %slice_bitcast_fusion), channel_id=1, source_target_pairs={{0,4},{4,0},{1,5},{5,1},{2,6},{6,2},{3,7},{7,3},{8,12},{12,8},{9,1... | collective-permute-start | bytes 9830408 | tf_op jit(solution)/shard_map/ppermute | solution.py:47
  420.7 13.9 %collective-permute-start.42 = (bf16[2,128,1024]{2,1,0:T(8,128)(2,1)S(1)}, bf16[2,128,1024]{2,1,0:T(8,128)(2,1)S(1)}, u32[]{:S(2)}, u32[]{:S(2)}) collective-permute-start(bf16[2,128,1024]{2,1,0:T(8,128)(2,1)S(1)} %pad_maximum_fusion.23), channel_id=1, source_target_pairs={{0,1},{1,0},{2,3},{3,2},{4,5},{5,4},{6,7},{7,6},{8,9},{9,8},{10,11... | collective-permute-start | bytes 1572872 | tf_op jit(solution)/shard_map/ppermute | solution.py:91
  422.2 13.6 %collective-permute-start.44 = (bf16[2,128,1024]{2,1,0:T(8,128)(2,1)S(1)}, bf16[2,128,1024]{2,1,0:T(8,128)(2,1)S(1)}, u32[]{:S(2)}, u32[]{:S(2)}) collective-permute-start(bf16[2,128,1024]{2,1,0:T(8,128)(2,1)S(1)} %pad_maximum_fusion.24), channel_id=1, source_target_pairs={{0,2},{2,0},{1,3},{3,1},{4,6},{6,4},{5,7},{7,5},{8,10},{10,8},{9,1... | collective-permute-start | bytes 1572872 | tf_op jit(solution)/shard_map/ppermute | solution.py:91
  436.6 19.3 %collective-permute-start.47 = (bf16[2,64,3200]{2,1,0:T(8,128)(2,1)}, bf16[2,64,3200]{2,1,0:T(8,128)(2,1)}, u32[]{:S(2)}, u32[]{:S(2)}) collective-permute-start(bf16[2,64,3200]{2,1,0:T(8,128)(2,1)} %pad_maximum_fusion.21), channel_id=1, source_target_pairs={{0,1},{1,0},{2,3},{3,2},{4,5},{5,4},{6,7},{7,6},{8,9},{9,8},{10,11... | collective-permute-start | bytes 2457608 | tf_op jit(solution)/shard_map/ppermute | solution.py:91
  437.6 19.3 %collective-permute-start.48 = (bf16[2,64,3200]{2,1,0:T(8,128)(2,1)}, bf16[2,64,3200]{2,1,0:T(8,128)(2,1)}, u32[]{:S(2)}, u32[]{:S(2)}) collective-permute-start(bf16[2,64,3200]{2,1,0:T(8,128)(2,1)} %stack.170), channel_id=1, source_target_pairs={{0,2},{2,0},{1,3},{3,1},{4,6},{6,4},{5,7},{7,5},{8,10},{10,8},{9,1... | collective-permute-start | bytes 2457608 | tf_op jit(solution)/shard_map/ppermute | solution.py:91
  458.2 9.4 %collective-permute-start.49 = (bf16[64,3200]{1,0:T(8,128)(2,1)S(1)}, bf16[64,3200]{1,0:T(8,128)(2,1)S(1)}, u32[]{:S(2)}, u32[]{:S(2)}) collective-permute-start(bf16[64,3200]{1,0:T(8,128)(2,1)S(1)} %get-tuple-element.247), channel_id=1, source_target_pairs={{0,2},{2,0},{1,3},{3,1},{4,6},{6,4},{5,7},{7,5},{8,10},{10,8},{9,1... | collective-permute-start | bytes 1228808 | tf_op jit(solution)/shard_map/ppermute | solution.py:98
  459.3 9.1 %collective-permute-start.50 = (bf16[64,3200]{1,0:T(8,128)(2,1)S(1)}, bf16[64,3200]{1,0:T(8,128)(2,1)S(1)}, u32[]{:S(2)}, u32[]{:S(2)}) collective-permute-start(bf16[64,3200]{1,0:T(8,128)(2,1)S(1)} %get-tuple-element.246), channel_id=1, source_target_pairs={{0,1},{1,0},{2,3},{3,2},{4,5},{5,4},{6,7},{7,6},{8,9},{9,8},{10,11... | collective-permute-start | bytes 1228808 | tf_op jit(solution)/shard_map/ppermute | solution.py:99
  461.6 20.8 %collective-permute-start.41 = (bf16[256,1024]{1,0:T(8,128)(2,1)S(1)}, bf16[256,1024]{1,0:T(8,128)(2,1)S(1)}, u32[]{:S(2)}, u32[]{:S(2)}) collective-permute-start(bf16[256,1024]{1,0:T(8,128)(2,1)S(1)} %copy-done.46), channel_id=1, source_target_pairs={{0,16},{8,24},{16,0},{24,8},{1,17},{9,25},{17,1},{25,9},{2,18},{10... | collective-permute-start | bytes 1572872 | tf_op jit(solution)/shard_map/ppermute | solution.py:51
  482.7 23.5 %copy-start.16 = (f32[256,1024]{1,0:T(8,128)S(1)}, f32[256,1024]{1,0:T(8,128)}, u32[]{:S(2)}) copy-start(f32[256,1024]{1,0:T(8,128)} %get-tuple-element.113.refs_5_) | copy-start | bytes 3145732
  482.7 23.5 %copy-start.41 = (bf16[256,1024]{1,0:T(8,128)(2,1)S(1)}, bf16[256,1024]{1,0:T(8,128)(2,1)}, u32[]{:S(2)}) copy-start(bf16[256,1024]{1,0:T(8,128)(2,1)} %copy-done.40) | copy-start | bytes 1572868
  482.8 9.9 %collective-permute-start.51 = (bf16[32,3200]{1,0:T(8,128)(2,1)S(1)}, bf16[32,3200]{1,0:T(8,128)(2,1)S(1)}, u32[]{:S(2)}, u32[]{:S(2)}) collective-permute-start(bf16[32,3200]{1,0:T(8,128)(2,1)S(1)} %get-tuple-element.286), channel_id=1, source_target_pairs={{0,8},{8,16},{16,24},{24,0},{1,9},{9,17},{17,25},{25,1},{2,10},{10... | collective-permute-start | bytes 614408 | tf_op jit(solution)/shard_map/ppermute | solution.py:51
  482.8 17.7 %collective-permute-start.52 = (bf16[32,3200]{1,0:T(8,128)(2,1)S(1)}, bf16[32,3200]{1,0:T(8,128)(2,1)S(1)}, u32[]{:S(2)}, u32[]{:S(2)}) collective-permute-start(bf16[32,3200]{1,0:T(8,128)(2,1)S(1)} %get-tuple-element.288), channel_id=1, source_target_pairs={{0,16},{8,24},{16,0},{24,8},{1,17},{9,25},{17,1},{25,9},{2,18},{10... | collective-permute-start | bytes 614408 | tf_op jit(solution)/shard_map/ppermute | solution.py:51
  485.8 14.8 %collective-permute-start.53 = (bf16[32,3200]{1,0:T(8,128)(2,1)S(1)}, bf16[32,3200]{1,0:T(8,128)(2,1)S(1)}, u32[]{:S(2)}, u32[]{:S(2)}) collective-permute-start(bf16[32,3200]{1,0:T(8,128)(2,1)S(1)} %get-tuple-element.287), channel_id=1, source_target_pairs={{0,24},{8,0},{16,8},{24,16},{1,25},{9,1},{17,9},{25,17},{2,26},{10... | collective-permute-start | bytes 614408 | tf_op jit(solution)/shard_map/ppermute | solution.py:51
  487.9 20.8 %collective-permute-start.43 = (bf16[128,1024]{1,0:T(8,128)(2,1)S(1)}, bf16[128,1024]{1,0:T(8,128)(2,1)S(1)}, u32[]{:S(2)}, u32[]{:S(2)}) collective-permute-start(bf16[128,1024]{1,0:T(8,128)(2,1)S(1)} %get-tuple-element.264), channel_id=1, source_target_pairs={{0,2},{2,0},{1,3},{3,1},{4,6},{6,4},{5,7},{7,5},{8,10},{10,8},{9,1... | collective-permute-start | bytes 786440 | tf_op jit(solution)/shard_map/ppermute | solution.py:98
  488.9 19.7 %collective-permute-start.45 = (bf16[128,1024]{1,0:T(8,128)(2,1)S(1)}, bf16[128,1024]{1,0:T(8,128)(2,1)S(1)}, u32[]{:S(2)}, u32[]{:S(2)}) collective-permute-start(bf16[128,1024]{1,0:T(8,128)(2,1)S(1)} %get-tuple-element.263), channel_id=1, source_target_pairs={{0,1},{1,0},{2,3},{3,2},{4,5},{5,4},{6,7},{7,6},{8,9},{9,8},{10,11... | collective-permute-start | bytes 786440 | tf_op jit(solution)/shard_map/ppermute | solution.py:99
  500.6 8.5 %collective-permute-start.54 = (bf16[32,3200]{1,0:T(8,128)(2,1)S(1)}, bf16[32,3200]{1,0:T(8,128)(2,1)S(1)}, u32[]{:S(2)}, u32[]{:S(2)}) collective-permute-start(bf16[32,3200]{1,0:T(8,128)(2,1)S(1)} %add_convert_fusion.6), channel_id=1, source_target_pairs={{0,24},{8,0},{16,8},{24,16},{1,25},{9,1},{17,9},{25,17},{2,26},{10... | collective-permute-start | bytes 614408 | tf_op jit(solution)/shard_map/ppermute | solution.py:51
  503.6 19.9 %collective-permute-start.55 = (bf16[32,3200]{1,0:T(8,128)(2,1)S(1)}, bf16[32,3200]{1,0:T(8,128)(2,1)S(1)}, u32[]{:S(2)}, u32[]{:S(2)}) collective-permute-start(bf16[32,3200]{1,0:T(8,128)(2,1)S(1)} %add_convert_fusion.6), channel_id=1, source_target_pairs={{0,16},{8,24},{16,0},{24,8},{1,17},{9,25},{17,1},{25,9},{2,18},{10... | collective-permute-start | bytes 614408 | tf_op jit(solution)/shard_map/ppermute | solution.py:51
  506.2 17.3 %collective-permute-start.56 = (bf16[32,3200]{1,0:T(8,128)(2,1)S(1)}, bf16[32,3200]{1,0:T(8,128)(2,1)S(1)}, u32[]{:S(2)}, u32[]{:S(2)}) collective-permute-start(bf16[32,3200]{1,0:T(8,128)(2,1)S(1)} %add_convert_fusion.6), channel_id=1, source_target_pairs={{0,8},{8,16},{16,24},{24,0},{1,9},{9,17},{17,25},{25,1},{2,10},{10... | collective-permute-start | bytes 614408 | tf_op jit(solution)/shard_map/ppermute | solution.py:51
  525.2 3.1 collective-permute-start.57
  (47 other events, 212.7 us)

commit v6 on v5

--- a/solution.py
+++ b/solution.py
@@ -192,9 +192,15 @@
     def kernel(lead_ref, packed_ref, *rest):
         first = lead_ref[0]
         if with_gates:
-            rows_ref, router_ref, out_ref, gate_out = rest
+            router_ref, out_ref, gate_out, rows_ref = rest[pieces:]
+            for p in range(pieces):
+
+                @pl.when(pl.program_id(0) == p)
+                def _():
+                    rows_ref[...] = rest[p][...]
+
             table = unpack_code(packed_ref[0], tokens)
-            source = rows_ref[0]
+            source = rows_ref[...]
         else:
             (out_ref,) = rest
             table = unpack_code(packed_ref[0, tokens:, :], tokens)
@@ -224,19 +230,23 @@
     if with_gates:
         in_specs = [
             pl.BlockSpec((1, 16, width), lambda p, lead: (p, tokens // 16, 0)),
-            pl.BlockSpec((1, tokens, width), lambda p, lead: (p, 0, 0)),
+            *[pl.BlockSpec((tokens, width), lambda p, lead: (0, 0)) for _ in rows],
             pl.BlockSpec((EXPERTS, width), lambda p, lead: (0, 0)),
         ]
         out_specs.append(pl.BlockSpec((1, slots, 128), lambda p, lead: (p, 0, 0)))
         out_shape.append(jax.ShapeDtypeStruct((pieces, slots, 128), F32))
-        args += [rows, router]
+        args += [*rows, router]
     else:
         in_specs = [pl.BlockSpec((1, packed_rows, width), lambda p, lead: (p, 0, 0))]
     return pl.pallas_call(
         kernel,
         out_shape=out_shape,
         grid_spec=pltpu.PrefetchScalarGridSpec(
-            num_scalar_prefetch=1, grid=(pieces,), in_specs=in_specs, out_specs=out_specs
+            num_scalar_prefetch=1,
+            grid=(pieces,),
+            in_specs=in_specs,
+            out_specs=out_specs,
+            scratch_shapes=[pltpu.VMEM((tokens, width), B16)] if with_gates else [],
         ),
         compiler_params=pltpu.CompilerParams(vmem_limit_bytes=VMEM_LIMIT),
         name="dispatch",
@@ -264,9 +274,15 @@
                 select, rest[h][0], (((0,), (0,)), ((), ())), preferred_element_type=F32
             )
             total = part if total is None else total + part
-        if addend is not None:
-            total = total + rest[halves][0].astype(F32)
-        rest[-1][0] = total.astype(B16)
+        if addend is None:
+            rest[halves][0] = total.astype(B16)
+        else:
+            low = (total + rest[halves][0].astype(F32)).astype(B16)
+            for p in range(pieces):
+
+                @pl.when(pl.program_id(0) == p)
+                def _():
+                    rest[halves + 1 + p][...] = low
 
     in_specs = [pl.BlockSpec((1, 16, code_width), lambda p, lead: (p, tokens // 16, 0))]
     in_specs += [
@@ -274,14 +290,20 @@
     ]
     added = [] if addend is None else [addend]
     in_specs += [pl.BlockSpec((1, tokens, width), lambda p, lead: (p, 0, 0)) for _ in added]
+    if addend is None:
+        out_shape = jax.ShapeDtypeStruct((pieces, tokens, width), B16)
+        out_specs = pl.BlockSpec((1, tokens, width), lambda p, lead: (p, 0, 0))
+    else:
+        out_shape = [jax.ShapeDtypeStruct((tokens, width), B16)] * pieces
+        out_specs = [pl.BlockSpec((tokens, width), lambda p, lead: (0, 0))] * pieces
     return pl.pallas_call(
         kernel,
-        out_shape=jax.ShapeDtypeStruct((pieces, tokens, width), B16),
+        out_shape=out_shape,
         grid_spec=pltpu.PrefetchScalarGridSpec(
             num_scalar_prefetch=1,
             grid=(pieces,),
             in_specs=in_specs,
-            out_specs=pl.BlockSpec((1, tokens, width), lambda p, lead: (p, 0, 0)),
+            out_specs=out_specs,
         ),
         compiler_params=pltpu.CompilerParams(vmem_limit_bytes=VMEM_LIMIT),
         name="combine",
@@ -642,7 +664,7 @@
             grad_ref, residual_ref, gates_ref, misc_ref, tail_ref, wo_ref, att_ref, moe_ref,
             normed_ref, q_ref, k_ref, v_ref, total_ref,
             x_ref, wq_ref, wk_ref, wv_ref, bias_ref, cos_ref, sin_ref,
-            dense_out, normed_out, residual_out,
+            keep_out, give_out, first_a_out, first_b_out, rest_a_out, rest_b_out, residual_out,
             normed_t, grad_sum, og_ref, logit_ref, gain_ref,
         ) = refs[terms:]
         step = pl.program_id(0)
@@ -652,7 +674,7 @@
         def _():
             normed_t[...] = jnp.transpose(normed_ref[...])
             grad_sum[...] = jnp.zeros((seq_len, width), F32)
-            total = sums[0][0].astype(F32)
+            total = sums[0][...].astype(F32)
             for ref in sums[1:]:
                 total = total + ref[...].astype(F32)
             behind = total[:, width:]
@@ -712,12 +734,21 @@
             [turn(query_grad[:, 128 * j : 128 * (j + 1)], cos, sin) for j in range(2)], axis=1
         ).astype(B16)
 
+        def put(at, lanes, rows):
+            for c in range(2):
+
+                @pl.when(core == c)
+                def _():
+                    keep_out[at, :, lanes] = rows[c].astype(B16)
+                    give_out[at, :, lanes] = rows[1 - c].astype(B16)
+
         def give(grad, lanes):
             for m in range(4):
-                for c in range(2):
-                    dense_out[core ^ c, dp ^ m, :, lanes] = grad[
-                        (2 * m + c) * block : (2 * m + c + 1) * block
-                    ].astype(B16)
+                put(
+                    dp ^ m,
+                    lanes,
+                    [grad[(2 * m + c) * block : (2 * m + c + 1) * block] for c in range(2)],
+                )
 
         give(
             jnp.dot(normed_t[:, :tok_rows], query_grad, preferred_element_type=F32),
@@ -728,9 +759,7 @@
             pl.ds(pl.multiple_of(wide + step * 256, 256), 256),
         )
         out_part = lax.dot_general(att_ref[...], og, TN, preferred_element_type=F32).astype(B16)
-        for c in range(2):
-            rows = slice(c * block, (c + 1) * block)
-            dense_out[core ^ c, dp ^ step, :, output_at : output_at + width] = out_part[rows]
+        put(dp ^ step, slice(output_at, output_at + width), [out_part[:block], out_part[block:]])
         kv_weights = jnp.concatenate([wk_ref[...], wv_ref[...]], axis=1)
         grad_sum[...] += lax.dot_general(kv_grad, kv_weights, NT, preferred_element_type=F32)
         grad_sum[:tok_rows, :] += lax.dot_general(
@@ -740,7 +769,16 @@
         @pl.when(step == GROUPS - 1)
         def _():
             total = grad_sum[...]
-            normed_out[...] = total.astype(B16)
+            low = total.astype(B16)
+            half = tok_rows // 2
+            first_a_out[0] = low[tok_rows : tok_rows + half]
+            first_a_out[1] = low[3 * tok_rows : 3 * tok_rows + half]
+            first_b_out[0] = low[2 * tok_rows + half : 3 * tok_rows]
+            first_b_out[1] = low[3 * tok_rows + half :]
+            rest_a_out[0] = low[:half]
+            rest_a_out[1] = low[2 * tok_rows : 2 * tok_rows + half]
+            rest_b_out[0] = low[half:tok_rows]
+            rest_b_out[1] = low[tok_rows + half : 2 * tok_rows]
             x = x_ref[...].astype(F32)
             lifted = x * lax.rsqrt(jnp.mean(x * x, axis=1, keepdims=True) + EPSILON)
             gain = jnp.sum(total * lifted, axis=0, keepdims=True)
@@ -760,19 +798,18 @@
         return pl.BlockSpec((rows, cols), lambda i, here: (0, lead + i))
 
     shapes = [
-        jax.ShapeDtypeStruct((2, 4, block, output_at + width + EXTRA), B16),
-        jax.ShapeDtypeStruct((seq_len, width), B16),
+        *[jax.ShapeDtypeStruct((4, block, output_at + width + EXTRA), B16)] * 2,
+        *[jax.ShapeDtypeStruct((2, tok_rows // 2, width), B16)] * 4,
         jax.ShapeDtypeStruct((tok_rows, width), F32),
     ]
-    return pl.pallas_call(
+    keep, give, *parts, residual_grad = pl.pallas_call(
         kernel,
         out_shape=shapes,
         grid_spec=pltpu.PrefetchScalarGridSpec(
             num_scalar_prefetch=1,
             grid=(GROUPS,),
             in_specs=[
-                pl.BlockSpec((1, tok_rows, width + 128), lambda i, here: (0, 0, 0)),
-                *[fixed(tok_rows, width + 128)] * (terms - 1),
+                *[fixed(tok_rows, width + 128)] * terms,
                 fixed(tok_rows, width),
                 fixed(tok_rows, width),
                 fixed(tok_rows, 128),
@@ -812,6 +849,75 @@
         moe_in, normed_all, query_rot, key_rot, value_all, totals,
         x_all, dense_full, dense_full, dense_full, bias, cosine, sine,
     )
+    return keep, give, tuple(parts[:2]), parts[2], parts[3], residual_grad
+
+
+def core_halves(keep, got, hold):
+    _, rows, cols = keep.shape
+    half = rows // 2
+    keep = after(keep, hold)
+
+    def kernel(keep_ref, got_ref, first_a, first_b, rest_a, rest_b):
+        def total(j, lo):
+            mine = keep_ref[j, lo : lo + half, :].astype(F32)
+            return (mine + got_ref[j, lo : lo + half, :].astype(F32)).astype(B16)
+
+        first_a[0], first_a[1] = total(1, 0), total(3, 0)
+        first_b[0], first_b[1] = total(2, half), total(3, half)
+        rest_a[0], rest_a[1] = total(0, 0), total(2, 0)
+        rest_b[0], rest_b[1] = total(0, half), total(1, half)
+
+    step = cols // 5
+    first_a, first_b, rest_a, rest_b = pl.pallas_call(
+        kernel,
+        grid=(5,),
+        in_specs=[pl.BlockSpec((4, rows, step), lambda i: (0, 0, i))] * 2,
+        out_specs=[pl.BlockSpec((2, half, step), lambda i: (0, 0, i))] * 4,
+        out_shape=[jax.ShapeDtypeStruct((2, half, cols), B16)] * 4,
+        compiler_params=pltpu.CompilerParams(vmem_limit_bytes=VMEM_LIMIT),
+        name="core_halves",
+    )(keep, got)
+    return (first_a, first_b), rest_a, rest_b
+
+
+def dense_outputs(core, mine, other, wide, narrow):
+    rows, cols = mine.shape
+    at = wide + 2 * narrow
+    shapes = [(2 * rows, wide), (2 * rows, narrow), (2 * rows, narrow), (2 * rows, cols - at - EXTRA)]
+    shapes.append((2 * rows, EXTRA))
+
+    def kernel(core_ref, mine_ref, other_ref, query, key, value, output, extra):
+        for c in range(2):
+            for ref, side in ((mine_ref, c), (other_ref, 1 - c)):
+
+                @pl.when(core_ref[0] == c)
+                def _():
+                    lines = slice(side * rows, (side + 1) * rows)
+                    query[lines, :] = ref[:, :wide].astype(F32)
+                    for i in range(GROUPS):
+                        lead = wide + 256 * i
+                        lanes = slice(128 * i, 128 * (i + 1))
+                        key[lines, lanes] = ref[:, lead : lead + 128].astype(F32)
+                        value[lines, lanes] = ref[:, lead + 128 : lead + 256].astype(F32)
+                    output[lines, :] = ref[:, at : cols - EXTRA].astype(F32)
+                    extra[lines, :] = ref[:, cols - EXTRA :].astype(F32)
+
+    def fixed(shape):
+        return pl.BlockSpec(shape, lambda i, core: (0, 0))
+
+    query, key, value, output, extra = pl.pallas_call(
+        kernel,
+        out_shape=[jax.ShapeDtypeStruct(shape, F32) for shape in shapes],
+        grid_spec=pltpu.PrefetchScalarGridSpec(
+            num_scalar_prefetch=1,
+            grid=(1,),
+            in_specs=[fixed(mine.shape)] * 2,
+            out_specs=[fixed(shape) for shape in shapes],
+        ),
+        compiler_params=pltpu.CompilerParams(vmem_limit_bytes=VMEM_LIMIT),
+        name="dense_outputs",
+    )(core.astype(jnp.int32)[None], mine, other)
+    return query, key, value, output, extra[:, :EXPERTS], extra[:, EXPERTS], extra[:, EXPERTS + 1]
 
 
 def make_body(z_size, small_grid):
@@ -830,7 +936,7 @@
 
     def across_z(mine, z):
         if z_size != 4:
-            return lax.psum(mine.astype(F32), "z")
+            return lax.psum(mine.astype(F32), "z").astype(B16)
         rows = mine.shape[0] // z_size
         low = mine.astype(B16)
         total = lax.dynamic_slice_in_dim(mine, z * rows, rows, 0)
@@ -840,17 +946,7 @@
         total = total.astype(B16)
         quarters = [total] + [cyclic(total, z_size, -k) for k in range(1, z_size)]
         places = (jnp.arange(z_size, dtype=jnp.int32) - z) % z_size
-        return jnp.take(jnp.stack(quarters), places, axis=0).reshape(mine.shape).astype(F32)
-
-    def core_sum(blocks):
-        return (blocks[0].astype(F32) + swap_core(blocks[1]).astype(F32)).astype(B16)
-
-    def dense_finish(halves, z, core):
-        low = across_z(jnp.concatenate(halves, axis=0), z).astype(B16)
-        other = swap_core(low)
-        first = jnp.where(core == 0, low, other)
-        second = jnp.where(core == 0, other, low)
-        return jnp.concatenate([first, second], axis=0).astype(F32)
+        return jnp.take(jnp.stack(quarters), places, axis=0).reshape(mine.shape)
 
     def dense_sum(grads):
         return lax.psum_scatter(
@@ -907,9 +1003,10 @@
         if small_grid:
             side = tok_rows // 2
             x_pack = jnp.concatenate([layer_input[:side], layer_input[side:]], axis=1)
-            start_parts = grid_gather(jnp.concatenate([x_pack, core_half(dense_pack, core)], axis=1))
+            start_parts = gather_near(jnp.concatenate([x_pack, core_half(dense_pack, core)], axis=1))
+            start_parts += gather_far(after(start_parts, *grad_pieces[1::2]))
             dense_parts = [part[:, 2 * model_width :] for part in start_parts]
-            dense_full = dense_assemble(dense_pack, dense_parts, dp_index, core, grad_pieces[1])
+            dense_full = dense_assemble(dense_pack, dense_parts, dp_index, core)
         else:
             dense_full = lax.all_gather(dense_pack, ("y", "x"), axis=0, tiled=True)
             full_output = dense_full[:, :model_width]
@@ -941,13 +1038,10 @@
             weights = [every[j] for j in range(dp_size)]
             near_0 = ()
         order = jnp.concatenate([relative, lead])
-        grads_mine = jnp.stack(after(grad_pieces, *near_0, dense_full))
-        grads_other = swap_core(grads_mine)
         visible = (key_pos[None, :] <= query_pos[:, None]) | (key_pos[None, :] < prefix_len[0])
         chunks = []
         if small_grid:
-            bias_hold = (grads_mine, *near_0)
-            bias = after(jnp.where(visible.T, 0.0, MASKED_SCORE), *bias_hold)
+            bias = after(jnp.where(visible.T, 0.0, MASKED_SCORE), *near_0)
             cosine, sine = turn_tables(key_pos.astype(F32))
             (
                 x_all, normed_all, query_rot, key_rot, value_all, attended, totals, misc, residual,
@@ -961,7 +1055,7 @@
                 sine,
                 jnp.pad(routed.astype(F32), ((0, 0), (0, 128 - EXPERTS))),
             )
-            moe_in = after(moe_in, grads_other, *near_1, *far_0)
+            moe_in = after(moe_in, *near_1, *far_0)
             router_rows = misc[:EXPERTS].astype(B16)
             full_attn_gain = misc[EXPERTS]
             full_moe_gain = misc[EXPERTS + 1]
@@ -1007,11 +1101,13 @@
             moe_in = rms_norm(residual, full_moe_gain).astype(B16)
 
         row_pieces = column_pieces(moe_in, z_size)
+        grads_mine = jnp.stack(after(grad_pieces, moe_in))
+        grads_other = swap_core(grads_mine)
         stage_1 = stage_2 = last_far = ()
         if small_grid:
             middle = pack.shape[1] // 2
             stage_1 = far_and_next(after(near_1, moe_in), pack[2])
-        (slot_grads_mine,) = dispatch_rows(lead, after(grads_mine, moe_in), None, None, local, capacity)
+        (slot_grads_mine,) = dispatch_rows(lead, grads_mine, None, None, local, capacity)
         (slot_grads_other,) = dispatch_rows(
             lead,
             after(grads_other, slot_grads_mine, *stage_1, row_pieces[1], row_pieces[-1]),
@@ -1030,8 +1126,8 @@
                 [(part, middle) for part in stage_2] + [(part, 0) for part in last_far],
             ]
         row_pieces = after(row_pieces, slot_grads_other)
-        rows_mine = after(jnp.stack(row_pieces), *stage_2)
-        rows_other = jnp.stack([swap_core(piece) for piece in row_pieces])
+        rows_mine = after(row_pieces, *stage_2)
+        rows_other = [swap_core(piece) for piece in row_pieces]
         slot_rows_mine, slot_gates_mine = dispatch_rows(
             lead, grads_mine, rows_mine, router_rows, local, capacity
         )
@@ -1082,21 +1178,17 @@
             early_got = second_step(early, via, late[3], late[7])
         dx_other = swap_core(combine_rows(lead, z_size, grads_other, dxs, local, capacity))
         dx_low = combine_rows(lead, 0, grads_mine, dxs, local, capacity, dx_other)
-        dx_pieces = column_send_some(dx_low, z_size)
+        dx_pieces = column_send_some(dx_low, z_size) + column_send_last(dx_low, z_size)
         y_other = combine_rows(lead, z_size, grads_other, after(ys, dx_low), local, capacity)
         dx_pieces, y_other = after((dx_pieces, y_other), y_other, *dx_pieces)
-        dx_pieces += column_send_last(dx_low, z_size, *dx_pieces)
-        ys, y_other = after((ys, swap_core(y_other)), *dx_pieces)
-        y_low = combine_rows(lead, 0, grads_mine, ys, local, capacity, y_other)
-        dx_pieces = after(dx_pieces, y_low)
-        y_pieces = column_send_some(y_low, z_size)
+        y_other = swap_core(y_other)
         if small_grid:
-            early_got = after(early_got, y_low)
+            early_got = after(early_got, *dx_pieces)
             late_got = second_step(late, [got[2:3] for got in early_got])
         if small_grid:
-            dense_blocks, normed_part, residual_grad = attention_backward(
+            keep, give, normed_first, normed_a, normed_b, residual_grad = attention_backward(
                 jnp.stack([dp_index, core]).astype(jnp.int32),
-                (dx_low, *dx_pieces),
+                (dx_low[0], *dx_pieces),
                 out_grad,
                 residual,
                 gates,
@@ -1109,40 +1201,29 @@
                 cosine,
                 sine,
             )
-            late_got, y_pieces = after((late_got, y_pieces), normed_part)
-            normed_part, dense_blocks = after((normed_part, dense_blocks), *late_got, *y_pieces)
+            late_got, y_other = after((late_got, y_other), residual_grad)
+            normed_first, keep, give = after((normed_first, keep, give), *late_got, y_other)
+            y_low = combine_rows(lead, 0, grads_mine, ys, local, capacity, y_other)
+            y_pieces = column_send_some(y_low, z_size)
             y_pieces += column_send_last(y_low, z_size, *y_pieces)
-            normed_first, normed_a, normed_b = row_halves(
-                normed_part.reshape(4, tok_rows, model_width)
-            )
-            dense_first, dense_a, dense_b = row_halves(core_sum(dense_blocks))
+            dense_first, dense_a, dense_b = core_halves(keep, swap_core(give), y_low[0])
             normed_got = grid_scatter_first(*normed_first)
             dense_got = grid_scatter_first(*after(dense_first, *normed_got))
-            dense_halves = after(grid_scatter_second(dense_got, dense_a, dense_b), *y_pieces)
-            dense_total = dense_finish(dense_halves, z, core)
+            dense_low = across_z(
+                jnp.concatenate(grid_scatter_second(dense_got, dense_a, dense_b), axis=0), z
+            )
+            (
+                query_sum, key_sum, value_sum, output_sum, router_sum, attn_gain_sum, moe_gain_sum,
+            ) = dense_outputs(core, dense_low, swap_core(dense_low), wide, narrow)
+            y_pieces = after(y_pieces, query_sum)
             normed_grad = jnp.concatenate(
                 grid_scatter_second(normed_got, normed_a, normed_b, *dense_got), axis=0
             )
             first_value, first_pull = jax.vjp(lambda v: rms_norm(v, full_attn_gain), in_float)
             input_grad = residual_grad + first_pull(normed_grad)[0]
-            kv_at = wide + 2 * narrow
-            query_sum = dense_total[:, :wide]
-            key_sum, value_sum = [
-                jnp.concatenate(
-                    [
-                        dense_total[:, wide + 256 * i + lead_col : wide + 256 * i + lead_col + 128]
-                        for i in range(GROUPS)
-                    ],
-                    axis=1,
-                )
-                for lead_col in (0, 128)
-            ]
-            output_sum = dense_total[:, kv_at : kv_at + model_width]
-            router_sum = dense_total[:, kv_at + model_width : kv_at + model_width + EXPERTS]
-            attn_gain_sum = dense_total[:, kv_at + model_width + EXPERTS]
-            moe_gain_sum = dense_total[:, kv_at + model_width + EXPERTS + 1]
         else:
-            y_pieces += column_send_last(y_low, z_size)
+            y_low = combine_rows(lead, 0, grads_mine, ys, local, capacity, y_other)
+            y_pieces = column_send_some(y_low, z_size) + column_send_last(y_low, z_size)
             moe_sum = column_sum(dx_low[0], dx_pieces)
             moe_in_grad = moe_sum[:, :model_width]
             gate_grad = (

time: 552 us -> 523 us (0.947)
  the two profiles are of different devices: /device:TPU:0 before, /device:TPU:25 now
where the time goes in v6:
time: 523 us; the launch traced here: 513 us
  waiting for transfers between devices  189 us (36%)
  Pallas kernels  176 us (34%)
  starting transfers between devices  70.8 us (14%)
  other arithmetic  44.2 us (8%)
  local copies, waits for them, and re-layouts  31.6 us (6%)
    ppermute x18, waiting for transfers between devices, cyclic(): lax.ppermute(rows, 'z', [(i, (i + shift) % size) for i in range(size)])  144 us
    pallas_call x2, Pallas kernels, experts(): pl.pallas_call(kernel, out_shape=out_shape, grid_spec=pltpu.PrefetchScala...  48.4 us
    pallas_call x1, Pallas kernels, attention_backward(): pl.pallas_call(kernel, out_shape=shapes, grid_spec=pltpu.PrefetchScalarGr...  44.3 us
    ppermute x18, starting transfers between devices, cyclic(): lax.ppermute(rows, 'z', [(i, (i + shift) % size) for i in range(size)])  33.8 us
    pallas_call x1, Pallas kernels, attention_forward(): pl.pallas_call(kernel, grid=(GROUPS,), in_specs=[fixed(tok_rows, width),...  25.4 us
    pallas_call x4, Pallas kernels, combine_rows(): pl.pallas_call(kernel, out_shape=out_shape, grid_spec=pltpu.PrefetchScala...  21.6 us
    pallas_call x4, Pallas kernels, dispatch_rows(): pl.pallas_call(kernel, out_shape=out_shape, grid_spec=pltpu.PrefetchScala...  19.8 us
    ppermute x4, waiting for transfers between devices, grid_scatter_first(): return (lax.ppermute(first_a, 'x', SWAP), lax.ppermute(first_b, 'y', SWAP))  16.9 us
  transfers between devices with their start and end apart: 58, of which 22 were waited for; matrix products, arithmetic and copies ran while one was open for 10% of the time, Pallas kernels for 28%

profile of v6, /device:TPU:25, one launch (start us, length us, event | category | flops | bytes accessed | tf_op | source)
XLA Modules:
  0.0 513.5 jit_solution(1701376282419536660)
XLA Ops:
  4.1 2.4 concatenate.57.shard_ref
  11.5 2.6 convert_reduce_fusion
  15.4 3.1 collective-permute-start.3
  18.5 11.8 %collective-permute-done.2 = bf16[272,1024]{1,0:T(8,128)(2,1)S(1)} collective-permute-done((bf16[272,1024]{1,0:T(8,128)(2,1)}, bf16[272,1024]{1,0:T(8,128)(2,1)S(1)}, u32[]{:S(2)}, u32[]{:S(2)}) %collective-permute-start.2) | collective-permute-done | bytes 557088 | tf_op jit(solution)/shard_map/ppermute | solution.py:51
  30.3 10.2 %collective-permute-done.3 = bf16[272,1024]{1,0:T(8,128)(2,1)S(1)} collective-permute-done((bf16[272,1024]{1,0:T(8,128)(2,1)}, bf16[272,1024]{1,0:T(8,128)(2,1)S(1)}, u32[]{:S(2)}, u32[]{:S(2)}) %collective-permute-start.3) | collective-permute-done | bytes 557088 | tf_op jit(solution)/shard_map/ppermute | solution.py:51
  42.8 13.1 %collective-permute-done.5.ea_ref.eb_ref = bf16[64,5248]{1,0:T(8,128)(2,1)S(1)} collective-permute-done((bf16[64,5248]{1,0:T(8,128)(2,1)S(1)}, bf16[64,5248]{1,0:T(8,128)(2,1)S(1)}, u32[]{:S(2)}, u32[]{:S(2)}) %collective-permute-start.5) | collective-permute-done | bytes 671776 | tf_op jit(solution)/shard_map/ppermute | solution.py:65
  57.0 1.7 pad_maximum_fusion.2.moved_ref
  58.7 3.2 collective-permute-start.6
  62.3 1.5 slice_bitcast_fusion
  66.3 2.0 collective-permute-start.9
  69.0 6.7 %assemble.1.tail_ref.wo_ref.wq_ref.wk_ref.wv_ref.refs_8_.refs_9_.refs_18_.refs_19_.refs_20_ = bf16[1024,3200]{1,0:T(8,128)(2,1)} custom-call(s32[7]{0:T(128)} %stack.78.places_ref, bf16[256,3200]{1,0:T(8,128)(2,1)} %copy-done.4, bf16[384,3200]{1,0:T(8,128)(2,1)} %pad_maximum_fusion.2.moved_ref, bf16[384,3200]{1,0:T(8,128)(2,1)} %collective-permute-done.6.other_ref), custom_call_target="tpu_custom_call" | custom-call | tf_op jit(solution)/shard_map/assemble/pallas_call | solution.py:148
  75.7 6.9 %collective-permute-done.7.refs_7_ = bf16[768,512]{1,0:T(8,128)(2,1)S(1)} collective-permute-done((bf16[768,512]{1,0:T(8,128)(2,1)}, bf16[768,512]{1,0:T(8,128)(2,1)S(1)}, u32[]{:S(2)}, u32[]{:S(2)}) %collective-permute-start.7) | collective-permute-done | bytes 786464 | tf_op jit(solution)/shard_map/ppermute | solution.py:59
  84.3 3.0 fusion.5
  93.3 25.4 %attention.1 = (bf16[1024,1024]{1,0:T(8,128)(2,1)}, bf16[1024,1024]{1,0:T(8,128)(2,1)}, bf16[256,1024]{1,0:T(8,128)(2,1)}, bf16[1024,512]{1,0:T(8,128)(2,1)}, bf...) custom-call(bf16[256,1024]{1,0:T(8,128)(2,1)} %own_ref.1, ...), custom_call_target="tpu_custom_call" | custom-call | tf_op jit(solution)/shard_map/attention/pallas_call | solution.py:594
  119.5 1.7 pad_maximum_fusion.5.packed_ref.code_ref
  121.2 3.7 collective-permute-start.17
  127.0 1.7 pad_maximum_fusion.16
  129.4 3.5 collective-permute-start.16
  133.0 4.6 dispatch.4.refs_2_
  137.5 6.5 %collective-permute-done.14.rest_1_ = bf16[256,1024]{1,0:T(8,128)(2,1)} collective-permute-done((bf16[256,1024]{1,0:T(8,128)(2,1)}, bf16[256,1024]{1,0:T(8,128)(2,1)}, u32[]{:S(2)}, u32[]{:S(2)}) %collective-permute-start.14) | collective-permute-done | bytes 524320 | tf_op jit(solution)/shard_map/ppermute | solution.py:51
  144.0 11.2 %collective-permute-done.16.rest_3_ = bf16[256,1024]{1,0:T(8,128)(2,1)} collective-permute-done((bf16[256,1024]{1,0:T(8,128)(2,1)}, bf16[256,1024]{1,0:T(8,128)(2,1)}, u32[]{:S(2)}, u32[]{:S(2)}) %collective-permute-start.16) | collective-permute-done | bytes 524320 | tf_op jit(solution)/shard_map/ppermute | solution.py:51
  156.2 5.0 dispatch.5.refs_3_
  164.1 1.4 collective-permute-start.15
  165.6 23.8 %collective-permute-done.15.rest_2_ = bf16[256,1024]{1,0:T(8,128)(2,1)S(1)} collective-permute-done((bf16[256,1024]{1,0:T(8,128)(2,1)}, bf16[256,1024]{1,0:T(8,128)(2,1)S(1)}, u32[]{:S(2)}, u32[]{:S(2)}) %collective-permute-start.15) | collective-permute-done | bytes 524320 | tf_op jit(solution)/shard_map/ppermute | solution.py:51
  189.3 1.5 collective-permute-start.22
  195.1 1.5 slice.309.rest_4_
  196.6 5.1 dispatch.6
  202.5 5.1 dispatch.7
  207.6 23.4 %experts.2 = (bf16[8,160,1024]{2,1,0:T(8,128)(2,1)}, bf16[8,160,1152]{2,1,0:T(8,128)(2,1)}, bf16[1,1,768,512]{3,2,1,0:T(8,128)(2,1)}, bf16[1,1,768,512]{3,2,1,0:...) custom-call(s32[5]{0:T(128)} %pad_add_fusion.order_ref, ...), custom_call_target="tpu_custom_call" | custom-call | tf_op jit(solution)/shard_map/experts/pallas_call | solution.py:470
  232.7 25.0 %experts.3 = (bf16[8,160,1024]{2,1,0:T(8,128)(2,1)}, bf16[8,160,1152]{2,1,0:T(8,128)(2,1)}, bf16[1,1,768,512]{3,2,1,0:T(8,128)(2,1)}, bf16[1,1,768,512]{3,2,1,0:...) custom-call(s32[5]{0:T(128)} %pad_add_fusion.order_ref, ...), custom_call_target="tpu_custom_call" | custom-call | tf_op jit(solution)/shard_map/experts/pallas_call | solution.py:470
  257.8 5.2 %combine.4 = bf16[4,256,1152]{2,1,0:T(8,128)(2,1)} custom-call(s32[1]{0:T(128)} %bitcast.11.lead_ref, bf16[4,272,1024]{2,1,0:T(8,128)(2,1)} %collective-permute-done.17.packed_ref.code_ref, bf16[8,160,1152]{2,1,0:T(8,128)(2,1)} %get-tuple-element.181.rest_0_, bf16[8,160,1152]{2,1,0:T(8,128)(2,1)} %get-tuple-element.182.rest_1_), custom_call_target="tpu_custom_call" | custom-call | tf_op jit(solution)/shard_map/combine/pallas_call | solution.py:299
  262.9 1.5 collective-permute-start.32
  266.3 1.7 pad_maximum_fusion.4
  268.9 6.0 %combine.5 = (bf16[256,1152]{1,0:T(8,128)(2,1)}, bf16[256,1152]{1,0:T(8,128)(2,1)}, bf16[256,1152]{1,0:T(8,128)(2,1)}, bf16[256,1152]{1,0:T(8,128)(2,1)}) custom-call(s32[1]{0:T(128)} %bitcast.11.lead_ref, bf16[4,272,1024]{2,1,0:T(8,128)(2,1)} %copy-done, bf16[8,160,1152]{2,1,0:T(8,128)(2,1)} %get-tuple-element.181.rest_0_, ...), custom_call_target="tpu_custom_call" | custom-call | tf_op jit(solution)/shard_map/combine/pallas_call | solution.py:299
  274.9 1.6 collective-permute-start.33
  277.5 4.8 combine.6
  282.3 6.9 %collective-permute-done.33.refs_1_ = bf16[256,1152]{1,0:T(8,128)(2,1)S(1)} collective-permute-done((bf16[256,1152]{1,0:T(8,128)(2,1)}, bf16[256,1152]{1,0:T(8,128)(2,1)S(1)}, u32[]{:S(2)}, u32[]{:S(2)}) %collective-permute-start.33) | collective-permute-done | bytes 589856 | tf_op jit(solution)/shard_map/ppermute | solution.py:51
  289.2 13.6 %collective-permute-done.34.refs_2_ = bf16[256,1152]{1,0:T(8,128)(2,1)S(1)} collective-permute-done((bf16[256,1152]{1,0:T(8,128)(2,1)}, bf16[256,1152]{1,0:T(8,128)(2,1)S(1)}, u32[]{:S(2)}, u32[]{:S(2)}) %collective-permute-start.34) | collective-permute-done | bytes 589856 | tf_op jit(solution)/shard_map/ppermute | solution.py:51
  302.8 23.7 %collective-permute-done.35.refs_3_ = bf16[256,1152]{1,0:T(8,128)(2,1)S(1)} collective-permute-done((bf16[256,1152]{1,0:T(8,128)(2,1)}, bf16[256,1152]{1,0:T(8,128)(2,1)S(1)}, u32[]{:S(2)}, u32[]{:S(2)}) %collective-permute-start.35) | collective-permute-done | bytes 589856 | tf_op jit(solution)/shard_map/ppermute | solution.py:51
  326.5 2.4 collective-permute-start.38
  328.9 4.4 add_bitcast_fusion.3
  338.3 44.3 %attention_grad.1 = (bf16[4,128,3200]{2,1,0:T(8,128)(2,1)}, bf16[4,128,3200]{2,1,0:T(8,128)(2,1)}, bf16[2,128,1024]{2,1,0:T(8,128)(2,1)}, bf16[2,128,1024]{2,1,0...) custom-call(s32[2]{0:T(128)} %pad_add_fusion.1.here_ref, ...), custom_call_target="tpu_custom_call" | custom-call | tf_op jit(solution)/shard_map/attention_grad/pallas_call | solution.py:805
  385.2 5.6 %combine.7 = (bf16[256,1024]{1,0:T(8,128)(2,1)}, bf16[256,1024]{1,0:T(8,128)(2,1)}, bf16[256,1024]{1,0:T(8,128)(2,1)}, bf16[256,1024]{1,0:T(8,128)(2,1)}) custom-call(s32[1]{0:T(128)} %bitcast.11.lead_ref, bf16[4,272,1024]{2,1,0:T(8,128)(2,1)} %copy-done, bf16[8,160,1024]{2,1,0:T(8,128)(2,1)} %get-tuple-element.187.rest_0_, ...), custom_call_target="tpu_custom_call" | custom-call | tf_op jit(solution)/shard_map/combine/pallas_call | solution.py:299
  390.8 6.0 %core_halves.1 = (bf16[2,64,3200]{2,1,0:T(8,128)(2,1)}, bf16[2,64,3200]{2,1,0:T(8,128)(2,1)}, bf16[2,64,3200]{2,1,0:T(8,128)(2,1)}, bf16[2,64,3200]{2,1,0:T(8,128)(2,1)}) custom-call(bf16[4,128,3200]{2,1,0:T(8,128)(2,1)} %get-tuple-element.220.keep_ref, bf16[4,128,3200]{2,1,0:T(8,128)(2,1)} %collective-permute-done.42.got_ref), custom_call_target="tpu_custom_call" | custom-call | tf_op jit(solution)/shard_map/core_halves/pallas_call | solution.py:871
  399.9 2.4 collective-permute-start.39
  402.2 3.0 add_bitcast_fusion.1
  407.0 10.0 %collective-permute-done.45 = bf16[2,64,3200]{2,1,0:T(8,128)(2,1)} collective-permute-done((bf16[2,64,3200]{2,1,0:T(8,128)(2,1)}, bf16[2,64,3200]{2,1,0:T(8,128)(2,1)}, u32[]{:S(2)}, u32[]{:S(2)}) %collective-permute-start.45) | collective-permute-done | bytes 819232 | tf_op jit(solution)/shard_map/ppermute | solution.py:91
  418.7 5.8 %collective-permute-done.47 = bf16[2,64,3200]{2,1,0:T(8,128)(2,1)S(1)} collective-permute-done((bf16[2,64,3200]{2,1,0:T(8,128)(2,1)S(1)}, bf16[2,64,3200]{2,1,0:T(8,128)(2,1)S(1)}, u32[]{:S(2)}, u32[]{:S(2)}) %collective-permute-start.47) | collective-permute-done | bytes 819232 | tf_op jit(solution)/shard_map/ppermute | solution.py:91
  428.0 5.2 %collective-permute-done.46 = bf16[64,3200]{1,0:T(8,128)(2,1)S(1)} collective-permute-done((bf16[64,3200]{1,0:T(8,128)(2,1)S(1)}, bf16[64,3200]{1,0:T(8,128)(2,1)S(1)}, u32[]{:S(2)}, u32[]{:S(2)}) %collective-permute-start.46) | collective-permute-done | bytes 409632 | tf_op jit(solution)/shard_map/ppermute | solution.py:98
  435.3 3.2 collective-permute-start.50
  438.6 2.8 fusion.23
  441.4 1.5 fusion
  442.9 1.4 collective-permute-start.41
  444.3 10.5 %collective-permute-done.50 = bf16[32,3200]{1,0:T(8,128)(2,1)S(1)} collective-permute-done((bf16[32,3200]{1,0:T(8,128)(2,1)S(1)}, bf16[32,3200]{1,0:T(8,128)(2,1)S(1)}, u32[]{:S(2)}, u32[]{:S(2)}) %collective-permute-start.50) | collective-permute-done | bytes 204832 | tf_op jit(solution)/shard_map/ppermute | solution.py:51
  455.0 10.5 %collective-permute-start.54 = (bf16[32,3200]{1,0:T(8,128)(2,1)S(1)}, bf16[32,3200]{1,0:T(8,128)(2,1)S(1)}, u32[]{:S(2)}, u32[]{:S(2)}) collective-permute-start(bf16[32,3200]{1,0:T(8,128)(2,1)S(1)} %fusion.12), channel_id=1, source_target_pairs={{0,8},{8,16},{16,24},{24,0},{1,9},{9,17},{17,25},{25,1},{2,10},{10... | collective-permute-start | bytes 614408 | tf_op jit(solution)/shard_map/ppermute | solution.py:51
  465.5 3.2 collective-permute-start.53
  469.7 3.0 collective-permute-done.54
  472.7 23.1 %collective-permute-done.53 = bf16[32,3200]{1,0:T(8,128)(2,1)S(1)} collective-permute-done((bf16[32,3200]{1,0:T(8,128)(2,1)S(1)}, bf16[32,3200]{1,0:T(8,128)(2,1)S(1)}, u32[]{:S(2)}, u32[]{:S(2)}) %collective-permute-start.53) | collective-permute-done | bytes 204832 | tf_op jit(solution)/shard_map/ppermute | solution.py:51
  496.0 1.5 gather_fusion
  498.9 2.1 collective-permute-start.55
  503.8 3.3 dense_outputs.1
  507.1 1.8 slice_reduce_fusion
  508.9 1.6 copy.46
  510.5 2.6 add_convert_fusion.4
  (260 shorter events, 66.4 us)
Async XLA Ops:
  8.8 31.6 %collective-permute-start = (bf16[128,5248]{1,0:T(8,128)(2,1)}, bf16[128,5248]{1,0:T(8,128)(2,1)S(1)}, u32[]{:S(2)}, u32[]{:S(2)}) collective-permute-start(bf16[128,5248]{1,0:T(8,128)(2,1)} %pad_maximum_fusion.15), channel_id=1, source_target_pairs={{0,1},{1,0},{2,3},{3,2},{4,5},{5,4},{6,7},{7,6},{8,9},{9,8},{10,11... | collective-permute-start | bytes 4030472 | tf_op jit(solution)/shard_map/ppermute | solution.py:59
  10.0 31.2 %collective-permute-start.1 = (bf16[128,5248]{1,0:T(8,128)(2,1)}, bf16[128,5248]{1,0:T(8,128)(2,1)S(1)}, u32[]{:S(2)}, u32[]{:S(2)}) collective-permute-start(bf16[128,5248]{1,0:T(8,128)(2,1)} %pad_maximum_fusion.15), channel_id=1, source_target_pairs={{0,2},{2,0},{1,3},{3,1},{4,6},{6,4},{5,7},{7,5},{8,10},{10,8},{9,1... | collective-permute-start | bytes 4030472 | tf_op jit(solution)/shard_map/ppermute | solution.py:59
  15.2 15.0 %collective-permute-start.2 = (bf16[272,1024]{1,0:T(8,128)(2,1)}, bf16[272,1024]{1,0:T(8,128)(2,1)S(1)}, u32[]{:S(2)}, u32[]{:S(2)}) collective-permute-start(bf16[272,1024]{1,0:T(8,128)(2,1)} %maximum_maximum_fusion), channel_id=1, source_target_pairs={{0,24},{8,0},{16,8},{24,16},{1,25},{9,1},{17,9},{25,17},{2,26},{10... | collective-permute-start | bytes 1671176 | tf_op jit(solution)/shard_map/ppermute | solution.py:51
  15.4 25.1 %collective-permute-start.3 = (bf16[272,1024]{1,0:T(8,128)(2,1)}, bf16[272,1024]{1,0:T(8,128)(2,1)S(1)}, u32[]{:S(2)}, u32[]{:S(2)}) collective-permute-start(bf16[272,1024]{1,0:T(8,128)(2,1)} %maximum_maximum_fusion), channel_id=1, source_target_pairs={{0,8},{8,16},{16,24},{24,0},{1,9},{9,17},{17,25},{25,1},{2,10},{10... | collective-permute-start | bytes 1671176 | tf_op jit(solution)/shard_map/ppermute | solution.py:51
  41.3 14.6 %collective-permute-start.5 = (bf16[64,5248]{1,0:T(8,128)(2,1)S(1)}, bf16[64,5248]{1,0:T(8,128)(2,1)S(1)}, u32[]{:S(2)}, u32[]{:S(2)}) collective-permute-start(bf16[64,5248]{1,0:T(8,128)(2,1)S(1)} %slice.195), channel_id=1, source_target_pairs={{0,1},{1,0},{2,3},{3,2},{4,5},{5,4},{6,7},{7,6},{8,9},{9,8},{10,11... | collective-permute-start | bytes 2015240 | tf_op jit(solution)/shard_map/ppermute | solution.py:65
  41.7 14.3 %collective-permute-start.4 = (bf16[64,5248]{1,0:T(8,128)(2,1)S(1)}, bf16[64,5248]{1,0:T(8,128)(2,1)S(1)}, u32[]{:S(2)}, u32[]{:S(2)}) collective-permute-start(bf16[64,5248]{1,0:T(8,128)(2,1)S(1)} %slice.194), channel_id=1, source_target_pairs={{0,2},{2,0},{1,3},{3,1},{4,6},{6,4},{5,7},{7,5},{8,10},{10,8},{9,1... | collective-permute-start | bytes 2015240 | tf_op jit(solution)/shard_map/ppermute | solution.py:65
  58.7 10.3 %collective-permute-start.6 = (bf16[384,3200]{1,0:T(8,128)(2,1)}, bf16[384,3200]{1,0:T(8,128)(2,1)}, u32[]{:S(2)}, u32[]{:S(2)}) collective-permute-start(bf16[384,3200]{1,0:T(8,128)(2,1)} %pad_maximum_fusion.2.moved_ref), channel_id=1, source_target_pairs={{0,4},{4,0},{1,5},{5,1},{2,6},{6,2},{3,7},{7,3},{8,12},{12,8},{9,1... | collective-permute-start | bytes 7372808 | tf_op jit(solution)/shard_map/ppermute | solution.py:47
  64.8 17.9 %collective-permute-start.7 = (bf16[768,512]{1,0:T(8,128)(2,1)}, bf16[768,512]{1,0:T(8,128)(2,1)S(1)}, u32[]{:S(2)}, u32[]{:S(2)}) collective-permute-start(bf16[768,512]{1,0:T(8,128)(2,1)} %get-tuple-element.132), channel_id=1, source_target_pairs={{0,1},{1,0},{2,3},{3,2},{4,5},{5,4},{6,7},{7,6},{8,9},{9,8},{10,11... | collective-permute-start | bytes 2359304 | tf_op jit(solution)/shard_map/ppermute | solution.py:59
  66.0 17.6 %collective-permute-start.8 = (bf16[768,512]{1,0:T(8,128)(2,1)}, bf16[768,512]{1,0:T(8,128)(2,1)S(1)}, u32[]{:S(2)}, u32[]{:S(2)}) collective-permute-start(bf16[768,512]{1,0:T(8,128)(2,1)} %get-tuple-element.132), channel_id=1, source_target_pairs={{0,2},{2,0},{1,3},{3,1},{4,6},{6,4},{5,7},{7,5},{8,10},{10,8},{9,1... | collective-permute-start | bytes 2359304 | tf_op jit(solution)/shard_map/ppermute | solution.py:59
  66.3 52.4 %collective-permute-start.9 = (bf16[272,1024]{1,0:T(8,128)(2,1)}, bf16[272,1024]{1,0:T(8,128)(2,1)S(1)}, u32[]{:S(2)}, u32[]{:S(2)}) collective-permute-start(bf16[272,1024]{1,0:T(8,128)(2,1)} %maximum_maximum_fusion), channel_id=1, source_target_pairs={{0,16},{8,24},{16,0},{24,8},{1,17},{9,25},{17,1},{25,9},{2,18},{10... | collective-permute-start | bytes 1671176 | tf_op jit(solution)/shard_map/ppermute | solution.py:51
  82.7 36.0 %copy-start.15 = (bf16[768,512]{1,0:T(8,128)(2,1)}, bf16[768,512]{1,0:T(8,128)(2,1)S(1)}, u32[]{:S(2)}) copy-start(bf16[768,512]{1,0:T(8,128)(2,1)S(1)} %collective-permute-done.7.refs_7_) | copy-start | bytes 2359300
  83.6 35.0 %copy-start.16 = (bf16[768,512]{1,0:T(8,128)(2,1)}, bf16[768,512]{1,0:T(8,128)(2,1)S(1)}, u32[]{:S(2)}) copy-start(bf16[768,512]{1,0:T(8,128)(2,1)S(1)} %collective-permute-done.8.refs_8_) | copy-start | bytes 2359300
  83.6 35.1 %collective-permute-start.10 = (bf16[768,512]{1,0:T(8,128)(2,1)}, bf16[768,512]{1,0:T(8,128)(2,1)}, u32[]{:S(2)}, u32[]{:S(2)}) collective-permute-start(bf16[768,512]{1,0:T(8,128)(2,1)} %get-tuple-element.136), channel_id=1, source_target_pairs={{0,1},{1,0},{2,3},{3,2},{4,5},{5,4},{6,7},{7,6},{8,9},{9,8},{10,11... | collective-permute-start | bytes 2359304 | tf_op jit(solution)/shard_map/ppermute | solution.py:59
  84.0 34.7 %collective-permute-start.11 = (bf16[768,512]{1,0:T(8,128)(2,1)}, bf16[768,512]{1,0:T(8,128)(2,1)}, u32[]{:S(2)}, u32[]{:S(2)}) collective-permute-start(bf16[768,512]{1,0:T(8,128)(2,1)} %get-tuple-element.136), channel_id=1, source_target_pairs={{0,2},{2,0},{1,3},{3,1},{4,6},{6,4},{5,7},{7,5},{8,10},{10,8},{9,1... | collective-permute-start | bytes 2359304 | tf_op jit(solution)/shard_map/ppermute | solution.py:59
  88.0 30.7 %collective-permute-start.12 = (bf16[384,512]{1,0:T(8,128)(2,1)S(1)}, bf16[384,512]{1,0:T(8,128)(2,1)}, u32[]{:S(2)}, u32[]{:S(2)}) collective-permute-start(bf16[384,512]{1,0:T(8,128)(2,1)S(1)} %slice.204), channel_id=1, source_target_pairs={{0,2},{2,0},{1,3},{3,1},{4,6},{6,4},{5,7},{7,5},{8,10},{10,8},{9,1... | collective-permute-start | bytes 1179656 | tf_op jit(solution)/shard_map/ppermute | solution.py:65
  90.0 28.7 %collective-permute-start.13 = (bf16[384,512]{1,0:T(8,128)(2,1)}, bf16[384,512]{1,0:T(8,128)(2,1)}, u32[]{:S(2)}, u32[]{:S(2)}) collective-permute-start(bf16[384,512]{1,0:T(8,128)(2,1)} %slice.205), channel_id=1, source_target_pairs={{0,1},{1,0},{2,3},{3,2},{4,5},{5,4},{6,7},{7,6},{8,9},{9,8},{10,11... | collective-permute-start | bytes 1179656 | tf_op jit(solution)/shard_map/ppermute | solution.py:65
  93.3 26.3 %copy-start.35 = (bf16[272,1024]{1,0:T(8,128)(2,1)S(1)}, bf16[272,1024]{1,0:T(8,128)(2,1)}, u32[]{:S(2)}) copy-start(bf16[272,1024]{1,0:T(8,128)(2,1)} %copy-done.34) | copy-start | bytes 1671172
  121.2 35.0 %collective-permute-start.17 = (bf16[4,272,1024]{2,1,0:T(8,128)(2,1)S(1)}, bf16[4,272,1024]{2,1,0:T(8,128)(2,1)}, u32[]{:S(2)}, u32[]{:S(2)}) collective-permute-start(bf16[4,272,1024]{2,1,0:T(8,128)(2,1)S(1)} %pad_maximum_fusion.5.packed_ref.code_ref), channel_id=1, source_target_pairs={{0,4},{4,0},{1,5},{5,1},{2,6},{6,2},{3,7},{7,3},{8,12},{12,8},{9,1... | collective-permute-start | bytes 6684680 | tf_op jit(solution)/shard_map/ppermute | solution.py:47
  128.7 27.5 %collective-permute-start.18 = (bf16[1152,512]{1,0:T(8,128)(2,1)}, bf16[1152,512]{1,0:T(8,128)(2,1)S(1)}, u32[]{:S(2)}, u32[]{:S(2)}) collective-permute-start(bf16[1152,512]{1,0:T(8,128)(2,1)} %get-tuple-element.308), channel_id=1, source_target_pairs={{0,1},{1,0},{2,3},{3,2},{4,5},{5,4},{6,7},{7,6},{8,9},{9,8},{10,11... | collective-permute-start | bytes 3538952 | tf_op jit(solution)/shard_map/ppermute | solution.py:74
  128.9 27.3 %collective-permute-start.19 = (bf16[1152,512]{1,0:T(8,128)(2,1)}, bf16[1152,512]{1,0:T(8,128)(2,1)}, u32[]{:S(2)}, u32[]{:S(2)}) collective-permute-start(bf16[1152,512]{1,0:T(8,128)(2,1)} %get-tuple-element.307), channel_id=1, source_target_pairs={{0,2},{2,0},{1,3},{3,1},{4,6},{6,4},{5,7},{7,5},{8,10},{10,8},{9,1... | collective-permute-start | bytes 3538952 | tf_op jit(solution)/shard_map/ppermute | solution.py:74
  129.2 14.8 %collective-permute-start.14 = (bf16[256,1024]{1,0:T(8,128)(2,1)}, bf16[256,1024]{1,0:T(8,128)(2,1)}, u32[]{:S(2)}, u32[]{:S(2)}) collective-permute-start(bf16[256,1024]{1,0:T(8,128)(2,1)} %get-tuple-element.153.rest_0_.refs_11_), channel_id=1, source_target_pairs={{0,24},{8,0},{16,8},{24,16},{1,25},{9,1},{17,9},{25,17},{2,26},{10... | collective-permute-start | bytes 1572872 | tf_op jit(solution)/shard_map/ppermute | solution.py:51
  129.4 25.8 %collective-permute-start.16 = (bf16[256,1024]{1,0:T(8,128)(2,1)}, bf16[256,1024]{1,0:T(8,128)(2,1)}, u32[]{:S(2)}, u32[]{:S(2)}) collective-permute-start(bf16[256,1024]{1,0:T(8,128)(2,1)} %get-tuple-element.153.rest_0_.refs_11_), channel_id=1, source_target_pairs={{0,8},{8,16},{16,24},{24,0},{1,9},{9,17},{17,25},{25,1},{2,10},{10... | collective-permute-start | bytes 1572872 | tf_op jit(solution)/shard_map/ppermute | solution.py:51
  162.5 28.9 %collective-permute-start.20 = (bf16[1152,512]{1,0:T(8,128)(2,1)S(1)}, bf16[1152,512]{1,0:T(8,128)(2,1)S(1)}, u32[]{:S(2)}, u32[]{:S(2)}) collective-permute-start(bf16[1152,512]{1,0:T(8,128)(2,1)S(1)} %get-tuple-element.306), channel_id=1, source_target_pairs={{0,1},{1,0},{2,3},{3,2},{4,5},{5,4},{6,7},{7,6},{8,9},{9,8},{10,11... | collective-permute-start | bytes 3538952 | tf_op jit(solution)/shard_map/ppermute | solution.py:74
  163.3 29.0 %collective-permute-start.21 = (bf16[1152,512]{1,0:T(8,128)(2,1)S(1)}, bf16[1152,512]{1,0:T(8,128)(2,1)S(1)}, u32[]{:S(2)}, u32[]{:S(2)}) collective-permute-start(bf16[1152,512]{1,0:T(8,128)(2,1)S(1)} %get-tuple-element.305), channel_id=1, source_target_pairs={{0,2},{2,0},{1,3},{3,1},{4,6},{6,4},{5,7},{7,5},{8,10},{10,8},{9,1... | collective-permute-start | bytes 3538952 | tf_op jit(solution)/shard_map/ppermute | solution.py:74
  164.1 25.2 %collective-permute-start.15 = (bf16[256,1024]{1,0:T(8,128)(2,1)}, bf16[256,1024]{1,0:T(8,128)(2,1)S(1)}, u32[]{:S(2)}, u32[]{:S(2)}) collective-permute-start(bf16[256,1024]{1,0:T(8,128)(2,1)} %get-tuple-element.153.rest_0_.refs_11_), channel_id=1, source_target_pairs={{0,16},{8,24},{16,0},{24,8},{1,17},{9,25},{17,1},{25,9},{2,18},{10... | collective-permute-start | bytes 1572872 | tf_op jit(solution)/shard_map/ppermute | solution.py:51
  189.3 4.4 collective-permute-start.22
  190.8 10.9 %collective-permute-start.23 = (bf16[256,1024]{1,0:T(8,128)(2,1)}, bf16[256,1024]{1,0:T(8,128)(2,1)S(1)}, u32[]{:S(2)}, u32[]{:S(2)}) collective-permute-start(bf16[256,1024]{1,0:T(8,128)(2,1)} %collective-permute-done.14.rest_1_), channel_id=1, source_target_pairs={{0,4},{4,0},{1,5},{5,1},{2,6},{6,2},{3,7},{7,3},{8,12},{12,8},{9,1... | collective-permute-start | bytes 1572872 | tf_op jit(solution)/shard_map/ppermute | solution.py:47
  190.8 10.9 %collective-permute-start.24 = (bf16[256,1024]{1,0:T(8,128)(2,1)S(1)}, bf16[256,1024]{1,0:T(8,128)(2,1)}, u32[]{:S(2)}, u32[]{:S(2)}) collective-permute-start(bf16[256,1024]{1,0:T(8,128)(2,1)S(1)} %collective-permute-done.15.rest_2_), channel_id=1, source_target_pairs={{0,4},{4,0},{1,5},{5,1},{2,6},{6,2},{3,7},{7,3},{8,12},{12,8},{9,1... | collective-permute-start | bytes 1572872 | tf_op jit(solution)/shard_map/ppermute | solution.py:47
  191.3 10.4 %collective-permute-start.25 = (bf16[256,1024]{1,0:T(8,128)(2,1)}, bf16[256,1024]{1,0:T(8,128)(2,1)}, u32[]{:S(2)}, u32[]{:S(2)}) collective-permute-start(bf16[256,1024]{1,0:T(8,128)(2,1)} %collective-permute-done.16.rest_3_), channel_id=1, source_target_pairs={{0,4},{4,0},{1,5},{5,1},{2,6},{6,2},{3,7},{7,3},{8,12},{12,8},{9,1... | collective-permute-start | bytes 1572872 | tf_op jit(solution)/shard_map/ppermute | solution.py:47
  192.3 15.3 %collective-permute-start.26 = (bf16[384,512]{1,0:T(8,128)(2,1)}, bf16[384,512]{1,0:T(8,128)(2,1)}, u32[]{:S(2)}, u32[]{:S(2)}) collective-permute-start(bf16[384,512]{1,0:T(8,128)(2,1)} %slice.264), channel_id=1, source_target_pairs={{0,2},{2,0},{1,3},{3,1},{4,6},{6,4},{5,7},{7,5},{8,10},{10,8},{9,1... | collective-permute-start | bytes 1179656 | tf_op jit(solution)/shard_map/ppermute | solution.py:65
  193.8 13.8 %collective-permute-start.27 = (bf16[384,512]{1,0:T(8,128)(2,1)}, bf16[384,512]{1,0:T(8,128)(2,1)}, u32[]{:S(2)}, u32[]{:S(2)}) collective-permute-start(bf16[384,512]{1,0:T(8,128)(2,1)} %slice.265), channel_id=1, source_target_pairs={{0,1},{1,0},{2,3},{3,2},{4,5},{5,4},{6,7},{7,6},{8,9},{9,8},{10,11... | collective-permute-start | bytes 1179656 | tf_op jit(solution)/shard_map/ppermute | solution.py:65
  231.0 26.7 %collective-permute-start.28 = (bf16[1,1,768,512]{3,2,1,0:T(8,128)(2,1)}, bf16[1,1,768,512]{3,2,1,0:T(8,128)(2,1)S(1)}, u32[]{:S(2)}, u32[]{:S(2)}) collective-permute-start(bf16[1,1,768,512]{3,2,1,0:T(8,128)(2,1)} %get-tuple-element.173), channel_id=1, source_target_pairs={{0,2},{2,0},{1,3},{3,1},{4,6},{6,4},{5,7},{7,5},{8,10},{10,8},{9,1... | collective-permute-start | bytes 2359304 | tf_op jit(solution)/shard_map/ppermute | solution.py:74
  231.6 26.2 %collective-permute-start.30 = (bf16[1,1,768,512]{3,2,1,0:T(8,128)(2,1)}, bf16[1,1,768,512]{3,2,1,0:T(8,128)(2,1)S(1)}, u32[]{:S(2)}, u32[]{:S(2)}) collective-permute-start(bf16[1,1,768,512]{3,2,1,0:T(8,128)(2,1)} %get-tuple-element.177), channel_id=1, source_target_pairs={{0,1},{1,0},{2,3},{3,2},{4,5},{5,4},{6,7},{7,6},{8,9},{9,8},{10,11... | collective-permute-start | bytes 2359304 | tf_op jit(solution)/shard_map/ppermute | solution.py:74
  262.9 6.0 %collective-permute-start.32 = (bf16[4,256,1152]{2,1,0:T(8,128)(2,1)}, bf16[4,256,1152]{2,1,0:T(8,128)(2,1)}, u32[]{:S(2)}, u32[]{:S(2)}) collective-permute-start(bf16[4,256,1152]{2,1,0:T(8,128)(2,1)} %combine.4), channel_id=1, source_target_pairs={{0,4},{4,0},{1,5},{5,1},{2,6},{6,2},{3,7},{7,3},{8,12},{12,8},{9,1... | collective-permute-start | bytes 7077896 | tf_op jit(solution)/shard_map/ppermute | solution.py:47
  264.9 61.6 %collective-permute-start.29 = (bf16[3,1,768,512]{3,2,1,0:T(8,128)(2,1)S(1)}, bf16[3,1,768,512]{3,2,1,0:T(8,128)(2,1)}, u32[]{:S(2)}, u32[]{:S(2)}) collective-permute-start(bf16[3,1,768,512]{3,2,1,0:T(8,128)(2,1)S(1)} %pad_maximum_fusion.3), channel_id=1, source_target_pairs={{0,1},{1,0},{2,3},{3,2},{4,5},{5,4},{6,7},{7,6},{8,9},{9,8},{10,11... | collective-permute-start | bytes 7077896 | tf_op jit(solution)/shard_map/ppermute | solution.py:74
  268.0 58.5 %collective-permute-start.31 = (bf16[3,1,768,512]{3,2,1,0:T(8,128)(2,1)}, bf16[3,1,768,512]{3,2,1,0:T(8,128)(2,1)}, u32[]{:S(2)}, u32[]{:S(2)}) collective-permute-start(bf16[3,1,768,512]{3,2,1,0:T(8,128)(2,1)} %pad_maximum_fusion.4), channel_id=1, source_target_pairs={{0,2},{2,0},{1,3},{3,1},{4,6},{6,4},{5,7},{7,5},{8,10},{10,8},{9,1... | collective-permute-start | bytes 7077896 | tf_op jit(solution)/shard_map/ppermute | solution.py:74
  274.9 14.3 %collective-permute-start.33 = (bf16[256,1152]{1,0:T(8,128)(2,1)}, bf16[256,1152]{1,0:T(8,128)(2,1)S(1)}, u32[]{:S(2)}, u32[]{:S(2)}) collective-permute-start(bf16[256,1152]{1,0:T(8,128)(2,1)} %get-tuple-element.183), channel_id=1, source_target_pairs={{0,8},{8,16},{16,24},{24,0},{1,9},{9,17},{17,25},{25,1},{2,10},{10... | collective-permute-start | bytes 1769480 | tf_op jit(solution)/shard_map/ppermute | solution.py:51
  276.5 26.3 %collective-permute-start.34 = (bf16[256,1152]{1,0:T(8,128)(2,1)}, bf16[256,1152]{1,0:T(8,128)(2,1)S(1)}, u32[]{:S(2)}, u32[]{:S(2)}) collective-permute-start(bf16[256,1152]{1,0:T(8,128)(2,1)} %get-tuple-element.184), channel_id=1, source_target_pairs={{0,24},{8,0},{16,8},{24,16},{1,25},{9,1},{17,9},{25,17},{2,26},{10... | collective-permute-start | bytes 1769480 | tf_op jit(solution)/shard_map/ppermute | solution.py:51
  276.5 50.0 %collective-permute-start.35 = (bf16[256,1152]{1,0:T(8,128)(2,1)}, bf16[256,1152]{1,0:T(8,128)(2,1)S(1)}, u32[]{:S(2)}, u32[]{:S(2)}) collective-permute-start(bf16[256,1152]{1,0:T(8,128)(2,1)} %get-tuple-element.185), channel_id=1, source_target_pairs={{0,16},{8,24},{16,0},{24,8},{1,17},{9,25},{17,1},{25,9},{2,18},{10... | collective-permute-start | bytes 1769480 | tf_op jit(solution)/shard_map/ppermute | solution.py:51
  289.2 39.7 %copy-start.31 = (bf16[256,1152]{1,0:T(8,128)(2,1)}, bf16[256,1152]{1,0:T(8,128)(2,1)S(1)}, u32[]{:S(2)}) copy-start(bf16[256,1152]{1,0:T(8,128)(2,1)S(1)} %collective-permute-done.33.refs_1_) | copy-start | bytes 1769476
  302.8 26.1 %copy-start.32 = (bf16[256,1152]{1,0:T(8,128)(2,1)}, bf16[256,1152]{1,0:T(8,128)(2,1)S(1)}, u32[]{:S(2)}) copy-start(bf16[256,1152]{1,0:T(8,128)(2,1)S(1)} %collective-permute-done.34.refs_2_) | copy-start | bytes 1769476
  326.5 56.2 %collective-permute-start.38 = (bf16[4,256,1024]{2,1,0:T(8,128)(2,1)}, bf16[4,256,1024]{2,1,0:T(8,128)(2,1)}, u32[]{:S(2)}, u32[]{:S(2)}) collective-permute-start(bf16[4,256,1024]{2,1,0:T(8,128)(2,1)} %combine.6), channel_id=1, source_target_pairs={{0,4},{4,0},{1,5},{5,1},{2,6},{6,2},{3,7},{7,3},{8,12},{12,8},{9,1... | collective-permute-start | bytes 6291464 | tf_op jit(solution)/shard_map/ppermute | solution.py:47
  334.6 48.0 %collective-permute-start.36 = (bf16[2,1,768,512]{3,2,1,0:T(8,128)(2,1)}, bf16[2,1,768,512]{3,2,1,0:T(8,128)(2,1)}, u32[]{:S(2)}, u32[]{:S(2)}) collective-permute-start(bf16[2,1,768,512]{3,2,1,0:T(8,128)(2,1)} %pad_maximum_fusion.13), channel_id=1, source_target_pairs={{0,1},{1,0},{2,3},{3,2},{4,5},{5,4},{6,7},{7,6},{8,9},{9,8},{10,11... | collective-permute-start | bytes 4718600 | tf_op jit(solution)/shard_map/ppermute | solution.py:74
  336.8 45.9 %collective-permute-start.37 = (bf16[2,1,768,512]{3,2,1,0:T(8,128)(2,1)}, bf16[2,1,768,512]{3,2,1,0:T(8,128)(2,1)}, u32[]{:S(2)}, u32[]{:S(2)}) collective-permute-start(bf16[2,1,768,512]{3,2,1,0:T(8,128)(2,1)} %pad_maximum_fusion.14), channel_id=1, source_target_pairs={{0,2},{2,0},{1,3},{3,1},{4,6},{6,4},{5,7},{7,5},{8,10},{10,8},{9,1... | collective-permute-start | bytes 4718600 | tf_op jit(solution)/shard_map/ppermute | solution.py:74
  382.7 8.1 %collective-permute-start.42 = (bf16[4,128,3200]{2,1,0:T(8,128)(2,1)}, bf16[4,128,3200]{2,1,0:T(8,128)(2,1)}, u32[]{:S(2)}, u32[]{:S(2)}) collective-permute-start(bf16[4,128,3200]{2,1,0:T(8,128)(2,1)} %get-tuple-element.221), channel_id=1, source_target_pairs={{0,4},{4,0},{1,5},{5,1},{2,6},{6,2},{3,7},{7,3},{8,12},{12,8},{9,1... | collective-permute-start | bytes 9830408 | tf_op jit(solution)/shard_map/ppermute | solution.py:47
  384.0 13.7 %collective-permute-start.43 = (bf16[2,128,1024]{2,1,0:T(8,128)(2,1)}, bf16[2,128,1024]{2,1,0:T(8,128)(2,1)}, u32[]{:S(2)}, u32[]{:S(2)}) collective-permute-start(bf16[2,128,1024]{2,1,0:T(8,128)(2,1)} %get-tuple-element.225), channel_id=1, source_target_pairs={{0,1},{1,0},{2,3},{3,2},{4,5},{5,4},{6,7},{7,6},{8,9},{9,8},{10,11... | collective-permute-start | bytes 1572872 | tf_op jit(solution)/shard_map/ppermute | solution.py:91
  384.6 13.4 %collective-permute-start.44 = (bf16[2,128,1024]{2,1,0:T(8,128)(2,1)}, bf16[2,128,1024]{2,1,0:T(8,128)(2,1)}, u32[]{:S(2)}, u32[]{:S(2)}) collective-permute-start(bf16[2,128,1024]{2,1,0:T(8,128)(2,1)} %get-tuple-element.226), channel_id=1, source_target_pairs={{0,2},{2,0},{1,3},{3,1},{4,6},{6,4},{5,7},{7,5},{8,10},{10,8},{9,1... | collective-permute-start | bytes 1572872 | tf_op jit(solution)/shard_map/ppermute | solution.py:91
  398.0 18.9 %collective-permute-start.45 = (bf16[2,64,3200]{2,1,0:T(8,128)(2,1)}, bf16[2,64,3200]{2,1,0:T(8,128)(2,1)}, u32[]{:S(2)}, u32[]{:S(2)}) collective-permute-start(bf16[2,64,3200]{2,1,0:T(8,128)(2,1)} %get-tuple-element.227), channel_id=1, source_target_pairs={{0,1},{1,0},{2,3},{3,2},{4,5},{5,4},{6,7},{7,6},{8,9},{9,8},{10,11... | collective-permute-start | bytes 2457608 | tf_op jit(solution)/shard_map/ppermute | solution.py:91
  399.9 35.4 %collective-permute-start.39 = (bf16[256,1024]{1,0:T(8,128)(2,1)}, bf16[256,1024]{1,0:T(8,128)(2,1)}, u32[]{:S(2)}, u32[]{:S(2)}) collective-permute-start(bf16[256,1024]{1,0:T(8,128)(2,1)} %get-tuple-element.209), channel_id=1, source_target_pairs={{0,8},{8,16},{16,24},{24,0},{1,9},{9,17},{17,25},{25,1},{2,10},{10... | collective-permute-start | bytes 1572872 | tf_op jit(solution)/shard_map/ppermute | solution.py:51
  402.2 36.3 %collective-permute-start.40 = (bf16[256,1024]{1,0:T(8,128)(2,1)}, bf16[256,1024]{1,0:T(8,128)(2,1)}, u32[]{:S(2)}, u32[]{:S(2)}) collective-permute-start(bf16[256,1024]{1,0:T(8,128)(2,1)} %get-tuple-element.210), channel_id=1, source_target_pairs={{0,24},{8,0},{16,8},{24,16},{1,25},{9,1},{17,9},{25,17},{2,26},{10... | collective-permute-start | bytes 1572872 | tf_op jit(solution)/shard_map/ppermute | solution.py:51
  406.4 18.1 %collective-permute-start.47 = (bf16[2,64,3200]{2,1,0:T(8,128)(2,1)S(1)}, bf16[2,64,3200]{2,1,0:T(8,128)(2,1)S(1)}, u32[]{:S(2)}, u32[]{:S(2)}) collective-permute-start(bf16[2,64,3200]{2,1,0:T(8,128)(2,1)S(1)} %copy-done.48), channel_id=1, source_target_pairs={{0,2},{2,0},{1,3},{3,1},{4,6},{6,4},{5,7},{7,5},{8,10},{10,8},{9,1... | collective-permute-start | bytes 2457608 | tf_op jit(solution)/shard_map/ppermute | solution.py:91
  418.0 15.1 %collective-permute-start.46 = (bf16[64,3200]{1,0:T(8,128)(2,1)S(1)}, bf16[64,3200]{1,0:T(8,128)(2,1)S(1)}, u32[]{:S(2)}, u32[]{:S(2)}) collective-permute-start(bf16[64,3200]{1,0:T(8,128)(2,1)S(1)} %fusion.6), channel_id=1, source_target_pairs={{0,2},{2,0},{1,3},{3,1},{4,6},{6,4},{5,7},{7,5},{8,10},{10,8},{9,1... | collective-permute-start | bytes 1228808 | tf_op jit(solution)/shard_map/ppermute | solution.py:98
  424.6 9.2 %collective-permute-start.48 = (bf16[64,3200]{1,0:T(8,128)(2,1)S(1)}, bf16[64,3200]{1,0:T(8,128)(2,1)S(1)}, u32[]{:S(2)}, u32[]{:S(2)}) collective-permute-start(bf16[64,3200]{1,0:T(8,128)(2,1)S(1)} %fusion.7), channel_id=1, source_target_pairs={{0,1},{1,0},{2,3},{3,2},{4,5},{5,4},{6,7},{7,6},{8,9},{9,8},{10,11... | collective-permute-start | bytes 1228808 | tf_op jit(solution)/shard_map/ppermute | solution.py:99
  426.3 16.6 %collective-permute-start.56 = (bf16[128,1024]{1,0:T(8,128)(2,1)S(1)}, bf16[128,1024]{1,0:T(8,128)(2,1)S(1)}, u32[]{:S(2)}, u32[]{:S(2)}) collective-permute-start(bf16[128,1024]{1,0:T(8,128)(2,1)S(1)} %fusion.13), channel_id=1, source_target_pairs={{0,2},{2,0},{1,3},{3,1},{4,6},{6,4},{5,7},{7,5},{8,10},{10,8},{9,1... | collective-permute-start | bytes 786440 | tf_op jit(solution)/shard_map/ppermute | solution.py:98
  433.2 11.1 %collective-permute-start.57 = (bf16[128,1024]{1,0:T(8,128)(2,1)S(1)}, bf16[128,1024]{1,0:T(8,128)(2,1)S(1)}, u32[]{:S(2)}, u32[]{:S(2)}) collective-permute-start(bf16[128,1024]{1,0:T(8,128)(2,1)S(1)} %fusion.14), channel_id=1, source_target_pairs={{0,1},{1,0},{2,3},{3,2},{4,5},{5,4},{6,7},{7,6},{8,9},{9,8},{10,11... | collective-permute-start | bytes 786440 | tf_op jit(solution)/shard_map/ppermute | solution.py:99
  435.2 9.1 %collective-permute-start.51 = (bf16[32,3200]{1,0:T(8,128)(2,1)S(1)}, bf16[32,3200]{1,0:T(8,128)(2,1)S(1)}, u32[]{:S(2)}, u32[]{:S(2)}) collective-permute-start(bf16[32,3200]{1,0:T(8,128)(2,1)S(1)} %get-tuple-element.303), channel_id=1, source_target_pairs={{0,24},{8,0},{16,8},{24,16},{1,25},{9,1},{17,9},{25,17},{2,26},{10... | collective-permute-start | bytes 614408 | tf_op jit(solution)/shard_map/ppermute | solution.py:51
  435.3 19.5 %collective-permute-start.50 = (bf16[32,3200]{1,0:T(8,128)(2,1)S(1)}, bf16[32,3200]{1,0:T(8,128)(2,1)S(1)}, u32[]{:S(2)}, u32[]{:S(2)}) collective-permute-start(bf16[32,3200]{1,0:T(8,128)(2,1)S(1)} %get-tuple-element.304), channel_id=1, source_target_pairs={{0,16},{8,24},{16,0},{24,8},{1,17},{9,25},{17,1},{25,9},{2,18},{10... | collective-permute-start | bytes 614408 | tf_op jit(solution)/shard_map/ppermute | solution.py:51
  438.6 16.2 %collective-permute-start.49 = (bf16[32,3200]{1,0:T(8,128)(2,1)S(1)}, bf16[32,3200]{1,0:T(8,128)(2,1)S(1)}, u32[]{:S(2)}, u32[]{:S(2)}) collective-permute-start(bf16[32,3200]{1,0:T(8,128)(2,1)S(1)} %get-tuple-element.302), channel_id=1, source_target_pairs={{0,8},{8,16},{16,24},{24,0},{1,9},{9,17},{17,25},{25,1},{2,10},{10... | collective-permute-start | bytes 614408 | tf_op jit(solution)/shard_map/ppermute | solution.py:51
  442.9 52.9 %copy-start.45 = (bf16[128,1024]{1,0:T(8,128)(2,1)}, bf16[128,1024]{1,0:T(8,128)(2,1)S(1)}, u32[]{:S(2)}) copy-start(bf16[128,1024]{1,0:T(8,128)(2,1)S(1)} %collective-permute-done.56) | copy-start | bytes 786436
  442.9 64.2 %collective-permute-start.41 = (bf16[256,1024]{1,0:T(8,128)(2,1)}, bf16[256,1024]{1,0:T(8,128)(2,1)}, u32[]{:S(2)}, u32[]{:S(2)}) collective-permute-start(bf16[256,1024]{1,0:T(8,128)(2,1)} %get-tuple-element.212), channel_id=1, source_target_pairs={{0,16},{8,24},{16,0},{24,8},{1,17},{9,25},{17,1},{25,9},{2,18},{10... | collective-permute-start | bytes 1572872 | tf_op jit(solution)/shard_map/ppermute | solution.py:51
  455.0 17.7 %collective-permute-start.54 = (bf16[32,3200]{1,0:T(8,128)(2,1)S(1)}, bf16[32,3200]{1,0:T(8,128)(2,1)S(1)}, u32[]{:S(2)}, u32[]{:S(2)}) collective-permute-start(bf16[32,3200]{1,0:T(8,128)(2,1)S(1)} %fusion.12), channel_id=1, source_target_pairs={{0,8},{8,16},{16,24},{24,0},{1,9},{9,17},{17,25},{25,1},{2,10},{10... | collective-permute-start | bytes 614408 | tf_op jit(solution)/shard_map/ppermute | solution.py:51
  465.5 30.3 %collective-permute-start.53 = (bf16[32,3200]{1,0:T(8,128)(2,1)S(1)}, bf16[32,3200]{1,0:T(8,128)(2,1)S(1)}, u32[]{:S(2)}, u32[]{:S(2)}) collective-permute-start(bf16[32,3200]{1,0:T(8,128)(2,1)S(1)} %fusion.12), channel_id=1, source_target_pairs={{0,16},{8,24},{16,0},{24,8},{1,17},{9,25},{17,1},{25,9},{2,18},{10... | collective-permute-start | bytes 614408 | tf_op jit(solution)/shard_map/ppermute | solution.py:51
  468.6 27.2 %collective-permute-start.52 = (bf16[32,3200]{1,0:T(8,128)(2,1)S(1)}, bf16[32,3200]{1,0:T(8,128)(2,1)S(1)}, u32[]{:S(2)}, u32[]{:S(2)}) collective-permute-start(bf16[32,3200]{1,0:T(8,128)(2,1)S(1)} %fusion.12), channel_id=1, source_target_pairs={{0,24},{8,0},{16,8},{24,16},{1,25},{9,1},{17,9},{25,17},{2,26},{10... | collective-permute-start | bytes 614408 | tf_op jit(solution)/shard_map/ppermute | solution.py:51
  498.9 4.9 collective-permute-start.55
  (45 other events, 264.8 us)

commit v7 on v6

--- a/solution.py
+++ b/solution.py
@@ -317,7 +317,7 @@
     n = 4 if split else len(weights)
     extra = [array for chunk in chunks for array, _ in chunk]
     given = len(weights) + len(extra)
-    pack_rows, eff = weights[0].shape[1:]
+    pack_rows, eff = chunks[0][0][0].shape if split else weights[0].shape[1:]
     folds = width // eff
     total_rows = pieces * capacity
     first_half = count // 2
@@ -362,12 +362,13 @@
         for j in range(len(weights)):
             load(j, lambda lo, hi, ref=pack[j]: ref[0, lo:hi])
         for c in range(len(chunks)):
-            from_x, from_y, diag_a, diag_b = [
-                rows_from(pack[1 + 4 * c + i], chunks[c][i][1]) for i in range(4)
+            own, from_x, from_y, diag_a, diag_b = [
+                rows_from(pack[5 * c + i], chunks[c][i][1]) for i in range(5)
             ]
 
             @pl.when(pl.program_id(0) == c)
             def _():
+                load(0, own)
                 load(1, from_x)
                 load(2, from_y)
                 load(3, two_halves(diag_a, diag_b))
@@ -664,7 +665,7 @@
             grad_ref, residual_ref, gates_ref, misc_ref, tail_ref, wo_ref, att_ref, moe_ref,
             normed_ref, q_ref, k_ref, v_ref, total_ref,
             x_ref, wq_ref, wk_ref, wv_ref, bias_ref, cos_ref, sin_ref,
-            keep_out, give_out, first_a_out, first_b_out, rest_a_out, rest_b_out, residual_out,
+            dense_out, first_a_out, first_b_out, rest_a_out, rest_b_out, residual_out,
             normed_t, grad_sum, og_ref, logit_ref, gain_ref,
         ) = refs[terms:]
         step = pl.program_id(0)
@@ -736,11 +737,7 @@
 
         def put(at, lanes, rows):
             for c in range(2):
-
-                @pl.when(core == c)
-                def _():
-                    keep_out[at, :, lanes] = rows[c].astype(B16)
-                    give_out[at, :, lanes] = rows[1 - c].astype(B16)
+                dense_out[core ^ c, at, :, lanes] = rows[c].astype(B16)
 
         def give(grad, lanes):
             for m in range(4):
@@ -798,11 +795,11 @@
         return pl.BlockSpec((rows, cols), lambda i, here: (0, lead + i))
 
     shapes = [
-        *[jax.ShapeDtypeStruct((4, block, output_at + width + EXTRA), B16)] * 2,
+        jax.ShapeDtypeStruct((2, 4, block, output_at + width + EXTRA), B16),
         *[jax.ShapeDtypeStruct((2, tok_rows // 2, width), B16)] * 4,
         jax.ShapeDtypeStruct((tok_rows, width), F32),
     ]
-    keep, give, *parts, residual_grad = pl.pallas_call(
+    dense, *parts, residual_grad = pl.pallas_call(
         kernel,
         out_shape=shapes,
         grid_spec=pltpu.PrefetchScalarGridSpec(
@@ -849,17 +846,16 @@
         moe_in, normed_all, query_rot, key_rot, value_all, totals,
         x_all, dense_full, dense_full, dense_full, bias, cosine, sine,
     )
-    return keep, give, tuple(parts[:2]), parts[2], parts[3], residual_grad
-
-
-def core_halves(keep, got, hold):
-    _, rows, cols = keep.shape
+    return dense, tuple(parts[:2]), parts[2], parts[3], residual_grad
+
+
+def core_halves(blocks, got):
+    _, _, rows, cols = blocks.shape
     half = rows // 2
-    keep = after(keep, hold)
 
     def kernel(keep_ref, got_ref, first_a, first_b, rest_a, rest_b):
         def total(j, lo):
-            mine = keep_ref[j, lo : lo + half, :].astype(F32)
+            mine = keep_ref[0, j, lo : lo + half, :].astype(F32)
             return (mine + got_ref[j, lo : lo + half, :].astype(F32)).astype(B16)
 
         first_a[0], first_a[1] = total(1, 0), total(3, 0)
@@ -871,12 +867,15 @@
     first_a, first_b, rest_a, rest_b = pl.pallas_call(
         kernel,
         grid=(5,),
-        in_specs=[pl.BlockSpec((4, rows, step), lambda i: (0, 0, i))] * 2,
+        in_specs=[
+            pl.BlockSpec((1, 4, rows, step), lambda i: (0, 0, 0, i)),
+            pl.BlockSpec((4, rows, step), lambda i: (0, 0, i)),
+        ],
         out_specs=[pl.BlockSpec((2, half, step), lambda i: (0, 0, i))] * 4,
         out_shape=[jax.ShapeDtypeStruct((2, half, cols), B16)] * 4,
         compiler_params=pltpu.CompilerParams(vmem_limit_bytes=VMEM_LIMIT),
         name="core_halves",
-    )(keep, got)
+    )(blocks, got)
     return (first_a, first_b), rest_a, rest_b
 
 
@@ -1000,11 +999,36 @@
         lead = ((2 * z + core) * local).astype(jnp.int32)[None]
         grad_pieces = column_pieces(jnp.concatenate([out_grad, code], axis=0), z_size)
 
+        query_pos = dp_index * tok_rows + jnp.arange(tok_rows, dtype=jnp.int32)
+        in_float = layer_input.astype(F32)
+        steps = jnp.arange(tok_rows, dtype=jnp.int32)
+        eff = w_gate.shape[2]
+        in_rows, mid_rows = w_gate.shape[1], w_down.shape[1]
+        folds = [w_down[:, :, f * eff : (f + 1) * eff] for f in range(model_width // eff)]
+        if small_grid:
+            relative = dp_index ^ jnp.arange(4, dtype=jnp.int32)
+            key_pos = (relative[:, None] * tok_rows + steps[None, :]).reshape(seq_len)
+        else:
+            relative = jnp.arange(dp_size, dtype=jnp.int32)
+            key_pos = jnp.arange(seq_len, dtype=jnp.int32)
+        order = jnp.concatenate([relative, lead])
+        visible = (key_pos[None, :] <= query_pos[:, None]) | (key_pos[None, :] < prefix_len[0])
         if small_grid:
             side = tok_rows // 2
             x_pack = jnp.concatenate([layer_input[:side], layer_input[side:]], axis=1)
             start_parts = gather_near(jnp.concatenate([x_pack, core_half(dense_pack, core)], axis=1))
-            start_parts += gather_far(after(start_parts, *grad_pieces[1::2]))
+            tables = (
+                *turn_tables(key_pos.astype(F32)),
+                jnp.where(visible.T, 0.0, MASKED_SCORE),
+                jnp.pad(routed.astype(F32), ((0, 0), (0, 128 - EXPERTS))),
+                [
+                    jnp.concatenate([part[e] for part in (w_gate, w_up, *folds)], axis=0)
+                    for e in range(local)
+                ],
+            )
+            tables, grad_near = lax.optimization_barrier((tables, grad_pieces[1::2]))
+            cosine, sine, bias, routed_wide, packs = tables
+            start_parts += gather_far(after(start_parts, tables, *grad_near))
             dense_parts = [part[:, 2 * model_width :] for part in start_parts]
             dense_full = dense_assemble(dense_pack, dense_parts, dp_index, core)
         else:
@@ -1015,34 +1039,20 @@
             full_key = head_full[:, wide : wide + narrow]
             full_value = head_full[:, wide + narrow : wide + 2 * narrow]
 
-        query_pos = dp_index * tok_rows + jnp.arange(tok_rows, dtype=jnp.int32)
-        in_float = layer_input.astype(F32)
-        steps = jnp.arange(tok_rows, dtype=jnp.int32)
-        eff = w_gate.shape[2]
-        in_rows, mid_rows = w_gate.shape[1], w_down.shape[1]
-        folds = [w_down[:, :, f * eff : (f + 1) * eff] for f in range(model_width // eff)]
-        pack = jnp.concatenate([w_gate, w_up, *folds], axis=1)
         if small_grid:
-            relative = dp_index ^ jnp.arange(4, dtype=jnp.int32)
-            key_pos = (relative[:, None] * tok_rows + steps[None, :]).reshape(seq_len)
             halves, per = 2, local // 2
-            weights = [pack]
-            near_0 = gather_near(after(pack[0], *start_parts[2:]))
+            weights = []
+            near_0 = gather_near(after(packs[0], *start_parts[2:]))
             far_0 = gather_far(after(near_0, dense_full))
-            near_1 = gather_near(after(pack[1], *near_0, dense_full))
+            near_1 = gather_near(after(packs[1], *near_0, dense_full))
         else:
-            relative = jnp.arange(dp_size, dtype=jnp.int32)
-            key_pos = jnp.arange(seq_len, dtype=jnp.int32)
             halves, per = 1, local
+            pack = jnp.concatenate([w_gate, w_up, *folds], axis=1)
             every = lax.all_gather(pack, ("y", "x"), axis=0, tiled=False)
             weights = [every[j] for j in range(dp_size)]
-            near_0 = ()
-        order = jnp.concatenate([relative, lead])
-        visible = (key_pos[None, :] <= query_pos[:, None]) | (key_pos[None, :] < prefix_len[0])
         chunks = []
         if small_grid:
-            bias = after(jnp.where(visible.T, 0.0, MASKED_SCORE), *near_0)
-            cosine, sine = turn_tables(key_pos.astype(F32))
+            bias = after(bias, *near_0)
             (
                 x_all, normed_all, query_rot, key_rot, value_all, attended, totals, misc, residual,
                 moe_in, gates,
@@ -1053,7 +1063,7 @@
                 bias,
                 cosine,
                 sine,
-                jnp.pad(routed.astype(F32), ((0, 0), (0, 128 - EXPERTS))),
+                routed_wide,
             )
             moe_in = after(moe_in, *near_1, *far_0)
             router_rows = misc[:EXPERTS].astype(B16)
@@ -1105,8 +1115,8 @@
         grads_other = swap_core(grads_mine)
         stage_1 = stage_2 = last_far = ()
         if small_grid:
-            middle = pack.shape[1] // 2
-            stage_1 = far_and_next(after(near_1, moe_in), pack[2])
+            middle = packs[0].shape[0] // 2
+            stage_1 = far_and_next(after(near_1, moe_in), packs[2])
         (slot_grads_mine,) = dispatch_rows(lead, grads_mine, None, None, local, capacity)
         (slot_grads_other,) = dispatch_rows(
             lead,
@@ -1117,13 +1127,17 @@
             capacity,
         )
         if small_grid:
-            stage_2 = far_and_next(after(stage_1, slot_grads_other), pack[3])
+            stage_2 = far_and_next(after(stage_1, slot_grads_other), packs[3])
             last_far = gather_far([part[middle:] for part in stage_2])
             chunks = [
-                [(part, 0) for part in [*near_0, *far_0]],
-                [(part, 0) for part in [*near_1, *stage_1[::-1]]],
-                [(part, middle) for part in stage_1] + [(part, 0) for part in stage_2[::-1]],
-                [(part, middle) for part in stage_2] + [(part, 0) for part in last_far],
+                [(part, 0) for part in [packs[0], *near_0, *far_0]],
+                [(part, 0) for part in [packs[1], *near_1, *stage_1[::-1]]],
+                [(packs[2], 0)]
+                + [(part, middle) for part in stage_1]
+                + [(part, 0) for part in stage_2[::-1]],
+                [(packs[3], 0)]
+                + [(part, middle) for part in stage_2]
+                + [(part, 0) for part in last_far],
             ]
         row_pieces = after(row_pieces, slot_grads_other)
         rows_mine = after(row_pieces, *stage_2)
@@ -1176,17 +1190,20 @@
             via = cross(early[3], early[7])
             dxs = after(dxs, *via)
             early_got = second_step(early, via, late[3], late[7])
-        dx_other = swap_core(combine_rows(lead, z_size, grads_other, dxs, local, capacity))
+        dx_other = combine_rows(lead, z_size, grads_other, dxs, local, capacity)
+        y_other = combine_rows(lead, z_size, grads_other, after(ys, dx_other), local, capacity)
+        dx_other = after(swap_core(dx_other), y_other)
         dx_low = combine_rows(lead, 0, grads_mine, dxs, local, capacity, dx_other)
+        dx_low, y_other = after((dx_low, swap_core(y_other)), dx_low[0])
         dx_pieces = column_send_some(dx_low, z_size) + column_send_last(dx_low, z_size)
-        y_other = combine_rows(lead, z_size, grads_other, after(ys, dx_low), local, capacity)
-        dx_pieces, y_other = after((dx_pieces, y_other), y_other, *dx_pieces)
-        y_other = swap_core(y_other)
+        y_low = combine_rows(lead, 0, grads_mine, ys, local, capacity, y_other)
+        dx_pieces = after(dx_pieces, *y_low)
+        y_pieces = column_send_some(after(y_low, *dx_pieces), z_size)
         if small_grid:
             early_got = after(early_got, *dx_pieces)
             late_got = second_step(late, [got[2:3] for got in early_got])
         if small_grid:
-            keep, give, normed_first, normed_a, normed_b, residual_grad = attention_backward(
+            dense_blocks, normed_first, normed_a, normed_b, residual_grad = attention_backward(
                 jnp.stack([dp_index, core]).astype(jnp.int32),
                 (dx_low[0], *dx_pieces),
                 out_grad,
@@ -1201,12 +1218,12 @@
                 cosine,
                 sine,
             )
-            late_got, y_other = after((late_got, y_other), residual_grad)
-            normed_first, keep, give = after((normed_first, keep, give), *late_got, y_other)
-            y_low = combine_rows(lead, 0, grads_mine, ys, local, capacity, y_other)
-            y_pieces = column_send_some(y_low, z_size)
+            late_got, y_pieces = after((late_got, y_pieces), residual_grad)
+            normed_first, dense_blocks = after((normed_first, dense_blocks), *late_got, *y_pieces)
             y_pieces += column_send_last(y_low, z_size, *y_pieces)
-            dense_first, dense_a, dense_b = core_halves(keep, swap_core(give), y_low[0])
+            dense_first, dense_a, dense_b = core_halves(
+                dense_blocks, swap_core(dense_blocks[1])
+            )
             normed_got = grid_scatter_first(*normed_first)
             dense_got = grid_scatter_first(*after(dense_first, *normed_got))
             dense_low = across_z(
@@ -1215,15 +1232,14 @@
             (
                 query_sum, key_sum, value_sum, output_sum, router_sum, attn_gain_sum, moe_gain_sum,
             ) = dense_outputs(core, dense_low, swap_core(dense_low), wide, narrow)
-            y_pieces = after(y_pieces, query_sum)
+            y_pieces = after(y_pieces, *dense_got)
             normed_grad = jnp.concatenate(
                 grid_scatter_second(normed_got, normed_a, normed_b, *dense_got), axis=0
             )
             first_value, first_pull = jax.vjp(lambda v: rms_norm(v, full_attn_gain), in_float)
             input_grad = residual_grad + first_pull(normed_grad)[0]
         else:
-            y_low = combine_rows(lead, 0, grads_mine, ys, local, capacity, y_other)
-            y_pieces = column_send_some(y_low, z_size) + column_send_last(y_low, z_size)
+            y_pieces += column_send_last(y_low, z_size)
             moe_sum = column_sum(dx_low[0], dx_pieces)
             moe_in_grad = moe_sum[:, :model_width]
             gate_grad = (

time: 523 us -> 502 us (0.960)
  the two profiles are of different devices: /device:TPU:25 before, /device:TPU:24 now
where the time goes in v7:
time: 502 us; the launch traced here: 493 us
  waiting for transfers between devices  176 us (35%)
  Pallas kernels  168 us (33%)
  starting transfers between devices  60.5 us (12%)
  local copies, waits for them, and re-layouts  43.2 us (9%)
  other arithmetic  42.6 us (8%)
    ppermute x18, waiting for transfers between devices, cyclic(): lax.ppermute(rows, 'z', [(i, (i + shift) % size) for i in range(size)])  120 us
    pallas_call x2, Pallas kernels, experts(): pl.pallas_call(kernel, out_shape=out_shape, grid_spec=pltpu.PrefetchScala...  48.8 us
    pallas_call x1, Pallas kernels, attention_backward(): pl.pallas_call(kernel, out_shape=shapes, grid_spec=pltpu.PrefetchScalarGr...  36.8 us
    ppermute x18, starting transfers between devices, cyclic(): lax.ppermute(rows, 'z', [(i, (i + shift) % size) for i in range(size)])  27.1 us
    pallas_call x1, Pallas kernels, attention_forward(): pl.pallas_call(kernel, grid=(GROUPS,), in_specs=[fixed(tok_rows, width),...  25.4 us
    ppermute x4, waiting for transfers between devices, grid_scatter_first(): return (lax.ppermute(first_a, 'x', SWAP), lax.ppermute(first_b, 'y', SWAP))  24.8 us
    pallas_call x4, Pallas kernels, combine_rows(): pl.pallas_call(kernel, out_shape=out_shape, grid_spec=pltpu.PrefetchScala...  21.7 us
    pallas_call x4, Pallas kernels, dispatch_rows(): pl.pallas_call(kernel, out_shape=out_shape, grid_spec=pltpu.PrefetchScala...  19.2 us
  transfers between devices with their start and end apart: 58, of which 25 were waited for; matrix products, arithmetic and copies ran while one was open for 9% of the time, Pallas kernels for 27%

profile of v7, /device:TPU:24, one launch (start us, length us, event | category | flops | bytes accessed | tf_op | source)
XLA Modules:
  0.0 492.8 jit_solution(9840479802393508432)
XLA Ops:
  4.2 2.1 concatenate.66.shard_ref
  10.2 1.5 collective-permute-start.1
  11.9 2.6 convert_reduce_fusion
  16.1 3.4 collective-permute-start.3
  26.0 3.1 fusion.5
  30.3 2.9 collective-permute-done.2
  33.2 8.6 %collective-permute-done.3 = bf16[272,1024]{1,0:T(8,128)(2,1)} collective-permute-done((bf16[272,1024]{1,0:T(8,128)(2,1)}, bf16[272,1024]{1,0:T(8,128)(2,1)}, u32[]{:S(2)}, u32[]{:S(2)}) %collective-permute-start.3) | collective-permute-done | bytes 557088 | tf_op jit(solution)/shard_map/ppermute | solution.py:51
  43.6 13.7 %collective-permute-done.5.ea_ref.eb_ref = bf16[64,5248]{1,0:T(8,128)(2,1)S(1)} collective-permute-done((bf16[64,5248]{1,0:T(8,128)(2,1)S(1)}, bf16[64,5248]{1,0:T(8,128)(2,1)S(1)}, u32[]{:S(2)}, u32[]{:S(2)}) %collective-permute-start.5) | collective-permute-done | bytes 671776 | tf_op jit(solution)/shard_map/ppermute | solution.py:65
  59.2 1.6 pad_maximum_fusion.1.moved_ref
  63.9 1.8 collective-permute-done.6.other_ref
  65.7 1.5 copy-done.15
  67.2 6.8 %assemble.1.tail_ref.wo_ref.wq_ref.wk_ref.wv_ref.refs_8_.refs_9_.refs_18_.refs_19_.refs_20_ = bf16[1024,3200]{1,0:T(8,128)(2,1)} custom-call(s32[7]{0:T(128)} %stack.78.places_ref, bf16[256,3200]{1,0:T(8,128)(2,1)} %copy-done.3, bf16[384,3200]{1,0:T(8,128)(2,1)} %pad_maximum_fusion.1.moved_ref, bf16[384,3200]{1,0:T(8,128)(2,1)} %copy-done.15), custom_call_target="tpu_custom_call" | custom-call | tf_op jit(solution)/shard_map/assemble/pallas_call | solution.py:148
  73.9 7.1 %collective-permute-done.7.refs_7_ = bf16[768,512]{1,0:T(8,128)(2,1)} collective-permute-done((bf16[768,512]{1,0:T(8,128)(2,1)}, bf16[768,512]{1,0:T(8,128)(2,1)}, u32[]{:S(2)}, u32[]{:S(2)}) %collective-permute-start.7) | collective-permute-done | bytes 786464 | tf_op jit(solution)/shard_map/ppermute | solution.py:59
  85.6 1.8 slice.259
  87.4 1.5 collective-permute-start.12
  89.0 1.8 slice.260
  91.7 25.4 %attention.1 = (bf16[1024,1024]{1,0:T(8,128)(2,1)}, bf16[1024,1024]{1,0:T(8,128)(2,1)}, bf16[256,1024]{1,0:T(8,128)(2,1)}, bf16[1024,512]{1,0:T(8,128)(2,1)}, bf...) custom-call(bf16[256,1024]{1,0:T(8,128)(2,1)} %own_ref.1, ...), custom_call_target="tpu_custom_call" | custom-call | tf_op jit(solution)/shard_map/attention/pallas_call | solution.py:595
  118.4 1.8 pad_maximum_fusion.4.packed_ref.code_ref
  122.0 1.6 pad_maximum_fusion.15
  125.5 3.9 collective-permute-start.16
  129.4 4.5 dispatch.4.refs_2_
  133.9 8.1 %collective-permute-done.14.rest_1_ = bf16[256,1024]{1,0:T(8,128)(2,1)} collective-permute-done((bf16[256,1024]{1,0:T(8,128)(2,1)}, bf16[256,1024]{1,0:T(8,128)(2,1)}, u32[]{:S(2)}, u32[]{:S(2)}) %collective-permute-start.14) | collective-permute-done | bytes 524320 | tf_op jit(solution)/shard_map/ppermute | solution.py:51
  142.1 7.4 %collective-permute-done.16.rest_3_ = bf16[256,1024]{1,0:T(8,128)(2,1)} collective-permute-done((bf16[256,1024]{1,0:T(8,128)(2,1)}, bf16[256,1024]{1,0:T(8,128)(2,1)}, u32[]{:S(2)}, u32[]{:S(2)}) %collective-permute-start.16) | collective-permute-done | bytes 524320 | tf_op jit(solution)/shard_map/ppermute | solution.py:51
  151.5 4.5 dispatch.5.refs_3_
  159.0 1.5 collective-permute-start.15
  160.5 22.2 %collective-permute-done.15.rest_2_ = bf16[256,1024]{1,0:T(8,128)(2,1)S(1)} collective-permute-done((bf16[256,1024]{1,0:T(8,128)(2,1)}, bf16[256,1024]{1,0:T(8,128)(2,1)S(1)}, u32[]{:S(2)}, u32[]{:S(2)}) %collective-permute-start.15) | collective-permute-done | bytes 524320 | tf_op jit(solution)/shard_map/ppermute | solution.py:51
  188.2 1.5 slice.372.rest_4_
  189.8 5.1 %dispatch.6 = (bf16[4,320,1024]{2,1,0:T(8,128)(2,1)}, f32[4,320,128]{2,1,0:T(8,128)}) custom-call(s32[1]{0:T(128)} %bitcast.26.lead_ref, bf16[4,272,1024]{2,1,0:T(8,128)(2,1)} %copy-done, bf16[256,1024]{1,0:T(8,128)(2,1)} %get-tuple-element.174.rest_0_.refs_11_, bf16[256,1024]{1,0:T(8,128)(2,1)} %collective-permute-done.14.rest_1_, ...), custom_call_target="tpu_custom_call" | custom-call | tf_op jit(solution)/shard_map/dispatch/pallas_call | solution.py:241
  195.7 5.1 %dispatch.7 = (bf16[4,320,1024]{2,1,0:T(8,128)(2,1)}, f32[4,320,128]{2,1,0:T(8,128)}) custom-call(s32[1]{0:T(128)} %bitcast.26.lead_ref, bf16[4,272,1024]{2,1,0:T(8,128)(2,1)} %collective-permute-done.17.packed_ref.code_ref, bf16[256,1024]{1,0:T(8,128)(2,1)} %copy-done.44, bf16[256,1024]{1,0:T(8,128)(2,1)} %copy-done.45, ...), custom_call_target="tpu_custom_call" | custom-call | tf_op jit(solution)/shard_map/dispatch/pallas_call | solution.py:241
  200.8 23.7 %experts.2 = (bf16[8,160,1024]{2,1,0:T(8,128)(2,1)}, bf16[8,160,1152]{2,1,0:T(8,128)(2,1)}, bf16[1,1,768,512]{3,2,1,0:T(8,128)(2,1)}, bf16[1,1,768,512]{3,2,1,0:...) custom-call(s32[5]{0:T(128)} %pad_add_fusion.order_ref, ...), custom_call_target="tpu_custom_call" | custom-call | tf_op jit(solution)/shard_map/experts/pallas_call | solution.py:471
  226.4 25.1 %experts.3 = (bf16[8,160,1024]{2,1,0:T(8,128)(2,1)}, bf16[8,160,1152]{2,1,0:T(8,128)(2,1)}, bf16[1,1,768,512]{3,2,1,0:T(8,128)(2,1)}, bf16[1,1,768,512]{3,2,1,0:...) custom-call(s32[5]{0:T(128)} %pad_add_fusion.order_ref, ...), custom_call_target="tpu_custom_call" | custom-call | tf_op jit(solution)/shard_map/experts/pallas_call | solution.py:471
  251.5 5.2 %combine.4 = bf16[4,256,1152]{2,1,0:T(8,128)(2,1)} custom-call(s32[1]{0:T(128)} %bitcast.26.lead_ref, bf16[4,272,1024]{2,1,0:T(8,128)(2,1)} %collective-permute-done.17.packed_ref.code_ref, bf16[8,160,1152]{2,1,0:T(8,128)(2,1)} %get-tuple-element.194.rest_0_, bf16[8,160,1152]{2,1,0:T(8,128)(2,1)} %get-tuple-element.195.rest_1_), custom_call_target="tpu_custom_call" | custom-call | tf_op jit(solution)/shard_map/combine/pallas_call | solution.py:299
  259.4 4.9 combine.5
  265.7 1.6 pad_maximum_fusion.3
  268.5 6.1 %combine.6 = (bf16[256,1152]{1,0:T(8,128)(2,1)}, bf16[256,1152]{1,0:T(8,128)(2,1)}, bf16[256,1152]{1,0:T(8,128)(2,1)}, bf16[256,1152]{1,0:T(8,128)(2,1)}) custom-call(s32[1]{0:T(128)} %bitcast.26.lead_ref, bf16[4,272,1024]{2,1,0:T(8,128)(2,1)} %copy-done, bf16[8,160,1152]{2,1,0:T(8,128)(2,1)} %get-tuple-element.194.rest_0_, ...), custom_call_target="tpu_custom_call" | custom-call | tf_op jit(solution)/shard_map/combine/pallas_call | solution.py:299
  274.6 1.9 collective-permute-start.34
  277.1 5.6 %combine.7 = (bf16[256,1024]{1,0:T(8,128)(2,1)}, bf16[256,1024]{1,0:T(8,128)(2,1)}, bf16[256,1024]{1,0:T(8,128)(2,1)}, bf16[256,1024]{1,0:T(8,128)(2,1)}) custom-call(s32[1]{0:T(128)} %bitcast.26.lead_ref, bf16[4,272,1024]{2,1,0:T(8,128)(2,1)} %copy-done, bf16[8,160,1024]{2,1,0:T(8,128)(2,1)} %get-tuple-element.196.rest_0_, ...), custom_call_target="tpu_custom_call" | custom-call | tf_op jit(solution)/shard_map/combine/pallas_call | solution.py:299
  282.8 19.1 %collective-permute-done.34.refs_1_ = bf16[256,1152]{1,0:T(8,128)(2,1)S(1)} collective-permute-done((bf16[256,1152]{1,0:T(8,128)(2,1)}, bf16[256,1152]{1,0:T(8,128)(2,1)S(1)}, u32[]{:S(2)}, u32[]{:S(2)}) %collective-permute-start.34) | collective-permute-done | bytes 589856 | tf_op jit(solution)/shard_map/ppermute | solution.py:51
  301.8 1.8 collective-permute-done.35.refs_2_
  303.6 23.6 %collective-permute-done.36.refs_3_ = bf16[256,1152]{1,0:T(8,128)(2,1)S(1)} collective-permute-done((bf16[256,1152]{1,0:T(8,128)(2,1)}, bf16[256,1152]{1,0:T(8,128)(2,1)S(1)}, u32[]{:S(2)}, u32[]{:S(2)}) %collective-permute-start.36) | collective-permute-done | bytes 589856 | tf_op jit(solution)/shard_map/ppermute | solution.py:51
  328.1 4.4 add_bitcast_fusion.3
  336.1 1.7 collective-permute-start.38
  337.8 2.1 collective-permute-start.39
  340.6 36.8 %attention_grad.1 = (bf16[2,4,128,3200]{3,2,1,0:T(8,128)(2,1)}, bf16[2,128,1024]{2,1,0:T(8,128)(2,1)}, bf16[2,128,1024]{2,1,0:T(8,128)(2,1)}, bf16[2,128,1024]{2...) custom-call(s32[2]{0:T(128)} %pad_add_fusion.1.here_ref, ...), custom_call_target="tpu_custom_call" | custom-call | tf_op jit(solution)/shard_map/attention_grad/pallas_call | solution.py:802
  377.5 4.1 slice_bitcast_fusion
  384.9 2.8 collective-permute-done.42.got_ref
  387.7 6.0 %core_halves.1 = (bf16[2,64,3200]{2,1,0:T(8,128)(2,1)}, bf16[2,64,3200]{2,1,0:T(8,128)(2,1)}, bf16[2,64,3200]{2,1,0:T(8,128)(2,1)}, bf16[2,64,3200]{2,1,0:T(8,128)(2,1)}) custom-call(bf16[2,4,128,3200]{3,2,1,0:T(8,128)(2,1)} %get-tuple-element.247.keep_ref, bf16[4,128,3200]{2,1,0:T(8,128)(2,1)} %collective-permute-done.42.got_ref), custom_call_target="tpu_custom_call" | custom-call | tf_op jit(solution)/shard_map/core_halves/pallas_call | solution.py:867
  393.8 2.4 collective-permute-done.43
  398.0 3.0 add_bitcast_fusion.1
  407.3 11.0 %collective-permute-done.45 = bf16[2,64,3200]{2,1,0:T(8,128)(2,1)S(1)} collective-permute-done((bf16[2,64,3200]{2,1,0:T(8,128)(2,1)}, bf16[2,64,3200]{2,1,0:T(8,128)(2,1)S(1)}, u32[]{:S(2)}, u32[]{:S(2)}) %collective-permute-start.45) | collective-permute-done | bytes 819232 | tf_op jit(solution)/shard_map/ppermute | solution.py:91
  419.3 10.6 %collective-permute-done.46 = bf16[2,64,3200]{2,1,0:T(8,128)(2,1)S(1)} collective-permute-done((bf16[2,64,3200]{2,1,0:T(8,128)(2,1)S(1)}, bf16[2,64,3200]{2,1,0:T(8,128)(2,1)S(1)}, u32[]{:S(2)}, u32[]{:S(2)}) %collective-permute-start.46) | collective-permute-done | bytes 819232 | tf_op jit(solution)/shard_map/ppermute | solution.py:91
  431.1 2.8 fusion.23
  433.9 1.5 fusion
  438.5 4.4 collective-permute-start.52
  443.9 4.4 collective-permute-done.53
  448.3 5.2 %collective-permute-done.52 = bf16[32,3200]{1,0:T(8,128)(2,1)S(1)} collective-permute-done((bf16[32,3200]{1,0:T(8,128)(2,1)S(1)}, bf16[32,3200]{1,0:T(8,128)(2,1)S(1)}, u32[]{:S(2)}, u32[]{:S(2)}) %collective-permute-start.52) | collective-permute-done | bytes 204832 | tf_op jit(solution)/shard_map/ppermute | solution.py:51
  453.6 4.8 collective-permute-start.56
  458.4 1.5 collective-permute-start.55
  461.4 2.4 collective-permute-done.56
  463.8 14.3 %collective-permute-done.55 = bf16[32,3200]{1,0:T(8,128)(2,1)S(1)} collective-permute-done((bf16[32,3200]{1,0:T(8,128)(2,1)S(1)}, bf16[32,3200]{1,0:T(8,128)(2,1)S(1)}, u32[]{:S(2)}, u32[]{:S(2)}) %collective-permute-start.55) | collective-permute-done | bytes 204832 | tf_op jit(solution)/shard_map/ppermute | solution.py:51
  482.5 2.3 add_convert_fusion.4
  485.6 3.4 dense_outputs.1
  489.0 1.8 slice_reduce_fusion
  490.8 1.6 copy.46
  (271 shorter events, 81.6 us)
Async XLA Ops:
  8.7 33.2 %collective-permute-start = (bf16[128,5248]{1,0:T(8,128)(2,1)}, bf16[128,5248]{1,0:T(8,128)(2,1)S(1)}, u32[]{:S(2)}, u32[]{:S(2)}) collective-permute-start(bf16[128,5248]{1,0:T(8,128)(2,1)} %pad_maximum_fusion.14), channel_id=1, source_target_pairs={{0,1},{1,0},{2,3},{3,2},{4,5},{5,4},{6,7},{7,6},{8,9},{9,8},{10,11... | collective-permute-start | bytes 4030472 | tf_op jit(solution)/shard_map/ppermute | solution.py:59
  10.2 31.7 %collective-permute-start.1 = (bf16[128,5248]{1,0:T(8,128)(2,1)}, bf16[128,5248]{1,0:T(8,128)(2,1)S(1)}, u32[]{:S(2)}, u32[]{:S(2)}) collective-permute-start(bf16[128,5248]{1,0:T(8,128)(2,1)} %pad_maximum_fusion.14), channel_id=1, source_target_pairs={{0,2},{2,0},{1,3},{3,1},{4,6},{6,4},{5,7},{7,5},{8,10},{10,8},{9,1... | collective-permute-start | bytes 4030472 | tf_op jit(solution)/shard_map/ppermute | solution.py:59
  15.6 17.6 %collective-permute-start.2 = (bf16[272,1024]{1,0:T(8,128)(2,1)}, bf16[272,1024]{1,0:T(8,128)(2,1)}, u32[]{:S(2)}, u32[]{:S(2)}) collective-permute-start(bf16[272,1024]{1,0:T(8,128)(2,1)} %maximum_maximum_fusion), channel_id=1, source_target_pairs={{0,24},{8,0},{16,8},{24,16},{1,25},{9,1},{17,9},{25,17},{2,26},{10... | collective-permute-start | bytes 1671176 | tf_op jit(solution)/shard_map/ppermute | solution.py:51
  16.1 25.8 %collective-permute-start.3 = (bf16[272,1024]{1,0:T(8,128)(2,1)}, bf16[272,1024]{1,0:T(8,128)(2,1)}, u32[]{:S(2)}, u32[]{:S(2)}) collective-permute-start(bf16[272,1024]{1,0:T(8,128)(2,1)} %maximum_maximum_fusion), channel_id=1, source_target_pairs={{0,8},{8,16},{16,24},{24,0},{1,9},{9,17},{17,25},{25,1},{2,10},{10... | collective-permute-start | bytes 1671176 | tf_op jit(solution)/shard_map/ppermute | solution.py:51
  25.9 94.4 %copy-start.5 = (bf16[768,512]{1,0:T(8,128)(2,1)}, bf16[768,512]{1,0:T(8,128)(2,1)S(1)}, u32[]{:S(2)}) copy-start(bf16[768,512]{1,0:T(8,128)(2,1)S(1)} %get-tuple-element.149.refs_6_) | copy-start | bytes 2359300
  41.9 15.4 %collective-permute-start.5 = (bf16[64,5248]{1,0:T(8,128)(2,1)S(1)}, bf16[64,5248]{1,0:T(8,128)(2,1)S(1)}, u32[]{:S(2)}, u32[]{:S(2)}) collective-permute-start(bf16[64,5248]{1,0:T(8,128)(2,1)S(1)} %slice.254), channel_id=1, source_target_pairs={{0,1},{1,0},{2,3},{3,2},{4,5},{5,4},{6,7},{7,6},{8,9},{9,8},{10,11... | collective-permute-start | bytes 2015240 | tf_op jit(solution)/shard_map/ppermute | solution.py:65
  42.6 15.7 %collective-permute-start.4 = (bf16[64,5248]{1,0:T(8,128)(2,1)S(1)}, bf16[64,5248]{1,0:T(8,128)(2,1)S(1)}, u32[]{:S(2)}, u32[]{:S(2)}) collective-permute-start(bf16[64,5248]{1,0:T(8,128)(2,1)S(1)} %slice.253), channel_id=1, source_target_pairs={{0,2},{2,0},{1,3},{3,1},{4,6},{6,4},{5,7},{7,5},{8,10},{10,8},{9,1... | collective-permute-start | bytes 2015240 | tf_op jit(solution)/shard_map/ppermute | solution.py:65
  60.8 4.9 collective-permute-start.6
  60.8 20.3 %collective-permute-start.7 = (bf16[768,512]{1,0:T(8,128)(2,1)}, bf16[768,512]{1,0:T(8,128)(2,1)}, u32[]{:S(2)}, u32[]{:S(2)}) collective-permute-start(bf16[768,512]{1,0:T(8,128)(2,1)} %get-tuple-element.153.refs_6_), channel_id=1, source_target_pairs={{0,1},{1,0},{2,3},{3,2},{4,5},{5,4},{6,7},{7,6},{8,9},{9,8},{10,11... | collective-permute-start | bytes 2359304 | tf_op jit(solution)/shard_map/ppermute | solution.py:59
  61.8 20.0 %collective-permute-start.8 = (bf16[768,512]{1,0:T(8,128)(2,1)}, bf16[768,512]{1,0:T(8,128)(2,1)}, u32[]{:S(2)}, u32[]{:S(2)}) collective-permute-start(bf16[768,512]{1,0:T(8,128)(2,1)} %get-tuple-element.153.refs_6_), channel_id=1, source_target_pairs={{0,2},{2,0},{1,3},{3,1},{4,6},{6,4},{5,7},{7,5},{8,10},{10,8},{9,1... | collective-permute-start | bytes 2359304 | tf_op jit(solution)/shard_map/ppermute | solution.py:59
  63.9 17.9 %copy-start.14 = (bf16[768,512]{1,0:T(8,128)(2,1)S(1)}, bf16[768,512]{1,0:T(8,128)(2,1)}, u32[]{:S(2)}) copy-start(bf16[768,512]{1,0:T(8,128)(2,1)} %get-tuple-element.157.refs_11_) | copy-start | bytes 2359300
  81.8 35.3 %collective-permute-start.10 = (bf16[768,512]{1,0:T(8,128)(2,1)S(1)}, bf16[768,512]{1,0:T(8,128)(2,1)S(1)}, u32[]{:S(2)}, u32[]{:S(2)}) collective-permute-start(bf16[768,512]{1,0:T(8,128)(2,1)S(1)} %copy-done.14), channel_id=1, source_target_pairs={{0,1},{1,0},{2,3},{3,2},{4,5},{5,4},{6,7},{7,6},{8,9},{9,8},{10,11... | collective-permute-start | bytes 2359304 | tf_op jit(solution)/shard_map/ppermute | solution.py:59
  82.8 34.3 %collective-permute-start.11 = (bf16[768,512]{1,0:T(8,128)(2,1)S(1)}, bf16[768,512]{1,0:T(8,128)(2,1)S(1)}, u32[]{:S(2)}, u32[]{:S(2)}) collective-permute-start(bf16[768,512]{1,0:T(8,128)(2,1)S(1)} %copy-done.14), channel_id=1, source_target_pairs={{0,2},{2,0},{1,3},{3,1},{4,6},{6,4},{5,7},{7,5},{8,10},{10,8},{9,1... | collective-permute-start | bytes 2359304 | tf_op jit(solution)/shard_map/ppermute | solution.py:59
  84.2 32.9 %collective-permute-start.9 = (bf16[272,1024]{1,0:T(8,128)(2,1)}, bf16[272,1024]{1,0:T(8,128)(2,1)S(1)}, u32[]{:S(2)}, u32[]{:S(2)}) collective-permute-start(bf16[272,1024]{1,0:T(8,128)(2,1)} %maximum_maximum_fusion), channel_id=1, source_target_pairs={{0,16},{8,24},{16,0},{24,8},{1,17},{9,25},{17,1},{25,9},{2,18},{10... | collective-permute-start | bytes 1671176 | tf_op jit(solution)/shard_map/ppermute | solution.py:51
  87.4 29.6 %collective-permute-start.12 = (bf16[384,512]{1,0:T(8,128)(2,1)}, bf16[384,512]{1,0:T(8,128)(2,1)}, u32[]{:S(2)}, u32[]{:S(2)}) collective-permute-start(bf16[384,512]{1,0:T(8,128)(2,1)} %slice.259), channel_id=1, source_target_pairs={{0,2},{2,0},{1,3},{3,1},{4,6},{6,4},{5,7},{7,5},{8,10},{10,8},{9,1... | collective-permute-start | bytes 1179656 | tf_op jit(solution)/shard_map/ppermute | solution.py:65
  90.7 26.4 %collective-permute-start.13 = (bf16[384,512]{1,0:T(8,128)(2,1)}, bf16[384,512]{1,0:T(8,128)(2,1)}, u32[]{:S(2)}, u32[]{:S(2)}) collective-permute-start(bf16[384,512]{1,0:T(8,128)(2,1)} %slice.260), channel_id=1, source_target_pairs={{0,1},{1,0},{2,3},{3,2},{4,5},{5,4},{6,7},{7,6},{8,9},{9,8},{10,11... | collective-permute-start | bytes 1179656 | tf_op jit(solution)/shard_map/ppermute | solution.py:65
  120.3 31.2 %collective-permute-start.17 = (bf16[4,272,1024]{2,1,0:T(8,128)(2,1)S(1)}, bf16[4,272,1024]{2,1,0:T(8,128)(2,1)}, u32[]{:S(2)}, u32[]{:S(2)}) collective-permute-start(bf16[4,272,1024]{2,1,0:T(8,128)(2,1)S(1)} %pad_maximum_fusion.4.packed_ref.code_ref), channel_id=1, source_target_pairs={{0,4},{4,0},{1,5},{5,1},{2,6},{6,2},{3,7},{7,3},{8,12},{12,8},{9,1... | collective-permute-start | bytes 6684680 | tf_op jit(solution)/shard_map/ppermute | solution.py:47
  123.6 27.0 %collective-permute-start.18 = (bf16[1152,512]{1,0:T(8,128)(2,1)}, bf16[1152,512]{1,0:T(8,128)(2,1)S(1)}, u32[]{:S(2)}, u32[]{:S(2)}) collective-permute-start(bf16[1152,512]{1,0:T(8,128)(2,1)} %get-tuple-element.344), channel_id=1, source_target_pairs={{0,1},{1,0},{2,3},{3,2},{4,5},{5,4},{6,7},{7,6},{8,9},{9,8},{10,11... | collective-permute-start | bytes 3538952 | tf_op jit(solution)/shard_map/ppermute | solution.py:74
  124.6 26.8 %collective-permute-start.19 = (bf16[1152,512]{1,0:T(8,128)(2,1)}, bf16[1152,512]{1,0:T(8,128)(2,1)}, u32[]{:S(2)}, u32[]{:S(2)}) collective-permute-start(bf16[1152,512]{1,0:T(8,128)(2,1)} %get-tuple-element.343), channel_id=1, source_target_pairs={{0,2},{2,0},{1,3},{3,1},{4,6},{6,4},{5,7},{7,5},{8,10},{10,8},{9,1... | collective-permute-start | bytes 3538952 | tf_op jit(solution)/shard_map/ppermute | solution.py:74
  125.2 16.9 %collective-permute-start.14 = (bf16[256,1024]{1,0:T(8,128)(2,1)}, bf16[256,1024]{1,0:T(8,128)(2,1)}, u32[]{:S(2)}, u32[]{:S(2)}) collective-permute-start(bf16[256,1024]{1,0:T(8,128)(2,1)} %get-tuple-element.174.rest_0_.refs_11_), channel_id=1, source_target_pairs={{0,24},{8,0},{16,8},{24,16},{1,25},{9,1},{17,9},{25,17},{2,26},{10... | collective-permute-start | bytes 1572872 | tf_op jit(solution)/shard_map/ppermute | solution.py:51
  125.5 23.9 %collective-permute-start.16 = (bf16[256,1024]{1,0:T(8,128)(2,1)}, bf16[256,1024]{1,0:T(8,128)(2,1)}, u32[]{:S(2)}, u32[]{:S(2)}) collective-permute-start(bf16[256,1024]{1,0:T(8,128)(2,1)} %get-tuple-element.174.rest_0_.refs_11_), channel_id=1, source_target_pairs={{0,8},{8,16},{16,24},{24,0},{1,9},{9,17},{17,25},{25,1},{2,10},{10... | collective-permute-start | bytes 1572872 | tf_op jit(solution)/shard_map/ppermute | solution.py:51
  157.4 25.8 %collective-permute-start.20 = (bf16[1152,512]{1,0:T(8,128)(2,1)S(1)}, bf16[1152,512]{1,0:T(8,128)(2,1)S(1)}, u32[]{:S(2)}, u32[]{:S(2)}) collective-permute-start(bf16[1152,512]{1,0:T(8,128)(2,1)S(1)} %get-tuple-element.342), channel_id=1, source_target_pairs={{0,1},{1,0},{2,3},{3,2},{4,5},{5,4},{6,7},{7,6},{8,9},{9,8},{10,11... | collective-permute-start | bytes 3538952 | tf_op jit(solution)/shard_map/ppermute | solution.py:74
  158.5 26.1 %collective-permute-start.21 = (bf16[1152,512]{1,0:T(8,128)(2,1)S(1)}, bf16[1152,512]{1,0:T(8,128)(2,1)S(1)}, u32[]{:S(2)}, u32[]{:S(2)}) collective-permute-start(bf16[1152,512]{1,0:T(8,128)(2,1)S(1)} %get-tuple-element.341), channel_id=1, source_target_pairs={{0,2},{2,0},{1,3},{3,1},{4,6},{6,4},{5,7},{7,5},{8,10},{10,8},{9,1... | collective-permute-start | bytes 3538952 | tf_op jit(solution)/shard_map/ppermute | solution.py:74
  159.0 23.8 %collective-permute-start.15 = (bf16[256,1024]{1,0:T(8,128)(2,1)}, bf16[256,1024]{1,0:T(8,128)(2,1)S(1)}, u32[]{:S(2)}, u32[]{:S(2)}) collective-permute-start(bf16[256,1024]{1,0:T(8,128)(2,1)} %get-tuple-element.174.rest_0_.refs_11_), channel_id=1, source_target_pairs={{0,16},{8,24},{16,0},{24,8},{1,17},{9,25},{17,1},{25,9},{2,18},{10... | collective-permute-start | bytes 1572872 | tf_op jit(solution)/shard_map/ppermute | solution.py:51
  182.7 3.8 collective-permute-start.22
  182.7 12.2 %collective-permute-start.23 = (bf16[256,1024]{1,0:T(8,128)(2,1)}, bf16[256,1024]{1,0:T(8,128)(2,1)S(1)}, u32[]{:S(2)}, u32[]{:S(2)}) collective-permute-start(bf16[256,1024]{1,0:T(8,128)(2,1)} %collective-permute-done.14.rest_1_), channel_id=1, source_target_pairs={{0,4},{4,0},{1,5},{5,1},{2,6},{6,2},{3,7},{7,3},{8,12},{12,8},{9,1... | collective-permute-start | bytes 1572872 | tf_op jit(solution)/shard_map/ppermute | solution.py:47
  183.2 11.7 %collective-permute-start.24 = (bf16[256,1024]{1,0:T(8,128)(2,1)S(1)}, bf16[256,1024]{1,0:T(8,128)(2,1)}, u32[]{:S(2)}, u32[]{:S(2)}) collective-permute-start(bf16[256,1024]{1,0:T(8,128)(2,1)S(1)} %collective-permute-done.15.rest_2_), channel_id=1, source_target_pairs={{0,4},{4,0},{1,5},{5,1},{2,6},{6,2},{3,7},{7,3},{8,12},{12,8},{9,1... | collective-permute-start | bytes 1572872 | tf_op jit(solution)/shard_map/ppermute | solution.py:47
  183.3 11.7 %collective-permute-start.25 = (bf16[256,1024]{1,0:T(8,128)(2,1)}, bf16[256,1024]{1,0:T(8,128)(2,1)}, u32[]{:S(2)}, u32[]{:S(2)}) collective-permute-start(bf16[256,1024]{1,0:T(8,128)(2,1)} %collective-permute-done.16.rest_3_), channel_id=1, source_target_pairs={{0,4},{4,0},{1,5},{5,1},{2,6},{6,2},{3,7},{7,3},{8,12},{12,8},{9,1... | collective-permute-start | bytes 1572872 | tf_op jit(solution)/shard_map/ppermute | solution.py:47
  184.6 16.2 %collective-permute-start.26 = (bf16[384,512]{1,0:T(8,128)(2,1)}, bf16[384,512]{1,0:T(8,128)(2,1)}, u32[]{:S(2)}, u32[]{:S(2)}) collective-permute-start(bf16[384,512]{1,0:T(8,128)(2,1)} %slice.314), channel_id=1, source_target_pairs={{0,2},{2,0},{1,3},{3,1},{4,6},{6,4},{5,7},{7,5},{8,10},{10,8},{9,1... | collective-permute-start | bytes 1179656 | tf_op jit(solution)/shard_map/ppermute | solution.py:65
  186.5 14.3 %collective-permute-start.27 = (bf16[384,512]{1,0:T(8,128)(2,1)}, bf16[384,512]{1,0:T(8,128)(2,1)}, u32[]{:S(2)}, u32[]{:S(2)}) collective-permute-start(bf16[384,512]{1,0:T(8,128)(2,1)} %slice.315), channel_id=1, source_target_pairs={{0,1},{1,0},{2,3},{3,2},{4,5},{5,4},{6,7},{7,6},{8,9},{9,8},{10,11... | collective-permute-start | bytes 1179656 | tf_op jit(solution)/shard_map/ppermute | solution.py:65
  224.5 27.0 %collective-permute-start.29 = (bf16[1,1,768,512]{3,2,1,0:T(8,128)(2,1)}, bf16[1,1,768,512]{3,2,1,0:T(8,128)(2,1)S(1)}, u32[]{:S(2)}, u32[]{:S(2)}) collective-permute-start(bf16[1,1,768,512]{3,2,1,0:T(8,128)(2,1)} %get-tuple-element.193), channel_id=1, source_target_pairs={{0,2},{2,0},{1,3},{3,1},{4,6},{6,4},{5,7},{7,5},{8,10},{10,8},{9,1... | collective-permute-start | bytes 2359304 | tf_op jit(solution)/shard_map/ppermute | solution.py:74
  225.4 26.1 %collective-permute-start.28 = (bf16[1,1,768,512]{3,2,1,0:T(8,128)(2,1)}, bf16[1,1,768,512]{3,2,1,0:T(8,128)(2,1)S(1)}, u32[]{:S(2)}, u32[]{:S(2)}) collective-permute-start(bf16[1,1,768,512]{3,2,1,0:T(8,128)(2,1)} %get-tuple-element.192), channel_id=1, source_target_pairs={{0,1},{1,0},{2,3},{3,2},{4,5},{5,4},{6,7},{7,6},{8,9},{9,8},{10,11... | collective-permute-start | bytes 2359304 | tf_op jit(solution)/shard_map/ppermute | solution.py:74
  256.7 11.8 %collective-permute-start.30 = (bf16[4,256,1152]{2,1,0:T(8,128)(2,1)}, bf16[4,256,1152]{2,1,0:T(8,128)(2,1)}, u32[]{:S(2)}, u32[]{:S(2)}) collective-permute-start(bf16[4,256,1152]{2,1,0:T(8,128)(2,1)} %combine.4), channel_id=1, source_target_pairs={{0,4},{4,0},{1,5},{5,1},{2,6},{6,2},{3,7},{7,3},{8,12},{12,8},{9,1... | collective-permute-start | bytes 7077896 | tf_op jit(solution)/shard_map/ppermute | solution.py:47
  258.3 68.9 %collective-permute-start.32 = (bf16[3,1,768,512]{3,2,1,0:T(8,128)(2,1)S(1)}, bf16[3,1,768,512]{3,2,1,0:T(8,128)(2,1)}, u32[]{:S(2)}, u32[]{:S(2)}) collective-permute-start(bf16[3,1,768,512]{3,2,1,0:T(8,128)(2,1)S(1)} %pad_maximum_fusion.2), channel_id=1, source_target_pairs={{0,1},{1,0},{2,3},{3,2},{4,5},{5,4},{6,7},{7,6},{8,9},{9,8},{10,11... | collective-permute-start | bytes 7077896 | tf_op jit(solution)/shard_map/ppermute | solution.py:74
  264.3 10.3 %collective-permute-start.31 = (bf16[4,256,1024]{2,1,0:T(8,128)(2,1)}, bf16[4,256,1024]{2,1,0:T(8,128)(2,1)}, u32[]{:S(2)}, u32[]{:S(2)}) collective-permute-start(bf16[4,256,1024]{2,1,0:T(8,128)(2,1)} %combine.5), channel_id=1, source_target_pairs={{0,4},{4,0},{1,5},{5,1},{2,6},{6,2},{3,7},{7,3},{8,12},{12,8},{9,1... | collective-permute-start | bytes 6291464 | tf_op jit(solution)/shard_map/ppermute | solution.py:47
  267.3 59.9 %collective-permute-start.33 = (bf16[3,1,768,512]{3,2,1,0:T(8,128)(2,1)}, bf16[3,1,768,512]{3,2,1,0:T(8,128)(2,1)}, u32[]{:S(2)}, u32[]{:S(2)}) collective-permute-start(bf16[3,1,768,512]{3,2,1,0:T(8,128)(2,1)} %pad_maximum_fusion.3), channel_id=1, source_target_pairs={{0,2},{2,0},{1,3},{3,1},{4,6},{6,4},{5,7},{7,5},{8,10},{10,8},{9,1... | collective-permute-start | bytes 7077896 | tf_op jit(solution)/shard_map/ppermute | solution.py:74
  274.6 27.3 %collective-permute-start.34 = (bf16[256,1152]{1,0:T(8,128)(2,1)}, bf16[256,1152]{1,0:T(8,128)(2,1)S(1)}, u32[]{:S(2)}, u32[]{:S(2)}) collective-permute-start(bf16[256,1152]{1,0:T(8,128)(2,1)} %get-tuple-element.213), channel_id=1, source_target_pairs={{0,8},{8,16},{16,24},{24,0},{1,9},{9,17},{17,25},{25,1},{2,10},{10... | collective-permute-start | bytes 1769480 | tf_op jit(solution)/shard_map/ppermute | solution.py:51
  276.5 27.1 %collective-permute-start.35 = (bf16[256,1152]{1,0:T(8,128)(2,1)}, bf16[256,1152]{1,0:T(8,128)(2,1)S(1)}, u32[]{:S(2)}, u32[]{:S(2)}) collective-permute-start(bf16[256,1152]{1,0:T(8,128)(2,1)} %get-tuple-element.214), channel_id=1, source_target_pairs={{0,24},{8,0},{16,8},{24,16},{1,25},{9,1},{17,9},{25,17},{2,26},{10... | collective-permute-start | bytes 1769480 | tf_op jit(solution)/shard_map/ppermute | solution.py:51
  276.6 50.6 %collective-permute-start.36 = (bf16[256,1152]{1,0:T(8,128)(2,1)}, bf16[256,1152]{1,0:T(8,128)(2,1)S(1)}, u32[]{:S(2)}, u32[]{:S(2)}) collective-permute-start(bf16[256,1152]{1,0:T(8,128)(2,1)} %get-tuple-element.215), channel_id=1, source_target_pairs={{0,16},{8,24},{16,0},{24,8},{1,17},{9,25},{17,1},{25,9},{2,18},{10... | collective-permute-start | bytes 1769480 | tf_op jit(solution)/shard_map/ppermute | solution.py:51
  301.8 25.4 %copy-start.33 = (bf16[256,1152]{1,0:T(8,128)(2,1)}, bf16[256,1152]{1,0:T(8,128)(2,1)S(1)}, u32[]{:S(2)}) copy-start(bf16[256,1152]{1,0:T(8,128)(2,1)S(1)} %collective-permute-done.34.refs_1_) | copy-start | bytes 1769476
  303.6 23.6 %copy-start.34 = (bf16[256,1152]{1,0:T(8,128)(2,1)}, bf16[256,1152]{1,0:T(8,128)(2,1)S(1)}, u32[]{:S(2)}) copy-start(bf16[256,1152]{1,0:T(8,128)(2,1)S(1)} %collective-permute-done.35.refs_2_) | copy-start | bytes 1769476
  333.9 43.6 %collective-permute-start.37 = (bf16[2,1,768,512]{3,2,1,0:T(8,128)(2,1)}, bf16[2,1,768,512]{3,2,1,0:T(8,128)(2,1)}, u32[]{:S(2)}, u32[]{:S(2)}) collective-permute-start(bf16[2,1,768,512]{3,2,1,0:T(8,128)(2,1)} %pad_maximum_fusion.12), channel_id=1, source_target_pairs={{0,1},{1,0},{2,3},{3,2},{4,5},{5,4},{6,7},{7,6},{8,9},{9,8},{10,11... | collective-permute-start | bytes 4718600 | tf_op jit(solution)/shard_map/ppermute | solution.py:74
  336.1 41.4 %collective-permute-start.38 = (bf16[2,1,768,512]{3,2,1,0:T(8,128)(2,1)}, bf16[2,1,768,512]{3,2,1,0:T(8,128)(2,1)}, u32[]{:S(2)}, u32[]{:S(2)}) collective-permute-start(bf16[2,1,768,512]{3,2,1,0:T(8,128)(2,1)} %pad_maximum_fusion.13), channel_id=1, source_target_pairs={{0,2},{2,0},{1,3},{3,1},{4,6},{6,4},{5,7},{7,5},{8,10},{10,8},{9,1... | collective-permute-start | bytes 4718600 | tf_op jit(solution)/shard_map/ppermute | solution.py:74
  337.8 39.6 %collective-permute-start.39 = (bf16[256,1024]{1,0:T(8,128)(2,1)}, bf16[256,1024]{1,0:T(8,128)(2,1)S(1)}, u32[]{:S(2)}, u32[]{:S(2)}) collective-permute-start(bf16[256,1024]{1,0:T(8,128)(2,1)} %get-tuple-element.226), channel_id=1, source_target_pairs={{0,8},{8,16},{16,24},{24,0},{1,9},{9,17},{17,25},{25,1},{2,10},{10... | collective-permute-start | bytes 1572872 | tf_op jit(solution)/shard_map/ppermute | solution.py:51
  340.0 37.5 %collective-permute-start.40 = (bf16[256,1024]{1,0:T(8,128)(2,1)}, bf16[256,1024]{1,0:T(8,128)(2,1)}, u32[]{:S(2)}, u32[]{:S(2)}) collective-permute-start(bf16[256,1024]{1,0:T(8,128)(2,1)} %get-tuple-element.227), channel_id=1, source_target_pairs={{0,24},{8,0},{16,8},{24,16},{1,25},{9,1},{17,9},{25,17},{2,26},{10... | collective-permute-start | bytes 1572872 | tf_op jit(solution)/shard_map/ppermute | solution.py:51
  381.6 6.2 %collective-permute-start.42 = (bf16[4,128,3200]{2,1,0:T(8,128)(2,1)}, bf16[4,128,3200]{2,1,0:T(8,128)(2,1)}, u32[]{:S(2)}, u32[]{:S(2)}) collective-permute-start(bf16[4,128,3200]{2,1,0:T(8,128)(2,1)} %slice_bitcast_fusion), channel_id=1, source_target_pairs={{0,4},{4,0},{1,5},{5,1},{2,6},{6,2},{3,7},{7,3},{8,12},{12,8},{9,1... | collective-permute-start | bytes 9830408 | tf_op jit(solution)/shard_map/ppermute | solution.py:47
  381.6 14.7 %collective-permute-start.43 = (bf16[2,128,1024]{2,1,0:T(8,128)(2,1)}, bf16[2,128,1024]{2,1,0:T(8,128)(2,1)}, u32[]{:S(2)}, u32[]{:S(2)}) collective-permute-start(bf16[2,128,1024]{2,1,0:T(8,128)(2,1)} %get-tuple-element.250), channel_id=1, source_target_pairs={{0,1},{1,0},{2,3},{3,2},{4,5},{5,4},{6,7},{7,6},{8,9},{9,8},{10,11... | collective-permute-start | bytes 1572872 | tf_op jit(solution)/shard_map/ppermute | solution.py:91
  382.6 14.4 %collective-permute-start.44 = (bf16[2,128,1024]{2,1,0:T(8,128)(2,1)}, bf16[2,128,1024]{2,1,0:T(8,128)(2,1)}, u32[]{:S(2)}, u32[]{:S(2)}) collective-permute-start(bf16[2,128,1024]{2,1,0:T(8,128)(2,1)} %get-tuple-element.251), channel_id=1, source_target_pairs={{0,2},{2,0},{1,3},{3,1},{4,6},{6,4},{5,7},{7,5},{8,10},{10,8},{9,1... | collective-permute-start | bytes 1572872 | tf_op jit(solution)/shard_map/ppermute | solution.py:91
  384.4 76.7 %collective-permute-start.41 = (bf16[256,1024]{1,0:T(8,128)(2,1)}, bf16[256,1024]{1,0:T(8,128)(2,1)S(1)}, u32[]{:S(2)}, u32[]{:S(2)}) collective-permute-start(bf16[256,1024]{1,0:T(8,128)(2,1)} %get-tuple-element.241), channel_id=1, source_target_pairs={{0,16},{8,24},{16,0},{24,8},{1,17},{9,25},{17,1},{25,9},{2,18},{10... | collective-permute-start | bytes 1572872 | tf_op jit(solution)/shard_map/ppermute | solution.py:51
  397.0 21.3 %collective-permute-start.45 = (bf16[2,64,3200]{2,1,0:T(8,128)(2,1)}, bf16[2,64,3200]{2,1,0:T(8,128)(2,1)S(1)}, u32[]{:S(2)}, u32[]{:S(2)}) collective-permute-start(bf16[2,64,3200]{2,1,0:T(8,128)(2,1)} %get-tuple-element.252), channel_id=1, source_target_pairs={{0,1},{1,0},{2,3},{3,2},{4,5},{5,4},{6,7},{7,6},{8,9},{9,8},{10,11... | collective-permute-start | bytes 2457608 | tf_op jit(solution)/shard_map/ppermute | solution.py:91
  401.0 17.4 %copy-start.24 = (bf16[2,64,3200]{2,1,0:T(8,128)(2,1)S(1)}, bf16[2,64,3200]{2,1,0:T(8,128)(2,1)}, u32[]{:S(2)}) copy-start(bf16[2,64,3200]{2,1,0:T(8,128)(2,1)} %get-tuple-element.261) | copy-start | bytes 2457604
  401.9 27.9 %copy-start.23 = (bf16[2,64,3200]{2,1,0:T(8,128)(2,1)S(1)}, bf16[2,64,3200]{2,1,0:T(8,128)(2,1)}, u32[]{:S(2)}) copy-start(bf16[2,64,3200]{2,1,0:T(8,128)(2,1)} %get-tuple-element.262) | copy-start | bytes 2457604
  403.1 32.3 %collective-permute-start.47 = (bf16[128,1024]{1,0:T(8,128)(2,1)S(1)}, bf16[128,1024]{1,0:T(8,128)(2,1)S(1)}, u32[]{:S(2)}, u32[]{:S(2)}) collective-permute-start(bf16[128,1024]{1,0:T(8,128)(2,1)S(1)} %fusion.13), channel_id=1, source_target_pairs={{0,2},{2,0},{1,3},{3,1},{4,6},{6,4},{5,7},{7,5},{8,10},{10,8},{9,1... | collective-permute-start | bytes 786440 | tf_op jit(solution)/shard_map/ppermute | solution.py:98
  405.0 30.4 %collective-permute-start.48 = (bf16[128,1024]{1,0:T(8,128)(2,1)S(1)}, bf16[128,1024]{1,0:T(8,128)(2,1)S(1)}, u32[]{:S(2)}, u32[]{:S(2)}) collective-permute-start(bf16[128,1024]{1,0:T(8,128)(2,1)S(1)} %fusion.14), channel_id=1, source_target_pairs={{0,1},{1,0},{2,3},{3,2},{4,5},{5,4},{6,7},{7,6},{8,9},{9,8},{10,11... | collective-permute-start | bytes 786440 | tf_op jit(solution)/shard_map/ppermute | solution.py:99
  406.1 23.8 %collective-permute-start.46 = (bf16[2,64,3200]{2,1,0:T(8,128)(2,1)S(1)}, bf16[2,64,3200]{2,1,0:T(8,128)(2,1)S(1)}, u32[]{:S(2)}, u32[]{:S(2)}) collective-permute-start(bf16[2,64,3200]{2,1,0:T(8,128)(2,1)S(1)} %copy-done.51), channel_id=1, source_target_pairs={{0,2},{2,0},{1,3},{3,1},{4,6},{6,4},{5,7},{7,5},{8,10},{10,8},{9,1... | collective-permute-start | bytes 2457608 | tf_op jit(solution)/shard_map/ppermute | solution.py:91
  418.4 18.3 %collective-permute-start.49 = (bf16[64,3200]{1,0:T(8,128)(2,1)S(1)}, bf16[64,3200]{1,0:T(8,128)(2,1)S(1)}, u32[]{:S(2)}, u32[]{:S(2)}) collective-permute-start(bf16[64,3200]{1,0:T(8,128)(2,1)S(1)} %fusion.6), channel_id=1, source_target_pairs={{0,2},{2,0},{1,3},{3,1},{4,6},{6,4},{5,7},{7,5},{8,10},{10,8},{9,1... | collective-permute-start | bytes 1228808 | tf_op jit(solution)/shard_map/ppermute | solution.py:98
  430.0 8.0 %collective-permute-start.50 = (bf16[64,3200]{1,0:T(8,128)(2,1)S(1)}, bf16[64,3200]{1,0:T(8,128)(2,1)S(1)}, u32[]{:S(2)}, u32[]{:S(2)}) collective-permute-start(bf16[64,3200]{1,0:T(8,128)(2,1)S(1)} %fusion.7), channel_id=1, source_target_pairs={{0,1},{1,0},{2,3},{3,2},{4,5},{5,4},{6,7},{7,6},{8,9},{9,8},{10,11... | collective-permute-start | bytes 1228808 | tf_op jit(solution)/shard_map/ppermute | solution.py:99
  438.4 9.9 %collective-permute-start.53 = (bf16[32,3200]{1,0:T(8,128)(2,1)S(1)}, bf16[32,3200]{1,0:T(8,128)(2,1)S(1)}, u32[]{:S(2)}, u32[]{:S(2)}) collective-permute-start(bf16[32,3200]{1,0:T(8,128)(2,1)S(1)} %get-tuple-element.339), channel_id=1, source_target_pairs={{0,24},{8,0},{16,8},{24,16},{1,25},{9,1},{17,9},{25,17},{2,26},{10... | collective-permute-start | bytes 614408 | tf_op jit(solution)/shard_map/ppermute | solution.py:51
  438.5 15.0 %collective-permute-start.52 = (bf16[32,3200]{1,0:T(8,128)(2,1)S(1)}, bf16[32,3200]{1,0:T(8,128)(2,1)S(1)}, u32[]{:S(2)}, u32[]{:S(2)}) collective-permute-start(bf16[32,3200]{1,0:T(8,128)(2,1)S(1)} %get-tuple-element.340), channel_id=1, source_target_pairs={{0,16},{8,24},{16,0},{24,8},{1,17},{9,25},{17,1},{25,9},{2,18},{10... | collective-permute-start | bytes 614408 | tf_op jit(solution)/shard_map/ppermute | solution.py:51
  442.9 10.6 %collective-permute-start.51 = (bf16[32,3200]{1,0:T(8,128)(2,1)S(1)}, bf16[32,3200]{1,0:T(8,128)(2,1)S(1)}, u32[]{:S(2)}, u32[]{:S(2)}) collective-permute-start(bf16[32,3200]{1,0:T(8,128)(2,1)S(1)} %get-tuple-element.338), channel_id=1, source_target_pairs={{0,8},{8,16},{16,24},{24,0},{1,9},{9,17},{17,25},{25,1},{2,10},{10... | collective-permute-start | bytes 614408 | tf_op jit(solution)/shard_map/ppermute | solution.py:51
  453.6 10.2 %collective-permute-start.56 = (bf16[32,3200]{1,0:T(8,128)(2,1)S(1)}, bf16[32,3200]{1,0:T(8,128)(2,1)S(1)}, u32[]{:S(2)}, u32[]{:S(2)}) collective-permute-start(bf16[32,3200]{1,0:T(8,128)(2,1)S(1)} %fusion.12), channel_id=1, source_target_pairs={{0,8},{8,16},{16,24},{24,0},{1,9},{9,17},{17,25},{25,1},{2,10},{10... | collective-permute-start | bytes 614408 | tf_op jit(solution)/shard_map/ppermute | solution.py:51
  458.4 19.7 %collective-permute-start.55 = (bf16[32,3200]{1,0:T(8,128)(2,1)S(1)}, bf16[32,3200]{1,0:T(8,128)(2,1)S(1)}, u32[]{:S(2)}, u32[]{:S(2)}) collective-permute-start(bf16[32,3200]{1,0:T(8,128)(2,1)S(1)} %fusion.12), channel_id=1, source_target_pairs={{0,16},{8,24},{16,0},{24,8},{1,17},{9,25},{17,1},{25,9},{2,18},{10... | collective-permute-start | bytes 614408 | tf_op jit(solution)/shard_map/ppermute | solution.py:51
  460.0 18.1 %collective-permute-start.54 = (bf16[32,3200]{1,0:T(8,128)(2,1)S(1)}, bf16[32,3200]{1,0:T(8,128)(2,1)S(1)}, u32[]{:S(2)}, u32[]{:S(2)}) collective-permute-start(bf16[32,3200]{1,0:T(8,128)(2,1)S(1)} %fusion.12), channel_id=1, source_target_pairs={{0,24},{8,0},{16,8},{24,16},{1,25},{9,1},{17,9},{25,17},{2,26},{10... | collective-permute-start | bytes 614408 | tf_op jit(solution)/shard_map/ppermute | solution.py:51
  479.1 5.6 %collective-permute-start.57 = (bf16[128,3200]{1,0:T(8,128)(2,1)S(1)}, bf16[128,3200]{1,0:T(8,128)(2,1)S(1)}, u32[]{:S(2)}, u32[]{:S(2)}) collective-permute-start(bf16[128,3200]{1,0:T(8,128)(2,1)S(1)} %bitcast_select_fusion.mine_ref), channel_id=1, source_target_pairs={{0,4},{4,0},{1,5},{5,1},{2,6},{6,2},{3,7},{7,3},{8,12},{12,8},{9,1... | collective-permute-start | bytes 2457608 | tf_op jit(solution)/shard_map/ppermute | solution.py:47
  (50 other events, 204.2 us)

commit v8 on v7

--- a/solution.py
+++ b/solution.py
@@ -91,13 +91,12 @@
     return lax.ppermute(first_a, "x", SWAP), lax.ppermute(first_b, "y", SWAP)
 
 
-def grid_scatter_second(got, rest_a, rest_b, *hold):
-    got_a, got_b = got
+def grid_scatter_second(got, rest_a, rest_b, *early):
+    got_a, got_b = after(got, *early)
     onward_a = (rest_a[1].astype(F32) + got_a[1].astype(F32)).astype(B16)
     onward_b = (rest_b[1].astype(F32) + got_b[1].astype(F32)).astype(B16)
     last_a = lax.ppermute(onward_a, "y", SWAP)
     last_b = lax.ppermute(onward_b, "x", SWAP)
-    last_a, last_b = after((last_a, last_b), *hold)
     return (
         rest_a[0].astype(F32) + got_a[0].astype(F32) + last_a.astype(F32),
         rest_b[0].astype(F32) + got_b[0].astype(F32) + last_b.astype(F32),
@@ -665,7 +664,7 @@
             grad_ref, residual_ref, gates_ref, misc_ref, tail_ref, wo_ref, att_ref, moe_ref,
             normed_ref, q_ref, k_ref, v_ref, total_ref,
             x_ref, wq_ref, wk_ref, wv_ref, bias_ref, cos_ref, sin_ref,
-            dense_out, first_a_out, first_b_out, rest_a_out, rest_b_out, residual_out,
+            keep_out, give_out, first_a_out, first_b_out, rest_a_out, rest_b_out, residual_out,
             normed_t, grad_sum, og_ref, logit_ref, gain_ref,
         ) = refs[terms:]
         step = pl.program_id(0)
@@ -736,8 +735,8 @@
         ).astype(B16)
 
         def put(at, lanes, rows):
-            for c in range(2):
-                dense_out[core ^ c, at, :, lanes] = rows[c].astype(B16)
+            keep_out[at, :, lanes] = jnp.where(core == 0, rows[0], rows[1]).astype(B16)
+            give_out[at, :, lanes] = jnp.where(core == 0, rows[1], rows[0]).astype(B16)
 
         def give(grad, lanes):
             for m in range(4):
@@ -795,11 +794,11 @@
         return pl.BlockSpec((rows, cols), lambda i, here: (0, lead + i))
 
     shapes = [
-        jax.ShapeDtypeStruct((2, 4, block, output_at + width + EXTRA), B16),
+        *[jax.ShapeDtypeStruct((4, block, output_at + width + EXTRA), B16)] * 2,
         *[jax.ShapeDtypeStruct((2, tok_rows // 2, width), B16)] * 4,
         jax.ShapeDtypeStruct((tok_rows, width), F32),
     ]
-    dense, *parts, residual_grad = pl.pallas_call(
+    keep, give, *parts, residual_grad = pl.pallas_call(
         kernel,
         out_shape=shapes,
         grid_spec=pltpu.PrefetchScalarGridSpec(
@@ -846,16 +845,16 @@
         moe_in, normed_all, query_rot, key_rot, value_all, totals,
         x_all, dense_full, dense_full, dense_full, bias, cosine, sine,
     )
-    return dense, tuple(parts[:2]), parts[2], parts[3], residual_grad
-
-
-def core_halves(blocks, got):
-    _, _, rows, cols = blocks.shape
+    return keep, give, tuple(parts[:2]), parts[2], parts[3], residual_grad
+
+
+def core_halves(keep, got):
+    _, rows, cols = keep.shape
     half = rows // 2
 
     def kernel(keep_ref, got_ref, first_a, first_b, rest_a, rest_b):
         def total(j, lo):
-            mine = keep_ref[0, j, lo : lo + half, :].astype(F32)
+            mine = keep_ref[j, lo : lo + half, :].astype(F32)
             return (mine + got_ref[j, lo : lo + half, :].astype(F32)).astype(B16)
 
         first_a[0], first_a[1] = total(1, 0), total(3, 0)
@@ -867,25 +866,49 @@
     first_a, first_b, rest_a, rest_b = pl.pallas_call(
         kernel,
         grid=(5,),
-        in_specs=[
-            pl.BlockSpec((1, 4, rows, step), lambda i: (0, 0, 0, i)),
-            pl.BlockSpec((4, rows, step), lambda i: (0, 0, i)),
-        ],
+        in_specs=[pl.BlockSpec((4, rows, step), lambda i: (0, 0, i))] * 2,
         out_specs=[pl.BlockSpec((2, half, step), lambda i: (0, 0, i))] * 4,
         out_shape=[jax.ShapeDtypeStruct((2, half, cols), B16)] * 4,
         compiler_params=pltpu.CompilerParams(vmem_limit_bytes=VMEM_LIMIT),
         name="core_halves",
-    )(blocks, got)
+    )(keep, got)
     return (first_a, first_b), rest_a, rest_b
+
+
+def join_parts(to_x, to_y):
+    count = len(to_x) - 1
+    shape = to_x[0].shape[1:]
+
+    def kernel(*refs):
+        for i in range(2):
+            direct, mine, via = refs[i * (count + 1) : i * (count + 1) + 3]
+            out = refs[2 * (count + 1) + i]
+            out[0] = direct[0]
+            out[1] = plus_low(mine[0], via[0])
+            if count == 3:
+                out[2] = refs[i * (count + 1) + 3][0]
+
+    steps = 4
+    rows = shape[1] // steps
+    part = pl.BlockSpec((1, shape[0], rows, shape[2]), lambda i: (0, 0, i, 0))
+    return pl.pallas_call(
+        kernel,
+        grid=(steps,),
+        in_specs=[part] * (2 * (count + 1)),
+        out_specs=[pl.BlockSpec((count, shape[0], rows, shape[2]), lambda i: (0, 0, i, 0))] * 2,
+        out_shape=[jax.ShapeDtypeStruct((count, *shape), B16)] * 2,
+        compiler_params=pltpu.CompilerParams(vmem_limit_bytes=VMEM_LIMIT),
+        name="join_parts",
+    )(*to_x, *to_y)
 
 
 def dense_outputs(core, mine, other, wide, narrow):
     rows, cols = mine.shape
     at = wide + 2 * narrow
     shapes = [(2 * rows, wide), (2 * rows, narrow), (2 * rows, narrow), (2 * rows, cols - at - EXTRA)]
-    shapes.append((2 * rows, EXTRA))
-
-    def kernel(core_ref, mine_ref, other_ref, query, key, value, output, extra):
+    shapes += [(2 * rows, EXPERTS), (8, 2 * rows)]
+
+    def kernel(core_ref, mine_ref, other_ref, query, key, value, output, router, gains, extra):
         for c in range(2):
             for ref, side in ((mine_ref, c), (other_ref, 1 - c)):
 
@@ -900,11 +923,13 @@
                         value[lines, lanes] = ref[:, lead + 128 : lead + 256].astype(F32)
                     output[lines, :] = ref[:, at : cols - EXTRA].astype(F32)
                     extra[lines, :] = ref[:, cols - EXTRA :].astype(F32)
+        router[...] = extra[:, :EXPERTS]
+        gains[...] = jnp.transpose(extra[...])[EXPERTS : EXPERTS + 8, :]
 
     def fixed(shape):
         return pl.BlockSpec(shape, lambda i, core: (0, 0))
 
-    query, key, value, output, extra = pl.pallas_call(
+    query, key, value, output, router, gains = pl.pallas_call(
         kernel,
         out_shape=[jax.ShapeDtypeStruct(shape, F32) for shape in shapes],
         grid_spec=pltpu.PrefetchScalarGridSpec(
@@ -912,11 +937,12 @@
             grid=(1,),
             in_specs=[fixed(mine.shape)] * 2,
             out_specs=[fixed(shape) for shape in shapes],
+            scratch_shapes=[pltpu.VMEM((2 * rows, EXTRA), F32)],
         ),
         compiler_params=pltpu.CompilerParams(vmem_limit_bytes=VMEM_LIMIT),
         name="dense_outputs",
     )(core.astype(jnp.int32)[None], mine, other)
-    return query, key, value, output, extra[:, :EXPERTS], extra[:, EXPERTS], extra[:, EXPERTS + 1]
+    return query, key, value, output, router, gains[0], gains[1]
 
 
 def make_body(z_size, small_grid):
@@ -1065,7 +1091,7 @@
                 sine,
                 routed_wide,
             )
-            moe_in = after(moe_in, *near_1, *far_0)
+            moe_in = after(moe_in, *near_1, *far_0, *grad_pieces)
             router_rows = misc[:EXPERTS].astype(B16)
             full_attn_gain = misc[EXPERTS]
             full_moe_gain = misc[EXPERTS + 1]
@@ -1117,17 +1143,22 @@
         if small_grid:
             middle = packs[0].shape[0] // 2
             stage_1 = far_and_next(after(near_1, moe_in), packs[2])
-        (slot_grads_mine,) = dispatch_rows(lead, grads_mine, None, None, local, capacity)
+        last = z_size // 2
+        rows_near = [row_pieces[k] for k in range(z_size) if k != last]
+        own_other = swap_core(moe_in)
+        if small_grid:
+            stage_2 = far_and_next(after(stage_1, *rows_near, grads_other, own_other), packs[3])
+        rows_near_other = [own_other] + [
+            swap_core(piece) for piece in after(rows_near[1:], *stage_1)
+        ]
+        (slot_grads_mine,) = dispatch_rows(
+            lead, after(grads_mine, *rows_near_other), None, None, local, capacity
+        )
+        row_last = after(row_pieces[last], slot_grads_mine)
         (slot_grads_other,) = dispatch_rows(
-            lead,
-            after(grads_other, slot_grads_mine, *stage_1, row_pieces[1], row_pieces[-1]),
-            None,
-            None,
-            local,
-            capacity,
+            lead, after(grads_other, row_last), None, None, local, capacity
         )
         if small_grid:
-            stage_2 = far_and_next(after(stage_1, slot_grads_other), packs[3])
             last_far = gather_far([part[middle:] for part in stage_2])
             chunks = [
                 [(part, 0) for part in [packs[0], *near_0, *far_0]],
@@ -1139,9 +1170,8 @@
                 + [(part, middle) for part in stage_2]
                 + [(part, 0) for part in last_far],
             ]
-        row_pieces = after(row_pieces, slot_grads_other)
-        rows_mine = after(row_pieces, *stage_2)
-        rows_other = [swap_core(piece) for piece in row_pieces]
+        rows_mine = after([*rows_near[:last], row_last, *rows_near[last:]], *stage_2)
+        rows_other = [*rows_near_other[:last], swap_core(row_last), *rows_near_other[last:]]
         slot_rows_mine, slot_gates_mine = dispatch_rows(
             lead, grads_mine, rows_mine, router_rows, local, capacity
         )
@@ -1178,12 +1208,7 @@
 
         def second_step(grads, via, *more):
             _, x_a, y_a, _, _, x_b, y_b, _ = grads
-            to_x = [x_a, plus_low(x_b, via[1])]
-            to_y = [y_b, plus_low(y_a, via[0])]
-            if more:
-                to_x.append(more[0])
-                to_y.append(more[1])
-            return cross(jnp.concatenate(to_x, axis=0), jnp.concatenate(to_y, axis=0))
+            return cross(*join_parts((x_a, x_b, via[1], *more[:1]), (y_b, y_a, via[0], *more[1:])))
 
         if small_grid:
             early, late = weight_grads
@@ -1203,7 +1228,7 @@
             early_got = after(early_got, *dx_pieces)
             late_got = second_step(late, [got[2:3] for got in early_got])
         if small_grid:
-            dense_blocks, normed_first, normed_a, normed_b, residual_grad = attention_backward(
+            keep, give, normed_first, normed_a, normed_b, residual_grad = attention_backward(
                 jnp.stack([dp_index, core]).astype(jnp.int32),
                 (dx_low[0], *dx_pieces),
                 out_grad,
@@ -1219,11 +1244,9 @@
                 sine,
             )
             late_got, y_pieces = after((late_got, y_pieces), residual_grad)
-            normed_first, dense_blocks = after((normed_first, dense_blocks), *late_got, *y_pieces)
+            normed_first, keep, give = after((normed_first, keep, give), *late_got, *y_pieces)
             y_pieces += column_send_last(y_low, z_size, *y_pieces)
-            dense_first, dense_a, dense_b = core_halves(
-                dense_blocks, swap_core(dense_blocks[1])
-            )
+            dense_first, dense_a, dense_b = core_halves(keep, swap_core(give))
             normed_got = grid_scatter_first(*normed_first)
             dense_got = grid_scatter_first(*after(dense_first, *normed_got))
             dense_low = across_z(

time: 502 us -> 500 us (level)
  the two profiles are of different devices: /device:TPU:24 before, /device:TPU:0 now
where the time goes in v8:
time: 500 us; the launch traced here: 490 us
  Pallas kernels  180 us (36%)
  waiting for transfers between devices  169 us (34%)
  starting transfers between devices  63.7 us (13%)
  other arithmetic  43 us (9%)
  local copies, waits for them, and re-layouts  32.8 us (7%)
    ppermute x18, waiting for transfers between devices, cyclic(): lax.ppermute(rows, 'z', [(i, (i + shift) % size) for i in range(size)])  113 us
    pallas_call x2, Pallas kernels, experts(): pl.pallas_call(kernel, out_shape=out_shape, grid_spec=pltpu.PrefetchScala...  48.9 us
    pallas_call x1, Pallas kernels, attention_backward(): pl.pallas_call(kernel, out_shape=shapes, grid_spec=pltpu.PrefetchScalarGr...  36.9 us
    ppermute x18, starting transfers between devices, cyclic(): lax.ppermute(rows, 'z', [(i, (i + shift) % size) for i in range(size)])  30.8 us
    pallas_call x1, Pallas kernels, attention_forward(): pl.pallas_call(kernel, grid=(GROUPS,), in_specs=[fixed(tok_rows, width),...  25.4 us
    pallas_call x4, Pallas kernels, combine_rows(): pl.pallas_call(kernel, out_shape=out_shape, grid_spec=pltpu.PrefetchScala...  22.2 us
    ppermute x6, waiting for transfers between devices, gather_near(): return [lax.ppermute(shard, 'x', SWAP), lax.ppermute(shard, 'y', SWAP)]  19.8 us
    pallas_call x4, Pallas kernels, dispatch_rows(): pl.pallas_call(kernel, out_shape=out_shape, grid_spec=pltpu.PrefetchScala...  19.7 us
  transfers between devices with their start and end apart: 58, of which 23 were waited for; matrix products, arithmetic and copies ran while one was open for 9% of the time, Pallas kernels for 29%

profile of v8, /device:TPU:0, one launch (start us, length us, event | category | flops | bytes accessed | tf_op | source)
XLA Modules:
  0.0 490.3 jit_solution(10976437053522022567)
XLA Ops:
  2.4 2.6 convert_reduce_fusion
  5.1 2.0 maximum_maximum_fusion
  7.1 5.1 %collective-permute-start.2 = (bf16[272,1024]{1,0:T(8,128)(2,1)}, bf16[272,1024]{1,0:T(8,128)(2,1)}, u32[]{:S(2)}, u32[]{:S(2)}) collective-permute-start(bf16[272,1024]{1,0:T(8,128)(2,1)} %maximum_maximum_fusion), channel_id=1, source_target_pairs={{0,24},{8,0},{16,8},{24,16},{1,25},{9,1},{17,9},{25,17},{2,26},{10... | collective-permute-start | bytes 1671176 | tf_op jit(solution)/shard_map/ppermute | solution.py:51
  12.7 2.3 concatenate.54.shard_ref
  18.8 1.5 collective-permute-start.1
  26.2 3.1 fusion.5
  30.6 6.7 %collective-permute-done.3 = bf16[272,1024]{1,0:T(8,128)(2,1)} collective-permute-done((bf16[272,1024]{1,0:T(8,128)(2,1)}, bf16[272,1024]{1,0:T(8,128)(2,1)}, u32[]{:S(2)}, u32[]{:S(2)}) %collective-permute-start.3) | collective-permute-done | bytes 557088 | tf_op jit(solution)/shard_map/ppermute | solution.py:51
  37.3 11.1 %collective-permute-done.xa_ref.xb_ref = bf16[128,5248]{1,0:T(8,128)(2,1)S(1)} collective-permute-done((bf16[128,5248]{1,0:T(8,128)(2,1)}, bf16[128,5248]{1,0:T(8,128)(2,1)S(1)}, u32[]{:S(2)}, u32[]{:S(2)}) %collective-permute-start) | collective-permute-done | bytes 1343520 | tf_op jit(solution)/shard_map/ppermute | solution.py:59
  49.7 1.6 collective-permute-start.4
  51.9 13.2 %collective-permute-done.4.da_ref.db_ref = bf16[64,5248]{1,0:T(8,128)(2,1)S(1)} collective-permute-done((bf16[64,5248]{1,0:T(8,128)(2,1)S(1)}, bf16[64,5248]{1,0:T(8,128)(2,1)S(1)}, u32[]{:S(2)}, u32[]{:S(2)}) %collective-permute-start.4) | collective-permute-done | bytes 671776 | tf_op jit(solution)/shard_map/ppermute | solution.py:65
  67.4 1.7 pad_maximum_fusion.1.moved_ref
  71.4 2.6 collective-permute-done.6.other_ref
  74.0 1.5 copy-done.20
  75.6 6.7 %assemble.1.tail_ref.wo_ref.wq_ref.wk_ref.wv_ref.refs_8_.refs_9_.refs_18_.refs_19_.refs_20_ = bf16[1024,3200]{1,0:T(8,128)(2,1)} custom-call(s32[7]{0:T(128)} %stack.78.places_ref, bf16[256,3200]{1,0:T(8,128)(2,1)} %copy-done.6, bf16[384,3200]{1,0:T(8,128)(2,1)} %pad_maximum_fusion.1.moved_ref, bf16[384,3200]{1,0:T(8,128)(2,1)} %copy-done.20), custom_call_target="tpu_custom_call" | custom-call | tf_op jit(solution)/shard_map/assemble/pallas_call | solution.py:147
  82.3 7.1 %collective-permute-done.7.refs_7_ = bf16[768,512]{1,0:T(8,128)(2,1)} collective-permute-done((bf16[768,512]{1,0:T(8,128)(2,1)}, bf16[768,512]{1,0:T(8,128)(2,1)}, u32[]{:S(2)}, u32[]{:S(2)}) %collective-permute-start.7) | collective-permute-done | bytes 786464 | tf_op jit(solution)/shard_map/ppermute | solution.py:59
  92.7 1.8 slice.253
  95.4 1.8 slice.254
  97.8 25.4 %attention.1 = (bf16[1024,1024]{1,0:T(8,128)(2,1)}, bf16[1024,1024]{1,0:T(8,128)(2,1)}, bf16[256,1024]{1,0:T(8,128)(2,1)}, bf16[1024,512]{1,0:T(8,128)(2,1)}, bf...) custom-call(bf16[256,1024]{1,0:T(8,128)(2,1)} %own_ref.1, ...), custom_call_target="tpu_custom_call" | custom-call | tf_op jit(solution)/shard_map/attention/pallas_call | solution.py:594
  123.2 2.2 pad_maximum_fusion.2.packed_ref.code_ref
  129.3 2.8 collective-permute-start.14
  133.1 12.7 %collective-permute-done.14.rest_1_ = bf16[256,1024]{1,0:T(8,128)(2,1)} collective-permute-done((bf16[256,1024]{1,0:T(8,128)(2,1)}, bf16[256,1024]{1,0:T(8,128)(2,1)}, u32[]{:S(2)}, u32[]{:S(2)}) %collective-permute-start.14) | collective-permute-done | bytes 524320 | tf_op jit(solution)/shard_map/ppermute | solution.py:51
  145.8 9.9 %collective-permute-done.17.rest_3_ = bf16[256,1024]{1,0:T(8,128)(2,1)} collective-permute-done((bf16[256,1024]{1,0:T(8,128)(2,1)}, bf16[256,1024]{1,0:T(8,128)(2,1)}, u32[]{:S(2)}, u32[]{:S(2)}) %collective-permute-start.17) | collective-permute-done | bytes 524320 | tf_op jit(solution)/shard_map/ppermute | solution.py:51
  156.6 1.7 pad_maximum_fusion.13
  161.0 2.5 collective-permute-start.15
  163.5 4.9 %dispatch.4.refs_2_ = bf16[4,320,1024]{2,1,0:T(8,128)(2,1)} custom-call(s32[1]{0:T(128)} %bitcast.26.lead_ref, bf16[4,272,1024]{2,1,0:T(8,128)(2,1)} %copy-done), custom_call_target="tpu_custom_call" | custom-call | tf_op jit(solution)/shard_map/dispatch/pallas_call | solution.py:240
  168.4 18.9 %collective-permute-done.15.rest_2_ = bf16[256,1024]{1,0:T(8,128)(2,1)} collective-permute-done((bf16[256,1024]{1,0:T(8,128)(2,1)}, bf16[256,1024]{1,0:T(8,128)(2,1)}, u32[]{:S(2)}, u32[]{:S(2)}) %collective-permute-start.15) | collective-permute-done | bytes 524320 | tf_op jit(solution)/shard_map/ppermute | solution.py:51
  188.5 1.5 collective-permute-start.27
  190.6 1.5 slice.351.rest_4_
  192.1 4.6 dispatch.7.refs_3_
  196.7 5.1 %dispatch.5 = (bf16[4,320,1024]{2,1,0:T(8,128)(2,1)}, f32[4,320,128]{2,1,0:T(8,128)}) custom-call(s32[1]{0:T(128)} %bitcast.26.lead_ref, bf16[4,272,1024]{2,1,0:T(8,128)(2,1)} %copy-done, bf16[256,1024]{1,0:T(8,128)(2,1)} %get-tuple-element.180.rest_0_.refs_11_, bf16[256,1024]{1,0:T(8,128)(2,1)} %collective-permute-done.14.rest_1_, ...), custom_call_target="tpu_custom_call" | custom-call | tf_op jit(solution)/shard_map/dispatch/pallas_call | solution.py:240
  202.7 5.1 %dispatch.6 = (bf16[4,320,1024]{2,1,0:T(8,128)(2,1)}, f32[4,320,128]{2,1,0:T(8,128)}) custom-call(s32[1]{0:T(128)} %bitcast.26.lead_ref, bf16[4,272,1024]{2,1,0:T(8,128)(2,1)} %copy-done.1, bf16[256,1024]{1,0:T(8,128)(2,1)} %copy-done.41, bf16[256,1024]{1,0:T(8,128)(2,1)} %copy-done.42, bf16[256,1024]{1,0:T(8,128)(2,1)} %copy-done.44, ...), custom_call_target="tpu_custom_call" | custom-call | tf_op jit(solution)/shard_map/dispatch/pallas_call | solution.py:240
  207.8 23.7 %experts.2 = (bf16[8,160,1024]{2,1,0:T(8,128)(2,1)}, bf16[8,160,1152]{2,1,0:T(8,128)(2,1)}, bf16[1,1,768,512]{3,2,1,0:T(8,128)(2,1)}, bf16[1,1,768,512]{3,2,1,0:...) custom-call(s32[5]{0:T(128)} %pad_add_fusion.order_ref, ...), custom_call_target="tpu_custom_call" | custom-call | tf_op jit(solution)/shard_map/experts/pallas_call | solution.py:470
  233.1 25.3 %experts.3 = (bf16[8,160,1024]{2,1,0:T(8,128)(2,1)}, bf16[8,160,1152]{2,1,0:T(8,128)(2,1)}, bf16[1,1,768,512]{3,2,1,0:T(8,128)(2,1)}, bf16[1,1,768,512]{3,2,1,0:...) custom-call(s32[5]{0:T(128)} %pad_add_fusion.order_ref, ...), custom_call_target="tpu_custom_call" | custom-call | tf_op jit(solution)/shard_map/experts/pallas_call | solution.py:470
  258.4 5.6 %combine.4 = bf16[4,256,1152]{2,1,0:T(8,128)(2,1)} custom-call(s32[1]{0:T(128)} %bitcast.26.lead_ref, bf16[4,272,1024]{2,1,0:T(8,128)(2,1)} %copy-done.1, bf16[8,160,1152]{2,1,0:T(8,128)(2,1)} %get-tuple-element.201.rest_0_, bf16[8,160,1152]{2,1,0:T(8,128)(2,1)} %get-tuple-element.202.rest_1_), custom_call_target="tpu_custom_call" | custom-call | tf_op jit(solution)/shard_map/combine/pallas_call | solution.py:298
  264.1 4.8 combine.5
  269.4 5.5 %join_parts.2 = (bf16[3,1,768,512]{3,2,1,0:T(8,128)(2,1)}, bf16[3,1,768,512]{3,2,1,0:T(8,128)(2,1)}) custom-call(bf16[1,1,768,512]{3,2,1,0:T(8,128)(2,1)} %get-tuple-element.214.refs_0_, bf16[1,1,768,512]{3,2,1,0:T(8,128)(2,1)} %get-tuple-element.215.refs_1_, bf16[1,1,768,512]{3,2,1,0:T(8,128)(2,1)} %copy-done.31, ...), custom_call_target="tpu_custom_call" | custom-call | tf_op jit(solution)/shard_map/join_parts/pallas_call | solution.py:894
  278.8 6.1 %combine.6 = (bf16[256,1152]{1,0:T(8,128)(2,1)}, bf16[256,1152]{1,0:T(8,128)(2,1)}, bf16[256,1152]{1,0:T(8,128)(2,1)}, bf16[256,1152]{1,0:T(8,128)(2,1)}) custom-call(s32[1]{0:T(128)} %bitcast.26.lead_ref, bf16[4,272,1024]{2,1,0:T(8,128)(2,1)} %copy-done, bf16[8,160,1152]{2,1,0:T(8,128)(2,1)} %get-tuple-element.201.rest_0_, ...), custom_call_target="tpu_custom_call" | custom-call | tf_op jit(solution)/shard_map/combine/pallas_call | solution.py:298
  284.9 2.5 collective-permute-start.34
  288.9 5.7 %combine.7 = (bf16[256,1024]{1,0:T(8,128)(2,1)}, bf16[256,1024]{1,0:T(8,128)(2,1)}, bf16[256,1024]{1,0:T(8,128)(2,1)}, bf16[256,1024]{1,0:T(8,128)(2,1)}) custom-call(s32[1]{0:T(128)} %bitcast.26.lead_ref, bf16[4,272,1024]{2,1,0:T(8,128)(2,1)} %copy-done, bf16[8,160,1024]{2,1,0:T(8,128)(2,1)} %get-tuple-element.203.rest_0_, ...), custom_call_target="tpu_custom_call" | custom-call | tf_op jit(solution)/shard_map/combine/pallas_call | solution.py:298
  294.6 8.5 %collective-permute-done.34.refs_1_ = bf16[256,1152]{1,0:T(8,128)(2,1)S(1)} collective-permute-done((bf16[256,1152]{1,0:T(8,128)(2,1)}, bf16[256,1152]{1,0:T(8,128)(2,1)S(1)}, u32[]{:S(2)}, u32[]{:S(2)}) %collective-permute-start.34) | collective-permute-done | bytes 589856 | tf_op jit(solution)/shard_map/ppermute | solution.py:51
  303.2 11.1 %collective-permute-done.35.refs_2_ = bf16[256,1152]{1,0:T(8,128)(2,1)S(1)} collective-permute-done((bf16[256,1152]{1,0:T(8,128)(2,1)}, bf16[256,1152]{1,0:T(8,128)(2,1)S(1)}, u32[]{:S(2)}, u32[]{:S(2)}) %collective-permute-start.35) | collective-permute-done | bytes 589856 | tf_op jit(solution)/shard_map/ppermute | solution.py:51
  314.3 25.3 %collective-permute-done.36.refs_3_ = bf16[256,1152]{1,0:T(8,128)(2,1)S(1)} collective-permute-done((bf16[256,1152]{1,0:T(8,128)(2,1)}, bf16[256,1152]{1,0:T(8,128)(2,1)S(1)}, u32[]{:S(2)}, u32[]{:S(2)}) %collective-permute-start.36) | collective-permute-done | bytes 589856 | tf_op jit(solution)/shard_map/ppermute | solution.py:51
  339.6 2.3 slice.262.refs_2_
  341.8 2.1 slice.263.refs_5_
  343.9 4.8 join_parts.3
  350.4 3.8 collective-permute-start.40
  354.8 36.9 %attention_grad.1 = (bf16[4,128,3200]{2,1,0:T(8,128)(2,1)}, bf16[4,128,3200]{2,1,0:T(8,128)(2,1)}, bf16[2,128,1024]{2,1,0:T(8,128)(2,1)}, bf16[2,128,1024]{2,1,0...) custom-call(s32[2]{0:T(128)} %pad_add_fusion.1.here_ref, ...), custom_call_target="tpu_custom_call" | custom-call | tf_op jit(solution)/shard_map/attention_grad/pallas_call | solution.py:801
  395.3 2.9 add_bitcast_fusion.3
  398.3 4.1 add_bitcast_fusion.1
  402.4 6.1 %core_halves.1 = (bf16[2,64,3200]{2,1,0:T(8,128)(2,1)}, bf16[2,64,3200]{2,1,0:T(8,128)(2,1)}, bf16[2,64,3200]{2,1,0:T(8,128)(2,1)}, bf16[2,64,3200]{2,1,0:T(8,128)(2,1)}) custom-call(bf16[4,128,3200]{2,1,0:T(8,128)(2,1)} %get-tuple-element.259.keep_ref, bf16[4,128,3200]{2,1,0:T(8,128)(2,1)} %collective-permute-done.42.got_ref), custom_call_target="tpu_custom_call" | custom-call | tf_op jit(solution)/shard_map/core_halves/pallas_call | solution.py:866
  410.2 2.9 fusion
  414.1 2.8 fusion.23
  416.9 11.9 %collective-permute-done.45 = bf16[2,64,3200]{2,1,0:T(8,128)(2,1)S(1)} collective-permute-done((bf16[2,64,3200]{2,1,0:T(8,128)(2,1)}, bf16[2,64,3200]{2,1,0:T(8,128)(2,1)S(1)}, u32[]{:S(2)}, u32[]{:S(2)}) %collective-permute-start.45) | collective-permute-done | bytes 819232 | tf_op jit(solution)/shard_map/ppermute | solution.py:91
  434.0 1.7 fusion.14
  436.3 5.3 %collective-permute-done.50 = bf16[64,3200]{1,0:T(8,128)(2,1)S(1)} collective-permute-done((bf16[64,3200]{1,0:T(8,128)(2,1)S(1)}, bf16[64,3200]{1,0:T(8,128)(2,1)S(1)}, u32[]{:S(2)}, u32[]{:S(2)}) %collective-permute-start.50) | collective-permute-done | bytes 409632 | tf_op jit(solution)/shard_map/ppermute | solution.py:99
  443.8 2.4 collective-permute-start.52
  446.3 2.8 collective-permute-start.53
  449.1 2.4 add_convert_fusion
  451.9 5.2 %collective-permute-done.52 = bf16[32,3200]{1,0:T(8,128)(2,1)S(1)} collective-permute-done((bf16[32,3200]{1,0:T(8,128)(2,1)S(1)}, bf16[32,3200]{1,0:T(8,128)(2,1)S(1)}, u32[]{:S(2)}, u32[]{:S(2)}) %collective-permute-start.52) | collective-permute-done | bytes 204832 | tf_op jit(solution)/shard_map/ppermute | solution.py:51
  457.2 4.8 collective-permute-start.54
  463.7 3.8 collective-permute-done.54
  467.5 11.0 %collective-permute-done.55 = bf16[32,3200]{1,0:T(8,128)(2,1)S(1)} collective-permute-done((bf16[32,3200]{1,0:T(8,128)(2,1)S(1)}, bf16[32,3200]{1,0:T(8,128)(2,1)S(1)}, u32[]{:S(2)}, u32[]{:S(2)}) %collective-permute-start.55) | collective-permute-done | bytes 204832 | tf_op jit(solution)/shard_map/ppermute | solution.py:51
  483.6 3.4 dense_outputs.1
  486.9 1.6 copy.46
  (266 shorter events, 67.4 us)
Async XLA Ops:
  7.1 23.5 %collective-permute-start.2 = (bf16[272,1024]{1,0:T(8,128)(2,1)}, bf16[272,1024]{1,0:T(8,128)(2,1)}, u32[]{:S(2)}, u32[]{:S(2)}) collective-permute-start(bf16[272,1024]{1,0:T(8,128)(2,1)} %maximum_maximum_fusion), channel_id=1, source_target_pairs={{0,24},{8,0},{16,8},{24,16},{1,25},{9,1},{17,9},{25,17},{2,26},{10... | collective-permute-start | bytes 1671176 | tf_op jit(solution)/shard_map/ppermute | solution.py:51
  12.2 25.0 %collective-permute-start.3 = (bf16[272,1024]{1,0:T(8,128)(2,1)}, bf16[272,1024]{1,0:T(8,128)(2,1)}, u32[]{:S(2)}, u32[]{:S(2)}) collective-permute-start(bf16[272,1024]{1,0:T(8,128)(2,1)} %maximum_maximum_fusion), channel_id=1, source_target_pairs={{0,8},{8,16},{16,24},{24,0},{1,9},{9,17},{17,25},{25,1},{2,10},{10... | collective-permute-start | bytes 1671176 | tf_op jit(solution)/shard_map/ppermute | solution.py:51
  17.3 31.1 %collective-permute-start = (bf16[128,5248]{1,0:T(8,128)(2,1)}, bf16[128,5248]{1,0:T(8,128)(2,1)S(1)}, u32[]{:S(2)}, u32[]{:S(2)}) collective-permute-start(bf16[128,5248]{1,0:T(8,128)(2,1)} %pad_maximum_fusion.10), channel_id=1, source_target_pairs={{0,1},{1,0},{2,3},{3,2},{4,5},{5,4},{6,7},{7,6},{8,9},{9,8},{10,11... | collective-permute-start | bytes 4030472 | tf_op jit(solution)/shard_map/ppermute | solution.py:59
  18.8 30.9 %collective-permute-start.1 = (bf16[128,5248]{1,0:T(8,128)(2,1)}, bf16[128,5248]{1,0:T(8,128)(2,1)S(1)}, u32[]{:S(2)}, u32[]{:S(2)}) collective-permute-start(bf16[128,5248]{1,0:T(8,128)(2,1)} %pad_maximum_fusion.10), channel_id=1, source_target_pairs={{0,2},{2,0},{1,3},{3,1},{4,6},{6,4},{5,7},{7,5},{8,10},{10,8},{9,1... | collective-permute-start | bytes 4030472 | tf_op jit(solution)/shard_map/ppermute | solution.py:59
  26.2 99.4 %copy-start.9 = (bf16[768,512]{1,0:T(8,128)(2,1)}, bf16[768,512]{1,0:T(8,128)(2,1)S(1)}, u32[]{:S(2)}) copy-start(bf16[768,512]{1,0:T(8,128)(2,1)S(1)} %get-tuple-element.156.refs_6_) | copy-start | bytes 2359300
  49.7 15.5 %collective-permute-start.4 = (bf16[64,5248]{1,0:T(8,128)(2,1)S(1)}, bf16[64,5248]{1,0:T(8,128)(2,1)S(1)}, u32[]{:S(2)}, u32[]{:S(2)}) collective-permute-start(bf16[64,5248]{1,0:T(8,128)(2,1)S(1)} %slice.247), channel_id=1, source_target_pairs={{0,2},{2,0},{1,3},{3,1},{4,6},{6,4},{5,7},{7,5},{8,10},{10,8},{9,1... | collective-permute-start | bytes 2015240 | tf_op jit(solution)/shard_map/ppermute | solution.py:65
  51.3 15.2 %collective-permute-start.5 = (bf16[64,5248]{1,0:T(8,128)(2,1)S(1)}, bf16[64,5248]{1,0:T(8,128)(2,1)S(1)}, u32[]{:S(2)}, u32[]{:S(2)}) collective-permute-start(bf16[64,5248]{1,0:T(8,128)(2,1)S(1)} %slice.248), channel_id=1, source_target_pairs={{0,1},{1,0},{2,3},{3,2},{4,5},{5,4},{6,7},{7,6},{8,9},{9,8},{10,11... | collective-permute-start | bytes 2015240 | tf_op jit(solution)/shard_map/ppermute | solution.py:65
  69.1 4.9 collective-permute-start.6
  69.1 20.3 %collective-permute-start.7 = (bf16[768,512]{1,0:T(8,128)(2,1)}, bf16[768,512]{1,0:T(8,128)(2,1)}, u32[]{:S(2)}, u32[]{:S(2)}) collective-permute-start(bf16[768,512]{1,0:T(8,128)(2,1)} %get-tuple-element.160.refs_6_), channel_id=1, source_target_pairs={{0,1},{1,0},{2,3},{3,2},{4,5},{5,4},{6,7},{7,6},{8,9},{9,8},{10,11... | collective-permute-start | bytes 2359304 | tf_op jit(solution)/shard_map/ppermute | solution.py:59
  69.7 20.0 %collective-permute-start.8 = (bf16[768,512]{1,0:T(8,128)(2,1)}, bf16[768,512]{1,0:T(8,128)(2,1)}, u32[]{:S(2)}, u32[]{:S(2)}) collective-permute-start(bf16[768,512]{1,0:T(8,128)(2,1)} %get-tuple-element.160.refs_6_), channel_id=1, source_target_pairs={{0,2},{2,0},{1,3},{3,1},{4,6},{6,4},{5,7},{7,5},{8,10},{10,8},{9,1... | collective-permute-start | bytes 2359304 | tf_op jit(solution)/shard_map/ppermute | solution.py:59
  89.7 33.5 %collective-permute-start.10 = (bf16[768,512]{1,0:T(8,128)(2,1)S(1)}, bf16[768,512]{1,0:T(8,128)(2,1)S(1)}, u32[]{:S(2)}, u32[]{:S(2)}) collective-permute-start(bf16[768,512]{1,0:T(8,128)(2,1)S(1)} %copy-done.19), channel_id=1, source_target_pairs={{0,1},{1,0},{2,3},{3,2},{4,5},{5,4},{6,7},{7,6},{8,9},{9,8},{10,11... | collective-permute-start | bytes 2359304 | tf_op jit(solution)/shard_map/ppermute | solution.py:59
  91.2 32.0 %collective-permute-start.11 = (bf16[768,512]{1,0:T(8,128)(2,1)S(1)}, bf16[768,512]{1,0:T(8,128)(2,1)S(1)}, u32[]{:S(2)}, u32[]{:S(2)}) collective-permute-start(bf16[768,512]{1,0:T(8,128)(2,1)S(1)} %copy-done.19), channel_id=1, source_target_pairs={{0,2},{2,0},{1,3},{3,1},{4,6},{6,4},{5,7},{7,5},{8,10},{10,8},{9,1... | collective-permute-start | bytes 2359304 | tf_op jit(solution)/shard_map/ppermute | solution.py:59
  92.2 30.9 %collective-permute-start.9 = (bf16[272,1024]{1,0:T(8,128)(2,1)}, bf16[272,1024]{1,0:T(8,128)(2,1)S(1)}, u32[]{:S(2)}, u32[]{:S(2)}) collective-permute-start(bf16[272,1024]{1,0:T(8,128)(2,1)} %maximum_maximum_fusion), channel_id=1, source_target_pairs={{0,16},{8,24},{16,0},{24,8},{1,17},{9,25},{17,1},{25,9},{2,18},{10... | collective-permute-start | bytes 1671176 | tf_op jit(solution)/shard_map/ppermute | solution.py:51
  94.5 28.7 %collective-permute-start.12 = (bf16[384,512]{1,0:T(8,128)(2,1)}, bf16[384,512]{1,0:T(8,128)(2,1)}, u32[]{:S(2)}, u32[]{:S(2)}) collective-permute-start(bf16[384,512]{1,0:T(8,128)(2,1)} %slice.253), channel_id=1, source_target_pairs={{0,2},{2,0},{1,3},{3,1},{4,6},{6,4},{5,7},{7,5},{8,10},{10,8},{9,1... | collective-permute-start | bytes 1179656 | tf_op jit(solution)/shard_map/ppermute | solution.py:65
  97.2 26.0 %collective-permute-start.13 = (bf16[384,512]{1,0:T(8,128)(2,1)}, bf16[384,512]{1,0:T(8,128)(2,1)}, u32[]{:S(2)}, u32[]{:S(2)}) collective-permute-start(bf16[384,512]{1,0:T(8,128)(2,1)} %slice.254), channel_id=1, source_target_pairs={{0,1},{1,0},{2,3},{3,2},{4,5},{5,4},{6,7},{7,6},{8,9},{9,8},{10,11... | collective-permute-start | bytes 1179656 | tf_op jit(solution)/shard_map/ppermute | solution.py:65
  125.5 31.0 %collective-permute-start.22 = (bf16[4,272,1024]{2,1,0:T(8,128)(2,1)S(1)}, bf16[4,272,1024]{2,1,0:T(8,128)(2,1)S(1)}, u32[]{:S(2)}, u32[]{:S(2)}) collective-permute-start(bf16[4,272,1024]{2,1,0:T(8,128)(2,1)S(1)} %pad_maximum_fusion.2.packed_ref.code_ref), channel_id=1, source_target_pairs={{0,4},{4,0},{1,5},{5,1},{2,6},{6,2},{3,7},{7,3},{8,12},{12,8},{9,1... | collective-permute-start | bytes 6684680 | tf_op jit(solution)/shard_map/ppermute | solution.py:47
  126.8 29.8 %copy-start.10 = (bf16[768,512]{1,0:T(8,128)(2,1)S(1)}, bf16[768,512]{1,0:T(8,128)(2,1)}, u32[]{:S(2)}) copy-start(bf16[768,512]{1,0:T(8,128)(2,1)} %get-tuple-element.157.refs_11_) | copy-start | bytes 2359300
  126.8 28.9 %collective-permute-start.18 = (bf16[1152,512]{1,0:T(8,128)(2,1)S(1)}, bf16[1152,512]{1,0:T(8,128)(2,1)S(1)}, u32[]{:S(2)}, u32[]{:S(2)}) collective-permute-start(bf16[1152,512]{1,0:T(8,128)(2,1)S(1)} %get-tuple-element.354), channel_id=1, source_target_pairs={{0,1},{1,0},{2,3},{3,2},{4,5},{5,4},{6,7},{7,6},{8,9},{9,8},{10,11... | collective-permute-start | bytes 3538952 | tf_op jit(solution)/shard_map/ppermute | solution.py:74
  128.3 27.5 %collective-permute-start.19 = (bf16[1152,512]{1,0:T(8,128)(2,1)S(1)}, bf16[1152,512]{1,0:T(8,128)(2,1)S(1)}, u32[]{:S(2)}, u32[]{:S(2)}) collective-permute-start(bf16[1152,512]{1,0:T(8,128)(2,1)S(1)} %get-tuple-element.353), channel_id=1, source_target_pairs={{0,2},{2,0},{1,3},{3,1},{4,6},{6,4},{5,7},{7,5},{8,10},{10,8},{9,1... | collective-permute-start | bytes 3538952 | tf_op jit(solution)/shard_map/ppermute | solution.py:74
  129.3 16.5 %collective-permute-start.14 = (bf16[256,1024]{1,0:T(8,128)(2,1)}, bf16[256,1024]{1,0:T(8,128)(2,1)}, u32[]{:S(2)}, u32[]{:S(2)}) collective-permute-start(bf16[256,1024]{1,0:T(8,128)(2,1)} %get-tuple-element.180.rest_0_.refs_11_), channel_id=1, source_target_pairs={{0,24},{8,0},{16,8},{24,16},{1,25},{9,1},{17,9},{25,17},{2,26},{10... | collective-permute-start | bytes 1572872 | tf_op jit(solution)/shard_map/ppermute | solution.py:51
  132.1 23.6 %collective-permute-start.17 = (bf16[256,1024]{1,0:T(8,128)(2,1)}, bf16[256,1024]{1,0:T(8,128)(2,1)}, u32[]{:S(2)}, u32[]{:S(2)}) collective-permute-start(bf16[256,1024]{1,0:T(8,128)(2,1)} %get-tuple-element.180.rest_0_.refs_11_), channel_id=1, source_target_pairs={{0,8},{8,16},{16,24},{24,0},{1,9},{9,17},{17,25},{25,1},{2,10},{10... | collective-permute-start | bytes 1572872 | tf_op jit(solution)/shard_map/ppermute | solution.py:51
  145.8 9.9 %collective-permute-start.16 = (bf16[256,1024]{1,0:T(8,128)(2,1)}, bf16[256,1024]{1,0:T(8,128)(2,1)S(1)}, u32[]{:S(2)}, u32[]{:S(2)}) collective-permute-start(bf16[256,1024]{1,0:T(8,128)(2,1)} %get-tuple-element.180.rest_0_.refs_11_), channel_id=1, source_target_pairs={{0,4},{4,0},{1,5},{5,1},{2,6},{6,2},{3,7},{7,3},{8,12},{12,8},{9,1... | collective-permute-start | bytes 1572872 | tf_op jit(solution)/shard_map/ppermute | solution.py:47
  158.9 28.4 %collective-permute-start.23 = (bf16[1152,512]{1,0:T(8,128)(2,1)}, bf16[1152,512]{1,0:T(8,128)(2,1)S(1)}, u32[]{:S(2)}, u32[]{:S(2)}) collective-permute-start(bf16[1152,512]{1,0:T(8,128)(2,1)} %get-tuple-element.352), channel_id=1, source_target_pairs={{0,1},{1,0},{2,3},{3,2},{4,5},{5,4},{6,7},{7,6},{8,9},{9,8},{10,11... | collective-permute-start | bytes 3538952 | tf_op jit(solution)/shard_map/ppermute | solution.py:74
  159.5 28.9 %collective-permute-start.24 = (bf16[1152,512]{1,0:T(8,128)(2,1)}, bf16[1152,512]{1,0:T(8,128)(2,1)S(1)}, u32[]{:S(2)}, u32[]{:S(2)}) collective-permute-start(bf16[1152,512]{1,0:T(8,128)(2,1)} %get-tuple-element.351), channel_id=1, source_target_pairs={{0,2},{2,0},{1,3},{3,1},{4,6},{6,4},{5,7},{7,5},{8,10},{10,8},{9,1... | collective-permute-start | bytes 3538952 | tf_op jit(solution)/shard_map/ppermute | solution.py:74
  160.5 3.0 collective-permute-start.20
  160.5 3.0 collective-permute-start.21
  161.0 26.3 %collective-permute-start.15 = (bf16[256,1024]{1,0:T(8,128)(2,1)}, bf16[256,1024]{1,0:T(8,128)(2,1)}, u32[]{:S(2)}, u32[]{:S(2)}) collective-permute-start(bf16[256,1024]{1,0:T(8,128)(2,1)} %get-tuple-element.180.rest_0_.refs_11_), channel_id=1, source_target_pairs={{0,16},{8,24},{16,0},{24,8},{1,17},{9,25},{17,1},{25,9},{2,18},{10... | collective-permute-start | bytes 1572872 | tf_op jit(solution)/shard_map/ppermute | solution.py:51
  187.3 14.6 %collective-permute-start.25 = (bf16[256,1024]{1,0:T(8,128)(2,1)}, bf16[256,1024]{1,0:T(8,128)(2,1)S(1)}, u32[]{:S(2)}, u32[]{:S(2)}) collective-permute-start(bf16[256,1024]{1,0:T(8,128)(2,1)} %collective-permute-done.15.rest_2_), channel_id=1, source_target_pairs={{0,4},{4,0},{1,5},{5,1},{2,6},{6,2},{3,7},{7,3},{8,12},{12,8},{9,1... | collective-permute-start | bytes 1572872 | tf_op jit(solution)/shard_map/ppermute | solution.py:47
  187.3 20.5 %collective-permute-start.26 = (bf16[384,512]{1,0:T(8,128)(2,1)S(1)}, bf16[384,512]{1,0:T(8,128)(2,1)S(1)}, u32[]{:S(2)}, u32[]{:S(2)}) collective-permute-start(bf16[384,512]{1,0:T(8,128)(2,1)S(1)} %slice.306), channel_id=1, source_target_pairs={{0,2},{2,0},{1,3},{3,1},{4,6},{6,4},{5,7},{7,5},{8,10},{10,8},{9,1... | collective-permute-start | bytes 1179656 | tf_op jit(solution)/shard_map/ppermute | solution.py:65
  188.5 19.4 %collective-permute-start.27 = (bf16[384,512]{1,0:T(8,128)(2,1)S(1)}, bf16[384,512]{1,0:T(8,128)(2,1)}, u32[]{:S(2)}, u32[]{:S(2)}) collective-permute-start(bf16[384,512]{1,0:T(8,128)(2,1)S(1)} %slice.307), channel_id=1, source_target_pairs={{0,1},{1,0},{2,3},{3,2},{4,5},{5,4},{6,7},{7,6},{8,9},{9,8},{10,11... | collective-permute-start | bytes 1179656 | tf_op jit(solution)/shard_map/ppermute | solution.py:65
  207.8 23.7 %copy-start.46 = (bf16[384,512]{1,0:T(8,128)(2,1)}, bf16[384,512]{1,0:T(8,128)(2,1)S(1)}, u32[]{:S(2)}) copy-start(bf16[384,512]{1,0:T(8,128)(2,1)S(1)} %collective-permute-done.26.refs_14_) | copy-start | bytes 1179652
  231.5 26.9 %collective-permute-start.28 = (bf16[1,1,768,512]{3,2,1,0:T(8,128)(2,1)}, bf16[1,1,768,512]{3,2,1,0:T(8,128)(2,1)S(1)}, u32[]{:S(2)}, u32[]{:S(2)}) collective-permute-start(bf16[1,1,768,512]{3,2,1,0:T(8,128)(2,1)} %get-tuple-element.199), channel_id=1, source_target_pairs={{0,1},{1,0},{2,3},{3,2},{4,5},{5,4},{6,7},{7,6},{8,9},{9,8},{10,11... | collective-permute-start | bytes 2359304 | tf_op jit(solution)/shard_map/ppermute | solution.py:74
  232.2 26.3 %collective-permute-start.29 = (bf16[1,1,768,512]{3,2,1,0:T(8,128)(2,1)}, bf16[1,1,768,512]{3,2,1,0:T(8,128)(2,1)S(1)}, u32[]{:S(2)}, u32[]{:S(2)}) collective-permute-start(bf16[1,1,768,512]{3,2,1,0:T(8,128)(2,1)} %get-tuple-element.200), channel_id=1, source_target_pairs={{0,2},{2,0},{1,3},{3,1},{4,6},{6,4},{5,7},{7,5},{8,10},{10,8},{9,1... | collective-permute-start | bytes 2359304 | tf_op jit(solution)/shard_map/ppermute | solution.py:74
  264.0 13.4 %collective-permute-start.30 = (bf16[4,256,1152]{2,1,0:T(8,128)(2,1)}, bf16[4,256,1152]{2,1,0:T(8,128)(2,1)S(1)}, u32[]{:S(2)}, u32[]{:S(2)}) collective-permute-start(bf16[4,256,1152]{2,1,0:T(8,128)(2,1)} %combine.4), channel_id=1, source_target_pairs={{0,4},{4,0},{1,5},{5,1},{2,6},{6,2},{3,7},{7,3},{8,12},{12,8},{9,1... | collective-permute-start | bytes 7077896 | tf_op jit(solution)/shard_map/ppermute | solution.py:47
  268.9 16.0 %collective-permute-start.31 = (bf16[4,256,1024]{2,1,0:T(8,128)(2,1)}, bf16[4,256,1024]{2,1,0:T(8,128)(2,1)}, u32[]{:S(2)}, u32[]{:S(2)}) collective-permute-start(bf16[4,256,1024]{2,1,0:T(8,128)(2,1)} %combine.5), channel_id=1, source_target_pairs={{0,4},{4,0},{1,5},{5,1},{2,6},{6,2},{3,7},{7,3},{8,12},{12,8},{9,1... | collective-permute-start | bytes 6291464 | tf_op jit(solution)/shard_map/ppermute | solution.py:47
  274.9 64.6 %collective-permute-start.32 = (bf16[3,1,768,512]{3,2,1,0:T(8,128)(2,1)}, bf16[3,1,768,512]{3,2,1,0:T(8,128)(2,1)}, u32[]{:S(2)}, u32[]{:S(2)}) collective-permute-start(bf16[3,1,768,512]{3,2,1,0:T(8,128)(2,1)} %get-tuple-element.220), channel_id=1, source_target_pairs={{0,1},{1,0},{2,3},{3,2},{4,5},{5,4},{6,7},{7,6},{8,9},{9,8},{10,11... | collective-permute-start | bytes 7077896 | tf_op jit(solution)/shard_map/ppermute | solution.py:74
  276.4 63.2 %collective-permute-start.33 = (bf16[3,1,768,512]{3,2,1,0:T(8,128)(2,1)}, bf16[3,1,768,512]{3,2,1,0:T(8,128)(2,1)}, u32[]{:S(2)}, u32[]{:S(2)}) collective-permute-start(bf16[3,1,768,512]{3,2,1,0:T(8,128)(2,1)} %get-tuple-element.221), channel_id=1, source_target_pairs={{0,2},{2,0},{1,3},{3,1},{4,6},{6,4},{5,7},{7,5},{8,10},{10,8},{9,1... | collective-permute-start | bytes 7077896 | tf_op jit(solution)/shard_map/ppermute | solution.py:74
  284.9 18.3 %collective-permute-start.34 = (bf16[256,1152]{1,0:T(8,128)(2,1)}, bf16[256,1152]{1,0:T(8,128)(2,1)S(1)}, u32[]{:S(2)}, u32[]{:S(2)}) collective-permute-start(bf16[256,1152]{1,0:T(8,128)(2,1)} %get-tuple-element.222), channel_id=1, source_target_pairs={{0,8},{8,16},{16,24},{24,0},{1,9},{9,17},{17,25},{25,1},{2,10},{10... | collective-permute-start | bytes 1769480 | tf_op jit(solution)/shard_map/ppermute | solution.py:51
  287.4 26.9 %collective-permute-start.35 = (bf16[256,1152]{1,0:T(8,128)(2,1)}, bf16[256,1152]{1,0:T(8,128)(2,1)S(1)}, u32[]{:S(2)}, u32[]{:S(2)}) collective-permute-start(bf16[256,1152]{1,0:T(8,128)(2,1)} %get-tuple-element.223), channel_id=1, source_target_pairs={{0,24},{8,0},{16,8},{24,16},{1,25},{9,1},{17,9},{25,17},{2,26},{10... | collective-permute-start | bytes 1769480 | tf_op jit(solution)/shard_map/ppermute | solution.py:51
  288.7 50.8 %collective-permute-start.36 = (bf16[256,1152]{1,0:T(8,128)(2,1)}, bf16[256,1152]{1,0:T(8,128)(2,1)S(1)}, u32[]{:S(2)}, u32[]{:S(2)}) collective-permute-start(bf16[256,1152]{1,0:T(8,128)(2,1)} %get-tuple-element.224), channel_id=1, source_target_pairs={{0,16},{8,24},{16,0},{24,8},{1,17},{9,25},{17,1},{25,9},{2,18},{10... | collective-permute-start | bytes 1769480 | tf_op jit(solution)/shard_map/ppermute | solution.py:51
  303.2 45.6 %copy-start.35 = (bf16[256,1152]{1,0:T(8,128)(2,1)}, bf16[256,1152]{1,0:T(8,128)(2,1)S(1)}, u32[]{:S(2)}) copy-start(bf16[256,1152]{1,0:T(8,128)(2,1)S(1)} %collective-permute-done.34.refs_1_) | copy-start | bytes 1769476
  314.3 34.4 %copy-start.36 = (bf16[256,1152]{1,0:T(8,128)(2,1)}, bf16[256,1152]{1,0:T(8,128)(2,1)S(1)}, u32[]{:S(2)}) copy-start(bf16[256,1152]{1,0:T(8,128)(2,1)S(1)} %collective-permute-done.35.refs_2_) | copy-start | bytes 1769476
  348.7 43.0 %collective-permute-start.37 = (bf16[2,1,768,512]{3,2,1,0:T(8,128)(2,1)}, bf16[2,1,768,512]{3,2,1,0:T(8,128)(2,1)}, u32[]{:S(2)}, u32[]{:S(2)}) collective-permute-start(bf16[2,1,768,512]{3,2,1,0:T(8,128)(2,1)} %get-tuple-element.235), channel_id=1, source_target_pairs={{0,1},{1,0},{2,3},{3,2},{4,5},{5,4},{6,7},{7,6},{8,9},{9,8},{10,11... | collective-permute-start | bytes 4718600 | tf_op jit(solution)/shard_map/ppermute | solution.py:74
  349.4 42.3 %collective-permute-start.38 = (bf16[2,1,768,512]{3,2,1,0:T(8,128)(2,1)}, bf16[2,1,768,512]{3,2,1,0:T(8,128)(2,1)}, u32[]{:S(2)}, u32[]{:S(2)}) collective-permute-start(bf16[2,1,768,512]{3,2,1,0:T(8,128)(2,1)} %get-tuple-element.236), channel_id=1, source_target_pairs={{0,2},{2,0},{1,3},{3,1},{4,6},{6,4},{5,7},{7,5},{8,10},{10,8},{9,1... | collective-permute-start | bytes 4718600 | tf_op jit(solution)/shard_map/ppermute | solution.py:74
  350.4 41.3 %collective-permute-start.39 = (bf16[256,1024]{1,0:T(8,128)(2,1)S(1)}, bf16[256,1024]{1,0:T(8,128)(2,1)}, u32[]{:S(2)}, u32[]{:S(2)}) collective-permute-start(bf16[256,1024]{1,0:T(8,128)(2,1)S(1)} %copy-done.51), channel_id=1, source_target_pairs={{0,8},{8,16},{16,24},{24,0},{1,9},{9,17},{17,25},{25,1},{2,10},{10... | collective-permute-start | bytes 1572872 | tf_op jit(solution)/shard_map/ppermute | solution.py:51
  350.4 41.3 %collective-permute-start.40 = (bf16[256,1024]{1,0:T(8,128)(2,1)S(1)}, bf16[256,1024]{1,0:T(8,128)(2,1)}, u32[]{:S(2)}, u32[]{:S(2)}) collective-permute-start(bf16[256,1024]{1,0:T(8,128)(2,1)S(1)} %copy-done.50), channel_id=1, source_target_pairs={{0,24},{8,0},{16,8},{24,16},{1,25},{9,1},{17,9},{25,17},{2,26},{10... | collective-permute-start | bytes 1572872 | tf_op jit(solution)/shard_map/ppermute | solution.py:51
  354.8 40.5 %copy-start.32 = (bf16[1,1,768,512]{3,2,1,0:T(8,128)(2,1)S(1)}, bf16[1,1,768,512]{3,2,1,0:T(8,128)(2,1)}, u32[]{:S(2)}) copy-start(bf16[1,1,768,512]{3,2,1,0:T(8,128)(2,1)} %get-tuple-element.284) | copy-start | bytes 2359300
  391.7 10.7 %collective-permute-start.42 = (bf16[4,128,3200]{2,1,0:T(8,128)(2,1)}, bf16[4,128,3200]{2,1,0:T(8,128)(2,1)}, u32[]{:S(2)}, u32[]{:S(2)}) collective-permute-start(bf16[4,128,3200]{2,1,0:T(8,128)(2,1)} %get-tuple-element.260), channel_id=1, source_target_pairs={{0,4},{4,0},{1,5},{5,1},{2,6},{6,2},{3,7},{7,3},{8,12},{12,8},{9,1... | collective-permute-start | bytes 9830408 | tf_op jit(solution)/shard_map/ppermute | solution.py:47
  392.8 15.6 %collective-permute-start.43 = (bf16[2,128,1024]{2,1,0:T(8,128)(2,1)}, bf16[2,128,1024]{2,1,0:T(8,128)(2,1)}, u32[]{:S(2)}, u32[]{:S(2)}) collective-permute-start(bf16[2,128,1024]{2,1,0:T(8,128)(2,1)} %get-tuple-element.263), channel_id=1, source_target_pairs={{0,1},{1,0},{2,3},{3,2},{4,5},{5,4},{6,7},{7,6},{8,9},{9,8},{10,11... | collective-permute-start | bytes 1572872 | tf_op jit(solution)/shard_map/ppermute | solution.py:91
  394.3 14.3 %collective-permute-start.44 = (bf16[2,128,1024]{2,1,0:T(8,128)(2,1)}, bf16[2,128,1024]{2,1,0:T(8,128)(2,1)}, u32[]{:S(2)}, u32[]{:S(2)}) collective-permute-start(bf16[2,128,1024]{2,1,0:T(8,128)(2,1)} %get-tuple-element.264), channel_id=1, source_target_pairs={{0,2},{2,0},{1,3},{3,1},{4,6},{6,4},{5,7},{7,5},{8,10},{10,8},{9,1... | collective-permute-start | bytes 1572872 | tf_op jit(solution)/shard_map/ppermute | solution.py:91
  398.2 38.1 %collective-permute-start.41 = (bf16[256,1024]{1,0:T(8,128)(2,1)}, bf16[256,1024]{1,0:T(8,128)(2,1)S(1)}, u32[]{:S(2)}, u32[]{:S(2)}) collective-permute-start(bf16[256,1024]{1,0:T(8,128)(2,1)} %get-tuple-element.252), channel_id=1, source_target_pairs={{0,16},{8,24},{16,0},{24,8},{1,17},{9,25},{17,1},{25,9},{2,18},{10... | collective-permute-start | bytes 1572872 | tf_op jit(solution)/shard_map/ppermute | solution.py:51
  408.6 20.2 %collective-permute-start.45 = (bf16[2,64,3200]{2,1,0:T(8,128)(2,1)}, bf16[2,64,3200]{2,1,0:T(8,128)(2,1)S(1)}, u32[]{:S(2)}, u32[]{:S(2)}) collective-permute-start(bf16[2,64,3200]{2,1,0:T(8,128)(2,1)} %get-tuple-element.265), channel_id=1, source_target_pairs={{0,1},{1,0},{2,3},{3,2},{4,5},{5,4},{6,7},{7,6},{8,9},{9,8},{10,11... | collective-permute-start | bytes 2457608 | tf_op jit(solution)/shard_map/ppermute | solution.py:91
  409.2 19.9 %collective-permute-start.46 = (bf16[2,64,3200]{2,1,0:T(8,128)(2,1)}, bf16[2,64,3200]{2,1,0:T(8,128)(2,1)S(1)}, u32[]{:S(2)}, u32[]{:S(2)}) collective-permute-start(bf16[2,64,3200]{2,1,0:T(8,128)(2,1)} %get-tuple-element.266), channel_id=1, source_target_pairs={{0,2},{2,0},{1,3},{3,1},{4,6},{6,4},{5,7},{7,5},{8,10},{10,8},{9,1... | collective-permute-start | bytes 2457608 | tf_op jit(solution)/shard_map/ppermute | solution.py:91
  429.2 12.4 %collective-permute-start.50 = (bf16[64,3200]{1,0:T(8,128)(2,1)S(1)}, bf16[64,3200]{1,0:T(8,128)(2,1)S(1)}, u32[]{:S(2)}, u32[]{:S(2)}) collective-permute-start(bf16[64,3200]{1,0:T(8,128)(2,1)S(1)} %fusion.7), channel_id=1, source_target_pairs={{0,1},{1,0},{2,3},{3,2},{4,5},{5,4},{6,7},{7,6},{8,9},{9,8},{10,11... | collective-permute-start | bytes 1228808 | tf_op jit(solution)/shard_map/ppermute | solution.py:99
  430.8 12.4 %collective-permute-start.49 = (bf16[64,3200]{1,0:T(8,128)(2,1)S(1)}, bf16[64,3200]{1,0:T(8,128)(2,1)S(1)}, u32[]{:S(2)}, u32[]{:S(2)}) collective-permute-start(bf16[64,3200]{1,0:T(8,128)(2,1)S(1)} %fusion.6), channel_id=1, source_target_pairs={{0,2},{2,0},{1,3},{3,1},{4,6},{6,4},{5,7},{7,5},{8,10},{10,8},{9,1... | collective-permute-start | bytes 1228808 | tf_op jit(solution)/shard_map/ppermute | solution.py:98
  432.9 29.8 %collective-permute-start.47 = (bf16[128,1024]{1,0:T(8,128)(2,1)S(1)}, bf16[128,1024]{1,0:T(8,128)(2,1)S(1)}, u32[]{:S(2)}, u32[]{:S(2)}) collective-permute-start(bf16[128,1024]{1,0:T(8,128)(2,1)S(1)} %fusion.13), channel_id=1, source_target_pairs={{0,2},{2,0},{1,3},{3,1},{4,6},{6,4},{5,7},{7,5},{8,10},{10,8},{9,1... | collective-permute-start | bytes 786440 | tf_op jit(solution)/shard_map/ppermute | solution.py:98
  435.7 43.9 %collective-permute-start.48 = (bf16[128,1024]{1,0:T(8,128)(2,1)}, bf16[128,1024]{1,0:T(8,128)(2,1)S(1)}, u32[]{:S(2)}, u32[]{:S(2)}) collective-permute-start(bf16[128,1024]{1,0:T(8,128)(2,1)} %fusion.14), channel_id=1, source_target_pairs={{0,1},{1,0},{2,3},{3,2},{4,5},{5,4},{6,7},{7,6},{8,9},{9,8},{10,11... | collective-permute-start | bytes 786440 | tf_op jit(solution)/shard_map/ppermute | solution.py:99
  443.5 8.4 %collective-permute-start.51 = (bf16[32,3200]{1,0:T(8,128)(2,1)S(1)}, bf16[32,3200]{1,0:T(8,128)(2,1)S(1)}, u32[]{:S(2)}, u32[]{:S(2)}) collective-permute-start(bf16[32,3200]{1,0:T(8,128)(2,1)S(1)} %get-tuple-element.348), channel_id=1, source_target_pairs={{0,8},{8,16},{16,24},{24,0},{1,9},{9,17},{17,25},{25,1},{2,10},{10... | collective-permute-start | bytes 614408 | tf_op jit(solution)/shard_map/ppermute | solution.py:51
  443.8 13.2 %collective-permute-start.52 = (bf16[32,3200]{1,0:T(8,128)(2,1)S(1)}, bf16[32,3200]{1,0:T(8,128)(2,1)S(1)}, u32[]{:S(2)}, u32[]{:S(2)}) collective-permute-start(bf16[32,3200]{1,0:T(8,128)(2,1)S(1)} %get-tuple-element.350), channel_id=1, source_target_pairs={{0,16},{8,24},{16,0},{24,8},{1,17},{9,25},{17,1},{25,9},{2,18},{10... | collective-permute-start | bytes 614408 | tf_op jit(solution)/shard_map/ppermute | solution.py:51
  446.3 10.8 %collective-permute-start.53 = (bf16[32,3200]{1,0:T(8,128)(2,1)S(1)}, bf16[32,3200]{1,0:T(8,128)(2,1)S(1)}, u32[]{:S(2)}, u32[]{:S(2)}) collective-permute-start(bf16[32,3200]{1,0:T(8,128)(2,1)S(1)} %get-tuple-element.349), channel_id=1, source_target_pairs={{0,24},{8,0},{16,8},{24,16},{1,25},{9,1},{17,9},{25,17},{2,26},{10... | collective-permute-start | bytes 614408 | tf_op jit(solution)/shard_map/ppermute | solution.py:51
  457.2 10.3 %collective-permute-start.54 = (bf16[32,3200]{1,0:T(8,128)(2,1)S(1)}, bf16[32,3200]{1,0:T(8,128)(2,1)S(1)}, u32[]{:S(2)}, u32[]{:S(2)}) collective-permute-start(bf16[32,3200]{1,0:T(8,128)(2,1)S(1)} %fusion.12), channel_id=1, source_target_pairs={{0,24},{8,0},{16,8},{24,16},{1,25},{9,1},{17,9},{25,17},{2,26},{10... | collective-permute-start | bytes 614408 | tf_op jit(solution)/shard_map/ppermute | solution.py:51
  462.0 16.5 %collective-permute-start.55 = (bf16[32,3200]{1,0:T(8,128)(2,1)S(1)}, bf16[32,3200]{1,0:T(8,128)(2,1)S(1)}, u32[]{:S(2)}, u32[]{:S(2)}) collective-permute-start(bf16[32,3200]{1,0:T(8,128)(2,1)S(1)} %fusion.12), channel_id=1, source_target_pairs={{0,16},{8,24},{16,0},{24,8},{1,17},{9,25},{17,1},{25,9},{2,18},{10... | collective-permute-start | bytes 614408 | tf_op jit(solution)/shard_map/ppermute | solution.py:51
  462.0 16.5 %collective-permute-start.56 = (bf16[32,3200]{1,0:T(8,128)(2,1)S(1)}, bf16[32,3200]{1,0:T(8,128)(2,1)S(1)}, u32[]{:S(2)}, u32[]{:S(2)}) collective-permute-start(bf16[32,3200]{1,0:T(8,128)(2,1)S(1)} %fusion.12), channel_id=1, source_target_pairs={{0,8},{8,16},{16,24},{24,0},{1,9},{9,17},{17,25},{25,1},{2,10},{10... | collective-permute-start | bytes 614408 | tf_op jit(solution)/shard_map/ppermute | solution.py:51
  479.5 3.1 collective-permute-start.57
  (48 other events, 293.3 us)

commit v9 on v8

--- a/solution.py
+++ b/solution.py
@@ -875,31 +875,33 @@
     return (first_a, first_b), rest_a, rest_b
 
 
-def join_parts(to_x, to_y):
-    count = len(to_x) - 1
+def join_parts(to_x, to_y, via):
+    count = len(to_x)
     shape = to_x[0].shape[1:]
 
     def kernel(*refs):
         for i in range(2):
-            direct, mine, via = refs[i * (count + 1) : i * (count + 1) + 3]
+            parts = refs[i * count : (i + 1) * count]
             out = refs[2 * (count + 1) + i]
-            out[0] = direct[0]
-            out[1] = plus_low(mine[0], via[0])
+            out[0] = parts[0][0]
+            out[1] = plus_low(parts[1][0], refs[2 * count + i][0])
             if count == 3:
-                out[2] = refs[i * (count + 1) + 3][0]
+                out[2] = parts[2][0]
 
     steps = 4
     rows = shape[1] // steps
     part = pl.BlockSpec((1, shape[0], rows, shape[2]), lambda i: (0, 0, i, 0))
+    end = via[0].shape[0] - 1
+    last = pl.BlockSpec((1, shape[0], rows, shape[2]), lambda i: (end, 0, i, 0))
     return pl.pallas_call(
         kernel,
         grid=(steps,),
-        in_specs=[part] * (2 * (count + 1)),
+        in_specs=[part] * (2 * count) + [last] * 2,
         out_specs=[pl.BlockSpec((count, shape[0], rows, shape[2]), lambda i: (0, 0, i, 0))] * 2,
         out_shape=[jax.ShapeDtypeStruct((count, *shape), B16)] * 2,
         compiler_params=pltpu.CompilerParams(vmem_limit_bytes=VMEM_LIMIT),
         name="join_parts",
-    )(*to_x, *to_y)
+    )(*to_x, *to_y, *via)
 
 
 def dense_outputs(core, mine, other, wide, narrow):
@@ -964,12 +966,14 @@
             return lax.psum(mine.astype(F32), "z").astype(B16)
         rows = mine.shape[0] // z_size
         low = mine.astype(B16)
-        total = lax.dynamic_slice_in_dim(mine, z * rows, rows, 0)
-        for k in range(1, z_size):
+        steps = [2, 1, 3]
+        got = []
+        for k in steps:
             theirs = lax.dynamic_slice_in_dim(low, (z + k) % z_size * rows, rows, 0)
-            total = total + cyclic(theirs, z_size, k).astype(F32)
-        total = total.astype(B16)
-        quarters = [total] + [cyclic(total, z_size, -k) for k in range(1, z_size)]
+            got.append(cyclic(theirs, z_size, k))
+        total = column_sum(lax.dynamic_slice_in_dim(mine, z * rows, rows, 0), got).astype(B16)
+        sent = {k: cyclic(total, z_size, -k) for k in steps}
+        quarters = [total] + [sent[k] for k in range(1, z_size)]
         places = (jnp.arange(z_size, dtype=jnp.int32) - z) % z_size
         return jnp.take(jnp.stack(quarters), places, axis=0).reshape(mine.shape)
 
@@ -1023,7 +1027,12 @@
         ranks = jnp.sum((place[:, :, None] < place.T[None, :, :]).astype(F32), axis=0)
         code = pack_code(jnp.where(routed.T, ranks, -1.0).astype(B16))
         lead = ((2 * z + core) * local).astype(jnp.int32)[None]
-        grad_pieces = column_pieces(jnp.concatenate([out_grad, code], axis=0), z_size)
+        if small_grid:
+            side = tok_rows // 2
+            x_pack = jnp.concatenate([layer_input[:side], layer_input[side:]], axis=1)
+            start_pack = jnp.concatenate([x_pack, core_half(dense_pack, core)], axis=1)
+        else:
+            grad_pieces = column_pieces(jnp.concatenate([out_grad, code], axis=0), z_size)
 
         query_pos = dp_index * tok_rows + jnp.arange(tok_rows, dtype=jnp.int32)
         in_float = layer_input.astype(F32)
@@ -1040,9 +1049,7 @@
         order = jnp.concatenate([relative, lead])
         visible = (key_pos[None, :] <= query_pos[:, None]) | (key_pos[None, :] < prefix_len[0])
         if small_grid:
-            side = tok_rows // 2
-            x_pack = jnp.concatenate([layer_input[:side], layer_input[side:]], axis=1)
-            start_parts = gather_near(jnp.concatenate([x_pack, core_half(dense_pack, core)], axis=1))
+            start_parts = gather_near(start_pack)
             tables = (
                 *turn_tables(key_pos.astype(F32)),
                 jnp.where(visible.T, 0.0, MASKED_SCORE),
@@ -1052,7 +1059,9 @@
                     for e in range(local)
                 ],
             )
-            tables, grad_near = lax.optimization_barrier((tables, grad_pieces[1::2]))
+            tables, code = lax.optimization_barrier((tables, code))
+            grad_pieces = column_pieces(jnp.concatenate([out_grad, code], axis=0), z_size)
+            grad_near = grad_pieces[1::2]
             cosine, sine, bias, routed_wide, packs = tables
             start_parts += gather_far(after(start_parts, tables, *grad_near))
             dense_parts = [part[:, 2 * model_width :] for part in start_parts]
@@ -1145,7 +1154,7 @@
             stage_1 = far_and_next(after(near_1, moe_in), packs[2])
         last = z_size // 2
         rows_near = [row_pieces[k] for k in range(z_size) if k != last]
-        own_other = swap_core(moe_in)
+        own_other = swap_core(after(moe_in, grads_other))
         if small_grid:
             stage_2 = far_and_next(after(stage_1, *rows_near, grads_other, own_other), packs[3])
         rows_near_other = [own_other] + [
@@ -1154,10 +1163,10 @@
         (slot_grads_mine,) = dispatch_rows(
             lead, after(grads_mine, *rows_near_other), None, None, local, capacity
         )
-        row_last = after(row_pieces[last], slot_grads_mine)
         (slot_grads_other,) = dispatch_rows(
-            lead, after(grads_other, row_last), None, None, local, capacity
+            lead, after(grads_other, slot_grads_mine), None, None, local, capacity
         )
+        row_last = after(row_pieces[last], slot_grads_other)
         if small_grid:
             last_far = gather_far([part[middle:] for part in stage_2])
             chunks = [
@@ -1208,7 +1217,7 @@
 
         def second_step(grads, via, *more):
             _, x_a, y_a, _, _, x_b, y_b, _ = grads
-            return cross(*join_parts((x_a, x_b, via[1], *more[:1]), (y_b, y_a, via[0], *more[1:])))
+            return cross(*join_parts((x_a, x_b, *more[:1]), (y_b, y_a, *more[1:]), via[::-1]))
 
         if small_grid:
             early, late = weight_grads
@@ -1220,13 +1229,13 @@
         dx_other = after(swap_core(dx_other), y_other)
         dx_low = combine_rows(lead, 0, grads_mine, dxs, local, capacity, dx_other)
         dx_low, y_other = after((dx_low, swap_core(y_other)), dx_low[0])
-        dx_pieces = column_send_some(dx_low, z_size) + column_send_last(dx_low, z_size)
+        dx_pieces = column_send_last(dx_low, z_size) + column_send_some(dx_low, z_size)
         y_low = combine_rows(lead, 0, grads_mine, ys, local, capacity, y_other)
         dx_pieces = after(dx_pieces, *y_low)
         y_pieces = column_send_some(after(y_low, *dx_pieces), z_size)
         if small_grid:
             early_got = after(early_got, *dx_pieces)
-            late_got = second_step(late, [got[2:3] for got in early_got])
+            late_got = second_step(late, early_got)
         if small_grid:
             keep, give, normed_first, normed_a, normed_b, residual_grad = attention_backward(
                 jnp.stack([dp_index, core]).astype(jnp.int32),

time: 500 us -> 492 us (0.984)
  waiting for transfers between devices: 169 us -> 160 us
  starting transfers between devices: 63.7 us -> 71.7 us
    ppermute x6, waiting for transfers between devices: 19.8 us -> 7.38 us  [gather_near(): return [lax.ppermute(shard, 'x', SWAP), lax.ppermute(shard, 'y', SWAP)]]
    ppermute x18, starting transfers between devices: 30.8 us -> 37.5 us  [cyclic(): lax.ppermute(rows, 'z', [(i, (i + shift) % size) for i in range(size)])]
    unnamed x107 -> x110, local copies, waits for them, and re-layouts: 12.3 us -> 11.2 us
  transfers between devices with their start and end apart: 58 -> 58, of which waited for: 23 -> 21; matrix products, arithmetic and copies ran while one was open for 9% -> 9% of each run, Pallas kernels for 29% -> 29%
where the time goes in v9:
time: 492 us; the launch traced here: 482 us
  Pallas kernels  179 us (36%)
  waiting for transfers between devices  160 us (33%)
  starting transfers between devices  71.7 us (15%)
  other arithmetic  39.6 us (8%)
  local copies, waits for them, and re-layouts  29.6 us (6%)
    ppermute x18, waiting for transfers between devices, cyclic(): lax.ppermute(rows, 'z', [(i, (i + shift) % size) for i in range(size)])  113 us
    pallas_call x2, Pallas kernels, experts(): pl.pallas_call(kernel, out_shape=out_shape, grid_spec=pltpu.PrefetchScala...  48.9 us
    ppermute x18, starting transfers between devices, cyclic(): lax.ppermute(rows, 'z', [(i, (i + shift) % size) for i in range(size)])  37.5 us
    pallas_call x1, Pallas kernels, attention_backward(): pl.pallas_call(kernel, out_shape=shapes, grid_spec=pltpu.PrefetchScalarGr...  36.9 us
    pallas_call x1, Pallas kernels, attention_forward(): pl.pallas_call(kernel, grid=(GROUPS,), in_specs=[fixed(tok_rows, width),...  25.4 us
    pallas_call x4, Pallas kernels, combine_rows(): pl.pallas_call(kernel, out_shape=out_shape, grid_spec=pltpu.PrefetchScala...  22.2 us
    pallas_call x4, Pallas kernels, dispatch_rows(): pl.pallas_call(kernel, out_shape=out_shape, grid_spec=pltpu.PrefetchScala...  19.6 us
    ppermute x3, waiting for transfers between devices, gather_far(): lax.ppermute(from_x[:half], 'y', SWAP)  14 us
  transfers between devices with their start and end apart: 58, of which 21 were waited for; matrix products, arithmetic and copies ran while one was open for 9% of the time, Pallas kernels for 29%

profile of v9, /device:TPU:0, one launch (start us, length us, event | category | flops | bytes accessed | tf_op | source)
XLA Modules:
  0.0 482.4 jit_solution(7153051591521484939)
XLA Ops:
  4.2 2.1 concatenate.57.shard_ref
  8.7 3.0 collective-permute-start
  11.7 1.5 collective-permute-start.1
  13.6 2.6 convert_reduce_fusion
  21.6 3.1 fusion.5
  26.1 3.7 collective-permute-start.2
  29.7 13.0 %collective-permute-done.2 = bf16[272,1024]{1,0:T(8,128)(2,1)S(1)} collective-permute-done((bf16[272,1024]{1,0:T(8,128)(2,1)S(1)}, bf16[272,1024]{1,0:T(8,128)(2,1)S(1)}, u32[]{:S(2)}, u32[]{:S(2)}) %collective-permute-start.2) | collective-permute-done | bytes 557088 | tf_op jit(solution)/shard_map/ppermute | solution.py:51
  42.7 11.1 %collective-permute-done.3 = bf16[272,1024]{1,0:T(8,128)(2,1)S(1)} collective-permute-done((bf16[272,1024]{1,0:T(8,128)(2,1)S(1)}, bf16[272,1024]{1,0:T(8,128)(2,1)S(1)}, u32[]{:S(2)}, u32[]{:S(2)}) %collective-permute-start.3) | collective-permute-done | bytes 557088 | tf_op jit(solution)/shard_map/ppermute | solution.py:51
  56.2 14.0 %collective-permute-done.4.da_ref.db_ref = bf16[64,5248]{1,0:T(8,128)(2,1)S(1)} collective-permute-done((bf16[64,5248]{1,0:T(8,128)(2,1)S(1)}, bf16[64,5248]{1,0:T(8,128)(2,1)S(1)}, u32[]{:S(2)}, u32[]{:S(2)}) %collective-permute-start.4) | collective-permute-done | bytes 671776 | tf_op jit(solution)/shard_map/ppermute | solution.py:65
  72.0 1.7 pad_maximum_fusion.1.moved_ref
  75.9 2.8 collective-permute-done.6.other_ref
  78.6 1.5 copy-done.20
  80.1 6.7 %assemble.1.tail_ref.wo_ref.wq_ref.wk_ref.wv_ref.refs_8_.refs_9_.refs_18_.refs_19_.refs_20_ = bf16[1024,3200]{1,0:T(8,128)(2,1)} custom-call(s32[7]{0:T(128)} %stack.78.places_ref, bf16[256,3200]{1,0:T(8,128)(2,1)} %copy-done.6, bf16[384,3200]{1,0:T(8,128)(2,1)} %pad_maximum_fusion.1.moved_ref, bf16[384,3200]{1,0:T(8,128)(2,1)} %copy-done.20), custom_call_target="tpu_custom_call" | custom-call | tf_op jit(solution)/shard_map/assemble/pallas_call | solution.py:147
  86.9 7.1 %collective-permute-done.7.refs_7_ = bf16[768,512]{1,0:T(8,128)(2,1)} collective-permute-done((bf16[768,512]{1,0:T(8,128)(2,1)}, bf16[768,512]{1,0:T(8,128)(2,1)}, u32[]{:S(2)}, u32[]{:S(2)}) %collective-permute-start.7) | collective-permute-done | bytes 786464 | tf_op jit(solution)/shard_map/ppermute | solution.py:59
  94.3 1.5 collective-permute-start.10
  97.3 1.8 slice.247
  100.2 1.8 slice.248
  102.5 25.4 %attention.1 = (bf16[1024,1024]{1,0:T(8,128)(2,1)}, bf16[1024,1024]{1,0:T(8,128)(2,1)}, bf16[256,1024]{1,0:T(8,128)(2,1)}, bf16[1024,512]{1,0:T(8,128)(2,1)}, bf...) custom-call(bf16[256,1024]{1,0:T(8,128)(2,1)} %own_ref.1, ...), custom_call_target="tpu_custom_call" | custom-call | tf_op jit(solution)/shard_map/attention/pallas_call | solution.py:594
  128.0 2.2 pad_maximum_fusion.2.packed_ref.code_ref
  134.0 3.4 collective-permute-start.14
  138.0 12.1 %collective-permute-done.14.rest_1_ = bf16[256,1024]{1,0:T(8,128)(2,1)} collective-permute-done((bf16[256,1024]{1,0:T(8,128)(2,1)}, bf16[256,1024]{1,0:T(8,128)(2,1)}, u32[]{:S(2)}, u32[]{:S(2)}) %collective-permute-start.14) | collective-permute-done | bytes 524320 | tf_op jit(solution)/shard_map/ppermute | solution.py:51
  150.1 10.1 %collective-permute-done.18.rest_3_ = bf16[256,1024]{1,0:T(8,128)(2,1)} collective-permute-done((bf16[256,1024]{1,0:T(8,128)(2,1)}, bf16[256,1024]{1,0:T(8,128)(2,1)}, u32[]{:S(2)}, u32[]{:S(2)}) %collective-permute-start.18) | collective-permute-done | bytes 524320 | tf_op jit(solution)/shard_map/ppermute | solution.py:51
  160.3 1.8 pad_maximum_fusion.13
  164.4 2.1 collective-permute-start.15
  166.8 4.7 dispatch.4.refs_2_
  171.5 4.5 dispatch.5.refs_3_
  176.0 14.7 %collective-permute-done.15.rest_2_ = bf16[256,1024]{1,0:T(8,128)(2,1)} collective-permute-done((bf16[256,1024]{1,0:T(8,128)(2,1)}, bf16[256,1024]{1,0:T(8,128)(2,1)}, u32[]{:S(2)}, u32[]{:S(2)}) %collective-permute-start.15) | collective-permute-done | bytes 524320 | tf_op jit(solution)/shard_map/ppermute | solution.py:51
  191.8 1.6 collective-permute-start.27
  194.1 1.5 slice.343.rest_4_
  195.6 5.2 %dispatch.6 = (bf16[4,320,1024]{2,1,0:T(8,128)(2,1)}, f32[4,320,128]{2,1,0:T(8,128)}) custom-call(s32[1]{0:T(128)} %bitcast.26.lead_ref, bf16[4,272,1024]{2,1,0:T(8,128)(2,1)} %copy-done, bf16[256,1024]{1,0:T(8,128)(2,1)} %get-tuple-element.185.rest_0_.refs_11_, bf16[256,1024]{1,0:T(8,128)(2,1)} %collective-permute-done.14.rest_1_, ...), custom_call_target="tpu_custom_call" | custom-call | tf_op jit(solution)/shard_map/dispatch/pallas_call | solution.py:240
  201.6 5.2 %dispatch.7 = (bf16[4,320,1024]{2,1,0:T(8,128)(2,1)}, f32[4,320,128]{2,1,0:T(8,128)}) custom-call(s32[1]{0:T(128)} %bitcast.26.lead_ref, bf16[4,272,1024]{2,1,0:T(8,128)(2,1)} %copy-done.1, bf16[256,1024]{1,0:T(8,128)(2,1)} %collective-permute-done.17.rest_0_, bf16[256,1024]{1,0:T(8,128)(2,1)} %copy-done.45, bf16[256,1024]{1,0:T(8,128)(2,1)} %copy-done.47, ...), custom_call_target="tpu_custom_call" | custom-call | tf_op jit(solution)/shard_map/dispatch/pallas_call | solution.py:240
  206.8 23.7 %experts.2 = (bf16[8,160,1024]{2,1,0:T(8,128)(2,1)}, bf16[8,160,1152]{2,1,0:T(8,128)(2,1)}, bf16[1,1,768,512]{3,2,1,0:T(8,128)(2,1)}, bf16[1,1,768,512]{3,2,1,0:...) custom-call(s32[5]{0:T(128)} %pad_add_fusion.order_ref, ...), custom_call_target="tpu_custom_call" | custom-call | tf_op jit(solution)/shard_map/experts/pallas_call | solution.py:470
  232.1 25.2 %experts.3 = (bf16[8,160,1024]{2,1,0:T(8,128)(2,1)}, bf16[8,160,1152]{2,1,0:T(8,128)(2,1)}, bf16[1,1,768,512]{3,2,1,0:T(8,128)(2,1)}, bf16[1,1,768,512]{3,2,1,0:...) custom-call(s32[5]{0:T(128)} %pad_add_fusion.order_ref, ...), custom_call_target="tpu_custom_call" | custom-call | tf_op jit(solution)/shard_map/experts/pallas_call | solution.py:470
  257.4 5.6 %combine.4 = bf16[4,256,1152]{2,1,0:T(8,128)(2,1)} custom-call(s32[1]{0:T(128)} %bitcast.26.lead_ref, bf16[4,272,1024]{2,1,0:T(8,128)(2,1)} %copy-done.1, bf16[8,160,1152]{2,1,0:T(8,128)(2,1)} %get-tuple-element.205.rest_0_, bf16[8,160,1152]{2,1,0:T(8,128)(2,1)} %get-tuple-element.206.rest_1_), custom_call_target="tpu_custom_call" | custom-call | tf_op jit(solution)/shard_map/combine/pallas_call | solution.py:298
  263.0 4.8 combine.5
  268.3 5.5 %join_parts.2 = (bf16[3,1,768,512]{3,2,1,0:T(8,128)(2,1)}, bf16[3,1,768,512]{3,2,1,0:T(8,128)(2,1)}) custom-call(bf16[1,1,768,512]{3,2,1,0:T(8,128)(2,1)} %get-tuple-element.220.refs_0_, bf16[1,1,768,512]{3,2,1,0:T(8,128)(2,1)} %get-tuple-element.221.refs_1_, bf16[1,1,768,512]{3,2,1,0:T(8,128)(2,1)} %get-tuple-element.222.refs_2_, ...), custom_call_target="tpu_custom_call" | custom-call | tf_op jit(solution)/shard_map/join_parts/pallas_call | solution.py:896
  276.3 6.1 %combine.6 = (bf16[256,1152]{1,0:T(8,128)(2,1)}, bf16[256,1152]{1,0:T(8,128)(2,1)}, bf16[256,1152]{1,0:T(8,128)(2,1)}, bf16[256,1152]{1,0:T(8,128)(2,1)}) custom-call(s32[1]{0:T(128)} %bitcast.26.lead_ref, bf16[4,272,1024]{2,1,0:T(8,128)(2,1)} %copy-done, bf16[8,160,1152]{2,1,0:T(8,128)(2,1)} %get-tuple-element.205.rest_0_, ...), custom_call_target="tpu_custom_call" | custom-call | tf_op jit(solution)/shard_map/combine/pallas_call | solution.py:298
  282.5 3.5 collective-permute-start.35
  286.4 5.6 %combine.7 = (bf16[256,1024]{1,0:T(8,128)(2,1)}, bf16[256,1024]{1,0:T(8,128)(2,1)}, bf16[256,1024]{1,0:T(8,128)(2,1)}, bf16[256,1024]{1,0:T(8,128)(2,1)}) custom-call(s32[1]{0:T(128)} %bitcast.26.lead_ref, bf16[4,272,1024]{2,1,0:T(8,128)(2,1)} %copy-done, bf16[8,160,1024]{2,1,0:T(8,128)(2,1)} %get-tuple-element.207.rest_0_, ...), custom_call_target="tpu_custom_call" | custom-call | tf_op jit(solution)/shard_map/combine/pallas_call | solution.py:298
  292.0 32.0 %collective-permute-done.34.refs_1_ = bf16[256,1152]{1,0:T(8,128)(2,1)S(1)} collective-permute-done((bf16[256,1152]{1,0:T(8,128)(2,1)}, bf16[256,1152]{1,0:T(8,128)(2,1)S(1)}, u32[]{:S(2)}, u32[]{:S(2)}) %collective-permute-start.34) | collective-permute-done | bytes 589856 | tf_op jit(solution)/shard_map/ppermute | solution.py:51
  325.2 2.0 collective-permute-done.32.refs_5_
  328.6 4.7 join_parts.3
  335.8 8.7 %collective-permute-start.39 = (bf16[256,1024]{1,0:T(8,128)(2,1)}, bf16[256,1024]{1,0:T(8,128)(2,1)}, u32[]{:S(2)}, u32[]{:S(2)}) collective-permute-start(bf16[256,1024]{1,0:T(8,128)(2,1)} %get-tuple-element.241), channel_id=1, source_target_pairs={{0,8},{8,16},{16,24},{24,0},{1,9},{9,17},{17,25},{25,1},{2,10},{10... | collective-permute-start | bytes 1572872 | tf_op jit(solution)/shard_map/ppermute | solution.py:51
  345.2 36.9 %attention_grad.1 = (bf16[4,128,3200]{2,1,0:T(8,128)(2,1)}, bf16[4,128,3200]{2,1,0:T(8,128)(2,1)}, bf16[2,128,1024]{2,1,0:T(8,128)(2,1)}, bf16[2,128,1024]{2,1,0...) custom-call(s32[2]{0:T(128)} %pad_add_fusion.1.here_ref, ...), custom_call_target="tpu_custom_call" | custom-call | tf_op jit(solution)/shard_map/attention_grad/pallas_call | solution.py:801
  385.7 2.9 add_bitcast_fusion.3
  388.6 1.8 collective-permute-start.41
  390.4 4.1 add_bitcast_fusion.1
  394.5 6.0 %core_halves.1 = (bf16[2,64,3200]{2,1,0:T(8,128)(2,1)}, bf16[2,64,3200]{2,1,0:T(8,128)(2,1)}, bf16[2,64,3200]{2,1,0:T(8,128)(2,1)}, bf16[2,64,3200]{2,1,0:T(8,128)(2,1)}) custom-call(bf16[4,128,3200]{2,1,0:T(8,128)(2,1)} %get-tuple-element.263.keep_ref, bf16[4,128,3200]{2,1,0:T(8,128)(2,1)} %collective-permute-done.42.got_ref), custom_call_target="tpu_custom_call" | custom-call | tf_op jit(solution)/shard_map/core_halves/pallas_call | solution.py:866
  402.2 2.9 fusion
  406.1 2.8 fusion.28
  408.9 11.7 %collective-permute-done.45 = bf16[2,64,3200]{2,1,0:T(8,128)(2,1)S(1)} collective-permute-done((bf16[2,64,3200]{2,1,0:T(8,128)(2,1)}, bf16[2,64,3200]{2,1,0:T(8,128)(2,1)S(1)}, u32[]{:S(2)}, u32[]{:S(2)}) %collective-permute-start.45) | collective-permute-done | bytes 819232 | tf_op jit(solution)/shard_map/ppermute | solution.py:91
  421.0 1.5 collective-permute-start.50
  425.8 1.7 fusion.12
  428.1 5.3 %collective-permute-done.50 = bf16[64,3200]{1,0:T(8,128)(2,1)S(1)} collective-permute-done((bf16[64,3200]{1,0:T(8,128)(2,1)S(1)}, bf16[64,3200]{1,0:T(8,128)(2,1)S(1)}, u32[]{:S(2)}, u32[]{:S(2)}) %collective-permute-start.50) | collective-permute-done | bytes 409632 | tf_op jit(solution)/shard_map/ppermute | solution.py:99
  433.5 1.5 collective-permute-done.49
  436.6 2.0 collective-permute-start.52
  438.6 1.8 collective-permute-start.53
  440.4 2.4 add_convert_fusion
  442.9 5.8 %collective-permute-done.51 = bf16[32,3200]{1,0:T(8,128)(2,1)S(1)} collective-permute-done((bf16[32,3200]{1,0:T(8,128)(2,1)S(1)}, bf16[32,3200]{1,0:T(8,128)(2,1)S(1)}, u32[]{:S(2)}, u32[]{:S(2)}) %collective-permute-start.51) | collective-permute-done | bytes 204832 | tf_op jit(solution)/shard_map/ppermute | solution.py:51
  448.9 4.5 collective-permute-start.54
  454.7 1.9 collective-permute-start.56
  458.8 11.8 %collective-permute-done.55 = bf16[32,3200]{1,0:T(8,128)(2,1)S(1)} collective-permute-done((bf16[32,3200]{1,0:T(8,128)(2,1)S(1)}, bf16[32,3200]{1,0:T(8,128)(2,1)S(1)}, u32[]{:S(2)}, u32[]{:S(2)}) %collective-permute-start.55) | collective-permute-done | bytes 204832 | tf_op jit(solution)/shard_map/ppermute | solution.py:51
  475.6 3.4 dense_outputs.1
  479.0 1.6 copy.46
  (266 shorter events, 64.3 us)
Async XLA Ops:
  8.7 45.2 %collective-permute-start = (bf16[128,5248]{1,0:T(8,128)(2,1)}, bf16[128,5248]{1,0:T(8,128)(2,1)S(1)}, u32[]{:S(2)}, u32[]{:S(2)}) collective-permute-start(bf16[128,5248]{1,0:T(8,128)(2,1)} %pad_maximum_fusion.10), channel_id=1, source_target_pairs={{0,1},{1,0},{2,3},{3,2},{4,5},{5,4},{6,7},{7,6},{8,9},{9,8},{10,11... | collective-permute-start | bytes 4030472 | tf_op jit(solution)/shard_map/ppermute | solution.py:59
  11.7 43.0 %collective-permute-start.1 = (bf16[128,5248]{1,0:T(8,128)(2,1)}, bf16[128,5248]{1,0:T(8,128)(2,1)S(1)}, u32[]{:S(2)}, u32[]{:S(2)}) collective-permute-start(bf16[128,5248]{1,0:T(8,128)(2,1)} %pad_maximum_fusion.10), channel_id=1, source_target_pairs={{0,2},{2,0},{1,3},{3,1},{4,6},{6,4},{5,7},{7,5},{8,10},{10,8},{9,1... | collective-permute-start | bytes 4030472 | tf_op jit(solution)/shard_map/ppermute | solution.py:59
  21.6 108.7 %copy-start.8 = (bf16[768,512]{1,0:T(8,128)(2,1)}, bf16[768,512]{1,0:T(8,128)(2,1)S(1)}, u32[]{:S(2)}) copy-start(bf16[768,512]{1,0:T(8,128)(2,1)S(1)} %get-tuple-element.158.refs_6_) | copy-start | bytes 2359300
  26.1 27.8 %copy-start.21 = (bf16[272,1024]{1,0:T(8,128)(2,1)}, bf16[272,1024]{1,0:T(8,128)(2,1)S(1)}, u32[]{:S(2)}) copy-start(bf16[272,1024]{1,0:T(8,128)(2,1)S(1)} %constant_dynamic-update-slice_fusion) | copy-start | bytes 1671172
  26.1 16.7 %collective-permute-start.2 = (bf16[272,1024]{1,0:T(8,128)(2,1)S(1)}, bf16[272,1024]{1,0:T(8,128)(2,1)S(1)}, u32[]{:S(2)}, u32[]{:S(2)}) collective-permute-start(bf16[272,1024]{1,0:T(8,128)(2,1)S(1)} %constant_dynamic-update-slice_fusion), channel_id=1, source_target_pairs={{0,24},{8,0},{16,8},{24,16},{1,25},{9,1},{17,9},{25,17},{2,26},{10... | collective-permute-start | bytes 1671176 | tf_op jit(solution)/shard_map/ppermute | solution.py:51
  29.7 24.2 %collective-permute-start.3 = (bf16[272,1024]{1,0:T(8,128)(2,1)S(1)}, bf16[272,1024]{1,0:T(8,128)(2,1)S(1)}, u32[]{:S(2)}, u32[]{:S(2)}) collective-permute-start(bf16[272,1024]{1,0:T(8,128)(2,1)S(1)} %constant_dynamic-update-slice_fusion), channel_id=1, source_target_pairs={{0,8},{8,16},{16,24},{24,0},{1,9},{9,17},{17,25},{25,1},{2,10},{10... | collective-permute-start | bytes 1671176 | tf_op jit(solution)/shard_map/ppermute | solution.py:51
  54.8 15.5 %collective-permute-start.4 = (bf16[64,5248]{1,0:T(8,128)(2,1)S(1)}, bf16[64,5248]{1,0:T(8,128)(2,1)S(1)}, u32[]{:S(2)}, u32[]{:S(2)}) collective-permute-start(bf16[64,5248]{1,0:T(8,128)(2,1)S(1)} %slice.241), channel_id=1, source_target_pairs={{0,2},{2,0},{1,3},{3,1},{4,6},{6,4},{5,7},{7,5},{8,10},{10,8},{9,1... | collective-permute-start | bytes 2015240 | tf_op jit(solution)/shard_map/ppermute | solution.py:65
  55.4 15.7 %collective-permute-start.5 = (bf16[64,5248]{1,0:T(8,128)(2,1)S(1)}, bf16[64,5248]{1,0:T(8,128)(2,1)S(1)}, u32[]{:S(2)}, u32[]{:S(2)}) collective-permute-start(bf16[64,5248]{1,0:T(8,128)(2,1)S(1)} %slice.242), channel_id=1, source_target_pairs={{0,1},{1,0},{2,3},{3,2},{4,5},{5,4},{6,7},{7,6},{8,9},{9,8},{10,11... | collective-permute-start | bytes 2015240 | tf_op jit(solution)/shard_map/ppermute | solution.py:65
  73.7 4.9 %collective-permute-start.6 = (bf16[384,3200]{1,0:T(8,128)(2,1)}, bf16[384,3200]{1,0:T(8,128)(2,1)S(1)}, u32[]{:S(2)}, u32[]{:S(2)}) collective-permute-start(bf16[384,3200]{1,0:T(8,128)(2,1)} %pad_maximum_fusion.1.moved_ref), channel_id=1, source_target_pairs={{0,4},{4,0},{1,5},{5,1},{2,6},{6,2},{3,7},{7,3},{8,12},{12,8},{9,1... | collective-permute-start | bytes 7372808 | tf_op jit(solution)/shard_map/ppermute | solution.py:47
  73.7 20.3 %collective-permute-start.7 = (bf16[768,512]{1,0:T(8,128)(2,1)}, bf16[768,512]{1,0:T(8,128)(2,1)}, u32[]{:S(2)}, u32[]{:S(2)}) collective-permute-start(bf16[768,512]{1,0:T(8,128)(2,1)} %get-tuple-element.163.refs_6_), channel_id=1, source_target_pairs={{0,1},{1,0},{2,3},{3,2},{4,5},{5,4},{6,7},{7,6},{8,9},{9,8},{10,11... | collective-permute-start | bytes 2359304 | tf_op jit(solution)/shard_map/ppermute | solution.py:59
  74.3 20.0 %collective-permute-start.8 = (bf16[768,512]{1,0:T(8,128)(2,1)}, bf16[768,512]{1,0:T(8,128)(2,1)}, u32[]{:S(2)}, u32[]{:S(2)}) collective-permute-start(bf16[768,512]{1,0:T(8,128)(2,1)} %get-tuple-element.163.refs_6_), channel_id=1, source_target_pairs={{0,2},{2,0},{1,3},{3,1},{4,6},{6,4},{5,7},{7,5},{8,10},{10,8},{9,1... | collective-permute-start | bytes 2359304 | tf_op jit(solution)/shard_map/ppermute | solution.py:59
  94.3 33.7 %collective-permute-start.10 = (bf16[768,512]{1,0:T(8,128)(2,1)S(1)}, bf16[768,512]{1,0:T(8,128)(2,1)S(1)}, u32[]{:S(2)}, u32[]{:S(2)}) collective-permute-start(bf16[768,512]{1,0:T(8,128)(2,1)S(1)} %copy-done.19), channel_id=1, source_target_pairs={{0,1},{1,0},{2,3},{3,2},{4,5},{5,4},{6,7},{7,6},{8,9},{9,8},{10,11... | collective-permute-start | bytes 2359304 | tf_op jit(solution)/shard_map/ppermute | solution.py:59
  95.7 32.2 %collective-permute-start.11 = (bf16[768,512]{1,0:T(8,128)(2,1)S(1)}, bf16[768,512]{1,0:T(8,128)(2,1)S(1)}, u32[]{:S(2)}, u32[]{:S(2)}) collective-permute-start(bf16[768,512]{1,0:T(8,128)(2,1)S(1)} %copy-done.19), channel_id=1, source_target_pairs={{0,2},{2,0},{1,3},{3,1},{4,6},{6,4},{5,7},{7,5},{8,10},{10,8},{9,1... | collective-permute-start | bytes 2359304 | tf_op jit(solution)/shard_map/ppermute | solution.py:59
  96.7 31.1 %collective-permute-start.9 = (bf16[272,1024]{1,0:T(8,128)(2,1)}, bf16[272,1024]{1,0:T(8,128)(2,1)}, u32[]{:S(2)}, u32[]{:S(2)}) collective-permute-start(bf16[272,1024]{1,0:T(8,128)(2,1)} %copy-done.21), channel_id=1, source_target_pairs={{0,16},{8,24},{16,0},{24,8},{1,17},{9,25},{17,1},{25,9},{2,18},{10... | collective-permute-start | bytes 1671176 | tf_op jit(solution)/shard_map/ppermute | solution.py:51
  99.1 28.8 %collective-permute-start.12 = (bf16[384,512]{1,0:T(8,128)(2,1)}, bf16[384,512]{1,0:T(8,128)(2,1)}, u32[]{:S(2)}, u32[]{:S(2)}) collective-permute-start(bf16[384,512]{1,0:T(8,128)(2,1)} %slice.247), channel_id=1, source_target_pairs={{0,2},{2,0},{1,3},{3,1},{4,6},{6,4},{5,7},{7,5},{8,10},{10,8},{9,1... | collective-permute-start | bytes 1179656 | tf_op jit(solution)/shard_map/ppermute | solution.py:65
  101.9 26.0 %copy-start.22 = (bf16[272,1024]{1,0:T(8,128)(2,1)S(1)}, bf16[272,1024]{1,0:T(8,128)(2,1)}, u32[]{:S(2)}) copy-start(bf16[272,1024]{1,0:T(8,128)(2,1)} %copy-done.21) | copy-start | bytes 1671172
  101.9 26.0 %collective-permute-start.13 = (bf16[384,512]{1,0:T(8,128)(2,1)}, bf16[384,512]{1,0:T(8,128)(2,1)}, u32[]{:S(2)}, u32[]{:S(2)}) collective-permute-start(bf16[384,512]{1,0:T(8,128)(2,1)} %slice.248), channel_id=1, source_target_pairs={{0,1},{1,0},{2,3},{3,2},{4,5},{5,4},{6,7},{7,6},{8,9},{9,8},{10,11... | collective-permute-start | bytes 1179656 | tf_op jit(solution)/shard_map/ppermute | solution.py:65
  130.2 7.7 %collective-permute-start.16 = (bf16[4,272,1024]{2,1,0:T(8,128)(2,1)S(1)}, bf16[4,272,1024]{2,1,0:T(8,128)(2,1)S(1)}, u32[]{:S(2)}, u32[]{:S(2)}) collective-permute-start(bf16[4,272,1024]{2,1,0:T(8,128)(2,1)S(1)} %pad_maximum_fusion.2.packed_ref.code_ref), channel_id=1, source_target_pairs={{0,4},{4,0},{1,5},{5,1},{2,6},{6,2},{3,7},{7,3},{8,12},{12,8},{9,1... | collective-permute-start | bytes 6684680 | tf_op jit(solution)/shard_map/ppermute | solution.py:47
  131.5 28.7 %copy-start.9 = (bf16[768,512]{1,0:T(8,128)(2,1)S(1)}, bf16[768,512]{1,0:T(8,128)(2,1)}, u32[]{:S(2)}) copy-start(bf16[768,512]{1,0:T(8,128)(2,1)} %get-tuple-element.159.refs_11_) | copy-start | bytes 2359300
  131.5 28.6 %collective-permute-start.19 = (bf16[1152,512]{1,0:T(8,128)(2,1)S(1)}, bf16[1152,512]{1,0:T(8,128)(2,1)S(1)}, u32[]{:S(2)}, u32[]{:S(2)}) collective-permute-start(bf16[1152,512]{1,0:T(8,128)(2,1)S(1)} %get-tuple-element.358), channel_id=1, source_target_pairs={{0,1},{1,0},{2,3},{3,2},{4,5},{5,4},{6,7},{7,6},{8,9},{9,8},{10,11... | collective-permute-start | bytes 3538952 | tf_op jit(solution)/shard_map/ppermute | solution.py:74
  133.0 27.2 %collective-permute-start.20 = (bf16[1152,512]{1,0:T(8,128)(2,1)S(1)}, bf16[1152,512]{1,0:T(8,128)(2,1)S(1)}, u32[]{:S(2)}, u32[]{:S(2)}) collective-permute-start(bf16[1152,512]{1,0:T(8,128)(2,1)S(1)} %get-tuple-element.357), channel_id=1, source_target_pairs={{0,2},{2,0},{1,3},{3,1},{4,6},{6,4},{5,7},{7,5},{8,10},{10,8},{9,1... | collective-permute-start | bytes 3538952 | tf_op jit(solution)/shard_map/ppermute | solution.py:74
  134.0 16.1 %collective-permute-start.14 = (bf16[256,1024]{1,0:T(8,128)(2,1)}, bf16[256,1024]{1,0:T(8,128)(2,1)}, u32[]{:S(2)}, u32[]{:S(2)}) collective-permute-start(bf16[256,1024]{1,0:T(8,128)(2,1)} %get-tuple-element.185.rest_0_.refs_11_), channel_id=1, source_target_pairs={{0,24},{8,0},{16,8},{24,16},{1,25},{9,1},{17,9},{25,17},{2,26},{10... | collective-permute-start | bytes 1572872 | tf_op jit(solution)/shard_map/ppermute | solution.py:51
  137.4 22.7 %collective-permute-start.18 = (bf16[256,1024]{1,0:T(8,128)(2,1)}, bf16[256,1024]{1,0:T(8,128)(2,1)}, u32[]{:S(2)}, u32[]{:S(2)}) collective-permute-start(bf16[256,1024]{1,0:T(8,128)(2,1)} %get-tuple-element.185.rest_0_.refs_11_), channel_id=1, source_target_pairs={{0,8},{8,16},{16,24},{24,0},{1,9},{9,17},{17,25},{25,1},{2,10},{10... | collective-permute-start | bytes 1572872 | tf_op jit(solution)/shard_map/ppermute | solution.py:51
  137.9 24.2 %copy-start.1 = (bf16[4,272,1024]{2,1,0:T(8,128)(2,1)}, bf16[4,272,1024]{2,1,0:T(8,128)(2,1)S(1)}, u32[]{:S(2)}) copy-start(bf16[4,272,1024]{2,1,0:T(8,128)(2,1)S(1)} %collective-permute-done.16.packed_ref.code_ref) | copy-start | bytes 6684676
  137.9 22.3 %collective-permute-start.17 = (bf16[256,1024]{1,0:T(8,128)(2,1)}, bf16[256,1024]{1,0:T(8,128)(2,1)}, u32[]{:S(2)}, u32[]{:S(2)}) collective-permute-start(bf16[256,1024]{1,0:T(8,128)(2,1)} %get-tuple-element.185.rest_0_.refs_11_), channel_id=1, source_target_pairs={{0,4},{4,0},{1,5},{5,1},{2,6},{6,2},{3,7},{7,3},{8,12},{12,8},{9,1... | collective-permute-start | bytes 1572872 | tf_op jit(solution)/shard_map/ppermute | solution.py:47
  162.3 28.4 %collective-permute-start.23 = (bf16[1152,512]{1,0:T(8,128)(2,1)}, bf16[1152,512]{1,0:T(8,128)(2,1)S(1)}, u32[]{:S(2)}, u32[]{:S(2)}) collective-permute-start(bf16[1152,512]{1,0:T(8,128)(2,1)} %get-tuple-element.356), channel_id=1, source_target_pairs={{0,1},{1,0},{2,3},{3,2},{4,5},{5,4},{6,7},{7,6},{8,9},{9,8},{10,11... | collective-permute-start | bytes 3538952 | tf_op jit(solution)/shard_map/ppermute | solution.py:74
  162.9 28.9 %collective-permute-start.24 = (bf16[1152,512]{1,0:T(8,128)(2,1)}, bf16[1152,512]{1,0:T(8,128)(2,1)S(1)}, u32[]{:S(2)}, u32[]{:S(2)}) collective-permute-start(bf16[1152,512]{1,0:T(8,128)(2,1)} %get-tuple-element.355), channel_id=1, source_target_pairs={{0,2},{2,0},{1,3},{3,1},{4,6},{6,4},{5,7},{7,5},{8,10},{10,8},{9,1... | collective-permute-start | bytes 3538952 | tf_op jit(solution)/shard_map/ppermute | solution.py:74
  163.9 2.6 collective-permute-start.21
  163.9 2.9 collective-permute-start.22
  164.4 26.3 %collective-permute-start.15 = (bf16[256,1024]{1,0:T(8,128)(2,1)}, bf16[256,1024]{1,0:T(8,128)(2,1)}, u32[]{:S(2)}, u32[]{:S(2)}) collective-permute-start(bf16[256,1024]{1,0:T(8,128)(2,1)} %get-tuple-element.185.rest_0_.refs_11_), channel_id=1, source_target_pairs={{0,16},{8,24},{16,0},{24,8},{1,17},{9,25},{17,1},{25,9},{2,18},{10... | collective-permute-start | bytes 1572872 | tf_op jit(solution)/shard_map/ppermute | solution.py:51
  190.7 10.1 %collective-permute-start.25 = (bf16[256,1024]{1,0:T(8,128)(2,1)}, bf16[256,1024]{1,0:T(8,128)(2,1)S(1)}, u32[]{:S(2)}, u32[]{:S(2)}) collective-permute-start(bf16[256,1024]{1,0:T(8,128)(2,1)} %collective-permute-done.15.rest_2_), channel_id=1, source_target_pairs={{0,4},{4,0},{1,5},{5,1},{2,6},{6,2},{3,7},{7,3},{8,12},{12,8},{9,1... | collective-permute-start | bytes 1572872 | tf_op jit(solution)/shard_map/ppermute | solution.py:47
  190.8 16.0 %collective-permute-start.26 = (bf16[384,512]{1,0:T(8,128)(2,1)S(1)}, bf16[384,512]{1,0:T(8,128)(2,1)S(1)}, u32[]{:S(2)}, u32[]{:S(2)}) collective-permute-start(bf16[384,512]{1,0:T(8,128)(2,1)S(1)} %slice.298), channel_id=1, source_target_pairs={{0,2},{2,0},{1,3},{3,1},{4,6},{6,4},{5,7},{7,5},{8,10},{10,8},{9,1... | collective-permute-start | bytes 1179656 | tf_op jit(solution)/shard_map/ppermute | solution.py:65
  191.8 15.0 %collective-permute-start.27 = (bf16[384,512]{1,0:T(8,128)(2,1)S(1)}, bf16[384,512]{1,0:T(8,128)(2,1)}, u32[]{:S(2)}, u32[]{:S(2)}) collective-permute-start(bf16[384,512]{1,0:T(8,128)(2,1)S(1)} %slice.299), channel_id=1, source_target_pairs={{0,1},{1,0},{2,3},{3,2},{4,5},{5,4},{6,7},{7,6},{8,9},{9,8},{10,11... | collective-permute-start | bytes 1179656 | tf_op jit(solution)/shard_map/ppermute | solution.py:65
  230.5 26.9 %collective-permute-start.28 = (bf16[1,1,768,512]{3,2,1,0:T(8,128)(2,1)}, bf16[1,1,768,512]{3,2,1,0:T(8,128)(2,1)S(1)}, u32[]{:S(2)}, u32[]{:S(2)}) collective-permute-start(bf16[1,1,768,512]{3,2,1,0:T(8,128)(2,1)} %get-tuple-element.203), channel_id=1, source_target_pairs={{0,1},{1,0},{2,3},{3,2},{4,5},{5,4},{6,7},{7,6},{8,9},{9,8},{10,11... | collective-permute-start | bytes 2359304 | tf_op jit(solution)/shard_map/ppermute | solution.py:74
  231.1 26.3 %collective-permute-start.29 = (bf16[1,1,768,512]{3,2,1,0:T(8,128)(2,1)}, bf16[1,1,768,512]{3,2,1,0:T(8,128)(2,1)S(1)}, u32[]{:S(2)}, u32[]{:S(2)}) collective-permute-start(bf16[1,1,768,512]{3,2,1,0:T(8,128)(2,1)} %get-tuple-element.204), channel_id=1, source_target_pairs={{0,2},{2,0},{1,3},{3,1},{4,6},{6,4},{5,7},{7,5},{8,10},{10,8},{9,1... | collective-permute-start | bytes 2359304 | tf_op jit(solution)/shard_map/ppermute | solution.py:74
  263.0 13.4 %collective-permute-start.30 = (bf16[4,256,1152]{2,1,0:T(8,128)(2,1)}, bf16[4,256,1152]{2,1,0:T(8,128)(2,1)}, u32[]{:S(2)}, u32[]{:S(2)}) collective-permute-start(bf16[4,256,1152]{2,1,0:T(8,128)(2,1)} %combine.4), channel_id=1, source_target_pairs={{0,4},{4,0},{1,5},{5,1},{2,6},{6,2},{3,7},{7,3},{8,12},{12,8},{9,1... | collective-permute-start | bytes 7077896 | tf_op jit(solution)/shard_map/ppermute | solution.py:47
  267.9 14.6 %collective-permute-start.31 = (bf16[4,256,1024]{2,1,0:T(8,128)(2,1)}, bf16[4,256,1024]{2,1,0:T(8,128)(2,1)}, u32[]{:S(2)}, u32[]{:S(2)}) collective-permute-start(bf16[4,256,1024]{2,1,0:T(8,128)(2,1)} %combine.5), channel_id=1, source_target_pairs={{0,4},{4,0},{1,5},{5,1},{2,6},{6,2},{3,7},{7,3},{8,12},{12,8},{9,1... | collective-permute-start | bytes 6291464 | tf_op jit(solution)/shard_map/ppermute | solution.py:47
  273.8 53.4 %collective-permute-start.32 = (bf16[3,1,768,512]{3,2,1,0:T(8,128)(2,1)}, bf16[3,1,768,512]{3,2,1,0:T(8,128)(2,1)S(1)}, u32[]{:S(2)}, u32[]{:S(2)}) collective-permute-start(bf16[3,1,768,512]{3,2,1,0:T(8,128)(2,1)} %get-tuple-element.226), channel_id=1, source_target_pairs={{0,1},{1,0},{2,3},{3,2},{4,5},{5,4},{6,7},{7,6},{8,9},{9,8},{10,11... | collective-permute-start | bytes 7077896 | tf_op jit(solution)/shard_map/ppermute | solution.py:74
  275.3 53.2 %collective-permute-start.33 = (bf16[3,1,768,512]{3,2,1,0:T(8,128)(2,1)}, bf16[3,1,768,512]{3,2,1,0:T(8,128)(2,1)}, u32[]{:S(2)}, u32[]{:S(2)}) collective-permute-start(bf16[3,1,768,512]{3,2,1,0:T(8,128)(2,1)} %get-tuple-element.227), channel_id=1, source_target_pairs={{0,2},{2,0},{1,3},{3,1},{4,6},{6,4},{5,7},{7,5},{8,10},{10,8},{9,1... | collective-permute-start | bytes 7077896 | tf_op jit(solution)/shard_map/ppermute | solution.py:74
  282.5 41.5 %collective-permute-start.34 = (bf16[256,1152]{1,0:T(8,128)(2,1)}, bf16[256,1152]{1,0:T(8,128)(2,1)S(1)}, u32[]{:S(2)}, u32[]{:S(2)}) collective-permute-start(bf16[256,1152]{1,0:T(8,128)(2,1)} %get-tuple-element.228), channel_id=1, source_target_pairs={{0,16},{8,24},{16,0},{24,8},{1,17},{9,25},{17,1},{25,9},{2,18},{10... | collective-permute-start | bytes 1769480 | tf_op jit(solution)/shard_map/ppermute | solution.py:51
  282.5 41.5 %collective-permute-start.35 = (bf16[256,1152]{1,0:T(8,128)(2,1)}, bf16[256,1152]{1,0:T(8,128)(2,1)S(1)}, u32[]{:S(2)}, u32[]{:S(2)}) collective-permute-start(bf16[256,1152]{1,0:T(8,128)(2,1)} %get-tuple-element.229), channel_id=1, source_target_pairs={{0,8},{8,16},{16,24},{24,0},{1,9},{9,17},{17,25},{25,1},{2,10},{10... | collective-permute-start | bytes 1769480 | tf_op jit(solution)/shard_map/ppermute | solution.py:51
  286.0 39.3 %collective-permute-start.36 = (bf16[256,1152]{1,0:T(8,128)(2,1)}, bf16[256,1152]{1,0:T(8,128)(2,1)S(1)}, u32[]{:S(2)}, u32[]{:S(2)}) collective-permute-start(bf16[256,1152]{1,0:T(8,128)(2,1)} %get-tuple-element.230), channel_id=1, source_target_pairs={{0,24},{8,0},{16,8},{24,16},{1,25},{9,1},{17,9},{25,17},{2,26},{10... | collective-permute-start | bytes 1769480 | tf_op jit(solution)/shard_map/ppermute | solution.py:51
  333.3 48.8 %collective-permute-start.37 = (bf16[2,1,768,512]{3,2,1,0:T(8,128)(2,1)}, bf16[2,1,768,512]{3,2,1,0:T(8,128)(2,1)}, u32[]{:S(2)}, u32[]{:S(2)}) collective-permute-start(bf16[2,1,768,512]{3,2,1,0:T(8,128)(2,1)} %get-tuple-element.239), channel_id=1, source_target_pairs={{0,1},{1,0},{2,3},{3,2},{4,5},{5,4},{6,7},{7,6},{8,9},{9,8},{10,11... | collective-permute-start | bytes 4718600 | tf_op jit(solution)/shard_map/ppermute | solution.py:74
  334.8 47.4 %collective-permute-start.38 = (bf16[2,1,768,512]{3,2,1,0:T(8,128)(2,1)}, bf16[2,1,768,512]{3,2,1,0:T(8,128)(2,1)}, u32[]{:S(2)}, u32[]{:S(2)}) collective-permute-start(bf16[2,1,768,512]{3,2,1,0:T(8,128)(2,1)} %get-tuple-element.240), channel_id=1, source_target_pairs={{0,2},{2,0},{1,3},{3,1},{4,6},{6,4},{5,7},{7,5},{8,10},{10,8},{9,1... | collective-permute-start | bytes 4718600 | tf_op jit(solution)/shard_map/ppermute | solution.py:74
  335.8 46.3 %collective-permute-start.39 = (bf16[256,1024]{1,0:T(8,128)(2,1)}, bf16[256,1024]{1,0:T(8,128)(2,1)}, u32[]{:S(2)}, u32[]{:S(2)}) collective-permute-start(bf16[256,1024]{1,0:T(8,128)(2,1)} %get-tuple-element.241), channel_id=1, source_target_pairs={{0,8},{8,16},{16,24},{24,0},{1,9},{9,17},{17,25},{25,1},{2,10},{10... | collective-permute-start | bytes 1572872 | tf_op jit(solution)/shard_map/ppermute | solution.py:51
  344.5 37.6 %collective-permute-start.40 = (bf16[256,1024]{1,0:T(8,128)(2,1)}, bf16[256,1024]{1,0:T(8,128)(2,1)}, u32[]{:S(2)}, u32[]{:S(2)}) collective-permute-start(bf16[256,1024]{1,0:T(8,128)(2,1)} %get-tuple-element.242), channel_id=1, source_target_pairs={{0,24},{8,0},{16,8},{24,16},{1,25},{9,1},{17,9},{25,17},{2,26},{10... | collective-permute-start | bytes 1572872 | tf_op jit(solution)/shard_map/ppermute | solution.py:51
  345.2 40.6 %copy-start.34 = (bf16[1,1,768,512]{3,2,1,0:T(8,128)(2,1)S(1)}, bf16[1,1,768,512]{3,2,1,0:T(8,128)(2,1)}, u32[]{:S(2)}) copy-start(bf16[1,1,768,512]{3,2,1,0:T(8,128)(2,1)} %get-tuple-element.288) | copy-start | bytes 2359300
  382.1 12.4 %collective-permute-start.42 = (bf16[4,128,3200]{2,1,0:T(8,128)(2,1)}, bf16[4,128,3200]{2,1,0:T(8,128)(2,1)}, u32[]{:S(2)}, u32[]{:S(2)}) collective-permute-start(bf16[4,128,3200]{2,1,0:T(8,128)(2,1)} %get-tuple-element.264), channel_id=1, source_target_pairs={{0,4},{4,0},{1,5},{5,1},{2,6},{6,2},{3,7},{7,3},{8,12},{12,8},{9,1... | collective-permute-start | bytes 9830408 | tf_op jit(solution)/shard_map/ppermute | solution.py:47
  383.2 17.3 %collective-permute-start.43 = (bf16[2,128,1024]{2,1,0:T(8,128)(2,1)}, bf16[2,128,1024]{2,1,0:T(8,128)(2,1)}, u32[]{:S(2)}, u32[]{:S(2)}) collective-permute-start(bf16[2,128,1024]{2,1,0:T(8,128)(2,1)} %get-tuple-element.267), channel_id=1, source_target_pairs={{0,1},{1,0},{2,3},{3,2},{4,5},{5,4},{6,7},{7,6},{8,9},{9,8},{10,11... | collective-permute-start | bytes 1572872 | tf_op jit(solution)/shard_map/ppermute | solution.py:91
  384.7 15.8 %collective-permute-start.44 = (bf16[2,128,1024]{2,1,0:T(8,128)(2,1)}, bf16[2,128,1024]{2,1,0:T(8,128)(2,1)}, u32[]{:S(2)}, u32[]{:S(2)}) collective-permute-start(bf16[2,128,1024]{2,1,0:T(8,128)(2,1)} %get-tuple-element.268), channel_id=1, source_target_pairs={{0,2},{2,0},{1,3},{3,1},{4,6},{6,4},{5,7},{7,5},{8,10},{10,8},{9,1... | collective-permute-start | bytes 1572872 | tf_op jit(solution)/shard_map/ppermute | solution.py:91
  388.6 39.5 %collective-permute-start.41 = (bf16[256,1024]{1,0:T(8,128)(2,1)}, bf16[256,1024]{1,0:T(8,128)(2,1)S(1)}, u32[]{:S(2)}, u32[]{:S(2)}) collective-permute-start(bf16[256,1024]{1,0:T(8,128)(2,1)} %get-tuple-element.256), channel_id=1, source_target_pairs={{0,16},{8,24},{16,0},{24,8},{1,17},{9,25},{17,1},{25,9},{2,18},{10... | collective-permute-start | bytes 1572872 | tf_op jit(solution)/shard_map/ppermute | solution.py:51
  400.6 20.0 %collective-permute-start.45 = (bf16[2,64,3200]{2,1,0:T(8,128)(2,1)}, bf16[2,64,3200]{2,1,0:T(8,128)(2,1)S(1)}, u32[]{:S(2)}, u32[]{:S(2)}) collective-permute-start(bf16[2,64,3200]{2,1,0:T(8,128)(2,1)} %get-tuple-element.269), channel_id=1, source_target_pairs={{0,1},{1,0},{2,3},{3,2},{4,5},{5,4},{6,7},{7,6},{8,9},{9,8},{10,11... | collective-permute-start | bytes 2457608 | tf_op jit(solution)/shard_map/ppermute | solution.py:91
  401.2 19.7 %collective-permute-start.46 = (bf16[2,64,3200]{2,1,0:T(8,128)(2,1)}, bf16[2,64,3200]{2,1,0:T(8,128)(2,1)S(1)}, u32[]{:S(2)}, u32[]{:S(2)}) collective-permute-start(bf16[2,64,3200]{2,1,0:T(8,128)(2,1)} %get-tuple-element.270), channel_id=1, source_target_pairs={{0,2},{2,0},{1,3},{3,1},{4,6},{6,4},{5,7},{7,5},{8,10},{10,8},{9,1... | collective-permute-start | bytes 2457608 | tf_op jit(solution)/shard_map/ppermute | solution.py:91
  421.0 12.4 %collective-permute-start.50 = (bf16[64,3200]{1,0:T(8,128)(2,1)S(1)}, bf16[64,3200]{1,0:T(8,128)(2,1)S(1)}, u32[]{:S(2)}, u32[]{:S(2)}) collective-permute-start(bf16[64,3200]{1,0:T(8,128)(2,1)S(1)} %fusion.7), channel_id=1, source_target_pairs={{0,1},{1,0},{2,3},{3,2},{4,5},{5,4},{6,7},{7,6},{8,9},{9,8},{10,11... | collective-permute-start | bytes 1228808 | tf_op jit(solution)/shard_map/ppermute | solution.py:99
  422.6 12.4 %collective-permute-start.49 = (bf16[64,3200]{1,0:T(8,128)(2,1)S(1)}, bf16[64,3200]{1,0:T(8,128)(2,1)S(1)}, u32[]{:S(2)}, u32[]{:S(2)}) collective-permute-start(bf16[64,3200]{1,0:T(8,128)(2,1)S(1)} %fusion.6), channel_id=1, source_target_pairs={{0,2},{2,0},{1,3},{3,1},{4,6},{6,4},{5,7},{7,5},{8,10},{10,8},{9,1... | collective-permute-start | bytes 1228808 | tf_op jit(solution)/shard_map/ppermute | solution.py:98
  424.7 31.9 %collective-permute-start.47 = (bf16[128,1024]{1,0:T(8,128)(2,1)S(1)}, bf16[128,1024]{1,0:T(8,128)(2,1)S(1)}, u32[]{:S(2)}, u32[]{:S(2)}) collective-permute-start(bf16[128,1024]{1,0:T(8,128)(2,1)S(1)} %fusion.11), channel_id=1, source_target_pairs={{0,2},{2,0},{1,3},{3,1},{4,6},{6,4},{5,7},{7,5},{8,10},{10,8},{9,1... | collective-permute-start | bytes 786440 | tf_op jit(solution)/shard_map/ppermute | solution.py:98
  427.5 44.1 %collective-permute-start.48 = (bf16[128,1024]{1,0:T(8,128)(2,1)}, bf16[128,1024]{1,0:T(8,128)(2,1)S(1)}, u32[]{:S(2)}, u32[]{:S(2)}) collective-permute-start(bf16[128,1024]{1,0:T(8,128)(2,1)} %fusion.12), channel_id=1, source_target_pairs={{0,1},{1,0},{2,3},{3,2},{4,5},{5,4},{6,7},{7,6},{8,9},{9,8},{10,11... | collective-permute-start | bytes 786440 | tf_op jit(solution)/shard_map/ppermute | solution.py:99
  435.3 13.3 %collective-permute-start.51 = (bf16[32,3200]{1,0:T(8,128)(2,1)S(1)}, bf16[32,3200]{1,0:T(8,128)(2,1)S(1)}, u32[]{:S(2)}, u32[]{:S(2)}) collective-permute-start(bf16[32,3200]{1,0:T(8,128)(2,1)S(1)} %get-tuple-element.352), channel_id=1, source_target_pairs={{0,16},{8,24},{16,0},{24,8},{1,17},{9,25},{17,1},{25,9},{2,18},{10... | collective-permute-start | bytes 614408 | tf_op jit(solution)/shard_map/ppermute | solution.py:51
  436.6 12.1 %collective-permute-start.52 = (bf16[32,3200]{1,0:T(8,128)(2,1)S(1)}, bf16[32,3200]{1,0:T(8,128)(2,1)S(1)}, u32[]{:S(2)}, u32[]{:S(2)}) collective-permute-start(bf16[32,3200]{1,0:T(8,128)(2,1)S(1)} %get-tuple-element.354), channel_id=1, source_target_pairs={{0,8},{8,16},{16,24},{24,0},{1,9},{9,17},{17,25},{25,1},{2,10},{10... | collective-permute-start | bytes 614408 | tf_op jit(solution)/shard_map/ppermute | solution.py:51
  438.6 10.1 %collective-permute-start.53 = (bf16[32,3200]{1,0:T(8,128)(2,1)S(1)}, bf16[32,3200]{1,0:T(8,128)(2,1)S(1)}, u32[]{:S(2)}, u32[]{:S(2)}) collective-permute-start(bf16[32,3200]{1,0:T(8,128)(2,1)S(1)} %get-tuple-element.353), channel_id=1, source_target_pairs={{0,24},{8,0},{16,8},{24,16},{1,25},{9,1},{17,9},{25,17},{2,26},{10... | collective-permute-start | bytes 614408 | tf_op jit(solution)/shard_map/ppermute | solution.py:51
  448.9 9.9 %collective-permute-start.54 = (bf16[32,3200]{1,0:T(8,128)(2,1)S(1)}, bf16[32,3200]{1,0:T(8,128)(2,1)S(1)}, u32[]{:S(2)}, u32[]{:S(2)}) collective-permute-start(bf16[32,3200]{1,0:T(8,128)(2,1)S(1)} %fusion.10), channel_id=1, source_target_pairs={{0,24},{8,0},{16,8},{24,16},{1,25},{9,1},{17,9},{25,17},{2,26},{10... | collective-permute-start | bytes 614408 | tf_op jit(solution)/shard_map/ppermute | solution.py:51
  453.3 17.2 %collective-permute-start.55 = (bf16[32,3200]{1,0:T(8,128)(2,1)S(1)}, bf16[32,3200]{1,0:T(8,128)(2,1)S(1)}, u32[]{:S(2)}, u32[]{:S(2)}) collective-permute-start(bf16[32,3200]{1,0:T(8,128)(2,1)S(1)} %fusion.10), channel_id=1, source_target_pairs={{0,16},{8,24},{16,0},{24,8},{1,17},{9,25},{17,1},{25,9},{2,18},{10... | collective-permute-start | bytes 614408 | tf_op jit(solution)/shard_map/ppermute | solution.py:51
  454.7 15.9 %collective-permute-start.56 = (bf16[32,3200]{1,0:T(8,128)(2,1)S(1)}, bf16[32,3200]{1,0:T(8,128)(2,1)S(1)}, u32[]{:S(2)}, u32[]{:S(2)}) collective-permute-start(bf16[32,3200]{1,0:T(8,128)(2,1)S(1)} %fusion.10), channel_id=1, source_target_pairs={{0,8},{8,16},{16,24},{24,0},{1,9},{9,17},{17,25},{25,1},{2,10},{10... | collective-permute-start | bytes 614408 | tf_op jit(solution)/shard_map/ppermute | solution.py:51
  471.6 3.1 collective-permute-start.57
  (49 other events, 335.1 us)

commit v10 on v9

--- a/solution.py
+++ b/solution.py
@@ -74,12 +74,12 @@
     return lax.ppermute(to_x, "x", SWAP), lax.ppermute(to_y, "y", SWAP)
 
 
-def far_and_next(near, shard):
-    from_x, from_y = near
-    half = shard.shape[0] // 2
+def far_and_next(nears, shard):
+    rows = shard.shape[0]
+    half = rows // 2
     return cross(
-        jnp.concatenate([from_y[-half:], shard], axis=0),
-        jnp.concatenate([from_x[-2 * half : -half], shard], axis=0),
+        jnp.concatenate([from_y[-half:] for _, from_y in nears] + [shard], axis=0),
+        jnp.concatenate([from_x[-rows:-half] for from_x, _ in nears] + [shard], axis=0),
     )
 
 
@@ -973,8 +973,9 @@
             got.append(cyclic(theirs, z_size, k))
         total = column_sum(lax.dynamic_slice_in_dim(mine, z * rows, rows, 0), got).astype(B16)
         sent = {k: cyclic(total, z_size, -k) for k in steps}
-        quarters = [total] + [sent[k] for k in range(1, z_size)]
+        quarters = [total] + [sent[k] for k in steps]
         places = (jnp.arange(z_size, dtype=jnp.int32) - z) % z_size
+        places = jnp.where((places == 1) | (places == 2), 3 - places, places)
         return jnp.take(jnp.stack(quarters), places, axis=0).reshape(mine.shape)
 
     def dense_sum(grads):
@@ -1059,11 +1060,12 @@
                     for e in range(local)
                 ],
             )
-            tables, code = lax.optimization_barrier((tables, code))
+            code = after(code, *tables[:3])
             grad_pieces = column_pieces(jnp.concatenate([out_grad, code], axis=0), z_size)
             grad_near = grad_pieces[1::2]
+            start_parts, tables = after((start_parts, tables), *grad_near)
             cosine, sine, bias, routed_wide, packs = tables
-            start_parts += gather_far(after(start_parts, tables, *grad_near))
+            start_parts += gather_far(after(start_parts, tables))
             dense_parts = [part[:, 2 * model_width :] for part in start_parts]
             dense_full = dense_assemble(dense_pack, dense_parts, dp_index, core)
         else:
@@ -1078,8 +1080,7 @@
             halves, per = 2, local // 2
             weights = []
             near_0 = gather_near(after(packs[0], *start_parts[2:]))
-            far_0 = gather_far(after(near_0, dense_full))
-            near_1 = gather_near(after(packs[1], *near_0, dense_full))
+            near_1 = gather_near(after(packs[1], dense_full))
         else:
             halves, per = 1, local
             pack = jnp.concatenate([w_gate, w_up, *folds], axis=1)
@@ -1087,7 +1088,6 @@
             weights = [every[j] for j in range(dp_size)]
         chunks = []
         if small_grid:
-            bias = after(bias, *near_0)
             (
                 x_all, normed_all, query_rot, key_rot, value_all, attended, totals, misc, residual,
                 moe_in, gates,
@@ -1100,7 +1100,7 @@
                 sine,
                 routed_wide,
             )
-            moe_in = after(moe_in, *near_1, *far_0, *grad_pieces)
+            moe_in = after(moe_in, *near_0, *near_1, *grad_pieces)
             router_rows = misc[:EXPERTS].astype(B16)
             full_attn_gain = misc[EXPERTS]
             full_moe_gain = misc[EXPERTS + 1]
@@ -1151,12 +1151,14 @@
         stage_1 = stage_2 = last_far = ()
         if small_grid:
             middle = packs[0].shape[0] // 2
-            stage_1 = far_and_next(after(near_1, moe_in), packs[2])
+            stage_1 = far_and_next(after((near_0, near_1), moe_in), packs[2])
         last = z_size // 2
         rows_near = [row_pieces[k] for k in range(z_size) if k != last]
         own_other = swap_core(after(moe_in, grads_other))
         if small_grid:
-            stage_2 = far_and_next(after(stage_1, *rows_near, grads_other, own_other), packs[3])
+            stage_2 = far_and_next(
+                [after(stage_1, *rows_near, grads_other, own_other)], packs[3]
+            )
         rows_near_other = [own_other] + [
             swap_core(piece) for piece in after(rows_near[1:], *stage_1)
         ]
@@ -1170,10 +1172,11 @@
         if small_grid:
             last_far = gather_far([part[middle:] for part in stage_2])
             chunks = [
-                [(part, 0) for part in [packs[0], *near_0, *far_0]],
-                [(part, 0) for part in [packs[1], *near_1, *stage_1[::-1]]],
+                [(part, 0) for part in [packs[0], *near_0, *stage_1[::-1]]],
+                [(part, 0) for part in [packs[1], *near_1]]
+                + [(part, middle) for part in stage_1[::-1]],
                 [(packs[2], 0)]
-                + [(part, middle) for part in stage_1]
+                + [(part, 2 * middle) for part in stage_1]
                 + [(part, 0) for part in stage_2[::-1]],
                 [(packs[3], 0)]
                 + [(part, middle) for part in stage_2]
@@ -1258,6 +1261,7 @@
             dense_first, dense_a, dense_b = core_halves(keep, swap_core(give))
             normed_got = grid_scatter_first(*normed_first)
             dense_got = grid_scatter_first(*after(dense_first, *normed_got))
+            early_got, late_got = after((early_got, late_got), *dense_got)
             dense_low = across_z(
                 jnp.concatenate(grid_scatter_second(dense_got, dense_a, dense_b), axis=0), z
             )

time: 492 us -> 487 us (0.990)
  starting transfers between devices: 71.7 us -> 65.7 us
  other arithmetic: 39.6 us -> 34.6 us
    ppermute x10, waiting for transfers between devices: 3.35 us -> 13.4 us  [cross(): return (lax.ppermute(to_x, 'x', SWAP), lax.ppermute(to_y, 'y', SWAP))]
    ppermute x6, waiting for transfers between devices: 7.38 us -> 0.02 us  [gather_near(): return [lax.ppermute(shard, 'x', SWAP), lax.ppermute(shard, 'y', SWAP)]]
    ppermute x2, waiting for transfers between devices: 5.3 us -> 0.01 us  [grid_scatter_second(): last_b = lax.ppermute(onward_b, 'x', SWAP)]
    ppermute x18, waiting for transfers between devices: 113 us -> 108 us  [cyclic(): lax.ppermute(rows, 'z', [(i, (i + shift) % size) for i in range(size)])]
    unnamed x110 -> x108, local copies, waits for them, and re-layouts: 11.2 us -> 15 us
    ppermute x3 -> x2, waiting for transfers between devices: 14 us -> 14 us  [gather_far(): lax.ppermute(from_x[:half], 'y', SWAP)]
  transfers between devices with their start and end apart: 58 -> 56, of which waited for: 21 -> 23; matrix products, arithmetic and copies ran while one was open for 9% -> 9% of each run, Pallas kernels for 29% -> 30%
where the time goes in v10:
time: 487 us; the launch traced here: 478 us
  Pallas kernels  181 us (37%)
  waiting for transfers between devices  160 us (33%)
  starting transfers between devices  65.7 us (13%)
  other arithmetic  34.6 us (7%)
  local copies, waits for them, and re-layouts  34 us (7%)
    ppermute x18, waiting for transfers between devices, cyclic(): lax.ppermute(rows, 'z', [(i, (i + shift) % size) for i in range(size)])  108 us
    pallas_call x2, Pallas kernels, experts(): pl.pallas_call(kernel, out_shape=out_shape, grid_spec=pltpu.PrefetchScala...  51.2 us
    pallas_call x1, Pallas kernels, attention_backward(): pl.pallas_call(kernel, out_shape=shapes, grid_spec=pltpu.PrefetchScalarGr...  36.6 us
    ppermute x18, starting transfers between devices, cyclic(): lax.ppermute(rows, 'z', [(i, (i + shift) % size) for i in range(size)])  34.5 us
    pallas_call x1, Pallas kernels, attention_forward(): pl.pallas_call(kernel, grid=(GROUPS,), in_specs=[fixed(tok_rows, width),...  25.3 us
    pallas_call x4, Pallas kernels, combine_rows(): pl.pallas_call(kernel, out_shape=out_shape, grid_spec=pltpu.PrefetchScala...  22.2 us
    pallas_call x4, Pallas kernels, dispatch_rows(): pl.pallas_call(kernel, out_shape=out_shape, grid_spec=pltpu.PrefetchScala...  19.3 us
    ppermute x4, waiting for transfers between devices, grid_scatter_first(): return (lax.ppermute(first_a, 'x', SWAP), lax.ppermute(first_b, 'y', SWAP))  16.9 us
  transfers between devices with their start and end apart: 56, of which 23 were waited for; matrix products, arithmetic and copies ran while one was open for 9% of the time, Pallas kernels for 30%

profile of v10, /device:TPU:0, one launch (start us, length us, event | category | flops | bytes accessed | tf_op | source)
XLA Modules:
  0.0 477.8 jit_solution(1121523119138622396)
XLA Ops:
  4.2 2.1 concatenate.57.shard_ref
  8.7 3.0 collective-permute-start
  11.7 1.5 collective-permute-start.1
  13.4 2.6 convert_reduce_fusion
  19.0 3.0 fusion.5
  22.7 3.6 collective-permute-start.2
  27.1 1.3 slice_bitcast_fusion.1
  31.1 8.5 %collective-permute-done.2 = bf16[272,1024]{1,0:T(8,128)(2,1)} collective-permute-done((bf16[272,1024]{1,0:T(8,128)(2,1)}, bf16[272,1024]{1,0:T(8,128)(2,1)}, u32[]{:S(2)}, u32[]{:S(2)}) %collective-permute-start.2) | collective-permute-done | bytes 557088 | tf_op jit(solution)/shard_map/ppermute | solution.py:51
  39.6 11.1 %collective-permute-done.3 = bf16[272,1024]{1,0:T(8,128)(2,1)} collective-permute-done((bf16[272,1024]{1,0:T(8,128)(2,1)}, bf16[272,1024]{1,0:T(8,128)(2,1)}, u32[]{:S(2)}, u32[]{:S(2)}) %collective-permute-start.3) | collective-permute-done | bytes 557088 | tf_op jit(solution)/shard_map/ppermute | solution.py:51
  52.3 14.0 %collective-permute-done.4.da_ref.db_ref = bf16[64,5248]{1,0:T(8,128)(2,1)S(1)} collective-permute-done((bf16[64,5248]{1,0:T(8,128)(2,1)S(1)}, bf16[64,5248]{1,0:T(8,128)(2,1)S(1)}, u32[]{:S(2)}, u32[]{:S(2)}) %collective-permute-start.4) | collective-permute-done | bytes 671776 | tf_op jit(solution)/shard_map/ppermute | solution.py:65
  68.1 1.6 pad_maximum_fusion.1.moved_ref
  71.9 2.9 collective-permute-done.6.other_ref
  74.7 6.8 %assemble.1.tail_ref.wo_ref.wq_ref.wk_ref.wv_ref.refs_8_.refs_9_.refs_18_.refs_19_.refs_20_ = bf16[1024,3200]{1,0:T(8,128)(2,1)} custom-call(s32[7]{0:T(128)} %stack.78.places_ref, bf16[256,3200]{1,0:T(8,128)(2,1)} %copy-done.6, bf16[384,3200]{1,0:T(8,128)(2,1)} %pad_maximum_fusion.1.moved_ref, bf16[384,3200]{1,0:T(8,128)(2,1)} %collective-permute-done.6.other_ref), custom_call_target="tpu_custom_call" | custom-call | tf_op jit(solution)/shard_map/assemble/pallas_call | solution.py:147
  83.6 25.3 %attention.1 = (bf16[1024,1024]{1,0:T(8,128)(2,1)}, bf16[1024,1024]{1,0:T(8,128)(2,1)}, bf16[256,1024]{1,0:T(8,128)(2,1)}, bf16[1024,512]{1,0:T(8,128)(2,1)}, bf...) custom-call(bf16[256,1024]{1,0:T(8,128)(2,1)} %own_ref.1, ...), custom_call_target="tpu_custom_call" | custom-call | tf_op jit(solution)/shard_map/attention/pallas_call | solution.py:594
  111.3 1.8 pad_maximum_fusion.2.packed_ref.code_ref
  113.3 1.6 slice.247
  117.2 1.6 collective-permute-start.17
  119.8 2.3 collective-permute-start.12
  122.5 12.2 %collective-permute-done.12.rest_1_ = bf16[256,1024]{1,0:T(8,128)(2,1)S(1)} collective-permute-done((bf16[256,1024]{1,0:T(8,128)(2,1)}, bf16[256,1024]{1,0:T(8,128)(2,1)S(1)}, u32[]{:S(2)}, u32[]{:S(2)}) %collective-permute-start.12) | collective-permute-done | bytes 524320 | tf_op jit(solution)/shard_map/ppermute | solution.py:51
  134.7 10.4 %collective-permute-done.16.rest_3_ = bf16[256,1024]{1,0:T(8,128)(2,1)} collective-permute-done((bf16[256,1024]{1,0:T(8,128)(2,1)}, bf16[256,1024]{1,0:T(8,128)(2,1)}, u32[]{:S(2)}, u32[]{:S(2)}) %collective-permute-start.16) | collective-permute-done | bytes 524320 | tf_op jit(solution)/shard_map/ppermute | solution.py:51
  145.1 8.3 %collective-permute-done.17.refs_10_.refs_15_.refs_7_ = bf16[1536,512]{1,0:T(8,128)(2,1)S(1)} collective-permute-done((bf16[1536,512]{1,0:T(8,128)(2,1)S(1)}, bf16[1536,512]{1,0:T(8,128)(2,1)S(1)}, u32[]{:S(2)}, u32[]{:S(2)}) %collective-permute-start.17) | collective-permute-done | bytes 1572896 | tf_op jit(solution)/shard_map/ppermute | solution.py:74
  155.9 1.6 pad_maximum_fusion.13
  162.1 4.5 dispatch.4.refs_2_
  166.6 4.5 dispatch.5.refs_3_
  171.1 14.9 %collective-permute-done.13.rest_2_ = bf16[256,1024]{1,0:T(8,128)(2,1)} collective-permute-done((bf16[256,1024]{1,0:T(8,128)(2,1)}, bf16[256,1024]{1,0:T(8,128)(2,1)}, u32[]{:S(2)}, u32[]{:S(2)}) %collective-permute-start.13) | collective-permute-done | bytes 524320 | tf_op jit(solution)/shard_map/ppermute | solution.py:51
  187.1 1.3 collective-permute-start.25
  189.1 1.5 slice.341.rest_4_
  190.7 5.1 %dispatch.6 = (bf16[4,320,1024]{2,1,0:T(8,128)(2,1)}, f32[4,320,128]{2,1,0:T(8,128)}) custom-call(s32[1]{0:T(128)} %bitcast.26.lead_ref, bf16[4,272,1024]{2,1,0:T(8,128)(2,1)} %copy-done, bf16[256,1024]{1,0:T(8,128)(2,1)} %get-tuple-element.191.rest_0_.refs_11_, bf16[256,1024]{1,0:T(8,128)(2,1)} %copy-done.44, ...), custom_call_target="tpu_custom_call" | custom-call | tf_op jit(solution)/shard_map/dispatch/pallas_call | solution.py:240
  196.6 5.1 %dispatch.7 = (bf16[4,320,1024]{2,1,0:T(8,128)(2,1)}, f32[4,320,128]{2,1,0:T(8,128)}) custom-call(s32[1]{0:T(128)} %bitcast.26.lead_ref, bf16[4,272,1024]{2,1,0:T(8,128)(2,1)} %copy-done.1, bf16[256,1024]{1,0:T(8,128)(2,1)} %collective-permute-done.15.rest_0_, bf16[256,1024]{1,0:T(8,128)(2,1)} %copy-done.45, bf16[256,1024]{1,0:T(8,128)(2,1)} %copy-done.46, ...), custom_call_target="tpu_custom_call" | custom-call | tf_op jit(solution)/shard_map/dispatch/pallas_call | solution.py:240
  201.7 25.3 %experts.2 = (bf16[8,160,1024]{2,1,0:T(8,128)(2,1)}, bf16[8,160,1152]{2,1,0:T(8,128)(2,1)}, bf16[1,1,768,512]{3,2,1,0:T(8,128)(2,1)}, bf16[1,1,768,512]{3,2,1,0:...) custom-call(s32[5]{0:T(128)} %pad_add_fusion.order_ref, ...), custom_call_target="tpu_custom_call" | custom-call | tf_op jit(solution)/shard_map/experts/pallas_call | solution.py:470
  228.9 25.9 %experts.3 = (bf16[8,160,1024]{2,1,0:T(8,128)(2,1)}, bf16[8,160,1152]{2,1,0:T(8,128)(2,1)}, bf16[1,1,768,512]{3,2,1,0:T(8,128)(2,1)}, bf16[1,1,768,512]{3,2,1,0:...) custom-call(s32[5]{0:T(128)} %pad_add_fusion.order_ref, ...), custom_call_target="tpu_custom_call" | custom-call | tf_op jit(solution)/shard_map/experts/pallas_call | solution.py:470
  254.8 5.6 %combine.4 = bf16[4,256,1152]{2,1,0:T(8,128)(2,1)} custom-call(s32[1]{0:T(128)} %bitcast.26.lead_ref, bf16[4,272,1024]{2,1,0:T(8,128)(2,1)} %copy-done.1, bf16[8,160,1152]{2,1,0:T(8,128)(2,1)} %get-tuple-element.211.rest_0_, bf16[8,160,1152]{2,1,0:T(8,128)(2,1)} %get-tuple-element.212.rest_1_), custom_call_target="tpu_custom_call" | custom-call | tf_op jit(solution)/shard_map/combine/pallas_call | solution.py:298
  260.5 4.8 %combine.5 = bf16[4,256,1024]{2,1,0:T(8,128)(2,1)} custom-call(s32[1]{0:T(128)} %bitcast.26.lead_ref, bf16[4,272,1024]{2,1,0:T(8,128)(2,1)} %copy-done.1, bf16[8,160,1024]{2,1,0:T(8,128)(2,1)} %get-tuple-element.213.rest_0_, bf16[8,160,1024]{2,1,0:T(8,128)(2,1)} %get-tuple-element.214.rest_1_), custom_call_target="tpu_custom_call" | custom-call | tf_op jit(solution)/shard_map/combine/pallas_call | solution.py:298
  265.8 5.4 %join_parts.2 = (bf16[3,1,768,512]{3,2,1,0:T(8,128)(2,1)}, bf16[3,1,768,512]{3,2,1,0:T(8,128)(2,1)}) custom-call(bf16[1,1,768,512]{3,2,1,0:T(8,128)(2,1)} %get-tuple-element.226.refs_0_, bf16[1,1,768,512]{3,2,1,0:T(8,128)(2,1)} %get-tuple-element.227.refs_1_, bf16[1,1,768,512]{3,2,1,0:T(8,128)(2,1)} %get-tuple-element.228.refs_2_, ...), custom_call_target="tpu_custom_call" | custom-call | tf_op jit(solution)/shard_map/join_parts/pallas_call | solution.py:896
  273.5 6.1 %combine.6 = (bf16[256,1152]{1,0:T(8,128)(2,1)}, bf16[256,1152]{1,0:T(8,128)(2,1)}, bf16[256,1152]{1,0:T(8,128)(2,1)}, bf16[256,1152]{1,0:T(8,128)(2,1)}) custom-call(s32[1]{0:T(128)} %bitcast.26.lead_ref, bf16[4,272,1024]{2,1,0:T(8,128)(2,1)} %copy-done, bf16[8,160,1152]{2,1,0:T(8,128)(2,1)} %get-tuple-element.211.rest_0_, ...), custom_call_target="tpu_custom_call" | custom-call | tf_op jit(solution)/shard_map/combine/pallas_call | solution.py:298
  279.6 2.7 collective-permute-start.33
  283.4 5.7 %combine.7 = (bf16[256,1024]{1,0:T(8,128)(2,1)}, bf16[256,1024]{1,0:T(8,128)(2,1)}, bf16[256,1024]{1,0:T(8,128)(2,1)}, bf16[256,1024]{1,0:T(8,128)(2,1)}) custom-call(s32[1]{0:T(128)} %bitcast.26.lead_ref, bf16[4,272,1024]{2,1,0:T(8,128)(2,1)} %copy-done, bf16[8,160,1024]{2,1,0:T(8,128)(2,1)} %get-tuple-element.213.rest_0_, ...), custom_call_target="tpu_custom_call" | custom-call | tf_op jit(solution)/shard_map/combine/pallas_call | solution.py:298
  289.1 31.1 %collective-permute-done.32.refs_1_ = bf16[256,1152]{1,0:T(8,128)(2,1)S(1)} collective-permute-done((bf16[256,1152]{1,0:T(8,128)(2,1)}, bf16[256,1152]{1,0:T(8,128)(2,1)S(1)}, u32[]{:S(2)}, u32[]{:S(2)}) %collective-permute-start.32) | collective-permute-done | bytes 589856 | tf_op jit(solution)/shard_map/ppermute | solution.py:51
  320.2 1.6 collective-permute-done.34.refs_3_
  321.9 2.8 collective-permute-done.30.refs_5_
  326.1 4.7 join_parts.3
  333.0 8.4 %collective-permute-start.37 = (bf16[256,1024]{1,0:T(8,128)(2,1)}, bf16[256,1024]{1,0:T(8,128)(2,1)}, u32[]{:S(2)}, u32[]{:S(2)}) collective-permute-start(bf16[256,1024]{1,0:T(8,128)(2,1)} %get-tuple-element.247), channel_id=1, source_target_pairs={{0,8},{8,16},{16,24},{24,0},{1,9},{9,17},{17,25},{25,1},{2,10},{10... | collective-permute-start | bytes 1572872 | tf_op jit(solution)/shard_map/ppermute | solution.py:51
  342.0 36.6 %attention_grad.1 = (bf16[4,128,3200]{2,1,0:T(8,128)(2,1)}, bf16[4,128,3200]{2,1,0:T(8,128)(2,1)}, bf16[2,128,1024]{2,1,0:T(8,128)(2,1)}, bf16[2,128,1024]{2,1,0...) custom-call(s32[2]{0:T(128)} %pad_add_fusion.1.here_ref, ...), custom_call_target="tpu_custom_call" | custom-call | tf_op jit(solution)/shard_map/attention_grad/pallas_call | solution.py:801
  382.6 3.8 collective-permute-done.40.got_ref
  386.4 1.7 copy-done.17
  388.2 6.1 %core_halves.1 = (bf16[2,64,3200]{2,1,0:T(8,128)(2,1)}, bf16[2,64,3200]{2,1,0:T(8,128)(2,1)}, bf16[2,64,3200]{2,1,0:T(8,128)(2,1)}, bf16[2,64,3200]{2,1,0:T(8,128)(2,1)}) custom-call(bf16[4,128,3200]{2,1,0:T(8,128)(2,1)} %get-tuple-element.269.keep_ref, bf16[4,128,3200]{2,1,0:T(8,128)(2,1)} %copy-done.17), custom_call_target="tpu_custom_call" | custom-call | tf_op jit(solution)/shard_map/core_halves/pallas_call | solution.py:866
  398.7 2.3 collective-permute-start.39
  401.0 14.8 %collective-permute-done.43 = bf16[2,64,3200]{2,1,0:T(8,128)(2,1)S(1)} collective-permute-done((bf16[2,64,3200]{2,1,0:T(8,128)(2,1)}, bf16[2,64,3200]{2,1,0:T(8,128)(2,1)S(1)}, u32[]{:S(2)}, u32[]{:S(2)}) %collective-permute-start.43) | collective-permute-done | bytes 819232 | tf_op jit(solution)/shard_map/ppermute | solution.py:91
  417.4 1.3 collective-permute-start.48
  422.1 1.8 fusion.12
  424.7 2.1 add_bitcast_fusion.3
  429.0 2.8 fusion.28
  432.3 2.3 collective-permute-start.49
  434.6 3.8 collective-permute-start.51
  438.4 2.4 add_convert_fusion
  440.9 1.5 fusion
  442.4 5.3 %collective-permute-done.49 = bf16[32,3200]{1,0:T(8,128)(2,1)S(1)} collective-permute-done((bf16[32,3200]{1,0:T(8,128)(2,1)S(1)}, bf16[32,3200]{1,0:T(8,128)(2,1)S(1)}, u32[]{:S(2)}, u32[]{:S(2)}) %collective-permute-start.49) | collective-permute-done | bytes 204832 | tf_op jit(solution)/shard_map/ppermute | solution.py:51
  447.8 3.7 collective-permute-start.52
  451.5 2.1 collective-permute-start.53
  454.7 11.3 %collective-permute-done.52 = bf16[32,3200]{1,0:T(8,128)(2,1)S(1)} collective-permute-done((bf16[32,3200]{1,0:T(8,128)(2,1)S(1)}, bf16[32,3200]{1,0:T(8,128)(2,1)S(1)}, u32[]{:S(2)}, u32[]{:S(2)}) %collective-permute-start.52) | collective-permute-done | bytes 204832 | tf_op jit(solution)/shard_map/ppermute | solution.py:51
  467.2 1.5 bitcast_add_fusion.2
  471.3 3.4 dense_outputs.1
  474.6 1.6 copy.46
  476.2 1.3 fusion.31
  (261 shorter events, 67.1 us)
Async XLA Ops:
  8.7 42.0 %collective-permute-start = (bf16[128,5248]{1,0:T(8,128)(2,1)}, bf16[128,5248]{1,0:T(8,128)(2,1)S(1)}, u32[]{:S(2)}, u32[]{:S(2)}) collective-permute-start(bf16[128,5248]{1,0:T(8,128)(2,1)} %pad_maximum_fusion.12), channel_id=1, source_target_pairs={{0,1},{1,0},{2,3},{3,2},{4,5},{5,4},{6,7},{7,6},{8,9},{9,8},{10,11... | collective-permute-start | bytes 4030472 | tf_op jit(solution)/shard_map/ppermute | solution.py:59
  11.7 39.1 %collective-permute-start.1 = (bf16[128,5248]{1,0:T(8,128)(2,1)}, bf16[128,5248]{1,0:T(8,128)(2,1)S(1)}, u32[]{:S(2)}, u32[]{:S(2)}) collective-permute-start(bf16[128,5248]{1,0:T(8,128)(2,1)} %pad_maximum_fusion.12), channel_id=1, source_target_pairs={{0,2},{2,0},{1,3},{3,1},{4,6},{6,4},{5,7},{7,5},{8,10},{10,8},{9,1... | collective-permute-start | bytes 4030472 | tf_op jit(solution)/shard_map/ppermute | solution.py:59
  22.7 16.9 %collective-permute-start.2 = (bf16[272,1024]{1,0:T(8,128)(2,1)}, bf16[272,1024]{1,0:T(8,128)(2,1)}, u32[]{:S(2)}, u32[]{:S(2)}) collective-permute-start(bf16[272,1024]{1,0:T(8,128)(2,1)} %constant_dynamic-update-slice_fusion), channel_id=1, source_target_pairs={{0,24},{8,0},{16,8},{24,16},{1,25},{9,1},{17,9},{25,17},{2,26},{10... | collective-permute-start | bytes 1671176 | tf_op jit(solution)/shard_map/ppermute | solution.py:51
  26.3 24.5 %collective-permute-start.3 = (bf16[272,1024]{1,0:T(8,128)(2,1)}, bf16[272,1024]{1,0:T(8,128)(2,1)}, u32[]{:S(2)}, u32[]{:S(2)}) collective-permute-start(bf16[272,1024]{1,0:T(8,128)(2,1)} %constant_dynamic-update-slice_fusion), channel_id=1, source_target_pairs={{0,8},{8,16},{16,24},{24,0},{1,9},{9,17},{17,25},{25,1},{2,10},{10... | collective-permute-start | bytes 1671176 | tf_op jit(solution)/shard_map/ppermute | solution.py:51
  31.0 85.9 %copy-start.8 = (bf16[768,512]{1,0:T(8,128)(2,1)}, bf16[768,512]{1,0:T(8,128)(2,1)S(1)}, u32[]{:S(2)}) copy-start(bf16[768,512]{1,0:T(8,128)(2,1)S(1)} %get-tuple-element.166.refs_6_) | copy-start | bytes 2359300
  50.8 15.5 %collective-permute-start.4 = (bf16[64,5248]{1,0:T(8,128)(2,1)S(1)}, bf16[64,5248]{1,0:T(8,128)(2,1)S(1)}, u32[]{:S(2)}, u32[]{:S(2)}) collective-permute-start(bf16[64,5248]{1,0:T(8,128)(2,1)S(1)} %slice.241), channel_id=1, source_target_pairs={{0,2},{2,0},{1,3},{3,1},{4,6},{6,4},{5,7},{7,5},{8,10},{10,8},{9,1... | collective-permute-start | bytes 2015240 | tf_op jit(solution)/shard_map/ppermute | solution.py:65
  51.4 15.7 %collective-permute-start.5 = (bf16[64,5248]{1,0:T(8,128)(2,1)S(1)}, bf16[64,5248]{1,0:T(8,128)(2,1)S(1)}, u32[]{:S(2)}, u32[]{:S(2)}) collective-permute-start(bf16[64,5248]{1,0:T(8,128)(2,1)S(1)} %slice.242), channel_id=1, source_target_pairs={{0,1},{1,0},{2,3},{3,2},{4,5},{5,4},{6,7},{7,6},{8,9},{9,8},{10,11... | collective-permute-start | bytes 2015240 | tf_op jit(solution)/shard_map/ppermute | solution.py:65
  69.7 5.0 %collective-permute-start.6 = (bf16[384,3200]{1,0:T(8,128)(2,1)}, bf16[384,3200]{1,0:T(8,128)(2,1)}, u32[]{:S(2)}, u32[]{:S(2)}) collective-permute-start(bf16[384,3200]{1,0:T(8,128)(2,1)} %pad_maximum_fusion.1.moved_ref), channel_id=1, source_target_pairs={{0,4},{4,0},{1,5},{5,1},{2,6},{6,2},{3,7},{7,3},{8,12},{12,8},{9,1... | collective-permute-start | bytes 7372808 | tf_op jit(solution)/shard_map/ppermute | solution.py:47
  70.4 39.8 %collective-permute-start.8 = (bf16[768,512]{1,0:T(8,128)(2,1)S(1)}, bf16[768,512]{1,0:T(8,128)(2,1)S(1)}, u32[]{:S(2)}, u32[]{:S(2)}) collective-permute-start(bf16[768,512]{1,0:T(8,128)(2,1)S(1)} %copy-done.19), channel_id=1, source_target_pairs={{0,1},{1,0},{2,3},{3,2},{4,5},{5,4},{6,7},{7,6},{8,9},{9,8},{10,11... | collective-permute-start | bytes 2359304 | tf_op jit(solution)/shard_map/ppermute | solution.py:59
  70.9 39.3 %collective-permute-start.9 = (bf16[768,512]{1,0:T(8,128)(2,1)S(1)}, bf16[768,512]{1,0:T(8,128)(2,1)}, u32[]{:S(2)}, u32[]{:S(2)}) collective-permute-start(bf16[768,512]{1,0:T(8,128)(2,1)S(1)} %copy-done.19), channel_id=1, source_target_pairs={{0,2},{2,0},{1,3},{3,1},{4,6},{6,4},{5,7},{7,5},{8,10},{10,8},{9,1... | collective-permute-start | bytes 2359304 | tf_op jit(solution)/shard_map/ppermute | solution.py:59
  81.5 28.7 %collective-permute-start.10 = (bf16[768,512]{1,0:T(8,128)(2,1)S(1)}, bf16[768,512]{1,0:T(8,128)(2,1)}, u32[]{:S(2)}, u32[]{:S(2)}) collective-permute-start(bf16[768,512]{1,0:T(8,128)(2,1)S(1)} %copy-done.20), channel_id=1, source_target_pairs={{0,1},{1,0},{2,3},{3,2},{4,5},{5,4},{6,7},{7,6},{8,9},{9,8},{10,11... | collective-permute-start | bytes 2359304 | tf_op jit(solution)/shard_map/ppermute | solution.py:59
  82.0 28.1 %collective-permute-start.11 = (bf16[768,512]{1,0:T(8,128)(2,1)S(1)}, bf16[768,512]{1,0:T(8,128)(2,1)}, u32[]{:S(2)}, u32[]{:S(2)}) collective-permute-start(bf16[768,512]{1,0:T(8,128)(2,1)S(1)} %copy-done.20), channel_id=1, source_target_pairs={{0,2},{2,0},{1,3},{3,1},{4,6},{6,4},{5,7},{7,5},{8,10},{10,8},{9,1... | collective-permute-start | bytes 2359304 | tf_op jit(solution)/shard_map/ppermute | solution.py:59
  83.0 27.2 %collective-permute-start.7 = (bf16[272,1024]{1,0:T(8,128)(2,1)}, bf16[272,1024]{1,0:T(8,128)(2,1)S(1)}, u32[]{:S(2)}, u32[]{:S(2)}) collective-permute-start(bf16[272,1024]{1,0:T(8,128)(2,1)} %constant_dynamic-update-slice_fusion), channel_id=1, source_target_pairs={{0,16},{8,24},{16,0},{24,8},{1,17},{9,25},{17,1},{25,9},{2,18},{10... | collective-permute-start | bytes 1671176 | tf_op jit(solution)/shard_map/ppermute | solution.py:51
  113.2 9.2 %collective-permute-start.14 = (bf16[4,272,1024]{2,1,0:T(8,128)(2,1)S(1)}, bf16[4,272,1024]{2,1,0:T(8,128)(2,1)S(1)}, u32[]{:S(2)}, u32[]{:S(2)}) collective-permute-start(bf16[4,272,1024]{2,1,0:T(8,128)(2,1)S(1)} %pad_maximum_fusion.2.packed_ref.code_ref), channel_id=1, source_target_pairs={{0,4},{4,0},{1,5},{5,1},{2,6},{6,2},{3,7},{7,3},{8,12},{12,8},{9,1... | collective-permute-start | bytes 6684680 | tf_op jit(solution)/shard_map/ppermute | solution.py:47
  117.2 38.7 %copy-start.9 = (bf16[768,512]{1,0:T(8,128)(2,1)S(1)}, bf16[768,512]{1,0:T(8,128)(2,1)}, u32[]{:S(2)}) copy-start(bf16[768,512]{1,0:T(8,128)(2,1)} %get-tuple-element.167.refs_11_) | copy-start | bytes 2359300
  117.2 36.3 %collective-permute-start.17 = (bf16[1536,512]{1,0:T(8,128)(2,1)S(1)}, bf16[1536,512]{1,0:T(8,128)(2,1)S(1)}, u32[]{:S(2)}, u32[]{:S(2)}) collective-permute-start(bf16[1536,512]{1,0:T(8,128)(2,1)S(1)} %get-tuple-element.368), channel_id=1, source_target_pairs={{0,1},{1,0},{2,3},{3,2},{4,5},{5,4},{6,7},{7,6},{8,9},{9,8},{10,11... | collective-permute-start | bytes 4718600 | tf_op jit(solution)/shard_map/ppermute | solution.py:74
  118.8 35.9 %collective-permute-start.18 = (bf16[1536,512]{1,0:T(8,128)(2,1)S(1)}, bf16[1536,512]{1,0:T(8,128)(2,1)S(1)}, u32[]{:S(2)}, u32[]{:S(2)}) collective-permute-start(bf16[1536,512]{1,0:T(8,128)(2,1)S(1)} %get-tuple-element.367), channel_id=1, source_target_pairs={{0,2},{2,0},{1,3},{3,1},{4,6},{6,4},{5,7},{7,5},{8,10},{10,8},{9,1... | collective-permute-start | bytes 4718600 | tf_op jit(solution)/shard_map/ppermute | solution.py:74
  119.8 14.9 %collective-permute-start.12 = (bf16[256,1024]{1,0:T(8,128)(2,1)}, bf16[256,1024]{1,0:T(8,128)(2,1)S(1)}, u32[]{:S(2)}, u32[]{:S(2)}) collective-permute-start(bf16[256,1024]{1,0:T(8,128)(2,1)} %get-tuple-element.191.rest_0_.refs_11_), channel_id=1, source_target_pairs={{0,24},{8,0},{16,8},{24,16},{1,25},{9,1},{17,9},{25,17},{2,26},{10... | collective-permute-start | bytes 1572872 | tf_op jit(solution)/shard_map/ppermute | solution.py:51
  122.1 23.0 %collective-permute-start.16 = (bf16[256,1024]{1,0:T(8,128)(2,1)}, bf16[256,1024]{1,0:T(8,128)(2,1)}, u32[]{:S(2)}, u32[]{:S(2)}) collective-permute-start(bf16[256,1024]{1,0:T(8,128)(2,1)} %get-tuple-element.191.rest_0_.refs_11_), channel_id=1, source_target_pairs={{0,8},{8,16},{16,24},{24,0},{1,9},{9,17},{17,25},{25,1},{2,10},{10... | collective-permute-start | bytes 1572872 | tf_op jit(solution)/shard_map/ppermute | solution.py:51
  122.4 35.1 %copy-start.1 = (bf16[4,272,1024]{2,1,0:T(8,128)(2,1)}, bf16[4,272,1024]{2,1,0:T(8,128)(2,1)S(1)}, u32[]{:S(2)}) copy-start(bf16[4,272,1024]{2,1,0:T(8,128)(2,1)S(1)} %collective-permute-done.14.packed_ref.code_ref) | copy-start | bytes 6684676
  122.4 32.3 %collective-permute-start.15 = (bf16[256,1024]{1,0:T(8,128)(2,1)}, bf16[256,1024]{1,0:T(8,128)(2,1)}, u32[]{:S(2)}, u32[]{:S(2)}) collective-permute-start(bf16[256,1024]{1,0:T(8,128)(2,1)} %get-tuple-element.191.rest_0_.refs_11_), channel_id=1, source_target_pairs={{0,4},{4,0},{1,5},{5,1},{2,6},{6,2},{3,7},{7,3},{8,12},{12,8},{9,1... | collective-permute-start | bytes 1572872 | tf_op jit(solution)/shard_map/ppermute | solution.py:47
  134.7 31.9 %copy-start.44 = (bf16[256,1024]{1,0:T(8,128)(2,1)}, bf16[256,1024]{1,0:T(8,128)(2,1)S(1)}, u32[]{:S(2)}) copy-start(bf16[256,1024]{1,0:T(8,128)(2,1)S(1)} %collective-permute-done.12.rest_1_) | copy-start | bytes 1572868
  157.5 28.6 %collective-permute-start.21 = (bf16[1152,512]{1,0:T(8,128)(2,1)}, bf16[1152,512]{1,0:T(8,128)(2,1)S(1)}, u32[]{:S(2)}, u32[]{:S(2)}) collective-permute-start(bf16[1152,512]{1,0:T(8,128)(2,1)} %get-tuple-element.366), channel_id=1, source_target_pairs={{0,1},{1,0},{2,3},{3,2},{4,5},{5,4},{6,7},{7,6},{8,9},{9,8},{10,11... | collective-permute-start | bytes 3538952 | tf_op jit(solution)/shard_map/ppermute | solution.py:74
  158.2 28.9 %collective-permute-start.22 = (bf16[1152,512]{1,0:T(8,128)(2,1)}, bf16[1152,512]{1,0:T(8,128)(2,1)S(1)}, u32[]{:S(2)}, u32[]{:S(2)}) collective-permute-start(bf16[1152,512]{1,0:T(8,128)(2,1)} %get-tuple-element.365), channel_id=1, source_target_pairs={{0,2},{2,0},{1,3},{3,1},{4,6},{6,4},{5,7},{7,5},{8,10},{10,8},{9,1... | collective-permute-start | bytes 3538952 | tf_op jit(solution)/shard_map/ppermute | solution.py:74
  159.3 1.9 collective-permute-start.19
  159.3 2.8 collective-permute-start.20
  159.8 26.2 %collective-permute-start.13 = (bf16[256,1024]{1,0:T(8,128)(2,1)}, bf16[256,1024]{1,0:T(8,128)(2,1)}, u32[]{:S(2)}, u32[]{:S(2)}) collective-permute-start(bf16[256,1024]{1,0:T(8,128)(2,1)} %get-tuple-element.191.rest_0_.refs_11_), channel_id=1, source_target_pairs={{0,16},{8,24},{16,0},{24,8},{1,17},{9,25},{17,1},{25,9},{2,18},{10... | collective-permute-start | bytes 1572872 | tf_op jit(solution)/shard_map/ppermute | solution.py:51
  186.0 9.8 %collective-permute-start.23 = (bf16[256,1024]{1,0:T(8,128)(2,1)}, bf16[256,1024]{1,0:T(8,128)(2,1)S(1)}, u32[]{:S(2)}, u32[]{:S(2)}) collective-permute-start(bf16[256,1024]{1,0:T(8,128)(2,1)} %collective-permute-done.13.rest_2_), channel_id=1, source_target_pairs={{0,4},{4,0},{1,5},{5,1},{2,6},{6,2},{3,7},{7,3},{8,12},{12,8},{9,1... | collective-permute-start | bytes 1572872 | tf_op jit(solution)/shard_map/ppermute | solution.py:47
  186.1 15.6 %collective-permute-start.24 = (bf16[384,512]{1,0:T(8,128)(2,1)S(1)}, bf16[384,512]{1,0:T(8,128)(2,1)S(1)}, u32[]{:S(2)}, u32[]{:S(2)}) collective-permute-start(bf16[384,512]{1,0:T(8,128)(2,1)S(1)} %slice.296), channel_id=1, source_target_pairs={{0,2},{2,0},{1,3},{3,1},{4,6},{6,4},{5,7},{7,5},{8,10},{10,8},{9,1... | collective-permute-start | bytes 1179656 | tf_op jit(solution)/shard_map/ppermute | solution.py:65
  187.1 14.6 %collective-permute-start.25 = (bf16[384,512]{1,0:T(8,128)(2,1)S(1)}, bf16[384,512]{1,0:T(8,128)(2,1)}, u32[]{:S(2)}, u32[]{:S(2)}) collective-permute-start(bf16[384,512]{1,0:T(8,128)(2,1)S(1)} %slice.297), channel_id=1, source_target_pairs={{0,1},{1,0},{2,3},{3,2},{4,5},{5,4},{6,7},{7,6},{8,9},{9,8},{10,11... | collective-permute-start | bytes 1179656 | tf_op jit(solution)/shard_map/ppermute | solution.py:65
  201.7 25.3 %copy-start.49 = (bf16[384,512]{1,0:T(8,128)(2,1)}, bf16[384,512]{1,0:T(8,128)(2,1)S(1)}, u32[]{:S(2)}) copy-start(bf16[384,512]{1,0:T(8,128)(2,1)S(1)} %collective-permute-done.24.refs_14_) | copy-start | bytes 1179652
  227.0 27.8 %collective-permute-start.26 = (bf16[1,1,768,512]{3,2,1,0:T(8,128)(2,1)}, bf16[1,1,768,512]{3,2,1,0:T(8,128)(2,1)S(1)}, u32[]{:S(2)}, u32[]{:S(2)}) collective-permute-start(bf16[1,1,768,512]{3,2,1,0:T(8,128)(2,1)} %get-tuple-element.209), channel_id=1, source_target_pairs={{0,1},{1,0},{2,3},{3,2},{4,5},{5,4},{6,7},{7,6},{8,9},{9,8},{10,11... | collective-permute-start | bytes 2359304 | tf_op jit(solution)/shard_map/ppermute | solution.py:74
  227.8 27.0 %collective-permute-start.27 = (bf16[1,1,768,512]{3,2,1,0:T(8,128)(2,1)}, bf16[1,1,768,512]{3,2,1,0:T(8,128)(2,1)S(1)}, u32[]{:S(2)}, u32[]{:S(2)}) collective-permute-start(bf16[1,1,768,512]{3,2,1,0:T(8,128)(2,1)} %get-tuple-element.210), channel_id=1, source_target_pairs={{0,2},{2,0},{1,3},{3,1},{4,6},{6,4},{5,7},{7,5},{8,10},{10,8},{9,1... | collective-permute-start | bytes 2359304 | tf_op jit(solution)/shard_map/ppermute | solution.py:74
  260.4 13.0 %collective-permute-start.28 = (bf16[4,256,1152]{2,1,0:T(8,128)(2,1)}, bf16[4,256,1152]{2,1,0:T(8,128)(2,1)}, u32[]{:S(2)}, u32[]{:S(2)}) collective-permute-start(bf16[4,256,1152]{2,1,0:T(8,128)(2,1)} %combine.4), channel_id=1, source_target_pairs={{0,4},{4,0},{1,5},{5,1},{2,6},{6,2},{3,7},{7,3},{8,12},{12,8},{9,1... | collective-permute-start | bytes 7077896 | tf_op jit(solution)/shard_map/ppermute | solution.py:47
  265.3 14.2 %collective-permute-start.29 = (bf16[4,256,1024]{2,1,0:T(8,128)(2,1)}, bf16[4,256,1024]{2,1,0:T(8,128)(2,1)}, u32[]{:S(2)}, u32[]{:S(2)}) collective-permute-start(bf16[4,256,1024]{2,1,0:T(8,128)(2,1)} %combine.5), channel_id=1, source_target_pairs={{0,4},{4,0},{1,5},{5,1},{2,6},{6,2},{3,7},{7,3},{8,12},{12,8},{9,1... | collective-permute-start | bytes 6291464 | tf_op jit(solution)/shard_map/ppermute | solution.py:47
  271.2 53.4 %collective-permute-start.30 = (bf16[3,1,768,512]{3,2,1,0:T(8,128)(2,1)}, bf16[3,1,768,512]{3,2,1,0:T(8,128)(2,1)S(1)}, u32[]{:S(2)}, u32[]{:S(2)}) collective-permute-start(bf16[3,1,768,512]{3,2,1,0:T(8,128)(2,1)} %get-tuple-element.232), channel_id=1, source_target_pairs={{0,1},{1,0},{2,3},{3,2},{4,5},{5,4},{6,7},{7,6},{8,9},{9,8},{10,11... | collective-permute-start | bytes 7077896 | tf_op jit(solution)/shard_map/ppermute | solution.py:74
  272.5 53.2 %collective-permute-start.31 = (bf16[3,1,768,512]{3,2,1,0:T(8,128)(2,1)}, bf16[3,1,768,512]{3,2,1,0:T(8,128)(2,1)}, u32[]{:S(2)}, u32[]{:S(2)}) collective-permute-start(bf16[3,1,768,512]{3,2,1,0:T(8,128)(2,1)} %get-tuple-element.233), channel_id=1, source_target_pairs={{0,2},{2,0},{1,3},{3,1},{4,6},{6,4},{5,7},{7,5},{8,10},{10,8},{9,1... | collective-permute-start | bytes 7077896 | tf_op jit(solution)/shard_map/ppermute | solution.py:74
  279.5 40.7 %collective-permute-start.32 = (bf16[256,1152]{1,0:T(8,128)(2,1)}, bf16[256,1152]{1,0:T(8,128)(2,1)S(1)}, u32[]{:S(2)}, u32[]{:S(2)}) collective-permute-start(bf16[256,1152]{1,0:T(8,128)(2,1)} %get-tuple-element.234), channel_id=1, source_target_pairs={{0,16},{8,24},{16,0},{24,8},{1,17},{9,25},{17,1},{25,9},{2,18},{10... | collective-permute-start | bytes 1769480 | tf_op jit(solution)/shard_map/ppermute | solution.py:51
  279.6 40.7 %collective-permute-start.33 = (bf16[256,1152]{1,0:T(8,128)(2,1)}, bf16[256,1152]{1,0:T(8,128)(2,1)}, u32[]{:S(2)}, u32[]{:S(2)}) collective-permute-start(bf16[256,1152]{1,0:T(8,128)(2,1)} %get-tuple-element.235), channel_id=1, source_target_pairs={{0,8},{8,16},{16,24},{24,0},{1,9},{9,17},{17,25},{25,1},{2,10},{10... | collective-permute-start | bytes 1769480 | tf_op jit(solution)/shard_map/ppermute | solution.py:51
  282.2 39.6 %collective-permute-start.34 = (bf16[256,1152]{1,0:T(8,128)(2,1)}, bf16[256,1152]{1,0:T(8,128)(2,1)}, u32[]{:S(2)}, u32[]{:S(2)}) collective-permute-start(bf16[256,1152]{1,0:T(8,128)(2,1)} %get-tuple-element.236), channel_id=1, source_target_pairs={{0,24},{8,0},{16,8},{24,16},{1,25},{9,1},{17,9},{25,17},{2,26},{10... | collective-permute-start | bytes 1769480 | tf_op jit(solution)/shard_map/ppermute | solution.py:51
  320.2 21.8 %copy-start.39 = (bf16[256,1152]{1,0:T(8,128)(2,1)}, bf16[256,1152]{1,0:T(8,128)(2,1)S(1)}, u32[]{:S(2)}) copy-start(bf16[256,1152]{1,0:T(8,128)(2,1)S(1)} %collective-permute-done.32.refs_1_) | copy-start | bytes 1769476
  330.8 48.0 %collective-permute-start.35 = (bf16[2,1,768,512]{3,2,1,0:T(8,128)(2,1)}, bf16[2,1,768,512]{3,2,1,0:T(8,128)(2,1)S(1)}, u32[]{:S(2)}, u32[]{:S(2)}) collective-permute-start(bf16[2,1,768,512]{3,2,1,0:T(8,128)(2,1)} %get-tuple-element.245), channel_id=1, source_target_pairs={{0,1},{1,0},{2,3},{3,2},{4,5},{5,4},{6,7},{7,6},{8,9},{9,8},{10,11... | collective-permute-start | bytes 4718600 | tf_op jit(solution)/shard_map/ppermute | solution.py:74
  332.0 46.7 %collective-permute-start.36 = (bf16[2,1,768,512]{3,2,1,0:T(8,128)(2,1)}, bf16[2,1,768,512]{3,2,1,0:T(8,128)(2,1)S(1)}, u32[]{:S(2)}, u32[]{:S(2)}) collective-permute-start(bf16[2,1,768,512]{3,2,1,0:T(8,128)(2,1)} %get-tuple-element.246), channel_id=1, source_target_pairs={{0,2},{2,0},{1,3},{3,1},{4,6},{6,4},{5,7},{7,5},{8,10},{10,8},{9,1... | collective-permute-start | bytes 4718600 | tf_op jit(solution)/shard_map/ppermute | solution.py:74
  333.0 45.7 %collective-permute-start.37 = (bf16[256,1024]{1,0:T(8,128)(2,1)}, bf16[256,1024]{1,0:T(8,128)(2,1)}, u32[]{:S(2)}, u32[]{:S(2)}) collective-permute-start(bf16[256,1024]{1,0:T(8,128)(2,1)} %get-tuple-element.247), channel_id=1, source_target_pairs={{0,8},{8,16},{16,24},{24,0},{1,9},{9,17},{17,25},{25,1},{2,10},{10... | collective-permute-start | bytes 1572872 | tf_op jit(solution)/shard_map/ppermute | solution.py:51
  341.4 37.3 %collective-permute-start.38 = (bf16[256,1024]{1,0:T(8,128)(2,1)}, bf16[256,1024]{1,0:T(8,128)(2,1)}, u32[]{:S(2)}, u32[]{:S(2)}) collective-permute-start(bf16[256,1024]{1,0:T(8,128)(2,1)} %get-tuple-element.248), channel_id=1, source_target_pairs={{0,24},{8,0},{16,8},{24,16},{1,25},{9,1},{17,9},{25,17},{2,26},{10... | collective-permute-start | bytes 1572872 | tf_op jit(solution)/shard_map/ppermute | solution.py:51
  380.4 6.1 %collective-permute-start.40 = (bf16[4,128,3200]{2,1,0:T(8,128)(2,1)}, bf16[4,128,3200]{2,1,0:T(8,128)(2,1)S(1)}, u32[]{:S(2)}, u32[]{:S(2)}) collective-permute-start(bf16[4,128,3200]{2,1,0:T(8,128)(2,1)} %get-tuple-element.270), channel_id=1, source_target_pairs={{0,4},{4,0},{1,5},{5,1},{2,6},{6,2},{3,7},{7,3},{8,12},{12,8},{9,1... | collective-permute-start | bytes 9830408 | tf_op jit(solution)/shard_map/ppermute | solution.py:47
  380.4 14.7 %collective-permute-start.41 = (bf16[2,128,1024]{2,1,0:T(8,128)(2,1)}, bf16[2,128,1024]{2,1,0:T(8,128)(2,1)}, u32[]{:S(2)}, u32[]{:S(2)}) collective-permute-start(bf16[2,128,1024]{2,1,0:T(8,128)(2,1)} %get-tuple-element.273), channel_id=1, source_target_pairs={{0,1},{1,0},{2,3},{3,2},{4,5},{5,4},{6,7},{7,6},{8,9},{9,8},{10,11... | collective-permute-start | bytes 1572872 | tf_op jit(solution)/shard_map/ppermute | solution.py:91
  381.7 14.4 %collective-permute-start.42 = (bf16[2,128,1024]{2,1,0:T(8,128)(2,1)}, bf16[2,128,1024]{2,1,0:T(8,128)(2,1)}, u32[]{:S(2)}, u32[]{:S(2)}) collective-permute-start(bf16[2,128,1024]{2,1,0:T(8,128)(2,1)} %get-tuple-element.274), channel_id=1, source_target_pairs={{0,2},{2,0},{1,3},{3,1},{4,6},{6,4},{5,7},{7,5},{8,10},{10,8},{9,1... | collective-permute-start | bytes 1572872 | tf_op jit(solution)/shard_map/ppermute | solution.py:91
  388.2 36.5 %copy-start.36 = (bf16[1,1,768,512]{3,2,1,0:T(8,128)(2,1)S(1)}, bf16[1,1,768,512]{3,2,1,0:T(8,128)(2,1)}, u32[]{:S(2)}) copy-start(bf16[1,1,768,512]{3,2,1,0:T(8,128)(2,1)} %get-tuple-element.297) | copy-start | bytes 2359300
  394.3 24.4 %copy-start.31 = (bf16[2,64,3200]{2,1,0:T(8,128)(2,1)S(1)}, bf16[2,64,3200]{2,1,0:T(8,128)(2,1)}, u32[]{:S(2)}) copy-start(bf16[2,64,3200]{2,1,0:T(8,128)(2,1)} %get-tuple-element.284) | copy-start | bytes 2457604
  396.0 19.7 %collective-permute-start.43 = (bf16[2,64,3200]{2,1,0:T(8,128)(2,1)}, bf16[2,64,3200]{2,1,0:T(8,128)(2,1)S(1)}, u32[]{:S(2)}, u32[]{:S(2)}) collective-permute-start(bf16[2,64,3200]{2,1,0:T(8,128)(2,1)} %get-tuple-element.275), channel_id=1, source_target_pairs={{0,1},{1,0},{2,3},{3,2},{4,5},{5,4},{6,7},{7,6},{8,9},{9,8},{10,11... | collective-permute-start | bytes 2457608 | tf_op jit(solution)/shard_map/ppermute | solution.py:91
  396.8 19.4 %collective-permute-start.44 = (bf16[2,64,3200]{2,1,0:T(8,128)(2,1)}, bf16[2,64,3200]{2,1,0:T(8,128)(2,1)S(1)}, u32[]{:S(2)}, u32[]{:S(2)}) collective-permute-start(bf16[2,64,3200]{2,1,0:T(8,128)(2,1)} %get-tuple-element.276), channel_id=1, source_target_pairs={{0,2},{2,0},{1,3},{3,1},{4,6},{6,4},{5,7},{7,5},{8,10},{10,8},{9,1... | collective-permute-start | bytes 2457608 | tf_op jit(solution)/shard_map/ppermute | solution.py:91
  398.7 30.3 %collective-permute-start.39 = (bf16[256,1024]{1,0:T(8,128)(2,1)}, bf16[256,1024]{1,0:T(8,128)(2,1)S(1)}, u32[]{:S(2)}, u32[]{:S(2)}) collective-permute-start(bf16[256,1024]{1,0:T(8,128)(2,1)} %get-tuple-element.262), channel_id=1, source_target_pairs={{0,16},{8,24},{16,0},{24,8},{1,17},{9,25},{17,1},{25,9},{2,18},{10... | collective-permute-start | bytes 1572872 | tf_op jit(solution)/shard_map/ppermute | solution.py:51
  417.4 14.4 %collective-permute-start.48 = (bf16[64,3200]{1,0:T(8,128)(2,1)S(1)}, bf16[64,3200]{1,0:T(8,128)(2,1)S(1)}, u32[]{:S(2)}, u32[]{:S(2)}) collective-permute-start(bf16[64,3200]{1,0:T(8,128)(2,1)S(1)} %fusion.7), channel_id=1, source_target_pairs={{0,1},{1,0},{2,3},{3,2},{4,5},{5,4},{6,7},{7,6},{8,9},{9,8},{10,11... | collective-permute-start | bytes 1228808 | tf_op jit(solution)/shard_map/ppermute | solution.py:99
  418.9 13.1 %collective-permute-start.47 = (bf16[64,3200]{1,0:T(8,128)(2,1)S(1)}, bf16[64,3200]{1,0:T(8,128)(2,1)S(1)}, u32[]{:S(2)}, u32[]{:S(2)}) collective-permute-start(bf16[64,3200]{1,0:T(8,128)(2,1)S(1)} %fusion.6), channel_id=1, source_target_pairs={{0,2},{2,0},{1,3},{3,1},{4,6},{6,4},{5,7},{7,5},{8,10},{10,8},{9,1... | collective-permute-start | bytes 1228808 | tf_op jit(solution)/shard_map/ppermute | solution.py:98
  421.0 32.7 %collective-permute-start.45 = (bf16[128,1024]{1,0:T(8,128)(2,1)S(1)}, bf16[128,1024]{1,0:T(8,128)(2,1)S(1)}, u32[]{:S(2)}, u32[]{:S(2)}) collective-permute-start(bf16[128,1024]{1,0:T(8,128)(2,1)S(1)} %fusion.11), channel_id=1, source_target_pairs={{0,2},{2,0},{1,3},{3,1},{4,6},{6,4},{5,7},{7,5},{8,10},{10,8},{9,1... | collective-permute-start | bytes 786440 | tf_op jit(solution)/shard_map/ppermute | solution.py:98
  423.9 43.2 %collective-permute-start.46 = (bf16[128,1024]{1,0:T(8,128)(2,1)}, bf16[128,1024]{1,0:T(8,128)(2,1)}, u32[]{:S(2)}, u32[]{:S(2)}) collective-permute-start(bf16[128,1024]{1,0:T(8,128)(2,1)} %fusion.12), channel_id=1, source_target_pairs={{0,1},{1,0},{2,3},{3,2},{4,5},{5,4},{6,7},{7,6},{8,9},{9,8},{10,11... | collective-permute-start | bytes 786440 | tf_op jit(solution)/shard_map/ppermute | solution.py:99
  432.3 15.4 %collective-permute-start.49 = (bf16[32,3200]{1,0:T(8,128)(2,1)S(1)}, bf16[32,3200]{1,0:T(8,128)(2,1)S(1)}, u32[]{:S(2)}, u32[]{:S(2)}) collective-permute-start(bf16[32,3200]{1,0:T(8,128)(2,1)S(1)} %get-tuple-element.362), channel_id=1, source_target_pairs={{0,16},{8,24},{16,0},{24,8},{1,17},{9,25},{17,1},{25,9},{2,18},{10... | collective-permute-start | bytes 614408 | tf_op jit(solution)/shard_map/ppermute | solution.py:51
  434.6 13.0 %collective-permute-start.50 = (bf16[32,3200]{1,0:T(8,128)(2,1)S(1)}, bf16[32,3200]{1,0:T(8,128)(2,1)S(1)}, u32[]{:S(2)}, u32[]{:S(2)}) collective-permute-start(bf16[32,3200]{1,0:T(8,128)(2,1)S(1)} %get-tuple-element.364), channel_id=1, source_target_pairs={{0,8},{8,16},{16,24},{24,0},{1,9},{9,17},{17,25},{25,1},{2,10},{10... | collective-permute-start | bytes 614408 | tf_op jit(solution)/shard_map/ppermute | solution.py:51
  434.6 13.0 %collective-permute-start.51 = (bf16[32,3200]{1,0:T(8,128)(2,1)S(1)}, bf16[32,3200]{1,0:T(8,128)(2,1)S(1)}, u32[]{:S(2)}, u32[]{:S(2)}) collective-permute-start(bf16[32,3200]{1,0:T(8,128)(2,1)S(1)} %get-tuple-element.363), channel_id=1, source_target_pairs={{0,24},{8,0},{16,8},{24,16},{1,25},{9,1},{17,9},{25,17},{2,26},{10... | collective-permute-start | bytes 614408 | tf_op jit(solution)/shard_map/ppermute | solution.py:51
  447.8 18.2 %collective-permute-start.52 = (bf16[32,3200]{1,0:T(8,128)(2,1)S(1)}, bf16[32,3200]{1,0:T(8,128)(2,1)S(1)}, u32[]{:S(2)}, u32[]{:S(2)}) collective-permute-start(bf16[32,3200]{1,0:T(8,128)(2,1)S(1)} %fusion.10), channel_id=1, source_target_pairs={{0,16},{8,24},{16,0},{24,8},{1,17},{9,25},{17,1},{25,9},{2,18},{10... | collective-permute-start | bytes 614408 | tf_op jit(solution)/shard_map/ppermute | solution.py:51
  451.5 14.5 %collective-permute-start.53 = (bf16[32,3200]{1,0:T(8,128)(2,1)S(1)}, bf16[32,3200]{1,0:T(8,128)(2,1)S(1)}, u32[]{:S(2)}, u32[]{:S(2)}) collective-permute-start(bf16[32,3200]{1,0:T(8,128)(2,1)S(1)} %fusion.10), channel_id=1, source_target_pairs={{0,24},{8,0},{16,8},{24,16},{1,25},{9,1},{17,9},{25,17},{2,26},{10... | collective-permute-start | bytes 614408 | tf_op jit(solution)/shard_map/ppermute | solution.py:51
  453.6 12.4 %collective-permute-start.54 = (bf16[32,3200]{1,0:T(8,128)(2,1)S(1)}, bf16[32,3200]{1,0:T(8,128)(2,1)S(1)}, u32[]{:S(2)}, u32[]{:S(2)}) collective-permute-start(bf16[32,3200]{1,0:T(8,128)(2,1)S(1)} %fusion.10), channel_id=1, source_target_pairs={{0,8},{8,16},{16,24},{24,0},{1,9},{9,17},{17,25},{25,1},{2,10},{10... | collective-permute-start | bytes 614408 | tf_op jit(solution)/shard_map/ppermute | solution.py:51
  467.1 3.3 collective-permute-start.55
  (47 other events, 200.9 us)

commit v11 on v10

--- a/solution.py
+++ b/solution.py
@@ -1063,11 +1063,11 @@
             code = after(code, *tables[:3])
             grad_pieces = column_pieces(jnp.concatenate([out_grad, code], axis=0), z_size)
             grad_near = grad_pieces[1::2]
-            start_parts, tables = after((start_parts, tables), *grad_near)
+            start_parts, tables = after((start_parts, tables), grad_near[0])
             cosine, sine, bias, routed_wide, packs = tables
             start_parts += gather_far(after(start_parts, tables))
             dense_parts = [part[:, 2 * model_width :] for part in start_parts]
-            dense_full = dense_assemble(dense_pack, dense_parts, dp_index, core)
+            dense_full = dense_assemble(dense_pack, dense_parts, dp_index, core, *grad_near[1:])
         else:
             dense_full = lax.all_gather(dense_pack, ("y", "x"), axis=0, tiled=True)
             full_output = dense_full[:, :model_width]

time: 487 us -> 481 us (0.988)
  the two profiles are of different devices: /device:TPU:0 before, /device:TPU:9 now
where the time goes in v11:
time: 481 us; the launch traced here: 472 us
  Pallas kernels  181 us (38%)
  waiting for transfers between devices  167 us (35%)
  starting transfers between devices  52.8 us (11%)
  local copies, waits for them, and re-layouts  34.2 us (7%)
  other arithmetic  34.2 us (7%)
    ppermute x18, waiting for transfers between devices, cyclic(): lax.ppermute(rows, 'z', [(i, (i + shift) % size) for i in range(size)])  114 us
    pallas_call x2, Pallas kernels, experts(): pl.pallas_call(kernel, out_shape=out_shape, grid_spec=pltpu.PrefetchScala...  51.2 us
    pallas_call x1, Pallas kernels, attention_backward(): pl.pallas_call(kernel, out_shape=shapes, grid_spec=pltpu.PrefetchScalarGr...  36.7 us
    pallas_call x1, Pallas kernels, attention_forward(): pl.pallas_call(kernel, grid=(GROUPS,), in_specs=[fixed(tok_rows, width),...  25.3 us
    pallas_call x4, Pallas kernels, combine_rows(): pl.pallas_call(kernel, out_shape=out_shape, grid_spec=pltpu.PrefetchScala...  22.1 us
    pallas_call x4, Pallas kernels, dispatch_rows(): pl.pallas_call(kernel, out_shape=out_shape, grid_spec=pltpu.PrefetchScala...  19.3 us
    ppermute x4, waiting for transfers between devices, grid_scatter_first(): return (lax.ppermute(first_a, 'x', SWAP), lax.ppermute(first_b, 'y', SWAP))  17.4 us
    ppermute x18, starting transfers between devices, cyclic(): lax.ppermute(rows, 'z', [(i, (i + shift) % size) for i in range(size)])  16.1 us
  transfers between devices with their start and end apart: 56, of which 24 were waited for; matrix products, arithmetic and copies ran while one was open for 9% of the time, Pallas kernels for 30%

profile of v11, /device:TPU:9, one launch (start us, length us, event | category | flops | bytes accessed | tf_op | source)
XLA Modules:
  0.0 471.5 jit_solution(17049964566926052178)
XLA Ops:
  4.2 2.1 concatenate.57.shard_ref
  11.4 2.6 convert_reduce_fusion
  15.7 1.3 or_select_fusion.bias_ref.refs_21_
  17.0 3.0 fusion.5
  21.6 1.3 slice_bitcast_fusion.1
  25.6 8.3 %collective-permute-done.2 = bf16[272,1024]{1,0:T(8,128)(2,1)} collective-permute-done((bf16[272,1024]{1,0:T(8,128)(2,1)}, bf16[272,1024]{1,0:T(8,128)(2,1)}, u32[]{:S(2)}, u32[]{:S(2)}) %collective-permute-start.2) | collective-permute-done | bytes 557088 | tf_op jit(solution)/shard_map/ppermute | solution.py:51
  33.9 5.4 %collective-permute-done.xa_ref.xb_ref = bf16[128,5248]{1,0:T(8,128)(2,1)S(1)} collective-permute-done((bf16[128,5248]{1,0:T(8,128)(2,1)}, bf16[128,5248]{1,0:T(8,128)(2,1)S(1)}, u32[]{:S(2)}, u32[]{:S(2)}) %collective-permute-start) | collective-permute-done | bytes 1343520 | tf_op jit(solution)/shard_map/ppermute | solution.py:59
  40.3 1.3 collective-permute-start.3
  43.3 12.0 %collective-permute-done.3.da_ref.db_ref = bf16[64,5248]{1,0:T(8,128)(2,1)S(1)} collective-permute-done((bf16[64,5248]{1,0:T(8,128)(2,1)S(1)}, bf16[64,5248]{1,0:T(8,128)(2,1)S(1)}, u32[]{:S(2)}, u32[]{:S(2)}) %collective-permute-start.3) | collective-permute-done | bytes 671776 | tf_op jit(solution)/shard_map/ppermute | solution.py:65
  57.2 1.6 pad_maximum_fusion.1.moved_ref
  58.9 2.8 collective-permute-start.6
  63.4 2.9 collective-permute-done.6.other_ref
  66.4 6.8 %assemble.1.tail_ref.wo_ref.wq_ref.wk_ref.wv_ref.refs_8_.refs_9_.refs_18_.refs_19_.refs_20_ = bf16[1024,3200]{1,0:T(8,128)(2,1)} custom-call(s32[7]{0:T(128)} %stack.78.places_ref, bf16[256,3200]{1,0:T(8,128)(2,1)} %copy-done.6, bf16[384,3200]{1,0:T(8,128)(2,1)} %pad_maximum_fusion.1.moved_ref, bf16[384,3200]{1,0:T(8,128)(2,1)} %collective-permute-done.6.other_ref), custom_call_target="tpu_custom_call" | custom-call | tf_op jit(solution)/shard_map/assemble/pallas_call | solution.py:147
  74.2 2.3 collective-permute-start.7
  76.5 25.3 %attention.1 = (bf16[1024,1024]{1,0:T(8,128)(2,1)}, bf16[1024,1024]{1,0:T(8,128)(2,1)}, bf16[256,1024]{1,0:T(8,128)(2,1)}, bf16[1024,512]{1,0:T(8,128)(2,1)}, bf...) custom-call(bf16[256,1024]{1,0:T(8,128)(2,1)} %own_ref.1, ...), custom_call_target="tpu_custom_call" | custom-call | tf_op jit(solution)/shard_map/attention/pallas_call | solution.py:594
  103.0 1.8 pad_maximum_fusion.2.packed_ref.code_ref
  111.6 1.6 collective-permute-start.16
  113.2 1.7 collective-permute-start.15
  114.9 9.0 %collective-permute-done.12.rest_1_ = bf16[256,1024]{1,0:T(8,128)(2,1)S(1)} collective-permute-done((bf16[256,1024]{1,0:T(8,128)(2,1)}, bf16[256,1024]{1,0:T(8,128)(2,1)S(1)}, u32[]{:S(2)}, u32[]{:S(2)}) %collective-permute-start.12) | collective-permute-done | bytes 524320 | tf_op jit(solution)/shard_map/ppermute | solution.py:51
  124.0 13.1 %collective-permute-done.16.rest_3_ = bf16[256,1024]{1,0:T(8,128)(2,1)} collective-permute-done((bf16[256,1024]{1,0:T(8,128)(2,1)}, bf16[256,1024]{1,0:T(8,128)(2,1)}, u32[]{:S(2)}, u32[]{:S(2)}) %collective-permute-start.16) | collective-permute-done | bytes 524320 | tf_op jit(solution)/shard_map/ppermute | solution.py:51
  137.1 7.8 %collective-permute-done.17.refs_10_.refs_15_.refs_7_ = bf16[1536,512]{1,0:T(8,128)(2,1)S(1)} collective-permute-done((bf16[1536,512]{1,0:T(8,128)(2,1)S(1)}, bf16[1536,512]{1,0:T(8,128)(2,1)S(1)}, u32[]{:S(2)}, u32[]{:S(2)}) %collective-permute-start.17) | collective-permute-done | bytes 1572896 | tf_op jit(solution)/shard_map/ppermute | solution.py:74
  147.1 1.6 pad_maximum_fusion.13
  150.1 2.0 collective-permute-start.19
  152.1 1.7 collective-permute-start.13
  154.5 4.5 dispatch.4.refs_2_
  159.1 4.5 dispatch.5.refs_3_
  163.6 11.7 %collective-permute-done.13.rest_2_ = bf16[256,1024]{1,0:T(8,128)(2,1)} collective-permute-done((bf16[256,1024]{1,0:T(8,128)(2,1)}, bf16[256,1024]{1,0:T(8,128)(2,1)}, u32[]{:S(2)}, u32[]{:S(2)}) %collective-permute-start.13) | collective-permute-done | bytes 524320 | tf_op jit(solution)/shard_map/ppermute | solution.py:51
  178.4 1.5 slice.341.rest_4_
  179.9 5.1 %dispatch.6 = (bf16[4,320,1024]{2,1,0:T(8,128)(2,1)}, f32[4,320,128]{2,1,0:T(8,128)}) custom-call(s32[1]{0:T(128)} %bitcast.26.lead_ref, bf16[4,272,1024]{2,1,0:T(8,128)(2,1)} %copy-done, bf16[256,1024]{1,0:T(8,128)(2,1)} %get-tuple-element.193.rest_0_.refs_11_, bf16[256,1024]{1,0:T(8,128)(2,1)} %copy-done.44, ...), custom_call_target="tpu_custom_call" | custom-call | tf_op jit(solution)/shard_map/dispatch/pallas_call | solution.py:240
  185.8 5.1 %dispatch.7 = (bf16[4,320,1024]{2,1,0:T(8,128)(2,1)}, f32[4,320,128]{2,1,0:T(8,128)}) custom-call(s32[1]{0:T(128)} %bitcast.26.lead_ref, bf16[4,272,1024]{2,1,0:T(8,128)(2,1)} %copy-done.1, bf16[256,1024]{1,0:T(8,128)(2,1)} %collective-permute-done.15.rest_0_, bf16[256,1024]{1,0:T(8,128)(2,1)} %copy-done.45, bf16[256,1024]{1,0:T(8,128)(2,1)} %copy-done.46, ...), custom_call_target="tpu_custom_call" | custom-call | tf_op jit(solution)/shard_map/dispatch/pallas_call | solution.py:240
  191.0 25.3 %experts.2 = (bf16[8,160,1024]{2,1,0:T(8,128)(2,1)}, bf16[8,160,1152]{2,1,0:T(8,128)(2,1)}, bf16[1,1,768,512]{3,2,1,0:T(8,128)(2,1)}, bf16[1,1,768,512]{3,2,1,0:...) custom-call(s32[5]{0:T(128)} %pad_add_fusion.order_ref, ...), custom_call_target="tpu_custom_call" | custom-call | tf_op jit(solution)/shard_map/experts/pallas_call | solution.py:470
  217.5 25.9 %experts.3 = (bf16[8,160,1024]{2,1,0:T(8,128)(2,1)}, bf16[8,160,1152]{2,1,0:T(8,128)(2,1)}, bf16[1,1,768,512]{3,2,1,0:T(8,128)(2,1)}, bf16[1,1,768,512]{3,2,1,0:...) custom-call(s32[5]{0:T(128)} %pad_add_fusion.order_ref, ...), custom_call_target="tpu_custom_call" | custom-call | tf_op jit(solution)/shard_map/experts/pallas_call | solution.py:470
  243.4 5.6 %combine.4 = bf16[4,256,1152]{2,1,0:T(8,128)(2,1)} custom-call(s32[1]{0:T(128)} %bitcast.26.lead_ref, bf16[4,272,1024]{2,1,0:T(8,128)(2,1)} %copy-done.1, bf16[8,160,1152]{2,1,0:T(8,128)(2,1)} %get-tuple-element.213.rest_0_, bf16[8,160,1152]{2,1,0:T(8,128)(2,1)} %get-tuple-element.214.rest_1_), custom_call_target="tpu_custom_call" | custom-call | tf_op jit(solution)/shard_map/combine/pallas_call | solution.py:298
  249.0 2.7 collective-permute-start.28
  251.7 4.8 %combine.5 = bf16[4,256,1024]{2,1,0:T(8,128)(2,1)} custom-call(s32[1]{0:T(128)} %bitcast.26.lead_ref, bf16[4,272,1024]{2,1,0:T(8,128)(2,1)} %copy-done.1, bf16[8,160,1024]{2,1,0:T(8,128)(2,1)} %get-tuple-element.215.rest_0_, bf16[8,160,1024]{2,1,0:T(8,128)(2,1)} %get-tuple-element.216.rest_1_), custom_call_target="tpu_custom_call" | custom-call | tf_op jit(solution)/shard_map/combine/pallas_call | solution.py:298
  256.5 5.4 %join_parts.2 = (bf16[3,1,768,512]{3,2,1,0:T(8,128)(2,1)}, bf16[3,1,768,512]{3,2,1,0:T(8,128)(2,1)}) custom-call(bf16[1,1,768,512]{3,2,1,0:T(8,128)(2,1)} %get-tuple-element.228.refs_0_, bf16[1,1,768,512]{3,2,1,0:T(8,128)(2,1)} %get-tuple-element.229.refs_1_, bf16[1,1,768,512]{3,2,1,0:T(8,128)(2,1)} %get-tuple-element.230.refs_2_, ...), custom_call_target="tpu_custom_call" | custom-call | tf_op jit(solution)/shard_map/join_parts/pallas_call | solution.py:896
  263.4 6.1 %combine.6 = (bf16[256,1152]{1,0:T(8,128)(2,1)}, bf16[256,1152]{1,0:T(8,128)(2,1)}, bf16[256,1152]{1,0:T(8,128)(2,1)}, bf16[256,1152]{1,0:T(8,128)(2,1)}) custom-call(s32[1]{0:T(128)} %bitcast.26.lead_ref, bf16[4,272,1024]{2,1,0:T(8,128)(2,1)} %copy-done, bf16[8,160,1152]{2,1,0:T(8,128)(2,1)} %get-tuple-element.213.rest_0_, ...), custom_call_target="tpu_custom_call" | custom-call | tf_op jit(solution)/shard_map/combine/pallas_call | solution.py:298
  269.5 2.0 collective-permute-start.32
  271.4 1.4 collective-permute-start.33
  272.9 5.7 %combine.7 = (bf16[256,1024]{1,0:T(8,128)(2,1)}, bf16[256,1024]{1,0:T(8,128)(2,1)}, bf16[256,1024]{1,0:T(8,128)(2,1)}, bf16[256,1024]{1,0:T(8,128)(2,1)}) custom-call(s32[1]{0:T(128)} %bitcast.26.lead_ref, bf16[4,272,1024]{2,1,0:T(8,128)(2,1)} %copy-done, bf16[8,160,1024]{2,1,0:T(8,128)(2,1)} %get-tuple-element.215.rest_0_, ...), custom_call_target="tpu_custom_call" | custom-call | tf_op jit(solution)/shard_map/combine/pallas_call | solution.py:298
  278.6 19.4 %collective-permute-done.32.refs_1_ = bf16[256,1152]{1,0:T(8,128)(2,1)S(1)} collective-permute-done((bf16[256,1152]{1,0:T(8,128)(2,1)}, bf16[256,1152]{1,0:T(8,128)(2,1)S(1)}, u32[]{:S(2)}, u32[]{:S(2)}) %collective-permute-start.32) | collective-permute-done | bytes 589856 | tf_op jit(solution)/shard_map/ppermute | solution.py:51
  298.0 24.7 %collective-permute-done.33.refs_2_ = bf16[256,1152]{1,0:T(8,128)(2,1)} collective-permute-done((bf16[256,1152]{1,0:T(8,128)(2,1)}, bf16[256,1152]{1,0:T(8,128)(2,1)}, u32[]{:S(2)}, u32[]{:S(2)}) %collective-permute-start.33) | collective-permute-done | bytes 589856 | tf_op jit(solution)/shard_map/ppermute | solution.py:51
  323.9 1.5 copy-done.10
  325.4 4.7 join_parts.3
  333.6 36.7 %attention_grad.1 = (bf16[4,128,3200]{2,1,0:T(8,128)(2,1)}, bf16[4,128,3200]{2,1,0:T(8,128)(2,1)}, bf16[2,128,1024]{2,1,0:T(8,128)(2,1)}, bf16[2,128,1024]{2,1,0...) custom-call(s32[2]{0:T(128)} %pad_add_fusion.1.here_ref, ...), custom_call_target="tpu_custom_call" | custom-call | tf_op jit(solution)/shard_map/attention_grad/pallas_call | solution.py:801
  371.9 1.6 collective-permute-start.40
  375.0 4.2 collective-permute-done.40.got_ref
  379.2 1.7 copy-done.17
  381.0 6.1 %core_halves.1 = (bf16[2,64,3200]{2,1,0:T(8,128)(2,1)}, bf16[2,64,3200]{2,1,0:T(8,128)(2,1)}, bf16[2,64,3200]{2,1,0:T(8,128)(2,1)}, bf16[2,64,3200]{2,1,0:T(8,128)(2,1)}) custom-call(bf16[4,128,3200]{2,1,0:T(8,128)(2,1)} %get-tuple-element.271.keep_ref, bf16[4,128,3200]{2,1,0:T(8,128)(2,1)} %copy-done.17), custom_call_target="tpu_custom_call" | custom-call | tf_op jit(solution)/shard_map/core_halves/pallas_call | solution.py:866
  390.5 16.3 %collective-permute-done.43 = bf16[2,64,3200]{2,1,0:T(8,128)(2,1)S(1)} collective-permute-done((bf16[2,64,3200]{2,1,0:T(8,128)(2,1)}, bf16[2,64,3200]{2,1,0:T(8,128)(2,1)S(1)}, u32[]{:S(2)}, u32[]{:S(2)}) %collective-permute-start.43) | collective-permute-done | bytes 819232 | tf_op jit(solution)/shard_map/ppermute | solution.py:91
  411.9 1.8 fusion.12
  414.5 2.1 add_bitcast_fusion.3
  418.8 2.8 fusion.28
  424.0 2.4 add_convert_fusion
  426.4 1.5 fusion
  427.9 10.7 %collective-permute-done.50 = bf16[32,3200]{1,0:T(8,128)(2,1)S(1)} collective-permute-done((bf16[32,3200]{1,0:T(8,128)(2,1)S(1)}, bf16[32,3200]{1,0:T(8,128)(2,1)S(1)}, u32[]{:S(2)}, u32[]{:S(2)}) %collective-permute-start.50) | collective-permute-done | bytes 204832 | tf_op jit(solution)/shard_map/ppermute | solution.py:51
  438.6 1.6 collective-permute-done.51
  440.5 1.7 collective-permute-start.53
  443.3 7.6 %collective-permute-done.52 = bf16[32,3200]{1,0:T(8,128)(2,1)S(1)} collective-permute-done((bf16[32,3200]{1,0:T(8,128)(2,1)S(1)}, bf16[32,3200]{1,0:T(8,128)(2,1)S(1)}, u32[]{:S(2)}, u32[]{:S(2)}) %collective-permute-start.52) | collective-permute-done | bytes 204832 | tf_op jit(solution)/shard_map/ppermute | solution.py:51
  450.9 7.0 %collective-permute-done.53 = bf16[32,3200]{1,0:T(8,128)(2,1)S(1)} collective-permute-done((bf16[32,3200]{1,0:T(8,128)(2,1)S(1)}, bf16[32,3200]{1,0:T(8,128)(2,1)S(1)}, u32[]{:S(2)}, u32[]{:S(2)}) %collective-permute-start.53) | collective-permute-done | bytes 204832 | tf_op jit(solution)/shard_map/ppermute | solution.py:51
  459.0 2.3 collective-permute-start.55
  465.0 3.4 dense_outputs.1
  468.4 1.6 copy.46
  470.0 1.3 fusion.31
  (261 shorter events, 67.4 us)
Async XLA Ops:
  8.7 30.6 %collective-permute-start = (bf16[128,5248]{1,0:T(8,128)(2,1)}, bf16[128,5248]{1,0:T(8,128)(2,1)S(1)}, u32[]{:S(2)}, u32[]{:S(2)}) collective-permute-start(bf16[128,5248]{1,0:T(8,128)(2,1)} %pad_maximum_fusion.12), channel_id=1, source_target_pairs={{0,1},{1,0},{2,3},{3,2},{4,5},{5,4},{6,7},{7,6},{8,9},{9,8},{10,11... | collective-permute-start | bytes 4030472 | tf_op jit(solution)/shard_map/ppermute | solution.py:59
  9.9 30.3 %collective-permute-start.1 = (bf16[128,5248]{1,0:T(8,128)(2,1)}, bf16[128,5248]{1,0:T(8,128)(2,1)S(1)}, u32[]{:S(2)}, u32[]{:S(2)}) collective-permute-start(bf16[128,5248]{1,0:T(8,128)(2,1)} %pad_maximum_fusion.12), channel_id=1, source_target_pairs={{0,2},{2,0},{1,3},{3,1},{4,6},{6,4},{5,7},{7,5},{8,10},{10,8},{9,1... | collective-permute-start | bytes 4030472 | tf_op jit(solution)/shard_map/ppermute | solution.py:59
  20.6 13.3 %collective-permute-start.2 = (bf16[272,1024]{1,0:T(8,128)(2,1)}, bf16[272,1024]{1,0:T(8,128)(2,1)}, u32[]{:S(2)}, u32[]{:S(2)}) collective-permute-start(bf16[272,1024]{1,0:T(8,128)(2,1)} %constant_dynamic-update-slice_fusion), channel_id=1, source_target_pairs={{0,24},{8,0},{16,8},{24,16},{1,25},{9,1},{17,9},{25,17},{2,26},{10... | collective-permute-start | bytes 1671176 | tf_op jit(solution)/shard_map/ppermute | solution.py:51
  25.6 83.7 %copy-start.8 = (bf16[768,512]{1,0:T(8,128)(2,1)}, bf16[768,512]{1,0:T(8,128)(2,1)S(1)}, u32[]{:S(2)}) copy-start(bf16[768,512]{1,0:T(8,128)(2,1)S(1)} %get-tuple-element.167.refs_6_) | copy-start | bytes 2359300
  40.3 15.0 %collective-permute-start.3 = (bf16[64,5248]{1,0:T(8,128)(2,1)S(1)}, bf16[64,5248]{1,0:T(8,128)(2,1)S(1)}, u32[]{:S(2)}, u32[]{:S(2)}) collective-permute-start(bf16[64,5248]{1,0:T(8,128)(2,1)S(1)} %slice.241), channel_id=1, source_target_pairs={{0,2},{2,0},{1,3},{3,1},{4,6},{6,4},{5,7},{7,5},{8,10},{10,8},{9,1... | collective-permute-start | bytes 2015240 | tf_op jit(solution)/shard_map/ppermute | solution.py:65
  41.6 14.7 %collective-permute-start.4 = (bf16[64,5248]{1,0:T(8,128)(2,1)S(1)}, bf16[64,5248]{1,0:T(8,128)(2,1)S(1)}, u32[]{:S(2)}, u32[]{:S(2)}) collective-permute-start(bf16[64,5248]{1,0:T(8,128)(2,1)S(1)} %slice.242), channel_id=1, source_target_pairs={{0,1},{1,0},{2,3},{3,2},{4,5},{5,4},{6,7},{7,6},{8,9},{9,8},{10,11... | collective-permute-start | bytes 2015240 | tf_op jit(solution)/shard_map/ppermute | solution.py:65
  42.0 16.9 %collective-permute-start.5 = (bf16[272,1024]{1,0:T(8,128)(2,1)}, bf16[272,1024]{1,0:T(8,128)(2,1)}, u32[]{:S(2)}, u32[]{:S(2)}) collective-permute-start(bf16[272,1024]{1,0:T(8,128)(2,1)} %constant_dynamic-update-slice_fusion), channel_id=1, source_target_pairs={{0,8},{8,16},{16,24},{24,0},{1,9},{9,17},{17,25},{25,1},{2,10},{10... | collective-permute-start | bytes 1671176 | tf_op jit(solution)/shard_map/ppermute | solution.py:51
  58.9 7.5 %collective-permute-start.6 = (bf16[384,3200]{1,0:T(8,128)(2,1)}, bf16[384,3200]{1,0:T(8,128)(2,1)}, u32[]{:S(2)}, u32[]{:S(2)}) collective-permute-start(bf16[384,3200]{1,0:T(8,128)(2,1)} %pad_maximum_fusion.1.moved_ref), channel_id=1, source_target_pairs={{0,4},{4,0},{1,5},{5,1},{2,6},{6,2},{3,7},{7,3},{8,12},{12,8},{9,1... | collective-permute-start | bytes 7372808 | tf_op jit(solution)/shard_map/ppermute | solution.py:47
  62.4 39.5 %collective-permute-start.8 = (bf16[768,512]{1,0:T(8,128)(2,1)S(1)}, bf16[768,512]{1,0:T(8,128)(2,1)S(1)}, u32[]{:S(2)}, u32[]{:S(2)}) collective-permute-start(bf16[768,512]{1,0:T(8,128)(2,1)S(1)} %copy-done.19), channel_id=1, source_target_pairs={{0,1},{1,0},{2,3},{3,2},{4,5},{5,4},{6,7},{7,6},{8,9},{9,8},{10,11... | collective-permute-start | bytes 2359304 | tf_op jit(solution)/shard_map/ppermute | solution.py:59
  62.7 39.3 %collective-permute-start.9 = (bf16[768,512]{1,0:T(8,128)(2,1)S(1)}, bf16[768,512]{1,0:T(8,128)(2,1)}, u32[]{:S(2)}, u32[]{:S(2)}) collective-permute-start(bf16[768,512]{1,0:T(8,128)(2,1)S(1)} %copy-done.19), channel_id=1, source_target_pairs={{0,2},{2,0},{1,3},{3,1},{4,6},{6,4},{5,7},{7,5},{8,10},{10,8},{9,1... | collective-permute-start | bytes 2359304 | tf_op jit(solution)/shard_map/ppermute | solution.py:59
  73.1 28.8 %collective-permute-start.10 = (bf16[768,512]{1,0:T(8,128)(2,1)S(1)}, bf16[768,512]{1,0:T(8,128)(2,1)}, u32[]{:S(2)}, u32[]{:S(2)}) collective-permute-start(bf16[768,512]{1,0:T(8,128)(2,1)S(1)} %copy-done.20), channel_id=1, source_target_pairs={{0,1},{1,0},{2,3},{3,2},{4,5},{5,4},{6,7},{7,6},{8,9},{9,8},{10,11... | collective-permute-start | bytes 2359304 | tf_op jit(solution)/shard_map/ppermute | solution.py:59
  73.4 28.5 %collective-permute-start.11 = (bf16[768,512]{1,0:T(8,128)(2,1)S(1)}, bf16[768,512]{1,0:T(8,128)(2,1)}, u32[]{:S(2)}, u32[]{:S(2)}) collective-permute-start(bf16[768,512]{1,0:T(8,128)(2,1)S(1)} %copy-done.20), channel_id=1, source_target_pairs={{0,2},{2,0},{1,3},{3,1},{4,6},{6,4},{5,7},{7,5},{8,10},{10,8},{9,1... | collective-permute-start | bytes 2359304 | tf_op jit(solution)/shard_map/ppermute | solution.py:59
  74.2 27.7 %collective-permute-start.7 = (bf16[272,1024]{1,0:T(8,128)(2,1)}, bf16[272,1024]{1,0:T(8,128)(2,1)S(1)}, u32[]{:S(2)}, u32[]{:S(2)}) collective-permute-start(bf16[272,1024]{1,0:T(8,128)(2,1)} %constant_dynamic-update-slice_fusion), channel_id=1, source_target_pairs={{0,16},{8,24},{16,0},{24,8},{1,17},{9,25},{17,1},{25,9},{2,18},{10... | collective-permute-start | bytes 1671176 | tf_op jit(solution)/shard_map/ppermute | solution.py:51
  104.9 8.3 %collective-permute-start.14 = (bf16[4,272,1024]{2,1,0:T(8,128)(2,1)S(1)}, bf16[4,272,1024]{2,1,0:T(8,128)(2,1)S(1)}, u32[]{:S(2)}, u32[]{:S(2)}) collective-permute-start(bf16[4,272,1024]{2,1,0:T(8,128)(2,1)S(1)} %pad_maximum_fusion.2.packed_ref.code_ref), channel_id=1, source_target_pairs={{0,4},{4,0},{1,5},{5,1},{2,6},{6,2},{3,7},{7,3},{8,12},{12,8},{9,1... | collective-permute-start | bytes 6684680 | tf_op jit(solution)/shard_map/ppermute | solution.py:47
  109.5 37.5 %copy-start.9 = (bf16[768,512]{1,0:T(8,128)(2,1)S(1)}, bf16[768,512]{1,0:T(8,128)(2,1)}, u32[]{:S(2)}) copy-start(bf16[768,512]{1,0:T(8,128)(2,1)} %get-tuple-element.168.refs_11_) | copy-start | bytes 2359300
  109.5 35.4 %collective-permute-start.17 = (bf16[1536,512]{1,0:T(8,128)(2,1)S(1)}, bf16[1536,512]{1,0:T(8,128)(2,1)S(1)}, u32[]{:S(2)}, u32[]{:S(2)}) collective-permute-start(bf16[1536,512]{1,0:T(8,128)(2,1)S(1)} %get-tuple-element.370), channel_id=1, source_target_pairs={{0,1},{1,0},{2,3},{3,2},{4,5},{5,4},{6,7},{7,6},{8,9},{9,8},{10,11... | collective-permute-start | bytes 4718600 | tf_op jit(solution)/shard_map/ppermute | solution.py:74
  110.8 35.1 %collective-permute-start.18 = (bf16[1536,512]{1,0:T(8,128)(2,1)S(1)}, bf16[1536,512]{1,0:T(8,128)(2,1)S(1)}, u32[]{:S(2)}, u32[]{:S(2)}) collective-permute-start(bf16[1536,512]{1,0:T(8,128)(2,1)S(1)} %get-tuple-element.369), channel_id=1, source_target_pairs={{0,2},{2,0},{1,3},{3,1},{4,6},{6,4},{5,7},{7,5},{8,10},{10,8},{9,1... | collective-permute-start | bytes 4718600 | tf_op jit(solution)/shard_map/ppermute | solution.py:74
  111.5 12.5 %collective-permute-start.12 = (bf16[256,1024]{1,0:T(8,128)(2,1)}, bf16[256,1024]{1,0:T(8,128)(2,1)S(1)}, u32[]{:S(2)}, u32[]{:S(2)}) collective-permute-start(bf16[256,1024]{1,0:T(8,128)(2,1)} %get-tuple-element.193.rest_0_.refs_11_), channel_id=1, source_target_pairs={{0,24},{8,0},{16,8},{24,16},{1,25},{9,1},{17,9},{25,17},{2,26},{10... | collective-permute-start | bytes 1572872 | tf_op jit(solution)/shard_map/ppermute | solution.py:51
  111.6 25.5 %collective-permute-start.16 = (bf16[256,1024]{1,0:T(8,128)(2,1)}, bf16[256,1024]{1,0:T(8,128)(2,1)}, u32[]{:S(2)}, u32[]{:S(2)}) collective-permute-start(bf16[256,1024]{1,0:T(8,128)(2,1)} %get-tuple-element.193.rest_0_.refs_11_), channel_id=1, source_target_pairs={{0,8},{8,16},{16,24},{24,0},{1,9},{9,17},{17,25},{25,1},{2,10},{10... | collective-permute-start | bytes 1572872 | tf_op jit(solution)/shard_map/ppermute | solution.py:51
  113.2 35.4 %copy-start.1 = (bf16[4,272,1024]{2,1,0:T(8,128)(2,1)}, bf16[4,272,1024]{2,1,0:T(8,128)(2,1)S(1)}, u32[]{:S(2)}) copy-start(bf16[4,272,1024]{2,1,0:T(8,128)(2,1)S(1)} %collective-permute-done.14.packed_ref.code_ref) | copy-start | bytes 6684676
  113.2 32.6 %collective-permute-start.15 = (bf16[256,1024]{1,0:T(8,128)(2,1)}, bf16[256,1024]{1,0:T(8,128)(2,1)}, u32[]{:S(2)}, u32[]{:S(2)}) collective-permute-start(bf16[256,1024]{1,0:T(8,128)(2,1)} %get-tuple-element.193.rest_0_.refs_11_), channel_id=1, source_target_pairs={{0,4},{4,0},{1,5},{5,1},{2,6},{6,2},{3,7},{7,3},{8,12},{12,8},{9,1... | collective-permute-start | bytes 1572872 | tf_op jit(solution)/shard_map/ppermute | solution.py:47
  124.0 35.1 %copy-start.44 = (bf16[256,1024]{1,0:T(8,128)(2,1)}, bf16[256,1024]{1,0:T(8,128)(2,1)S(1)}, u32[]{:S(2)}) copy-start(bf16[256,1024]{1,0:T(8,128)(2,1)S(1)} %collective-permute-done.12.rest_1_) | copy-start | bytes 1572868
  148.6 27.1 %collective-permute-start.21 = (bf16[1152,512]{1,0:T(8,128)(2,1)}, bf16[1152,512]{1,0:T(8,128)(2,1)S(1)}, u32[]{:S(2)}, u32[]{:S(2)}) collective-permute-start(bf16[1152,512]{1,0:T(8,128)(2,1)} %get-tuple-element.368), channel_id=1, source_target_pairs={{0,1},{1,0},{2,3},{3,2},{4,5},{5,4},{6,7},{7,6},{8,9},{9,8},{10,11... | collective-permute-start | bytes 3538952 | tf_op jit(solution)/shard_map/ppermute | solution.py:74
  149.4 27.3 %collective-permute-start.22 = (bf16[1152,512]{1,0:T(8,128)(2,1)}, bf16[1152,512]{1,0:T(8,128)(2,1)S(1)}, u32[]{:S(2)}, u32[]{:S(2)}) collective-permute-start(bf16[1152,512]{1,0:T(8,128)(2,1)} %get-tuple-element.367), channel_id=1, source_target_pairs={{0,2},{2,0},{1,3},{3,1},{4,6},{6,4},{5,7},{7,5},{8,10},{10,8},{9,1... | collective-permute-start | bytes 3538952 | tf_op jit(solution)/shard_map/ppermute | solution.py:74
  150.1 3.7 collective-permute-start.19
  152.1 2.4 collective-permute-start.20
  152.1 23.1 %collective-permute-start.13 = (bf16[256,1024]{1,0:T(8,128)(2,1)}, bf16[256,1024]{1,0:T(8,128)(2,1)}, u32[]{:S(2)}, u32[]{:S(2)}) collective-permute-start(bf16[256,1024]{1,0:T(8,128)(2,1)} %get-tuple-element.193.rest_0_.refs_11_), channel_id=1, source_target_pairs={{0,16},{8,24},{16,0},{24,8},{1,17},{9,25},{17,1},{25,9},{2,18},{10... | collective-permute-start | bytes 1572872 | tf_op jit(solution)/shard_map/ppermute | solution.py:51
  175.2 9.8 %collective-permute-start.23 = (bf16[256,1024]{1,0:T(8,128)(2,1)}, bf16[256,1024]{1,0:T(8,128)(2,1)S(1)}, u32[]{:S(2)}, u32[]{:S(2)}) collective-permute-start(bf16[256,1024]{1,0:T(8,128)(2,1)} %collective-permute-done.13.rest_2_), channel_id=1, source_target_pairs={{0,4},{4,0},{1,5},{5,1},{2,6},{6,2},{3,7},{7,3},{8,12},{12,8},{9,1... | collective-permute-start | bytes 1572872 | tf_op jit(solution)/shard_map/ppermute | solution.py:47
  175.8 15.2 %collective-permute-start.24 = (bf16[384,512]{1,0:T(8,128)(2,1)S(1)}, bf16[384,512]{1,0:T(8,128)(2,1)S(1)}, u32[]{:S(2)}, u32[]{:S(2)}) collective-permute-start(bf16[384,512]{1,0:T(8,128)(2,1)S(1)} %slice.296), channel_id=1, source_target_pairs={{0,2},{2,0},{1,3},{3,1},{4,6},{6,4},{5,7},{7,5},{8,10},{10,8},{9,1... | collective-permute-start | bytes 1179656 | tf_op jit(solution)/shard_map/ppermute | solution.py:65
  176.7 14.2 %collective-permute-start.25 = (bf16[384,512]{1,0:T(8,128)(2,1)S(1)}, bf16[384,512]{1,0:T(8,128)(2,1)}, u32[]{:S(2)}, u32[]{:S(2)}) collective-permute-start(bf16[384,512]{1,0:T(8,128)(2,1)S(1)} %slice.297), channel_id=1, source_target_pairs={{0,1},{1,0},{2,3},{3,2},{4,5},{5,4},{6,7},{7,6},{8,9},{9,8},{10,11... | collective-permute-start | bytes 1179656 | tf_op jit(solution)/shard_map/ppermute | solution.py:65
  190.9 25.3 %copy-start.49 = (bf16[384,512]{1,0:T(8,128)(2,1)}, bf16[384,512]{1,0:T(8,128)(2,1)S(1)}, u32[]{:S(2)}) copy-start(bf16[384,512]{1,0:T(8,128)(2,1)S(1)} %collective-permute-done.24.refs_14_) | copy-start | bytes 1179652
  216.3 27.1 %collective-permute-start.26 = (bf16[1,1,768,512]{3,2,1,0:T(8,128)(2,1)}, bf16[1,1,768,512]{3,2,1,0:T(8,128)(2,1)S(1)}, u32[]{:S(2)}, u32[]{:S(2)}) collective-permute-start(bf16[1,1,768,512]{3,2,1,0:T(8,128)(2,1)} %get-tuple-element.211), channel_id=1, source_target_pairs={{0,1},{1,0},{2,3},{3,2},{4,5},{5,4},{6,7},{7,6},{8,9},{9,8},{10,11... | collective-permute-start | bytes 2359304 | tf_op jit(solution)/shard_map/ppermute | solution.py:74
  216.8 26.5 %collective-permute-start.27 = (bf16[1,1,768,512]{3,2,1,0:T(8,128)(2,1)}, bf16[1,1,768,512]{3,2,1,0:T(8,128)(2,1)S(1)}, u32[]{:S(2)}, u32[]{:S(2)}) collective-permute-start(bf16[1,1,768,512]{3,2,1,0:T(8,128)(2,1)} %get-tuple-element.212), channel_id=1, source_target_pairs={{0,2},{2,0},{1,3},{3,1},{4,6},{6,4},{5,7},{7,5},{8,10},{10,8},{9,1... | collective-permute-start | bytes 2359304 | tf_op jit(solution)/shard_map/ppermute | solution.py:74
  249.0 14.4 %collective-permute-start.28 = (bf16[4,256,1152]{2,1,0:T(8,128)(2,1)}, bf16[4,256,1152]{2,1,0:T(8,128)(2,1)}, u32[]{:S(2)}, u32[]{:S(2)}) collective-permute-start(bf16[4,256,1152]{2,1,0:T(8,128)(2,1)} %combine.4), channel_id=1, source_target_pairs={{0,4},{4,0},{1,5},{5,1},{2,6},{6,2},{3,7},{7,3},{8,12},{12,8},{9,1... | collective-permute-start | bytes 7077896 | tf_op jit(solution)/shard_map/ppermute | solution.py:47
  256.5 13.0 %collective-permute-start.29 = (bf16[4,256,1024]{2,1,0:T(8,128)(2,1)}, bf16[4,256,1024]{2,1,0:T(8,128)(2,1)}, u32[]{:S(2)}, u32[]{:S(2)}) collective-permute-start(bf16[4,256,1024]{2,1,0:T(8,128)(2,1)} %combine.5), channel_id=1, source_target_pairs={{0,4},{4,0},{1,5},{5,1},{2,6},{6,2},{3,7},{7,3},{8,12},{12,8},{9,1... | collective-permute-start | bytes 6291464 | tf_op jit(solution)/shard_map/ppermute | solution.py:47
  261.9 62.0 %collective-permute-start.30 = (bf16[3,1,768,512]{3,2,1,0:T(8,128)(2,1)}, bf16[3,1,768,512]{3,2,1,0:T(8,128)(2,1)S(1)}, u32[]{:S(2)}, u32[]{:S(2)}) collective-permute-start(bf16[3,1,768,512]{3,2,1,0:T(8,128)(2,1)} %get-tuple-element.234), channel_id=1, source_target_pairs={{0,1},{1,0},{2,3},{3,2},{4,5},{5,4},{6,7},{7,6},{8,9},{9,8},{10,11... | collective-permute-start | bytes 7077896 | tf_op jit(solution)/shard_map/ppermute | solution.py:74
  262.7 61.2 %collective-permute-start.31 = (bf16[3,1,768,512]{3,2,1,0:T(8,128)(2,1)}, bf16[3,1,768,512]{3,2,1,0:T(8,128)(2,1)}, u32[]{:S(2)}, u32[]{:S(2)}) collective-permute-start(bf16[3,1,768,512]{3,2,1,0:T(8,128)(2,1)} %get-tuple-element.235), channel_id=1, source_target_pairs={{0,2},{2,0},{1,3},{3,1},{4,6},{6,4},{5,7},{7,5},{8,10},{10,8},{9,1... | collective-permute-start | bytes 7077896 | tf_op jit(solution)/shard_map/ppermute | solution.py:74
  269.5 28.5 %collective-permute-start.32 = (bf16[256,1152]{1,0:T(8,128)(2,1)}, bf16[256,1152]{1,0:T(8,128)(2,1)S(1)}, u32[]{:S(2)}, u32[]{:S(2)}) collective-permute-start(bf16[256,1152]{1,0:T(8,128)(2,1)} %get-tuple-element.236), channel_id=1, source_target_pairs={{0,16},{8,24},{16,0},{24,8},{1,17},{9,25},{17,1},{25,9},{2,18},{10... | collective-permute-start | bytes 1769480 | tf_op jit(solution)/shard_map/ppermute | solution.py:51
  271.4 51.2 %collective-permute-start.33 = (bf16[256,1152]{1,0:T(8,128)(2,1)}, bf16[256,1152]{1,0:T(8,128)(2,1)}, u32[]{:S(2)}, u32[]{:S(2)}) collective-permute-start(bf16[256,1152]{1,0:T(8,128)(2,1)} %get-tuple-element.237), channel_id=1, source_target_pairs={{0,8},{8,16},{16,24},{24,0},{1,9},{9,17},{17,25},{25,1},{2,10},{10... | collective-permute-start | bytes 1769480 | tf_op jit(solution)/shard_map/ppermute | solution.py:51
  272.8 51.1 %collective-permute-start.34 = (bf16[256,1152]{1,0:T(8,128)(2,1)}, bf16[256,1152]{1,0:T(8,128)(2,1)}, u32[]{:S(2)}, u32[]{:S(2)}) collective-permute-start(bf16[256,1152]{1,0:T(8,128)(2,1)} %get-tuple-element.238), channel_id=1, source_target_pairs={{0,24},{8,0},{16,8},{24,16},{1,25},{9,1},{17,9},{25,17},{2,26},{10... | collective-permute-start | bytes 1769480 | tf_op jit(solution)/shard_map/ppermute | solution.py:51
  298.0 35.6 %copy-start.39 = (bf16[256,1152]{1,0:T(8,128)(2,1)}, bf16[256,1152]{1,0:T(8,128)(2,1)S(1)}, u32[]{:S(2)}) copy-start(bf16[256,1152]{1,0:T(8,128)(2,1)S(1)} %collective-permute-done.32.refs_1_) | copy-start | bytes 1769476
  330.0 40.2 %collective-permute-start.35 = (bf16[2,1,768,512]{3,2,1,0:T(8,128)(2,1)}, bf16[2,1,768,512]{3,2,1,0:T(8,128)(2,1)S(1)}, u32[]{:S(2)}, u32[]{:S(2)}) collective-permute-start(bf16[2,1,768,512]{3,2,1,0:T(8,128)(2,1)} %get-tuple-element.247), channel_id=1, source_target_pairs={{0,1},{1,0},{2,3},{3,2},{4,5},{5,4},{6,7},{7,6},{8,9},{9,8},{10,11... | collective-permute-start | bytes 4718600 | tf_op jit(solution)/shard_map/ppermute | solution.py:74
  330.7 39.6 %collective-permute-start.36 = (bf16[2,1,768,512]{3,2,1,0:T(8,128)(2,1)}, bf16[2,1,768,512]{3,2,1,0:T(8,128)(2,1)S(1)}, u32[]{:S(2)}, u32[]{:S(2)}) collective-permute-start(bf16[2,1,768,512]{3,2,1,0:T(8,128)(2,1)} %get-tuple-element.248), channel_id=1, source_target_pairs={{0,2},{2,0},{1,3},{3,1},{4,6},{6,4},{5,7},{7,5},{8,10},{10,8},{9,1... | collective-permute-start | bytes 4718600 | tf_op jit(solution)/shard_map/ppermute | solution.py:74
  331.5 38.7 %collective-permute-start.37 = (bf16[256,1024]{1,0:T(8,128)(2,1)}, bf16[256,1024]{1,0:T(8,128)(2,1)}, u32[]{:S(2)}, u32[]{:S(2)}) collective-permute-start(bf16[256,1024]{1,0:T(8,128)(2,1)} %get-tuple-element.249), channel_id=1, source_target_pairs={{0,8},{8,16},{16,24},{24,0},{1,9},{9,17},{17,25},{25,1},{2,10},{10... | collective-permute-start | bytes 1572872 | tf_op jit(solution)/shard_map/ppermute | solution.py:51
  332.2 38.1 %collective-permute-start.38 = (bf16[256,1024]{1,0:T(8,128)(2,1)}, bf16[256,1024]{1,0:T(8,128)(2,1)}, u32[]{:S(2)}, u32[]{:S(2)}) collective-permute-start(bf16[256,1024]{1,0:T(8,128)(2,1)} %get-tuple-element.250), channel_id=1, source_target_pairs={{0,24},{8,0},{16,8},{24,16},{1,25},{9,1},{17,9},{25,17},{2,26},{10... | collective-permute-start | bytes 1572872 | tf_op jit(solution)/shard_map/ppermute | solution.py:51
  371.9 7.3 %collective-permute-start.40 = (bf16[4,128,3200]{2,1,0:T(8,128)(2,1)}, bf16[4,128,3200]{2,1,0:T(8,128)(2,1)S(1)}, u32[]{:S(2)}, u32[]{:S(2)}) collective-permute-start(bf16[4,128,3200]{2,1,0:T(8,128)(2,1)} %get-tuple-element.272), channel_id=1, source_target_pairs={{0,4},{4,0},{1,5},{5,1},{2,6},{6,2},{3,7},{7,3},{8,12},{12,8},{9,1... | collective-permute-start | bytes 9830408 | tf_op jit(solution)/shard_map/ppermute | solution.py:47
  373.6 13.8 %collective-permute-start.41 = (bf16[2,128,1024]{2,1,0:T(8,128)(2,1)}, bf16[2,128,1024]{2,1,0:T(8,128)(2,1)}, u32[]{:S(2)}, u32[]{:S(2)}) collective-permute-start(bf16[2,128,1024]{2,1,0:T(8,128)(2,1)} %get-tuple-element.275), channel_id=1, source_target_pairs={{0,1},{1,0},{2,3},{3,2},{4,5},{5,4},{6,7},{7,6},{8,9},{9,8},{10,11... | collective-permute-start | bytes 1572872 | tf_op jit(solution)/shard_map/ppermute | solution.py:91
  374.3 13.5 %collective-permute-start.42 = (bf16[2,128,1024]{2,1,0:T(8,128)(2,1)}, bf16[2,128,1024]{2,1,0:T(8,128)(2,1)}, u32[]{:S(2)}, u32[]{:S(2)}) collective-permute-start(bf16[2,128,1024]{2,1,0:T(8,128)(2,1)} %get-tuple-element.276), channel_id=1, source_target_pairs={{0,2},{2,0},{1,3},{3,1},{4,6},{6,4},{5,7},{7,5},{8,10},{10,8},{9,1... | collective-permute-start | bytes 1572872 | tf_op jit(solution)/shard_map/ppermute | solution.py:91
  381.0 33.5 %copy-start.36 = (bf16[1,1,768,512]{3,2,1,0:T(8,128)(2,1)S(1)}, bf16[1,1,768,512]{3,2,1,0:T(8,128)(2,1)}, u32[]{:S(2)}) copy-start(bf16[1,1,768,512]{3,2,1,0:T(8,128)(2,1)} %get-tuple-element.299) | copy-start | bytes 2359300
  387.1 22.0 %copy-start.31 = (bf16[2,64,3200]{2,1,0:T(8,128)(2,1)S(1)}, bf16[2,64,3200]{2,1,0:T(8,128)(2,1)}, u32[]{:S(2)}) copy-start(bf16[2,64,3200]{2,1,0:T(8,128)(2,1)} %get-tuple-element.286) | copy-start | bytes 2457604
  387.8 18.9 %collective-permute-start.43 = (bf16[2,64,3200]{2,1,0:T(8,128)(2,1)}, bf16[2,64,3200]{2,1,0:T(8,128)(2,1)S(1)}, u32[]{:S(2)}, u32[]{:S(2)}) collective-permute-start(bf16[2,64,3200]{2,1,0:T(8,128)(2,1)} %get-tuple-element.277), channel_id=1, source_target_pairs={{0,1},{1,0},{2,3},{3,2},{4,5},{5,4},{6,7},{7,6},{8,9},{9,8},{10,11... | collective-permute-start | bytes 2457608 | tf_op jit(solution)/shard_map/ppermute | solution.py:91
  388.5 18.6 %collective-permute-start.44 = (bf16[2,64,3200]{2,1,0:T(8,128)(2,1)}, bf16[2,64,3200]{2,1,0:T(8,128)(2,1)S(1)}, u32[]{:S(2)}, u32[]{:S(2)}) collective-permute-start(bf16[2,64,3200]{2,1,0:T(8,128)(2,1)} %get-tuple-element.278), channel_id=1, source_target_pairs={{0,2},{2,0},{1,3},{3,1},{4,6},{6,4},{5,7},{7,5},{8,10},{10,8},{9,1... | collective-permute-start | bytes 2457608 | tf_op jit(solution)/shard_map/ppermute | solution.py:91
  390.2 28.6 %collective-permute-start.39 = (bf16[256,1024]{1,0:T(8,128)(2,1)}, bf16[256,1024]{1,0:T(8,128)(2,1)S(1)}, u32[]{:S(2)}, u32[]{:S(2)}) collective-permute-start(bf16[256,1024]{1,0:T(8,128)(2,1)} %get-tuple-element.264), channel_id=1, source_target_pairs={{0,16},{8,24},{16,0},{24,8},{1,17},{9,25},{17,1},{25,9},{2,18},{10... | collective-permute-start | bytes 1572872 | tf_op jit(solution)/shard_map/ppermute | solution.py:51
  408.3 13.3 %collective-permute-start.48 = (bf16[64,3200]{1,0:T(8,128)(2,1)S(1)}, bf16[64,3200]{1,0:T(8,128)(2,1)S(1)}, u32[]{:S(2)}, u32[]{:S(2)}) collective-permute-start(bf16[64,3200]{1,0:T(8,128)(2,1)S(1)} %fusion.7), channel_id=1, source_target_pairs={{0,1},{1,0},{2,3},{3,2},{4,5},{5,4},{6,7},{7,6},{8,9},{9,8},{10,11... | collective-permute-start | bytes 1228808 | tf_op jit(solution)/shard_map/ppermute | solution.py:99
  409.2 12.5 %collective-permute-start.47 = (bf16[64,3200]{1,0:T(8,128)(2,1)S(1)}, bf16[64,3200]{1,0:T(8,128)(2,1)S(1)}, u32[]{:S(2)}, u32[]{:S(2)}) collective-permute-start(bf16[64,3200]{1,0:T(8,128)(2,1)S(1)} %fusion.6), channel_id=1, source_target_pairs={{0,2},{2,0},{1,3},{3,1},{4,6},{6,4},{5,7},{7,5},{8,10},{10,8},{9,1... | collective-permute-start | bytes 1228808 | tf_op jit(solution)/shard_map/ppermute | solution.py:98
  411.1 31.1 %collective-permute-start.45 = (bf16[128,1024]{1,0:T(8,128)(2,1)S(1)}, bf16[128,1024]{1,0:T(8,128)(2,1)S(1)}, u32[]{:S(2)}, u32[]{:S(2)}) collective-permute-start(bf16[128,1024]{1,0:T(8,128)(2,1)S(1)} %fusion.11), channel_id=1, source_target_pairs={{0,2},{2,0},{1,3},{3,1},{4,6},{6,4},{5,7},{7,5},{8,10},{10,8},{9,1... | collective-permute-start | bytes 786440 | tf_op jit(solution)/shard_map/ppermute | solution.py:98
  413.7 47.6 %collective-permute-start.46 = (bf16[128,1024]{1,0:T(8,128)(2,1)}, bf16[128,1024]{1,0:T(8,128)(2,1)}, u32[]{:S(2)}, u32[]{:S(2)}) collective-permute-start(bf16[128,1024]{1,0:T(8,128)(2,1)} %fusion.12), channel_id=1, source_target_pairs={{0,1},{1,0},{2,3},{3,2},{4,5},{5,4},{6,7},{7,6},{8,9},{9,8},{10,11... | collective-permute-start | bytes 786440 | tf_op jit(solution)/shard_map/ppermute | solution.py:99
  422.1 5.9 %collective-permute-start.49 = (bf16[32,3200]{1,0:T(8,128)(2,1)S(1)}, bf16[32,3200]{1,0:T(8,128)(2,1)S(1)}, u32[]{:S(2)}, u32[]{:S(2)}) collective-permute-start(bf16[32,3200]{1,0:T(8,128)(2,1)S(1)} %get-tuple-element.364), channel_id=1, source_target_pairs={{0,16},{8,24},{16,0},{24,8},{1,17},{9,25},{17,1},{25,9},{2,18},{10... | collective-permute-start | bytes 614408 | tf_op jit(solution)/shard_map/ppermute | solution.py:51
  422.2 16.4 %collective-permute-start.50 = (bf16[32,3200]{1,0:T(8,128)(2,1)S(1)}, bf16[32,3200]{1,0:T(8,128)(2,1)S(1)}, u32[]{:S(2)}, u32[]{:S(2)}) collective-permute-start(bf16[32,3200]{1,0:T(8,128)(2,1)S(1)} %get-tuple-element.366), channel_id=1, source_target_pairs={{0,8},{8,16},{16,24},{24,0},{1,9},{9,17},{17,25},{25,1},{2,10},{10... | collective-permute-start | bytes 614408 | tf_op jit(solution)/shard_map/ppermute | solution.py:51
  423.0 17.2 %collective-permute-start.51 = (bf16[32,3200]{1,0:T(8,128)(2,1)S(1)}, bf16[32,3200]{1,0:T(8,128)(2,1)S(1)}, u32[]{:S(2)}, u32[]{:S(2)}) collective-permute-start(bf16[32,3200]{1,0:T(8,128)(2,1)S(1)} %get-tuple-element.365), channel_id=1, source_target_pairs={{0,24},{8,0},{16,8},{24,16},{1,25},{9,1},{17,9},{25,17},{2,26},{10... | collective-permute-start | bytes 614408 | tf_op jit(solution)/shard_map/ppermute | solution.py:51
  440.4 10.5 %collective-permute-start.52 = (bf16[32,3200]{1,0:T(8,128)(2,1)S(1)}, bf16[32,3200]{1,0:T(8,128)(2,1)S(1)}, u32[]{:S(2)}, u32[]{:S(2)}) collective-permute-start(bf16[32,3200]{1,0:T(8,128)(2,1)S(1)} %fusion.10), channel_id=1, source_target_pairs={{0,16},{8,24},{16,0},{24,8},{1,17},{9,25},{17,1},{25,9},{2,18},{10... | collective-permute-start | bytes 614408 | tf_op jit(solution)/shard_map/ppermute | solution.py:51
  440.5 17.5 %collective-permute-start.53 = (bf16[32,3200]{1,0:T(8,128)(2,1)S(1)}, bf16[32,3200]{1,0:T(8,128)(2,1)S(1)}, u32[]{:S(2)}, u32[]{:S(2)}) collective-permute-start(bf16[32,3200]{1,0:T(8,128)(2,1)S(1)} %fusion.10), channel_id=1, source_target_pairs={{0,24},{8,0},{16,8},{24,16},{1,25},{9,1},{17,9},{25,17},{2,26},{10... | collective-permute-start | bytes 614408 | tf_op jit(solution)/shard_map/ppermute | solution.py:51
  442.2 15.7 %collective-permute-start.54 = (bf16[32,3200]{1,0:T(8,128)(2,1)S(1)}, bf16[32,3200]{1,0:T(8,128)(2,1)S(1)}, u32[]{:S(2)}, u32[]{:S(2)}) collective-permute-start(bf16[32,3200]{1,0:T(8,128)(2,1)S(1)} %fusion.10), channel_id=1, source_target_pairs={{0,8},{8,16},{16,24},{24,0},{1,9},{9,17},{17,25},{25,1},{2,10},{10... | collective-permute-start | bytes 614408 | tf_op jit(solution)/shard_map/ppermute | solution.py:51
  459.0 5.1 %collective-permute-start.55 = (bf16[128,3200]{1,0:T(8,128)(2,1)S(1)}, bf16[128,3200]{1,0:T(8,128)(2,1)S(1)}, u32[]{:S(2)}, u32[]{:S(2)}) collective-permute-start(bf16[128,3200]{1,0:T(8,128)(2,1)S(1)} %bitcast_select_fusion.mine_ref), channel_id=1, source_target_pairs={{0,4},{4,0},{1,5},{5,1},{2,6},{6,2},{3,7},{7,3},{8,12},{12,8},{9,1... | collective-permute-start | bytes 2457608 | tf_op jit(solution)/shard_map/ppermute | solution.py:47
  (47 other events, 197.8 us)

commit v12 on v11

--- a/solution.py
+++ b/solution.py
@@ -1262,15 +1262,16 @@
             normed_got = grid_scatter_first(*normed_first)
             dense_got = grid_scatter_first(*after(dense_first, *normed_got))
             early_got, late_got = after((early_got, late_got), *dense_got)
+            dense_halves = grid_scatter_second(dense_got, dense_a, dense_b)
             dense_low = across_z(
-                jnp.concatenate(grid_scatter_second(dense_got, dense_a, dense_b), axis=0), z
+                jnp.concatenate(dense_halves, axis=0), z
             )
             (
                 query_sum, key_sum, value_sum, output_sum, router_sum, attn_gain_sum, moe_gain_sum,
             ) = dense_outputs(core, dense_low, swap_core(dense_low), wide, narrow)
-            y_pieces = after(y_pieces, *dense_got)
+            y_pieces = after(y_pieces, *dense_halves)
             normed_grad = jnp.concatenate(
-                grid_scatter_second(normed_got, normed_a, normed_b, *dense_got), axis=0
+                grid_scatter_second(normed_got, normed_a, normed_b, *dense_halves), axis=0
             )
             first_value, first_pull = jax.vjp(lambda v: rms_norm(v, full_attn_gain), in_float)
             input_grad = residual_grad + first_pull(normed_grad)[0]

time: 481 us -> 485 us (level)
  transfers between devices with their start and end apart: 56 -> 56, of which waited for: 24 -> 25; matrix products, arithmetic and copies ran while one was open for 9% -> 9% of each run, Pallas kernels for 30% -> 30%
where the time goes in v12:
time: 485 us; the launch traced here: 476 us
  Pallas kernels  181 us (37%)
  waiting for transfers between devices  170 us (35%)
  starting transfers between devices  52.9 us (11%)
  other arithmetic  34.9 us (7%)
  local copies, waits for them, and re-layouts  34.8 us (7%)
    ppermute x18, waiting for transfers between devices, cyclic(): lax.ppermute(rows, 'z', [(i, (i + shift) % size) for i in range(size)])  113 us
    pallas_call x2, Pallas kernels, experts(): pl.pallas_call(kernel, out_shape=out_shape, grid_spec=pltpu.PrefetchScala...  51.2 us
    pallas_call x1, Pallas kernels, attention_backward(): pl.pallas_call(kernel, out_shape=shapes, grid_spec=pltpu.PrefetchScalarGr...  36.7 us
    pallas_call x1, Pallas kernels, attention_forward(): pl.pallas_call(kernel, grid=(GROUPS,), in_specs=[fixed(tok_rows, width),...  25.3 us
    pallas_call x4, Pallas kernels, combine_rows(): pl.pallas_call(kernel, out_shape=out_shape, grid_spec=pltpu.PrefetchScala...  22 us
    pallas_call x4, Pallas kernels, dispatch_rows(): pl.pallas_call(kernel, out_shape=out_shape, grid_spec=pltpu.PrefetchScala...  19.3 us
    ppermute x4, waiting for transfers between devices, grid_scatter_first(): return (lax.ppermute(first_a, 'x', SWAP), lax.ppermute(first_b, 'y', SWAP))  17.7 us
    unnamed x108, local copies, waits for them, and re-layouts  16.5 us
  transfers between devices with their start and end apart: 56, of which 25 were waited for; matrix products, arithmetic and copies ran while one was open for 9% of the time, Pallas kernels for 30%

profile of v12, /device:TPU:9, one launch (start us, length us, event | category | flops | bytes accessed | tf_op | source)
XLA Modules:
  0.0 475.8 jit_solution(2146004127873898073)
XLA Ops:
  4.2 2.1 concatenate.57.shard_ref
  11.4 2.6 convert_reduce_fusion
  15.7 1.3 or_select_fusion.bias_ref.refs_21_
  17.0 3.0 fusion.5
  21.6 1.3 slice_bitcast_fusion.1
  25.6 8.3 %collective-permute-done.2 = bf16[272,1024]{1,0:T(8,128)(2,1)} collective-permute-done((bf16[272,1024]{1,0:T(8,128)(2,1)}, bf16[272,1024]{1,0:T(8,128)(2,1)}, u32[]{:S(2)}, u32[]{:S(2)}) %collective-permute-start.2) | collective-permute-done | bytes 557088 | tf_op jit(solution)/shard_map/ppermute | solution.py:51
  33.9 5.4 %collective-permute-done.xa_ref.xb_ref = bf16[128,5248]{1,0:T(8,128)(2,1)S(1)} collective-permute-done((bf16[128,5248]{1,0:T(8,128)(2,1)}, bf16[128,5248]{1,0:T(8,128)(2,1)S(1)}, u32[]{:S(2)}, u32[]{:S(2)}) %collective-permute-start) | collective-permute-done | bytes 1343520 | tf_op jit(solution)/shard_map/ppermute | solution.py:59
  40.3 1.3 collective-permute-start.3
  43.3 12.0 %collective-permute-done.3.da_ref.db_ref = bf16[64,5248]{1,0:T(8,128)(2,1)S(1)} collective-permute-done((bf16[64,5248]{1,0:T(8,128)(2,1)S(1)}, bf16[64,5248]{1,0:T(8,128)(2,1)S(1)}, u32[]{:S(2)}, u32[]{:S(2)}) %collective-permute-start.3) | collective-permute-done | bytes 671776 | tf_op jit(solution)/shard_map/ppermute | solution.py:65
  57.2 1.6 pad_maximum_fusion.1.moved_ref
  58.9 2.8 collective-permute-start.6
  63.4 2.9 collective-permute-done.6.other_ref
  66.4 6.8 %assemble.1.tail_ref.wo_ref.wq_ref.wk_ref.wv_ref.refs_8_.refs_9_.refs_18_.refs_19_.refs_20_ = bf16[1024,3200]{1,0:T(8,128)(2,1)} custom-call(s32[7]{0:T(128)} %stack.78.places_ref, bf16[256,3200]{1,0:T(8,128)(2,1)} %copy-done.6, bf16[384,3200]{1,0:T(8,128)(2,1)} %pad_maximum_fusion.1.moved_ref, bf16[384,3200]{1,0:T(8,128)(2,1)} %collective-permute-done.6.other_ref), custom_call_target="tpu_custom_call" | custom-call | tf_op jit(solution)/shard_map/assemble/pallas_call | solution.py:147
  74.2 2.3 collective-permute-start.7
  76.5 25.3 %attention.1 = (bf16[1024,1024]{1,0:T(8,128)(2,1)}, bf16[1024,1024]{1,0:T(8,128)(2,1)}, bf16[256,1024]{1,0:T(8,128)(2,1)}, bf16[1024,512]{1,0:T(8,128)(2,1)}, bf...) custom-call(bf16[256,1024]{1,0:T(8,128)(2,1)} %own_ref.1, ...), custom_call_target="tpu_custom_call" | custom-call | tf_op jit(solution)/shard_map/attention/pallas_call | solution.py:594
  103.0 1.8 pad_maximum_fusion.2.packed_ref.code_ref
  111.6 1.6 collective-permute-start.16
  113.2 1.7 collective-permute-start.15
  114.9 9.0 %collective-permute-done.12.rest_1_ = bf16[256,1024]{1,0:T(8,128)(2,1)S(1)} collective-permute-done((bf16[256,1024]{1,0:T(8,128)(2,1)}, bf16[256,1024]{1,0:T(8,128)(2,1)S(1)}, u32[]{:S(2)}, u32[]{:S(2)}) %collective-permute-start.12) | collective-permute-done | bytes 524320 | tf_op jit(solution)/shard_map/ppermute | solution.py:51
  124.0 13.1 %collective-permute-done.16.rest_3_ = bf16[256,1024]{1,0:T(8,128)(2,1)} collective-permute-done((bf16[256,1024]{1,0:T(8,128)(2,1)}, bf16[256,1024]{1,0:T(8,128)(2,1)}, u32[]{:S(2)}, u32[]{:S(2)}) %collective-permute-start.16) | collective-permute-done | bytes 524320 | tf_op jit(solution)/shard_map/ppermute | solution.py:51
  137.1 7.8 %collective-permute-done.17.refs_10_.refs_15_.refs_7_ = bf16[1536,512]{1,0:T(8,128)(2,1)S(1)} collective-permute-done((bf16[1536,512]{1,0:T(8,128)(2,1)S(1)}, bf16[1536,512]{1,0:T(8,128)(2,1)S(1)}, u32[]{:S(2)}, u32[]{:S(2)}) %collective-permute-start.17) | collective-permute-done | bytes 1572896 | tf_op jit(solution)/shard_map/ppermute | solution.py:74
  147.1 1.6 pad_maximum_fusion.13
  150.1 2.0 collective-permute-start.19
  152.1 1.7 collective-permute-start.13
  154.5 4.5 dispatch.4.refs_2_
  159.1 4.5 dispatch.5.refs_3_
  163.6 11.7 %collective-permute-done.13.rest_2_ = bf16[256,1024]{1,0:T(8,128)(2,1)} collective-permute-done((bf16[256,1024]{1,0:T(8,128)(2,1)}, bf16[256,1024]{1,0:T(8,128)(2,1)}, u32[]{:S(2)}, u32[]{:S(2)}) %collective-permute-start.13) | collective-permute-done | bytes 524320 | tf_op jit(solution)/shard_map/ppermute | solution.py:51
  178.4 1.5 slice.341.rest_4_
  179.9 5.1 %dispatch.6 = (bf16[4,320,1024]{2,1,0:T(8,128)(2,1)}, f32[4,320,128]{2,1,0:T(8,128)}) custom-call(s32[1]{0:T(128)} %bitcast.26.lead_ref, bf16[4,272,1024]{2,1,0:T(8,128)(2,1)} %copy-done, bf16[256,1024]{1,0:T(8,128)(2,1)} %get-tuple-element.193.rest_0_.refs_11_, bf16[256,1024]{1,0:T(8,128)(2,1)} %copy-done.44, ...), custom_call_target="tpu_custom_call" | custom-call | tf_op jit(solution)/shard_map/dispatch/pallas_call | solution.py:240
  185.8 5.1 %dispatch.7 = (bf16[4,320,1024]{2,1,0:T(8,128)(2,1)}, f32[4,320,128]{2,1,0:T(8,128)}) custom-call(s32[1]{0:T(128)} %bitcast.26.lead_ref, bf16[4,272,1024]{2,1,0:T(8,128)(2,1)} %copy-done.1, bf16[256,1024]{1,0:T(8,128)(2,1)} %collective-permute-done.15.rest_0_, bf16[256,1024]{1,0:T(8,128)(2,1)} %copy-done.45, bf16[256,1024]{1,0:T(8,128)(2,1)} %copy-done.46, ...), custom_call_target="tpu_custom_call" | custom-call | tf_op jit(solution)/shard_map/dispatch/pallas_call | solution.py:240
  191.0 25.3 %experts.2 = (bf16[8,160,1024]{2,1,0:T(8,128)(2,1)}, bf16[8,160,1152]{2,1,0:T(8,128)(2,1)}, bf16[1,1,768,512]{3,2,1,0:T(8,128)(2,1)}, bf16[1,1,768,512]{3,2,1,0:...) custom-call(s32[5]{0:T(128)} %pad_add_fusion.order_ref, ...), custom_call_target="tpu_custom_call" | custom-call | tf_op jit(solution)/shard_map/experts/pallas_call | solution.py:470
  217.5 25.9 %experts.3 = (bf16[8,160,1024]{2,1,0:T(8,128)(2,1)}, bf16[8,160,1152]{2,1,0:T(8,128)(2,1)}, bf16[1,1,768,512]{3,2,1,0:T(8,128)(2,1)}, bf16[1,1,768,512]{3,2,1,0:...) custom-call(s32[5]{0:T(128)} %pad_add_fusion.order_ref, ...), custom_call_target="tpu_custom_call" | custom-call | tf_op jit(solution)/shard_map/experts/pallas_call | solution.py:470
  243.4 5.6 %combine.4 = bf16[4,256,1152]{2,1,0:T(8,128)(2,1)} custom-call(s32[1]{0:T(128)} %bitcast.26.lead_ref, bf16[4,272,1024]{2,1,0:T(8,128)(2,1)} %copy-done.1, bf16[8,160,1152]{2,1,0:T(8,128)(2,1)} %get-tuple-element.213.rest_0_, bf16[8,160,1152]{2,1,0:T(8,128)(2,1)} %get-tuple-element.214.rest_1_), custom_call_target="tpu_custom_call" | custom-call | tf_op jit(solution)/shard_map/combine/pallas_call | solution.py:298
  248.9 2.7 collective-permute-start.28
  251.6 4.8 %combine.5 = bf16[4,256,1024]{2,1,0:T(8,128)(2,1)} custom-call(s32[1]{0:T(128)} %bitcast.26.lead_ref, bf16[4,272,1024]{2,1,0:T(8,128)(2,1)} %copy-done.1, bf16[8,160,1024]{2,1,0:T(8,128)(2,1)} %get-tuple-element.215.rest_0_, bf16[8,160,1024]{2,1,0:T(8,128)(2,1)} %get-tuple-element.216.rest_1_), custom_call_target="tpu_custom_call" | custom-call | tf_op jit(solution)/shard_map/combine/pallas_call | solution.py:298
  256.5 5.4 %join_parts.2 = (bf16[3,1,768,512]{3,2,1,0:T(8,128)(2,1)}, bf16[3,1,768,512]{3,2,1,0:T(8,128)(2,1)}) custom-call(bf16[1,1,768,512]{3,2,1,0:T(8,128)(2,1)} %get-tuple-element.228.refs_0_, bf16[1,1,768,512]{3,2,1,0:T(8,128)(2,1)} %get-tuple-element.229.refs_1_, bf16[1,1,768,512]{3,2,1,0:T(8,128)(2,1)} %get-tuple-element.230.refs_2_, ...), custom_call_target="tpu_custom_call" | custom-call | tf_op jit(solution)/shard_map/join_parts/pallas_call | solution.py:896
  263.4 6.0 %combine.6 = (bf16[256,1152]{1,0:T(8,128)(2,1)}, bf16[256,1152]{1,0:T(8,128)(2,1)}, bf16[256,1152]{1,0:T(8,128)(2,1)}, bf16[256,1152]{1,0:T(8,128)(2,1)}) custom-call(s32[1]{0:T(128)} %bitcast.26.lead_ref, bf16[4,272,1024]{2,1,0:T(8,128)(2,1)} %copy-done, bf16[8,160,1152]{2,1,0:T(8,128)(2,1)} %get-tuple-element.213.rest_0_, ...), custom_call_target="tpu_custom_call" | custom-call | tf_op jit(solution)/shard_map/combine/pallas_call | solution.py:298
  269.4 2.0 collective-permute-start.32
  271.4 1.4 collective-permute-start.33
  272.8 5.7 %combine.7 = (bf16[256,1024]{1,0:T(8,128)(2,1)}, bf16[256,1024]{1,0:T(8,128)(2,1)}, bf16[256,1024]{1,0:T(8,128)(2,1)}, bf16[256,1024]{1,0:T(8,128)(2,1)}) custom-call(s32[1]{0:T(128)} %bitcast.26.lead_ref, bf16[4,272,1024]{2,1,0:T(8,128)(2,1)} %copy-done, bf16[8,160,1024]{2,1,0:T(8,128)(2,1)} %get-tuple-element.215.rest_0_, ...), custom_call_target="tpu_custom_call" | custom-call | tf_op jit(solution)/shard_map/combine/pallas_call | solution.py:298
  278.5 19.4 %collective-permute-done.32.refs_1_ = bf16[256,1152]{1,0:T(8,128)(2,1)S(1)} collective-permute-done((bf16[256,1152]{1,0:T(8,128)(2,1)}, bf16[256,1152]{1,0:T(8,128)(2,1)S(1)}, u32[]{:S(2)}, u32[]{:S(2)}) %collective-permute-start.32) | collective-permute-done | bytes 589856 | tf_op jit(solution)/shard_map/ppermute | solution.py:51
  298.0 24.7 %collective-permute-done.33.refs_2_ = bf16[256,1152]{1,0:T(8,128)(2,1)} collective-permute-done((bf16[256,1152]{1,0:T(8,128)(2,1)}, bf16[256,1152]{1,0:T(8,128)(2,1)}, u32[]{:S(2)}, u32[]{:S(2)}) %collective-permute-start.33) | collective-permute-done | bytes 589856 | tf_op jit(solution)/shard_map/ppermute | solution.py:51
  323.8 1.4 copy-done.10
  325.2 4.7 join_parts.3
  333.4 36.7 %attention_grad.1 = (bf16[4,128,3200]{2,1,0:T(8,128)(2,1)}, bf16[4,128,3200]{2,1,0:T(8,128)(2,1)}, bf16[2,128,1024]{2,1,0:T(8,128)(2,1)}, bf16[2,128,1024]{2,1,0...) custom-call(s32[2]{0:T(128)} %pad_add_fusion.1.here_ref, ...), custom_call_target="tpu_custom_call" | custom-call | tf_op jit(solution)/shard_map/attention_grad/pallas_call | solution.py:801
  371.8 1.6 collective-permute-start.40
  374.9 4.2 collective-permute-done.40.got_ref
  379.1 1.7 copy-done.17
  380.8 6.1 %core_halves.1 = (bf16[2,64,3200]{2,1,0:T(8,128)(2,1)}, bf16[2,64,3200]{2,1,0:T(8,128)(2,1)}, bf16[2,64,3200]{2,1,0:T(8,128)(2,1)}, bf16[2,64,3200]{2,1,0:T(8,128)(2,1)}) custom-call(bf16[4,128,3200]{2,1,0:T(8,128)(2,1)} %get-tuple-element.271.keep_ref, bf16[4,128,3200]{2,1,0:T(8,128)(2,1)} %copy-done.17), custom_call_target="tpu_custom_call" | custom-call | tf_op jit(solution)/shard_map/core_halves/pallas_call | solution.py:866
  391.1 16.4 %collective-permute-done.43 = bf16[2,64,3200]{2,1,0:T(8,128)(2,1)S(1)} collective-permute-done((bf16[2,64,3200]{2,1,0:T(8,128)(2,1)}, bf16[2,64,3200]{2,1,0:T(8,128)(2,1)S(1)}, u32[]{:S(2)}, u32[]{:S(2)}) %collective-permute-start.43) | collective-permute-done | bytes 819232 | tf_op jit(solution)/shard_map/ppermute | solution.py:91
  411.2 2.6 add_bitcast_fusion.3
  416.0 1.5 fusion
  418.2 2.8 fusion.28
  422.2 3.9 collective-permute-done.45
  431.2 2.4 add_convert_fusion
  433.6 9.4 %collective-permute-done.50 = bf16[32,3200]{1,0:T(8,128)(2,1)S(1)} collective-permute-done((bf16[32,3200]{1,0:T(8,128)(2,1)S(1)}, bf16[32,3200]{1,0:T(8,128)(2,1)S(1)}, u32[]{:S(2)}, u32[]{:S(2)}) %collective-permute-start.50) | collective-permute-done | bytes 204832 | tf_op jit(solution)/shard_map/ppermute | solution.py:51
  443.0 1.7 collective-permute-done.51
  444.8 1.7 collective-permute-start.53
  447.6 7.8 %collective-permute-done.52 = bf16[32,3200]{1,0:T(8,128)(2,1)S(1)} collective-permute-done((bf16[32,3200]{1,0:T(8,128)(2,1)S(1)}, bf16[32,3200]{1,0:T(8,128)(2,1)S(1)}, u32[]{:S(2)}, u32[]{:S(2)}) %collective-permute-start.52) | collective-permute-done | bytes 204832 | tf_op jit(solution)/shard_map/ppermute | solution.py:51
  455.4 6.8 %collective-permute-done.53 = bf16[32,3200]{1,0:T(8,128)(2,1)S(1)} collective-permute-done((bf16[32,3200]{1,0:T(8,128)(2,1)S(1)}, bf16[32,3200]{1,0:T(8,128)(2,1)S(1)}, u32[]{:S(2)}, u32[]{:S(2)}) %collective-permute-start.53) | collective-permute-done | bytes 204832 | tf_op jit(solution)/shard_map/ppermute | solution.py:51
  463.3 2.4 collective-permute-start.55
  469.2 3.4 dense_outputs.1
  472.6 1.6 copy.46
  474.2 1.3 fusion.31
  (261 shorter events, 70.4 us)
Async XLA Ops:
  8.7 30.6 %collective-permute-start = (bf16[128,5248]{1,0:T(8,128)(2,1)}, bf16[128,5248]{1,0:T(8,128)(2,1)S(1)}, u32[]{:S(2)}, u32[]{:S(2)}) collective-permute-start(bf16[128,5248]{1,0:T(8,128)(2,1)} %pad_maximum_fusion.12), channel_id=1, source_target_pairs={{0,1},{1,0},{2,3},{3,2},{4,5},{5,4},{6,7},{7,6},{8,9},{9,8},{10,11... | collective-permute-start | bytes 4030472 | tf_op jit(solution)/shard_map/ppermute | solution.py:59
  9.9 30.3 %collective-permute-start.1 = (bf16[128,5248]{1,0:T(8,128)(2,1)}, bf16[128,5248]{1,0:T(8,128)(2,1)S(1)}, u32[]{:S(2)}, u32[]{:S(2)}) collective-permute-start(bf16[128,5248]{1,0:T(8,128)(2,1)} %pad_maximum_fusion.12), channel_id=1, source_target_pairs={{0,2},{2,0},{1,3},{3,1},{4,6},{6,4},{5,7},{7,5},{8,10},{10,8},{9,1... | collective-permute-start | bytes 4030472 | tf_op jit(solution)/shard_map/ppermute | solution.py:59
  20.6 13.3 %collective-permute-start.2 = (bf16[272,1024]{1,0:T(8,128)(2,1)}, bf16[272,1024]{1,0:T(8,128)(2,1)}, u32[]{:S(2)}, u32[]{:S(2)}) collective-permute-start(bf16[272,1024]{1,0:T(8,128)(2,1)} %constant_dynamic-update-slice_fusion), channel_id=1, source_target_pairs={{0,24},{8,0},{16,8},{24,16},{1,25},{9,1},{17,9},{25,17},{2,26},{10... | collective-permute-start | bytes 1671176 | tf_op jit(solution)/shard_map/ppermute | solution.py:51
  25.6 83.7 %copy-start.8 = (bf16[768,512]{1,0:T(8,128)(2,1)}, bf16[768,512]{1,0:T(8,128)(2,1)S(1)}, u32[]{:S(2)}) copy-start(bf16[768,512]{1,0:T(8,128)(2,1)S(1)} %get-tuple-element.167.refs_6_) | copy-start | bytes 2359300
  40.3 15.0 %collective-permute-start.3 = (bf16[64,5248]{1,0:T(8,128)(2,1)S(1)}, bf16[64,5248]{1,0:T(8,128)(2,1)S(1)}, u32[]{:S(2)}, u32[]{:S(2)}) collective-permute-start(bf16[64,5248]{1,0:T(8,128)(2,1)S(1)} %slice.241), channel_id=1, source_target_pairs={{0,2},{2,0},{1,3},{3,1},{4,6},{6,4},{5,7},{7,5},{8,10},{10,8},{9,1... | collective-permute-start | bytes 2015240 | tf_op jit(solution)/shard_map/ppermute | solution.py:65
  41.6 14.7 %collective-permute-start.4 = (bf16[64,5248]{1,0:T(8,128)(2,1)S(1)}, bf16[64,5248]{1,0:T(8,128)(2,1)S(1)}, u32[]{:S(2)}, u32[]{:S(2)}) collective-permute-start(bf16[64,5248]{1,0:T(8,128)(2,1)S(1)} %slice.242), channel_id=1, source_target_pairs={{0,1},{1,0},{2,3},{3,2},{4,5},{5,4},{6,7},{7,6},{8,9},{9,8},{10,11... | collective-permute-start | bytes 2015240 | tf_op jit(solution)/shard_map/ppermute | solution.py:65
  42.0 16.9 %collective-permute-start.5 = (bf16[272,1024]{1,0:T(8,128)(2,1)}, bf16[272,1024]{1,0:T(8,128)(2,1)}, u32[]{:S(2)}, u32[]{:S(2)}) collective-permute-start(bf16[272,1024]{1,0:T(8,128)(2,1)} %constant_dynamic-update-slice_fusion), channel_id=1, source_target_pairs={{0,8},{8,16},{16,24},{24,0},{1,9},{9,17},{17,25},{25,1},{2,10},{10... | collective-permute-start | bytes 1671176 | tf_op jit(solution)/shard_map/ppermute | solution.py:51
  43.3 14.0 %slice-start.1 = ((bf16[128,5248]{1,0:T(8,128)(2,1)}), bf16[128,3200]{1,0:T(8,128)(2,1)S(1)}, s32[]{:S(2)}) async-start(bf16[128,5248]{1,0:T(8,128)(2,1)} %copy-done.5), calls=%async_computation.1 | async-start | bytes 1638400 | tf_op jit(solution)/shard_map/slice | solution.py:1069
  58.9 7.5 %collective-permute-start.6 = (bf16[384,3200]{1,0:T(8,128)(2,1)}, bf16[384,3200]{1,0:T(8,128)(2,1)}, u32[]{:S(2)}, u32[]{:S(2)}) collective-permute-start(bf16[384,3200]{1,0:T(8,128)(2,1)} %pad_maximum_fusion.1.moved_ref), channel_id=1, source_target_pairs={{0,4},{4,0},{1,5},{5,1},{2,6},{6,2},{3,7},{7,3},{8,12},{12,8},{9,1... | collective-permute-start | bytes 7372808 | tf_op jit(solution)/shard_map/ppermute | solution.py:47
  62.4 39.5 %collective-permute-start.8 = (bf16[768,512]{1,0:T(8,128)(2,1)S(1)}, bf16[768,512]{1,0:T(8,128)(2,1)S(1)}, u32[]{:S(2)}, u32[]{:S(2)}) collective-permute-start(bf16[768,512]{1,0:T(8,128)(2,1)S(1)} %copy-done.19), channel_id=1, source_target_pairs={{0,1},{1,0},{2,3},{3,2},{4,5},{5,4},{6,7},{7,6},{8,9},{9,8},{10,11... | collective-permute-start | bytes 2359304 | tf_op jit(solution)/shard_map/ppermute | solution.py:59
  62.7 39.3 %collective-permute-start.9 = (bf16[768,512]{1,0:T(8,128)(2,1)S(1)}, bf16[768,512]{1,0:T(8,128)(2,1)}, u32[]{:S(2)}, u32[]{:S(2)}) collective-permute-start(bf16[768,512]{1,0:T(8,128)(2,1)S(1)} %copy-done.19), channel_id=1, source_target_pairs={{0,2},{2,0},{1,3},{3,1},{4,6},{6,4},{5,7},{7,5},{8,10},{10,8},{9,1... | collective-permute-start | bytes 2359304 | tf_op jit(solution)/shard_map/ppermute | solution.py:59
  73.1 28.8 %collective-permute-start.10 = (bf16[768,512]{1,0:T(8,128)(2,1)S(1)}, bf16[768,512]{1,0:T(8,128)(2,1)}, u32[]{:S(2)}, u32[]{:S(2)}) collective-permute-start(bf16[768,512]{1,0:T(8,128)(2,1)S(1)} %copy-done.20), channel_id=1, source_target_pairs={{0,1},{1,0},{2,3},{3,2},{4,5},{5,4},{6,7},{7,6},{8,9},{9,8},{10,11... | collective-permute-start | bytes 2359304 | tf_op jit(solution)/shard_map/ppermute | solution.py:59
  73.4 28.5 %collective-permute-start.11 = (bf16[768,512]{1,0:T(8,128)(2,1)S(1)}, bf16[768,512]{1,0:T(8,128)(2,1)}, u32[]{:S(2)}, u32[]{:S(2)}) collective-permute-start(bf16[768,512]{1,0:T(8,128)(2,1)S(1)} %copy-done.20), channel_id=1, source_target_pairs={{0,2},{2,0},{1,3},{3,1},{4,6},{6,4},{5,7},{7,5},{8,10},{10,8},{9,1... | collective-permute-start | bytes 2359304 | tf_op jit(solution)/shard_map/ppermute | solution.py:59
  74.2 27.7 %collective-permute-start.7 = (bf16[272,1024]{1,0:T(8,128)(2,1)}, bf16[272,1024]{1,0:T(8,128)(2,1)S(1)}, u32[]{:S(2)}, u32[]{:S(2)}) collective-permute-start(bf16[272,1024]{1,0:T(8,128)(2,1)} %constant_dynamic-update-slice_fusion), channel_id=1, source_target_pairs={{0,16},{8,24},{16,0},{24,8},{1,17},{9,25},{17,1},{25,9},{2,18},{10... | collective-permute-start | bytes 1671176 | tf_op jit(solution)/shard_map/ppermute | solution.py:51
  104.9 8.3 %collective-permute-start.14 = (bf16[4,272,1024]{2,1,0:T(8,128)(2,1)S(1)}, bf16[4,272,1024]{2,1,0:T(8,128)(2,1)S(1)}, u32[]{:S(2)}, u32[]{:S(2)}) collective-permute-start(bf16[4,272,1024]{2,1,0:T(8,128)(2,1)S(1)} %pad_maximum_fusion.2.packed_ref.code_ref), channel_id=1, source_target_pairs={{0,4},{4,0},{1,5},{5,1},{2,6},{6,2},{3,7},{7,3},{8,12},{12,8},{9,1... | collective-permute-start | bytes 6684680 | tf_op jit(solution)/shard_map/ppermute | solution.py:47
  109.5 37.5 %copy-start.9 = (bf16[768,512]{1,0:T(8,128)(2,1)S(1)}, bf16[768,512]{1,0:T(8,128)(2,1)}, u32[]{:S(2)}) copy-start(bf16[768,512]{1,0:T(8,128)(2,1)} %get-tuple-element.168.refs_11_) | copy-start | bytes 2359300
  109.5 35.4 %collective-permute-start.17 = (bf16[1536,512]{1,0:T(8,128)(2,1)S(1)}, bf16[1536,512]{1,0:T(8,128)(2,1)S(1)}, u32[]{:S(2)}, u32[]{:S(2)}) collective-permute-start(bf16[1536,512]{1,0:T(8,128)(2,1)S(1)} %get-tuple-element.370), channel_id=1, source_target_pairs={{0,1},{1,0},{2,3},{3,2},{4,5},{5,4},{6,7},{7,6},{8,9},{9,8},{10,11... | collective-permute-start | bytes 4718600 | tf_op jit(solution)/shard_map/ppermute | solution.py:74
  110.8 35.1 %collective-permute-start.18 = (bf16[1536,512]{1,0:T(8,128)(2,1)S(1)}, bf16[1536,512]{1,0:T(8,128)(2,1)S(1)}, u32[]{:S(2)}, u32[]{:S(2)}) collective-permute-start(bf16[1536,512]{1,0:T(8,128)(2,1)S(1)} %get-tuple-element.369), channel_id=1, source_target_pairs={{0,2},{2,0},{1,3},{3,1},{4,6},{6,4},{5,7},{7,5},{8,10},{10,8},{9,1... | collective-permute-start | bytes 4718600 | tf_op jit(solution)/shard_map/ppermute | solution.py:74
  111.5 12.5 %collective-permute-start.12 = (bf16[256,1024]{1,0:T(8,128)(2,1)}, bf16[256,1024]{1,0:T(8,128)(2,1)S(1)}, u32[]{:S(2)}, u32[]{:S(2)}) collective-permute-start(bf16[256,1024]{1,0:T(8,128)(2,1)} %get-tuple-element.193.rest_0_.refs_11_), channel_id=1, source_target_pairs={{0,24},{8,0},{16,8},{24,16},{1,25},{9,1},{17,9},{25,17},{2,26},{10... | collective-permute-start | bytes 1572872 | tf_op jit(solution)/shard_map/ppermute | solution.py:51
  111.6 25.5 %collective-permute-start.16 = (bf16[256,1024]{1,0:T(8,128)(2,1)}, bf16[256,1024]{1,0:T(8,128)(2,1)}, u32[]{:S(2)}, u32[]{:S(2)}) collective-permute-start(bf16[256,1024]{1,0:T(8,128)(2,1)} %get-tuple-element.193.rest_0_.refs_11_), channel_id=1, source_target_pairs={{0,8},{8,16},{16,24},{24,0},{1,9},{9,17},{17,25},{25,1},{2,10},{10... | collective-permute-start | bytes 1572872 | tf_op jit(solution)/shard_map/ppermute | solution.py:51
  113.2 35.4 %copy-start.1 = (bf16[4,272,1024]{2,1,0:T(8,128)(2,1)}, bf16[4,272,1024]{2,1,0:T(8,128)(2,1)S(1)}, u32[]{:S(2)}) copy-start(bf16[4,272,1024]{2,1,0:T(8,128)(2,1)S(1)} %collective-permute-done.14.packed_ref.code_ref) | copy-start | bytes 6684676
  113.2 32.6 %collective-permute-start.15 = (bf16[256,1024]{1,0:T(8,128)(2,1)}, bf16[256,1024]{1,0:T(8,128)(2,1)}, u32[]{:S(2)}, u32[]{:S(2)}) collective-permute-start(bf16[256,1024]{1,0:T(8,128)(2,1)} %get-tuple-element.193.rest_0_.refs_11_), channel_id=1, source_target_pairs={{0,4},{4,0},{1,5},{5,1},{2,6},{6,2},{3,7},{7,3},{8,12},{12,8},{9,1... | collective-permute-start | bytes 1572872 | tf_op jit(solution)/shard_map/ppermute | solution.py:47
  124.0 35.1 %copy-start.44 = (bf16[256,1024]{1,0:T(8,128)(2,1)}, bf16[256,1024]{1,0:T(8,128)(2,1)S(1)}, u32[]{:S(2)}) copy-start(bf16[256,1024]{1,0:T(8,128)(2,1)S(1)} %collective-permute-done.12.rest_1_) | copy-start | bytes 1572868
  148.6 27.1 %collective-permute-start.21 = (bf16[1152,512]{1,0:T(8,128)(2,1)}, bf16[1152,512]{1,0:T(8,128)(2,1)S(1)}, u32[]{:S(2)}, u32[]{:S(2)}) collective-permute-start(bf16[1152,512]{1,0:T(8,128)(2,1)} %get-tuple-element.368), channel_id=1, source_target_pairs={{0,1},{1,0},{2,3},{3,2},{4,5},{5,4},{6,7},{7,6},{8,9},{9,8},{10,11... | collective-permute-start | bytes 3538952 | tf_op jit(solution)/shard_map/ppermute | solution.py:74
  149.4 27.3 %collective-permute-start.22 = (bf16[1152,512]{1,0:T(8,128)(2,1)}, bf16[1152,512]{1,0:T(8,128)(2,1)S(1)}, u32[]{:S(2)}, u32[]{:S(2)}) collective-permute-start(bf16[1152,512]{1,0:T(8,128)(2,1)} %get-tuple-element.367), channel_id=1, source_target_pairs={{0,2},{2,0},{1,3},{3,1},{4,6},{6,4},{5,7},{7,5},{8,10},{10,8},{9,1... | collective-permute-start | bytes 3538952 | tf_op jit(solution)/shard_map/ppermute | solution.py:74
  150.1 3.7 collective-permute-start.19
  152.1 2.4 collective-permute-start.20
  152.1 23.1 %collective-permute-start.13 = (bf16[256,1024]{1,0:T(8,128)(2,1)}, bf16[256,1024]{1,0:T(8,128)(2,1)}, u32[]{:S(2)}, u32[]{:S(2)}) collective-permute-start(bf16[256,1024]{1,0:T(8,128)(2,1)} %get-tuple-element.193.rest_0_.refs_11_), channel_id=1, source_target_pairs={{0,16},{8,24},{16,0},{24,8},{1,17},{9,25},{17,1},{25,9},{2,18},{10... | collective-permute-start | bytes 1572872 | tf_op jit(solution)/shard_map/ppermute | solution.py:51
  175.2 9.8 %collective-permute-start.23 = (bf16[256,1024]{1,0:T(8,128)(2,1)}, bf16[256,1024]{1,0:T(8,128)(2,1)S(1)}, u32[]{:S(2)}, u32[]{:S(2)}) collective-permute-start(bf16[256,1024]{1,0:T(8,128)(2,1)} %collective-permute-done.13.rest_2_), channel_id=1, source_target_pairs={{0,4},{4,0},{1,5},{5,1},{2,6},{6,2},{3,7},{7,3},{8,12},{12,8},{9,1... | collective-permute-start | bytes 1572872 | tf_op jit(solution)/shard_map/ppermute | solution.py:47
  175.8 15.2 %collective-permute-start.24 = (bf16[384,512]{1,0:T(8,128)(2,1)S(1)}, bf16[384,512]{1,0:T(8,128)(2,1)S(1)}, u32[]{:S(2)}, u32[]{:S(2)}) collective-permute-start(bf16[384,512]{1,0:T(8,128)(2,1)S(1)} %slice.296), channel_id=1, source_target_pairs={{0,2},{2,0},{1,3},{3,1},{4,6},{6,4},{5,7},{7,5},{8,10},{10,8},{9,1... | collective-permute-start | bytes 1179656 | tf_op jit(solution)/shard_map/ppermute | solution.py:65
  176.7 14.2 %collective-permute-start.25 = (bf16[384,512]{1,0:T(8,128)(2,1)S(1)}, bf16[384,512]{1,0:T(8,128)(2,1)}, u32[]{:S(2)}, u32[]{:S(2)}) collective-permute-start(bf16[384,512]{1,0:T(8,128)(2,1)S(1)} %slice.297), channel_id=1, source_target_pairs={{0,1},{1,0},{2,3},{3,2},{4,5},{5,4},{6,7},{7,6},{8,9},{9,8},{10,11... | collective-permute-start | bytes 1179656 | tf_op jit(solution)/shard_map/ppermute | solution.py:65
  190.9 25.3 %copy-start.49 = (bf16[384,512]{1,0:T(8,128)(2,1)}, bf16[384,512]{1,0:T(8,128)(2,1)S(1)}, u32[]{:S(2)}) copy-start(bf16[384,512]{1,0:T(8,128)(2,1)S(1)} %collective-permute-done.24.refs_14_) | copy-start | bytes 1179652
  216.3 27.1 %collective-permute-start.26 = (bf16[1,1,768,512]{3,2,1,0:T(8,128)(2,1)}, bf16[1,1,768,512]{3,2,1,0:T(8,128)(2,1)S(1)}, u32[]{:S(2)}, u32[]{:S(2)}) collective-permute-start(bf16[1,1,768,512]{3,2,1,0:T(8,128)(2,1)} %get-tuple-element.211), channel_id=1, source_target_pairs={{0,1},{1,0},{2,3},{3,2},{4,5},{5,4},{6,7},{7,6},{8,9},{9,8},{10,11... | collective-permute-start | bytes 2359304 | tf_op jit(solution)/shard_map/ppermute | solution.py:74
  216.8 26.5 %collective-permute-start.27 = (bf16[1,1,768,512]{3,2,1,0:T(8,128)(2,1)}, bf16[1,1,768,512]{3,2,1,0:T(8,128)(2,1)S(1)}, u32[]{:S(2)}, u32[]{:S(2)}) collective-permute-start(bf16[1,1,768,512]{3,2,1,0:T(8,128)(2,1)} %get-tuple-element.212), channel_id=1, source_target_pairs={{0,2},{2,0},{1,3},{3,1},{4,6},{6,4},{5,7},{7,5},{8,10},{10,8},{9,1... | collective-permute-start | bytes 2359304 | tf_op jit(solution)/shard_map/ppermute | solution.py:74
  248.9 14.4 %collective-permute-start.28 = (bf16[4,256,1152]{2,1,0:T(8,128)(2,1)}, bf16[4,256,1152]{2,1,0:T(8,128)(2,1)}, u32[]{:S(2)}, u32[]{:S(2)}) collective-permute-start(bf16[4,256,1152]{2,1,0:T(8,128)(2,1)} %combine.4), channel_id=1, source_target_pairs={{0,4},{4,0},{1,5},{5,1},{2,6},{6,2},{3,7},{7,3},{8,12},{12,8},{9,1... | collective-permute-start | bytes 7077896 | tf_op jit(solution)/shard_map/ppermute | solution.py:47
  256.4 12.9 %collective-permute-start.29 = (bf16[4,256,1024]{2,1,0:T(8,128)(2,1)}, bf16[4,256,1024]{2,1,0:T(8,128)(2,1)}, u32[]{:S(2)}, u32[]{:S(2)}) collective-permute-start(bf16[4,256,1024]{2,1,0:T(8,128)(2,1)} %combine.5), channel_id=1, source_target_pairs={{0,4},{4,0},{1,5},{5,1},{2,6},{6,2},{3,7},{7,3},{8,12},{12,8},{9,1... | collective-permute-start | bytes 6291464 | tf_op jit(solution)/shard_map/ppermute | solution.py:47
  261.9 61.9 %collective-permute-start.30 = (bf16[3,1,768,512]{3,2,1,0:T(8,128)(2,1)}, bf16[3,1,768,512]{3,2,1,0:T(8,128)(2,1)S(1)}, u32[]{:S(2)}, u32[]{:S(2)}) collective-permute-start(bf16[3,1,768,512]{3,2,1,0:T(8,128)(2,1)} %get-tuple-element.234), channel_id=1, source_target_pairs={{0,1},{1,0},{2,3},{3,2},{4,5},{5,4},{6,7},{7,6},{8,9},{9,8},{10,11... | collective-permute-start | bytes 7077896 | tf_op jit(solution)/shard_map/ppermute | solution.py:74
  262.7 61.2 %collective-permute-start.31 = (bf16[3,1,768,512]{3,2,1,0:T(8,128)(2,1)}, bf16[3,1,768,512]{3,2,1,0:T(8,128)(2,1)}, u32[]{:S(2)}, u32[]{:S(2)}) collective-permute-start(bf16[3,1,768,512]{3,2,1,0:T(8,128)(2,1)} %get-tuple-element.235), channel_id=1, source_target_pairs={{0,2},{2,0},{1,3},{3,1},{4,6},{6,4},{5,7},{7,5},{8,10},{10,8},{9,1... | collective-permute-start | bytes 7077896 | tf_op jit(solution)/shard_map/ppermute | solution.py:74
  269.4 28.6 %collective-permute-start.32 = (bf16[256,1152]{1,0:T(8,128)(2,1)}, bf16[256,1152]{1,0:T(8,128)(2,1)S(1)}, u32[]{:S(2)}, u32[]{:S(2)}) collective-permute-start(bf16[256,1152]{1,0:T(8,128)(2,1)} %get-tuple-element.236), channel_id=1, source_target_pairs={{0,16},{8,24},{16,0},{24,8},{1,17},{9,25},{17,1},{25,9},{2,18},{10... | collective-permute-start | bytes 1769480 | tf_op jit(solution)/shard_map/ppermute | solution.py:51
  271.4 51.2 %collective-permute-start.33 = (bf16[256,1152]{1,0:T(8,128)(2,1)}, bf16[256,1152]{1,0:T(8,128)(2,1)}, u32[]{:S(2)}, u32[]{:S(2)}) collective-permute-start(bf16[256,1152]{1,0:T(8,128)(2,1)} %get-tuple-element.237), channel_id=1, source_target_pairs={{0,8},{8,16},{16,24},{24,0},{1,9},{9,17},{17,25},{25,1},{2,10},{10... | collective-permute-start | bytes 1769480 | tf_op jit(solution)/shard_map/ppermute | solution.py:51
  272.7 51.1 %collective-permute-start.34 = (bf16[256,1152]{1,0:T(8,128)(2,1)}, bf16[256,1152]{1,0:T(8,128)(2,1)}, u32[]{:S(2)}, u32[]{:S(2)}) collective-permute-start(bf16[256,1152]{1,0:T(8,128)(2,1)} %get-tuple-element.238), channel_id=1, source_target_pairs={{0,24},{8,0},{16,8},{24,16},{1,25},{9,1},{17,9},{25,17},{2,26},{10... | collective-permute-start | bytes 1769480 | tf_op jit(solution)/shard_map/ppermute | solution.py:51
  298.0 35.5 %copy-start.37 = (bf16[256,1152]{1,0:T(8,128)(2,1)}, bf16[256,1152]{1,0:T(8,128)(2,1)S(1)}, u32[]{:S(2)}) copy-start(bf16[256,1152]{1,0:T(8,128)(2,1)S(1)} %collective-permute-done.32.refs_1_) | copy-start | bytes 1769476
  329.9 40.3 %collective-permute-start.35 = (bf16[2,1,768,512]{3,2,1,0:T(8,128)(2,1)}, bf16[2,1,768,512]{3,2,1,0:T(8,128)(2,1)S(1)}, u32[]{:S(2)}, u32[]{:S(2)}) collective-permute-start(bf16[2,1,768,512]{3,2,1,0:T(8,128)(2,1)} %get-tuple-element.247), channel_id=1, source_target_pairs={{0,1},{1,0},{2,3},{3,2},{4,5},{5,4},{6,7},{7,6},{8,9},{9,8},{10,11... | collective-permute-start | bytes 4718600 | tf_op jit(solution)/shard_map/ppermute | solution.py:74
  330.6 39.6 %collective-permute-start.36 = (bf16[2,1,768,512]{3,2,1,0:T(8,128)(2,1)}, bf16[2,1,768,512]{3,2,1,0:T(8,128)(2,1)S(1)}, u32[]{:S(2)}, u32[]{:S(2)}) collective-permute-start(bf16[2,1,768,512]{3,2,1,0:T(8,128)(2,1)} %get-tuple-element.248), channel_id=1, source_target_pairs={{0,2},{2,0},{1,3},{3,1},{4,6},{6,4},{5,7},{7,5},{8,10},{10,8},{9,1... | collective-permute-start | bytes 4718600 | tf_op jit(solution)/shard_map/ppermute | solution.py:74
  331.3 38.8 %collective-permute-start.37 = (bf16[256,1024]{1,0:T(8,128)(2,1)}, bf16[256,1024]{1,0:T(8,128)(2,1)}, u32[]{:S(2)}, u32[]{:S(2)}) collective-permute-start(bf16[256,1024]{1,0:T(8,128)(2,1)} %get-tuple-element.249), channel_id=1, source_target_pairs={{0,8},{8,16},{16,24},{24,0},{1,9},{9,17},{17,25},{25,1},{2,10},{10... | collective-permute-start | bytes 1572872 | tf_op jit(solution)/shard_map/ppermute | solution.py:51
  332.0 38.1 %collective-permute-start.38 = (bf16[256,1024]{1,0:T(8,128)(2,1)}, bf16[256,1024]{1,0:T(8,128)(2,1)}, u32[]{:S(2)}, u32[]{:S(2)}) collective-permute-start(bf16[256,1024]{1,0:T(8,128)(2,1)} %get-tuple-element.250), channel_id=1, source_target_pairs={{0,24},{8,0},{16,8},{24,16},{1,25},{9,1},{17,9},{25,17},{2,26},{10... | collective-permute-start | bytes 1572872 | tf_op jit(solution)/shard_map/ppermute | solution.py:51
  371.8 7.3 %collective-permute-start.40 = (bf16[4,128,3200]{2,1,0:T(8,128)(2,1)}, bf16[4,128,3200]{2,1,0:T(8,128)(2,1)S(1)}, u32[]{:S(2)}, u32[]{:S(2)}) collective-permute-start(bf16[4,128,3200]{2,1,0:T(8,128)(2,1)} %get-tuple-element.272), channel_id=1, source_target_pairs={{0,4},{4,0},{1,5},{5,1},{2,6},{6,2},{3,7},{7,3},{8,12},{12,8},{9,1... | collective-permute-start | bytes 9830408 | tf_op jit(solution)/shard_map/ppermute | solution.py:47
  373.4 13.8 %collective-permute-start.41 = (bf16[2,128,1024]{2,1,0:T(8,128)(2,1)}, bf16[2,128,1024]{2,1,0:T(8,128)(2,1)}, u32[]{:S(2)}, u32[]{:S(2)}) collective-permute-start(bf16[2,128,1024]{2,1,0:T(8,128)(2,1)} %get-tuple-element.276), channel_id=1, source_target_pairs={{0,1},{1,0},{2,3},{3,2},{4,5},{5,4},{6,7},{7,6},{8,9},{9,8},{10,11... | collective-permute-start | bytes 1572872 | tf_op jit(solution)/shard_map/ppermute | solution.py:91
  374.2 13.5 %collective-permute-start.42 = (bf16[2,128,1024]{2,1,0:T(8,128)(2,1)}, bf16[2,128,1024]{2,1,0:T(8,128)(2,1)S(1)}, u32[]{:S(2)}, u32[]{:S(2)}) collective-permute-start(bf16[2,128,1024]{2,1,0:T(8,128)(2,1)} %get-tuple-element.277), channel_id=1, source_target_pairs={{0,2},{2,0},{1,3},{3,1},{4,6},{6,4},{5,7},{7,5},{8,10},{10,8},{9,1... | collective-permute-start | bytes 1572872 | tf_op jit(solution)/shard_map/ppermute | solution.py:91
  386.9 24.2 %copy-start.11 = (bf16[3,1,768,512]{3,2,1,0:T(8,128)(2,1)S(1)}, bf16[3,1,768,512]{3,2,1,0:T(8,128)(2,1)}, u32[]{:S(2)}) copy-start(bf16[3,1,768,512]{3,2,1,0:T(8,128)(2,1)} %copy-done.10) | copy-start | bytes 7077892
  388.5 19.1 %collective-permute-start.43 = (bf16[2,64,3200]{2,1,0:T(8,128)(2,1)}, bf16[2,64,3200]{2,1,0:T(8,128)(2,1)S(1)}, u32[]{:S(2)}, u32[]{:S(2)}) collective-permute-start(bf16[2,64,3200]{2,1,0:T(8,128)(2,1)} %get-tuple-element.278), channel_id=1, source_target_pairs={{0,1},{1,0},{2,3},{3,2},{4,5},{5,4},{6,7},{7,6},{8,9},{9,8},{10,11... | collective-permute-start | bytes 2457608 | tf_op jit(solution)/shard_map/ppermute | solution.py:91
  389.2 18.8 %collective-permute-start.44 = (bf16[2,64,3200]{2,1,0:T(8,128)(2,1)}, bf16[2,64,3200]{2,1,0:T(8,128)(2,1)}, u32[]{:S(2)}, u32[]{:S(2)}) collective-permute-start(bf16[2,64,3200]{2,1,0:T(8,128)(2,1)} %get-tuple-element.279), channel_id=1, source_target_pairs={{0,2},{2,0},{1,3},{3,1},{4,6},{6,4},{5,7},{7,5},{8,10},{10,8},{9,1... | collective-permute-start | bytes 2457608 | tf_op jit(solution)/shard_map/ppermute | solution.py:91
  390.9 39.3 %collective-permute-start.39 = (bf16[256,1024]{1,0:T(8,128)(2,1)}, bf16[256,1024]{1,0:T(8,128)(2,1)S(1)}, u32[]{:S(2)}, u32[]{:S(2)}) collective-permute-start(bf16[256,1024]{1,0:T(8,128)(2,1)} %get-tuple-element.264), channel_id=1, source_target_pairs={{0,16},{8,24},{16,0},{24,8},{1,17},{9,25},{17,1},{25,9},{2,18},{10... | collective-permute-start | bytes 1572872 | tf_op jit(solution)/shard_map/ppermute | solution.py:51
  409.2 11.7 %collective-permute-start.46 = (bf16[64,3200]{1,0:T(8,128)(2,1)S(1)}, bf16[64,3200]{1,0:T(8,128)(2,1)S(1)}, u32[]{:S(2)}, u32[]{:S(2)}) collective-permute-start(bf16[64,3200]{1,0:T(8,128)(2,1)S(1)} %fusion.7), channel_id=1, source_target_pairs={{0,1},{1,0},{2,3},{3,2},{4,5},{5,4},{6,7},{7,6},{8,9},{9,8},{10,11... | collective-permute-start | bytes 1228808 | tf_op jit(solution)/shard_map/ppermute | solution.py:99
  417.5 8.6 %collective-permute-start.45 = (bf16[64,3200]{1,0:T(8,128)(2,1)S(1)}, bf16[64,3200]{1,0:T(8,128)(2,1)S(1)}, u32[]{:S(2)}, u32[]{:S(2)}) collective-permute-start(bf16[64,3200]{1,0:T(8,128)(2,1)S(1)} %fusion.6), channel_id=1, source_target_pairs={{0,2},{2,0},{1,3},{3,1},{4,6},{6,4},{5,7},{7,5},{8,10},{10,8},{9,1... | collective-permute-start | bytes 1228808 | tf_op jit(solution)/shard_map/ppermute | solution.py:98
  426.4 7.2 %collective-permute-start.49 = (bf16[32,3200]{1,0:T(8,128)(2,1)S(1)}, bf16[32,3200]{1,0:T(8,128)(2,1)S(1)}, u32[]{:S(2)}, u32[]{:S(2)}) collective-permute-start(bf16[32,3200]{1,0:T(8,128)(2,1)S(1)} %get-tuple-element.364), channel_id=1, source_target_pairs={{0,16},{8,24},{16,0},{24,8},{1,17},{9,25},{17,1},{25,9},{2,18},{10... | collective-permute-start | bytes 614408 | tf_op jit(solution)/shard_map/ppermute | solution.py:51
  426.6 16.4 %collective-permute-start.50 = (bf16[32,3200]{1,0:T(8,128)(2,1)S(1)}, bf16[32,3200]{1,0:T(8,128)(2,1)S(1)}, u32[]{:S(2)}, u32[]{:S(2)}) collective-permute-start(bf16[32,3200]{1,0:T(8,128)(2,1)S(1)} %get-tuple-element.366), channel_id=1, source_target_pairs={{0,8},{8,16},{16,24},{24,0},{1,9},{9,17},{17,25},{25,1},{2,10},{10... | collective-permute-start | bytes 614408 | tf_op jit(solution)/shard_map/ppermute | solution.py:51
  427.4 17.2 %collective-permute-start.51 = (bf16[32,3200]{1,0:T(8,128)(2,1)S(1)}, bf16[32,3200]{1,0:T(8,128)(2,1)S(1)}, u32[]{:S(2)}, u32[]{:S(2)}) collective-permute-start(bf16[32,3200]{1,0:T(8,128)(2,1)S(1)} %get-tuple-element.365), channel_id=1, source_target_pairs={{0,24},{8,0},{16,8},{24,16},{1,25},{9,1},{17,9},{25,17},{2,26},{10... | collective-permute-start | bytes 614408 | tf_op jit(solution)/shard_map/ppermute | solution.py:51
  429.3 17.2 %collective-permute-start.47 = (bf16[128,1024]{1,0:T(8,128)(2,1)S(1)}, bf16[128,1024]{1,0:T(8,128)(2,1)S(1)}, u32[]{:S(2)}, u32[]{:S(2)}) collective-permute-start(bf16[128,1024]{1,0:T(8,128)(2,1)S(1)} %fusion.11), channel_id=1, source_target_pairs={{0,2},{2,0},{1,3},{3,1},{4,6},{6,4},{5,7},{7,5},{8,10},{10,8},{9,1... | collective-permute-start | bytes 786440 | tf_op jit(solution)/shard_map/ppermute | solution.py:98
  430.2 35.4 %collective-permute-start.48 = (bf16[128,1024]{1,0:T(8,128)(2,1)S(1)}, bf16[128,1024]{1,0:T(8,128)(2,1)}, u32[]{:S(2)}, u32[]{:S(2)}) collective-permute-start(bf16[128,1024]{1,0:T(8,128)(2,1)S(1)} %fusion.12), channel_id=1, source_target_pairs={{0,1},{1,0},{2,3},{3,2},{4,5},{5,4},{6,7},{7,6},{8,9},{9,8},{10,11... | collective-permute-start | bytes 786440 | tf_op jit(solution)/shard_map/ppermute | solution.py:99
  444.8 10.6 %collective-permute-start.52 = (bf16[32,3200]{1,0:T(8,128)(2,1)S(1)}, bf16[32,3200]{1,0:T(8,128)(2,1)S(1)}, u32[]{:S(2)}, u32[]{:S(2)}) collective-permute-start(bf16[32,3200]{1,0:T(8,128)(2,1)S(1)} %fusion.10), channel_id=1, source_target_pairs={{0,16},{8,24},{16,0},{24,8},{1,17},{9,25},{17,1},{25,9},{2,18},{10... | collective-permute-start | bytes 614408 | tf_op jit(solution)/shard_map/ppermute | solution.py:51
  444.8 17.4 %collective-permute-start.53 = (bf16[32,3200]{1,0:T(8,128)(2,1)S(1)}, bf16[32,3200]{1,0:T(8,128)(2,1)S(1)}, u32[]{:S(2)}, u32[]{:S(2)}) collective-permute-start(bf16[32,3200]{1,0:T(8,128)(2,1)S(1)} %fusion.10), channel_id=1, source_target_pairs={{0,24},{8,0},{16,8},{24,16},{1,25},{9,1},{17,9},{25,17},{2,26},{10... | collective-permute-start | bytes 614408 | tf_op jit(solution)/shard_map/ppermute | solution.py:51
  446.5 15.7 %collective-permute-start.54 = (bf16[32,3200]{1,0:T(8,128)(2,1)S(1)}, bf16[32,3200]{1,0:T(8,128)(2,1)S(1)}, u32[]{:S(2)}, u32[]{:S(2)}) collective-permute-start(bf16[32,3200]{1,0:T(8,128)(2,1)S(1)} %fusion.10), channel_id=1, source_target_pairs={{0,8},{8,16},{16,24},{24,0},{1,9},{9,17},{17,25},{25,1},{2,10},{10... | collective-permute-start | bytes 614408 | tf_op jit(solution)/shard_map/ppermute | solution.py:51
  463.3 5.1 %collective-permute-start.55 = (bf16[128,3200]{1,0:T(8,128)(2,1)S(1)}, bf16[128,3200]{1,0:T(8,128)(2,1)S(1)}, u32[]{:S(2)}, u32[]{:S(2)}) collective-permute-start(bf16[128,3200]{1,0:T(8,128)(2,1)S(1)} %bitcast_select_fusion.mine_ref), channel_id=1, source_target_pairs={{0,4},{4,0},{1,5},{5,1},{2,6},{6,2},{3,7},{7,3},{8,12},{12,8},{9,1... | collective-permute-start | bytes 2457608 | tf_op jit(solution)/shard_map/ppermute | solution.py:47
  (47 other events, 176.3 us)
